TPU v7x, 32 devices: a whole 2x2x4 slice. The times are simulated.
32 devices in a mesh: dp: 8 (over z, x), seq: 4 (over y, core).
Axes of the slice: x: 2, y: 2, z: 4, core: 2. Of those that a mesh axis runs over, the one named last changes fastest.
Arguments:
- tokens: bfloat16 [16, 1024, 512], P('dp', 'seq'), may hold values from -6 to 6
- memory: bfloat16 [16, 256, 512], P('dp', 'seq'), may hold values from -6 to 6
- target_ids: int32 [16, 1024], P('dp', 'seq'), may hold values from 0 to 3, never falling along the last dimension, each value on 1 to 768 neighbouring positions
- source_ids: int32 [16, 256], P('dp', 'seq'), may hold values from 0 to 3, never falling along the last dimension, each value on 1 to 192 neighbouring positions
- cotangent: bfloat16 [16, 1024, 512], P('dp', 'seq'), may hold values from -6 to 6
- query_weight: bfloat16 [512, 512], P(('dp', 'seq')), may hold values from -0.25 to 0.25
- key_weight: bfloat16 [512, 512], P(('dp', 'seq')), may hold values from -0.25 to 0.25
- value_weight: bfloat16 [512, 512], P(('dp', 'seq')), may hold values from -0.25 to 0.25
- output_weight: bfloat16 [512, 512], P(('dp', 'seq')), may hold values from -1 to 1
- query_bias: bfloat16 [512], P(('dp', 'seq')), may hold values from -1.796875 to 1.796875
- value_bias: bfloat16 [512], P(('dp', 'seq')), may hold values from -1.796875 to 1.796875
- output_bias: bfloat16 [512], P(('dp', 'seq')), may hold values from -1.796875 to 1.796875
- attention_gain: bfloat16 [512], P(('dp', 'seq')), may hold values from 0.5 to 1.5
- attention_shift: bfloat16 [512], P(('dp', 'seq')), may hold values from -1.1953125 to 1.1953125
- source_query: bfloat16 [512, 512], P(('dp', 'seq')), may hold values from -0.25 to 0.25
- source_key: bfloat16 [512, 512], P(('dp', 'seq')), may hold values from -0.25 to 0.25
- source_value: bfloat16 [512, 512], P(('dp', 'seq')), may hold values from -0.25 to 0.25
- source_output: bfloat16 [512, 512], P(('dp', 'seq')), may hold values from -1 to 1
- source_query_bias: bfloat16 [512], P(('dp', 'seq')), may hold values from -1.796875 to 1.796875
- source_value_bias: bfloat16 [512], P(('dp', 'seq')), may hold values from -1.796875 to 1.796875
- source_output_bias: bfloat16 [512], P(('dp', 'seq')), may hold values from -1.796875 to 1.796875
- source_gain: bfloat16 [512], P(('dp', 'seq')), may hold values from 0.5 to 1.5
- source_shift: bfloat16 [512], P(('dp', 'seq')), may hold values from -1.1953125 to 1.1953125
- inner_weight: bfloat16 [512, 2048], P(('dp', 'seq')), may hold values from -0.25 to 0.25
- inner_bias: bfloat16 [2048], P(('dp', 'seq')), may hold values from -1.796875 to 1.796875
- outer_weight: bfloat16 [2048, 512], P(('dp', 'seq')), may hold values from -0.125 to 0.125
- outer_bias: bfloat16 [512], P(('dp', 'seq')), may hold values from -1.796875 to 1.796875
- final_gain: bfloat16 [512], P(('dp', 'seq')), may hold values from 0.5 to 1.5
- final_shift: bfloat16 [512], P(('dp', 'seq')), may hold values from -1.1953125 to 1.1953125
Outputs:
- output: float32 [16, 1024, 512], P('dp', 'seq')
- input_gradient: float32 [16, 1024, 512], P('dp', 'seq')
- memory_gradient: float32 [16, 256, 512], P('dp', 'seq')
- query_weight_gradient: float32 [512, 512], P(('dp', 'seq'))
- key_weight_gradient: float32 [512, 512], P(('dp', 'seq'))
- value_weight_gradient: float32 [512, 512], P(('dp', 'seq'))
- output_weight_gradient: float32 [512, 512], P(('dp', 'seq'))
- query_bias_gradient: float32 [512], P(('dp', 'seq'))
- value_bias_gradient: float32 [512], P(('dp', 'seq'))
- output_bias_gradient: float32 [512], P(('dp', 'seq'))
- attention_gain_gradient: float32 [512], P(('dp', 'seq'))
- attention_shift_gradient: float32 [512], P(('dp', 'seq'))
- source_query_gradient: float32 [512, 512], P(('dp', 'seq'))
- source_key_gradient: float32 [512, 512], P(('dp', 'seq'))
- source_value_gradient: float32 [512, 512], P(('dp', 'seq'))
- source_output_gradient: float32 [512, 512], P(('dp', 'seq'))
- source_query_bias_gradient: float32 [512], P(('dp', 'seq'))
- source_value_bias_gradient: float32 [512], P(('dp', 'seq'))
- source_output_bias_gradient: float32 [512], P(('dp', 'seq'))
- source_gain_gradient: float32 [512], P(('dp', 'seq'))
- source_shift_gradient: float32 [512], P(('dp', 'seq'))
- inner_weight_gradient: float32 [512, 2048], P(('dp', 'seq'))
- inner_bias_gradient: float32 [2048], P(('dp', 'seq'))
- outer_weight_gradient: float32 [2048, 512], P(('dp', 'seq'))
- outer_bias_gradient: float32 [512], P(('dp', 'seq'))
- final_gain_gradient: float32 [512], P(('dp', 'seq'))
- final_shift_gradient: float32 [512], P(('dp', 'seq'))
Inputs may be any that keep to these rules, and one draw needn't show every extreme that they name: `target_ids`: along each row the ids never fall; every id of 0 to 3 covers at least one position of every row, none covers more than 768 positions of a row, and some row reaches that many. `source_ids`: along each row the ids never fall; every id of 0 to 3 covers at least one memory position of every row, none covers more than 192 positions of a row, and some row reaches that many.
All inputs are finite; a program needn't handle non-finite values.
Results may differ from a plain program's by a relative error of at most 0.018.
Values may be sent and summed in bfloat16 or wider, within the bound.
No kernel may reach another device: no remote copies, remote signals or barrier semaphores. Data moves between devices by JAX's collectives and lax.ppermute only.
A program may use at most 256 MiB of HBM per device.

v0:
```python
import jax
import jax.numpy as jnp
from jax import lax
from jax.sharding import PartitionSpec as P

HEADS = 8
HEAD_DIM = 64


EPSILON = 1e-05
MASKED = -1000000000.0


def product(former, latter):
    return jnp.dot(former, latter, preferred_element_type=jnp.float32)


def contract_rows(former, latter):
    return lax.dot_general(
        former, latter, (((0,), (0,)), ((), ())), preferred_element_type=jnp.float32
    )


def times_transpose(former, latter):
    return lax.dot_general(
        former, latter, (((1,), (1,)), ((), ())), preferred_element_type=jnp.float32
    )


def column_total(values):
    return jnp.sum(values.astype(jnp.float32), axis=0)


def smooth_gate(values):
    return jax.nn.gelu(values, approximate=False)


def smooth_gate_back(values, incoming):
    unused, pullback = jax.vjp(smooth_gate, values)
    return pullback(incoming)[0]


def layer_norm(total, gain, shift):
    average = jnp.mean(total, axis=-1, keepdims=True)
    centered = total - average
    variance = jnp.mean(centered * centered, axis=-1, keepdims=True)
    inverse = lax.rsqrt(variance + EPSILON)
    normed = centered * inverse
    return (normed * gain.astype(jnp.float32) + shift.astype(jnp.float32), normed, inverse)


def norm_back(upstream, normed, inverse, gain):
    scaled = upstream * gain.astype(jnp.float32)
    first_mean = jnp.mean(scaled, axis=-1, keepdims=True)
    second_mean = jnp.mean(scaled * normed, axis=-1, keepdims=True)
    lowered = inverse * (scaled - first_mean - normed * second_mean)
    return (lowered, jnp.sum(upstream * normed, axis=0), jnp.sum(upstream, axis=0))


def split_heads(block):
    return block.reshape(block.shape[0], 2, HEAD_DIM)


def pair_scores(heads_q, heads_k, query_ids, key_ids):
    scores = jnp.einsum(
        "qhd,khd->hqk", heads_q, heads_k, preferred_element_type=jnp.float32
    ) * HEAD_DIM ** (-0.5)
    matching = query_ids[:, None] == key_ids[None, :]
    return jnp.where(matching[None], scores, MASKED)


def pair_forward(queries, key_rows, values, query_ids, key_ids):
    scores = pair_scores(split_heads(queries), split_heads(key_rows), query_ids, key_ids)
    highest = jnp.max(scores, axis=-1, keepdims=True)
    weights = jnp.exp(scores - highest)
    denominator = jnp.sum(weights, axis=-1, keepdims=True)
    chances = (weights / denominator).astype(jnp.bfloat16)
    mixture = jnp.einsum(
        "hqk,khd->qhd", chances, split_heads(values), preferred_element_type=jnp.float32
    )
    return (
        mixture.reshape(queries.shape[0], 2 * HEAD_DIM),
        (highest + jnp.log(denominator))[:, :, 0],
    )


def attend(queries, key_rows, values, query_ids, key_ids):
    width = 2 * HEAD_DIM
    mixture_parts, total_parts = ([], [])
    for couple in range(HEADS // 2):
        columns = slice(couple * width, (couple + 1) * width)
        mixture, log_totals = pair_forward(
            queries[:, columns], key_rows[:, columns], values[:, columns], query_ids, key_ids
        )
        mixture_parts.append(mixture)
        total_parts.append(log_totals)
    return (jnp.concatenate(mixture_parts, axis=1), jnp.concatenate(total_parts, axis=0))


def pair_back(queries, key_rows, values, upstream, query_ids, key_ids, log_totals, deltas):
    scale = HEAD_DIM ** (-0.5)
    heads_q = split_heads(queries)
    heads_k = split_heads(key_rows)
    heads_g = split_heads(upstream)
    scores = pair_scores(heads_q, heads_k, query_ids, key_ids)
    chances = jnp.exp(scores - log_totals[:, :, None])
    slopes = jnp.einsum(
        "qhd,khd->hqk", heads_g, split_heads(values), preferred_element_type=jnp.float32
    )
    deltas = jnp.sum(chances * slopes, axis=-1)
    score_grad = (chances * (slopes - deltas[:, :, None])).astype(jnp.bfloat16)
    query_grad = (
        jnp.einsum("hqk,khd->qhd", score_grad, heads_k, preferred_element_type=jnp.float32) * scale
    )
    key_grad = (
        jnp.einsum("hqk,qhd->khd", score_grad, heads_q, preferred_element_type=jnp.float32) * scale
    )
    value_grad = jnp.einsum(
        "hqk,qhd->khd", chances.astype(jnp.bfloat16), heads_g, preferred_element_type=jnp.float32
    )
    width = 2 * HEAD_DIM
    return (
        query_grad.reshape(queries.shape[0], width),
        key_grad.reshape(key_rows.shape[0], width),
        value_grad.reshape(key_rows.shape[0], width),
        deltas,
    )


def attend_back(queries, key_rows, values, upstream, query_ids, key_ids, log_totals):
    width = 2 * HEAD_DIM
    query_parts, key_parts, value_parts, delta_parts = ([], [], [], [])
    for couple in range(HEADS // 2):
        columns = slice(couple * width, (couple + 1) * width)
        heads = slice(2 * couple, 2 * couple + 2)
        given = None
        found = pair_back(
            queries[:, columns],
            key_rows[:, columns],
            values[:, columns],
            upstream[:, columns],
            query_ids,
            key_ids,
            log_totals[heads],
            given,
        )
        query_parts.append(found[0])
        key_parts.append(found[1])
        value_parts.append(found[2])
        delta_parts.append(found[3])
    return (
        jnp.concatenate(query_parts, axis=1),
        jnp.concatenate(key_parts, axis=1),
        jnp.concatenate(value_parts, axis=1),
        jnp.concatenate(delta_parts, axis=0),
    )


def gather_self(
    query_weight,
    key_weight,
    value_weight,
    output_weight,
    query_bias,
    value_bias,
    output_bias,
    attention_gain,
    attention_shift,
):
    return (
        lax.all_gather(query_weight, ("dp", "seq"), axis=0, tiled=True),
        lax.all_gather(key_weight, ("dp", "seq"), axis=0, tiled=True),
        lax.all_gather(value_weight, ("dp", "seq"), axis=0, tiled=True),
        lax.all_gather(output_weight, ("dp", "seq"), axis=0, tiled=True),
        lax.all_gather(query_bias, ("dp", "seq"), axis=0, tiled=True),
        lax.all_gather(value_bias, ("dp", "seq"), axis=0, tiled=True),
        lax.all_gather(output_bias, ("dp", "seq"), axis=0, tiled=True),
        lax.all_gather(attention_gain, ("dp", "seq"), axis=0, tiled=True),
        lax.all_gather(attention_shift, ("dp", "seq"), axis=0, tiled=True),
    )


def gather_source(
    source_query,
    source_key,
    source_value,
    source_output,
    source_query_bias,
    source_value_bias,
    source_output_bias,
    source_gain,
    source_shift,
):
    return (
        lax.all_gather(source_query, ("dp", "seq"), axis=0, tiled=True),
        lax.all_gather(source_key, ("dp", "seq"), axis=0, tiled=True),
        lax.all_gather(source_value, ("dp", "seq"), axis=0, tiled=True),
        lax.all_gather(source_output, ("dp", "seq"), axis=0, tiled=True),
        lax.all_gather(source_query_bias, ("dp", "seq"), axis=0, tiled=True),
        lax.all_gather(source_value_bias, ("dp", "seq"), axis=0, tiled=True),
        lax.all_gather(source_output_bias, ("dp", "seq"), axis=0, tiled=True),
        lax.all_gather(source_gain, ("dp", "seq"), axis=0, tiled=True),
        lax.all_gather(source_shift, ("dp", "seq"), axis=0, tiled=True),
    )


def gather_inner(inner_weight, inner_bias, outer_weight, outer_bias, final_gain, final_shift):
    return (
        lax.all_gather(inner_weight, ("dp", "seq"), axis=0, tiled=True),
        lax.all_gather(inner_bias, ("dp", "seq"), axis=0, tiled=True),
        lax.all_gather(outer_weight, ("dp", "seq"), axis=0, tiled=True),
        lax.all_gather(outer_bias, ("dp", "seq"), axis=0, tiled=True),
        lax.all_gather(final_gain, ("dp", "seq"), axis=0, tiled=True),
        lax.all_gather(final_shift, ("dp", "seq"), axis=0, tiled=True),
    )


def per_device(
    tokens,
    memory,
    target_ids,
    source_ids,
    cotangent,
    query_weight,
    key_weight,
    value_weight,
    output_weight,
    query_bias,
    value_bias,
    output_bias,
    attention_gain,
    attention_shift,
    source_query,
    source_key,
    source_value,
    source_output,
    source_query_bias,
    source_value_bias,
    source_output_bias,
    source_gain,
    source_shift,
    inner_weight,
    inner_bias,
    outer_weight,
    outer_bias,
    final_gain,
    final_shift,
):
    row_count, row_length, width = tokens.shape
    memory_length = memory.shape[1]
    flat = tokens.reshape(row_count * row_length, width)
    memory_flat = memory.reshape(row_count * memory_length, width)
    self_set = gather_self(
        query_weight,
        key_weight,
        value_weight,
        output_weight,
        query_bias,
        value_bias,
        output_bias,
        attention_gain,
        attention_shift,
    )
    (
        query_full,
        key_full,
        value_full,
        output_full,
        query_bias_full,
        value_bias_full,
        output_bias_full,
        attention_gain_full,
        attention_shift_full,
    ) = self_set
    queries = (product(flat, query_full) + query_bias_full.astype(jnp.float32)).astype(jnp.bfloat16)
    key_local = product(flat, key_full).astype(jnp.bfloat16)
    value_local = (product(flat, value_full) + value_bias_full.astype(jnp.float32)).astype(
        jnp.bfloat16
    )
    key_rows, value_rows, id_rows, mixture_parts, total_rows = ([], [], [], [], [])
    for row in range(row_count):
        here = slice(row * row_length, (row + 1) * row_length)
        key_all, value_all, ids_all = (
            lax.all_gather(key_local[here], "seq", axis=0, tiled=True),
            lax.all_gather(value_local[here], "seq", axis=0, tiled=True),
            lax.all_gather(target_ids[row], "seq", axis=0, tiled=True),
        )
        mixture, log_totals = attend(queries[here], key_all, value_all, target_ids[row], ids_all)
        key_rows.append(key_all)
        value_rows.append(value_all)
        id_rows.append(ids_all)
        mixture_parts.append(mixture)
        total_rows.append(log_totals)
    mixture_low = jnp.concatenate(mixture_parts, axis=0).astype(jnp.bfloat16)
    first_sum = (
        flat.astype(jnp.float32)
        + product(mixture_low, output_full)
        + output_bias_full.astype(jnp.float32)
    )
    first, first_normed, first_inverse = layer_norm(
        first_sum, attention_gain_full, attention_shift_full
    )
    first_low = first.astype(jnp.bfloat16)
    source_set = gather_source(
        source_query,
        source_key,
        source_value,
        source_output,
        source_query_bias,
        source_value_bias,
        source_output_bias,
        source_gain,
        source_shift,
    )
    (
        source_query_full,
        source_key_full,
        source_value_full,
        source_output_full,
        source_query_bias_full,
        source_value_bias_full,
        source_output_bias_full,
        source_gain_full,
        source_shift_full,
    ) = source_set
    cross_queries = (
        product(first_low, source_query_full) + source_query_bias_full.astype(jnp.float32)
    ).astype(jnp.bfloat16)
    memory_keys = product(memory_flat, source_key_full).astype(jnp.bfloat16)
    memory_values = (
        product(memory_flat, source_value_full) + source_value_bias_full.astype(jnp.float32)
    ).astype(jnp.bfloat16)
    memory_key_rows, memory_value_rows, source_id_rows, cross_parts, cross_total_rows = (
        [],
        [],
        [],
        [],
        [],
    )
    for row in range(row_count):
        here = slice(row * row_length, (row + 1) * row_length)
        remote = slice(row * memory_length, (row + 1) * memory_length)
        memory_key_all, memory_value_all, source_all = (
            lax.all_gather(memory_keys[remote], "seq", axis=0, tiled=True),
            lax.all_gather(memory_values[remote], "seq", axis=0, tiled=True),
            lax.all_gather(source_ids[row], "seq", axis=0, tiled=True),
        )
        cross_mixture, cross_totals = attend(
            cross_queries[here], memory_key_all, memory_value_all, target_ids[row], source_all
        )
        memory_key_rows.append(memory_key_all)
        memory_value_rows.append(memory_value_all)
        source_id_rows.append(source_all)
        cross_parts.append(cross_mixture)
        cross_total_rows.append(cross_totals)
    cross_low = jnp.concatenate(cross_parts, axis=0).astype(jnp.bfloat16)
    second_sum = (
        first + product(cross_low, source_output_full) + source_output_bias_full.astype(jnp.float32)
    )
    second, second_normed, second_inverse = layer_norm(
        second_sum, source_gain_full, source_shift_full
    )
    second_low = second.astype(jnp.bfloat16)
    inner_set = gather_inner(
        inner_weight, inner_bias, outer_weight, outer_bias, final_gain, final_shift
    )
    inner_full, inner_bias_full, outer_full, outer_bias_full, final_gain_full, final_shift_full = (
        inner_set
    )
    inner_sum = product(second_low, inner_full) + inner_bias_full.astype(jnp.float32)
    active = smooth_gate(inner_sum).astype(jnp.bfloat16)
    third_sum = second + product(active, outer_full) + outer_bias_full.astype(jnp.float32)
    final, final_normed, final_inverse = layer_norm(third_sum, final_gain_full, final_shift_full)
    output = final.reshape(row_count, row_length, width)
    inner_set = gather_inner(
        inner_weight, inner_bias, outer_weight, outer_bias, final_gain, final_shift
    )
    inner_full, inner_bias_full, outer_full, outer_bias_full, final_gain_full, final_shift_full = (
        inner_set
    )
    upstream = cotangent.reshape(row_count * row_length, width).astype(jnp.float32)
    third_grad, final_gain_grad, final_shift_grad = norm_back(
        upstream, final_normed, final_inverse, final_gain_full
    )
    outer_low = third_grad.astype(jnp.bfloat16)
    outer_bias_grad = column_total(outer_low)
    outer_weight_grad = contract_rows(active, outer_low)
    inner_low = smooth_gate_back(inner_sum, times_transpose(outer_low, outer_full)).astype(
        jnp.bfloat16
    )
    inner_bias_grad = column_total(inner_low)
    inner_weight_grad = contract_rows(second_low, inner_low)
    second_grad = third_grad + times_transpose(inner_low, inner_full)
    (
        inner_weight_share,
        inner_bias_share,
        outer_weight_share,
        outer_bias_share,
        final_gain_share,
        final_shift_share,
    ) = (
        lax.psum_scatter(inner_weight_grad, ("dp", "seq"), scatter_dimension=0, tiled=True),
        lax.psum_scatter(inner_bias_grad, ("dp", "seq"), scatter_dimension=0, tiled=True),
        lax.psum_scatter(outer_weight_grad, ("dp", "seq"), scatter_dimension=0, tiled=True),
        lax.psum_scatter(outer_bias_grad, ("dp", "seq"), scatter_dimension=0, tiled=True),
        lax.psum_scatter(final_gain_grad, ("dp", "seq"), scatter_dimension=0, tiled=True),
        lax.psum_scatter(final_shift_grad, ("dp", "seq"), scatter_dimension=0, tiled=True),
    )
    source_set = gather_source(
        source_query,
        source_key,
        source_value,
        source_output,
        source_query_bias,
        source_value_bias,
        source_output_bias,
        source_gain,
        source_shift,
    )
    (
        source_query_full,
        source_key_full,
        source_value_full,
        source_output_full,
        source_query_bias_full,
        source_value_bias_full,
        source_output_bias_full,
        source_gain_full,
        source_shift_full,
    ) = source_set
    cross_grad, source_gain_grad, source_shift_grad = norm_back(
        second_grad, second_normed, second_inverse, source_gain_full
    )
    cross_branch_low = cross_grad.astype(jnp.bfloat16)
    source_output_bias_grad = column_total(cross_branch_low)
    source_output_grad = contract_rows(cross_low, cross_branch_low)
    cross_upstream = times_transpose(cross_branch_low, source_output_full).astype(jnp.bfloat16)
    cross_query_parts, memory_key_parts, memory_value_parts = ([], [], [])
    for row in range(row_count):
        here = slice(row * row_length, (row + 1) * row_length)
        query_part, key_part, value_part, unused_delta = attend_back(
            cross_queries[here],
            memory_key_rows[row],
            memory_value_rows[row],
            cross_upstream[here],
            target_ids[row],
            source_id_rows[row],
            cross_total_rows[row],
        )
        key_share, value_share = (
            lax.psum_scatter(
                key_part.astype(jnp.bfloat16), "seq", scatter_dimension=0, tiled=True
            ).astype(jnp.float32),
            lax.psum_scatter(
                value_part.astype(jnp.bfloat16), "seq", scatter_dimension=0, tiled=True
            ).astype(jnp.float32),
        )
        cross_query_parts.append(query_part)
        memory_key_parts.append(key_share)
        memory_value_parts.append(value_share)
    cross_query_low = jnp.concatenate(cross_query_parts, axis=0).astype(jnp.bfloat16)
    memory_key_low = jnp.concatenate(memory_key_parts, axis=0).astype(jnp.bfloat16)
    memory_value_low = jnp.concatenate(memory_value_parts, axis=0).astype(jnp.bfloat16)
    source_query_bias_grad = column_total(cross_query_low)
    source_query_grad = contract_rows(first_low, cross_query_low)
    source_key_grad = contract_rows(memory_flat, memory_key_low)
    source_value_grad = contract_rows(memory_flat, memory_value_low)
    source_value_bias_grad = column_total(memory_value_low)
    memory_gradient = (
        times_transpose(memory_key_low, source_key_full)
        + times_transpose(memory_value_low, source_value_full)
    ).reshape(row_count, memory_length, width)
    first_grad = cross_grad + times_transpose(cross_query_low, source_query_full)
    (
        source_query_share,
        source_key_share,
        source_value_share,
        source_output_share,
        source_query_bias_share,
        source_value_bias_share,
        source_output_bias_share,
        source_gain_share,
        source_shift_share,
    ) = (
        lax.psum_scatter(source_query_grad, ("dp", "seq"), scatter_dimension=0, tiled=True),
        lax.psum_scatter(source_key_grad, ("dp", "seq"), scatter_dimension=0, tiled=True),
        lax.psum_scatter(source_value_grad, ("dp", "seq"), scatter_dimension=0, tiled=True),
        lax.psum_scatter(source_output_grad, ("dp", "seq"), scatter_dimension=0, tiled=True),
        lax.psum_scatter(source_query_bias_grad, ("dp", "seq"), scatter_dimension=0, tiled=True),
        lax.psum_scatter(source_value_bias_grad, ("dp", "seq"), scatter_dimension=0, tiled=True),
        lax.psum_scatter(source_output_bias_grad, ("dp", "seq"), scatter_dimension=0, tiled=True),
        lax.psum_scatter(source_gain_grad, ("dp", "seq"), scatter_dimension=0, tiled=True),
        lax.psum_scatter(source_shift_grad, ("dp", "seq"), scatter_dimension=0, tiled=True),
    )
    self_set = gather_self(
        query_weight,
        key_weight,
        value_weight,
        output_weight,
        query_bias,
        value_bias,
        output_bias,
        attention_gain,
        attention_shift,
    )
    (
        query_full,
        key_full,
        value_full,
        output_full,
        query_bias_full,
        value_bias_full,
        output_bias_full,
        attention_gain_full,
        attention_shift_full,
    ) = self_set
    self_grad, attention_gain_grad, attention_shift_grad = norm_back(
        first_grad, first_normed, first_inverse, attention_gain_full
    )
    branch_low = self_grad.astype(jnp.bfloat16)
    output_bias_grad = column_total(branch_low)
    output_weight_grad = contract_rows(mixture_low, branch_low)
    self_upstream = times_transpose(branch_low, output_full).astype(jnp.bfloat16)
    query_parts, key_parts_all, value_parts_all = ([], [], [])
    for row in range(row_count):
        here = slice(row * row_length, (row + 1) * row_length)
        query_part, key_part, value_part, unused_delta = attend_back(
            queries[here],
            key_rows[row],
            value_rows[row],
            self_upstream[here],
            target_ids[row],
            id_rows[row],
            total_rows[row],
        )
        key_share, value_share = (
            lax.psum_scatter(
                key_part.astype(jnp.bfloat16), "seq", scatter_dimension=0, tiled=True
            ).astype(jnp.float32),
            lax.psum_scatter(
                value_part.astype(jnp.bfloat16), "seq", scatter_dimension=0, tiled=True
            ).astype(jnp.float32),
        )
        query_parts.append(query_part)
        key_parts_all.append(key_share)
        value_parts_all.append(value_share)
    query_low = jnp.concatenate(query_parts, axis=0).astype(jnp.bfloat16)
    key_low = jnp.concatenate(key_parts_all, axis=0).astype(jnp.bfloat16)
    value_low = jnp.concatenate(value_parts_all, axis=0).astype(jnp.bfloat16)
    query_bias_grad = column_total(query_low)
    query_weight_grad = contract_rows(flat, query_low)
    key_weight_grad = contract_rows(flat, key_low)
    value_weight_grad = contract_rows(flat, value_low)
    value_bias_grad = column_total(value_low)
    input_gradient = (
        self_grad
        + times_transpose(query_low, query_full)
        + times_transpose(key_low, key_full)
        + times_transpose(value_low, value_full)
    ).reshape(row_count, row_length, width)
    (
        query_weight_share,
        key_weight_share,
        value_weight_share,
        output_weight_share,
        query_bias_share,
        value_bias_share,
        output_bias_share,
        attention_gain_share,
        attention_shift_share,
    ) = (
        lax.psum_scatter(query_weight_grad, ("dp", "seq"), scatter_dimension=0, tiled=True),
        lax.psum_scatter(key_weight_grad, ("dp", "seq"), scatter_dimension=0, tiled=True),
        lax.psum_scatter(value_weight_grad, ("dp", "seq"), scatter_dimension=0, tiled=True),
        lax.psum_scatter(output_weight_grad, ("dp", "seq"), scatter_dimension=0, tiled=True),
        lax.psum_scatter(query_bias_grad, ("dp", "seq"), scatter_dimension=0, tiled=True),
        lax.psum_scatter(value_bias_grad, ("dp", "seq"), scatter_dimension=0, tiled=True),
        lax.psum_scatter(output_bias_grad, ("dp", "seq"), scatter_dimension=0, tiled=True),
        lax.psum_scatter(attention_gain_grad, ("dp", "seq"), scatter_dimension=0, tiled=True),
        lax.psum_scatter(attention_shift_grad, ("dp", "seq"), scatter_dimension=0, tiled=True),
    )
    return (
        output,
        input_gradient,
        memory_gradient,
        query_weight_share,
        key_weight_share,
        value_weight_share,
        output_weight_share,
        query_bias_share,
        value_bias_share,
        output_bias_share,
        attention_gain_share,
        attention_shift_share,
        source_query_share,
        source_key_share,
        source_value_share,
        source_output_share,
        source_query_bias_share,
        source_value_bias_share,
        source_output_bias_share,
        source_gain_share,
        source_shift_share,
        inner_weight_share,
        inner_bias_share,
        outer_weight_share,
        outer_bias_share,
        final_gain_share,
        final_shift_share,
    )


def solution(mesh):
    return jax.shard_map(
        per_device,
        mesh=mesh,
        in_specs=(
            P("dp", "seq", None),
            P("dp", "seq", None),
            P("dp", "seq"),
            P("dp", "seq"),
            P("dp", "seq", None),
            P(("dp", "seq"), None),
            P(("dp", "seq"), None),
            P(("dp", "seq"), None),
            P(("dp", "seq"), None),
            P(("dp", "seq")),
            P(("dp", "seq")),
            P(("dp", "seq")),
            P(("dp", "seq")),
            P(("dp", "seq")),
            P(("dp", "seq"), None),
            P(("dp", "seq"), None),
            P(("dp", "seq"), None),
            P(("dp", "seq"), None),
            P(("dp", "seq")),
            P(("dp", "seq")),
            P(("dp", "seq")),
            P(("dp", "seq")),
            P(("dp", "seq")),
            P(("dp", "seq"), None),
            P(("dp", "seq")),
            P(("dp", "seq"), None),
            P(("dp", "seq")),
            P(("dp", "seq")),
            P(("dp", "seq")),
        ),
        out_specs=(
            P("dp", "seq", None),
            P("dp", "seq", None),
            P("dp", "seq", None),
            P(("dp", "seq"), None),
            P(("dp", "seq"), None),
            P(("dp", "seq"), None),
            P(("dp", "seq"), None),
            P(("dp", "seq")),
            P(("dp", "seq")),
            P(("dp", "seq")),
            P(("dp", "seq")),
            P(("dp", "seq")),
            P(("dp", "seq"), None),
            P(("dp", "seq"), None),
            P(("dp", "seq"), None),
            P(("dp", "seq"), None),
            P(("dp", "seq")),
            P(("dp", "seq")),
            P(("dp", "seq")),
            P(("dp", "seq")),
            P(("dp", "seq")),
            P(("dp", "seq"), None),
            P(("dp", "seq")),
            P(("dp", "seq"), None),
            P(("dp", "seq")),
            P(("dp", "seq")),
            P(("dp", "seq")),
        ),
        check_vma=False,
    )
```

profile of v0, /device:TPU:0, one launch (start us, length us, event | category | flops | bytes accessed | tf_op | source)
XLA Modules:
  0.0 2110.4 jit_solution(13614706968621968368)
XLA Ops:
  19.2 42.3 %all-reduce.32 = (bf16[512]{0:T(512)(128)(2,1)S(1)}, bf16[512]{0:T(512)(128)(2,1)S(1)}, bf16[512]{0:T(512)(128)(2,1)S(1)}, bf16[512]{0:T(512)(128)(2,1)S(1)}, bf...) all-reduce(bf16[512]{0:T(512)(128)(2,1)S(1)} %dynamic-update-slice., ...), channel_id=1, replica_groups=mesh['dp'=8,'seq'=4] {'dp','seq'}, use_global_device_ids=true, to_apply=%add.2 | all-reduce | flops 8704 | bytes 34816
  61.5 41.9 %all_gather.121 = bf16[512,512]{1,0:T(8,128)(2,1)S(1)} all-gather(bf16[16,512]{1,0:T(8,128)(2,1)} %param.36), channel_id=1, replica_groups=mesh['dp'=8,'seq'=4] {'dp','seq'}, dimensions={0}, use_global_device_ids=true | all-gather | bytes 540672 | tf_op jit(solution)/shard_map/all_gather | solution.py:173
  107.4 38.4 %all_gather.127 = bf16[512,512]{1,0:T(8,128)(2,1)S(1)} all-gather(bf16[16,512]{1,0:T(8,128)(2,1)S(1)} %copy-done.253), channel_id=1, replica_groups=mesh['dp'=8,'seq'=4] {'dp','seq'}, dimensions={0}, use_global_device_ids=true | all-gather | bytes 540672 | tf_op jit(solution)/shard_map/all_gather | solution.py:172
  174.3 38.8 %all_gather.125 = bf16[512,512]{1,0:T(8,128)(2,1)S(1)} all-gather(bf16[16,512]{1,0:T(8,128)(2,1)S(1)} %copy-done.254), channel_id=1, replica_groups=mesh['dp'=8,'seq'=4] {'dp','seq'}, dimensions={0}, use_global_device_ids=true | all-gather | bytes 540672 | tf_op jit(solution)/shard_map/all_gather | solution.py:171
  214.4 41.9 %all_gather.132 = bf16[512,512]{1,0:T(8,128)(2,1)} all-gather(bf16[16,512]{1,0:T(8,128)(2,1)S(1)} %copy-done.255), channel_id=1, replica_groups=mesh['dp'=8,'seq'=4] {'dp','seq'}, dimensions={0}, use_global_device_ids=true | all-gather | bytes 540672 | tf_op jit(solution)/shard_map/all_gather | solution.py:174
  256.3 42.1 %all_gather.140 = bf16[512,512]{1,0:T(8,128)(2,1)} all-gather(bf16[16,512]{1,0:T(8,128)(2,1)S(1)} %copy-done.256), channel_id=1, replica_groups=mesh['dp'=8,'seq'=4] {'dp','seq'}, dimensions={0}, use_global_device_ids=true | all-gather | bytes 540672 | tf_op jit(solution)/shard_map/all_gather | solution.py:195
  298.4 38.7 %all_gather.142 = bf16[512,512]{1,0:T(8,128)(2,1)S(1)} all-gather(bf16[16,512]{1,0:T(8,128)(2,1)S(1)} %copy-done.257), channel_id=1, replica_groups=mesh['dp'=8,'seq'=4] {'dp','seq'}, dimensions={0}, use_global_device_ids=true | all-gather | bytes 540672 | tf_op jit(solution)/shard_map/all_gather | solution.py:196
  355.1 39.0 %all_gather.136 = bf16[512,512]{1,0:T(8,128)(2,1)S(1)} all-gather(bf16[16,512]{1,0:T(8,128)(2,1)S(1)} %copy-done.258), channel_id=1, replica_groups=mesh['dp'=8,'seq'=4] {'dp','seq'}, dimensions={0}, use_global_device_ids=true | all-gather | bytes 540672 | tf_op jit(solution)/shard_map/all_gather | solution.py:197
  412.1 41.8 %all_gather.147 = bf16[512,512]{1,0:T(8,128)(2,1)} all-gather(bf16[16,512]{1,0:T(8,128)(2,1)S(1)} %copy-done.259), channel_id=1, replica_groups=mesh['dp'=8,'seq'=4] {'dp','seq'}, dimensions={0}, use_global_device_ids=true | all-gather | bytes 540672 | tf_op jit(solution)/shard_map/all_gather | solution.py:198
  506.4 14.6 multiply_convert_fusion
  670.1 26.5 %reduce-scatter.43.cloned.1.call-done = bf16[256,512]{0,1:T(8,128)(2,1)} async-done(((bf16[1024,512]{0,1:T(8,128)(2,1)}), bf16[256,512]{0,1:T(8,128)(2,1)}) %reduce-scatter.43.cloned.1.call-update) | async-done | bytes 262160 | tf_op jit(solution)/shard_map/reduce_scatter | solution.py:540
  699.4 24.7 %reduce-scatter.37.cloned.1.call-done = bf16[256,512]{0,1:T(8,128)(2,1)} async-done(((bf16[1024,512]{0,1:T(8,128)(2,1)}), bf16[256,512]{0,1:T(8,128)(2,1)}) %reduce-scatter.37.cloned.1.call-update) | async-done | bytes 262160 | tf_op jit(solution)/shard_map/reduce_scatter | solution.py:537
  725.1 26.5 %reduce-scatter.39.cloned.1.call-done = bf16[256,512]{0,1:T(8,128)(2,1)} async-done(((bf16[1024,512]{0,1:T(8,128)(2,1)}), bf16[256,512]{0,1:T(8,128)(2,1)}) %reduce-scatter.39.cloned.1.call-update) | async-done | bytes 262160 | tf_op jit(solution)/shard_map/reduce_scatter | solution.py:537
  774.4 40.3 %all-reduce.31 = (f32[512]{0:T(512)S(1)}, f32[512]{0:T(512)S(1)}, f32[512]{0:T(512)S(1)}, f32[512]{0:T(512)S(1)}, f32[512]{0:T(512)S(1)}, /*index=5*/f32[512]{0:...) all-reduce(f32[512]{0:T(512)} %convert_reduce_fusion.7, ...), channel_id=18, replica_groups=mesh['dp'=8,'seq'=4] {'dp','seq'}, use_global_device_ids=true, to_apply=%region_73.74.clone | all-reduce | flops 8704 | bytes 69632
  824.9 64.3 %reduce-scatter.49.cloned.1.call-done = f32[16,512]{1,0:T(8,128)} async-done(((f32[512,512]{1,0:T(8,128)}), f32[16,512]{1,0:T(8,128)}) %reduce-scatter.49.cloned.1.call-update) | async-done | bytes 32784 | tf_op jit(solution)/shard_map/reduce_scatter | solution.py:488
  889.2 133.6 %reduce-scatter.47.cloned.1.call-done = f32[16,512]{1,0:T(8,128)} async-done(((f32[512,512]{1,0:T(8,128)}), f32[16,512]{1,0:T(8,128)}) %reduce-scatter.47.cloned.1.call-update) | async-done | bytes 32784 | tf_op jit(solution)/shard_map/reduce_scatter | solution.py:485
  1022.8 133.4 %reduce-scatter.45.cloned.1.call-done = f32[16,512]{1,0:T(8,128)} async-done(((f32[512,512]{1,0:T(8,128)}), f32[16,512]{1,0:T(8,128)}) %reduce-scatter.45.cloned.1.call-update) | async-done | bytes 32784 | tf_op jit(solution)/shard_map/reduce_scatter | solution.py:575
  1156.2 133.4 %reduce-scatter.63.cloned.1.call-done = f32[16,512]{1,0:T(8,128)} async-done(((f32[512,512]{1,0:T(8,128)}), f32[16,512]{1,0:T(8,128)}) %reduce-scatter.63.cloned.1.call-update) | async-done | bytes 32784
  1289.6 133.6 %reduce-scatter.71.cloned.1.call-done = f32[16,512]{1,0:T(8,128)} async-done(((f32[512,512]{1,0:T(8,128)}), f32[16,512]{1,0:T(8,128)}) %reduce-scatter.71.cloned.1.call-update) | async-done | bytes 32784
  1423.2 133.4 %reduce-scatter.69.cloned.1.call-done = f32[16,512]{1,0:T(8,128)} async-done(((f32[512,512]{1,0:T(8,128)}), f32[16,512]{1,0:T(8,128)}) %reduce-scatter.69.cloned.1.call-update) | async-done | bytes 32784
  1556.6 133.6 %reduce-scatter.67.cloned.1.call-done = f32[16,512]{1,0:T(8,128)} async-done(((f32[512,512]{1,0:T(8,128)}), f32[16,512]{1,0:T(8,128)}) %reduce-scatter.67.cloned.1.call-update) | async-done | bytes 32784
  1690.2 133.6 %reduce-scatter.65.cloned.1.call-done = f32[16,512]{1,0:T(8,128)} async-done(((f32[512,512]{1,0:T(8,128)}), f32[16,512]{1,0:T(8,128)}) %reduce-scatter.65.cloned.1.call-update) | async-done | bytes 32784
  1823.8 139.9 %reduce-scatter.51.cloned.1.call-done = f32[16,2048]{1,0:T(8,128)} async-done(((f32[512,2048]{1,0:T(8,128)}), f32[16,2048]{1,0:T(8,128)}) %reduce-scatter.51.cloned.1.call-update) | async-done | bytes 131088 | tf_op jit(solution)/shard_map/reduce_scatter | solution.py:402
  1963.7 139.4 %reduce-scatter.53.cloned.1.call-done = f32[64,512]{1,0:T(8,128)} async-done(((f32[2048,512]{1,0:T(8,128)}), f32[64,512]{1,0:T(8,128)}) %reduce-scatter.53.cloned.1.call-update) | async-done | bytes 131088 | tf_op jit(solution)/shard_map/reduce_scatter | solution.py:404
  (1000 shorter events, 315.6 us)
Async XLA Ops:
  7.2 446.6 %all-gather.11.cloned.1.call-start = ((), (), s32[]{:S(2)}) async-start(), calls=%async_computation.18 | async-start | bytes 1310720 | tf_op jit(solution)/shard_map/all_gather | solution.py:285
  106.6 349.4 %all-gather.15.cloned.1.call-start = ((), (), s32[]{:S(2)}) async-start(), calls=%async_computation.20 | async-start | bytes 1310720 | tf_op jit(solution)/shard_map/all_gather | solution.py:285
  107.3 355.2 %all-gather.13.cloned.1.call-start = ((), (), s32[]{:S(2)}) async-start(), calls=%async_computation.19 | async-start | bytes 1310720 | tf_op jit(solution)/shard_map/all_gather | solution.py:284
  147.9 316.8 %all-gather.17.cloned.1.call-start = ((), (), s32[]{:S(2)}) async-start(), calls=%async_computation.21 | async-start | bytes 1310720 | tf_op jit(solution)/shard_map/all_gather | solution.py:284
  148.4 358.0 %all-gather.19.cloned.1.call-start = ((), (), s32[]{:S(2)}) async-start(), calls=%async_computation.22 | async-start | bytes 2162688 | tf_op jit(solution)/shard_map/all_gather | solution.py:209
  149.0 372.0 %all-gather.21.cloned.1.call-start = ((), (), s32[]{:S(2)}) async-start(), calls=%async_computation.23 | async-start | bytes 2162688 | tf_op jit(solution)/shard_map/all_gather | solution.py:211
  149.6 501.3 %reduce-scatter.61.cloned.1.call-start = ((), (), s32[]{:S(2)}) async-start(), calls=%async_computation.36 | async-start | bytes 327680
  556.8 95.2 %reduce-scatter.59.cloned.1.call-start = ((), (), s32[]{:S(2)}) async-start(), calls=%async_computation.35 | async-start | bytes 327680
  572.5 82.1 %reduce-scatter.55.cloned.1.call-start = ((), (), s32[]{:S(2)}) async-start(), calls=%async_computation.33 | async-start | bytes 327680
  579.0 76.7 %reduce-scatter.57.cloned.1.call-start = ((), (), s32[]{:S(2)}) async-start(), calls=%async_computation.34 | async-start | bytes 327680
  585.1 84.0 %reduce-scatter.41.cloned.1.call-start = ((), (), s32[]{:S(2)}) async-start(), calls=%async_computation.26 | async-start | bytes 1310720 | tf_op jit(solution)/shard_map/reduce_scatter | solution.py:540
  597.0 99.7 %reduce-scatter.43.cloned.1.call-start = ((), (), s32[]{:S(2)}) async-start(), calls=%async_computation.27 | async-start | bytes 1310720 | tf_op jit(solution)/shard_map/reduce_scatter | solution.py:540
  612.2 111.9 %reduce-scatter.37.cloned.1.call-start = ((), (), s32[]{:S(2)}) async-start(), calls=%async_computation.24 | async-start | bytes 1310720 | tf_op jit(solution)/shard_map/reduce_scatter | solution.py:537
  625.5 126.1 %reduce-scatter.39.cloned.1.call-start = ((), (), s32[]{:S(2)}) async-start(), calls=%async_computation.25 | async-start | bytes 1310720 | tf_op jit(solution)/shard_map/reduce_scatter | solution.py:537
  634.6 254.6 %reduce-scatter.49.cloned.1.call-start = ((), (), s32[]{:S(2)}) async-start(), calls=%async_computation.30 | async-start | bytes 1081344 | tf_op jit(solution)/shard_map/reduce_scatter | solution.py:488
  637.3 385.5 %reduce-scatter.47.cloned.1.call-start = ((), (), s32[]{:S(2)}) async-start(), calls=%async_computation.29 | async-start | bytes 1081344 | tf_op jit(solution)/shard_map/reduce_scatter | solution.py:485
  640.2 516.0 %reduce-scatter.45.cloned.1.call-start = ((), (), s32[]{:S(2)}) async-start(), calls=%async_computation.28 | async-start | bytes 1081344 | tf_op jit(solution)/shard_map/reduce_scatter | solution.py:575
  642.8 646.9 %reduce-scatter.63.cloned.1.call-start = ((), (), s32[]{:S(2)}) async-start(), calls=%async_computation.37 | async-start | bytes 1081344
  650.9 772.3 %reduce-scatter.71.cloned.1.call-start = ((), (), s32[]{:S(2)}) async-start(), calls=%async_computation.41 | async-start | bytes 1081344
  654.6 902.0 %reduce-scatter.69.cloned.1.call-start = ((), (), s32[]{:S(2)}) async-start(), calls=%async_computation.40 | async-start | bytes 1081344
  658.4 1031.8 %reduce-scatter.67.cloned.1.call-start = ((), (), s32[]{:S(2)}) async-start(), calls=%async_computation.39 | async-start | bytes 1081344
  699.4 1124.4 %reduce-scatter.65.cloned.1.call-start = ((), (), s32[]{:S(2)}) async-start(), calls=%async_computation.38 | async-start | bytes 1081344
  754.4 1209.3 %reduce-scatter.51.cloned.1.call-start = ((), (), s32[]{:S(2)}) async-start(), calls=%async_computation.31 | async-start | bytes 4325376 | tf_op jit(solution)/shard_map/reduce_scatter | solution.py:402
  759.5 1343.6 %reduce-scatter.53.cloned.1.call-start = ((), (), s32[]{:S(2)}) async-start(), calls=%async_computation.32 | async-start | bytes 4325376 | tf_op jit(solution)/shard_map/reduce_scatter | solution.py:404
  (299 other events, 2218.4 us)
Sparse Core Ops, SparseCore 0:
  106.6 13.7 all-gather.10
  122.6 17.8 all-gather.14
  148.0 14.2 all-gather.12
  163.7 17.0 all-gather.16
  183.5 58.0 all-gather.18
  244.3 55.4 all-gather.20
  556.9 16.9 reduce-scatter.60
  576.5 20.0 reduce-scatter.58
  599.0 20.0 reduce-scatter.54
  621.5 20.0 reduce-scatter.56
  644.2 24.9 reduce-scatter.40
  671.7 24.9 reduce-scatter.42
  699.2 24.8 reduce-scatter.36
  726.6 24.9 reduce-scatter.38
  754.3 134.8 reduce-scatter.48
  891.9 130.8 reduce-scatter.46
  1025.5 130.7 reduce-scatter.44
  1159.0 130.6 reduce-scatter.62
  1292.4 130.7 reduce-scatter.70
  1426.0 130.6 reduce-scatter.68
  1559.4 130.7 reduce-scatter.66
  1693.1 130.6 reduce-scatter.64
  1826.6 137.0 reduce-scatter.50
  1966.4 136.6 reduce-scatter.52
where the time goes:
time: 2120 us; the launch traced here: 2110 us
  waiting for transfers between devices  1370 us (65%)
  blocking collectives  444 us (21%)
  matrix products  136 us (6%)
  local copies, waits for them, and re-layouts  84.8 us (4%)
  other arithmetic  55.7 us (3%)
    unnamed x33, waiting for transfers between devices  670 us
    reduce_scatter x1, waiting for transfers between devices, per_device(): lax.psum_scatter(inner_weight_grad, ('dp', 'seq'), scatter_dimension=0, t...  140 us
    reduce_scatter x1, waiting for transfers between devices, per_device(): lax.psum_scatter(outer_weight_grad, ('dp', 'seq'), scatter_dimension=0, t...  139 us
    reduce_scatter x1, waiting for transfers between devices, per_device(): lax.psum_scatter(source_query_grad, ('dp', 'seq'), scatter_dimension=0, t...  134 us
    reduce_scatter x1, waiting for transfers between devices, per_device(): lax.psum_scatter(output_weight_grad, ('dp', 'seq'), scatter_dimension=0,...  133 us
    unnamed x3, blocking collectives  87.7 us
    reduce_scatter x1, waiting for transfers between devices, per_device(): lax.psum_scatter(source_output_grad, ('dp', 'seq'), scatter_dimension=0,...  64.3 us
    unnamed x661, local copies, waits for them, and re-layouts  54.2 us
  transfers between devices with their start and end apart: 24, of which 14 were waited for; matrix products, arithmetic and copies ran while one was open for 10% of the time, Pallas kernels for 0%

commit v1 on v0

v1 whole, which is shorter than its diff:
```python
import functools
import math

import jax
import jax.numpy as jnp
from jax import lax
from jax.experimental import pallas as pl
from jax.experimental.pallas import tpu as pltpu
from jax.sharding import PartitionSpec as P

HEADS = 8
HEAD_DIM = 64
PAIR = 128
EPSILON = 1e-05
MASKED = 1e9
AXES = ("dp", "seq")
F32 = jnp.float32
BF16 = jnp.bfloat16

(
    QUERY_BIAS,
    VALUE_BIAS,
    OUTPUT_BIAS,
    ATTENTION_GAIN,
    ATTENTION_SHIFT,
    SOURCE_QUERY_BIAS,
    SOURCE_VALUE_BIAS,
    SOURCE_OUTPUT_BIAS,
    SOURCE_GAIN,
    SOURCE_SHIFT,
    OUTER_BIAS,
    FINAL_GAIN,
    FINAL_SHIFT,
    INNER_BIAS,
) = range(14)


def dot(a, b):
    return lax.dot_general(a, b, (((1,), (0,)), ((), ())), preferred_element_type=F32)


def dot_nt(a, b):
    return lax.dot_general(a, b, (((1,), (1,)), ((), ())), preferred_element_type=F32)


def dot_tn(a, b):
    return lax.dot_general(a, b, (((0,), (0,)), ((), ())), preferred_element_type=F32)


def total(values):
    return jnp.sum(values.astype(F32), axis=0, keepdims=True)


def normalize(h):
    average = jnp.mean(h, axis=-1, keepdims=True)
    centered = h - average
    variance = jnp.mean(centered * centered, axis=-1, keepdims=True)
    inverse = lax.rsqrt(variance + EPSILON)
    return centered * inverse, inverse


def normalize_back(upstream, normed, inverse, gain):
    scaled = upstream * gain
    first_mean = jnp.mean(scaled, axis=-1, keepdims=True)
    second_mean = jnp.mean(scaled * normed, axis=-1, keepdims=True)
    return inverse * (scaled - first_mean - normed * second_mean)


def normal_parts(v):
    density = 0.3989422804014327 * jnp.exp(-0.5 * v * v)
    t = 1.0 / (1.0 + 0.2316419 * jnp.abs(v))
    series = t * (
        0.319381530
        + t * (-0.356563782 + t * (1.781477937 + t * (-1.821255978 + t * 1.330274429)))
    )
    tail = density * series
    return jnp.where(v >= 0.0, 1.0 - tail, tail), density


class Layout:
    def __init__(self, devices):
        self.devices = devices
        bits = devices.bit_length() - 1
        rest = list(range(1, bits))
        self.groups = [[0]] + [rest[i : i + 2] for i in range(0, len(rest), 2)]
        self.packed = devices == 32

    def masks(self, group):
        found = [0]
        for bit in group:
            found = found + [m | (1 << bit) for m in found]
        return found


def swap(array, mask, devices):
    return lax.ppermute(array, AXES, [(i, i ^ mask) for i in range(devices)])


def unpack(me, pieces, layout, stride, first, rows, put):
    low, mid, high = (layout.masks(g) for g in layout.groups)
    for a, outer in enumerate(mid):
        for b, core in enumerate(low):
            ref = pieces[a * len(low) + b]
            for c, inner in enumerate(high):
                device = me ^ (outer | core | inner)
                put(device, ref[c * stride + first : c * stride + first + rows, :])


def weight(me, pieces, layout, stride, first, rows, scratch):
    def put(device, values):
        scratch[pl.ds(pl.multiple_of(device * rows, rows), rows), :] = values

    unpack(me, pieces, layout, stride, first, rows, put)


def pack(me, layout, rows, get, keep, send, first):
    low, mid, high = (layout.masks(g) for g in layout.groups)
    for a, outer in enumerate(mid):
        for c, inner in enumerate(high):
            slot = a * len(high) + c
            for core, ref in zip(low, (keep, send)):
                device = me ^ (outer | inner | core)
                ref[slot, first : first + rows, :] = get(device).astype(ref.dtype)


def segment_masks(ids):
    place = lax.broadcasted_iota(jnp.int32, (PAIR, ids.shape[1]), 0)
    same = place == ids
    hot = jnp.where(same, 1.0, 0.0).astype(F32)
    penalty = jnp.where(same | (place >= 4), 0.0, -MASKED)
    return hot.T.astype(BF16), penalty


def penalties(ids):
    place = lax.broadcasted_iota(jnp.int32, (PAIR, ids.shape[1]), 0)
    return jnp.where((place == ids) | (place >= 4), 0.0, -MASKED).astype(BF16)


def one_hot(ids):
    place = lax.broadcasted_iota(jnp.int32, (PAIR, ids.shape[1]), 0)
    return jnp.where(place == ids, 1.0, 0.0).astype(F32).T.astype(BF16)


def spread(part, half):
    empty = jnp.zeros_like(part)
    return [part, empty] if half == 0 else [empty, part]


def attend(query_t, keys, value_t, hot, penalty, mixture_t, logs):
    length = keys.shape[0]

    def pair(p, carry):
        columns = pl.ds(pl.multiple_of(p * PAIR, PAIR), PAIR)
        left = jnp.concatenate([keys[:, columns], hot[...]], axis=1)
        for half in range(2):
            rows = pl.ds(pl.multiple_of(p * PAIR + half * HEAD_DIM, HEAD_DIM), HEAD_DIM)
            right = jnp.concatenate(spread(query_t[rows, :], half) + [penalty[...]], axis=0)
            scores = dot(left, right)
            highest = jnp.max(scores, axis=0, keepdims=True)
            weights = jnp.exp(scores - highest).astype(BF16)
            values = jnp.concatenate(
                [value_t[rows, :], jnp.ones((16, length), BF16)], axis=0
            )
            found = dot(values, weights)
            denominator = found[HEAD_DIM : HEAD_DIM + 1, :]
            mixture_t[rows, :] = (found[:HEAD_DIM, :] / denominator).astype(BF16)
            logs[2 * p + half] = highest + jnp.log(denominator)
        return carry

    lax.fori_loop(0, HEADS // 2, pair, 0)


def attend_back(
    query_t, query, keys, key_t, values, slope_t, slope, hot, penalty, logs, deltas,
    query_grad_t, key_grad, value_grad,
):
    tokens = query.shape[0]
    lane = lax.broadcasted_iota(jnp.int32, (tokens, PAIR), 1)

    def pair(p, carry):
        columns = pl.ds(pl.multiple_of(p * PAIR, PAIR), PAIR)
        left = jnp.concatenate([keys[:, columns], hot[...]], axis=1)
        value_pair = values[:, columns]
        key_sum, value_sum = None, None
        for half in range(2):
            rows = pl.ds(pl.multiple_of(p * PAIR + half * HEAD_DIM, HEAD_DIM), HEAD_DIM)
            right = jnp.concatenate(spread(query_t[rows, :], half) + [penalty[...]], axis=0)
            chances = jnp.exp(dot(left, right) - logs[2 * p + half])
            slopes = dot(value_pair, jnp.concatenate(spread(slope_t[rows, :], half), axis=0))
            grads = (chances * (slopes - deltas[2 * p + half])).astype(BF16)
            query_grad_t[rows, :] = dot(key_t[rows, :], grads) * HEAD_DIM**-0.5
            mine = (lane < HEAD_DIM) if half == 0 else (lane >= HEAD_DIM)
            none = jnp.zeros((tokens, PAIR), BF16)
            value_part = dot(chances.astype(BF16), jnp.where(mine, slope[:, columns], none))
            key_part = dot(grads, jnp.where(mine, query[:, columns], none))
            value_sum = value_part if value_sum is None else value_sum + value_part
            key_sum = key_part if key_sum is None else key_sum + key_part
        key_grad[:, columns] = key_sum
        value_grad[:, columns] = value_sum
        return carry

    lax.fori_loop(0, HEADS // 2, pair, 0)


def deltas_of(slope_t, mixture_t, deltas):
    for head in range(HEADS):
        rows = slice(head * HEAD_DIM, (head + 1) * HEAD_DIM)
        deltas[head] = jnp.sum(
            slope_t[rows, :].astype(F32) * mixture_t[rows, :].astype(F32), axis=0, keepdims=True
        )


VM = pl.BlockSpec(memory_space=pltpu.VMEM)
SM = pl.BlockSpec(memory_space=pltpu.SMEM)


def call(kernel, outs, args, scratch, flops, name):
    moved = sum(math.prod(a.shape) * a.dtype.itemsize for a in args[1:])
    moved += sum(math.prod(s) * jnp.dtype(d).itemsize for s, d in outs)
    return pl.pallas_call(
        kernel,
        out_shape=[jax.ShapeDtypeStruct(s, d) for s, d in outs],
        in_specs=[SM] + [VM] * (len(args) - 1),
        out_specs=[VM] * len(outs),
        scratch_shapes=[pltpu.VMEM(s, d) for s, d in scratch],
        compiler_params=pltpu.CompilerParams(vmem_limit_bytes=56 << 20),
        cost_estimate=pl.CostEstimate(flops=flops, bytes_accessed=moved, transcendentals=0),
        name=name,
    )(*args)


def weights_from(refs, me, layout, stride, plan, scratch):
    if not layout.packed:
        return list(refs)
    for (first, rows), ref in zip(plan, scratch):
        weight(me, refs, layout, stride, first, rows, ref)
    return list(scratch)


def self_forward(me, layout, pieces, stride, tokens, ids, vectors):
    count = len(tokens)
    share, width = tokens[0].shape[0] - 0, tokens[0].shape[1]
    return count, share, width


def make_self_forward(layout, parts, share, width, stride, n_pieces):
    length = parts * share

    def kernel(*refs):
        me_ref, refs = refs[0], list(refs[1:])
        pieces, refs = refs[:n_pieces], refs[n_pieces:]
        tokens, refs = refs[:parts], refs[parts:]
        ids, vectors, query, keys, values, mixture_t, logs = refs[:7]
        scratch = refs[7:]
        query_t, value_t, hot, penalty = scratch[:4]
        me = me_ref[0]
        rows = width // layout.devices
        plan = [(i * rows, rows) for i in range(3)]
        query_w, key_w, value_w = weights_from(pieces, me, layout, stride, plan, scratch[4:])
        scaled = (dot(tokens[0][:share, :], query_w[...]) + vectors[QUERY_BIAS : QUERY_BIAS + 1, :]).astype(BF16) * BF16(HEAD_DIM**-0.5)
        query[...] = scaled
        query_t[...] = scaled.T
        for i in range(parts):
            here = slice(i * share, (i + 1) * share)
            keys[here, :] = dot(tokens[i][:share, :], key_w[...]).astype(BF16)
            found = (dot(tokens[i][:share, :], value_w[...]) + vectors[VALUE_BIAS : VALUE_BIAS + 1, :]).astype(BF16)
            values[here, :] = found
            value_t[:, here] = found.T
        hot[...] = one_hot(ids[...])
        penalty[...] = penalties(ids[:, :share])
        attend(query_t, keys, value_t, hot, penalty, mixture_t, logs)

    outs = [
        ((share, width), BF16),
        ((length, width), BF16),
        ((length, width), BF16),
        ((width, share), BF16),
        ((HEADS, 1, share), F32),
    ]
    scratch = [((width, share), BF16), ((width, length), BF16), ((length, PAIR), BF16), ((PAIR, share), BF16)]
    if layout.packed:
        scratch += [((width, width), BF16)] * 3
    flops = 2 * share * width * width + 4 * length * width * width + 4 * share * length * width
    return kernel, outs, scratch, flops


def make_cross_forward(layout, parts, share, memory_share, width, stride, n_pieces):
    memory_length = parts * memory_share

    def kernel(*refs):
        me_ref, refs = refs[0], list(refs[1:])
        pieces, refs = refs[:n_pieces], refs[n_pieces:]
        tokens, refs = refs[:parts], refs[parts:]
        ids, memory_ids, vectors, mixture_t = refs[:4]
        first_sum, second_sum, query, memory_keys, memory_values, cross_t, logs = refs[4:11]
        scratch = refs[11:]
        query_t, value_t, hot, penalty = scratch[:4]
        me = me_ref[0]
        rows = width // layout.devices
        plan = [(i * rows, rows) for i in range(5)]
        output_w, query_w, key_w, value_w, source_w = weights_from(
            pieces, me, layout, stride, plan, scratch[4:]
        )

        def vector(i):
            return vectors[i : i + 1, :]

        h = tokens[0][:share, :].astype(F32) + dot_tn(mixture_t[...], output_w[...]) + vector(OUTPUT_BIAS)
        first_sum[...] = h
        first = normalize(h)[0] * vector(ATTENTION_GAIN) + vector(ATTENTION_SHIFT)
        scaled = (dot(first.astype(BF16), query_w[...]) + vector(SOURCE_QUERY_BIAS)).astype(BF16) * BF16(HEAD_DIM**-0.5)
        query[...] = scaled
        query_t[...] = scaled.T
        for i in range(parts):
            here = slice(i * memory_share, (i + 1) * memory_share)
            memory = tokens[i][share:, :]
            memory_keys[here, :] = dot(memory, key_w[...]).astype(BF16)
            memory_values[here, :] = (dot(memory, value_w[...]) + vector(SOURCE_VALUE_BIAS)).astype(BF16)
        value_t[...] = memory_values[...].T
        hot[...] = one_hot(memory_ids[...])
        penalty[...] = penalties(ids[:, :share])
        attend(query_t, memory_keys, value_t, hot, penalty, cross_t, logs)
        first = normalize(first_sum[...])[0] * vector(ATTENTION_GAIN) + vector(ATTENTION_SHIFT)
        second_sum[...] = first + dot_tn(cross_t[...], source_w[...]) + vector(SOURCE_OUTPUT_BIAS)

    outs = [
        ((share, width), F32),
        ((share, width), F32),
        ((share, width), BF16),
        ((memory_length, width), BF16),
        ((memory_length, width), BF16),
        ((width, share), BF16),
        ((HEADS, 1, share), F32),
    ]
    scratch = [((width, share), BF16), ((width, memory_length), BF16), ((memory_length, PAIR), BF16), ((PAIR, share), BF16)]
    if layout.packed:
        scratch += [((width, width), BF16)] * 5
    flops = 6 * share * width * width + 4 * memory_length * width * width + 4 * share * memory_length * width
    return kernel, outs, scratch, flops


def grad_outs(layout, rows, width, natural):
    if layout.packed:
        slots = layout.devices // 2
        return [((slots, rows, width), BF16)] * 2
    return [(s, F32) for s in natural]


def make_inner(layout, share, width, hidden, stride, n_pieces):
    blocks = hidden // width
    half = share // 2

    def kernel(*refs):
        me_ref, refs = refs[0], list(refs[1:])
        pieces, refs = refs[:n_pieces], refs[n_pieces:]
        second_sum, cotangent, vectors = refs[:3]
        out_own, out_send, back, sums = refs[3:7]
        grads, scratch = refs[7:9], refs[9:]
        low, active, gate, slope = scratch[:4]
        me = me_ref[0]
        rows = width // layout.devices
        if layout.packed:
            inner_w, outer_w, gathered = scratch[4:7]

            for block in range(blocks):
                def put(device, values, block=block):
                    inner_w[block, pl.ds(pl.multiple_of(device * rows, rows), rows), :] = values

                unpack(me, pieces, layout, stride, block * rows, rows, put)

            def put_outer(device, values):
                per = width // (blocks * rows)
                inner_w_row = pl.multiple_of((device % per) * blocks * rows, blocks * rows)
                outer_w[device // per, pl.ds(inner_w_row, blocks * rows), :] = values

            unpack(me, pieces, layout, stride, blocks * rows, blocks * rows, put_outer)
        else:
            inner_w, outer_w = pieces

        def vector(i):
            return vectors[i : i + 1, :]

        second = normalize(second_sum[...])[0] * vector(SOURCE_GAIN) + vector(SOURCE_SHIFT)
        low[...] = second.astype(BF16)
        back[...] = second + vector(OUTER_BIAS)

        def forward(block, carry):
            inner = dot(low[...], inner_w[block]) + vectors[pl.ds(INNER_BIAS + block, 1), :]
            chance, density = normal_parts(inner)
            found = (inner * chance).astype(BF16)
            active[block] = found
            gate[block] = chance + inner * density
            back[...] += dot(found, outer_w[block])
            return carry

        lax.fori_loop(0, blocks, forward, 0)
        normed, inverse = normalize(back[...])
        final = normed * vector(FINAL_GAIN) + vector(FINAL_SHIFT)
        out_own[...] = final[:half, :]
        out_send[...] = final[half:, :].astype(BF16)
        upstream = cotangent[...].astype(F32)
        sums[0:1, :] = total(upstream * normed)
        sums[1:2, :] = total(upstream)
        back3 = normalize_back(upstream, normed, inverse, vector(FINAL_GAIN))
        slope[...] = back3.astype(BF16)
        sums[2:3, :] = total(slope[...])
        sums[7:8, :] = jnp.zeros_like(sums[7:8, :])
        back[...] = back3

        def backward(block, carry):
            grad = dot_nt(slope[...], outer_w[block]) * gate[block]
            inner_low = grad.astype(BF16)
            sums[pl.ds(3 + block, 1), :] = total(inner_low)
            outer_grad = dot_tn(active[block], slope[...])
            inner_grad = dot_tn(low[...], inner_low)
            back[...] += dot_nt(inner_low, inner_w[block])
            if layout.packed:
                gathered[block] = inner_grad
                gathered[blocks + block] = outer_grad
            else:
                grads[0][block] = inner_grad
                grads[1][block] = outer_grad
            return carry

        lax.fori_loop(0, blocks, backward, 0)
        if layout.packed:
            keep, send = grads
            for block in range(blocks):
                def get(device, block=block):
                    return gathered[block, pl.ds(pl.multiple_of(device * rows, rows), rows), :]

                pack(me, layout, rows, get, keep, send, block * rows)

            def get_outer(device):
                per = width // (blocks * rows)
                row = pl.multiple_of((device % per) * blocks * rows, blocks * rows)
                return gathered[blocks + device // per, pl.ds(row, blocks * rows), :]

            pack(me, layout, blocks * rows, get_outer, keep, send, blocks * rows)

    outs = [((half, width), F32), ((half, width), BF16), ((share, width), F32), ((8, width), F32)]
    outs += grad_outs(layout, 2 * blocks * (width // layout.devices), width, [(blocks, width, width)] * 2)
    scratch = [((share, width), BF16), ((blocks, share, width), BF16), ((blocks, share, width), F32), ((share, width), BF16)]
    if layout.packed:
        scratch += [((blocks, width, width), BF16)] * 2 + [((2 * blocks, width, width), F32)]
    return kernel, outs, scratch, 12 * share * width * hidden


def make_cross_back(layout, parts, share, memory_share, width, stride, n_pieces):
    memory_length = parts * memory_share

    def kernel(*refs):
        me_ref, refs = refs[0], list(refs[1:])
        pieces, refs = refs[:n_pieces], refs[n_pieces:]
        (back2_in, first_sum, second_sum, query, memory_keys, memory_values, cross_t, logs, ids,
         memory_ids, mixture_t, vectors) = refs[:12]
        refs = refs[12:]
        back1, self_slope, self_slope_t, self_deltas, sums, key_own, value_own = refs[:7]
        sends, refs = refs[7 : 7 + parts - 1], refs[7 + parts - 1 :]
        n_grads = 2 if layout.packed else 3
        grads, scratch = refs[:n_grads], refs[n_grads:]
        (slope_t, slope, key_t, hot, penalty, query_t, deltas, query_grad_t, key_grad, value_grad) = scratch[:10]
        me = me_ref[0]
        rows = width // layout.devices
        if layout.packed:
            plan = [(0, rows), (rows, rows), (4 * rows, rows)]
            output_w, query_w, source_w = weights_from(pieces, me, layout, stride, plan, scratch[10:13])
            dense = scratch[13]
        else:
            output_w, query_w, source_w = pieces

        def vector(i):
            return vectors[i : i + 1, :]

        def give(index, grad):
            if layout.packed:
                dense[...] = grad

                def get(device):
                    return dense[pl.ds(pl.multiple_of(device * rows, rows), rows), :]

                pack(me, layout, rows, get, grads[0], grads[1], index * rows)
            else:
                grads[index][...] = grad

        upstream = back2_in[...]
        normed, inverse = normalize(second_sum[...])
        sums[0:1, :] = total(upstream * normed)
        sums[1:2, :] = total(upstream)
        back2 = normalize_back(upstream, normed, inverse, vector(SOURCE_GAIN))
        back1[...] = back2
        cross_low = back2.astype(BF16)
        sums[2:3, :] = total(cross_low)
        give(0, dot(cross_t[...], cross_low))
        found = dot_nt(cross_low, source_w[...]).astype(BF16)
        slope[...] = found
        slope_t[...] = found.T
        deltas_of(slope_t, cross_t, deltas)
        query_t[...] = query[...].T
        key_t[...] = memory_keys[...].T
        hot[...] = one_hot(memory_ids[...])
        penalty[...] = penalties(ids[:, :share])
        attend_back(query_t, query, memory_keys, key_t, memory_values, slope_t, slope, hot, penalty,
                    logs, deltas, query_grad_t, key_grad, value_grad)
        key_own[...] = key_grad[:memory_share, :]
        value_own[...] = value_grad[:memory_share, :]
        for i in range(1, parts):
            here = slice(i * memory_share, (i + 1) * memory_share)
            sends[i - 1][:memory_share, :] = key_grad[here, :].astype(BF16)
            sends[i - 1][memory_share:, :] = value_grad[here, :].astype(BF16)
        query_low = query_grad_t[...].T.astype(BF16)
        sums[3:4, :] = total(query_low)
        normed, inverse = normalize(first_sum[...])
        first_low = (normed * vector(ATTENTION_GAIN) + vector(ATTENTION_SHIFT)).astype(BF16)
        give(1, dot_tn(first_low, query_low))
        upstream = back1[...] + dot_nt(query_low, query_w[...])
        sums[4:5, :] = total(upstream * normed)
        sums[5:6, :] = total(upstream)
        grad = normalize_back(upstream, normed, inverse, vector(ATTENTION_GAIN))
        back1[...] = grad
        branch_low = grad.astype(BF16)
        sums[6:7, :] = total(branch_low)
        sums[7:8, :] = jnp.zeros_like(sums[7:8, :])
        give(2, dot(mixture_t[...], branch_low))
        found = dot_nt(branch_low, output_w[...]).astype(BF16)
        self_slope[...] = found
        self_slope_t[...] = found.T
        deltas_of(self_slope_t, mixture_t, self_deltas)

    outs = [
        ((share, width), F32),
        ((share, width), BF16),
        ((width, share), BF16),
        ((HEADS, 1, share), F32),
        ((8, width), F32),
        ((memory_share, width), F32),
        ((memory_share, width), F32),
    ]
    outs += [((2 * memory_share, width), BF16)] * (parts - 1)
    outs += grad_outs(layout, 3 * (width // layout.devices), width, [(width, width)] * 3)
    scratch = [
        ((width, share), BF16),
        ((share, width), BF16),
        ((width, memory_length), BF16),
        ((memory_length, PAIR), BF16),
        ((PAIR, share), BF16),
        ((width, share), BF16),
        ((HEADS, 1, share), F32),
        ((width, share), F32),
        ((memory_length, width), F32),
        ((memory_length, width), F32),
    ]
    if layout.packed:
        scratch += [((width, width), BF16)] * 3 + [((width, width), F32)]
    flops = 14 * share * width * width + 10 * share * memory_length * width
    return kernel, outs, scratch, flops


def make_self_back(layout, parts, share, width):
    length = parts * share

    def kernel(*refs):
        query, keys, values, slope, slope_t, logs, deltas, ids = refs[1:9]
        query_low, key_own, value_own = refs[9:12]
        sends, scratch = refs[12 : 12 + parts - 1], refs[12 + parts - 1 :]
        query_t, key_t, hot, penalty, query_grad_t, key_grad, value_grad = scratch
        query_t[...] = query[...].T
        key_t[...] = keys[...].T
        hot[...] = one_hot(ids[...])
        penalty[...] = penalties(ids[:, :share])
        attend_back(query_t, query, keys, key_t, values, slope_t, slope, hot, penalty, logs, deltas,
                    query_grad_t, key_grad, value_grad)
        query_low[...] = query_grad_t[...].T.astype(BF16)
        key_own[...] = key_grad[:share, :]
        value_own[...] = value_grad[:share, :]
        for i in range(1, parts):
            here = slice(i * share, (i + 1) * share)
            sends[i - 1][:share, :] = key_grad[here, :].astype(BF16)
            sends[i - 1][share:, :] = value_grad[here, :].astype(BF16)

    outs = [((share, width), BF16), ((share, width), F32), ((share, width), F32)]
    outs += [((2 * share, width), BF16)] * (parts - 1)
    scratch = [
        ((width, share), BF16),
        ((width, length), BF16),
        ((length, PAIR), BF16),
        ((PAIR, share), BF16),
        ((width, share), F32),
        ((length, width), F32),
        ((length, width), F32),
    ]
    return kernel, outs, scratch, 10 * share * length * width


def make_last(layout, parts, share, memory_share, width, strides, n_pieces):
    half, memory_half = share // 2, memory_share // 2

    def kernel(*refs):
        me_ref, refs = refs[0], list(refs[1:])
        pieces, refs = refs[:n_pieces], refs[n_pieces:]
        others, refs = refs[:n_pieces] if layout.packed else refs[:2], refs[n_pieces if layout.packed else 2 :]
        tokens, back1, query_low, key_own, value_own, memory_key_own, memory_value_own = refs[:7]
        refs = refs[7:]
        received, refs = refs[: parts - 1], refs[parts - 1 :]
        memory_received, refs = refs[: parts - 1], refs[parts - 1 :]
        in_own, in_send, memory_own, memory_send, sums = refs[:5]
        n_grads = 2 if layout.packed else 5
        grads, scratch = refs[5 : 5 + n_grads], refs[5 + n_grads :]
        me = me_ref[0]
        rows = width // layout.devices
        if layout.packed:
            query_w, key_w, value_w = weights_from(pieces, me, layout, strides[0], [(i * rows, rows) for i in range(3)], scratch[:3])
            source_key, source_value = weights_from(others, me, layout, strides[1], [(2 * rows, rows), (3 * rows, rows)], scratch[3:5])
            dense = scratch[5]
        else:
            query_w, key_w, value_w = pieces
            source_key, source_value = others

        def give(index, grad):
            if layout.packed:
                dense[...] = grad

                def get(device):
                    return dense[pl.ds(pl.multiple_of(device * rows, rows), rows), :]

                pack(me, layout, rows, get, grads[0], grads[1], index * rows)
            else:
                grads[index][...] = grad

        memory = tokens[share:, :]
        key_sum, value_sum = memory_key_own[...], memory_value_own[...]
        for ref in memory_received:
            key_sum = key_sum + ref[:memory_share, :].astype(F32)
            value_sum = value_sum + ref[memory_share:, :].astype(F32)
        key_low, value_low = key_sum.astype(BF16), value_sum.astype(BF16)
        sums[2:3, :] = total(value_low)
        give(3, dot_tn(memory, key_low))
        give(4, dot_tn(memory, value_low))
        grad = dot_nt(key_low, source_key[...]) + dot_nt(value_low, source_value[...])
        memory_own[...] = grad[:memory_half, :]
        memory_send[...] = grad[memory_half:, :].astype(BF16)
        own = tokens[:share, :]
        key_sum, value_sum = key_own[...], value_own[...]
        for ref in received:
            key_sum = key_sum + ref[:share, :].astype(F32)
            value_sum = value_sum + ref[share:, :].astype(F32)
        key_low, value_low = key_sum.astype(BF16), value_sum.astype(BF16)
        sums[0:1, :] = total(query_low[...])
        sums[1:2, :] = total(value_low)
        sums[3:8, :] = jnp.zeros_like(sums[3:8, :])
        give(0, dot_tn(own, query_low[...]))
        give(1, dot_tn(own, key_low))
        give(2, dot_tn(own, value_low))
        grad = back1[...] + dot_nt(query_low[...], query_w[...]) + dot_nt(key_low, key_w[...]) + dot_nt(value_low, value_w[...])
        in_own[...] = grad[:half, :]
        in_send[...] = grad[half:, :].astype(BF16)

    outs = [
        ((half, width), F32),
        ((half, width), BF16),
        ((memory_half, width), F32),
        ((memory_half, width), BF16),
        ((8, width), F32),
    ]
    outs += grad_outs(layout, 5 * (width // layout.devices), width, [(width, width)] * 5)
    scratch = []
    if layout.packed:
        scratch = [((width, width), BF16)] * 5 + [((width, width), F32)]
    flops = 12 * share * width * width + 8 * memory_share * width * width
    return kernel, outs, scratch, flops


def combine(arrays, splits, out_dtype):
    count = arrays[0].shape[0] // splits
    shape = (count,) + arrays[0].shape[1:]

    def kernel(*refs):
        given, outs = refs[: len(arrays)], refs[len(arrays) :]
        for i, out in enumerate(outs):
            here = slice(i * count, (i + 1) * count)
            found = given[0][here].astype(F32)
            for ref in given[1:]:
                found = found + ref[here].astype(F32)
            out[...] = found.astype(out.dtype)

    moved = 2 * sum(math.prod(a.shape) * a.dtype.itemsize for a in arrays)
    return pl.pallas_call(
        kernel,
        out_shape=[jax.ShapeDtypeStruct(shape, out_dtype)] * splits,
        in_specs=[VM] * len(arrays),
        out_specs=[VM] * splits,
        compiler_params=pltpu.CompilerParams(vmem_limit_bytes=32 << 20),
        cost_estimate=pl.CostEstimate(flops=0, bytes_accessed=moved, transcendentals=0),
        name="combine",
    )(*arrays)


def gather_tree(block, layout):
    devices = layout.devices
    arrays = [block]
    for group in reversed(layout.groups):
        if group != [0]:
            joined = arrays[0] if len(arrays) == 1 else jnp.concatenate(arrays, axis=0)
            arrays = [joined] + [swap(joined, m, devices) for m in layout.masks(group)[1:]]
        else:
            arrays = [a for array in arrays for a in (array, swap(array, 1, devices))]
    return arrays


def scatter_tree(keep, send, layout):
    devices = layout.devices
    given = [keep, swap(send, 1, devices)]
    for group in layout.groups[1:]:
        masks = layout.masks(group)
        parts = combine(given, len(masks), BF16)
        given = [parts[0]] + [swap(a, m, devices) for a, m in zip(parts[1:], masks[1:])]
    return combine(given, 1, F32)[0]


def reduce_all(array, layout):
    for group in layout.groups[::-1]:
        array = sum([swap(array, m, layout.devices) for m in layout.masks(group)[1:]], array)
    return array


def per_device(
    tokens, memory, target_ids, source_ids, cotangent,
    query_weight, key_weight, value_weight, output_weight, query_bias, value_bias, output_bias,
    attention_gain, attention_shift,
    source_query, source_key, source_value, source_output, source_query_bias, source_value_bias,
    source_output_bias, source_gain, source_shift,
    inner_weight, inner_bias, outer_weight, outer_bias, final_gain, final_shift,
    *, devices, sequence,
):
    layout = Layout(devices)
    row_count, block, width = tokens.shape
    memory_block = memory.shape[1]
    parts = sequence // row_count
    share, memory_share = row_count * block, row_count * memory_block
    hidden = inner_weight.shape[1]
    blocks = hidden // width
    me = lax.axis_index(AXES)
    me_array = me.reshape(1).astype(jnp.int32)
    turn = (me // parts) % row_count
    narrow, wide = width // devices, hidden // devices

    def packet(arrays):
        return gather_tree(jnp.concatenate(arrays, axis=0), layout)

    def whole(array):
        return lax.all_gather(array, AXES, axis=0, tiled=True)

    if layout.packed:
        inner_rows = inner_weight.reshape(narrow, blocks, width).transpose(1, 0, 2).reshape(blocks * narrow, width)
        packet_self = packet([query_weight, key_weight, value_weight])
        packet_cross = packet([output_weight, source_query, source_key, source_value, source_output])
        packet_inner = packet([inner_rows, outer_weight])
        set_self, set_cross, set_inner = packet_self, packet_cross, packet_inner
        set_back, set_last, set_memory = packet_cross, packet_self, packet_cross
        strides = (3 * narrow, 5 * narrow, 2 * blocks * narrow)
    else:
        full = [whole(w) for w in (query_weight, key_weight, value_weight, output_weight, source_query, source_key, source_value, source_output)]
        set_self, set_cross = full[:3], full[3:]
        set_inner = [
            whole(inner_weight).reshape(width, blocks, width).transpose(1, 0, 2),
            whole(outer_weight).reshape(blocks, width, width),
        ]
        set_back, set_last, set_memory = [full[3], full[4], full[7]], full[:3], full[5:7]
        strides = (0, 0, 0)

    short = jnp.stack([query_bias, value_bias, output_bias, attention_gain, attention_shift,
                       source_query_bias, source_value_bias, source_output_bias, source_gain,
                       source_shift, outer_bias, final_gain, final_shift])
    lane = lax.broadcasted_iota(jnp.int32, (1, width), 1)
    spread_short = jnp.where(lane // narrow == me, jnp.tile(short, (1, devices)), 0)
    place = lax.broadcasted_iota(jnp.int32, (blocks, width), 0) * width + lane
    spread_wide = jnp.where(place // wide == me, jnp.tile(inner_bias.reshape(1, wide), (blocks, width // wide)), 0)
    vectors = jnp.concatenate([spread_short, spread_wide, jnp.zeros((7, width), BF16)], axis=0)
    vectors = reduce_all(vectors, layout).astype(F32)

    def pick(array, index):
        return lax.dynamic_index_in_dim(array, index, axis=0, keepdims=False)

    other = row_count - 1 - turn
    sent = jnp.concatenate([pick(tokens, other), pick(memory, other)], axis=0)
    came = swap(sent, parts, devices)
    own = jnp.concatenate([pick(tokens, turn), came[:block], pick(memory, turn), came[block:]], axis=0)
    row_tokens = [own] + [swap(own, m, devices) for m in range(1, parts)]
    cot = jnp.concatenate([pick(cotangent, turn), swap(pick(cotangent, other), parts, devices)], axis=0)
    all_ids = jnp.concatenate([target_ids, source_ids], axis=1)
    own_ids = jnp.stack([pick(all_ids, turn), swap(pick(all_ids, other), parts, devices)])
    row_ids = [own_ids] + [swap(own_ids, m, devices) for m in range(1, parts)]
    ids = jnp.concatenate([i[:, :block].reshape(1, share) for i in row_ids], axis=1)
    memory_ids = jnp.concatenate([i[:, block:].reshape(1, memory_share) for i in row_ids], axis=1)

    def run(made, name, *args):
        kernel, outs, scratch, flops = made
        return call(kernel, outs, (me_array,) + args, scratch, flops, name)

    query, keys, values, mixture_t, logs = run(
        make_self_forward(layout, parts, share, width, strides[0], len(set_self)), "self_forward",
        *set_self, *row_tokens, ids, vectors,
    )
    first_sum, second_sum, cross_query, memory_keys, memory_values, cross_t, cross_logs = run(
        make_cross_forward(layout, parts, share, memory_share, width, strides[1], len(set_cross)),
        "cross_forward", *set_cross, *row_tokens, ids, memory_ids, vectors, mixture_t,
    )
    out_own, out_send, back2_in, sums_inner, *grads_inner = run(
        make_inner(layout, share, width, hidden, strides[2], len(set_inner)), "inner",
        *set_inner, second_sum, cot, vectors,
    )
    found = run(
        make_cross_back(layout, parts, share, memory_share, width, strides[1], len(set_back)),
        "cross_back", *set_back, back2_in, first_sum, second_sum, cross_query, memory_keys,
        memory_values, cross_t, cross_logs, ids, memory_ids, mixture_t, vectors,
    )
    back1, slope, slope_t, deltas, sums_cross, memory_key_own, memory_value_own = found[:7]
    memory_sends, grads_cross = found[7 : 7 + parts - 1], found[7 + parts - 1 :]
    memory_received = [swap(a, m + 1, devices) for m, a in enumerate(memory_sends)]
    found = run(
        make_self_back(layout, parts, share, width), "self_back",
        query, keys, values, slope, slope_t, logs, deltas, ids,
    )
    query_low, key_own, value_own = found[:3]
    received = [swap(a, m + 1, devices) for m, a in enumerate(found[3:])]
    in_own, in_send, memory_own, memory_send, sums_last, *grads_last = run(
        make_last(layout, parts, share, memory_share, width, strides[:2], len(set_last)), "last",
        *set_last, *set_memory, own, back1, query_low, key_own, value_own, memory_key_own,
        memory_value_own, *received, *memory_received,
    )

    def regroup(mine, theirs):
        came = swap(theirs, parts, devices).astype(F32)
        return jnp.where(turn == 0, jnp.stack([mine, came]), jnp.stack([came, mine]))

    output = regroup(out_own, out_send)
    input_gradient = regroup(in_own, in_send)
    memory_gradient = regroup(memory_own, memory_send)

    if layout.packed:
        got = scatter_tree(*grads_inner, layout)[0]
        inner_share = got[: blocks * narrow].reshape(blocks, narrow, width).transpose(1, 0, 2).reshape(narrow, hidden)
        outer_share = got[blocks * narrow :]
        got = scatter_tree(*grads_cross, layout)[0]
        source_output_share, source_query_share, output_share = (got[i * narrow : (i + 1) * narrow] for i in range(3))
        got = scatter_tree(*grads_last, layout)[0]
        query_share, key_share, value_share, source_key_share, source_value_share = (got[i * narrow : (i + 1) * narrow] for i in range(5))
    else:
        def scatter(array):
            return lax.psum_scatter(array, AXES, scatter_dimension=0, tiled=True)

        inner_share = scatter(grads_inner[0].transpose(1, 0, 2).reshape(width, hidden))
        outer_share = scatter(grads_inner[1].reshape(hidden, width))
        source_output_share, source_query_share, output_share = (scatter(g) for g in grads_cross)
        query_share, key_share, value_share, source_key_share, source_value_share = (scatter(g) for g in grads_last)
    sums = reduce_all(jnp.concatenate([sums_inner, sums_cross, sums_last], axis=0), layout)

    def narrow_part(row):
        return lax.dynamic_slice(sums[row], (me * narrow,), (narrow,))

    inner_bias_share = lax.dynamic_slice(sums[3 : 3 + blocks].reshape(hidden), (me * wide,), (wide,))
    return (
        output,
        input_gradient,
        memory_gradient,
        query_share,
        key_share,
        value_share,
        output_share,
        narrow_part(16),
        narrow_part(17),
        narrow_part(14),
        narrow_part(12),
        narrow_part(13),
        source_query_share,
        source_key_share,
        source_value_share,
        source_output_share,
        narrow_part(11),
        narrow_part(18),
        narrow_part(10),
        narrow_part(8),
        narrow_part(9),
        inner_share,
        inner_bias_share,
        outer_share,
        narrow_part(2),
        narrow_part(0),
        narrow_part(1),
    )


def solution(mesh):
    sequence, devices = mesh.shape["seq"], mesh.size
    tokens, ids = P("dp", "seq", None), P("dp", "seq")
    matrix, vector = P(AXES, None), P(AXES)
    attention = (matrix,) * 4 + (vector,) * 5
    inner = (matrix, vector, matrix, vector, vector, vector)
    return jax.shard_map(
        functools.partial(per_device, devices=devices, sequence=sequence),
        mesh=mesh,
        in_specs=(tokens, tokens, ids, ids, tokens) + attention + attention + inner,
        out_specs=(tokens, tokens, tokens) + attention + attention + inner,
        check_vma=False,
    )
```

time: 2120 us -> 289 us (0.14)
  waiting for transfers between devices: 1370 us -> 103 us
  blocking collectives: 444 us -> 0 us
  matrix products: 136 us -> 0 us
  Pallas kernels: 0 us -> 77.9 us
  starting transfers between devices: 1.62 us -> 78.7 us
  local copies, waits for them, and re-layouts: 84.8 us -> 22.2 us
  other arithmetic: 55.7 us -> 5.9 us
    reduce_scatter x9 -> x0, waiting for transfers between devices: 699 us -> none  [the longest x1 140 us: per_device(): lax.psum_scatter(inner_weight_grad, ('dp', 'seq'), scatter_dimension=0, t...]
    unnamed x33 -> x0, waiting for transfers between devices: 670 us -> none
    all_gather x14 -> x0, blocking collectives: 356 us -> none  [the longest x1 42.1 us: gather_source(): lax.all_gather(source_query, ('dp', 'seq'), axis=0, tiled=True)]
    dot_general x126 -> x0, matrix products: 136 us -> none  [the longest x16 23.4 us: pair_back(): jnp.einsum('qhd,khd->hqk', heads_g, split_heads(values), preferred_elemen...]
    ppermute x0 -> x75, waiting for transfers between devices: none -> 103 us  [swap(): return lax.ppermute(array, AXES, [(i, i ^ mask) for i in range(devices)])]
    unnamed x3 -> x0, blocking collectives: 87.7 us -> none
    ppermute x0 -> x75, starting transfers between devices: none -> 78.7 us  [swap(): return lax.ppermute(array, AXES, [(i, i ^ mask) for i in range(devices)])]
    pallas_call x0 -> x15, Pallas kernels: none -> 77.9 us  [the longest x6 76.3 us: call(): pl.pallas_call(kernel, out_shape=[jax.ShapeDtypeStruct(s, d) for s, d in...]
  transfers between devices with their start and end apart: 24 -> 75, of which waited for: 14 -> 27; matrix products, arithmetic and copies ran while one was open for 10% -> 7% of each run, Pallas kernels for 0% -> 16%
where the time goes in v1:
time: 289 us
  waiting for transfers between devices  103 us (36%)
  starting transfers between devices  78.7 us (27%)
  Pallas kernels  77.9 us (27%)
  local copies, waits for them, and re-layouts  22.2 us (8%)
  other arithmetic  5.9 us (2%)
    ppermute x75, waiting for transfers between devices, swap(): return lax.ppermute(array, AXES, [(i, i ^ mask) for i in range(devices)])  103 us
    ppermute x75, starting transfers between devices, swap(): return lax.ppermute(array, AXES, [(i, i ^ mask) for i in range(devices)])  78.7 us
    pallas_call x6, Pallas kernels, call(): pl.pallas_call(kernel, out_shape=[jax.ShapeDtypeStruct(s, d) for s, d in...  76.3 us
    unnamed x108, local copies, waits for them, and re-layouts  8.09 us
  transfers between devices with their start and end apart: 75, of which 27 were waited for; matrix products, arithmetic and copies ran while one was open for 7% of the time, Pallas kernels for 16%

profile of v1, /device:TPU:0, one launch (start us, length us, event | category | flops | bytes accessed | tf_op | source)
XLA Modules:
  0.0 288.7 jit_solution(11736914130473136932)
XLA Ops:
  3.5 3.1 %collective-permute-start.24 = (bf16[24,512]{1,0:T(8,128)(2,1)S(1)}, bf16[24,512]{1,0:T(8,128)(2,1)S(1)}, u32[]{:S(2)}, u32[]{:S(2)}) collective-permute-start(bf16[24,512]{1,0:T(8,128)(2,1)S(1)} %maximum_maximum_fusion), channel_id=1, source_target_pairs={{0,8},{1,9},{2,10},{3,11},{4,12},{5,13},{6,14},{7,15},{8,0},{9,1},... | collective-permute-start | bytes 73736 | tf_op jit(solution)/shard_map/ppermute | solution.py:96
  17.9 3.6 %collective-permute-start.32 = (bf16[48,512]{1,0:T(8,128)(2,1)S(1)}, bf16[48,512]{1,0:T(8,128)(2,1)S(1)}, u32[]{:S(2)}, u32[]{:S(2)}) collective-permute-start(bf16[48,512]{1,0:T(8,128)(2,1)S(1)} %get-tuple-element.182), channel_id=1, source_target_pairs={{0,16},{1,17},{2,18},{3,19},{4,20},{5,21},{6,22},{7,23},{8,24},{9,... | collective-permute-start | bytes 147464 | tf_op jit(solution)/shard_map/ppermute | solution.py:96
  43.1 3.1 %collective-permute-done.1 = bf16[128,512]{1,0:T(8,128)(2,1)S(1)} collective-permute-done((bf16[128,512]{1,0:T(8,128)(2,1)S(1)}, bf16[128,512]{1,0:T(8,128)(2,1)S(1)}, u32[]{:S(2)}, u32[]{:S(2)}) %collective-permute-start.1) | collective-permute-done | bytes 131104 | tf_op jit(solution)/shard_map/ppermute | solution.py:96
  59.0 12.0 %collective-permute-done.20 = bf16[320,512]{1,0:T(8,128)(2,1)S(1)} collective-permute-done((bf16[320,512]{1,0:T(8,128)(2,1)S(1)}, bf16[320,512]{1,0:T(8,128)(2,1)S(1)}, u32[]{:S(2)}, u32[]{:S(2)}) %collective-permute-start.20) | collective-permute-done | bytes 327712 | tf_op jit(solution)/shard_map/ppermute | solution.py:96
  71.0 6.9 %collective-permute-done.14.refs_3_.refs_11_ = bf16[320,512]{1,0:T(8,128)(2,1)S(1)} collective-permute-done((bf16[320,512]{1,0:T(8,128)(2,1)S(1)}, bf16[320,512]{1,0:T(8,128)(2,1)S(1)}, u32[]{:S(2)}, u32[]{:S(2)}) %collective-permute-start.14) | collective-permute-done | bytes 327712 | tf_op jit(solution)/shard_map/ppermute | solution.py:96
  83.0 6.0 %collective-permute-done.4.refs_3_ = bf16[512,512]{1,0:T(8,128)(2,1)} collective-permute-done((bf16[512,512]{1,0:T(8,128)(2,1)}, bf16[512,512]{1,0:T(8,128)(2,1)}, u32[]{:S(2)}, u32[]{:S(2)}) %collective-permute-start.4) | collective-permute-done | bytes 524320 | tf_op jit(solution)/shard_map/ppermute | solution.py:96
  89.2 4.6 %collective-permute-done.6.refs_5_ = bf16[512,512]{1,0:T(8,128)(2,1)} collective-permute-done((bf16[512,512]{1,0:T(8,128)(2,1)}, bf16[512,512]{1,0:T(8,128)(2,1)}, u32[]{:S(2)}, u32[]{:S(2)}) %collective-permute-start.6) | collective-permute-done | bytes 524320 | tf_op jit(solution)/shard_map/ppermute | solution.py:96
  93.7 12.3 %collective-permute-done.8.refs_7_ = bf16[512,512]{1,0:T(8,128)(2,1)} collective-permute-done((bf16[512,512]{1,0:T(8,128)(2,1)}, bf16[512,512]{1,0:T(8,128)(2,1)}, u32[]{:S(2)}, u32[]{:S(2)}) %collective-permute-start.8) | collective-permute-done | bytes 524320 | tf_op jit(solution)/shard_map/ppermute | solution.py:96
  108.6 12.5 %self_forward.1 = (bf16[512,512]{1,0:T(8,128)(2,1)}, bf16[1024,512]{1,0:T(8,128)(2,1)}, bf16[1024,512]{1,0:T(8,128)(2,1)}, bf16[512,512]{1,0:T(8,128)(2,1)}, f32[8,1,512]{2,1,0:T(1,128)}) custom-call(s32[1]{0:T(128)} %bitcast.refs_0_, bf16[192,512]{1,0:T(8,128)(2,1)} %copy-done.19, bf16[192,512]{1,0:T(8,128)(2,1)} %collective-permute-done.34.refs_2_, ...), custom_call_target="tpu_custom_call" | custom-call | flops 2415919104 | bytes 6098944 | tf_op jit(solution)/shard_map/self_forward/pallas_call | solution.py:220
  121.9 8.7 %cross_forward.1 = (f32[512,512]{1,0:T(8,128)}, f32[512,512]{1,0:T(8,128)}, bf16[512,512]{1,0:T(8,128)(2,1)}, bf16[256,512]{1,0:T(8,128)(2,1)}, bf16[256,512]{1,...) custom-call(s32[1]{0:T(128)} %bitcast.refs_0_, bf16[320,512]{1,0:T(8,128)(2,1)} %copy-done.8, ...), custom_call_target="tpu_custom_call" | custom-call | flops 1342177280 | bytes 8197120 | tf_op jit(solution)/shard_map/cross_forward/pallas_call | solution.py:220
  131.9 17.8 %inner.1 = (f32[256,512]{1,0:T(8,128)}, bf16[256,512]{1,0:T(8,128)(2,1)}, f32[512,512]{1,0:T(8,128)}, f32[8,512]{1,0:T(8,128)}, bf16[16,128,512]{2,1,0:T(8,128)(2,1)}, /*index=5*/bf16[16,128,512]{2,1,0:T(8,128)(2,1)}) custom-call(s32[1]{0:T(128)} %bitcast.refs_0_, bf16[512,512]{1,0:T(8,128)(2,1)} %constant_dynamic-update-slice_fusion.refs_1_, ...), custom_call_target="tpu_custom_call" | custom-call | flops 6442450944 | bytes 11862016 | tf_op jit(solution)/shard_map/inner/pallas_call | solution.py:220
  149.7 13.6 %cross_back.1 = (f32[512,512]{1,0:T(8,128)}, bf16[512,512]{1,0:T(8,128)(2,1)}, bf16[512,512]{1,0:T(8,128)(2,1)}, f32[8,1,512]{2,1,0:T(1,128)}, f32[8,512]{1,0:T(...) custom-call(s32[1]{0:T(128)} %bitcast.refs_0_, ...), custom_call_target="tpu_custom_call" | custom-call | flops 2550136832 | bytes 12424192 | tf_op jit(solution)/shard_map/cross_back/pallas_call | solution.py:220
  163.5 15.8 %self_back.1 = (bf16[512,512]{1,0:T(8,128)(2,1)}, f32[512,512]{1,0:T(8,128)}, f32[512,512]{1,0:T(8,128)}, bf16[1024,512]{1,0:T(8,128)(2,1)}) custom-call(s32[1]{0:T(128)} %bitcast.refs_0_, bf16[512,512]{1,0:T(8,128)(2,1)} %get-tuple-element.102.refs_1_, bf16[1024,512]{1,0:T(8,128)(2,1)} %get-tuple-element.103.refs_2_, ...), custom_call_target="tpu_custom_call" | custom-call | flops 2684354560 | bytes 7376896 | tf_op jit(solution)/shard_map/self_back/pallas_call | solution.py:220
  183.6 12.9 %collective-permute-done.55.refs_1_ = bf16[4,48,512]{2,1,0:T(8,128)(2,1)S(1)} collective-permute-done((bf16[4,48,512]{2,1,0:T(8,128)(2,1)S(1)}, bf16[4,48,512]{2,1,0:T(8,128)(2,1)S(1)}, u32[]{:S(2)}, u32[]{:S(2)}) %collective-permute-start.55) | collective-permute-done | bytes 196640 | tf_op jit(solution)/shard_map/ppermute | solution.py:96
  197.9 2.9 collective-permute-start.59
  201.3 2.9 collective-permute-start.60
  208.4 7.9 %last.1 = (f32[256,512]{1,0:T(8,128)}, bf16[256,512]{1,0:T(8,128)(2,1)}, f32[64,512]{1,0:T(8,128)}, bf16[64,512]{1,0:T(8,128)(2,1)}, f32[8,512]{1,0:T(8,128)}, /...) custom-call(s32[1]{0:T(128)} %bitcast.refs_0_, bf16[192,512]{1,0:T(8,128)(2,1)} %copy-done.19, ...), custom_call_target="tpu_custom_call" | custom-call | flops 1879048192 | bytes 13975552 | tf_op jit(solution)/shard_map/last/pallas_call | solution.py:220
  223.2 3.2 %collective-permute-done.63 = f32[24,512]{1,0:T(8,128)S(1)} collective-permute-done((f32[24,512]{1,0:T(8,128)S(1)}, f32[24,512]{1,0:T(8,128)S(1)}, u32[]{:S(2)}, u32[]{:S(2)}) %collective-permute-start.63) | collective-permute-done | bytes 49184 | tf_op jit(solution)/shard_map/ppermute | solution.py:96
  246.6 5.6 %collective-permute-done.69.refs_1_ = bf16[4,128,512]{2,1,0:T(8,128)(2,1)S(1)} collective-permute-done((bf16[4,128,512]{2,1,0:T(8,128)(2,1)S(1)}, bf16[4,128,512]{2,1,0:T(8,128)(2,1)S(1)}, u32[]{:S(2)}, u32[]{:S(2)}) %collective-permute-start.69) | collective-permute-done | bytes 524320 | tf_op jit(solution)/shard_map/ppermute | solution.py:96
  254.6 10.4 %collective-permute-done.71.refs_3_ = bf16[4,128,512]{2,1,0:T(8,128)(2,1)S(1)} collective-permute-done((bf16[4,128,512]{2,1,0:T(8,128)(2,1)S(1)}, bf16[4,128,512]{2,1,0:T(8,128)(2,1)S(1)}, u32[]{:S(2)}, u32[]{:S(2)}) %collective-permute-start.71) | collective-permute-done | bytes 524320 | tf_op jit(solution)/shard_map/ppermute | solution.py:96
  265.3 3.1 %collective-permute-start.73 = (bf16[1,128,512]{2,1,0:T(8,128)(2,1)S(1)}, bf16[1,128,512]{2,1,0:T(8,128)(2,1)S(1)}, u32[]{:S(2)}, u32[]{:S(2)}) collective-permute-start(bf16[1,128,512]{2,1,0:T(8,128)(2,1)S(1)} %get-tuple-element.151), channel_id=1, source_target_pairs={{0,16},{1,17},{2,18},{3,19},{4,20},{5,21},{6,22},{7,23},{8,24},{9,... | collective-permute-start | bytes 393224 | tf_op jit(solution)/shard_map/ppermute | solution.py:96
  273.7 4.7 %collective-permute-done.50.refs_3_ = bf16[4,80,512]{2,1,0:T(8,128)(2,1)S(1)} collective-permute-done((bf16[4,80,512]{2,1,0:T(8,128)(2,1)S(1)}, bf16[4,80,512]{2,1,0:T(8,128)(2,1)S(1)}, u32[]{:S(2)}, u32[]{:S(2)}) %collective-permute-start.50) | collective-permute-done | bytes 327712 | tf_op jit(solution)/shard_map/ppermute | solution.py:96
  278.6 3.1 %collective-permute-start.52 = (bf16[1,80,512]{2,1,0:T(8,128)(2,1)S(1)}, bf16[1,80,512]{2,1,0:T(8,128)(2,1)S(1)}, u32[]{:S(2)}, u32[]{:S(2)}) collective-permute-start(bf16[1,80,512]{2,1,0:T(8,128)(2,1)S(1)} %get-tuple-element.128), channel_id=1, source_target_pairs={{0,16},{1,17},{2,18},{3,19},{4,20},{5,21},{6,22},{7,23},{8,24},{9,... | collective-permute-start | bytes 245768 | tf_op jit(solution)/shard_map/ppermute | solution.py:96
  284.4 3.6 %collective-permute-done.52.refs_2_ = bf16[1,80,512]{2,1,0:T(8,128)(2,1)S(1)} collective-permute-done((bf16[1,80,512]{2,1,0:T(8,128)(2,1)S(1)}, bf16[1,80,512]{2,1,0:T(8,128)(2,1)S(1)}, u32[]{:S(2)}, u32[]{:S(2)}) %collective-permute-start.52) | collective-permute-done | bytes 81952 | tf_op jit(solution)/shard_map/ppermute | solution.py:96
  (313 shorter events, 107.3 us)
Async XLA Ops:
  3.5 17.9 %collective-permute-start.24 = (bf16[24,512]{1,0:T(8,128)(2,1)S(1)}, bf16[24,512]{1,0:T(8,128)(2,1)S(1)}, u32[]{:S(2)}, u32[]{:S(2)}) collective-permute-start(bf16[24,512]{1,0:T(8,128)(2,1)S(1)} %maximum_maximum_fusion), channel_id=1, source_target_pairs={{0,8},{1,9},{2,10},{3,11},{4,12},{5,13},{6,14},{7,15},{8,0},{9,1},... | collective-permute-start | bytes 73736 | tf_op jit(solution)/shard_map/ppermute | solution.py:96
  46.2 24.8 %collective-permute-start.20 = (bf16[320,512]{1,0:T(8,128)(2,1)S(1)}, bf16[320,512]{1,0:T(8,128)(2,1)S(1)}, u32[]{:S(2)}, u32[]{:S(2)}) collective-permute-start(bf16[320,512]{1,0:T(8,128)(2,1)S(1)} %pad_maximum_fusion.2), channel_id=1, source_target_pairs={{0,2},{1,3},{2,0},{3,1},{4,6},{5,7},{6,4},{7,5},{8,10},{9,11},{10,... | collective-permute-start | bytes 983048 | tf_op jit(solution)/shard_map/ppermute | solution.py:96
  50.2 27.7 %collective-permute-start.14 = (bf16[320,512]{1,0:T(8,128)(2,1)S(1)}, bf16[320,512]{1,0:T(8,128)(2,1)S(1)}, u32[]{:S(2)}, u32[]{:S(2)}) collective-permute-start(bf16[320,512]{1,0:T(8,128)(2,1)S(1)} %constant_dynamic-update-slice_fusion.10.refs_1_.refs_9_), channel_id=1, source_target_pairs={{0,2},{1,3},{2,0},{3,1},{4,6},{5,7},{6,4},{7,5},{8,10},{9,11},{10,... | collective-permute-start | bytes 983048 | tf_op jit(solution)/shard_map/ppermute | solution.py:96
  54.0 24.0 %collective-permute-start.16 = (bf16[320,512]{1,0:T(8,128)(2,1)S(1)}, bf16[320,512]{1,0:T(8,128)(2,1)S(1)}, u32[]{:S(2)}, u32[]{:S(2)}) collective-permute-start(bf16[320,512]{1,0:T(8,128)(2,1)S(1)} %constant_dynamic-update-slice_fusion.10.refs_1_.refs_9_), channel_id=1, source_target_pairs={{0,4},{1,5},{2,6},{3,7},{4,0},{5,1},{6,2},{7,3},{8,12},{9,13},{10,... | collective-permute-start | bytes 983048 | tf_op jit(solution)/shard_map/ppermute | solution.py:96
  55.0 23.5 %collective-permute-start.18 = (bf16[320,512]{1,0:T(8,128)(2,1)S(1)}, bf16[320,512]{1,0:T(8,128)(2,1)S(1)}, u32[]{:S(2)}, u32[]{:S(2)}) collective-permute-start(bf16[320,512]{1,0:T(8,128)(2,1)S(1)} %constant_dynamic-update-slice_fusion.10.refs_1_.refs_9_), channel_id=1, source_target_pairs={{0,6},{1,7},{2,4},{3,5},{4,2},{5,3},{6,0},{7,1},{8,14},{9,15},{10,... | collective-permute-start | bytes 983048 | tf_op jit(solution)/shard_map/ppermute | solution.py:96
  56.9 32.2 %collective-permute-start.4 = (bf16[512,512]{1,0:T(8,128)(2,1)}, bf16[512,512]{1,0:T(8,128)(2,1)}, u32[]{:S(2)}, u32[]{:S(2)}) collective-permute-start(bf16[512,512]{1,0:T(8,128)(2,1)} %constant_dynamic-update-slice_fusion.refs_1_), channel_id=1, source_target_pairs={{0,2},{1,3},{2,0},{3,1},{4,6},{5,7},{6,4},{7,5},{8,10},{9,11},{10,... | collective-permute-start | bytes 1572872 | tf_op jit(solution)/shard_map/ppermute | solution.py:96
  79.4 26.6 %collective-permute-start.8 = (bf16[512,512]{1,0:T(8,128)(2,1)}, bf16[512,512]{1,0:T(8,128)(2,1)}, u32[]{:S(2)}, u32[]{:S(2)}) collective-permute-start(bf16[512,512]{1,0:T(8,128)(2,1)} %constant_dynamic-update-slice_fusion.refs_1_), channel_id=1, source_target_pairs={{0,6},{1,7},{2,4},{3,5},{4,2},{5,3},{6,0},{7,1},{8,14},{9,15},{10,... | collective-permute-start | bytes 1572872 | tf_op jit(solution)/shard_map/ppermute | solution.py:96
  82.3 24.9 %collective-permute-start.21 = (bf16[640,512]{1,0:T(8,128)(2,1)S(1)}, bf16[640,512]{1,0:T(8,128)(2,1)}, u32[]{:S(2)}, u32[]{:S(2)}) collective-permute-start(bf16[640,512]{1,0:T(8,128)(2,1)S(1)} %pad_maximum_fusion.refs_9_.refs_17_), channel_id=1, source_target_pairs={{0,1},{1,0},{2,3},{3,2},{4,5},{5,4},{6,7},{7,6},{8,9},{9,8},{10,11... | collective-permute-start | bytes 1966088 | tf_op jit(solution)/shard_map/ppermute | solution.py:96
  82.4 23.6 %collective-permute-start.15 = (bf16[320,512]{1,0:T(8,128)(2,1)S(1)}, bf16[320,512]{1,0:T(8,128)(2,1)S(1)}, u32[]{:S(2)}, u32[]{:S(2)}) collective-permute-start(bf16[320,512]{1,0:T(8,128)(2,1)S(1)} %collective-permute-done.14.refs_3_.refs_11_), channel_id=1, source_target_pairs={{0,1},{1,0},{2,3},{3,2},{4,5},{5,4},{6,7},{7,6},{8,9},{9,8},{10,11... | collective-permute-start | bytes 983048 | tf_op jit(solution)/shard_map/ppermute | solution.py:96
  89.0 17.5 %collective-permute-start.17 = (bf16[320,512]{1,0:T(8,128)(2,1)S(1)}, bf16[320,512]{1,0:T(8,128)(2,1)S(1)}, u32[]{:S(2)}, u32[]{:S(2)}) collective-permute-start(bf16[320,512]{1,0:T(8,128)(2,1)S(1)} %collective-permute-done.16.refs_5_.refs_13_), channel_id=1, source_target_pairs={{0,1},{1,0},{2,3},{3,2},{4,5},{5,4},{6,7},{7,6},{8,9},{9,8},{10,11... | collective-permute-start | bytes 983048 | tf_op jit(solution)/shard_map/ppermute | solution.py:96
  93.7 36.9 %collective-permute-start.3 = (bf16[512,512]{1,0:T(8,128)(2,1)}, bf16[512,512]{1,0:T(8,128)(2,1)S(1)}, u32[]{:S(2)}, u32[]{:S(2)}) collective-permute-start(bf16[512,512]{1,0:T(8,128)(2,1)} %constant_dynamic-update-slice_fusion.refs_1_), channel_id=1, source_target_pairs={{0,1},{1,0},{2,3},{3,2},{4,5},{5,4},{6,7},{7,6},{8,9},{9,8},{10,11... | collective-permute-start | bytes 1572872 | tf_op jit(solution)/shard_map/ppermute | solution.py:96
  106.0 24.6 %collective-permute-start.5 = (bf16[512,512]{1,0:T(8,128)(2,1)}, bf16[512,512]{1,0:T(8,128)(2,1)S(1)}, u32[]{:S(2)}, u32[]{:S(2)}) collective-permute-start(bf16[512,512]{1,0:T(8,128)(2,1)} %collective-permute-done.4.refs_3_), channel_id=1, source_target_pairs={{0,1},{1,0},{2,3},{3,2},{4,5},{5,4},{6,7},{7,6},{8,9},{9,8},{10,11... | collective-permute-start | bytes 1572872 | tf_op jit(solution)/shard_map/ppermute | solution.py:96
  106.0 24.6 %collective-permute-start.7 = (bf16[512,512]{1,0:T(8,128)(2,1)}, bf16[512,512]{1,0:T(8,128)(2,1)S(1)}, u32[]{:S(2)}, u32[]{:S(2)}) collective-permute-start(bf16[512,512]{1,0:T(8,128)(2,1)} %collective-permute-done.6.refs_5_), channel_id=1, source_target_pairs={{0,1},{1,0},{2,3},{3,2},{4,5},{5,4},{6,7},{7,6},{8,9},{9,8},{10,11... | collective-permute-start | bytes 1572872 | tf_op jit(solution)/shard_map/ppermute | solution.py:96
  106.5 24.1 %collective-permute-start.9 = (bf16[512,512]{1,0:T(8,128)(2,1)}, bf16[512,512]{1,0:T(8,128)(2,1)S(1)}, u32[]{:S(2)}, u32[]{:S(2)}) collective-permute-start(bf16[512,512]{1,0:T(8,128)(2,1)} %collective-permute-done.8.refs_7_), channel_id=1, source_target_pairs={{0,1},{1,0},{2,3},{3,2},{4,5},{5,4},{6,7},{7,6},{8,9},{9,8},{10,11... | collective-permute-start | bytes 1572872 | tf_op jit(solution)/shard_map/ppermute | solution.py:96
  179.3 28.0 %collective-permute-start.43 = (bf16[1024,512]{1,0:T(8,128)(2,1)}, bf16[1024,512]{1,0:T(8,128)(2,1)S(1)}, u32[]{:S(2)}, u32[]{:S(2)}) collective-permute-start(bf16[1024,512]{1,0:T(8,128)(2,1)} %get-tuple-element.114), channel_id=1, source_target_pairs={{0,1},{1,0},{2,3},{3,2},{4,5},{5,4},{6,7},{7,6},{8,9},{9,8},{10,11... | collective-permute-start | bytes 3145736 | tf_op jit(solution)/shard_map/ppermute | solution.py:96
  179.7 18.1 %collective-permute-start.42 = (bf16[256,512]{1,0:T(8,128)(2,1)S(1)}, bf16[256,512]{1,0:T(8,128)(2,1)S(1)}, u32[]{:S(2)}, u32[]{:S(2)}) collective-permute-start(bf16[256,512]{1,0:T(8,128)(2,1)S(1)} %copy-done.40), channel_id=1, source_target_pairs={{0,2},{1,3},{2,0},{3,1},{4,6},{5,7},{6,4},{7,5},{8,10},{9,11},{10,... | collective-permute-start | bytes 786440 | tf_op jit(solution)/shard_map/ppermute | solution.py:96
  180.0 16.5 %collective-permute-start.55 = (bf16[4,48,512]{2,1,0:T(8,128)(2,1)S(1)}, bf16[4,48,512]{2,1,0:T(8,128)(2,1)S(1)}, u32[]{:S(2)}, u32[]{:S(2)}) collective-permute-start(bf16[4,48,512]{2,1,0:T(8,128)(2,1)S(1)} %get-tuple-element.133), channel_id=1, source_target_pairs={{0,2},{1,3},{2,0},{3,1},{4,6},{5,7},{6,4},{7,5},{8,10},{9,11},{10,... | collective-permute-start | bytes 589832 | tf_op jit(solution)/shard_map/ppermute | solution.py:96
  196.5 40.4 %collective-permute-start.68 = (bf16[16,128,512]{2,1,0:T(8,128)(2,1)}, bf16[16,128,512]{2,1,0:T(8,128)(2,1)S(1)}, u32[]{:S(2)}, u32[]{:S(2)}) collective-permute-start(bf16[16,128,512]{2,1,0:T(8,128)(2,1)} %get-tuple-element.144), channel_id=1, source_target_pairs={{0,1},{1,0},{2,3},{3,2},{4,5},{5,4},{6,7},{7,6},{8,9},{9,8},{10,11... | collective-permute-start | bytes 6291464 | tf_op jit(solution)/shard_map/ppermute | solution.py:96
  222.1 20.7 %collective-permute-start.47 = (bf16[16,80,512]{2,1,0:T(8,128)(2,1)}, bf16[16,80,512]{2,1,0:T(8,128)(2,1)S(1)}, u32[]{:S(2)}, u32[]{:S(2)}) collective-permute-start(bf16[16,80,512]{2,1,0:T(8,128)(2,1)} %get-tuple-element.121), channel_id=1, source_target_pairs={{0,1},{1,0},{2,3},{3,2},{4,5},{5,4},{6,7},{7,6},{8,9},{9,8},{10,11... | collective-permute-start | bytes 3932168 | tf_op jit(solution)/shard_map/ppermute | solution.py:96
  240.4 24.6 %collective-permute-start.71 = (bf16[4,128,512]{2,1,0:T(8,128)(2,1)S(1)}, bf16[4,128,512]{2,1,0:T(8,128)(2,1)S(1)}, u32[]{:S(2)}, u32[]{:S(2)}) collective-permute-start(bf16[4,128,512]{2,1,0:T(8,128)(2,1)S(1)} %get-tuple-element.148), channel_id=1, source_target_pairs={{0,6},{1,7},{2,4},{3,5},{4,2},{5,3},{6,0},{7,1},{8,14},{9,15},{10,... | collective-permute-start | bytes 1572872 | tf_op jit(solution)/shard_map/ppermute | solution.py:96
  243.0 27.0 %collective-permute-start.48 = (bf16[4,80,512]{2,1,0:T(8,128)(2,1)S(1)}, bf16[4,80,512]{2,1,0:T(8,128)(2,1)S(1)}, u32[]{:S(2)}, u32[]{:S(2)}) collective-permute-start(bf16[4,80,512]{2,1,0:T(8,128)(2,1)S(1)} %get-tuple-element.123), channel_id=1, source_target_pairs={{0,2},{1,3},{2,0},{3,1},{4,6},{5,7},{6,4},{7,5},{8,10},{9,11},{10,... | collective-permute-start | bytes 983048 | tf_op jit(solution)/shard_map/ppermute | solution.py:96
  244.9 28.8 %collective-permute-start.49 = (bf16[4,80,512]{2,1,0:T(8,128)(2,1)S(1)}, bf16[4,80,512]{2,1,0:T(8,128)(2,1)S(1)}, u32[]{:S(2)}, u32[]{:S(2)}) collective-permute-start(bf16[4,80,512]{2,1,0:T(8,128)(2,1)S(1)} %get-tuple-element.124), channel_id=1, source_target_pairs={{0,4},{1,5},{2,6},{3,7},{4,0},{5,1},{6,2},{7,3},{8,12},{9,13},{10,... | collective-permute-start | bytes 983048 | tf_op jit(solution)/shard_map/ppermute | solution.py:96
  252.2 26.1 %collective-permute-start.50 = (bf16[4,80,512]{2,1,0:T(8,128)(2,1)S(1)}, bf16[4,80,512]{2,1,0:T(8,128)(2,1)S(1)}, u32[]{:S(2)}, u32[]{:S(2)}) collective-permute-start(bf16[4,80,512]{2,1,0:T(8,128)(2,1)S(1)} %get-tuple-element.125), channel_id=1, source_target_pairs={{0,6},{1,7},{2,4},{3,5},{4,2},{5,3},{6,0},{7,1},{8,14},{9,15},{10,... | collective-permute-start | bytes 983048 | tf_op jit(solution)/shard_map/ppermute | solution.py:96
  265.3 17.6 %collective-permute-start.73 = (bf16[1,128,512]{2,1,0:T(8,128)(2,1)S(1)}, bf16[1,128,512]{2,1,0:T(8,128)(2,1)S(1)}, u32[]{:S(2)}, u32[]{:S(2)}) collective-permute-start(bf16[1,128,512]{2,1,0:T(8,128)(2,1)S(1)} %get-tuple-element.151), channel_id=1, source_target_pairs={{0,16},{1,17},{2,18},{3,19},{4,20},{5,21},{6,22},{7,23},{8,24},{9,... | collective-permute-start | bytes 393224 | tf_op jit(solution)/shard_map/ppermute | solution.py:96
  (93 other events, 1071.1 us)

commit v2 on v1

v2 whole, which is shorter than its diff:
```python
import functools
import math

import jax
import jax.numpy as jnp
from jax import lax
from jax.experimental import pallas as pl
from jax.experimental.pallas import tpu as pltpu
from jax.sharding import PartitionSpec as P

HEADS = 8
HEAD_DIM = 64
PAIR = 128
EPSILON = 1e-05
MASKED = 1e9
AXES = ("dp", "seq")
F32 = jnp.float32
BF16 = jnp.bfloat16

(
    OUTPUT_BIAS,
    ATTENTION_GAIN,
    ATTENTION_SHIFT,
    SOURCE_QUERY_BIAS,
    SOURCE_VALUE_BIAS,
    SOURCE_OUTPUT_BIAS,
    SOURCE_GAIN,
    SOURCE_SHIFT,
    OUTER_BIAS,
    FINAL_GAIN,
    FINAL_SHIFT,
    INNER_BIAS,
) = range(12)
Z_MASKS = (0, 8, 16, 24)
VM = pl.BlockSpec(memory_space=pltpu.VMEM)
SM = pl.BlockSpec(memory_space=pltpu.SMEM)


def dot(a, b):
    return lax.dot_general(a, b, (((1,), (0,)), ((), ())), preferred_element_type=F32)


def dot_nt(a, b):
    return lax.dot_general(a, b, (((1,), (1,)), ((), ())), preferred_element_type=F32)


def dot_tn(a, b):
    return lax.dot_general(a, b, (((0,), (0,)), ((), ())), preferred_element_type=F32)


def total(values):
    return jnp.sum(values.astype(F32), axis=0, keepdims=True)


def normalize(h):
    average = jnp.mean(h, axis=-1, keepdims=True)
    centered = h - average
    variance = jnp.mean(centered * centered, axis=-1, keepdims=True)
    inverse = lax.rsqrt(variance + EPSILON)
    return centered * inverse, inverse


def normalize_back(upstream, normed, inverse, gain):
    scaled = upstream * gain
    first_mean = jnp.mean(scaled, axis=-1, keepdims=True)
    second_mean = jnp.mean(scaled * normed, axis=-1, keepdims=True)
    return inverse * (scaled - first_mean - normed * second_mean)


def normal_parts(v):
    density = 0.3989422804014327 * jnp.exp(-0.5 * v * v)
    t = 1.0 / (1.0 + 0.2316419 * jnp.abs(v))
    series = t * (
        0.319381530
        + t * (-0.356563782 + t * (1.781477937 + t * (-1.821255978 + t * 1.330274429)))
    )
    tail = density * series
    return jnp.where(v >= 0.0, 1.0 - tail, tail), density


def penalties(ids):
    place = lax.broadcasted_iota(jnp.int32, (PAIR, ids.shape[1]), 0)
    return jnp.where((place == ids) | (place >= 4), 0.0, -MASKED).astype(BF16)


def one_hot(ids):
    place = lax.broadcasted_iota(jnp.int32, (PAIR, ids.shape[1]), 0)
    return jnp.where(place == ids, 1.0, 0.0).astype(F32).T.astype(BF16)


def spread(part, half):
    empty = jnp.zeros_like(part)
    return [part, empty] if half == 0 else [empty, part]


def attend(query_t, keys, value_t, hot, penalty, mixture_t, logs):
    length = keys.shape[0]

    def pair(p, carry):
        columns = pl.ds(pl.multiple_of(p * PAIR, PAIR), PAIR)
        left = jnp.concatenate([keys[:, columns], hot[...]], axis=1)
        for half in range(2):
            rows = pl.ds(pl.multiple_of(p * PAIR + half * HEAD_DIM, HEAD_DIM), HEAD_DIM)
            right = jnp.concatenate(spread(query_t[rows, :], half) + [penalty[...]], axis=0)
            scores = dot(left, right)
            highest = jnp.max(scores, axis=0, keepdims=True)
            weights = jnp.exp(scores - highest).astype(BF16)
            values = jnp.concatenate(
                [value_t[rows, :], jnp.ones((16, length), BF16)], axis=0
            )
            found = dot(values, weights)
            denominator = found[HEAD_DIM : HEAD_DIM + 1, :]
            mixture_t[rows, :] = (found[:HEAD_DIM, :] / denominator).astype(BF16)
            logs[2 * p + half] = highest + jnp.log(denominator)
        return carry

    lax.fori_loop(0, HEADS // 2, pair, 0)


def attend_back(
    query_t, query, keys, key_t, values, slope_t, slope, hot, penalty, logs, deltas,
    query_grad_t, key_grad, value_grad,
):
    tokens = query.shape[0]
    lane = lax.broadcasted_iota(jnp.int32, (tokens, PAIR), 1)

    def pair(p, carry):
        columns = pl.ds(pl.multiple_of(p * PAIR, PAIR), PAIR)
        left = jnp.concatenate([keys[:, columns], hot[...]], axis=1)
        value_pair = values[:, columns]
        key_sum, value_sum = None, None
        for half in range(2):
            rows = pl.ds(pl.multiple_of(p * PAIR + half * HEAD_DIM, HEAD_DIM), HEAD_DIM)
            right = jnp.concatenate(spread(query_t[rows, :], half) + [penalty[...]], axis=0)
            chances = jnp.exp(dot(left, right) - logs[2 * p + half])
            slopes = dot(value_pair, jnp.concatenate(spread(slope_t[rows, :], half), axis=0))
            grads = (chances * (slopes - deltas[2 * p + half])).astype(BF16)
            query_grad_t[rows, :] = dot(key_t[rows, :], grads) * HEAD_DIM**-0.5
            mine = (lane < HEAD_DIM) if half == 0 else (lane >= HEAD_DIM)
            none = jnp.zeros((tokens, PAIR), BF16)
            value_part = dot(chances.astype(BF16), jnp.where(mine, slope[:, columns], none))
            key_part = dot(grads, jnp.where(mine, query[:, columns], none))
            value_sum = value_part if value_sum is None else value_sum + value_part
            key_sum = key_part if key_sum is None else key_sum + key_part
        key_grad[:, columns] = key_sum
        value_grad[:, columns] = value_sum
        return carry

    lax.fori_loop(0, HEADS // 2, pair, 0)


def deltas_of(slope_t, mixture_t, deltas):
    for head in range(HEADS):
        rows = slice(head * HEAD_DIM, (head + 1) * HEAD_DIM)
        deltas[head] = jnp.sum(
            slope_t[rows, :].astype(F32) * mixture_t[rows, :].astype(F32), axis=0, keepdims=True
        )


def swap(array, mask, devices):
    return lax.ppermute(array, AXES, [(i, i ^ mask) for i in range(devices)])


def turned_swap(array, step):
    pairs = []
    for i in range(32):
        near = 2 if i % 2 == 0 else 4
        pairs.append((i, i ^ (near if step == 1 else 6 - near)))
    return lax.ppermute(array, AXES, pairs)


def after(value, *others):
    return lax.optimization_barrier((value, others))[0]


def places(me):
    found = []
    for core in range(2):
        near = jnp.where(((me & 1) ^ core) == 0, 2, 4)
        for far in range(2):
            for step in range(2):
                for at, mask in enumerate(Z_MASKS):
                    device = me ^ (core | mask)
                    if step:
                        device = device ^ near
                    if far:
                        device = device ^ (6 - near)
                    found.append((core, far, step * 4 + at, device))
    return found


def unpack(me, pieces, stride, first, rows, scratch):
    for core, far, slot, device in places(me):
        ref = pieces[2 * core + far]
        at = slot * stride + first
        scratch[pl.ds(pl.multiple_of(device * rows, rows), rows), :] = ref[at : at + rows, :]


def vector_sum(pieces, stride, first):
    found = None
    for ref in pieces:
        for slot in range(8):
            part = ref[slot * stride + first : (slot + 1) * stride, :].astype(F32)
            found = part if found is None else found + part
    return found


class Grads:
    def __init__(self, me, refs, dense, rows):
        self.me, self.refs, self.dense, self.rows = me, refs, dense, rows

    def put(self, index, grad):
        if self.dense is None:
            self.refs[index][...] = grad
            return
        self.dense[...] = grad
        rows = self.rows
        for core, far, slot, device in places(self.me):
            found = self.dense[pl.ds(pl.multiple_of(device * rows, rows), rows), :]
            self.refs[core][far * 8 + slot, index * rows : (index + 1) * rows, :] = found.astype(BF16)

    def put_sums(self, first, sums):
        if self.dense is None:
            self.refs[-1][...] = sums
            return
        low = sums.astype(BF16)
        for ref in self.refs:
            for slot in range(16):
                ref[slot, first : first + sums.shape[0], :] = low


def grad_outs(packed, count, rows, width, sums):
    if packed:
        return [((16, count * rows + sums, width), BF16)] * 2
    return [((width, width), F32)] * count + [((sums, width), F32)]


def call(kernel, outs, args, scratch, micros, name):
    moved = sum(math.prod(a.shape) * a.dtype.itemsize for a in args[1:])
    moved += sum(math.prod(s) * jnp.dtype(d).itemsize for s, d in outs)
    return pl.pallas_call(
        kernel,
        out_shape=[jax.ShapeDtypeStruct(s, d) for s, d in outs],
        in_specs=[SM] + [VM] * (len(args) - 1),
        out_specs=[VM] * len(outs),
        scratch_shapes=[pltpu.VMEM(s, d) for s, d in scratch],
        compiler_params=pltpu.CompilerParams(vmem_limit_bytes=56 << 20),
        cost_estimate=pl.CostEstimate(
            flops=int(micros * 1.15e9), bytes_accessed=moved, transcendentals=0
        ),
        name=name,
    )(*args)


def make_tokens_packet(block, memory_block, width):
    rows = block + memory_block + 8

    def kernel(turn, tokens, memory, target_ids, source_ids, cotangent, sent, kept, cot_sent, cot_kept):
        mine = turn[0]
        for row, out, cot in ((1 - mine, sent, cot_sent), (mine, kept, cot_kept)):
            out[:block, :] = tokens[row]
            out[block : block + memory_block, :] = memory[row]
            ids = target_ids[pl.ds(row, 1), :].astype(F32)
            ids = jnp.concatenate([ids, jnp.zeros((1, width - block), F32)], axis=1)
            others = source_ids[pl.ds(row, 1), :].astype(F32)
            others = jnp.concatenate([others, jnp.zeros((1, width - memory_block), F32)], axis=1)
            place = lax.broadcasted_iota(jnp.int32, (8, width), 0)
            found = jnp.where(place == 0, ids, jnp.where(place == 1, others, 0.0))
            out[block + memory_block :, :] = found.astype(BF16)
            cot[...] = cotangent[row]

    return kernel, [((rows, width), BF16)] * 2 + [((block, width), BF16)] * 2


def placed(me, parts, width):
    here = lax.broadcasted_iota(jnp.int32, (parts.shape[1], width), 0) + me * parts.shape[1]
    lane = lax.broadcasted_iota(jnp.int32, (parts.shape[1], width), 1)
    return dot(parts, jnp.where(lane == here, 1.0, 0.0).astype(BF16))


def make_self_packet(narrow, width):
    def kernel(me_ref, query_w, key_w, value_w, biases, out):
        for i, ref in enumerate((query_w, key_w, value_w)):
            out[i * narrow : (i + 1) * narrow, :] = ref[...]
        found = placed(me_ref[0], biases[...], width)
        out[3 * narrow :, :] = jnp.concatenate([found, jnp.zeros((6, width), F32)], axis=0).astype(BF16)

    return kernel, [((3 * narrow + 8, width), BF16)]


def make_cross_packet(narrow, width, blocks):
    def kernel(me_ref, *refs):
        weights, short, wide, out = refs[:5], refs[5], refs[6], refs[7]
        me = me_ref[0]
        for i, ref in enumerate(weights):
            out[i * narrow : (i + 1) * narrow, :] = ref[...]
        found = placed(me, short[...], width)
        per = width // wide.shape[1]
        row = placed(me % per, wide[...], width)
        place = lax.broadcasted_iota(jnp.int32, (blocks, width), 0)
        spread_row = jnp.where(place == me // per, row, 0.0)
        rest = jnp.zeros((16 - found.shape[0] - blocks, width), F32)
        out[5 * narrow :, :] = jnp.concatenate([found, spread_row, rest], axis=0).astype(BF16)

    return kernel, [((5 * narrow + 16, width), BF16)]


def join(arrays):
    def kernel(*refs):
        at = 0
        for ref in refs[:-1]:
            refs[-1][at : at + ref.shape[0], :] = ref[...]
            at += ref.shape[0]

    rows = sum(a.shape[0] for a in arrays)
    return pl.pallas_call(
        kernel,
        out_shape=jax.ShapeDtypeStruct((rows, arrays[0].shape[1]), arrays[0].dtype),
        in_specs=[VM] * len(arrays),
        out_specs=VM,
        compiler_params=pltpu.CompilerParams(vmem_limit_bytes=16 << 20),
        cost_estimate=pl.CostEstimate(flops=1 << 20, bytes_accessed=0, transcendentals=0),
        name="join",
    )(*arrays)


def make_project(packed, parts, rows, block, memory_block, width, narrow, n_pieces):
    share = rows * block
    length = parts * share
    memory_share = rows * memory_block
    stride = 3 * narrow + 8

    def kernel(*refs):
        me_ref, refs = refs[0], list(refs[1:])
        pieces, refs = refs[:n_pieces], refs[n_pieces:]
        tokens, refs = refs[: parts * rows], refs[parts * rows :]
        query, query_t, keys, values, value_t, memory, ids, memory_ids = refs[:8]
        scratch = refs[8:]
        me = me_ref[0]
        if packed:
            for i in range(3):
                unpack(me, pieces, stride, i * narrow, narrow, scratch[i])
            query_w, key_w, value_w = scratch
            biases = vector_sum(pieces, stride, 3 * narrow)
        else:
            query_w, key_w, value_w = pieces[:3]
            biases = pieces[3][...]
        own = jnp.concatenate([t[:block, :] for t in tokens[:rows]], axis=0)
        scaled = (dot(own, query_w[...]) + biases[0:1, :]).astype(BF16) * BF16(HEAD_DIM**-0.5)
        query[...] = scaled
        query_t[...] = scaled.T
        for i in range(parts):
            here = slice(i * share, (i + 1) * share)
            some = tokens[i * rows : (i + 1) * rows]
            own = jnp.concatenate([t[:block, :] for t in some], axis=0)
            keys[here, :] = dot(own, key_w[...]).astype(BF16)
            found = (dot(own, value_w[...]) + biases[1:2, :]).astype(BF16)
            values[here, :] = found
            value_t[:, here] = found.T
        for i, t in enumerate(tokens):
            memory[i * memory_block : (i + 1) * memory_block, :] = t[block : block + memory_block, :]
            found = t[block + memory_block :, :].astype(F32).astype(jnp.int32)
            ids[:, i * block : (i + 1) * block] = found[0:1, :block]
        found = [t[block + memory_block :, :].astype(F32).astype(jnp.int32)[1:2, :memory_block] for t in tokens]
        memory_ids[...] = jnp.concatenate(found, axis=1)

    outs = [
        ((share, width), BF16),
        ((width, share), BF16),
        ((length, width), BF16),
        ((length, width), BF16),
        ((width, length), BF16),
        ((parts * memory_share, width), BF16),
        ((1, length), jnp.int32),
        ((1, parts * memory_share), jnp.int32),
    ]
    return kernel, outs, [((width, width), BF16)] * 3 if packed else []


def make_self_attention(share, length, width):
    def kernel(me_ref, query_t, keys, value_t, ids, mixture_t, logs, hot, penalty):
        hot[...] = one_hot(ids[...])
        penalty[...] = penalties(ids[:, :share])
        attend(query_t, keys, value_t, hot, penalty, mixture_t, logs)

    outs = [((width, share), BF16), ((HEADS, 1, share), F32)]
    return kernel, outs, [((length, PAIR), BF16), ((PAIR, share), BF16)]


def make_cross_forward(packed, rows, block, memory_length, width, narrow, n_pieces):
    share = rows * block
    stride = 5 * narrow + 16

    def kernel(*refs):
        me_ref, refs = refs[0], list(refs[1:])
        pieces, refs = refs[:n_pieces], refs[n_pieces:]
        tokens, refs = refs[:rows], refs[rows:]
        memory, ids, memory_ids, mixture_t = refs[:4]
        first_sum, second_sum, query, memory_keys, memory_values, cross_t, logs, vectors = refs[4:12]
        scratch = refs[12:]
        query_t, value_t, hot, penalty = scratch[:4]
        if packed:
            for i in range(5):
                unpack(me_ref[0], pieces, stride, i * narrow, narrow, scratch[4 + i])
            output_w, query_w, key_w, value_w, source_w = scratch[4:]
            vectors[...] = vector_sum(pieces, stride, 5 * narrow)
        else:
            output_w, query_w, key_w, value_w, source_w = pieces[:5]
            vectors[...] = pieces[5][...]

        def vector(i):
            return vectors[i : i + 1, :]

        own = jnp.concatenate([t[:block, :] for t in tokens], axis=0)
        h = own.astype(F32) + dot_tn(mixture_t[...], output_w[...]) + vector(OUTPUT_BIAS)
        first_sum[...] = h
        first = normalize(h)[0] * vector(ATTENTION_GAIN) + vector(ATTENTION_SHIFT)
        scaled = (dot(first.astype(BF16), query_w[...]) + vector(SOURCE_QUERY_BIAS)).astype(BF16) * BF16(HEAD_DIM**-0.5)
        query[...] = scaled
        query_t[...] = scaled.T
        memory_keys[...] = dot(memory[...], key_w[...]).astype(BF16)
        memory_values[...] = (dot(memory[...], value_w[...]) + vector(SOURCE_VALUE_BIAS)).astype(BF16)
        value_t[...] = memory_values[...].T
        hot[...] = one_hot(memory_ids[...])
        penalty[...] = penalties(ids[:, :share])
        attend(query_t, memory_keys, value_t, hot, penalty, cross_t, logs)
        first = normalize(first_sum[...])[0] * vector(ATTENTION_GAIN) + vector(ATTENTION_SHIFT)
        second_sum[...] = first + dot_tn(cross_t[...], source_w[...]) + vector(SOURCE_OUTPUT_BIAS)

    outs = [
        ((share, width), F32),
        ((share, width), F32),
        ((share, width), BF16),
        ((memory_length, width), BF16),
        ((memory_length, width), BF16),
        ((width, share), BF16),
        ((HEADS, 1, share), F32),
        ((16, width), F32),
    ]
    scratch = [((width, share), BF16), ((width, memory_length), BF16), ((memory_length, PAIR), BF16), ((PAIR, share), BF16)]
    if packed:
        scratch += [((width, width), BF16)] * 5
    return kernel, outs, scratch


def make_inner(packed, rows, block, width, hidden, narrow, n_pieces):
    blocks = hidden // width
    share = rows * block
    per = width // (blocks * narrow)

    def kernel(*refs):
        me_ref, refs = refs[0], list(refs[1:])
        pieces, refs = refs[:n_pieces], refs[n_pieces:]
        second_sum, cot_own, cot_came, vectors = refs[:4]
        out_own, out_send, back, sums = refs[4:8]
        grads, scratch = refs[8:10], refs[10:]
        low, active, gate, slope = scratch[:4]
        if packed:
            inner_w, outer_w, gathered = scratch[4:7]
            whole = pieces[0]
            for device in range(32):
                at = device * 2 * blocks * narrow
                for i in range(blocks):
                    inner_w[i, device * narrow : (device + 1) * narrow, :] = whole[at + i * narrow : at + (i + 1) * narrow, :]
                row = (device % per) * blocks * narrow
                outer_w[device // per, row : row + blocks * narrow, :] = whole[at + blocks * narrow : at + 2 * blocks * narrow, :]
        else:
            inner_w, outer_w = pieces

        def vector(i):
            return vectors[i : i + 1, :]

        second = normalize(second_sum[...])[0] * vector(SOURCE_GAIN) + vector(SOURCE_SHIFT)
        low[...] = second.astype(BF16)
        back[...] = second + vector(OUTER_BIAS)

        def forward(i, carry):
            inner = dot(low[...], inner_w[i]) + vectors[pl.ds(INNER_BIAS + i, 1), :]
            chance, density = normal_parts(inner)
            found = (inner * chance).astype(BF16)
            active[i] = found
            gate[i] = chance + inner * density
            back[...] += dot(found, outer_w[i])
            return carry

        lax.fori_loop(0, blocks, forward, 0)
        normed, inverse = normalize(back[...])
        final = normed * vector(FINAL_GAIN) + vector(FINAL_SHIFT)
        out_own[...] = final[:block, :]
        out_send[...] = final[block:, :].astype(BF16)
        upstream = jnp.concatenate([cot_own[...], cot_came[...]], axis=0).astype(F32)
        sums[0:1, :] = total(upstream * normed)
        sums[1:2, :] = total(upstream)
        back3 = normalize_back(upstream, normed, inverse, vector(FINAL_GAIN))
        slope[...] = back3.astype(BF16)
        sums[2:3, :] = total(slope[...])
        sums[7:8, :] = jnp.zeros_like(sums[7:8, :])
        back[...] = back3

        def backward(i, carry):
            grad = dot_nt(slope[...], outer_w[i]) * gate[i]
            inner_low = grad.astype(BF16)
            sums[pl.ds(3 + i, 1), :] = total(inner_low)
            outer_grad = dot_tn(active[i], slope[...])
            inner_grad = dot_tn(low[...], inner_low)
            back[...] += dot_nt(inner_low, inner_w[i])
            if packed:
                gathered[i] = inner_grad
                gathered[blocks + i] = outer_grad
            else:
                grads[0][i] = inner_grad
                grads[1][i] = outer_grad
            return carry

        lax.fori_loop(0, blocks, backward, 0)
        if packed:
            tall = blocks * narrow
            for core, far, slot, device in places(me_ref[0]):
                ref, at = grads[core], far * 8 + slot
                row = pl.multiple_of(device * narrow, narrow)
                for i in range(blocks):
                    ref[at, i * narrow : (i + 1) * narrow, :] = gathered[i, pl.ds(row, narrow), :].astype(BF16)
                row = pl.multiple_of((device % per) * tall, tall)
                ref[at, tall:, :] = gathered[blocks + device // per, pl.ds(row, tall), :].astype(BF16)

    outs = [((block, width), F32), ((block, width), BF16), ((share, width), F32), ((8, width), F32)]
    if packed:
        outs += [((16, 2 * blocks * narrow, width), BF16)] * 2
    else:
        outs += [((blocks, width, width), F32)] * 2
    scratch = [((share, width), BF16), ((blocks, share, width), BF16), ((blocks, share, width), F32), ((share, width), BF16)]
    if packed:
        scratch += [((blocks, width, width), BF16)] * 2 + [((2 * blocks, width, width), F32)]
    return kernel, outs, scratch


def make_cross_back(packed, parts, share, memory_share, width, narrow, n_pieces):
    memory_length = parts * memory_share
    stride = 5 * narrow + 16

    def kernel(*refs):
        me_ref, refs = refs[0], list(refs[1:])
        pieces, refs = refs[:n_pieces], refs[n_pieces:]
        (back2_in, first_sum, second_sum, query, memory_keys, memory_values, cross_t, logs, ids,
         memory_ids, mixture_t, vectors, sums_inner) = refs[:13]
        refs = refs[13:]
        back1, self_slope, self_slope_t, self_deltas, key_own, value_own = refs[:6]
        sends, refs = refs[6 : 6 + parts - 1], refs[6 + parts - 1 :]
        n_grads = 2 if packed else 4
        grad_refs, scratch = refs[:n_grads], refs[n_grads:]
        (slope_t, slope, key_t, hot, penalty, query_t, deltas, query_grad_t, key_grad, value_grad, sums) = scratch[:11]
        if packed:
            for i, at in enumerate((0, 1, 4)):
                unpack(me_ref[0], pieces, stride, at * narrow, narrow, scratch[11 + i])
            output_w, query_w, source_w = scratch[11:14]
        else:
            output_w, query_w, source_w = pieces
        grads = Grads(me_ref[0], grad_refs, scratch[14] if packed else None, narrow)

        def vector(i):
            return vectors[i : i + 1, :]

        sums[0:7, :] = sums_inner[0:7, :]
        upstream = back2_in[...]
        normed, inverse = normalize(second_sum[...])
        sums[7:8, :] = total(upstream * normed)
        sums[8:9, :] = total(upstream)
        back2 = normalize_back(upstream, normed, inverse, vector(SOURCE_GAIN))
        back1[...] = back2
        cross_low = back2.astype(BF16)
        sums[9:10, :] = total(cross_low)
        grads.put(0, dot(cross_t[...], cross_low))
        found = dot_nt(cross_low, source_w[...]).astype(BF16)
        slope[...] = found
        slope_t[...] = found.T
        deltas_of(slope_t, cross_t, deltas)
        query_t[...] = query[...].T
        key_t[...] = memory_keys[...].T
        hot[...] = one_hot(memory_ids[...])
        penalty[...] = penalties(ids[:, :share])
        attend_back(query_t, query, memory_keys, key_t, memory_values, slope_t, slope, hot, penalty,
                    logs, deltas, query_grad_t, key_grad, value_grad)
        key_own[...] = key_grad[:memory_share, :]
        value_own[...] = value_grad[:memory_share, :]
        for i in range(1, parts):
            here = slice(i * memory_share, (i + 1) * memory_share)
            sends[i - 1][:memory_share, :] = key_grad[here, :].astype(BF16)
            sends[i - 1][memory_share:, :] = value_grad[here, :].astype(BF16)
        query_low = query_grad_t[...].T.astype(BF16)
        sums[10:11, :] = total(query_low)
        normed, inverse = normalize(first_sum[...])
        first_low = (normed * vector(ATTENTION_GAIN) + vector(ATTENTION_SHIFT)).astype(BF16)
        grads.put(1, dot_tn(first_low, query_low))
        upstream = back1[...] + dot_nt(query_low, query_w[...])
        sums[11:12, :] = total(upstream * normed)
        sums[12:13, :] = total(upstream)
        grad = normalize_back(upstream, normed, inverse, vector(ATTENTION_GAIN))
        back1[...] = grad
        branch_low = grad.astype(BF16)
        sums[13:14, :] = total(branch_low)
        sums[14:16, :] = jnp.zeros_like(sums[14:16, :])
        grads.put_sums(3 * narrow, sums[...])
        grads.put(2, dot(mixture_t[...], branch_low))
        found = dot_nt(branch_low, output_w[...]).astype(BF16)
        self_slope[...] = found
        self_slope_t[...] = found.T
        deltas_of(self_slope_t, mixture_t, self_deltas)

    outs = [
        ((share, width), F32),
        ((share, width), BF16),
        ((width, share), BF16),
        ((HEADS, 1, share), F32),
        ((memory_share, width), F32),
        ((memory_share, width), F32),
    ]
    outs += [((2 * memory_share, width), BF16)] * (parts - 1)
    outs += grad_outs(packed, 3, narrow, width, 16)
    scratch = [
        ((width, share), BF16),
        ((share, width), BF16),
        ((width, memory_length), BF16),
        ((memory_length, PAIR), BF16),
        ((PAIR, share), BF16),
        ((width, share), BF16),
        ((HEADS, 1, share), F32),
        ((width, share), F32),
        ((memory_length, width), F32),
        ((memory_length, width), F32),
        ((16, width), F32),
    ]
    if packed:
        scratch += [((width, width), BF16)] * 3 + [((width, width), F32)]
    return kernel, outs, scratch


def make_self_back(packed, parts, rows, block, memory_block, width, narrow, n_pieces, n_others):
    share, memory_share = rows * block, rows * memory_block
    length = parts * share

    def kernel(*refs):
        me_ref, refs = refs[0], list(refs[1:])
        pieces, refs = refs[:n_pieces], refs[n_pieces:]
        others, refs = refs[:n_others], refs[n_others:]
        tokens, refs = refs[:rows], refs[rows:]
        (query, keys, values, slope, slope_t, logs, deltas, ids, back1, memory_key_own,
         memory_value_own) = refs[:11]
        memory_received, refs = refs[11 : 11 + parts - 1], refs[11 + parts - 1 :]
        in_part, key_own, value_own, memory_own, memory_send = refs[:5]
        sends, refs = refs[5 : 5 + parts - 1], refs[5 + parts - 1 :]
        n_grads = 2 if packed else 4
        grad_refs, scratch = refs[:n_grads], refs[n_grads:]
        query_t, key_t, hot, penalty, query_grad_t, key_grad, value_grad, sums = scratch[:8]
        me = me_ref[0]
        if packed:
            unpack(me, pieces, 3 * narrow + 8, 0, narrow, scratch[8])
            for i in range(2):
                unpack(me, others, 5 * narrow + 16, (2 + i) * narrow, narrow, scratch[9 + i])
            query_w, source_key, source_value = scratch[8:11]
        else:
            (query_w,) = pieces
            source_key, source_value = others
        grads = Grads(me, grad_refs, scratch[11] if packed else None, narrow)
        query_t[...] = query[...].T
        key_t[...] = keys[...].T
        hot[...] = one_hot(ids[...])
        penalty[...] = penalties(ids[:, :share])
        attend_back(query_t, query, keys, key_t, values, slope_t, slope, hot, penalty, logs, deltas,
                    query_grad_t, key_grad, value_grad)
        key_own[...] = key_grad[:share, :]
        value_own[...] = value_grad[:share, :]
        for i in range(1, parts):
            here = slice(i * share, (i + 1) * share)
            sends[i - 1][:share, :] = key_grad[here, :].astype(BF16)
            sends[i - 1][share:, :] = value_grad[here, :].astype(BF16)
        query_low = query_grad_t[...].T.astype(BF16)
        own = jnp.concatenate([t[:block, :] for t in tokens], axis=0)
        in_part[...] = back1[...] + dot_nt(query_low, query_w[...])
        sums[0:1, :] = total(query_low)
        grads.put(0, dot_tn(own, query_low))
        memory = jnp.concatenate([t[block : block + memory_block, :] for t in tokens], axis=0)
        key_sum, value_sum = memory_key_own[...], memory_value_own[...]
        for ref in memory_received:
            key_sum = key_sum + ref[:memory_share, :].astype(F32)
            value_sum = value_sum + ref[memory_share:, :].astype(F32)
        key_low, value_low = key_sum.astype(BF16), value_sum.astype(BF16)
        sums[1:2, :] = total(value_low)
        sums[2:8, :] = jnp.zeros_like(sums[2:8, :])
        grads.put_sums(3 * narrow, sums[...])
        grads.put(1, dot_tn(memory, key_low))
        grads.put(2, dot_tn(memory, value_low))
        grad = dot_nt(key_low, source_key[...]) + dot_nt(value_low, source_value[...])
        memory_own[...] = grad[:memory_block, :]
        memory_send[...] = grad[memory_block:, :].astype(BF16)

    outs = [((share, width), F32)] * 3 + [((memory_block, width), F32), ((memory_block, width), BF16)]
    outs += [((2 * share, width), BF16)] * (parts - 1)
    outs += grad_outs(packed, 3, narrow, width, 8)
    scratch = [
        ((width, share), BF16),
        ((width, length), BF16),
        ((length, PAIR), BF16),
        ((PAIR, share), BF16),
        ((width, share), F32),
        ((length, width), F32),
        ((length, width), F32),
        ((8, width), F32),
    ]
    if packed:
        scratch += [((width, width), BF16)] * 3 + [((width, width), F32)]
    return kernel, outs, scratch


def make_last(packed, parts, rows, block, memory_block, width, narrow, n_pieces):
    share = rows * block

    def kernel(*refs):
        me_ref, refs = refs[0], list(refs[1:])
        pieces, refs = refs[:n_pieces], refs[n_pieces:]
        tokens, refs = refs[:rows], refs[rows:]
        in_part, key_own, value_own, memory_send = refs[:4]
        received, refs = refs[4 : 4 + parts - 1], refs[4 + parts - 1 :]
        in_own, in_send = refs[:2]
        n_grads = 2 if packed else 3
        grad_refs, scratch = refs[2 : 2 + n_grads], refs[2 + n_grads :]
        sums = scratch[0]
        me = me_ref[0]
        if packed:
            for i in range(2):
                unpack(me, pieces, 3 * narrow + 8, (1 + i) * narrow, narrow, scratch[1 + i])
            key_w, value_w = scratch[1:3]
        else:
            key_w, value_w = pieces
        grads = Grads(me, grad_refs, scratch[3] if packed else None, narrow)
        own = jnp.concatenate([t[:block, :] for t in tokens], axis=0)
        key_sum, value_sum = key_own[...], value_own[...]
        for ref in received:
            key_sum = key_sum + ref[:share, :].astype(F32)
            value_sum = value_sum + ref[share:, :].astype(F32)
        key_low, value_low = key_sum.astype(BF16), value_sum.astype(BF16)
        sums[0:1, :] = total(value_low)
        sums[1:8, :] = jnp.zeros_like(sums[1:8, :])
        grads.put_sums(2 * narrow, sums[...])
        grads.put(0, dot_tn(own, key_low))
        grads.put(1, dot_tn(own, value_low))
        grad = in_part[...] + dot_nt(key_low, key_w[...]) + dot_nt(value_low, value_w[...])
        in_own[...] = grad[:block, :]
        in_send[:block, :] = grad[block:, :].astype(BF16)
        in_send[block:, :] = memory_send[...]

    outs = [((block, width), F32), ((block + memory_block, width), BF16)]
    outs += grad_outs(packed, 2, narrow, width, 8)
    scratch = [((8, width), F32)]
    if packed:
        scratch += [((width, width), BF16)] * 2 + [((width, width), F32)]
    return kernel, outs, scratch


def combine(arrays, splits):
    count = arrays[0].shape[0] // splits
    shape = (count,) + arrays[0].shape[1:]

    def kernel(*refs):
        given, outs = refs[: len(arrays)], refs[len(arrays) :]
        for i, out in enumerate(outs):
            here = slice(i * count, (i + 1) * count)
            found = given[0][here].astype(F32)
            for ref in given[1:]:
                found = found + ref[here].astype(F32)
            out[...] = found.astype(out.dtype)

    return pl.pallas_call(
        kernel,
        out_shape=[jax.ShapeDtypeStruct(shape, BF16)] * splits,
        in_specs=[VM] * len(arrays),
        out_specs=[VM] * splits,
        compiler_params=pltpu.CompilerParams(vmem_limit_bytes=32 << 20),
        cost_estimate=pl.CostEstimate(flops=1 << 20, bytes_accessed=0, transcendentals=0),
        name="combine",
    )(*arrays)


def finish(me_array, arrays, plan, shapes, name):
    def kernel(me_ref, *refs):
        given, outs = refs[: len(arrays)], refs[len(arrays) :]
        found = given[0][0].astype(F32)
        for ref in given[1:]:
            found = found + ref[0].astype(F32)
        plan(me_ref[0], found, outs)

    return call(kernel, [(s, F32) for s in shapes], (me_array, *arrays), [], 0.5, name)


def chosen(me, rows, wide):
    width = rows.shape[1]
    line = lax.broadcasted_iota(jnp.int32, (width, wide), 0)
    here = lax.broadcasted_iota(jnp.int32, (width, wide), 1) + me * wide
    choice = jnp.where(line == here, 1.0, 0.0)
    return lax.dot_general(rows, choice, (((1,), (0,)), ((), ())), precision=lax.Precision.HIGHEST, preferred_element_type=F32)


def reduce_all(array, devices):
    mask = 1
    while mask < devices:
        array = array + swap(array, mask, devices)
        mask *= 2
    return array


def per_device(
    tokens, memory, target_ids, source_ids, cotangent,
    query_weight, key_weight, value_weight, output_weight, query_bias, value_bias, output_bias,
    attention_gain, attention_shift,
    source_query, source_key, source_value, source_output, source_query_bias, source_value_bias,
    source_output_bias, source_gain, source_shift,
    inner_weight, inner_bias, outer_weight, outer_bias, final_gain, final_shift,
    *, devices, sequence,
):
    packed = devices == 32
    rows, block, width = tokens.shape
    memory_block = memory.shape[1]
    parts = sequence // rows
    share, memory_share = rows * block, rows * memory_block
    hidden = inner_weight.shape[1]
    blocks = hidden // width
    me = lax.axis_index(AXES)
    me_array = me.reshape(1).astype(jnp.int32)
    turn = lax.rem(lax.div(me, parts), rows)
    narrow, wide = width // devices, hidden // devices

    def run(made, micros, name, *args):
        kernel, outs, scratch = made
        return call(kernel, outs, (me_array,) + args, scratch, micros, name)

    short_self = jnp.stack([query_bias, value_bias])
    short_cross = jnp.stack([output_bias, attention_gain, attention_shift, source_query_bias,
                             source_value_bias, source_output_bias, source_gain, source_shift,
                             outer_bias, final_gain, final_shift])
    inner_rows = inner_weight.reshape(narrow, blocks, width).transpose(1, 0, 2).reshape(blocks * narrow, width)

    def whole(array):
        return lax.all_gather(array, AXES, axis=0, tiled=True)

    kernel, outs = make_tokens_packet(block, memory_block, width)
    sent, kept, cot_sent, cot_own = call(
        kernel, outs, (turn.reshape(1).astype(jnp.int32), tokens, memory, target_ids, source_ids, cotangent),
        [], 2.0, "tokens_packet",
    )

    if packed:
        set_inner = [whole(jnp.concatenate([inner_rows, outer_weight], axis=0))]
        kernel, outs = make_self_packet(narrow, width)
        (first,) = call(kernel, outs, (me_array, query_weight, key_weight, value_weight, short_self), [], 1.0, "self_packet")
        kernel, outs = make_cross_packet(narrow, width, blocks)
        (second,) = call(kernel, outs, (me_array, output_weight, source_query, source_key, source_value,
                         source_output, short_cross, inner_bias.reshape(1, wide)), [], 1.0, "cross_packet")
        first_z = [swap(first, m, 32) for m in Z_MASKS[1:]]
        came = swap(sent, parts, devices)
        second = after(second, *first_z)
        second_z = [swap(second, m, 32) for m in Z_MASKS[1:]]
        first_a = join(after([first, *first_z], sent))
        first_b = turned_swap(first_a, 1)
        first_c = join([first_a, first_b])
        first_d = turned_swap(first_c, 2)
        set_self = [first_c, first_d, swap(first_c, 1, 32), swap(first_d, 1, 32)]
        second_a = after(join([second, *second_z]), first_b)
        second_b = turned_swap(second_a, 1)
    else:
        came = swap(sent, parts, devices)
        full = [whole(w) for w in (query_weight, key_weight, value_weight, output_weight, source_query, source_key, source_value, source_output)]
        lane = lax.broadcasted_iota(jnp.int32, (1, width), 1)
        place = lax.broadcasted_iota(jnp.int32, (blocks, width), 0) * width + lane
        spread_wide = jnp.where(place // wide == me, jnp.tile(inner_bias.reshape(1, wide), (blocks, width // wide)), 0)

        def natural(short):
            return jnp.where(lane // narrow == me, jnp.tile(short, (1, devices)), 0)

        vectors = jnp.concatenate([natural(short_self), jnp.zeros((6, width), BF16), natural(short_cross), spread_wide, jnp.zeros((1, width), BF16)])
        vectors = reduce_all(vectors, devices).astype(F32)
        set_self = full[:3] + [vectors[:8]]
        set_cross = full[3:] + [vectors[8:]]
        set_inner = [
            whole(inner_weight).reshape(width, blocks, width).transpose(1, 0, 2),
            whole(outer_weight).reshape(blocks, width, width),
        ]
    row_tokens = [kept, came]
    for m in range(1, parts):
        row_tokens += [swap(kept, m, devices), swap(came, m, devices)]
    own_tokens = row_tokens[:rows]
    if packed:
        set_self[0] = after(set_self[0], *second_z)
    query, query_t, keys, values, value_t, row_memory, ids, memory_ids = run(
        make_project(packed, parts, rows, block, memory_block, width, narrow, len(set_self)), 4.0,
        "project", *set_self, *row_tokens,
    )
    if packed:
        second_c = join([second_a, second_b])
        second_d = turned_swap(second_c, 2)
        query_t = after(query_t, second_c)
        cot_sent = after(cot_sent, second_c)
        set_cross = [second_c, second_d, swap(second_c, 1, 32), swap(second_d, 1, 32)]
        set_back, set_query, set_last, set_memory = set_cross, set_self, set_self, set_cross
    else:
        set_back, set_query, set_last, set_memory = [full[3], full[4], full[7]], full[:1], full[1:3], full[5:7]
    cot_came = swap(cot_sent, parts, devices)
    mixture_t, logs = run(
        make_self_attention(share, parts * share, width), 9.0, "self_attention",
        query_t, keys, value_t, ids,
    )
    first_sum, second_sum, cross_query, memory_keys, memory_values, cross_t, cross_logs, vectors = run(
        make_cross_forward(packed, rows, block, parts * memory_share, width, narrow, len(set_cross)),
        9.0, "cross_forward", *set_cross, *own_tokens, row_memory, ids, memory_ids, mixture_t,
    )
    out_own, out_send, back2_in, sums_inner, *grads_inner = run(
        make_inner(packed, rows, block, width, hidden, narrow, len(set_inner)), 18.0, "inner",
        *set_inner, second_sum, cot_own, cot_came, vectors,
    )
    found = run(
        make_cross_back(packed, parts, share, memory_share, width, narrow, len(set_back)), 14.0,
        "cross_back", *set_back, back2_in, first_sum, second_sum, cross_query, memory_keys,
        memory_values, cross_t, cross_logs, ids, memory_ids, mixture_t, vectors, sums_inner,
    )
    back1, slope, slope_t, deltas, memory_key_own, memory_value_own = found[:6]
    memory_sends, grads_cross = found[6 : 6 + parts - 1], found[6 + parts - 1 :]
    memory_received = [swap(a, m + 1, devices) for m, a in enumerate(memory_sends)]
    if packed:
        keep, send = combine([grads_inner[0], swap(grads_inner[1], 1, 32)], 2)
        query = after(query, keep)
        inner_step = [keep, turned_swap(send, 2)]
    found = run(
        make_self_back(packed, parts, rows, block, memory_block, width, narrow, len(set_query), len(set_memory)),
        17.0, "self_back", *set_query, *set_memory, *own_tokens, query, keys, values, slope, slope_t,
        logs, deltas, ids, back1, memory_key_own, memory_value_own, *memory_received,
    )
    in_part, key_own, value_own, memory_own, memory_send = found[:5]
    received = [swap(a, m + 1, devices) for m, a in enumerate(found[5 : 5 + parts - 1])]
    grads_query = found[5 + parts - 1 :]
    if packed:
        keep, send = combine([grads_cross[0], swap(grads_cross[1], 1, 32)], 2)
        cross_step = [keep, turned_swap(send, 2)]
        keep_inner, send_inner = combine(inner_step, 2)
        key_own = after(key_own, keep, keep_inner)
        inner_step = [keep_inner, turned_swap(send_inner, 1)]
    in_own, in_send, *grads_last = run(
        make_last(packed, parts, rows, block, memory_block, width, narrow, len(set_last)), 6.0,
        "last", *set_last, *own_tokens, in_part, key_own, value_own, memory_send, *received,
    )

    def regroup(mine, came):
        came = came.astype(F32)
        return jnp.where(turn == 0, jnp.stack([mine, came]), jnp.stack([came, mine]))

    output = regroup(out_own, swap(out_send, parts, devices))
    in_came = swap(in_send, parts, devices)
    input_gradient = regroup(in_own, in_came[:block])
    memory_gradient = regroup(memory_own, in_came[block:])

    if packed:
        def lower(arrays):
            found = combine(arrays, 4)
            return [found[0]] + [swap(a, m, 32) for a, m in zip(found[1:], Z_MASKS[1:])]

        def rest(grads):
            keep, send = combine([grads[0], swap(grads[1], 1, 32)], 2)
            keep, send = combine([keep, turned_swap(send, 2)], 2)
            return lower([keep, turned_swap(send, 1)])

        def inner_plan(me, found, outs):
            for i in range(blocks):
                outs[0][:, i * width : (i + 1) * width] = found[i * narrow : (i + 1) * narrow, :]
            outs[1][...] = found[blocks * narrow :, :]

        def cross_plan(me, found, outs):
            for i in range(3):
                outs[i][...] = found[i * narrow : (i + 1) * narrow, :]
            sums = found[3 * narrow :, :]
            outs[3][...] = chosen(me, sums, narrow)
            per = width // wide
            line = lax.broadcasted_iota(jnp.int32, (blocks, width), 0)
            row = jnp.sum(jnp.where(line == me // per, sums[3 : 3 + blocks, :], 0.0), axis=0, keepdims=True)
            outs[4][...] = chosen(me % per, row, wide)

        def query_plan(me, found, outs):
            for i in range(3):
                outs[i][...] = found[i * narrow : (i + 1) * narrow, :]
            outs[3][...] = chosen(me, found[3 * narrow :, :], narrow)

        def last_plan(me, found, outs):
            for i in range(2):
                outs[i][...] = found[i * narrow : (i + 1) * narrow, :]
            outs[2][...] = chosen(me, found[2 * narrow :, :], narrow)

        part = (narrow, width)
        inner_step = lower(inner_step)
        keep, send = combine(cross_step, 2)
        cross_step = lower([keep, turned_swap(send, 1)])
        inner_share, outer_share = finish(me_array, inner_step, inner_plan, [(narrow, hidden), (wide, width)], "finish_inner")
        source_output_share, source_query_share, output_share, sums, inner_bias_share = finish(
            me_array, cross_step, cross_plan, [part] * 3 + [(16, narrow), (1, wide)], "finish_cross"
        )
        query_share, source_key_share, source_value_share, sums_query = finish(
            me_array, rest(grads_query), query_plan, [part] * 3 + [(8, narrow)], "finish_query"
        )
        key_share, value_share, sums_last = finish(
            me_array, rest(grads_last), last_plan, [part] * 2 + [(8, narrow)], "finish_last"
        )
        inner_bias_share = inner_bias_share.reshape(wide)
    else:
        def scatter(array):
            return lax.psum_scatter(array, AXES, scatter_dimension=0, tiled=True)

        inner_share = scatter(grads_inner[0].transpose(1, 0, 2).reshape(width, hidden))
        outer_share = scatter(grads_inner[1].reshape(hidden, width))
        source_output_share, source_query_share, output_share = (scatter(g) for g in grads_cross[:3])
        query_share, source_key_share, source_value_share = (scatter(g) for g in grads_query[:3])
        key_share, value_share = (scatter(g) for g in grads_last[:2])
        sums = jnp.concatenate([grads_cross[3], grads_query[3], grads_last[2]], axis=0)
        sums = reduce_all(sums, devices)
        inner_bias_share = lax.dynamic_slice(sums[3 : 3 + blocks].reshape(hidden), (me * wide,), (wide,))
        sums = lax.dynamic_slice(sums, (0, me * narrow), (sums.shape[0], narrow))
        sums, sums_query, sums_last = sums[:16], sums[16:24], sums[24:]
    return (
        output,
        input_gradient,
        memory_gradient,
        query_share,
        key_share,
        value_share,
        output_share,
        sums_query[0],
        sums_last[0],
        sums[13],
        sums[11],
        sums[12],
        source_query_share,
        source_key_share,
        source_value_share,
        source_output_share,
        sums[10],
        sums_query[1],
        sums[9],
        sums[7],
        sums[8],
        inner_share,
        inner_bias_share,
        outer_share,
        sums[2],
        sums[0],
        sums[1],
    )


def solution(mesh):
    sequence, devices = mesh.shape["seq"], mesh.size
    tokens, ids = P("dp", "seq", None), P("dp", "seq")
    matrix, vector = P(AXES, None), P(AXES)
    attention = (matrix,) * 4 + (vector,) * 5
    inner = (matrix, vector, matrix, vector, vector, vector)
    return jax.shard_map(
        functools.partial(per_device, devices=devices, sequence=sequence),
        mesh=mesh,
        in_specs=(tokens, tokens, ids, ids, tokens) + attention + attention + inner,
        out_specs=(tokens, tokens, tokens) + attention + attention + inner,
        check_vma=False,
    )
```

time: 289 us -> 246 us (0.85)
  waiting for transfers between devices: 103 us -> 55.5 us
  starting transfers between devices: 78.7 us -> 55.6 us
  Pallas kernels: 77.9 us -> 97.8 us
  between operations: 1.48 us -> 14.7 us
  local copies, waits for them, and re-layouts: 22.2 us -> 15 us
    ppermute x75 -> x34, waiting for transfers between devices: 103 us -> 19.8 us  [swap(): return lax.ppermute(array, AXES, [(i, i ^ mask) for i in range(devices)])]
    ppermute x75 -> x34, starting transfers between devices: 78.7 us -> 42 us  [swap(): return lax.ppermute(array, AXES, [(i, i ^ mask) for i in range(devices)])]
    ppermute x0 -> x12, waiting for transfers between devices: none -> 35.6 us  [turned_swap(): return lax.ppermute(array, AXES, pairs)]
    pallas_call x6 -> x14, Pallas kernels: 76.3 us -> 94.8 us  [call(): pl.pallas_call(kernel, out_shape=[jax.ShapeDtypeStruct(s, d) for s, d in...]
    ppermute x0 -> x12, starting transfers between devices: none -> 13.5 us  [turned_swap(): return lax.ppermute(array, AXES, pairs)]
    dynamic_slice x9 -> x0, local copies, waits for them, and re-layouts: 4.7 us -> none  [the longest x7 4.1 us: narrow_part(): return lax.dynamic_slice(sums[row], (me * narrow,), (narrow,))]
    concatenate x10 -> x0, local copies, waits for them, and re-layouts: 2.9 us -> none  [the longest x2 0.72 us: packet(): return gather_tree(jnp.concatenate(arrays, axis=0), layout)]
    unnamed x108 -> x106, local copies, waits for them, and re-layouts: 8.09 us -> 8.99 us
  transfers between devices with their start and end apart: 75 -> 47, of which waited for: 27 -> 17; matrix products, arithmetic and copies ran while one was open for 7% -> 3% of each run, Pallas kernels for 16% -> 32%
where the time goes in v2:
time: 246 us; the launch traced here: 244 us
  Pallas kernels  97.8 us (40%)
  starting transfers between devices  55.6 us (23%)
  waiting for transfers between devices  55.5 us (23%)
  local copies, waits for them, and re-layouts  15 us (6%)
  between operations  14.7 us (6%)
  other arithmetic  5.7 us (2%)
    pallas_call x14, Pallas kernels, call(): pl.pallas_call(kernel, out_shape=[jax.ShapeDtypeStruct(s, d) for s, d in...  94.8 us
    ppermute x34, starting transfers between devices, swap(): return lax.ppermute(array, AXES, [(i, i ^ mask) for i in range(devices)])  42 us
    ppermute x12, waiting for transfers between devices, turned_swap(): return lax.ppermute(array, AXES, pairs)  35.6 us
    ppermute x34, waiting for transfers between devices, swap(): return lax.ppermute(array, AXES, [(i, i ^ mask) for i in range(devices)])  19.8 us
    ppermute x12, starting transfers between devices, turned_swap(): return lax.ppermute(array, AXES, pairs)  13.5 us
    unnamed x106, local copies, waits for them, and re-layouts  8.99 us
  transfers between devices with their start and end apart: 47, of which 17 were waited for; matrix products, arithmetic and copies ran while one was open for 3% of the time, Pallas kernels for 32%

profile of v2, /device:TPU:0, one launch (start us, length us, event | category | flops | bytes accessed | tf_op | source)
XLA Modules:
  0.0 244.2 jit_solution(16860148105841541977)
XLA Ops:
  12.3 3.0 %collective-permute-start = (bf16[56,512]{1,0:T(8,128)(2,1)}, bf16[56,512]{1,0:T(8,128)(2,1)S(1)}, u32[]{:S(2)}, u32[]{:S(2)}) collective-permute-start(bf16[56,512]{1,0:T(8,128)(2,1)} %self_packet.1.refs_0_), channel_id=1, source_target_pairs={{0,8},{1,9},{2,10},{3,11},{4,12},{5,13},{6,14},{7,15},{8,0},{9,1},... | collective-permute-start | bytes 172040 | tf_op jit(solution)/shard_map/ppermute | solution.py:161
  15.3 2.6 %collective-permute-start.1 = (bf16[56,512]{1,0:T(8,128)(2,1)}, bf16[56,512]{1,0:T(8,128)(2,1)S(1)}, u32[]{:S(2)}, u32[]{:S(2)}) collective-permute-start(bf16[56,512]{1,0:T(8,128)(2,1)} %self_packet.1.refs_0_), channel_id=1, source_target_pairs={{0,16},{1,17},{2,18},{3,19},{4,20},{5,21},{6,22},{7,23},{8,24},{9,... | collective-permute-start | bytes 172040 | tf_op jit(solution)/shard_map/ppermute | solution.py:161
  18.1 2.4 %tokens_packet.1 = (bf16[328,512]{1,0:T(8,128)(2,1)}, bf16[328,512]{1,0:T(8,128)(2,1)}, bf16[256,512]{1,0:T(8,128)(2,1)}, bf16[256,512]{1,0:T(8,128)(2,1)}) custom-call(s32[1]{0:T(128)} %bitcast.17.turn, bf16[2,256,512]{2,1,0:T(8,128)(2,1)} %tokens.1, bf16[2,64,512]{2,1,0:T(8,128)(2,1)} %memory.1, s32[2,256]{1,0:T(2,128)} %target_ids.1, s32[2,64]{1,0:T(2,128)} %source_ids.1, ...), custom_call_target="tpu_custom_call" | custom-call | flops 2300000000 | bytes 2378240 | tf_op jit(solution)/shard_map/tokens_packet/pallas_call | solution.py:241
  27.0 3.2 %collective-permute-done.6.refs_1_ = bf16[224,512]{1,0:T(8,128)(2,1)S(1)} collective-permute-done((bf16[224,512]{1,0:T(8,128)(2,1)S(1)}, bf16[224,512]{1,0:T(8,128)(2,1)S(1)}, u32[]{:S(2)}, u32[]{:S(2)}) %collective-permute-start.6) | collective-permute-done | bytes 229408 | tf_op jit(solution)/shard_map/ppermute | solution.py:169
  46.5 5.5 %collective-permute-done.7.refs_1_ = bf16[384,512]{1,0:T(8,128)(2,1)S(1)} collective-permute-done((bf16[384,512]{1,0:T(8,128)(2,1)S(1)}, bf16[384,512]{1,0:T(8,128)(2,1)S(1)}, u32[]{:S(2)}, u32[]{:S(2)}) %collective-permute-start.7) | collective-permute-done | bytes 393248 | tf_op jit(solution)/shard_map/ppermute | solution.py:169
  53.3 5.2 %collective-permute-done.11.refs_6_.refs_10_ = bf16[328,512]{1,0:T(8,128)(2,1)S(1)} collective-permute-done((bf16[328,512]{1,0:T(8,128)(2,1)S(1)}, bf16[328,512]{1,0:T(8,128)(2,1)S(1)}, u32[]{:S(2)}, u32[]{:S(2)}) %collective-permute-start.11) | collective-permute-done | bytes 335904 | tf_op jit(solution)/shard_map/ppermute | solution.py:161
  62.3 4.9 %project.1 = (bf16[512,512]{1,0:T(8,128)(2,1)}, bf16[512,512]{1,0:T(8,128)(2,1)}, bf16[1024,512]{1,0:T(8,128)(2,1)}, bf16[1024,512]{1,0:T(8,128)(2,1)}, bf16[512...) custom-call(s32[1]{0:T(128)} %bitcast.me_ref.refs_0_, ...), custom_call_target="tpu_custom_call" | custom-call | flops 4600000000 | bytes 7640064 | tf_op jit(solution)/shard_map/project/pallas_call | solution.py:241
  67.3 3.2 %collective-permute-done.8.refs_2_.refs_6_ = bf16[768,512]{1,0:T(8,128)(2,1)S(1)} collective-permute-done((bf16[768,512]{1,0:T(8,128)(2,1)S(1)}, bf16[768,512]{1,0:T(8,128)(2,1)S(1)}, u32[]{:S(2)}, u32[]{:S(2)}) %collective-permute-start.8) | collective-permute-done | bytes 786464 | tf_op jit(solution)/shard_map/ppermute | solution.py:169
  71.6 10.8 %self_attention.1 = (bf16[512,512]{1,0:T(8,128)(2,1)}, f32[8,1,512]{2,1,0:T(1,128)}) custom-call(s32[1]{0:T(128)} %bitcast.me_ref.refs_0_, bf16[512,512]{1,0:T(8,128)(2,1)} %get-tuple-element.146.query_t, bf16[1024,512]{1,0:T(8,128)(2,1)} %get-tuple-element.147.keys.refs_12_, bf16[512,1024]{1,0:T(8,128)(2,1)} %get-tuple-element.148.value_t, ...), custom_call_target="tpu_custom_call" | custom-call | flops 10350000128 | bytes 3166208 | tf_op jit(solution)/shard_map/self_attention/pallas_call | solution.py:241
  83.5 8.8 %cross_forward.1 = (f32[512,512]{1,0:T(8,128)}, f32[512,512]{1,0:T(8,128)}, bf16[512,512]{1,0:T(8,128)(2,1)}, bf16[256,512]{1,0:T(8,128)(2,1)}, bf16[256,512]{1,...) custom-call(s32[1]{0:T(128)} %bitcast.me_ref.refs_0_, ...), custom_call_target="tpu_custom_call" | custom-call | flops 10350000128 | bytes 8328192 | tf_op jit(solution)/shard_map/cross_forward/pallas_call | solution.py:241
  93.0 17.8 %inner.1 = (f32[256,512]{1,0:T(8,128)}, bf16[256,512]{1,0:T(8,128)(2,1)}, f32[512,512]{1,0:T(8,128)}, f32[8,512]{1,0:T(8,128)}, bf16[16,128,512]{2,1,0:T(8,128)(2,1)}, /*index=5*/bf16[16,128,512]{2,1,0:T(8,128)(2,1)}) custom-call(s32[1]{0:T(128)} %bitcast.me_ref.refs_0_, bf16[4096,512]{1,0:T(8,128)(2,1)} %all-gather.2.cloned.1.call-done.refs_1_, ...), custom_call_target="tpu_custom_call" | custom-call | flops 20700000256 | bytes 11845632 | tf_op jit(solution)/shard_map/inner/pallas_call | solution.py:241
  111.1 14.1 %cross_back.1 = (f32[512,512]{1,0:T(8,128)}, bf16[512,512]{1,0:T(8,128)(2,1)}, bf16[512,512]{1,0:T(8,128)(2,1)}, f32[8,1,512]{2,1,0:T(1,128)}, f32[128,512]{1,0:...) custom-call(s32[1]{0:T(128)} %bitcast.me_ref.refs_0_, ...), custom_call_target="tpu_custom_call" | custom-call | flops 16099999744 | bytes 13456384 | tf_op jit(solution)/shard_map/cross_back/pallas_call | solution.py:241
  129.4 20.3 %self_back.1 = (f32[512,512]{1,0:T(8,128)}, f32[512,512]{1,0:T(8,128)}, f32[512,512]{1,0:T(8,128)}, f32[64,512]{1,0:T(8,128)}, bf16[64,512]{1,0:T(8,128)(2,1)}, ...) custom-call(s32[1]{0:T(128)} %bitcast.me_ref.refs_0_, ...), custom_call_target="tpu_custom_call" | custom-call | flops 19549999104 | bytes 17420288 | tf_op jit(solution)/shard_map/self_back/pallas_call | solution.py:241
  152.4 7.1 %collective-permute-done.37.refs_1_ = bf16[8,64,512]{2,1,0:T(8,128)(2,1)S(1)} collective-permute-done((bf16[8,64,512]{2,1,0:T(8,128)(2,1)S(1)}, bf16[8,64,512]{2,1,0:T(8,128)(2,1)S(1)}, u32[]{:S(2)}, u32[]{:S(2)}) %collective-permute-start.37) | collective-permute-done | bytes 524320 | tf_op jit(solution)/shard_map/ppermute | solution.py:169
  162.0 5.3 %collective-permute-done.38.refs_1_ = bf16[4,64,512]{2,1,0:T(8,128)(2,1)S(1)} collective-permute-done((bf16[4,64,512]{2,1,0:T(8,128)(2,1)S(1)}, bf16[4,64,512]{2,1,0:T(8,128)(2,1)S(1)}, u32[]{:S(2)}, u32[]{:S(2)}) %collective-permute-start.38) | collective-permute-done | bytes 262176 | tf_op jit(solution)/shard_map/ppermute | solution.py:169
  167.3 5.0 %collective-permute-start.39 = (bf16[1,64,512]{2,1,0:T(8,128)(2,1)S(1)}, bf16[1,64,512]{2,1,0:T(8,128)(2,1)S(1)}, u32[]{:S(2)}, u32[]{:S(2)}) collective-permute-start(bf16[1,64,512]{2,1,0:T(8,128)(2,1)S(1)} %get-tuple-element.220), channel_id=1, source_target_pairs={{0,8},{1,9},{2,10},{3,11},{4,12},{5,13},{6,14},{7,15},{8,0},{9,1},... | collective-permute-start | bytes 196616 | tf_op jit(solution)/shard_map/ppermute | solution.py:161
  172.3 3.4 %collective-permute-start.40 = (bf16[1,64,512]{2,1,0:T(8,128)(2,1)S(1)}, bf16[1,64,512]{2,1,0:T(8,128)(2,1)S(1)}, u32[]{:S(2)}, u32[]{:S(2)}) collective-permute-start(bf16[1,64,512]{2,1,0:T(8,128)(2,1)S(1)} %get-tuple-element.221), channel_id=1, source_target_pairs={{0,16},{1,17},{2,18},{3,19},{4,20},{5,21},{6,22},{7,23},{8,24},{9,... | collective-permute-start | bytes 196616 | tf_op jit(solution)/shard_map/ppermute | solution.py:161
  177.3 5.4 %last.1 = (f32[256,512]{1,0:T(8,128)}, bf16[320,512]{1,0:T(8,128)(2,1)}, bf16[16,40,512]{2,1,0:T(8,128)(2,1)}, bf16[16,40,512]{2,1,0:T(8,128)(2,1)}) custom-call(s32[1]{0:T(128)} %bitcast.me_ref.refs_0_, bf16[448,512]{1,0:T(8,128)(2,1)} %copy-done.5, bf16[448,512]{1,0:T(8,128)(2,1)} %copy-done.29, bf16[448,512]{1,0:T(8,128)(2,1)} %copy-done.30, ...), custom_call_target="tpu_custom_call" | custom-call | flops 6899999744 | bytes 8929280 | tf_op jit(solution)/shard_map/last/pallas_call | solution.py:241
  193.7 6.0 %collective-permute-done.26.refs_1_ = bf16[8,56,512]{2,1,0:T(8,128)(2,1)S(1)} collective-permute-done((bf16[8,56,512]{2,1,0:T(8,128)(2,1)S(1)}, bf16[8,56,512]{2,1,0:T(8,128)(2,1)S(1)}, u32[]{:S(2)}, u32[]{:S(2)}) %collective-permute-start.26) | collective-permute-done | bytes 458784 | tf_op jit(solution)/shard_map/ppermute | solution.py:169
  203.7 2.5 %collective-permute-done.27.refs_1_ = bf16[4,56,512]{2,1,0:T(8,128)(2,1)S(1)} collective-permute-done((bf16[4,56,512]{2,1,0:T(8,128)(2,1)S(1)}, bf16[4,56,512]{2,1,0:T(8,128)(2,1)S(1)}, u32[]{:S(2)}, u32[]{:S(2)}) %collective-permute-start.27) | collective-permute-done | bytes 229408 | tf_op jit(solution)/shard_map/ppermute | solution.py:169
  206.8 2.4 collective-permute-start.29
  212.2 3.0 %collective-permute-start.44 = (bf16[1,128,512]{2,1,0:T(8,128)(2,1)S(1)}, bf16[1,128,512]{2,1,0:T(8,128)(2,1)S(1)}, u32[]{:S(2)}, u32[]{:S(2)}) collective-permute-start(bf16[1,128,512]{2,1,0:T(8,128)(2,1)S(1)} %get-tuple-element.234), channel_id=1, source_target_pairs={{0,16},{1,17},{2,18},{3,19},{4,20},{5,21},{6,22},{7,23},{8,24},{9,... | collective-permute-start | bytes 393224 | tf_op jit(solution)/shard_map/ppermute | solution.py:161
  221.4 3.0 %collective-permute-done.33.refs_1_ = bf16[4,40,512]{2,1,0:T(8,128)(2,1)S(1)} collective-permute-done((bf16[4,40,512]{2,1,0:T(8,128)(2,1)S(1)}, bf16[4,40,512]{2,1,0:T(8,128)(2,1)S(1)}, u32[]{:S(2)}, u32[]{:S(2)}) %collective-permute-start.33) | collective-permute-done | bytes 163872 | tf_op jit(solution)/shard_map/ppermute | solution.py:169
  225.1 3.0 %collective-permute-start.35 = (bf16[1,40,512]{2,1,0:T(8,128)(2,1)S(1)}, bf16[1,40,512]{2,1,0:T(8,128)(2,1)S(1)}, u32[]{:S(2)}, u32[]{:S(2)}) collective-permute-start(bf16[1,40,512]{2,1,0:T(8,128)(2,1)S(1)} %get-tuple-element.212), channel_id=1, source_target_pairs={{0,16},{1,17},{2,18},{3,19},{4,20},{5,21},{6,22},{7,23},{8,24},{9,... | collective-permute-start | bytes 122888 | tf_op jit(solution)/shard_map/ppermute | solution.py:161
  (220 shorter events, 81.9 us)
Async XLA Ops:
  7.2 85.1 %all-gather.2.cloned.1.call-start = ((), (), s32[]{:S(2)}) async-start(), calls=%async_computation | async-start | bytes 4325376 | tf_op jit(solution)/shard_map/all_gather | solution.py:842
  30.3 15.7 %collective-permute-start.12 = (bf16[448,512]{1,0:T(8,128)(2,1)S(1)}, bf16[448,512]{1,0:T(8,128)(2,1)S(1)}, u32[]{:S(2)}, u32[]{:S(2)}) collective-permute-start(bf16[448,512]{1,0:T(8,128)(2,1)S(1)} %join.7.refs_1_), channel_id=1, source_target_pairs={{0,4},{1,3},{2,6},{3,1},{4,0},{5,7},{6,2},{7,5},{8,12},{9,11},{10,... | collective-permute-start | bytes 1376264 | tf_op jit(solution)/shard_map/ppermute | solution.py:169
  44.5 14.0 %collective-permute-start.11 = (bf16[328,512]{1,0:T(8,128)(2,1)S(1)}, bf16[328,512]{1,0:T(8,128)(2,1)S(1)}, u32[]{:S(2)}, u32[]{:S(2)}) collective-permute-start(bf16[328,512]{1,0:T(8,128)(2,1)S(1)} %copy-done.34), channel_id=1, source_target_pairs={{0,2},{1,3},{2,0},{3,1},{4,6},{5,7},{6,4},{7,5},{8,10},{9,11},{10,... | collective-permute-start | bytes 1007624 | tf_op jit(solution)/shard_map/ppermute | solution.py:161
  46.0 14.7 %collective-permute-start.13 = (bf16[448,512]{1,0:T(8,128)(2,1)S(1)}, bf16[448,512]{1,0:T(8,128)(2,1)S(1)}, u32[]{:S(2)}, u32[]{:S(2)}) collective-permute-start(bf16[448,512]{1,0:T(8,128)(2,1)S(1)} %join.7.refs_1_), channel_id=1, source_target_pairs={{0,1},{1,0},{2,3},{3,2},{4,5},{5,4},{6,7},{7,6},{8,9},{9,8},{10,11... | collective-permute-start | bytes 1376264 | tf_op jit(solution)/shard_map/ppermute | solution.py:161
  46.0 14.7 %collective-permute-start.14 = (bf16[448,512]{1,0:T(8,128)(2,1)S(1)}, bf16[448,512]{1,0:T(8,128)(2,1)S(1)}, u32[]{:S(2)}, u32[]{:S(2)}) collective-permute-start(bf16[448,512]{1,0:T(8,128)(2,1)S(1)} %collective-permute-done.12.refs_2_), channel_id=1, source_target_pairs={{0,1},{1,0},{2,3},{3,2},{4,5},{5,4},{6,7},{7,6},{8,9},{9,8},{10,11... | collective-permute-start | bytes 1376264 | tf_op jit(solution)/shard_map/ppermute | solution.py:161
  52.1 18.4 %collective-permute-start.8 = (bf16[768,512]{1,0:T(8,128)(2,1)S(1)}, bf16[768,512]{1,0:T(8,128)(2,1)S(1)}, u32[]{:S(2)}, u32[]{:S(2)}) collective-permute-start(bf16[768,512]{1,0:T(8,128)(2,1)S(1)} %join.6.refs_1_.refs_5_), channel_id=1, source_target_pairs={{0,4},{1,3},{2,6},{3,1},{4,0},{5,7},{6,2},{7,5},{8,12},{9,11},{10,... | collective-permute-start | bytes 2359304 | tf_op jit(solution)/shard_map/ppermute | solution.py:169
  58.5 23.8 %collective-permute-start.9 = (bf16[768,512]{1,0:T(8,128)(2,1)S(1)}, bf16[768,512]{1,0:T(8,128)(2,1)S(1)}, u32[]{:S(2)}, u32[]{:S(2)}) collective-permute-start(bf16[768,512]{1,0:T(8,128)(2,1)S(1)} %join.6.refs_1_.refs_5_), channel_id=1, source_target_pairs={{0,1},{1,0},{2,3},{3,2},{4,5},{5,4},{6,7},{7,6},{8,9},{9,8},{10,11... | collective-permute-start | bytes 2359304 | tf_op jit(solution)/shard_map/ppermute | solution.py:161
  60.7 31.6 %collective-permute-start.17 = (bf16[256,512]{1,0:T(8,128)(2,1)S(1)}, bf16[256,512]{1,0:T(8,128)(2,1)S(1)}, u32[]{:S(2)}, u32[]{:S(2)}) collective-permute-start(bf16[256,512]{1,0:T(8,128)(2,1)S(1)} %copy-done.37), channel_id=1, source_target_pairs={{0,2},{1,3},{2,0},{3,1},{4,6},{5,7},{6,4},{7,5},{8,10},{9,11},{10,... | collective-permute-start | bytes 786440 | tf_op jit(solution)/shard_map/ppermute | solution.py:161
  70.4 11.9 %collective-permute-start.10 = (bf16[768,512]{1,0:T(8,128)(2,1)S(1)}, bf16[768,512]{1,0:T(8,128)(2,1)S(1)}, u32[]{:S(2)}, u32[]{:S(2)}) collective-permute-start(bf16[768,512]{1,0:T(8,128)(2,1)S(1)} %collective-permute-done.8.refs_2_.refs_6_), channel_id=1, source_target_pairs={{0,1},{1,0},{2,3},{3,2},{4,5},{5,4},{6,7},{7,6},{8,9},{9,8},{10,11... | collective-permute-start | bytes 2359304 | tf_op jit(solution)/shard_map/ppermute | solution.py:161
  110.8 14.9 %collective-permute-start.19 = (bf16[16,128,512]{2,1,0:T(8,128)(2,1)}, bf16[16,128,512]{2,1,0:T(8,128)(2,1)S(1)}, u32[]{:S(2)}, u32[]{:S(2)}) collective-permute-start(bf16[16,128,512]{2,1,0:T(8,128)(2,1)} %get-tuple-element.159), channel_id=1, source_target_pairs={{0,1},{1,0},{2,3},{3,2},{4,5},{5,4},{6,7},{7,6},{8,9},{9,8},{10,11... | collective-permute-start | bytes 6291464 | tf_op jit(solution)/shard_map/ppermute | solution.py:161
  125.4 24.6 %collective-permute-start.21 = (bf16[16,64,512]{2,1,0:T(8,128)(2,1)}, bf16[16,64,512]{2,1,0:T(8,128)(2,1)S(1)}, u32[]{:S(2)}, u32[]{:S(2)}) collective-permute-start(bf16[16,64,512]{2,1,0:T(8,128)(2,1)} %get-tuple-element.182), channel_id=1, source_target_pairs={{0,1},{1,0},{2,3},{3,2},{4,5},{5,4},{6,7},{7,6},{8,9},{9,8},{10,11... | collective-permute-start | bytes 3145736 | tf_op jit(solution)/shard_map/ppermute | solution.py:161
  127.2 48.5 %collective-permute-start.22 = (bf16[8,128,512]{2,1,0:T(8,128)(2,1)}, bf16[8,128,512]{2,1,0:T(8,128)(2,1)S(1)}, u32[]{:S(2)}, u32[]{:S(2)}) collective-permute-start(bf16[8,128,512]{2,1,0:T(8,128)(2,1)} %get-tuple-element.184), channel_id=1, source_target_pairs={{0,4},{1,3},{2,6},{3,1},{4,0},{5,7},{6,2},{7,5},{8,12},{9,11},{10,... | collective-permute-start | bytes 3145736 | tf_op jit(solution)/shard_map/ppermute | solution.py:169
  149.7 27.6 %collective-permute-start.23 = (bf16[1024,512]{1,0:T(8,128)(2,1)}, bf16[1024,512]{1,0:T(8,128)(2,1)}, u32[]{:S(2)}, u32[]{:S(2)}) collective-permute-start(bf16[1024,512]{1,0:T(8,128)(2,1)} %get-tuple-element.189), channel_id=1, source_target_pairs={{0,1},{1,0},{2,3},{3,2},{4,5},{5,4},{6,7},{7,6},{8,9},{9,8},{10,11... | collective-permute-start | bytes 3145736 | tf_op jit(solution)/shard_map/ppermute | solution.py:161
  150.7 11.3 %collective-permute-start.18 = (bf16[256,512]{1,0:T(8,128)(2,1)S(1)}, bf16[256,512]{1,0:T(8,128)(2,1)S(1)}, u32[]{:S(2)}, u32[]{:S(2)}) collective-permute-start(bf16[256,512]{1,0:T(8,128)(2,1)S(1)} %copy-done.38), channel_id=1, source_target_pairs={{0,2},{1,3},{2,0},{3,1},{4,6},{5,7},{6,4},{7,5},{8,10},{9,11},{10,... | collective-permute-start | bytes 786440 | tf_op jit(solution)/shard_map/ppermute | solution.py:161
  160.0 27.1 %collective-permute-start.25 = (bf16[16,56,512]{2,1,0:T(8,128)(2,1)}, bf16[16,56,512]{2,1,0:T(8,128)(2,1)S(1)}, u32[]{:S(2)}, u32[]{:S(2)}) collective-permute-start(bf16[16,56,512]{2,1,0:T(8,128)(2,1)} %get-tuple-element.194), channel_id=1, source_target_pairs={{0,1},{1,0},{2,3},{3,2},{4,5},{5,4},{6,7},{7,6},{8,9},{9,8},{10,11... | collective-permute-start | bytes 2752520 | tf_op jit(solution)/shard_map/ppermute | solution.py:161
  167.3 15.5 %collective-permute-start.39 = (bf16[1,64,512]{2,1,0:T(8,128)(2,1)S(1)}, bf16[1,64,512]{2,1,0:T(8,128)(2,1)S(1)}, u32[]{:S(2)}, u32[]{:S(2)}) collective-permute-start(bf16[1,64,512]{2,1,0:T(8,128)(2,1)S(1)} %get-tuple-element.220), channel_id=1, source_target_pairs={{0,8},{1,9},{2,10},{3,11},{4,12},{5,13},{6,14},{7,15},{8,0},{9,1},... | collective-permute-start | bytes 196616 | tf_op jit(solution)/shard_map/ppermute | solution.py:161
  172.3 12.2 %collective-permute-start.40 = (bf16[1,64,512]{2,1,0:T(8,128)(2,1)S(1)}, bf16[1,64,512]{2,1,0:T(8,128)(2,1)S(1)}, u32[]{:S(2)}, u32[]{:S(2)}) collective-permute-start(bf16[1,64,512]{2,1,0:T(8,128)(2,1)S(1)} %get-tuple-element.221), channel_id=1, source_target_pairs={{0,16},{1,17},{2,18},{3,19},{4,20},{5,21},{6,22},{7,23},{8,24},{9,... | collective-permute-start | bytes 196616 | tf_op jit(solution)/shard_map/ppermute | solution.py:161
  182.7 18.4 %collective-permute-start.31 = (bf16[16,40,512]{2,1,0:T(8,128)(2,1)}, bf16[16,40,512]{2,1,0:T(8,128)(2,1)S(1)}, u32[]{:S(2)}, u32[]{:S(2)}) collective-permute-start(bf16[16,40,512]{2,1,0:T(8,128)(2,1)} %get-tuple-element.205), channel_id=1, source_target_pairs={{0,1},{1,0},{2,3},{3,2},{4,5},{5,4},{6,7},{7,6},{8,9},{9,8},{10,11... | collective-permute-start | bytes 1966088 | tf_op jit(solution)/shard_map/ppermute | solution.py:161
  187.3 12.3 %collective-permute-start.26 = (bf16[8,56,512]{2,1,0:T(8,128)(2,1)S(1)}, bf16[8,56,512]{2,1,0:T(8,128)(2,1)S(1)}, u32[]{:S(2)}, u32[]{:S(2)}) collective-permute-start(bf16[8,56,512]{2,1,0:T(8,128)(2,1)S(1)} %get-tuple-element.196), channel_id=1, source_target_pairs={{0,4},{1,3},{2,6},{3,1},{4,0},{5,7},{6,2},{7,5},{8,12},{9,11},{10,... | collective-permute-start | bytes 1376264 | tf_op jit(solution)/shard_map/ppermute | solution.py:169
  190.9 20.5 %collective-permute-start.42 = (bf16[4,128,512]{2,1,0:T(8,128)(2,1)S(1)}, bf16[4,128,512]{2,1,0:T(8,128)(2,1)S(1)}, u32[]{:S(2)}, u32[]{:S(2)}) collective-permute-start(bf16[4,128,512]{2,1,0:T(8,128)(2,1)S(1)} %get-tuple-element.231), channel_id=1, source_target_pairs={{0,2},{1,5},{2,0},{3,7},{4,6},{5,1},{6,4},{7,3},{8,10},{9,13},{10,... | collective-permute-start | bytes 1572872 | tf_op jit(solution)/shard_map/ppermute | solution.py:169
  201.3 17.6 %collective-permute-start.32 = (bf16[8,40,512]{2,1,0:T(8,128)(2,1)S(1)}, bf16[8,40,512]{2,1,0:T(8,128)(2,1)S(1)}, u32[]{:S(2)}, u32[]{:S(2)}) collective-permute-start(bf16[8,40,512]{2,1,0:T(8,128)(2,1)S(1)} %get-tuple-element.207), channel_id=1, source_target_pairs={{0,4},{1,3},{2,6},{3,1},{4,0},{5,7},{6,2},{7,5},{8,12},{9,11},{10,... | collective-permute-start | bytes 983048 | tf_op jit(solution)/shard_map/ppermute | solution.py:169
  212.2 15.9 %collective-permute-start.43 = (bf16[1,128,512]{2,1,0:T(8,128)(2,1)S(1)}, bf16[1,128,512]{2,1,0:T(8,128)(2,1)S(1)}, u32[]{:S(2)}, u32[]{:S(2)}) collective-permute-start(bf16[1,128,512]{2,1,0:T(8,128)(2,1)S(1)} %get-tuple-element.233), channel_id=1, source_target_pairs={{0,8},{1,9},{2,10},{3,11},{4,12},{5,13},{6,14},{7,15},{8,0},{9,1},... | collective-permute-start | bytes 393224 | tf_op jit(solution)/shard_map/ppermute | solution.py:161
  212.2 17.3 %collective-permute-start.44 = (bf16[1,128,512]{2,1,0:T(8,128)(2,1)S(1)}, bf16[1,128,512]{2,1,0:T(8,128)(2,1)S(1)}, u32[]{:S(2)}, u32[]{:S(2)}) collective-permute-start(bf16[1,128,512]{2,1,0:T(8,128)(2,1)S(1)} %get-tuple-element.234), channel_id=1, source_target_pairs={{0,16},{1,17},{2,18},{3,19},{4,20},{5,21},{6,22},{7,23},{8,24},{9,... | collective-permute-start | bytes 393224 | tf_op jit(solution)/shard_map/ppermute | solution.py:161
  215.2 14.3 %collective-permute-start.45 = (bf16[1,128,512]{2,1,0:T(8,128)(2,1)S(1)}, bf16[1,128,512]{2,1,0:T(8,128)(2,1)S(1)}, u32[]{:S(2)}, u32[]{:S(2)}) collective-permute-start(bf16[1,128,512]{2,1,0:T(8,128)(2,1)S(1)} %get-tuple-element.235), channel_id=1, source_target_pairs={{0,24},{1,25},{2,26},{3,27},{4,28},{5,29},{6,30},{7,31},{8,16},{9,... | collective-permute-start | bytes 393224 | tf_op jit(solution)/shard_map/ppermute | solution.py:161
  (76 other events, 504.8 us)
Sparse Core Ops, SparseCore 0:
  11.5 71.3 all-gather.1

commit v3 on v2

--- a/solution.py
+++ b/solution.py
@@ -114,7 +114,7 @@
             logs[2 * p + half] = highest + jnp.log(denominator)
         return carry
 
-    lax.fori_loop(0, HEADS // 2, pair, 0)
+    lax.fori_loop(0, keys.shape[1] // PAIR, pair, 0)
 
 
 def attend_back(
@@ -146,11 +146,11 @@
         value_grad[:, columns] = value_sum
         return carry
 
-    lax.fori_loop(0, HEADS // 2, pair, 0)
+    lax.fori_loop(0, keys.shape[1] // PAIR, pair, 0)
 
 
 def deltas_of(slope_t, mixture_t, deltas):
-    for head in range(HEADS):
+    for head in range(slope_t.shape[0] // HEAD_DIM):
         rows = slice(head * HEAD_DIM, (head + 1) * HEAD_DIM)
         deltas[head] = jnp.sum(
             slope_t[rows, :].astype(F32) * mixture_t[rows, :].astype(F32), axis=0, keepdims=True
@@ -255,9 +255,9 @@
 def make_tokens_packet(block, memory_block, width):
     rows = block + memory_block + 8
 
-    def kernel(turn, tokens, memory, target_ids, source_ids, cotangent, sent, kept, cot_sent, cot_kept):
+    def kernel(turn, tokens, memory, target_ids, source_ids, sent, kept):
         mine = turn[0]
-        for row, out, cot in ((1 - mine, sent, cot_sent), (mine, kept, cot_kept)):
+        for row, out in ((1 - mine, sent), (mine, kept)):
             out[:block, :] = tokens[row]
             out[block : block + memory_block, :] = memory[row]
             ids = target_ids[pl.ds(row, 1), :].astype(F32)
@@ -267,9 +267,25 @@
             place = lax.broadcasted_iota(jnp.int32, (8, width), 0)
             found = jnp.where(place == 0, ids, jnp.where(place == 1, others, 0.0))
             out[block + memory_block :, :] = found.astype(BF16)
-            cot[...] = cotangent[row]
-
-    return kernel, [((rows, width), BF16)] * 2 + [((block, width), BF16)] * 2
+
+    return kernel, [((rows, width), BF16)] * 2
+
+
+def make_cot_packet(block, width):
+    def kernel(turn, cotangent, sent, kept):
+        sent[...] = cotangent[1 - turn[0]]
+        kept[...] = cotangent[turn[0]]
+
+    return kernel, [((block, width), BF16)] * 2
+
+
+def make_inner_packet(narrow, width, blocks):
+    def kernel(me_ref, inner, outer, out):
+        for i in range(blocks):
+            out[i * narrow : (i + 1) * narrow, :] = inner[:, i * width : (i + 1) * width]
+        out[blocks * narrow :, :] = outer[...]
+
+    return kernel, [((2 * blocks * narrow, width), BF16)]
 
 
 def placed(me, parts, width):
@@ -282,7 +298,7 @@
     def kernel(me_ref, query_w, key_w, value_w, biases, out):
         for i, ref in enumerate((query_w, key_w, value_w)):
             out[i * narrow : (i + 1) * narrow, :] = ref[...]
-        found = placed(me_ref[0], biases[...], width)
+        found = placed(me_ref[0], biases[0:2, :], width)
         out[3 * narrow :, :] = jnp.concatenate([found, jnp.zeros((6, width), F32)], axis=0).astype(BF16)
 
     return kernel, [((3 * narrow + 8, width), BF16)]
@@ -294,11 +310,11 @@
         me = me_ref[0]
         for i, ref in enumerate(weights):
             out[i * narrow : (i + 1) * narrow, :] = ref[...]
-        found = placed(me, short[...], width)
+        found = placed(me, short[2:, :], width)
         per = width // wide.shape[1]
-        row = placed(me % per, wide[...], width)
+        row = placed(lax.rem(me, per), wide[...], width)
         place = lax.broadcasted_iota(jnp.int32, (blocks, width), 0)
-        spread_row = jnp.where(place == me // per, row, 0.0)
+        spread_row = jnp.where(place == lax.div(me, per), row, 0.0)
         rest = jnp.zeros((16 - found.shape[0] - blocks, width), F32)
         out[5 * narrow :, :] = jnp.concatenate([found, spread_row, rest], axis=0).astype(BF16)
 
@@ -329,13 +345,15 @@
     length = parts * share
     memory_share = rows * memory_block
     stride = 3 * narrow + 8
+    half = width // 2
 
     def kernel(*refs):
         me_ref, refs = refs[0], list(refs[1:])
         pieces, refs = refs[:n_pieces], refs[n_pieces:]
         tokens, refs = refs[: parts * rows], refs[parts * rows :]
-        query, query_t, keys, values, value_t, memory, ids, memory_ids = refs[:8]
-        scratch = refs[8:]
+        query, query_t, keys, values, value_t = (refs[2 * i : 2 * i + 2] for i in range(5))
+        memory, ids, memory_ids = refs[10:13]
+        scratch = refs[13:]
         me = me_ref[0]
         if packed:
             for i in range(3):
@@ -345,18 +363,22 @@
         else:
             query_w, key_w, value_w = pieces[:3]
             biases = pieces[3][...]
-        own = jnp.concatenate([t[:block, :] for t in tokens[:rows]], axis=0)
-        scaled = (dot(own, query_w[...]) + biases[0:1, :]).astype(BF16) * BF16(HEAD_DIM**-0.5)
-        query[...] = scaled
-        query_t[...] = scaled.T
         for i in range(parts):
             here = slice(i * share, (i + 1) * share)
             some = tokens[i * rows : (i + 1) * rows]
             own = jnp.concatenate([t[:block, :] for t in some], axis=0)
-            keys[here, :] = dot(own, key_w[...]).astype(BF16)
+            if i == 0:
+                scaled = (dot(own, query_w[...]) + biases[0:1, :]).astype(BF16) * BF16(HEAD_DIM**-0.5)
+            key = dot(own, key_w[...]).astype(BF16)
             found = (dot(own, value_w[...]) + biases[1:2, :]).astype(BF16)
-            values[here, :] = found
-            value_t[:, here] = found.T
+            for side in range(2):
+                columns = slice(side * half, (side + 1) * half)
+                if i == 0:
+                    query[side][...] = scaled[:, columns]
+                    query_t[side][...] = scaled[:, columns].T
+                keys[side][here, :] = key[:, columns]
+                values[side][here, :] = found[:, columns]
+                value_t[side][:, here] = found[:, columns].T
         for i, t in enumerate(tokens):
             memory[i * memory_block : (i + 1) * memory_block, :] = t[block : block + memory_block, :]
             found = t[block + memory_block :, :].astype(F32).astype(jnp.int32)
@@ -364,12 +386,9 @@
         found = [t[block + memory_block :, :].astype(F32).astype(jnp.int32)[1:2, :memory_block] for t in tokens]
         memory_ids[...] = jnp.concatenate(found, axis=1)
 
-    outs = [
-        ((share, width), BF16),
-        ((width, share), BF16),
-        ((length, width), BF16),
-        ((length, width), BF16),
-        ((width, length), BF16),
+    outs = [((share, half), BF16)] * 2 + [((half, share), BF16)] * 2
+    outs += [((length, half), BF16)] * 4 + [((half, length), BF16)] * 2
+    outs += [
         ((parts * memory_share, width), BF16),
         ((1, length), jnp.int32),
         ((1, parts * memory_share), jnp.int32),
@@ -383,7 +402,7 @@
         penalty[...] = penalties(ids[:, :share])
         attend(query_t, keys, value_t, hot, penalty, mixture_t, logs)
 
-    outs = [((width, share), BF16), ((HEADS, 1, share), F32)]
+    outs = [((width // 2, share), BF16), ((HEADS // 2, 1, share), F32)]
     return kernel, outs, [((length, PAIR), BF16), ((PAIR, share), BF16)]
 
 
@@ -395,9 +414,9 @@
         me_ref, refs = refs[0], list(refs[1:])
         pieces, refs = refs[:n_pieces], refs[n_pieces:]
         tokens, refs = refs[:rows], refs[rows:]
-        memory, ids, memory_ids, mixture_t = refs[:4]
-        first_sum, second_sum, query, memory_keys, memory_values, cross_t, logs, vectors = refs[4:12]
-        scratch = refs[12:]
+        memory, ids, memory_ids, upper, lower = refs[:5]
+        first_sum, second_sum, query, memory_keys, memory_values, cross_t, logs, vectors = refs[5:13]
+        scratch = refs[13:]
         query_t, value_t, hot, penalty = scratch[:4]
         if packed:
             for i in range(5):
@@ -412,7 +431,8 @@
             return vectors[i : i + 1, :]
 
         own = jnp.concatenate([t[:block, :] for t in tokens], axis=0)
-        h = own.astype(F32) + dot_tn(mixture_t[...], output_w[...]) + vector(OUTPUT_BIAS)
+        mixture_t = jnp.concatenate([upper[...], lower[...]], axis=0)
+        h = own.astype(F32) + dot_tn(mixture_t, output_w[...]) + vector(OUTPUT_BIAS)
         first_sum[...] = h
         first = normalize(h)[0] * vector(ATTENTION_GAIN) + vector(ATTENTION_SHIFT)
         scaled = (dot(first.astype(BF16), query_w[...]) + vector(SOURCE_QUERY_BIAS)).astype(BF16) * BF16(HEAD_DIM**-0.5)
@@ -457,13 +477,14 @@
         low, active, gate, slope = scratch[:4]
         if packed:
             inner_w, outer_w, gathered = scratch[4:7]
-            whole = pieces[0]
-            for device in range(32):
-                at = device * 2 * blocks * narrow
+            tall = blocks * narrow
+            for core, far, slot, device in places(me_ref[0]):
+                ref, at = pieces[2 * core + far], slot * 2 * tall
+                row = pl.multiple_of(device * narrow, narrow)
                 for i in range(blocks):
-                    inner_w[i, device * narrow : (device + 1) * narrow, :] = whole[at + i * narrow : at + (i + 1) * narrow, :]
-                row = (device % per) * blocks * narrow
-                outer_w[device // per, row : row + blocks * narrow, :] = whole[at + blocks * narrow : at + 2 * blocks * narrow, :]
+                    inner_w[i, pl.ds(row, narrow), :] = ref[at + i * narrow : at + (i + 1) * narrow, :]
+                row = pl.multiple_of(lax.rem(device, per) * tall, tall)
+                outer_w[lax.div(device, per), pl.ds(row, tall), :] = ref[at + tall : at + 2 * tall, :]
         else:
             inner_w, outer_w = pieces
 
@@ -520,8 +541,8 @@
                 row = pl.multiple_of(device * narrow, narrow)
                 for i in range(blocks):
                     ref[at, i * narrow : (i + 1) * narrow, :] = gathered[i, pl.ds(row, narrow), :].astype(BF16)
-                row = pl.multiple_of((device % per) * tall, tall)
-                ref[at, tall:, :] = gathered[blocks + device // per, pl.ds(row, tall), :].astype(BF16)
+                row = pl.multiple_of(lax.rem(device, per) * tall, tall)
+                ref[at, tall:, :] = gathered[blocks + lax.div(device, per), pl.ds(row, tall), :].astype(BF16)
 
     outs = [((block, width), F32), ((block, width), BF16), ((share, width), F32), ((8, width), F32)]
     if packed:
@@ -542,20 +563,20 @@
         me_ref, refs = refs[0], list(refs[1:])
         pieces, refs = refs[:n_pieces], refs[n_pieces:]
         (back2_in, first_sum, second_sum, query, memory_keys, memory_values, cross_t, logs, ids,
-         memory_ids, mixture_t, vectors, sums_inner) = refs[:13]
-        refs = refs[13:]
-        back1, self_slope, self_slope_t, self_deltas, key_own, value_own = refs[:6]
-        sends, refs = refs[6 : 6 + parts - 1], refs[6 + parts - 1 :]
-        n_grads = 2 if packed else 4
-        grad_refs, scratch = refs[:n_grads], refs[n_grads:]
-        (slope_t, slope, key_t, hot, penalty, query_t, deltas, query_grad_t, key_grad, value_grad, sums) = scratch[:11]
+         memory_ids, vectors, sums_inner) = refs[:12]
+        mixtures, refs = refs[12:14], refs[14:]
+        back1, key_own, value_own, sums = refs[:4]
+        self_slope, self_slope_t, self_deltas = (refs[4 + 2 * i : 6 + 2 * i] for i in range(3))
+        sends, refs = refs[10 : 10 + parts - 1], refs[10 + parts - 1 :]
+        grads, scratch = refs[:3], refs[3:]
+        (slope_t, slope, key_t, hot, penalty, query_t, deltas, query_grad_t, key_grad, value_grad) = scratch[:10]
+        upper, lower = mixtures
         if packed:
             for i, at in enumerate((0, 1, 4)):
-                unpack(me_ref[0], pieces, stride, at * narrow, narrow, scratch[11 + i])
-            output_w, query_w, source_w = scratch[11:14]
+                unpack(me_ref[0], pieces, stride, at * narrow, narrow, scratch[10 + i])
+            output_w, query_w, source_w = scratch[10:13]
         else:
             output_w, query_w, source_w = pieces
-        grads = Grads(me_ref[0], grad_refs, scratch[14] if packed else None, narrow)
 
         def vector(i):
             return vectors[i : i + 1, :]
@@ -569,7 +590,7 @@
         back1[...] = back2
         cross_low = back2.astype(BF16)
         sums[9:10, :] = total(cross_low)
-        grads.put(0, dot(cross_t[...], cross_low))
+        grads[0][...] = dot(cross_t[...], cross_low).astype(BF16)
         found = dot_nt(cross_low, source_w[...]).astype(BF16)
         slope[...] = found
         slope_t[...] = found.T
@@ -590,7 +611,7 @@
         sums[10:11, :] = total(query_low)
         normed, inverse = normalize(first_sum[...])
         first_low = (normed * vector(ATTENTION_GAIN) + vector(ATTENTION_SHIFT)).astype(BF16)
-        grads.put(1, dot_tn(first_low, query_low))
+        grads[1][...] = dot_tn(first_low, query_low).astype(BF16)
         upstream = back1[...] + dot_nt(query_low, query_w[...])
         sums[11:12, :] = total(upstream * normed)
         sums[12:13, :] = total(upstream)
@@ -599,23 +620,26 @@
         branch_low = grad.astype(BF16)
         sums[13:14, :] = total(branch_low)
         sums[14:16, :] = jnp.zeros_like(sums[14:16, :])
-        grads.put_sums(3 * narrow, sums[...])
-        grads.put(2, dot(mixture_t[...], branch_low))
+        mixture_t = jnp.concatenate([upper[...], lower[...]], axis=0)
+        grads[2][...] = dot(mixture_t, branch_low).astype(BF16)
         found = dot_nt(branch_low, output_w[...]).astype(BF16)
-        self_slope[...] = found
-        self_slope_t[...] = found.T
-        deltas_of(self_slope_t, mixture_t, self_deltas)
-
+        for side in range(2):
+            columns = slice(side * width // 2, (side + 1) * width // 2)
+            self_slope[side][...] = found[:, columns]
+            self_slope_t[side][...] = found[:, columns].T
+            deltas_of(self_slope_t[side], mixtures[side], self_deltas[side])
+
+    half = width // 2
     outs = [
         ((share, width), F32),
-        ((share, width), BF16),
-        ((width, share), BF16),
-        ((HEADS, 1, share), F32),
         ((memory_share, width), F32),
         ((memory_share, width), F32),
+        ((16, width), F32),
     ]
+    outs += [((share, half), BF16)] * 2 + [((half, share), BF16)] * 2
+    outs += [((HEADS // 2, 1, share), F32)] * 2
     outs += [((2 * memory_share, width), BF16)] * (parts - 1)
-    outs += grad_outs(packed, 3, narrow, width, 16)
+    outs += [((width, width), BF16)] * 3
     scratch = [
         ((width, share), BF16),
         ((share, width), BF16),
@@ -627,99 +651,157 @@
         ((width, share), F32),
         ((memory_length, width), F32),
         ((memory_length, width), F32),
-        ((16, width), F32),
     ]
     if packed:
-        scratch += [((width, width), BF16)] * 3 + [((width, width), F32)]
+        scratch += [((width, width), BF16)] * 3
     return kernel, outs, scratch
 
 
-def make_self_back(packed, parts, rows, block, memory_block, width, narrow, n_pieces, n_others):
+def attention_back_half(refs, share, scratch):
+    query, keys, values, slope, slope_t, logs, deltas, ids = refs
+    query_t, key_t, hot, penalty, query_grad_t, key_grad, value_grad = scratch
+    query_t[...] = query[...].T
+    key_t[...] = keys[...].T
+    hot[...] = one_hot(ids[...])
+    penalty[...] = penalties(ids[:, :share])
+    attend_back(query_t, query, keys, key_t, values, slope_t, slope, hot, penalty, logs, deltas,
+                query_grad_t, key_grad, value_grad)
+
+
+def half_scratch(share, length, half):
+    return [
+        ((half, share), BF16),
+        ((half, length), BF16),
+        ((length, PAIR), BF16),
+        ((PAIR, share), BF16),
+        ((half, share), F32),
+        ((length, half), F32),
+        ((length, half), F32),
+    ]
+
+
+def give_half(share, scratch, own, sends):
+    key_grad, value_grad = scratch[5:7]
+    own[:share, :] = key_grad[:share, :]
+    own[share:, :] = value_grad[:share, :]
+    for i, send in enumerate(sends):
+        here = slice((i + 1) * share, (i + 2) * share)
+        send[:share, :] = key_grad[here, :].astype(BF16)
+        send[share:, :] = value_grad[here, :].astype(BF16)
+
+
+def make_self_back_upper(packed, parts, rows, block, memory_block, width, narrow, n_pieces):
     share, memory_share = rows * block, rows * memory_block
-    length = parts * share
+    length, half = parts * share, width // 2
 
     def kernel(*refs):
         me_ref, refs = refs[0], list(refs[1:])
         pieces, refs = refs[:n_pieces], refs[n_pieces:]
-        others, refs = refs[:n_others], refs[n_others:]
         tokens, refs = refs[:rows], refs[rows:]
-        (query, keys, values, slope, slope_t, logs, deltas, ids, back1, memory_key_own,
-         memory_value_own) = refs[:11]
-        memory_received, refs = refs[11 : 11 + parts - 1], refs[11 + parts - 1 :]
-        in_part, key_own, value_own, memory_own, memory_send = refs[:5]
-        sends, refs = refs[5 : 5 + parts - 1], refs[5 + parts - 1 :]
-        n_grads = 2 if packed else 4
+        operands, refs = refs[:8], refs[8:]
+        memory_key_own, memory_value_own, sums_in = refs[:3]
+        early, refs = refs[3:6], refs[6:]
+        memory_received, refs = refs[: parts - 1], refs[parts - 1 :]
+        query_grad, own, memory_own, memory_send = refs[:4]
+        sends, refs = refs[4 : 4 + parts - 1], refs[4 + parts - 1 :]
+        n_grads = 2 if packed else 3
         grad_refs, scratch = refs[:n_grads], refs[n_grads:]
-        query_t, key_t, hot, penalty, query_grad_t, key_grad, value_grad, sums = scratch[:8]
+        sums = scratch[7]
         me = me_ref[0]
         if packed:
-            unpack(me, pieces, 3 * narrow + 8, 0, narrow, scratch[8])
             for i in range(2):
-                unpack(me, others, 5 * narrow + 16, (2 + i) * narrow, narrow, scratch[9 + i])
-            query_w, source_key, source_value = scratch[8:11]
+                unpack(me, pieces, 5 * narrow + 16, (2 + i) * narrow, narrow, scratch[8 + i])
+            source_key, source_value = scratch[8:10]
         else:
-            (query_w,) = pieces
-            source_key, source_value = others
-        grads = Grads(me, grad_refs, scratch[11] if packed else None, narrow)
-        query_t[...] = query[...].T
-        key_t[...] = keys[...].T
-        hot[...] = one_hot(ids[...])
-        penalty[...] = penalties(ids[:, :share])
-        attend_back(query_t, query, keys, key_t, values, slope_t, slope, hot, penalty, logs, deltas,
-                    query_grad_t, key_grad, value_grad)
-        key_own[...] = key_grad[:share, :]
-        value_own[...] = value_grad[:share, :]
-        for i in range(1, parts):
-            here = slice(i * share, (i + 1) * share)
-            sends[i - 1][:share, :] = key_grad[here, :].astype(BF16)
-            sends[i - 1][share:, :] = value_grad[here, :].astype(BF16)
-        query_low = query_grad_t[...].T.astype(BF16)
-        own = jnp.concatenate([t[:block, :] for t in tokens], axis=0)
-        in_part[...] = back1[...] + dot_nt(query_low, query_w[...])
-        sums[0:1, :] = total(query_low)
-        grads.put(0, dot_tn(own, query_low))
+            source_key, source_value = pieces
+        grads = Grads(me, grad_refs, scratch[10] if packed else None, narrow)
         memory = jnp.concatenate([t[block : block + memory_block, :] for t in tokens], axis=0)
         key_sum, value_sum = memory_key_own[...], memory_value_own[...]
         for ref in memory_received:
             key_sum = key_sum + ref[:memory_share, :].astype(F32)
             value_sum = value_sum + ref[memory_share:, :].astype(F32)
         key_low, value_low = key_sum.astype(BF16), value_sum.astype(BF16)
-        sums[1:2, :] = total(value_low)
-        sums[2:8, :] = jnp.zeros_like(sums[2:8, :])
-        grads.put_sums(3 * narrow, sums[...])
-        grads.put(1, dot_tn(memory, key_low))
-        grads.put(2, dot_tn(memory, value_low))
+        sums[...] = sums_in[...]
+        sums[14:15, :] = total(value_low)
+        grads.put_sums(5 * narrow, sums[...])
+        grads.put(0, dot_tn(memory, key_low))
+        grads.put(1, dot_tn(memory, value_low))
+        if packed:
+            for i, ref in enumerate(early):
+                grads.put(2 + i, ref[...].astype(F32))
         grad = dot_nt(key_low, source_key[...]) + dot_nt(value_low, source_value[...])
         memory_own[...] = grad[:memory_block, :]
         memory_send[...] = grad[memory_block:, :].astype(BF16)
-
-    outs = [((share, width), F32)] * 3 + [((memory_block, width), F32), ((memory_block, width), BF16)]
-    outs += [((2 * share, width), BF16)] * (parts - 1)
-    outs += grad_outs(packed, 3, narrow, width, 8)
-    scratch = [
-        ((width, share), BF16),
-        ((width, length), BF16),
-        ((length, PAIR), BF16),
-        ((PAIR, share), BF16),
-        ((width, share), F32),
-        ((length, width), F32),
-        ((length, width), F32),
-        ((8, width), F32),
+        attention_back_half(operands, share, scratch[:7])
+        query_grad[...] = scratch[4][...].T.astype(BF16)
+        give_half(share, scratch, own, sends)
+
+    outs = [
+        ((share, half), BF16),
+        ((2 * share, half), F32),
+        ((memory_block, width), F32),
+        ((memory_block, width), BF16),
     ]
-    if packed:
-        scratch += [((width, width), BF16)] * 3 + [((width, width), F32)]
+    outs += [((2 * share, half), BF16)] * (parts - 1)
+    if packed:
+        outs += [((16, 5 * narrow + 16, width), BF16)] * 2
+    else:
+        outs += [((width, width), F32)] * 2 + [((16, width), F32)]
+    scratch = half_scratch(share, length, half) + [((16, width), F32)]
+    if packed:
+        scratch += [((width, width), BF16)] * 2 + [((width, width), F32)]
     return kernel, outs, scratch
 
 
-def make_last(packed, parts, rows, block, memory_block, width, narrow, n_pieces):
+def make_self_back_lower(packed, parts, rows, block, width, narrow, n_pieces):
     share = rows * block
+    length, half = parts * share, width // 2
 
     def kernel(*refs):
         me_ref, refs = refs[0], list(refs[1:])
         pieces, refs = refs[:n_pieces], refs[n_pieces:]
         tokens, refs = refs[:rows], refs[rows:]
-        in_part, key_own, value_own, memory_send = refs[:4]
-        received, refs = refs[4 : 4 + parts - 1], refs[4 + parts - 1 :]
+        operands, refs = refs[:8], refs[8:]
+        back1, query_upper = refs[:2]
+        in_part, query_sum, query_w_grad, own = refs[2:6]
+        sends, scratch = refs[6 : 6 + parts - 1], refs[6 + parts - 1 :]
+        if packed:
+            unpack(me_ref[0], pieces, 3 * narrow + 8, 0, narrow, scratch[7])
+            query_w = scratch[7]
+        else:
+            (query_w,) = pieces
+        attention_back_half(operands, share, scratch[:7])
+        give_half(share, scratch, own, sends)
+        query_low = jnp.concatenate([query_upper[...], scratch[4][...].T.astype(BF16)], axis=1)
+        tokens_own = jnp.concatenate([t[:block, :] for t in tokens], axis=0)
+        in_part[...] = back1[...] + dot_nt(query_low, query_w[...])
+        query_sum[...] = jnp.concatenate([total(query_low), jnp.zeros((7, width), F32)], axis=0)
+        query_w_grad[...] = dot_tn(tokens_own, query_low).astype(query_w_grad.dtype)
+
+    outs = [
+        ((share, width), F32),
+        ((8, width), F32),
+        ((width, width), BF16 if packed else F32),
+        ((2 * share, half), F32),
+    ]
+    outs += [((2 * share, half), BF16)] * (parts - 1)
+    scratch = half_scratch(share, length, half)
+    if packed:
+        scratch += [((width, width), BF16)]
+    return kernel, outs, scratch
+
+
+def make_last(packed, parts, rows, block, memory_block, width, narrow, n_pieces):
+    share = rows * block
+
+    def kernel(*refs):
+        me_ref, refs = refs[0], list(refs[1:])
+        pieces, refs = refs[:n_pieces], refs[n_pieces:]
+        tokens, refs = refs[:rows], refs[rows:]
+        in_part, query_sum, query_w_grad, memory_send = refs[:4]
+        owns, refs = refs[4:6], refs[6:]
+        received = [refs[: parts - 1], refs[parts - 1 : 2 * (parts - 1)]]
+        refs = refs[2 * (parts - 1) :]
         in_own, in_send = refs[:2]
         n_grads = 2 if packed else 3
         grad_refs, scratch = refs[2 : 2 + n_grads], refs[2 + n_grads :]
@@ -732,24 +814,32 @@
         else:
             key_w, value_w = pieces
         grads = Grads(me, grad_refs, scratch[3] if packed else None, narrow)
-        own = jnp.concatenate([t[:block, :] for t in tokens], axis=0)
-        key_sum, value_sum = key_own[...], value_own[...]
-        for ref in received:
-            key_sum = key_sum + ref[:share, :].astype(F32)
-            value_sum = value_sum + ref[share:, :].astype(F32)
-        key_low, value_low = key_sum.astype(BF16), value_sum.astype(BF16)
-        sums[0:1, :] = total(value_low)
-        sums[1:8, :] = jnp.zeros_like(sums[1:8, :])
-        grads.put_sums(2 * narrow, sums[...])
-        grads.put(0, dot_tn(own, key_low))
-        grads.put(1, dot_tn(own, value_low))
+        if packed:
+            grads.put(2, query_w_grad[...].astype(F32))
+        lows = []
+        for own, others in zip(owns, received):
+            found = own[...]
+            for ref in others:
+                found = found + ref[...].astype(F32)
+            lows.append(found.astype(BF16))
+        key_low = jnp.concatenate([low[:share, :] for low in lows], axis=1)
+        value_low = jnp.concatenate([low[share:, :] for low in lows], axis=1)
+        tokens_own = jnp.concatenate([t[:block, :] for t in tokens], axis=0)
+        sums[...] = query_sum[...]
+        sums[1:2, :] = total(value_low)
+        grads.put_sums(3 * narrow, sums[...])
+        grads.put(0, dot_tn(tokens_own, key_low))
+        grads.put(1, dot_tn(tokens_own, value_low))
         grad = in_part[...] + dot_nt(key_low, key_w[...]) + dot_nt(value_low, value_w[...])
         in_own[...] = grad[:block, :]
         in_send[:block, :] = grad[block:, :].astype(BF16)
         in_send[block:, :] = memory_send[...]
 
     outs = [((block, width), F32), ((block + memory_block, width), BF16)]
-    outs += grad_outs(packed, 2, narrow, width, 8)
+    if packed:
+        outs += [((16, 3 * narrow + 8, width), BF16)] * 2
+    else:
+        outs += [((width, width), F32)] * 2 + [((8, width), F32)]
     scratch = [((8, width), F32)]
     if packed:
         scratch += [((width, width), BF16)] * 2 + [((width, width), F32)]
@@ -778,17 +868,6 @@
         cost_estimate=pl.CostEstimate(flops=1 << 20, bytes_accessed=0, transcendentals=0),
         name="combine",
     )(*arrays)
-
-
-def finish(me_array, arrays, plan, shapes, name):
-    def kernel(me_ref, *refs):
-        given, outs = refs[: len(arrays)], refs[len(arrays) :]
-        found = given[0][0].astype(F32)
-        for ref in given[1:]:
-            found = found + ref[0].astype(F32)
-        plan(me_ref[0], found, outs)
-
-    return call(kernel, [(s, F32) for s in shapes], (me_array, *arrays), [], 0.5, name)
 
 
 def chosen(me, rows, wide):
@@ -829,53 +908,65 @@
     narrow, wide = width // devices, hidden // devices
 
     def run(made, micros, name, *args):
-        kernel, outs, scratch = made
-        return call(kernel, outs, (me_array,) + args, scratch, micros, name)
-
-    short_self = jnp.stack([query_bias, value_bias])
-    short_cross = jnp.stack([output_bias, attention_gain, attention_shift, source_query_bias,
-                             source_value_bias, source_output_bias, source_gain, source_shift,
-                             outer_bias, final_gain, final_shift])
-    inner_rows = inner_weight.reshape(narrow, blocks, width).transpose(1, 0, 2).reshape(blocks * narrow, width)
+        kernel, outs, *scratch = made
+        return call(kernel, outs, (me_array,) + args, scratch[0] if scratch else [], micros, name)
+
+    turn_array = turn.reshape(1).astype(jnp.int32)
+
+    def turned(made, name, *args):
+        kernel, outs = made
+        return call(kernel, outs, (turn_array,) + args, [], 1.0, name)
+
+    short = jnp.stack([query_bias, value_bias, output_bias, attention_gain, attention_shift,
+                       source_query_bias, source_value_bias, source_output_bias, source_gain,
+                       source_shift, outer_bias, final_gain, final_shift])
 
     def whole(array):
         return lax.all_gather(array, AXES, axis=0, tiled=True)
 
-    kernel, outs = make_tokens_packet(block, memory_block, width)
-    sent, kept, cot_sent, cot_own = call(
-        kernel, outs, (turn.reshape(1).astype(jnp.int32), tokens, memory, target_ids, source_ids, cotangent),
-        [], 2.0, "tokens_packet",
+    sent, kept = turned(
+        make_tokens_packet(block, memory_block, width), "tokens_packet",
+        tokens, memory, target_ids, source_ids,
     )
-
-    if packed:
-        set_inner = [whole(jnp.concatenate([inner_rows, outer_weight], axis=0))]
-        kernel, outs = make_self_packet(narrow, width)
-        (first,) = call(kernel, outs, (me_array, query_weight, key_weight, value_weight, short_self), [], 1.0, "self_packet")
-        kernel, outs = make_cross_packet(narrow, width, blocks)
-        (second,) = call(kernel, outs, (me_array, output_weight, source_query, source_key, source_value,
-                         source_output, short_cross, inner_bias.reshape(1, wide)), [], 1.0, "cross_packet")
+    came = swap(sent, parts, devices)
+    row_tokens = [kept, came]
+    kept_swaps = [swap(kept, m, devices) for m in range(1, parts)]
+    came_swaps = [swap(came, m, devices) for m in range(1, parts)]
+    for pair in zip(kept_swaps, came_swaps):
+        row_tokens += pair
+    own_tokens = row_tokens[:rows]
+
+    if packed:
+        (first,) = run(make_self_packet(narrow, width), 1.0, "self_packet",
+                       query_weight, key_weight, value_weight, short)
+        first = after(first, sent)
         first_z = [swap(first, m, 32) for m in Z_MASKS[1:]]
-        came = swap(sent, parts, devices)
-        second = after(second, *first_z)
+        (second,) = run(make_cross_packet(narrow, width, blocks), 1.0, "cross_packet", output_weight,
+                        source_query, source_key, source_value, source_output, short,
+                        inner_bias.reshape(1, wide))
+        (third,) = run(make_inner_packet(narrow, width, blocks), 1.0, "inner_packet", inner_weight, outer_weight)
+        first_a = join(after([first, *first_z], second, third))
+        first_b = turned_swap(first_a, 1)
+        second = after(second, first_a)
         second_z = [swap(second, m, 32) for m in Z_MASKS[1:]]
-        first_a = join(after([first, *first_z], sent))
-        first_b = turned_swap(first_a, 1)
-        first_c = join([first_a, first_b])
+        first_c = join(after([first_a, first_b], came, *kept_swaps))
         first_d = turned_swap(first_c, 2)
+        second_a = join([second, *second_z])
+        first_d = after(first_d, second_a, *came_swaps)
+        third = after(third, second_a)
+        third_z = [swap(third, m, 32) for m in Z_MASKS[1:]]
         set_self = [first_c, first_d, swap(first_c, 1, 32), swap(first_d, 1, 32)]
-        second_a = after(join([second, *second_z]), first_b)
         second_b = turned_swap(second_a, 1)
     else:
-        came = swap(sent, parts, devices)
         full = [whole(w) for w in (query_weight, key_weight, value_weight, output_weight, source_query, source_key, source_value, source_output)]
         lane = lax.broadcasted_iota(jnp.int32, (1, width), 1)
         place = lax.broadcasted_iota(jnp.int32, (blocks, width), 0) * width + lane
         spread_wide = jnp.where(place // wide == me, jnp.tile(inner_bias.reshape(1, wide), (blocks, width // wide)), 0)
 
-        def natural(short):
-            return jnp.where(lane // narrow == me, jnp.tile(short, (1, devices)), 0)
-
-        vectors = jnp.concatenate([natural(short_self), jnp.zeros((6, width), BF16), natural(short_cross), spread_wide, jnp.zeros((1, width), BF16)])
+        def natural(rows):
+            return jnp.where(lane // narrow == me, jnp.tile(rows, (1, devices)), 0)
+
+        vectors = jnp.concatenate([natural(short[:2]), jnp.zeros((6, width), BF16), natural(short[2:]), spread_wide, jnp.zeros((1, width), BF16)])
         vectors = reduce_all(vectors, devices).astype(F32)
         set_self = full[:3] + [vectors[:8]]
         set_cross = full[3:] + [vectors[8:]]
@@ -883,126 +974,134 @@
             whole(inner_weight).reshape(width, blocks, width).transpose(1, 0, 2),
             whole(outer_weight).reshape(blocks, width, width),
         ]
-    row_tokens = [kept, came]
-    for m in range(1, parts):
-        row_tokens += [swap(kept, m, devices), swap(came, m, devices)]
-    own_tokens = row_tokens[:rows]
-    if packed:
-        set_self[0] = after(set_self[0], *second_z)
-    query, query_t, keys, values, value_t, row_memory, ids, memory_ids = run(
-        make_project(packed, parts, rows, block, memory_block, width, narrow, len(set_self)), 4.0,
+    found = run(
+        make_project(packed, parts, rows, block, memory_block, width, narrow, len(set_self)), 5.0,
         "project", *set_self, *row_tokens,
     )
-    if packed:
-        second_c = join([second_a, second_b])
+    query, query_t, keys, values, value_t = (found[2 * i : 2 * i + 2] for i in range(5))
+    row_memory, ids, memory_ids = found[10:]
+    attention = make_self_attention(share, parts * share, width)
+    if packed:
+        second_c = join(after([second_a, second_b], query_t[1]))
         second_d = turned_swap(second_c, 2)
-        query_t = after(query_t, second_c)
-        cot_sent = after(cot_sent, second_c)
-        set_cross = [second_c, second_d, swap(second_c, 1, 32), swap(second_d, 1, 32)]
+        third_a = join(after([third, *third_z], query_t[1]))
+        third_b = turned_swap(third_a, 1)
+        second_e = swap(second_c, 1, 32)
+        query_t = [after(query_t[0], second_c, third_a), query_t[1]]
+    upper = run(attention, 5.5, "self_upper", query_t[0], keys[0], value_t[0], ids)
+    if packed:
+        second_d = after(second_d, upper[0])
+        set_cross = [second_c, second_d, second_e, swap(second_d, 1, 32)]
+        third_c = join(after([third_a, third_b], upper[0]))
+        third_d = turned_swap(third_c, 2)
+        set_inner = [third_c, third_d, swap(third_c, 1, 32), swap(third_d, 1, 32)]
+        query_t = [query_t[0], after(query_t[1], third_c, second_d)]
         set_back, set_query, set_last, set_memory = set_cross, set_self, set_self, set_cross
+        cotangent = after(cotangent, third_c)
     else:
         set_back, set_query, set_last, set_memory = [full[3], full[4], full[7]], full[:1], full[1:3], full[5:7]
+    cot_sent, cot_own = turned(make_cot_packet(block, width), "cot_packet", cotangent)
     cot_came = swap(cot_sent, parts, devices)
-    mixture_t, logs = run(
-        make_self_attention(share, parts * share, width), 9.0, "self_attention",
-        query_t, keys, value_t, ids,
-    )
+    lower = run(attention, 5.5, "self_lower", query_t[1], keys[1], value_t[1], ids)
+    mixtures, logs = (upper[0], lower[0]), (upper[1], lower[1])
     first_sum, second_sum, cross_query, memory_keys, memory_values, cross_t, cross_logs, vectors = run(
         make_cross_forward(packed, rows, block, parts * memory_share, width, narrow, len(set_cross)),
-        9.0, "cross_forward", *set_cross, *own_tokens, row_memory, ids, memory_ids, mixture_t,
+        9.0, "cross_forward", *set_cross, *own_tokens, row_memory, ids, memory_ids, *mixtures,
     )
     out_own, out_send, back2_in, sums_inner, *grads_inner = run(
         make_inner(packed, rows, block, width, hidden, narrow, len(set_inner)), 18.0, "inner",
         *set_inner, second_sum, cot_own, cot_came, vectors,
     )
+    out_came = swap(out_send, parts, devices)
     found = run(
         make_cross_back(packed, parts, share, memory_share, width, narrow, len(set_back)), 14.0,
         "cross_back", *set_back, back2_in, first_sum, second_sum, cross_query, memory_keys,
-        memory_values, cross_t, cross_logs, ids, memory_ids, mixture_t, vectors, sums_inner,
+        memory_values, cross_t, cross_logs, ids, memory_ids, vectors, sums_inner, *mixtures,
     )
-    back1, slope, slope_t, deltas, memory_key_own, memory_value_own = found[:6]
-    memory_sends, grads_cross = found[6 : 6 + parts - 1], found[6 + parts - 1 :]
-    memory_received = [swap(a, m + 1, devices) for m, a in enumerate(memory_sends)]
+    back1, memory_key_own, memory_value_own, sums_cross = found[:4]
+    slope, slope_t, deltas = (found[4 + 2 * i : 6 + 2 * i] for i in range(3))
+    memory_received = [swap(a, m + 1, devices) for m, a in enumerate(found[10 : 10 + parts - 1])]
+    grads_early = found[10 + parts - 1 :]
+    query = list(query)
     if packed:
         keep, send = combine([grads_inner[0], swap(grads_inner[1], 1, 32)], 2)
-        query = after(query, keep)
+        query[0] = after(query[0], keep, out_came)
         inner_step = [keep, turned_swap(send, 2)]
     found = run(
-        make_self_back(packed, parts, rows, block, memory_block, width, narrow, len(set_query), len(set_memory)),
-        17.0, "self_back", *set_query, *set_memory, *own_tokens, query, keys, values, slope, slope_t,
-        logs, deltas, ids, back1, memory_key_own, memory_value_own, *memory_received,
+        make_self_back_upper(packed, parts, rows, block, memory_block, width, narrow, len(set_memory)),
+        12.0, "self_back_upper", *set_memory, *own_tokens, query[0], keys[0], values[0], slope[0],
+        slope_t[0], logs[0], deltas[0], ids, memory_key_own, memory_value_own, sums_cross,
+        *grads_early, *memory_received,
     )
-    in_part, key_own, value_own, memory_own, memory_send = found[:5]
-    received = [swap(a, m + 1, devices) for m, a in enumerate(found[5 : 5 + parts - 1])]
-    grads_query = found[5 + parts - 1 :]
-    if packed:
-        keep, send = combine([grads_cross[0], swap(grads_cross[1], 1, 32)], 2)
-        cross_step = [keep, turned_swap(send, 2)]
-        keep_inner, send_inner = combine(inner_step, 2)
-        key_own = after(key_own, keep, keep_inner)
-        inner_step = [keep_inner, turned_swap(send_inner, 1)]
+    query_upper, own_upper, memory_own, memory_send = found[:4]
+    received_upper = [swap(a, m + 1, devices) for m, a in enumerate(found[4 : 4 + parts - 1])]
+    grads_cross = found[4 + parts - 1 :]
+    if packed:
+        keep, send = combine(inner_step, 2)
+        inner_step = [keep, turned_swap(send, 1)]
+        query[1] = after(query[1], keep)
+    in_part, query_sum, query_w_grad, own_lower, *sends = run(
+        make_self_back_lower(packed, parts, rows, block, width, narrow, len(set_query)), 11.0,
+        "self_back_lower", *set_query, *own_tokens, query[1], keys[1], values[1], slope[1],
+        slope_t[1], logs[1], deltas[1], ids, back1, query_upper,
+    )
+    received_lower = [swap(a, m + 1, devices) for m, a in enumerate(sends)]
+    if packed:
+        def lowest(arrays):
+            found = combine(arrays, 4)
+            return [found[0]] + [swap(a, m, 32) for a, m in zip(found[1:], Z_MASKS[1:])]
+
+        keep_cross, send = combine([grads_cross[0], swap(grads_cross[1], 1, 32)], 2)
+        cross_step = [keep_cross, turned_swap(send, 2)]
+        inner_step = lowest(inner_step)
+        in_part = after(in_part, keep_cross, inner_step[0])
     in_own, in_send, *grads_last = run(
         make_last(packed, parts, rows, block, memory_block, width, narrow, len(set_last)), 6.0,
-        "last", *set_last, *own_tokens, in_part, key_own, value_own, memory_send, *received,
+        "last", *set_last, *own_tokens, in_part, query_sum, query_w_grad, memory_send, own_upper,
+        own_lower, *received_upper, *received_lower,
     )
 
     def regroup(mine, came):
         came = came.astype(F32)
         return jnp.where(turn == 0, jnp.stack([mine, came]), jnp.stack([came, mine]))
 
-    output = regroup(out_own, swap(out_send, parts, devices))
+    output = regroup(out_own, out_came)
     in_came = swap(in_send, parts, devices)
     input_gradient = regroup(in_own, in_came[:block])
     memory_gradient = regroup(memory_own, in_came[block:])
 
     if packed:
-        def lower(arrays):
-            found = combine(arrays, 4)
-            return [found[0]] + [swap(a, m, 32) for a, m in zip(found[1:], Z_MASKS[1:])]
-
-        def rest(grads):
-            keep, send = combine([grads[0], swap(grads[1], 1, 32)], 2)
-            keep, send = combine([keep, turned_swap(send, 2)], 2)
-            return lower([keep, turned_swap(send, 1)])
-
-        def inner_plan(me, found, outs):
+        keep, send = combine(cross_step, 2)
+        cross_step = lowest([keep, turned_swap(send, 1)])
+        keep, send = combine([grads_last[0], swap(grads_last[1], 1, 32)], 2)
+        keep, send = combine(after([keep, turned_swap(send, 2)], *inner_step), 2)
+        last_step = lowest([keep, turned_swap(send, 1)])
+
+        def plan(me_ref, *refs):
+            me = me_ref[0]
+            steps, outs = [refs[:4], refs[4:8], refs[8:12]], refs[12:]
+            inner, cross, last = (sum(r[0].astype(F32) for r in given) for given in steps)
             for i in range(blocks):
-                outs[0][:, i * width : (i + 1) * width] = found[i * narrow : (i + 1) * narrow, :]
-            outs[1][...] = found[blocks * narrow :, :]
-
-        def cross_plan(me, found, outs):
+                outs[0][:, i * width : (i + 1) * width] = inner[i * narrow : (i + 1) * narrow, :]
+            outs[1][...] = inner[blocks * narrow :, :]
+            for i in range(5):
+                outs[2 + i][...] = cross[i * narrow : (i + 1) * narrow, :]
             for i in range(3):
-                outs[i][...] = found[i * narrow : (i + 1) * narrow, :]
-            sums = found[3 * narrow :, :]
-            outs[3][...] = chosen(me, sums, narrow)
+                outs[7 + i][...] = last[i * narrow : (i + 1) * narrow, :]
+            rows_in = jnp.concatenate([cross[5 * narrow :, :], last[3 * narrow :, :]], axis=0)
+            outs[10][...] = chosen(me, rows_in, narrow)
             per = width // wide
             line = lax.broadcasted_iota(jnp.int32, (blocks, width), 0)
-            row = jnp.sum(jnp.where(line == me // per, sums[3 : 3 + blocks, :], 0.0), axis=0, keepdims=True)
-            outs[4][...] = chosen(me % per, row, wide)
-
-        def query_plan(me, found, outs):
-            for i in range(3):
-                outs[i][...] = found[i * narrow : (i + 1) * narrow, :]
-            outs[3][...] = chosen(me, found[3 * narrow :, :], narrow)
-
-        def last_plan(me, found, outs):
-            for i in range(2):
-                outs[i][...] = found[i * narrow : (i + 1) * narrow, :]
-            outs[2][...] = chosen(me, found[2 * narrow :, :], narrow)
+            row = jnp.sum(jnp.where(line == lax.div(me, per), rows_in[3 : 3 + blocks, :], 0.0), axis=0, keepdims=True)
+            outs[11][...] = chosen(lax.rem(me, per), row, wide)
 
         part = (narrow, width)
-        inner_step = lower(inner_step)
-        keep, send = combine(cross_step, 2)
-        cross_step = lower([keep, turned_swap(send, 1)])
-        inner_share, outer_share = finish(me_array, inner_step, inner_plan, [(narrow, hidden), (wide, width)], "finish_inner")
-        source_output_share, source_query_share, output_share, sums, inner_bias_share = finish(
-            me_array, cross_step, cross_plan, [part] * 3 + [(16, narrow), (1, wide)], "finish_cross"
-        )
-        query_share, source_key_share, source_value_share, sums_query = finish(
-            me_array, rest(grads_query), query_plan, [part] * 3 + [(8, narrow)], "finish_query"
-        )
-        key_share, value_share, sums_last = finish(
-            me_array, rest(grads_last), last_plan, [part] * 2 + [(8, narrow)], "finish_last"
+        shapes = [(narrow, hidden), (wide, width)] + [part] * 8 + [(24, narrow), (1, wide)]
+        (inner_share, outer_share, source_key_share, source_value_share, source_output_share,
+         source_query_share, output_share, key_share, value_share, query_share, sums,
+         inner_bias_share) = call(
+            plan, [(s, F32) for s in shapes], (me_array, *inner_step, *cross_step, *last_step), [], 2.0,
+            "finish",
         )
         inner_bias_share = inner_bias_share.reshape(wide)
     else:
@@ -1011,14 +1110,13 @@
 
         inner_share = scatter(grads_inner[0].transpose(1, 0, 2).reshape(width, hidden))
         outer_share = scatter(grads_inner[1].reshape(hidden, width))
-        source_output_share, source_query_share, output_share = (scatter(g) for g in grads_cross[:3])
-        query_share, source_key_share, source_value_share = (scatter(g) for g in grads_query[:3])
+        source_output_share, source_query_share, output_share = (scatter(g.astype(F32)) for g in grads_early)
+        source_key_share, source_value_share = (scatter(g) for g in grads_cross[:2])
         key_share, value_share = (scatter(g) for g in grads_last[:2])
-        sums = jnp.concatenate([grads_cross[3], grads_query[3], grads_last[2]], axis=0)
-        sums = reduce_all(sums, devices)
+        query_share = scatter(query_w_grad)
+        sums = reduce_all(jnp.concatenate([grads_cross[2], grads_last[2]], axis=0), devices)
         inner_bias_share = lax.dynamic_slice(sums[3 : 3 + blocks].reshape(hidden), (me * wide,), (wide,))
         sums = lax.dynamic_slice(sums, (0, me * narrow), (sums.shape[0], narrow))
-        sums, sums_query, sums_last = sums[:16], sums[16:24], sums[24:]
     return (
         output,
         input_gradient,
@@ -1027,8 +1125,8 @@
         key_share,
         value_share,
         output_share,
-        sums_query[0],
-        sums_last[0],
+        sums[16],
+        sums[17],
         sums[13],
         sums[11],
         sums[12],
@@ -1037,7 +1135,7 @@
         source_value_share,
         source_output_share,
         sums[10],
-        sums_query[1],
+        sums[14],
         sums[9],
         sums[7],
         sums[8],

time: 246 us -> 227 us (0.923)
  between operations: 14.7 us -> 1.46 us
  starting transfers between devices: 55.6 us -> 45.8 us
  waiting for transfers between devices: 55.5 us -> 62.3 us
  local copies, waits for them, and re-layouts: 15 us -> 12.1 us
    ppermute x34 -> x36, starting transfers between devices: 42 us -> 33.3 us  [swap(): return lax.ppermute(array, AXES, [(i, i ^ mask) for i in range(devices)])]
    ppermute x34 -> x36, waiting for transfers between devices: 19.8 us -> 23.6 us  [swap(): return lax.ppermute(array, AXES, [(i, i ^ mask) for i in range(devices)])]
    ppermute x12, waiting for transfers between devices: 35.6 us -> 38.7 us  [turned_swap(): return lax.ppermute(array, AXES, pairs)]
    squeeze x2 -> x0, local copies, waits for them, and re-layouts: 2.47 us -> none  [the longest x1 1.28 us: per_device(): sums_query[1]]
    pallas_call x14 -> x15, Pallas kernels: 94.8 us -> 97.1 us  [call(): pl.pallas_call(kernel, out_shape=[jax.ShapeDtypeStruct(s, d) for s, d in...]
    unnamed x106 -> x84, local copies, waits for them, and re-layouts: 8.99 us -> 7.94 us
  transfers between devices with their start and end apart: 47 -> 48, of which waited for: 17 -> 18; matrix products, arithmetic and copies ran while one was open for 3% -> 2% of each run, Pallas kernels for 32% -> 31%
where the time goes in v3:
time: 227 us; the launch traced here: 225 us
  Pallas kernels  99.1 us (44%)
  waiting for transfers between devices  62.3 us (27%)
  starting transfers between devices  45.8 us (20%)
  local copies, waits for them, and re-layouts  12.1 us (5%)
  other arithmetic  3.93 us (2%)
    pallas_call x15, Pallas kernels, call(): pl.pallas_call(kernel, out_shape=[jax.ShapeDtypeStruct(s, d) for s, d in...  97.1 us
    ppermute x12, waiting for transfers between devices, turned_swap(): return lax.ppermute(array, AXES, pairs)  38.7 us
    ppermute x36, starting transfers between devices, swap(): return lax.ppermute(array, AXES, [(i, i ^ mask) for i in range(devices)])  33.3 us
    ppermute x36, waiting for transfers between devices, swap(): return lax.ppermute(array, AXES, [(i, i ^ mask) for i in range(devices)])  23.6 us
    ppermute x12, starting transfers between devices, turned_swap(): return lax.ppermute(array, AXES, pairs)  12.4 us
    unnamed x84, local copies, waits for them, and re-layouts  7.94 us
  transfers between devices with their start and end apart: 48, of which 18 were waited for; matrix products, arithmetic and copies ran while one was open for 2% of the time, Pallas kernels for 31%

profile of v3, /device:TPU:0, one launch (start us, length us, event | category | flops | bytes accessed | tf_op | source)
XLA Modules:
  0.0 224.7 jit_solution(11340450229732407450)
XLA Ops:
  0.7 2.7 %stack.106.refs_5_.biases = bf16[13,16]{1,0:T(8,128)(2,1)} concatenate(bf16[1,16]{1,0:T(2,128)(2,1)} %bitcast.62, bf16[1,16]{1,0:T(2,128)(2,1)} %bitcast.63, bf16[1,16]{1,0:T(2,128)(2,1)} %bitcast.64, bf16[1,16]{1,0:T(2,128)(2,1)} %bitcast.65, bf16[1,16]{1,0:T(2,128)(2,1)} %bitcast.66, bf16[1,16]{1,0:T(2,128)(2,1)} %bitcast.67, bf16[1,16]{1,0:T(2,128)(2,1)} %bitcast.68, ...), dimensions={0} | concatenate | bytes 832 | tf_op jit(solution)/shard_map/stack | solution.py:920
  6.9 5.0 %collective-permute-start.2 = (bf16[56,512]{1,0:T(8,128)(2,1)S(1)}, bf16[56,512]{1,0:T(8,128)(2,1)S(1)}, u32[]{:S(2)}, u32[]{:S(2)}) collective-permute-start(bf16[56,512]{1,0:T(8,128)(2,1)S(1)} %copy-done.8), channel_id=1, source_target_pairs={{0,24},{1,25},{2,26},{3,27},{4,28},{5,29},{6,30},{7,31},{8,16},{9,... | collective-permute-start | bytes 172040 | tf_op jit(solution)/shard_map/ppermute | solution.py:161
  18.7 5.7 %collective-permute-done.9.refs_1_ = bf16[224,512]{1,0:T(8,128)(2,1)S(1)} collective-permute-done((bf16[224,512]{1,0:T(8,128)(2,1)S(1)}, bf16[224,512]{1,0:T(8,128)(2,1)S(1)}, u32[]{:S(2)}, u32[]{:S(2)}) %collective-permute-start.9) | collective-permute-done | bytes 229408 | tf_op jit(solution)/shard_map/ppermute | solution.py:169
  25.9 3.5 %collective-permute-start.5 = (bf16[96,512]{1,0:T(8,128)(2,1)}, bf16[96,512]{1,0:T(8,128)(2,1)S(1)}, u32[]{:S(2)}, u32[]{:S(2)}) collective-permute-start(bf16[96,512]{1,0:T(8,128)(2,1)} %cross_packet.1.refs_0_), channel_id=1, source_target_pairs={{0,24},{1,25},{2,26},{3,27},{4,28},{5,29},{6,30},{7,31},{8,16},{9,... | collective-permute-start | bytes 294920 | tf_op jit(solution)/shard_map/ppermute | solution.py:161
  30.3 3.3 %collective-permute-done.5.refs_3_ = bf16[96,512]{1,0:T(8,128)(2,1)S(1)} collective-permute-done((bf16[96,512]{1,0:T(8,128)(2,1)}, bf16[96,512]{1,0:T(8,128)(2,1)S(1)}, u32[]{:S(2)}, u32[]{:S(2)}) %collective-permute-start.5) | collective-permute-done | bytes 98336 | tf_op jit(solution)/shard_map/ppermute | solution.py:161
  33.6 4.9 %collective-permute-done.4.refs_2_ = bf16[96,512]{1,0:T(8,128)(2,1)S(1)} collective-permute-done((bf16[96,512]{1,0:T(8,128)(2,1)}, bf16[96,512]{1,0:T(8,128)(2,1)S(1)}, u32[]{:S(2)}, u32[]{:S(2)}) %collective-permute-start.4) | collective-permute-done | bytes 98336 | tf_op jit(solution)/shard_map/ppermute | solution.py:161
  40.1 2.4 %collective-permute-start.8 = (bf16[128,512]{1,0:T(8,128)(2,1)S(1)}, bf16[128,512]{1,0:T(8,128)(2,1)S(1)}, u32[]{:S(2)}, u32[]{:S(2)}) collective-permute-start(bf16[128,512]{1,0:T(8,128)(2,1)S(1)} %copy-done.6), channel_id=1, source_target_pairs={{0,24},{1,25},{2,26},{3,27},{4,28},{5,29},{6,30},{7,31},{8,16},{9,... | collective-permute-start | bytes 393224 | tf_op jit(solution)/shard_map/ppermute | solution.py:161
  46.8 4.9 %project.1 = (bf16[512,256]{1,0:T(8,128)(2,1)}, bf16[512,256]{1,0:T(8,128)(2,1)}, bf16[256,512]{1,0:T(8,128)(2,1)}, bf16[256,512]{1,0:T(8,128)(2,1)}, bf16[1024,...) custom-call(s32[1]{0:T(128)} %bitcast.me_ref.refs_0_, ...), custom_call_target="tpu_custom_call" | custom-call | flops 5750000128 | bytes 7640064 | tf_op jit(solution)/shard_map/project/pallas_call | solution.py:241
  55.7 6.6 %self_upper.1 = (bf16[256,512]{1,0:T(8,128)(2,1)}, f32[4,1,512]{2,1,0:T(1,128)}) custom-call(s32[1]{0:T(128)} %bitcast.me_ref.refs_0_, bf16[256,512]{1,0:T(8,128)(2,1)} %get-tuple-element.175.query_t, bf16[1024,256]{1,0:T(8,128)(2,1)} %get-tuple-element.176.keys.refs_8_, bf16[256,1024]{1,0:T(8,128)(2,1)} %get-tuple-element.177.value_t, ...), custom_call_target="tpu_custom_call" | custom-call | flops 6325000192 | bytes 1585152 | tf_op jit(solution)/shard_map/self_upper/pallas_call | solution.py:241
  65.5 21.2 %collective-permute-done.21.refs_2_ = bf16[768,512]{1,0:T(8,128)(2,1)S(1)} collective-permute-done((bf16[768,512]{1,0:T(8,128)(2,1)S(1)}, bf16[768,512]{1,0:T(8,128)(2,1)S(1)}, u32[]{:S(2)}, u32[]{:S(2)}) %collective-permute-start.21) | collective-permute-done | bytes 786464 | tf_op jit(solution)/shard_map/ppermute | solution.py:169
  90.6 6.5 %self_lower.1 = (bf16[256,512]{1,0:T(8,128)(2,1)}, f32[4,1,512]{2,1,0:T(1,128)}) custom-call(s32[1]{0:T(128)} %bitcast.me_ref.refs_0_, bf16[256,512]{1,0:T(8,128)(2,1)} %get-tuple-element.185.query_t, bf16[1024,256]{1,0:T(8,128)(2,1)} %get-tuple-element.186.keys.refs_8_, bf16[256,1024]{1,0:T(8,128)(2,1)} %get-tuple-element.187.value_t, ...), custom_call_target="tpu_custom_call" | custom-call | flops 6325000192 | bytes 1585152 | tf_op jit(solution)/shard_map/self_lower/pallas_call | solution.py:241
  98.3 8.7 %cross_forward.1 = (f32[512,512]{1,0:T(8,128)}, f32[512,512]{1,0:T(8,128)}, bf16[512,512]{1,0:T(8,128)(2,1)}, bf16[256,512]{1,0:T(8,128)(2,1)}, bf16[256,512]{1,...) custom-call(s32[1]{0:T(128)} %bitcast.me_ref.refs_0_, ...), custom_call_target="tpu_custom_call" | custom-call | flops 10350000128 | bytes 8328192 | tf_op jit(solution)/shard_map/cross_forward/pallas_call | solution.py:241
  108.6 18.0 %inner.3 = (f32[256,512]{1,0:T(8,128)}, bf16[256,512]{1,0:T(8,128)(2,1)}, f32[512,512]{1,0:T(8,128)}, f32[8,512]{1,0:T(8,128)}, bf16[16,128,512]{2,1,0:T(8,128)(2,1)}, /*index=5*/bf16[16,128,512]{2,1,0:T(8,128)(2,1)}) custom-call(s32[1]{0:T(128)} %bitcast.me_ref.refs_0_, bf16[1024,512]{1,0:T(8,128)(2,1)} %copy-done.2, bf16[1024,512]{1,0:T(8,128)(2,1)} %copy-done.18, ...), custom_call_target="tpu_custom_call" | custom-call | flops 20700000256 | bytes 11845632 | tf_op jit(solution)/shard_map/inner/pallas_call | solution.py:241
  127.2 12.7 %cross_back.1 = (f32[512,512]{1,0:T(8,128)}, f32[128,512]{1,0:T(8,128)}, f32[128,512]{1,0:T(8,128)}, f32[16,512]{1,0:T(8,128)}, bf16[512,256]{1,0:T(8,128)(2,1)}...) custom-call(s32[1]{0:T(128)} %bitcast.me_ref.refs_0_, ...), custom_call_target="tpu_custom_call" | custom-call | flops 16099999744 | bytes 12964864 | tf_op jit(solution)/shard_map/cross_back/pallas_call | solution.py:241
  142.5 11.5 %self_back_upper.1 = (bf16[512,256]{1,0:T(8,128)(2,1)}, f32[1024,256]{1,0:T(8,128)}, f32[64,512]{1,0:T(8,128)}, bf16[64,512]{1,0:T(8,128)(2,1)}, bf16[1024,256]{...) custom-call(s32[1]{0:T(128)} %bitcast.me_ref.refs_0_, bf16[768,512]{1,0:T(8,128)(2,1)} %copy-done.4, ...), custom_call_target="tpu_custom_call" | custom-call | flops 13799999488 | bytes 13242368 | tf_op jit(solution)/shard_map/self_back_upper/pallas_call | solution.py:241
  157.3 11.2 %self_back_lower.1 = (f32[512,512]{1,0:T(8,128)}, f32[8,512]{1,0:T(8,128)}, bf16[512,512]{1,0:T(8,128)(2,1)}, f32[1024,256]{1,0:T(8,128)}, bf16[1024,256]{1,0:T(8,128)(2,1)}) custom-call(s32[1]{0:T(128)} %bitcast.me_ref.refs_0_, bf16[448,512]{1,0:T(8,128)(2,1)} %copy-done.5, bf16[448,512]{1,0:T(8,128)(2,1)} %copy-done.25, bf16[448,512]{1,0:T(8,128)(2,1)} %copy-done.26, ...), custom_call_target="tpu_custom_call" | custom-call | flops 12650000384 | bytes 8835072 | tf_op jit(solution)/shard_map/self_back_lower/pallas_call | solution.py:241
  171.4 6.0 %last.1 = (f32[256,512]{1,0:T(8,128)}, bf16[320,512]{1,0:T(8,128)(2,1)}, bf16[16,56,512]{2,1,0:T(8,128)(2,1)}, bf16[16,56,512]{2,1,0:T(8,128)(2,1)}) custom-call(s32[1]{0:T(128)} %bitcast.me_ref.refs_0_, bf16[448,512]{1,0:T(8,128)(2,1)} %copy-done.5, bf16[448,512]{1,0:T(8,128)(2,1)} %copy-done.25, bf16[448,512]{1,0:T(8,128)(2,1)} %copy-done.26, ...), custom_call_target="tpu_custom_call" | custom-call | flops 6899999744 | bytes 9994240 | tf_op jit(solution)/shard_map/last/pallas_call | solution.py:241
  186.2 3.4 %collective-permute-done.37.refs_1_ = bf16[8,96,512]{2,1,0:T(8,128)(2,1)S(1)} collective-permute-done((bf16[8,96,512]{2,1,0:T(8,128)(2,1)S(1)}, bf16[8,96,512]{2,1,0:T(8,128)(2,1)S(1)}, u32[]{:S(2)}, u32[]{:S(2)}) %collective-permute-start.37) | collective-permute-done | bytes 786464 | tf_op jit(solution)/shard_map/ppermute | solution.py:169
  193.2 3.3 %collective-permute-done.36.refs_3_ = bf16[1,128,512]{2,1,0:T(8,128)(2,1)S(1)} collective-permute-done((bf16[1,128,512]{2,1,0:T(8,128)(2,1)S(1)}, bf16[1,128,512]{2,1,0:T(8,128)(2,1)S(1)}, u32[]{:S(2)}, u32[]{:S(2)}) %collective-permute-start.36) | collective-permute-done | bytes 131104 | tf_op jit(solution)/shard_map/ppermute | solution.py:161
  197.2 6.1 %collective-permute-done.38.refs_1_ = bf16[4,96,512]{2,1,0:T(8,128)(2,1)S(1)} collective-permute-done((bf16[4,96,512]{2,1,0:T(8,128)(2,1)S(1)}, bf16[4,96,512]{2,1,0:T(8,128)(2,1)S(1)}, u32[]{:S(2)}, u32[]{:S(2)}) %collective-permute-start.38) | collective-permute-done | bytes 393248 | tf_op jit(solution)/shard_map/ppermute | solution.py:169
  204.6 3.0 %collective-permute-start.40 = (bf16[1,96,512]{2,1,0:T(8,128)(2,1)S(1)}, bf16[1,96,512]{2,1,0:T(8,128)(2,1)S(1)}, u32[]{:S(2)}, u32[]{:S(2)}) collective-permute-start(bf16[1,96,512]{2,1,0:T(8,128)(2,1)S(1)} %get-tuple-element.257), channel_id=1, source_target_pairs={{0,16},{1,17},{2,18},{3,19},{4,20},{5,21},{6,22},{7,23},{8,24},{9,... | collective-permute-start | bytes 294920 | tf_op jit(solution)/shard_map/ppermute | solution.py:161
  209.1 3.0 %collective-permute-start.46 = (bf16[1,56,512]{2,1,0:T(8,128)(2,1)S(1)}, bf16[1,56,512]{2,1,0:T(8,128)(2,1)S(1)}, u32[]{:S(2)}, u32[]{:S(2)}) collective-permute-start(bf16[1,56,512]{2,1,0:T(8,128)(2,1)S(1)} %get-tuple-element.269), channel_id=1, source_target_pairs={{0,16},{1,17},{2,18},{3,19},{4,20},{5,21},{6,22},{7,23},{8,24},{9,... | collective-permute-start | bytes 172040 | tf_op jit(solution)/shard_map/ppermute | solution.py:161
  214.7 5.2 %collective-permute-done.46.refs_10_ = bf16[1,56,512]{2,1,0:T(8,128)(2,1)S(1)} collective-permute-done((bf16[1,56,512]{2,1,0:T(8,128)(2,1)S(1)}, bf16[1,56,512]{2,1,0:T(8,128)(2,1)S(1)}, u32[]{:S(2)}, u32[]{:S(2)}) %collective-permute-start.46) | collective-permute-done | bytes 57376 | tf_op jit(solution)/shard_map/ppermute | solution.py:161
  220.5 2.5 %finish.1 = (f32[16,2048]{1,0:T(8,128)}, f32[64,512]{1,0:T(8,128)}, f32[16,512]{1,0:T(8,128)}, f32[16,512]{1,0:T(8,128)}, f32[16,512]{1,0:T(8,128)}, /*index=5*/...) custom-call(s32[1]{0:T(128)} %bitcast.me_ref.refs_0_, ...), custom_call_target="tpu_custom_call" | custom-call | flops 2300000000 | bytes 1672960 | tf_op jit(solution)/shard_map/finish/pallas_call | solution.py:241
  (194 shorter events, 62.1 us)
Async XLA Ops:
  12.6 11.7 %collective-permute-start.10 = (bf16[328,512]{1,0:T(8,128)(2,1)}, bf16[328,512]{1,0:T(8,128)(2,1)S(1)}, u32[]{:S(2)}, u32[]{:S(2)}) collective-permute-start(bf16[328,512]{1,0:T(8,128)(2,1)} %get-tuple-element.155), channel_id=1, source_target_pairs={{0,2},{1,3},{2,0},{3,1},{4,6},{5,7},{6,4},{7,5},{8,10},{9,11},{10,... | collective-permute-start | bytes 1007624 | tf_op jit(solution)/shard_map/ppermute | solution.py:161
  24.4 15.2 %collective-permute-start.12 = (bf16[448,512]{1,0:T(8,128)(2,1)S(1)}, bf16[448,512]{1,0:T(8,128)(2,1)S(1)}, u32[]{:S(2)}, u32[]{:S(2)}) collective-permute-start(bf16[448,512]{1,0:T(8,128)(2,1)S(1)} %join.8.refs_1_), channel_id=1, source_target_pairs={{0,4},{1,3},{2,6},{3,1},{4,0},{5,7},{6,2},{7,5},{8,12},{9,11},{10,... | collective-permute-start | bytes 1376264 | tf_op jit(solution)/shard_map/ppermute | solution.py:169
  25.9 13.6 %collective-permute-start.13 = (bf16[328,512]{1,0:T(8,128)(2,1)S(1)}, bf16[328,512]{1,0:T(8,128)(2,1)S(1)}, u32[]{:S(2)}, u32[]{:S(2)}) collective-permute-start(bf16[328,512]{1,0:T(8,128)(2,1)S(1)} %collective-permute-done.10.refs_6_), channel_id=1, source_target_pairs={{0,1},{1,0},{2,3},{3,2},{4,5},{5,4},{6,7},{7,6},{8,9},{9,8},{10,11... | collective-permute-start | bytes 1007624 | tf_op jit(solution)/shard_map/ppermute | solution.py:161
  40.1 12.2 %collective-permute-start.8 = (bf16[128,512]{1,0:T(8,128)(2,1)S(1)}, bf16[128,512]{1,0:T(8,128)(2,1)S(1)}, u32[]{:S(2)}, u32[]{:S(2)}) collective-permute-start(bf16[128,512]{1,0:T(8,128)(2,1)S(1)} %copy-done.6), channel_id=1, source_target_pairs={{0,24},{1,25},{2,26},{3,27},{4,28},{5,29},{6,30},{7,31},{8,16},{9,... | collective-permute-start | bytes 393224 | tf_op jit(solution)/shard_map/ppermute | solution.py:161
  42.5 11.6 %collective-permute-start.7 = (bf16[128,512]{1,0:T(8,128)(2,1)S(1)}, bf16[128,512]{1,0:T(8,128)(2,1)S(1)}, u32[]{:S(2)}, u32[]{:S(2)}) collective-permute-start(bf16[128,512]{1,0:T(8,128)(2,1)S(1)} %copy-done.6), channel_id=1, source_target_pairs={{0,16},{1,17},{2,18},{3,19},{4,20},{5,21},{6,22},{7,23},{8,24},{9,... | collective-permute-start | bytes 393224 | tf_op jit(solution)/shard_map/ppermute | solution.py:161
  42.5 11.6 %collective-permute-start.6 = (bf16[128,512]{1,0:T(8,128)(2,1)S(1)}, bf16[128,512]{1,0:T(8,128)(2,1)S(1)}, u32[]{:S(2)}, u32[]{:S(2)}) collective-permute-start(bf16[128,512]{1,0:T(8,128)(2,1)S(1)} %copy-done.6), channel_id=1, source_target_pairs={{0,8},{1,9},{2,10},{3,11},{4,12},{5,13},{6,14},{7,15},{8,0},{9,1},... | collective-permute-start | bytes 393224 | tf_op jit(solution)/shard_map/ppermute | solution.py:161
  63.4 27.2 %collective-permute-start.18 = (bf16[1024,512]{1,0:T(8,128)(2,1)S(1)}, bf16[1024,512]{1,0:T(8,128)(2,1)S(1)}, u32[]{:S(2)}, u32[]{:S(2)}) collective-permute-start(bf16[1024,512]{1,0:T(8,128)(2,1)S(1)} %join.11.refs_1_), channel_id=1, source_target_pairs={{0,4},{1,3},{2,6},{3,1},{4,0},{5,7},{6,2},{7,5},{8,12},{9,11},{10,... | collective-permute-start | bytes 3145736 | tf_op jit(solution)/shard_map/ppermute | solution.py:169
  64.0 22.7 %collective-permute-start.21 = (bf16[768,512]{1,0:T(8,128)(2,1)S(1)}, bf16[768,512]{1,0:T(8,128)(2,1)S(1)}, u32[]{:S(2)}, u32[]{:S(2)}) collective-permute-start(bf16[768,512]{1,0:T(8,128)(2,1)S(1)} %join.10.refs_1_), channel_id=1, source_target_pairs={{0,4},{1,3},{2,6},{3,1},{4,0},{5,7},{6,2},{7,5},{8,12},{9,11},{10,... | collective-permute-start | bytes 2359304 | tf_op jit(solution)/shard_map/ppermute | solution.py:169
  65.5 31.6 %collective-permute-start.22 = (bf16[768,512]{1,0:T(8,128)(2,1)S(1)}, bf16[768,512]{1,0:T(8,128)(2,1)S(1)}, u32[]{:S(2)}, u32[]{:S(2)}) collective-permute-start(bf16[768,512]{1,0:T(8,128)(2,1)S(1)} %join.10.refs_1_), channel_id=1, source_target_pairs={{0,1},{1,0},{2,3},{3,2},{4,5},{5,4},{6,7},{7,6},{8,9},{9,8},{10,11... | collective-permute-start | bytes 2359304 | tf_op jit(solution)/shard_map/ppermute | solution.py:161
  86.7 20.4 %collective-permute-start.19 = (bf16[1024,512]{1,0:T(8,128)(2,1)S(1)}, bf16[1024,512]{1,0:T(8,128)(2,1)S(1)}, u32[]{:S(2)}, u32[]{:S(2)}) collective-permute-start(bf16[1024,512]{1,0:T(8,128)(2,1)S(1)} %join.11.refs_1_), channel_id=1, source_target_pairs={{0,1},{1,0},{2,3},{3,2},{4,5},{5,4},{6,7},{7,6},{8,9},{9,8},{10,11... | collective-permute-start | bytes 3145736 | tf_op jit(solution)/shard_map/ppermute | solution.py:161
  89.1 17.9 %collective-permute-start.24 = (bf16[256,512]{1,0:T(8,128)(2,1)}, bf16[256,512]{1,0:T(8,128)(2,1)S(1)}, u32[]{:S(2)}, u32[]{:S(2)}) collective-permute-start(bf16[256,512]{1,0:T(8,128)(2,1)} %get-tuple-element.192), channel_id=1, source_target_pairs={{0,2},{1,3},{2,0},{3,1},{4,6},{5,7},{6,4},{7,5},{8,10},{9,11},{10,... | collective-permute-start | bytes 786440 | tf_op jit(solution)/shard_map/ppermute | solution.py:161
  90.6 16.4 %collective-permute-start.20 = (bf16[1024,512]{1,0:T(8,128)(2,1)S(1)}, bf16[1024,512]{1,0:T(8,128)(2,1)S(1)}, u32[]{:S(2)}, u32[]{:S(2)}) collective-permute-start(bf16[1024,512]{1,0:T(8,128)(2,1)S(1)} %collective-permute-done.18.refs_2_), channel_id=1, source_target_pairs={{0,1},{1,0},{2,3},{3,2},{4,5},{5,4},{6,7},{7,6},{8,9},{9,8},{10,11... | collective-permute-start | bytes 3145736 | tf_op jit(solution)/shard_map/ppermute | solution.py:161
  126.6 13.5 %collective-permute-start.26 = (bf16[16,128,512]{2,1,0:T(8,128)(2,1)}, bf16[16,128,512]{2,1,0:T(8,128)(2,1)S(1)}, u32[]{:S(2)}, u32[]{:S(2)}) collective-permute-start(bf16[16,128,512]{2,1,0:T(8,128)(2,1)} %get-tuple-element.198), channel_id=1, source_target_pairs={{0,1},{1,0},{2,3},{3,2},{4,5},{5,4},{6,7},{7,6},{8,9},{9,8},{10,11... | collective-permute-start | bytes 6291464 | tf_op jit(solution)/shard_map/ppermute | solution.py:161
  126.7 13.9 %collective-permute-start.25 = (bf16[256,512]{1,0:T(8,128)(2,1)}, bf16[256,512]{1,0:T(8,128)(2,1)S(1)}, u32[]{:S(2)}, u32[]{:S(2)}) collective-permute-start(bf16[256,512]{1,0:T(8,128)(2,1)} %get-tuple-element.195), channel_id=1, source_target_pairs={{0,2},{1,3},{2,0},{3,1},{4,6},{5,7},{6,4},{7,5},{8,10},{9,11},{10,... | collective-permute-start | bytes 786440 | tf_op jit(solution)/shard_map/ppermute | solution.py:161
  140.6 14.9 %collective-permute-start.27 = (bf16[8,128,512]{2,1,0:T(8,128)(2,1)S(1)}, bf16[8,128,512]{2,1,0:T(8,128)(2,1)S(1)}, u32[]{:S(2)}, u32[]{:S(2)}) collective-permute-start(bf16[8,128,512]{2,1,0:T(8,128)(2,1)S(1)} %get-tuple-element.200), channel_id=1, source_target_pairs={{0,4},{1,3},{2,6},{3,1},{4,0},{5,7},{6,2},{7,5},{8,12},{9,11},{10,... | collective-permute-start | bytes 3145736 | tf_op jit(solution)/shard_map/ppermute | solution.py:169
  154.0 15.3 %collective-permute-start.31 = (bf16[1024,256]{1,0:T(8,128)(2,1)}, bf16[1024,256]{1,0:T(8,128)(2,1)}, u32[]{:S(2)}, u32[]{:S(2)}) collective-permute-start(bf16[1024,256]{1,0:T(8,128)(2,1)} %get-tuple-element.244), channel_id=1, source_target_pairs={{0,1},{1,0},{2,3},{3,2},{4,5},{5,4},{6,7},{7,6},{8,9},{9,8},{10,11... | collective-permute-start | bytes 1572872 | tf_op jit(solution)/shard_map/ppermute | solution.py:161
  154.6 14.0 %collective-permute-start.29 = (bf16[16,96,512]{2,1,0:T(8,128)(2,1)}, bf16[16,96,512]{2,1,0:T(8,128)(2,1)S(1)}, u32[]{:S(2)}, u32[]{:S(2)}) collective-permute-start(bf16[16,96,512]{2,1,0:T(8,128)(2,1)} %get-tuple-element.234), channel_id=1, source_target_pairs={{0,1},{1,0},{2,3},{3,2},{4,5},{5,4},{6,7},{7,6},{8,9},{9,8},{10,11... | collective-permute-start | bytes 4718600 | tf_op jit(solution)/shard_map/ppermute | solution.py:161
  155.7 12.8 %collective-permute-start.30 = (bf16[4,128,512]{2,1,0:T(8,128)(2,1)S(1)}, bf16[4,128,512]{2,1,0:T(8,128)(2,1)S(1)}, u32[]{:S(2)}, u32[]{:S(2)}) collective-permute-start(bf16[4,128,512]{2,1,0:T(8,128)(2,1)S(1)} %get-tuple-element.236), channel_id=1, source_target_pairs={{0,2},{1,5},{2,0},{3,7},{4,6},{5,1},{6,4},{7,3},{8,10},{9,13},{10,... | collective-permute-start | bytes 1572872 | tf_op jit(solution)/shard_map/ppermute | solution.py:169
  177.6 12.0 %collective-permute-start.37 = (bf16[8,96,512]{2,1,0:T(8,128)(2,1)S(1)}, bf16[8,96,512]{2,1,0:T(8,128)(2,1)S(1)}, u32[]{:S(2)}, u32[]{:S(2)}) collective-permute-start(bf16[8,96,512]{2,1,0:T(8,128)(2,1)S(1)} %get-tuple-element.252), channel_id=1, source_target_pairs={{0,4},{1,3},{2,6},{3,1},{4,0},{5,7},{6,2},{7,5},{8,12},{9,11},{10,... | collective-permute-start | bytes 2359304 | tf_op jit(solution)/shard_map/ppermute | solution.py:169
  178.1 13.0 %collective-permute-start.33 = (bf16[320,512]{1,0:T(8,128)(2,1)}, bf16[320,512]{1,0:T(8,128)(2,1)S(1)}, u32[]{:S(2)}, u32[]{:S(2)}) collective-permute-start(bf16[320,512]{1,0:T(8,128)(2,1)} %get-tuple-element.247), channel_id=1, source_target_pairs={{0,2},{1,3},{2,0},{3,1},{4,6},{5,7},{6,4},{7,5},{8,10},{9,11},{10,... | collective-permute-start | bytes 983048 | tf_op jit(solution)/shard_map/ppermute | solution.py:161
  181.6 14.9 %collective-permute-start.43 = (bf16[8,56,512]{2,1,0:T(8,128)(2,1)S(1)}, bf16[8,56,512]{2,1,0:T(8,128)(2,1)S(1)}, u32[]{:S(2)}, u32[]{:S(2)}) collective-permute-start(bf16[8,56,512]{2,1,0:T(8,128)(2,1)S(1)} %get-tuple-element.262), channel_id=1, source_target_pairs={{0,4},{1,3},{2,6},{3,1},{4,0},{5,7},{6,2},{7,5},{8,12},{9,11},{10,... | collective-permute-start | bytes 1376264 | tf_op jit(solution)/shard_map/ppermute | solution.py:169
  191.2 12.1 %collective-permute-start.38 = (bf16[4,96,512]{2,1,0:T(8,128)(2,1)S(1)}, bf16[4,96,512]{2,1,0:T(8,128)(2,1)S(1)}, u32[]{:S(2)}, u32[]{:S(2)}) collective-permute-start(bf16[4,96,512]{2,1,0:T(8,128)(2,1)S(1)} %get-tuple-element.254), channel_id=1, source_target_pairs={{0,2},{1,5},{2,0},{3,7},{4,6},{5,1},{6,4},{7,3},{8,10},{9,13},{10,... | collective-permute-start | bytes 1179656 | tf_op jit(solution)/shard_map/ppermute | solution.py:169
  196.6 12.3 %collective-permute-start.44 = (bf16[4,56,512]{2,1,0:T(8,128)(2,1)S(1)}, bf16[4,56,512]{2,1,0:T(8,128)(2,1)S(1)}, u32[]{:S(2)}, u32[]{:S(2)}) collective-permute-start(bf16[4,56,512]{2,1,0:T(8,128)(2,1)S(1)} %get-tuple-element.266), channel_id=1, source_target_pairs={{0,2},{1,5},{2,0},{3,7},{4,6},{5,1},{6,4},{7,3},{8,10},{9,13},{10,... | collective-permute-start | bytes 688136 | tf_op jit(solution)/shard_map/ppermute | solution.py:169
  209.1 10.8 %collective-permute-start.46 = (bf16[1,56,512]{2,1,0:T(8,128)(2,1)S(1)}, bf16[1,56,512]{2,1,0:T(8,128)(2,1)S(1)}, u32[]{:S(2)}, u32[]{:S(2)}) collective-permute-start(bf16[1,56,512]{2,1,0:T(8,128)(2,1)S(1)} %get-tuple-element.269), channel_id=1, source_target_pairs={{0,16},{1,17},{2,18},{3,19},{4,20},{5,21},{6,22},{7,23},{8,24},{9,... | collective-permute-start | bytes 172040 | tf_op jit(solution)/shard_map/ppermute | solution.py:161
  (66 other events, 495.3 us)

commit v4 on v3

--- a/solution.py
+++ b/solution.py
@@ -235,16 +235,24 @@
     return [((width, width), F32)] * count + [((sums, width), F32)]
 
 
-def call(kernel, outs, args, scratch, micros, name):
+def padded(shape, dtype):
+    last = -(-shape[-1] // 128) * 128
+    tall = -(-shape[-2] // 16) * 16 if len(shape) > 1 else 16
+    return math.prod(shape[:-2]) * tall * last * jnp.dtype(dtype).itemsize
+
+
+def call(kernel, outs, args, scratch, micros, name, room=14):
     moved = sum(math.prod(a.shape) * a.dtype.itemsize for a in args[1:])
     moved += sum(math.prod(s) * jnp.dtype(d).itemsize for s, d in outs)
+    need = sum(padded(a.shape, a.dtype) for a in args[1:])
+    need += sum(padded(s, d) for s, d in list(outs) + list(scratch))
     return pl.pallas_call(
         kernel,
         out_shape=[jax.ShapeDtypeStruct(s, d) for s, d in outs],
         in_specs=[SM] + [VM] * (len(args) - 1),
         out_specs=[VM] * len(outs),
         scratch_shapes=[pltpu.VMEM(s, d) for s, d in scratch],
-        compiler_params=pltpu.CompilerParams(vmem_limit_bytes=56 << 20),
+        compiler_params=pltpu.CompilerParams(vmem_limit_bytes=min(need + (room << 20), 58 << 20)),
         cost_estimate=pl.CostEstimate(
             flops=int(micros * 1.15e9), bytes_accessed=moved, transcendentals=0
         ),
@@ -271,54 +279,47 @@
     return kernel, [((rows, width), BF16)] * 2
 
 
-def make_cot_packet(block, width):
-    def kernel(turn, cotangent, sent, kept):
-        sent[...] = cotangent[1 - turn[0]]
-        kept[...] = cotangent[turn[0]]
-
-    return kernel, [((block, width), BF16)] * 2
-
-
-def make_inner_packet(narrow, width, blocks):
-    def kernel(me_ref, inner, outer, out):
-        for i in range(blocks):
-            out[i * narrow : (i + 1) * narrow, :] = inner[:, i * width : (i + 1) * width]
-        out[blocks * narrow :, :] = outer[...]
-
-    return kernel, [((2 * blocks * narrow, width), BF16)]
-
-
 def placed(me, parts, width):
     here = lax.broadcasted_iota(jnp.int32, (parts.shape[1], width), 0) + me * parts.shape[1]
     lane = lax.broadcasted_iota(jnp.int32, (parts.shape[1], width), 1)
     return dot(parts, jnp.where(lane == here, 1.0, 0.0).astype(BF16))
 
 
-def make_self_packet(narrow, width):
-    def kernel(me_ref, query_w, key_w, value_w, biases, out):
-        for i, ref in enumerate((query_w, key_w, value_w)):
-            out[i * narrow : (i + 1) * narrow, :] = ref[...]
-        found = placed(me_ref[0], biases[0:2, :], width)
-        out[3 * narrow :, :] = jnp.concatenate([found, jnp.zeros((6, width), F32)], axis=0).astype(BF16)
-
-    return kernel, [((3 * narrow + 8, width), BF16)]
-
-
-def make_cross_packet(narrow, width, blocks):
+def make_weights_packet(narrow, width, blocks):
+    tall = blocks * narrow
+    starts = (0, 3 * narrow + 8, 8 * narrow + 24)
+
     def kernel(me_ref, *refs):
-        weights, short, wide, out = refs[:5], refs[5], refs[6], refs[7]
+        weights, inner, outer, short, wide, out = refs[:8], refs[8], refs[9], refs[10], refs[11], refs[12]
         me = me_ref[0]
         for i, ref in enumerate(weights):
-            out[i * narrow : (i + 1) * narrow, :] = ref[...]
-        found = placed(me, short[2:, :], width)
+            at = i * narrow if i < 3 else starts[1] + (i - 3) * narrow
+            out[at : at + narrow, :] = ref[...]
+        found = placed(me, short[...], width)
+        out[3 * narrow : starts[1], :] = jnp.concatenate([found[:2, :], jnp.zeros((6, width), F32)], axis=0).astype(BF16)
         per = width // wide.shape[1]
         row = placed(lax.rem(me, per), wide[...], width)
         place = lax.broadcasted_iota(jnp.int32, (blocks, width), 0)
         spread_row = jnp.where(place == lax.div(me, per), row, 0.0)
-        rest = jnp.zeros((16 - found.shape[0] - blocks, width), F32)
-        out[5 * narrow :, :] = jnp.concatenate([found, spread_row, rest], axis=0).astype(BF16)
-
-    return kernel, [((5 * narrow + 16, width), BF16)]
+        rest = jnp.zeros((16 - (found.shape[0] - 2) - blocks, width), F32)
+        out[starts[2] - 16 : starts[2], :] = jnp.concatenate([found[2:, :], spread_row, rest], axis=0).astype(BF16)
+        for i in range(blocks):
+            out[starts[2] + i * narrow : starts[2] + (i + 1) * narrow, :] = inner[:, i * width : (i + 1) * width]
+        out[starts[2] + tall :, :] = outer[...]
+
+    return kernel, [((starts[2] + 2 * tall, width), BF16)]
+
+
+def make_sort(rows, width):
+    def kernel(me_ref, *refs):
+        given, outs = refs[:4], refs[4:]
+        at = 0
+        for count, out in zip(rows, outs):
+            for i, ref in enumerate(given):
+                out[i * count : (i + 1) * count, :] = ref[at : at + count, :]
+            at += count
+
+    return kernel, [((4 * count, width), BF16) for count in rows]
 
 
 def join(arrays):
@@ -397,12 +398,15 @@
 
 
 def make_self_attention(share, length, width):
-    def kernel(me_ref, query_t, keys, value_t, ids, mixture_t, logs, hot, penalty):
+    def kernel(me_ref, *refs):
+        query_t, keys, value_t, ids = refs[:2], refs[2:4], refs[4:6], refs[6]
+        mixture_t, logs, hot, penalty = refs[7:9], refs[9:11], refs[11], refs[12]
         hot[...] = one_hot(ids[...])
         penalty[...] = penalties(ids[:, :share])
-        attend(query_t, keys, value_t, hot, penalty, mixture_t, logs)
-
-    outs = [((width // 2, share), BF16), ((HEADS // 2, 1, share), F32)]
+        for side in range(2):
+            attend(query_t[side], keys[side], value_t[side], hot, penalty, mixture_t[side], logs[side])
+
+    outs = [((width // 2, share), BF16)] * 2 + [((HEADS // 2, 1, share), F32)] * 2
     return kernel, outs, [((length, PAIR), BF16), ((PAIR, share), BF16)]
 
 
@@ -463,7 +467,7 @@
     return kernel, outs, scratch
 
 
-def make_inner(packed, rows, block, width, hidden, narrow, n_pieces):
+def make_inner(packed, parts, rows, block, width, hidden, narrow, n_pieces):
     blocks = hidden // width
     share = rows * block
     per = width // (blocks * narrow)
@@ -472,6 +476,7 @@
         me_ref, refs = refs[0], list(refs[1:])
         pieces, refs = refs[:n_pieces], refs[n_pieces:]
         second_sum, cot_own, cot_came, vectors = refs[:4]
+        turn = lax.rem(lax.div(me_ref[0], parts), rows)
         out_own, out_send, back, sums = refs[4:8]
         grads, scratch = refs[8:10], refs[10:]
         low, active, gate, slope = scratch[:4]
@@ -509,7 +514,7 @@
         final = normed * vector(FINAL_GAIN) + vector(FINAL_SHIFT)
         out_own[...] = final[:block, :]
         out_send[...] = final[block:, :].astype(BF16)
-        upstream = jnp.concatenate([cot_own[...], cot_came[...]], axis=0).astype(F32)
+        upstream = jnp.concatenate([cot_own[turn], cot_came[turn]], axis=0).astype(F32)
         sums[0:1, :] = total(upstream * normed)
         sums[1:2, :] = total(upstream)
         back3 = normalize_back(upstream, normed, inverse, vector(FINAL_GAIN))
@@ -864,7 +869,7 @@
         out_shape=[jax.ShapeDtypeStruct(shape, BF16)] * splits,
         in_specs=[VM] * len(arrays),
         out_specs=[VM] * splits,
-        compiler_params=pltpu.CompilerParams(vmem_limit_bytes=32 << 20),
+        compiler_params=pltpu.CompilerParams(vmem_limit_bytes=20 << 20),
         cost_estimate=pl.CostEstimate(flops=1 << 20, bytes_accessed=0, transcendentals=0),
         name="combine",
     )(*arrays)
@@ -937,24 +942,22 @@
     own_tokens = row_tokens[:rows]
 
     if packed:
-        (first,) = run(make_self_packet(narrow, width), 1.0, "self_packet",
-                       query_weight, key_weight, value_weight, short)
-        first = after(first, sent)
-        first_z = [swap(first, m, 32) for m in Z_MASKS[1:]]
-        (second,) = run(make_cross_packet(narrow, width, blocks), 1.0, "cross_packet", output_weight,
-                        source_query, source_key, source_value, source_output, short,
-                        inner_bias.reshape(1, wide))
-        (third,) = run(make_inner_packet(narrow, width, blocks), 1.0, "inner_packet", inner_weight, outer_weight)
-        first_a = join(after([first, *first_z], second, third))
-        first_b = turned_swap(first_a, 1)
-        second = after(second, first_a)
-        second_z = [swap(second, m, 32) for m in Z_MASKS[1:]]
+        (block_own,) = run(make_weights_packet(narrow, width, blocks), 1.0, "weights_packet",
+                           query_weight, key_weight, value_weight, output_weight, source_query,
+                           source_key, source_value, source_output, inner_weight, outer_weight,
+                           short, inner_bias.reshape(1, wide))
+        block_own = after(block_own, sent)
+        sizes = (3 * narrow + 8, 5 * narrow + 16, 2 * blocks * narrow)
+        first_a, second_a, third_a = run(
+            make_sort(sizes, width), 1.0, "sort", block_own, *[swap(block_own, m, 32) for m in Z_MASKS[1:]]
+        )
+        first_b, second_b = turned_swap(first_a, 1), turned_swap(second_a, 1)
         first_c = join(after([first_a, first_b], came, *kept_swaps))
         first_d = turned_swap(first_c, 2)
-        second_a = join([second, *second_z])
-        first_d = after(first_d, second_a, *came_swaps)
-        third = after(third, second_a)
-        third_z = [swap(third, m, 32) for m in Z_MASKS[1:]]
+        second_c = join([second_a, second_b])
+        second_d = turned_swap(second_c, 2)
+        third_b = turned_swap(third_a, 1)
+        first_d = after(first_d, second_c, *came_swaps)
         set_self = [first_c, first_d, swap(first_c, 1, 32), swap(first_d, 1, 32)]
         second_b = turned_swap(second_a, 1)
     else:
@@ -980,37 +983,33 @@
     )
     query, query_t, keys, values, value_t = (found[2 * i : 2 * i + 2] for i in range(5))
     row_memory, ids, memory_ids = found[10:]
-    attention = make_self_attention(share, parts * share, width)
-    if packed:
-        second_c = join(after([second_a, second_b], query_t[1]))
-        second_d = turned_swap(second_c, 2)
-        third_a = join(after([third, *third_z], query_t[1]))
-        third_b = turned_swap(third_a, 1)
-        second_e = swap(second_c, 1, 32)
-        query_t = [after(query_t[0], second_c, third_a), query_t[1]]
-    upper = run(attention, 5.5, "self_upper", query_t[0], keys[0], value_t[0], ids)
-    if packed:
-        second_d = after(second_d, upper[0])
-        set_cross = [second_c, second_d, second_e, swap(second_d, 1, 32)]
-        third_c = join(after([third_a, third_b], upper[0]))
+    query_t = list(query_t)
+    if packed:
+        third_c = join(after([third_a, third_b], query_t[0]))
         third_d = turned_swap(third_c, 2)
-        set_inner = [third_c, third_d, swap(third_c, 1, 32), swap(third_d, 1, 32)]
-        query_t = [query_t[0], after(query_t[1], third_c, second_d)]
+        second_d = after(second_d, query_t[0])
+        set_cross = [second_c, second_d, swap(second_c, 1, 32), swap(second_d, 1, 32)]
+        query_t[0] = after(query_t[0], third_c, second_d)
         set_back, set_query, set_last, set_memory = set_cross, set_self, set_self, set_cross
-        cotangent = after(cotangent, third_c)
     else:
         set_back, set_query, set_last, set_memory = [full[3], full[4], full[7]], full[:1], full[1:3], full[5:7]
-    cot_sent, cot_own = turned(make_cot_packet(block, width), "cot_packet", cotangent)
-    cot_came = swap(cot_sent, parts, devices)
-    lower = run(attention, 5.5, "self_lower", query_t[1], keys[1], value_t[1], ids)
-    mixtures, logs = (upper[0], lower[0]), (upper[1], lower[1])
+    cot_came = swap(cotangent, parts, devices)
+    found = run(
+        make_self_attention(share, parts * share, width), 12.0, "self_attention",
+        *query_t, *keys, *value_t, ids,
+    )
+    mixtures, logs = found[:2], found[2:]
+    if packed:
+        third_d = after(third_d, mixtures[0])
+        set_inner = [third_c, third_d, swap(third_c, 1, 32), swap(third_d, 1, 32)]
+        mixtures = [after(mixtures[0], third_d, cot_came), mixtures[1]]
     first_sum, second_sum, cross_query, memory_keys, memory_values, cross_t, cross_logs, vectors = run(
         make_cross_forward(packed, rows, block, parts * memory_share, width, narrow, len(set_cross)),
         9.0, "cross_forward", *set_cross, *own_tokens, row_memory, ids, memory_ids, *mixtures,
     )
     out_own, out_send, back2_in, sums_inner, *grads_inner = run(
-        make_inner(packed, rows, block, width, hidden, narrow, len(set_inner)), 18.0, "inner",
-        *set_inner, second_sum, cot_own, cot_came, vectors,
+        make_inner(packed, parts, rows, block, width, hidden, narrow, len(set_inner)), 18.0, "inner",
+        *set_inner, second_sum, cotangent, cot_came, vectors,
     )
     out_came = swap(out_send, parts, devices)
     found = run(
@@ -1039,7 +1038,9 @@
     if packed:
         keep, send = combine(inner_step, 2)
         inner_step = [keep, turned_swap(send, 1)]
-        query[1] = after(query[1], keep)
+        keep_cross, send = combine([grads_cross[0], swap(grads_cross[1], 1, 32)], 2)
+        cross_step = [keep_cross, turned_swap(send, 2)]
+        query[1] = after(query[1], keep, keep_cross)
     in_part, query_sum, query_w_grad, own_lower, *sends = run(
         make_self_back_lower(packed, parts, rows, block, width, narrow, len(set_query)), 11.0,
         "self_back_lower", *set_query, *own_tokens, query[1], keys[1], values[1], slope[1],
@@ -1051,9 +1052,9 @@
             found = combine(arrays, 4)
             return [found[0]] + [swap(a, m, 32) for a, m in zip(found[1:], Z_MASKS[1:])]
 
-        keep_cross, send = combine([grads_cross[0], swap(grads_cross[1], 1, 32)], 2)
-        cross_step = [keep_cross, turned_swap(send, 2)]
         inner_step = lowest(inner_step)
+        keep_cross, send = combine(cross_step, 2)
+        cross_step = [keep_cross, turned_swap(send, 1)]
         in_part = after(in_part, keep_cross, inner_step[0])
     in_own, in_send, *grads_last = run(
         make_last(packed, parts, rows, block, memory_block, width, narrow, len(set_last)), 6.0,
@@ -1071,11 +1072,12 @@
     memory_gradient = regroup(memory_own, in_came[block:])
 
     if packed:
-        keep, send = combine(cross_step, 2)
-        cross_step = lowest([keep, turned_swap(send, 1)])
+        grads_last[1] = after(grads_last[1], *cross_step, *inner_step)
         keep, send = combine([grads_last[0], swap(grads_last[1], 1, 32)], 2)
-        keep, send = combine(after([keep, turned_swap(send, 2)], *inner_step), 2)
-        last_step = lowest([keep, turned_swap(send, 1)])
+        last_step = [keep, turned_swap(send, 2)]
+        cross_step = lowest(cross_step)
+        keep, send = combine(after(last_step, cross_step[0]), 2)
+        last_step = lowest(after([keep, turned_swap(send, 1)], *cross_step))
 
         def plan(me_ref, *refs):
             me = me_ref[0]

time: 227 us -> 218 us (0.960)
  Pallas kernels: 99.1 us -> 58.6 us
  waiting for transfers between devices: 62.3 us -> 100 us
  starting transfers between devices: 45.8 us -> 40.8 us
    pallas_call x15 -> x12, Pallas kernels: 97.1 us -> 56.5 us  [call(): pl.pallas_call(kernel, out_shape=[jax.ShapeDtypeStruct(s, d) for s, d in...]
    ppermute x12, waiting for transfers between devices: 38.7 us -> 60.8 us  [turned_swap(): return lax.ppermute(array, AXES, pairs)]
    ppermute x36 -> x30, waiting for transfers between devices: 23.6 us -> 39.5 us  [swap(): return lax.ppermute(array, AXES, [(i, i ^ mask) for i in range(devices)])]
    ppermute x36 -> x30, starting transfers between devices: 33.3 us -> 26.5 us  [swap(): return lax.ppermute(array, AXES, [(i, i ^ mask) for i in range(devices)])]
    unnamed x84 -> x102, local copies, waits for them, and re-layouts: 7.94 us -> 11.7 us
    another operation x1, local copies, waits for them, and re-layouts: 2.68 us -> 0.06 us  [per_device(): jnp.stack([query_bias, value_bias, output_bias, attention_gain, attention...]
  transfers between devices with their start and end apart: 48 -> 42, of which waited for: 18 -> 18; matrix products, arithmetic and copies ran while one was open for 2% -> 2% of each run, Pallas kernels for 31% -> 16%
where the time goes in v4:
time: 218 us; the launch traced here: 217 us
  waiting for transfers between devices  100 us (46%)
  Pallas kernels  58.6 us (27%)
  starting transfers between devices  40.8 us (19%)
  local copies, waits for them, and re-layouts  12.3 us (6%)
  other arithmetic  3.93 us (2%)
    ppermute x12, waiting for transfers between devices, turned_swap(): return lax.ppermute(array, AXES, pairs)  60.8 us
    pallas_call x12, Pallas kernels, call(): pl.pallas_call(kernel, out_shape=[jax.ShapeDtypeStruct(s, d) for s, d in...  56.5 us
    ppermute x30, waiting for transfers between devices, swap(): return lax.ppermute(array, AXES, [(i, i ^ mask) for i in range(devices)])  39.5 us
    ppermute x30, starting transfers between devices, swap(): return lax.ppermute(array, AXES, [(i, i ^ mask) for i in range(devices)])  26.5 us
    ppermute x12, starting transfers between devices, turned_swap(): return lax.ppermute(array, AXES, pairs)  14.3 us
    unnamed x102, local copies, waits for them, and re-layouts  11.7 us
  transfers between devices with their start and end apart: 42, of which 18 were waited for; matrix products, arithmetic and copies ran while one was open for 2% of the time, Pallas kernels for 16%

profile of v4, /device:TPU:0, one launch (start us, length us, event | category | flops | bytes accessed | tf_op | source)
XLA Modules:
  0.0 217.4 jit_solution(10587267394366304899)
XLA Ops:
  5.3 5.1 %collective-permute-start.2 = (bf16[280,512]{1,0:T(8,128)(2,1)S(1)}, bf16[280,512]{1,0:T(8,128)(2,1)S(1)}, u32[]{:S(2)}, u32[]{:S(2)}) collective-permute-start(bf16[280,512]{1,0:T(8,128)(2,1)S(1)} %weights_packet.1.refs_0_), channel_id=1, source_target_pairs={{0,24},{1,25},{2,26},{3,27},{4,28},{5,29},{6,30},{7,31},{8,16},{9,... | collective-permute-start | bytes 860168 | tf_op jit(solution)/shard_map/ppermute | solution.py:161
  11.0 1.7 collective-permute-start.5
  12.7 5.5 %collective-permute-done.2.refs_3_ = bf16[280,512]{1,0:T(8,128)(2,1)S(1)} collective-permute-done((bf16[280,512]{1,0:T(8,128)(2,1)S(1)}, bf16[280,512]{1,0:T(8,128)(2,1)S(1)}, u32[]{:S(2)}, u32[]{:S(2)}) %collective-permute-start.2) | collective-permute-done | bytes 286752 | tf_op jit(solution)/shard_map/ppermute | solution.py:161
  18.2 16.6 %collective-permute-done.1.refs_2_ = bf16[280,512]{1,0:T(8,128)(2,1)S(1)} collective-permute-done((bf16[280,512]{1,0:T(8,128)(2,1)S(1)}, bf16[280,512]{1,0:T(8,128)(2,1)S(1)}, u32[]{:S(2)}, u32[]{:S(2)}) %collective-permute-start.1) | collective-permute-done | bytes 286752 | tf_op jit(solution)/shard_map/ppermute | solution.py:161
  36.5 4.5 %collective-permute-done.4.refs_1_ = bf16[224,512]{1,0:T(8,128)(2,1)S(1)} collective-permute-done((bf16[224,512]{1,0:T(8,128)(2,1)S(1)}, bf16[224,512]{1,0:T(8,128)(2,1)S(1)}, u32[]{:S(2)}, u32[]{:S(2)}) %collective-permute-start.4) | collective-permute-done | bytes 229408 | tf_op jit(solution)/shard_map/ppermute | solution.py:169
  44.6 6.5 %collective-permute-done.8.refs_1_ = bf16[384,512]{1,0:T(8,128)(2,1)S(1)} collective-permute-done((bf16[384,512]{1,0:T(8,128)(2,1)S(1)}, bf16[384,512]{1,0:T(8,128)(2,1)S(1)}, u32[]{:S(2)}, u32[]{:S(2)}) %collective-permute-start.8) | collective-permute-done | bytes 393248 | tf_op jit(solution)/shard_map/ppermute | solution.py:169
  55.9 1.7 project.1
  57.6 22.3 %collective-permute-done.3.refs_1_ = bf16[512,512]{1,0:T(8,128)(2,1)S(1)} collective-permute-done((bf16[512,512]{1,0:T(8,128)(2,1)S(1)}, bf16[512,512]{1,0:T(8,128)(2,1)S(1)}, u32[]{:S(2)}, u32[]{:S(2)}) %collective-permute-start.3) | collective-permute-done | bytes 524320 | tf_op jit(solution)/shard_map/ppermute | solution.py:169
  80.8 8.3 %self_attention.1 = (bf16[256,512]{1,0:T(8,128)(2,1)S(1)}, bf16[256,512]{1,0:T(8,128)(2,1)S(1)}, f32[4,1,512]{2,1,0:T(1,128)S(1)}, f32[4,1,512]{2,1,0:T(1,128)S(1)}) custom-call(s32[1]{0:T(128)} %bitcast.me_ref.refs_0_, bf16[256,512]{1,0:T(8,128)(2,1)S(1)} %get-tuple-element.160.refs_0_, bf16[256,512]{1,0:T(8,128)(2,1)S(1)} %get-tuple-element.161.refs_1_, ...), custom_call_target="tpu_custom_call" | custom-call | flops 13799999488 | bytes 3166208 | tf_op jit(solution)/shard_map/self_attention/pallas_call | solution.py:249
  89.1 5.8 %collective-permute-done.12.refs_2_ = bf16[1024,512]{1,0:T(8,128)(2,1)S(1)} collective-permute-done((bf16[1024,512]{1,0:T(8,128)(2,1)S(1)}, bf16[1024,512]{1,0:T(8,128)(2,1)S(1)}, u32[]{:S(2)}, u32[]{:S(2)}) %collective-permute-start.12) | collective-permute-done | bytes 1048608 | tf_op jit(solution)/shard_map/ppermute | solution.py:169
  95.0 5.4 %cross_forward.1 = (f32[512,512]{1,0:T(8,128)S(1)}, f32[512,512]{1,0:T(8,128)S(1)}, bf16[512,512]{1,0:T(8,128)(2,1)S(1)}, bf16[256,512]{1,0:T(8,128)(2,1)S(1)}, ...) custom-call(s32[1]{0:T(128)} %bitcast.me_ref.refs_0_, ...), custom_call_target="tpu_custom_call" | custom-call | flops 10350000128 | bytes 8328192 | tf_op jit(solution)/shard_map/cross_forward/pallas_call | solution.py:249
  101.9 14.6 %inner.1 = (f32[256,512]{1,0:T(8,128)S(1)}, bf16[256,512]{1,0:T(8,128)(2,1)S(1)}, f32[512,512]{1,0:T(8,128)S(1)}, f32[8,512]{1,0:T(8,128)S(1)}, bf16[16,128,512]...) custom-call(s32[1]{0:T(128)} %bitcast.me_ref.refs_0_, bf16[1024,512]{1,0:T(8,128)(2,1)S(1)} %join.5.refs_1_, ...), custom_call_target="tpu_custom_call" | custom-call | flops 20700000256 | bytes 12369920 | tf_op jit(solution)/shard_map/inner/pallas_call | solution.py:249
  120.5 8.4 %cross_back.1 = (f32[512,512]{1,0:T(8,128)S(1)}, f32[128,512]{1,0:T(8,128)S(1)}, f32[128,512]{1,0:T(8,128)S(1)}, f32[16,512]{1,0:T(8,128)S(1)}, bf16[512,256]{1,...) custom-call(s32[1]{0:T(128)} %bitcast.me_ref.refs_0_, ...), custom_call_target="tpu_custom_call" | custom-call | flops 16099999744 | bytes 12964864 | tf_op jit(solution)/shard_map/cross_back/pallas_call | solution.py:249
  130.5 7.2 %self_back_upper.1 = (bf16[512,256]{1,0:T(8,128)(2,1)S(1)}, f32[1024,256]{1,0:T(8,128)S(1)}, f32[64,512]{1,0:T(8,128)S(1)}, bf16[64,512]{1,0:T(8,128)(2,1)S(1)},...) custom-call(s32[1]{0:T(128)} %bitcast.me_ref.refs_0_, ...), custom_call_target="tpu_custom_call" | custom-call | flops 13799999488 | bytes 13242368 | tf_op jit(solution)/shard_map/self_back_upper/pallas_call | solution.py:249
  139.5 13.2 %collective-permute-done.21.refs_1_ = bf16[8,128,512]{2,1,0:T(8,128)(2,1)S(1)} collective-permute-done((bf16[8,128,512]{2,1,0:T(8,128)(2,1)S(1)}, bf16[8,128,512]{2,1,0:T(8,128)(2,1)S(1)}, u32[]{:S(2)}, u32[]{:S(2)}) %collective-permute-start.21) | collective-permute-done | bytes 1048608 | tf_op jit(solution)/shard_map/ppermute | solution.py:169
  155.5 7.1 %self_back_lower.1 = (f32[512,512]{1,0:T(8,128)S(1)}, f32[8,512]{1,0:T(8,128)S(1)}, bf16[512,512]{1,0:T(8,128)(2,1)S(1)}, f32[1024,256]{1,0:T(8,128)S(1)}, bf16[1024,256]{1,0:T(8,128)(2,1)S(1)}) custom-call(s32[1]{0:T(128)} %bitcast.me_ref.refs_0_, bf16[448,512]{1,0:T(8,128)(2,1)S(1)} %join.3.refs_1_, bf16[448,512]{1,0:T(8,128)(2,1)S(1)} %collective-permute-done.7.refs_2_, ...), custom_call_target="tpu_custom_call" | custom-call | flops 12650000384 | bytes 8835072 | tf_op jit(solution)/shard_map/self_back_lower/pallas_call | solution.py:249
  162.7 5.2 %collective-permute-done.25.refs_1_ = bf16[4,128,512]{2,1,0:T(8,128)(2,1)S(1)} collective-permute-done((bf16[4,128,512]{2,1,0:T(8,128)(2,1)S(1)}, bf16[4,128,512]{2,1,0:T(8,128)(2,1)S(1)}, u32[]{:S(2)}, u32[]{:S(2)}) %collective-permute-start.25) | collective-permute-done | bytes 524320 | tf_op jit(solution)/shard_map/ppermute | solution.py:169
  168.1 2.8 %collective-permute-start.30 = (bf16[1,128,512]{2,1,0:T(8,128)(2,1)S(1)}, bf16[1,128,512]{2,1,0:T(8,128)(2,1)S(1)}, u32[]{:S(2)}, u32[]{:S(2)}) collective-permute-start(bf16[1,128,512]{2,1,0:T(8,128)(2,1)S(1)} %get-tuple-element.233), channel_id=1, source_target_pairs={{0,16},{1,17},{2,18},{3,19},{4,20},{5,21},{6,22},{7,23},{8,24},{9,... | collective-permute-start | bytes 393224 | tf_op jit(solution)/shard_map/ppermute | solution.py:161
  174.2 2.4 %last.1 = (f32[256,512]{1,0:T(8,128)S(1)}, bf16[320,512]{1,0:T(8,128)(2,1)S(1)}, bf16[16,56,512]{2,1,0:T(8,128)(2,1)S(1)}, bf16[16,56,512]{2,1,0:T(8,128)(2,1)}) custom-call(s32[1]{0:T(128)} %bitcast.me_ref.refs_0_, bf16[448,512]{1,0:T(8,128)(2,1)S(1)} %join.3.refs_1_, bf16[448,512]{1,0:T(8,128)(2,1)S(1)} %collective-permute-done.7.refs_2_, ...), custom_call_target="tpu_custom_call" | custom-call | flops 6899999744 | bytes 9994240 | tf_op jit(solution)/shard_map/last/pallas_call | solution.py:249
  186.6 5.4 %collective-permute-done.28 = bf16[320,512]{1,0:T(8,128)(2,1)S(1)} collective-permute-done((bf16[320,512]{1,0:T(8,128)(2,1)}, bf16[320,512]{1,0:T(8,128)(2,1)S(1)}, u32[]{:S(2)}, u32[]{:S(2)}) %collective-permute-start.28) | collective-permute-done | bytes 327712 | tf_op jit(solution)/shard_map/ppermute | solution.py:161
  194.9 2.5 %collective-permute-start.34 = (bf16[1,96,512]{2,1,0:T(8,128)(2,1)S(1)}, bf16[1,96,512]{2,1,0:T(8,128)(2,1)S(1)}, u32[]{:S(2)}, u32[]{:S(2)}) collective-permute-start(bf16[1,96,512]{2,1,0:T(8,128)(2,1)S(1)} %get-tuple-element.238), channel_id=1, source_target_pairs={{0,16},{1,17},{2,18},{3,19},{4,20},{5,21},{6,22},{7,23},{8,24},{9,... | collective-permute-start | bytes 294920 | tf_op jit(solution)/shard_map/ppermute | solution.py:161
  200.5 4.4 %collective-permute-done.35.refs_7_ = bf16[1,96,512]{2,1,0:T(8,128)(2,1)S(1)} collective-permute-done((bf16[1,96,512]{2,1,0:T(8,128)(2,1)S(1)}, bf16[1,96,512]{2,1,0:T(8,128)(2,1)S(1)}, u32[]{:S(2)}, u32[]{:S(2)}) %collective-permute-start.35) | collective-permute-done | bytes 98336 | tf_op jit(solution)/shard_map/ppermute | solution.py:161
  204.9 2.4 %collective-permute-start.39 = (bf16[1,56,512]{2,1,0:T(8,128)(2,1)S(1)}, bf16[1,56,512]{2,1,0:T(8,128)(2,1)S(1)}, u32[]{:S(2)}, u32[]{:S(2)}) collective-permute-start(bf16[1,56,512]{2,1,0:T(8,128)(2,1)S(1)} %get-tuple-element.252), channel_id=1, source_target_pairs={{0,8},{1,9},{2,10},{3,11},{4,12},{5,13},{6,14},{7,15},{8,0},{9,1},... | collective-permute-start | bytes 172040 | tf_op jit(solution)/shard_map/ppermute | solution.py:161
  210.5 4.9 %collective-permute-done.40.refs_10_ = bf16[1,56,512]{2,1,0:T(8,128)(2,1)S(1)} collective-permute-done((bf16[1,56,512]{2,1,0:T(8,128)(2,1)S(1)}, bf16[1,56,512]{2,1,0:T(8,128)(2,1)S(1)}, u32[]{:S(2)}, u32[]{:S(2)}) %collective-permute-start.40) | collective-permute-done | bytes 57376 | tf_op jit(solution)/shard_map/ppermute | solution.py:161
  (194 shorter events, 52.0 us)
Async XLA Ops:
  5.3 12.9 %collective-permute-start.2 = (bf16[280,512]{1,0:T(8,128)(2,1)S(1)}, bf16[280,512]{1,0:T(8,128)(2,1)S(1)}, u32[]{:S(2)}, u32[]{:S(2)}) collective-permute-start(bf16[280,512]{1,0:T(8,128)(2,1)S(1)} %weights_packet.1.refs_0_), channel_id=1, source_target_pairs={{0,24},{1,25},{2,26},{3,27},{4,28},{5,29},{6,30},{7,31},{8,16},{9,... | collective-permute-start | bytes 860168 | tf_op jit(solution)/shard_map/ppermute | solution.py:161
  10.4 24.4 %collective-permute-start.1 = (bf16[280,512]{1,0:T(8,128)(2,1)S(1)}, bf16[280,512]{1,0:T(8,128)(2,1)S(1)}, u32[]{:S(2)}, u32[]{:S(2)}) collective-permute-start(bf16[280,512]{1,0:T(8,128)(2,1)S(1)} %weights_packet.1.refs_0_), channel_id=1, source_target_pairs={{0,16},{1,17},{2,18},{3,19},{4,20},{5,21},{6,22},{7,23},{8,24},{9,... | collective-permute-start | bytes 860168 | tf_op jit(solution)/shard_map/ppermute | solution.py:161
  10.4 24.4 %collective-permute-start = (bf16[280,512]{1,0:T(8,128)(2,1)S(1)}, bf16[280,512]{1,0:T(8,128)(2,1)S(1)}, u32[]{:S(2)}, u32[]{:S(2)}) collective-permute-start(bf16[280,512]{1,0:T(8,128)(2,1)S(1)} %weights_packet.1.refs_0_), channel_id=1, source_target_pairs={{0,8},{1,9},{2,10},{3,11},{4,12},{5,13},{6,14},{7,15},{8,0},{9,1},... | collective-permute-start | bytes 860168 | tf_op jit(solution)/shard_map/ppermute | solution.py:161
  11.0 25.5 %collective-permute-start.5 = (bf16[328,512]{1,0:T(8,128)(2,1)S(1)}, bf16[328,512]{1,0:T(8,128)(2,1)S(1)}, u32[]{:S(2)}, u32[]{:S(2)}) collective-permute-start(bf16[328,512]{1,0:T(8,128)(2,1)S(1)} %get-tuple-element.147), channel_id=1, source_target_pairs={{0,2},{1,3},{2,0},{3,1},{4,6},{5,7},{6,4},{7,5},{8,10},{9,11},{10,... | collective-permute-start | bytes 1007624 | tf_op jit(solution)/shard_map/ppermute | solution.py:161
  12.7 23.8 %collective-permute-start.6 = (bf16[328,512]{1,0:T(8,128)(2,1)S(1)}, bf16[328,512]{1,0:T(8,128)(2,1)S(1)}, u32[]{:S(2)}, u32[]{:S(2)}) collective-permute-start(bf16[328,512]{1,0:T(8,128)(2,1)S(1)} %get-tuple-element.151.refs_5_), channel_id=1, source_target_pairs={{0,1},{1,0},{2,3},{3,2},{4,5},{5,4},{6,7},{7,6},{8,9},{9,8},{10,11... | collective-permute-start | bytes 1007624 | tf_op jit(solution)/shard_map/ppermute | solution.py:161
  41.0 11.3 %collective-permute-start.7 = (bf16[448,512]{1,0:T(8,128)(2,1)S(1)}, bf16[448,512]{1,0:T(8,128)(2,1)S(1)}, u32[]{:S(2)}, u32[]{:S(2)}) collective-permute-start(bf16[448,512]{1,0:T(8,128)(2,1)S(1)} %join.3.refs_1_), channel_id=1, source_target_pairs={{0,4},{1,3},{2,6},{3,1},{4,0},{5,7},{6,2},{7,5},{8,12},{9,11},{10,... | collective-permute-start | bytes 1376264 | tf_op jit(solution)/shard_map/ppermute | solution.py:169
  44.1 11.8 %collective-permute-start.10 = (bf16[448,512]{1,0:T(8,128)(2,1)S(1)}, bf16[448,512]{1,0:T(8,128)(2,1)S(1)}, u32[]{:S(2)}, u32[]{:S(2)}) collective-permute-start(bf16[448,512]{1,0:T(8,128)(2,1)S(1)} %join.3.refs_1_), channel_id=1, source_target_pairs={{0,1},{1,0},{2,3},{3,2},{4,5},{5,4},{6,7},{7,6},{8,9},{9,8},{10,11... | collective-permute-start | bytes 1376264 | tf_op jit(solution)/shard_map/ppermute | solution.py:161
  52.4 28.3 %collective-permute-start.13 = (bf16[768,512]{1,0:T(8,128)(2,1)S(1)}, bf16[768,512]{1,0:T(8,128)(2,1)S(1)}, u32[]{:S(2)}, u32[]{:S(2)}) collective-permute-start(bf16[768,512]{1,0:T(8,128)(2,1)S(1)} %join.4.refs_1_), channel_id=1, source_target_pairs={{0,4},{1,3},{2,6},{3,1},{4,0},{5,7},{6,2},{7,5},{8,12},{9,11},{10,... | collective-permute-start | bytes 2359304 | tf_op jit(solution)/shard_map/ppermute | solution.py:169
  53.9 41.1 %collective-permute-start.18 = (bf16[2,256,512]{2,1,0:T(8,128)(2,1)S(1)}, bf16[2,256,512]{2,1,0:T(8,128)(2,1)S(1)}, u32[]{:S(2)}, u32[]{:S(2)}) collective-permute-start(bf16[2,256,512]{2,1,0:T(8,128)(2,1)S(1)} %copy-done.4), channel_id=1, source_target_pairs={{0,2},{1,3},{2,0},{3,1},{4,6},{5,7},{6,4},{7,5},{8,10},{9,11},{10,... | collective-permute-start | bytes 1572872 | tf_op jit(solution)/shard_map/ppermute | solution.py:161
  54.4 25.6 %collective-permute-start.3 = (bf16[512,512]{1,0:T(8,128)(2,1)S(1)}, bf16[512,512]{1,0:T(8,128)(2,1)S(1)}, u32[]{:S(2)}, u32[]{:S(2)}) collective-permute-start(bf16[512,512]{1,0:T(8,128)(2,1)S(1)} %get-tuple-element.157.refs_0_), channel_id=1, source_target_pairs={{0,2},{1,5},{2,0},{3,7},{4,6},{5,1},{6,4},{7,3},{8,10},{9,13},{10,... | collective-permute-start | bytes 1572872 | tf_op jit(solution)/shard_map/ppermute | solution.py:169
  55.9 39.1 %collective-permute-start.16 = (bf16[768,512]{1,0:T(8,128)(2,1)S(1)}, bf16[768,512]{1,0:T(8,128)(2,1)S(1)}, u32[]{:S(2)}, u32[]{:S(2)}) collective-permute-start(bf16[768,512]{1,0:T(8,128)(2,1)S(1)} %join.4.refs_1_), channel_id=1, source_target_pairs={{0,1},{1,0},{2,3},{3,2},{4,5},{5,4},{6,7},{7,6},{8,9},{9,8},{10,11... | collective-permute-start | bytes 2359304 | tf_op jit(solution)/shard_map/ppermute | solution.py:161
  80.0 21.9 %collective-permute-start.14 = (bf16[1024,512]{1,0:T(8,128)(2,1)S(1)}, bf16[1024,512]{1,0:T(8,128)(2,1)S(1)}, u32[]{:S(2)}, u32[]{:S(2)}) collective-permute-start(bf16[1024,512]{1,0:T(8,128)(2,1)S(1)} %join.5.refs_1_), channel_id=1, source_target_pairs={{0,1},{1,0},{2,3},{3,2},{4,5},{5,4},{6,7},{7,6},{8,9},{9,8},{10,11... | collective-permute-start | bytes 3145736 | tf_op jit(solution)/shard_map/ppermute | solution.py:161
  80.1 14.9 %collective-permute-start.12 = (bf16[1024,512]{1,0:T(8,128)(2,1)S(1)}, bf16[1024,512]{1,0:T(8,128)(2,1)S(1)}, u32[]{:S(2)}, u32[]{:S(2)}) collective-permute-start(bf16[1024,512]{1,0:T(8,128)(2,1)S(1)} %join.5.refs_1_), channel_id=1, source_target_pairs={{0,4},{1,3},{2,6},{3,1},{4,0},{5,7},{6,2},{7,5},{8,12},{9,11},{10,... | collective-permute-start | bytes 3145736 | tf_op jit(solution)/shard_map/ppermute | solution.py:169
  80.6 14.3 %collective-permute-start.17 = (bf16[768,512]{1,0:T(8,128)(2,1)S(1)}, bf16[768,512]{1,0:T(8,128)(2,1)S(1)}, u32[]{:S(2)}, u32[]{:S(2)}) collective-permute-start(bf16[768,512]{1,0:T(8,128)(2,1)S(1)} %collective-permute-done.13.refs_2_), channel_id=1, source_target_pairs={{0,1},{1,0},{2,3},{3,2},{4,5},{5,4},{6,7},{7,6},{8,9},{9,8},{10,11... | collective-permute-start | bytes 2359304 | tf_op jit(solution)/shard_map/ppermute | solution.py:161
  116.6 12.4 %collective-permute-start.20 = (bf16[16,128,512]{2,1,0:T(8,128)(2,1)}, bf16[16,128,512]{2,1,0:T(8,128)(2,1)S(1)}, u32[]{:S(2)}, u32[]{:S(2)}) collective-permute-start(bf16[16,128,512]{2,1,0:T(8,128)(2,1)} %get-tuple-element.179), channel_id=1, source_target_pairs={{0,1},{1,0},{2,3},{3,2},{4,5},{5,4},{6,7},{7,6},{8,9},{9,8},{10,11... | collective-permute-start | bytes 6291464 | tf_op jit(solution)/shard_map/ppermute | solution.py:161
  117.1 12.9 %collective-permute-start.19 = (bf16[256,512]{1,0:T(8,128)(2,1)S(1)}, bf16[256,512]{1,0:T(8,128)(2,1)}, u32[]{:S(2)}, u32[]{:S(2)}) collective-permute-start(bf16[256,512]{1,0:T(8,128)(2,1)S(1)} %get-tuple-element.176), channel_id=1, source_target_pairs={{0,2},{1,3},{2,0},{3,1},{4,6},{5,7},{6,4},{7,5},{8,10},{9,11},{10,... | collective-permute-start | bytes 786440 | tf_op jit(solution)/shard_map/ppermute | solution.py:161
  137.7 16.9 %collective-permute-start.23 = (bf16[16,96,512]{2,1,0:T(8,128)(2,1)S(1)}, bf16[16,96,512]{2,1,0:T(8,128)(2,1)S(1)}, u32[]{:S(2)}, u32[]{:S(2)}) collective-permute-start(bf16[16,96,512]{2,1,0:T(8,128)(2,1)S(1)} %get-tuple-element.206), channel_id=1, source_target_pairs={{0,1},{1,0},{2,3},{3,2},{4,5},{5,4},{6,7},{7,6},{8,9},{9,8},{10,11... | collective-permute-start | bytes 4718600 | tf_op jit(solution)/shard_map/ppermute | solution.py:161
  137.9 14.8 %collective-permute-start.21 = (bf16[8,128,512]{2,1,0:T(8,128)(2,1)S(1)}, bf16[8,128,512]{2,1,0:T(8,128)(2,1)S(1)}, u32[]{:S(2)}, u32[]{:S(2)}) collective-permute-start(bf16[8,128,512]{2,1,0:T(8,128)(2,1)S(1)} %get-tuple-element.181), channel_id=1, source_target_pairs={{0,4},{1,3},{2,6},{3,1},{4,0},{5,7},{6,2},{7,5},{8,12},{9,11},{10,... | collective-permute-start | bytes 3145736 | tf_op jit(solution)/shard_map/ppermute | solution.py:169
  138.4 34.3 %collective-permute-start.26 = (bf16[1024,256]{1,0:T(8,128)(2,1)S(1)}, bf16[1024,256]{1,0:T(8,128)(2,1)S(1)}, u32[]{:S(2)}, u32[]{:S(2)}) collective-permute-start(bf16[1024,256]{1,0:T(8,128)(2,1)S(1)} %get-tuple-element.227), channel_id=1, source_target_pairs={{0,1},{1,0},{2,3},{3,2},{4,5},{5,4},{6,7},{7,6},{8,9},{9,8},{10,11... | collective-permute-start | bytes 1572872 | tf_op jit(solution)/shard_map/ppermute | solution.py:161
  153.0 14.8 %collective-permute-start.25 = (bf16[4,128,512]{2,1,0:T(8,128)(2,1)S(1)}, bf16[4,128,512]{2,1,0:T(8,128)(2,1)S(1)}, u32[]{:S(2)}, u32[]{:S(2)}) collective-permute-start(bf16[4,128,512]{2,1,0:T(8,128)(2,1)S(1)} %get-tuple-element.219), channel_id=1, source_target_pairs={{0,2},{1,5},{2,0},{3,7},{4,6},{5,1},{6,4},{7,3},{8,10},{9,13},{10,... | collective-permute-start | bytes 1572872 | tf_op jit(solution)/shard_map/ppermute | solution.py:169
  155.0 15.9 %collective-permute-start.24 = (bf16[8,96,512]{2,1,0:T(8,128)(2,1)S(1)}, bf16[8,96,512]{2,1,0:T(8,128)(2,1)S(1)}, u32[]{:S(2)}, u32[]{:S(2)}) collective-permute-start(bf16[8,96,512]{2,1,0:T(8,128)(2,1)S(1)} %get-tuple-element.217), channel_id=1, source_target_pairs={{0,4},{1,3},{2,6},{3,1},{4,0},{5,7},{6,2},{7,5},{8,12},{9,11},{10,... | collective-permute-start | bytes 2359304 | tf_op jit(solution)/shard_map/ppermute | solution.py:169
  162.6 11.6 %collective-permute-start.27 = (bf16[1024,256]{1,0:T(8,128)(2,1)S(1)}, bf16[1024,256]{1,0:T(8,128)(2,1)S(1)}, u32[]{:S(2)}, u32[]{:S(2)}) collective-permute-start(bf16[1024,256]{1,0:T(8,128)(2,1)S(1)} %get-tuple-element.228), channel_id=1, source_target_pairs={{0,1},{1,0},{2,3},{3,2},{4,5},{5,4},{6,7},{7,6},{8,9},{9,8},{10,11... | collective-permute-start | bytes 1572872 | tf_op jit(solution)/shard_map/ppermute | solution.py:161
  181.2 10.7 %collective-permute-start.28 = (bf16[320,512]{1,0:T(8,128)(2,1)}, bf16[320,512]{1,0:T(8,128)(2,1)S(1)}, u32[]{:S(2)}, u32[]{:S(2)}) collective-permute-start(bf16[320,512]{1,0:T(8,128)(2,1)} %copy-done.7), channel_id=1, source_target_pairs={{0,2},{1,3},{2,0},{3,1},{4,6},{5,7},{6,4},{7,5},{8,10},{9,11},{10,... | collective-permute-start | bytes 983048 | tf_op jit(solution)/shard_map/ppermute | solution.py:161
  192.8 12.1 %collective-permute-start.38 = (bf16[4,56,512]{2,1,0:T(8,128)(2,1)S(1)}, bf16[4,56,512]{2,1,0:T(8,128)(2,1)S(1)}, u32[]{:S(2)}, u32[]{:S(2)}) collective-permute-start(bf16[4,56,512]{2,1,0:T(8,128)(2,1)S(1)} %get-tuple-element.248), channel_id=1, source_target_pairs={{0,2},{1,5},{2,0},{3,7},{4,6},{5,1},{6,4},{7,3},{8,10},{9,13},{10,... | collective-permute-start | bytes 688136 | tf_op jit(solution)/shard_map/ppermute | solution.py:169
  (69 other events, 463.2 us)

commit v5 on v4

--- a/solution.py
+++ b/solution.py
@@ -161,12 +161,11 @@
     return lax.ppermute(array, AXES, [(i, i ^ mask) for i in range(devices)])
 
 
+ORDERS = ((8, 16, 2, 4), (16, 8, 4, 2))
+
+
 def turned_swap(array, step):
-    pairs = []
-    for i in range(32):
-        near = 2 if i % 2 == 0 else 4
-        pairs.append((i, i ^ (near if step == 1 else 6 - near)))
-    return lax.ppermute(array, AXES, pairs)
+    return lax.ppermute(array, AXES, [(i, i ^ ORDERS[i % 2][step]) for i in range(32)])
 
 
 def after(value, *others):
@@ -176,16 +175,15 @@
 def places(me):
     found = []
     for core in range(2):
-        near = jnp.where(((me & 1) ^ core) == 0, 2, 4)
+        even = ((me & 1) ^ core) == 0
+        masks = [jnp.where(even, first, second) for first, second in zip(*ORDERS)]
         for far in range(2):
-            for step in range(2):
-                for at, mask in enumerate(Z_MASKS):
-                    device = me ^ (core | mask)
-                    if step:
-                        device = device ^ near
-                    if far:
-                        device = device ^ (6 - near)
-                    found.append((core, far, step * 4 + at, device))
+            for slot in range(8):
+                device = me ^ core if core else me
+                for step, bit in enumerate((slot & 1, slot & 2, slot & 4, far)):
+                    if bit:
+                        device = device ^ masks[step]
+                found.append((core, far, slot, device))
     return found
 
 
@@ -241,7 +239,7 @@
     return math.prod(shape[:-2]) * tall * last * jnp.dtype(dtype).itemsize
 
 
-def call(kernel, outs, args, scratch, micros, name, room=14):
+def call(kernel, outs, args, scratch, micros, name, room=10):
     moved = sum(math.prod(a.shape) * a.dtype.itemsize for a in args[1:])
     moved += sum(math.prod(s) * jnp.dtype(d).itemsize for s, d in outs)
     need = sum(padded(a.shape, a.dtype) for a in args[1:])
@@ -261,9 +259,9 @@
 
 
 def make_tokens_packet(block, memory_block, width):
-    rows = block + memory_block + 8
-
-    def kernel(turn, tokens, memory, target_ids, source_ids, sent, kept):
+    first = block + memory_block + 8
+
+    def kernel(turn, tokens, memory, target_ids, source_ids, cotangent, sent, kept):
         mine = turn[0]
         for row, out in ((1 - mine, sent), (mine, kept)):
             out[:block, :] = tokens[row]
@@ -274,9 +272,10 @@
             others = jnp.concatenate([others, jnp.zeros((1, width - memory_block), F32)], axis=1)
             place = lax.broadcasted_iota(jnp.int32, (8, width), 0)
             found = jnp.where(place == 0, ids, jnp.where(place == 1, others, 0.0))
-            out[block + memory_block :, :] = found.astype(BF16)
-
-    return kernel, [((rows, width), BF16)] * 2
+            out[block + memory_block : first, :] = found.astype(BF16)
+            out[first:, :] = cotangent[row]
+
+    return kernel, [((first + block, width), BF16)] * 2
 
 
 def placed(me, parts, width):
@@ -287,39 +286,29 @@
 
 def make_weights_packet(narrow, width, blocks):
     tall = blocks * narrow
-    starts = (0, 3 * narrow + 8, 8 * narrow + 24)
 
     def kernel(me_ref, *refs):
-        weights, inner, outer, short, wide, out = refs[:8], refs[8], refs[9], refs[10], refs[11], refs[12]
+        weights, inner, outer, short, wide = refs[:8], refs[8], refs[9], refs[10], refs[11]
+        first, second, third = refs[12:]
         me = me_ref[0]
         for i, ref in enumerate(weights):
-            at = i * narrow if i < 3 else starts[1] + (i - 3) * narrow
-            out[at : at + narrow, :] = ref[...]
+            if i < 3:
+                first[i * narrow : (i + 1) * narrow, :] = ref[...]
+            else:
+                second[(i - 3) * narrow : (i - 2) * narrow, :] = ref[...]
         found = placed(me, short[...], width)
-        out[3 * narrow : starts[1], :] = jnp.concatenate([found[:2, :], jnp.zeros((6, width), F32)], axis=0).astype(BF16)
+        first[3 * narrow :, :] = jnp.concatenate([found[:2, :], jnp.zeros((6, width), F32)], axis=0).astype(BF16)
         per = width // wide.shape[1]
         row = placed(lax.rem(me, per), wide[...], width)
         place = lax.broadcasted_iota(jnp.int32, (blocks, width), 0)
         spread_row = jnp.where(place == lax.div(me, per), row, 0.0)
         rest = jnp.zeros((16 - (found.shape[0] - 2) - blocks, width), F32)
-        out[starts[2] - 16 : starts[2], :] = jnp.concatenate([found[2:, :], spread_row, rest], axis=0).astype(BF16)
+        second[5 * narrow :, :] = jnp.concatenate([found[2:, :], spread_row, rest], axis=0).astype(BF16)
         for i in range(blocks):
-            out[starts[2] + i * narrow : starts[2] + (i + 1) * narrow, :] = inner[:, i * width : (i + 1) * width]
-        out[starts[2] + tall :, :] = outer[...]
-
-    return kernel, [((starts[2] + 2 * tall, width), BF16)]
-
-
-def make_sort(rows, width):
-    def kernel(me_ref, *refs):
-        given, outs = refs[:4], refs[4:]
-        at = 0
-        for count, out in zip(rows, outs):
-            for i, ref in enumerate(given):
-                out[i * count : (i + 1) * count, :] = ref[at : at + count, :]
-            at += count
-
-    return kernel, [((4 * count, width), BF16) for count in rows]
+            third[i * narrow : (i + 1) * narrow, :] = inner[:, i * width : (i + 1) * width]
+        third[tall:, :] = outer[...]
+
+    return kernel, [((rows, width), BF16) for rows in (3 * narrow + 8, 5 * narrow + 16, 2 * tall)]
 
 
 def join(arrays):
@@ -382,9 +371,9 @@
                 value_t[side][:, here] = found[:, columns].T
         for i, t in enumerate(tokens):
             memory[i * memory_block : (i + 1) * memory_block, :] = t[block : block + memory_block, :]
-            found = t[block + memory_block :, :].astype(F32).astype(jnp.int32)
+            found = t[block + memory_block : block + memory_block + 8, :].astype(F32).astype(jnp.int32)
             ids[:, i * block : (i + 1) * block] = found[0:1, :block]
-        found = [t[block + memory_block :, :].astype(F32).astype(jnp.int32)[1:2, :memory_block] for t in tokens]
+        found = [t[block + memory_block : block + memory_block + 8, :].astype(F32).astype(jnp.int32)[1:2, :memory_block] for t in tokens]
         memory_ids[...] = jnp.concatenate(found, axis=1)
 
     outs = [((share, half), BF16)] * 2 + [((half, share), BF16)] * 2
@@ -467,7 +456,7 @@
     return kernel, outs, scratch
 
 
-def make_inner(packed, parts, rows, block, width, hidden, narrow, n_pieces):
+def make_inner(packed, rows, block, width, hidden, narrow, n_pieces):
     blocks = hidden // width
     share = rows * block
     per = width // (blocks * narrow)
@@ -476,12 +465,11 @@
         me_ref, refs = refs[0], list(refs[1:])
         pieces, refs = refs[:n_pieces], refs[n_pieces:]
         second_sum, cot_own, cot_came, vectors = refs[:4]
-        turn = lax.rem(lax.div(me_ref[0], parts), rows)
         out_own, out_send, back, sums = refs[4:8]
         grads, scratch = refs[8:10], refs[10:]
         low, active, gate, slope = scratch[:4]
         if packed:
-            inner_w, outer_w, gathered = scratch[4:7]
+            inner_w, outer_w, gathered, dense = scratch[4:8]
             tall = blocks * narrow
             for core, far, slot, device in places(me_ref[0]):
                 ref, at = pieces[2 * core + far], slot * 2 * tall
@@ -514,7 +502,7 @@
         final = normed * vector(FINAL_GAIN) + vector(FINAL_SHIFT)
         out_own[...] = final[:block, :]
         out_send[...] = final[block:, :].astype(BF16)
-        upstream = jnp.concatenate([cot_own[turn], cot_came[turn]], axis=0).astype(F32)
+        upstream = jnp.concatenate([cot_own[-block:, :], cot_came[-block:, :]], axis=0).astype(F32)
         sums[0:1, :] = total(upstream * normed)
         sums[1:2, :] = total(upstream)
         back3 = normalize_back(upstream, normed, inverse, vector(FINAL_GAIN))
@@ -531,8 +519,12 @@
             inner_grad = dot_tn(low[...], inner_low)
             back[...] += dot_nt(inner_low, inner_w[i])
             if packed:
-                gathered[i] = inner_grad
-                gathered[blocks + i] = outer_grad
+                dense[...] = inner_grad
+                gathered[i] = outer_grad.astype(BF16)
+                here = pl.ds(pl.multiple_of(i * narrow, narrow), narrow)
+                for core, far, slot, device in places(me_ref[0]):
+                    row = pl.multiple_of(device * narrow, narrow)
+                    grads[core][far * 8 + slot, here, :] = dense[pl.ds(row, narrow), :].astype(BF16)
             else:
                 grads[0][i] = inner_grad
                 grads[1][i] = outer_grad
@@ -542,12 +534,8 @@
         if packed:
             tall = blocks * narrow
             for core, far, slot, device in places(me_ref[0]):
-                ref, at = grads[core], far * 8 + slot
-                row = pl.multiple_of(device * narrow, narrow)
-                for i in range(blocks):
-                    ref[at, i * narrow : (i + 1) * narrow, :] = gathered[i, pl.ds(row, narrow), :].astype(BF16)
                 row = pl.multiple_of(lax.rem(device, per) * tall, tall)
-                ref[at, tall:, :] = gathered[blocks + lax.div(device, per), pl.ds(row, tall), :].astype(BF16)
+                grads[core][far * 8 + slot, tall:, :] = gathered[lax.div(device, per), pl.ds(row, tall), :]
 
     outs = [((block, width), F32), ((block, width), BF16), ((share, width), F32), ((8, width), F32)]
     if packed:
@@ -556,7 +544,7 @@
         outs += [((blocks, width, width), F32)] * 2
     scratch = [((share, width), BF16), ((blocks, share, width), BF16), ((blocks, share, width), F32), ((share, width), BF16)]
     if packed:
-        scratch += [((blocks, width, width), BF16)] * 2 + [((2 * blocks, width, width), F32)]
+        scratch += [((blocks, width, width), BF16)] * 3 + [((width, width), F32)]
     return kernel, outs, scratch
 
 
@@ -870,7 +858,7 @@
         in_specs=[VM] * len(arrays),
         out_specs=[VM] * splits,
         compiler_params=pltpu.CompilerParams(vmem_limit_bytes=20 << 20),
-        cost_estimate=pl.CostEstimate(flops=1 << 20, bytes_accessed=0, transcendentals=0),
+        cost_estimate=pl.CostEstimate(flops=2 << 30, bytes_accessed=0, transcendentals=0),
         name="combine",
     )(*arrays)
 
@@ -930,8 +918,8 @@
         return lax.all_gather(array, AXES, axis=0, tiled=True)
 
     sent, kept = turned(
-        make_tokens_packet(block, memory_block, width), "tokens_packet",
-        tokens, memory, target_ids, source_ids,
+        make_tokens_packet(block, memory_block, width), "tokens_packet", tokens, memory,
+        target_ids, source_ids, cotangent,
     )
     came = swap(sent, parts, devices)
     row_tokens = [kept, came]
@@ -942,24 +930,26 @@
     own_tokens = row_tokens[:rows]
 
     if packed:
-        (block_own,) = run(make_weights_packet(narrow, width, blocks), 1.0, "weights_packet",
-                           query_weight, key_weight, value_weight, output_weight, source_query,
-                           source_key, source_value, source_output, inner_weight, outer_weight,
-                           short, inner_bias.reshape(1, wide))
-        block_own = after(block_own, sent)
-        sizes = (3 * narrow + 8, 5 * narrow + 16, 2 * blocks * narrow)
-        first_a, second_a, third_a = run(
-            make_sort(sizes, width), 1.0, "sort", block_own, *[swap(block_own, m, 32) for m in Z_MASKS[1:]]
-        )
-        first_b, second_b = turned_swap(first_a, 1), turned_swap(second_a, 1)
-        first_c = join(after([first_a, first_b], came, *kept_swaps))
-        first_d = turned_swap(first_c, 2)
-        second_c = join([second_a, second_b])
-        second_d = turned_swap(second_c, 2)
-        third_b = turned_swap(third_a, 1)
-        first_d = after(first_d, second_c, *came_swaps)
+        first, second, third = run(make_weights_packet(narrow, width, blocks), 1.0, "weights_packet",
+                                   query_weight, key_weight, value_weight, output_weight,
+                                   source_query, source_key, source_value, source_output,
+                                   inner_weight, outer_weight, short, inner_bias.reshape(1, wide))
+        first = after(first, sent)
+        first = join([first, turned_swap(first, 0)])
+        first_b = turned_swap(first, 1)
+        second = after(second, first)
+        second_b = turned_swap(second, 0)
+        first = join(after([first, first_b], second_b))
+        second = join([second, second_b])
+        third = after(third, second)
+        first_b, second_b, third_b = turned_swap(first, 2), turned_swap(second, 1), turned_swap(third, 0)
+        first_c = join(after([first, first_b], second_b, third_b, came, *kept_swaps))
+        second, third = join([second, second_b]), join([third, third_b])
+        first_d, second_b, third_b = turned_swap(first_c, 3), turned_swap(second, 2), turned_swap(third, 1)
+        second_c, third = join([second, second_b]), join([third, third_b])
+        first_d = after(first_d, second_c, third, *came_swaps)
+        second_d, third_b = turned_swap(second_c, 3), turned_swap(third, 2)
         set_self = [first_c, first_d, swap(first_c, 1, 32), swap(first_d, 1, 32)]
-        second_b = turned_swap(second_a, 1)
     else:
         full = [whole(w) for w in (query_weight, key_weight, value_weight, output_weight, source_query, source_key, source_value, source_output)]
         lane = lax.broadcasted_iota(jnp.int32, (1, width), 1)
@@ -985,15 +975,14 @@
     row_memory, ids, memory_ids = found[10:]
     query_t = list(query_t)
     if packed:
-        third_c = join(after([third_a, third_b], query_t[0]))
-        third_d = turned_swap(third_c, 2)
+        third_c = join(after([third, third_b], query_t[0]))
+        third_d = turned_swap(third_c, 3)
         second_d = after(second_d, query_t[0])
         set_cross = [second_c, second_d, swap(second_c, 1, 32), swap(second_d, 1, 32)]
         query_t[0] = after(query_t[0], third_c, second_d)
         set_back, set_query, set_last, set_memory = set_cross, set_self, set_self, set_cross
     else:
         set_back, set_query, set_last, set_memory = [full[3], full[4], full[7]], full[:1], full[1:3], full[5:7]
-    cot_came = swap(cotangent, parts, devices)
     found = run(
         make_self_attention(share, parts * share, width), 12.0, "self_attention",
         *query_t, *keys, *value_t, ids,
@@ -1002,14 +991,14 @@
     if packed:
         third_d = after(third_d, mixtures[0])
         set_inner = [third_c, third_d, swap(third_c, 1, 32), swap(third_d, 1, 32)]
-        mixtures = [after(mixtures[0], third_d, cot_came), mixtures[1]]
+        mixtures = [after(mixtures[0], third_d), mixtures[1]]
     first_sum, second_sum, cross_query, memory_keys, memory_values, cross_t, cross_logs, vectors = run(
         make_cross_forward(packed, rows, block, parts * memory_share, width, narrow, len(set_cross)),
         9.0, "cross_forward", *set_cross, *own_tokens, row_memory, ids, memory_ids, *mixtures,
     )
     out_own, out_send, back2_in, sums_inner, *grads_inner = run(
-        make_inner(packed, parts, rows, block, width, hidden, narrow, len(set_inner)), 18.0, "inner",
-        *set_inner, second_sum, cotangent, cot_came, vectors,
+        make_inner(packed, rows, block, width, hidden, narrow, len(set_inner)), 18.0, "inner",
+        *set_inner, second_sum, kept, came, vectors,
     )
     out_came = swap(out_send, parts, devices)
     found = run(
@@ -1025,7 +1014,7 @@
     if packed:
         keep, send = combine([grads_inner[0], swap(grads_inner[1], 1, 32)], 2)
         query[0] = after(query[0], keep, out_came)
-        inner_step = [keep, turned_swap(send, 2)]
+        inner_step = [keep, turned_swap(send, 3)]
     found = run(
         make_self_back_upper(packed, parts, rows, block, memory_block, width, narrow, len(set_memory)),
         12.0, "self_back_upper", *set_memory, *own_tokens, query[0], keys[0], values[0], slope[0],
@@ -1037,10 +1026,8 @@
     grads_cross = found[4 + parts - 1 :]
     if packed:
         keep, send = combine(inner_step, 2)
-        inner_step = [keep, turned_swap(send, 1)]
-        keep_cross, send = combine([grads_cross[0], swap(grads_cross[1], 1, 32)], 2)
-        cross_step = [keep_cross, turned_swap(send, 2)]
-        query[1] = after(query[1], keep, keep_cross)
+        inner_step = [keep, turned_swap(send, 2)]
+        query[1] = after(query[1], keep)
     in_part, query_sum, query_w_grad, own_lower, *sends = run(
         make_self_back_lower(packed, parts, rows, block, width, narrow, len(set_query)), 11.0,
         "self_back_lower", *set_query, *own_tokens, query[1], keys[1], values[1], slope[1],
@@ -1048,40 +1035,39 @@
     )
     received_lower = [swap(a, m + 1, devices) for m, a in enumerate(sends)]
     if packed:
-        def lowest(arrays):
-            found = combine(arrays, 4)
-            return [found[0]] + [swap(a, m, 32) for a, m in zip(found[1:], Z_MASKS[1:])]
-
-        inner_step = lowest(inner_step)
-        keep_cross, send = combine(cross_step, 2)
-        cross_step = [keep_cross, turned_swap(send, 1)]
-        in_part = after(in_part, keep_cross, inner_step[0])
+        keep, send = combine(inner_step, 2)
+        inner_step = [keep, turned_swap(send, 1)]
+        keep_cross, send = combine([grads_cross[0], swap(grads_cross[1], 1, 32)], 2)
+        cross_step = [keep_cross, turned_swap(send, 3)]
+        in_part = after(in_part, keep, keep_cross)
     in_own, in_send, *grads_last = run(
         make_last(packed, parts, rows, block, memory_block, width, narrow, len(set_last)), 6.0,
         "last", *set_last, *own_tokens, in_part, query_sum, query_w_grad, memory_send, own_upper,
         own_lower, *received_upper, *received_lower,
     )
 
-    def regroup(mine, came):
-        came = came.astype(F32)
-        return jnp.where(turn == 0, jnp.stack([mine, came]), jnp.stack([came, mine]))
-
-    output = regroup(out_own, out_came)
-    in_came = swap(in_send, parts, devices)
-    input_gradient = regroup(in_own, in_came[:block])
-    memory_gradient = regroup(memory_own, in_came[block:])
-
-    if packed:
-        grads_last[1] = after(grads_last[1], *cross_step, *inner_step)
-        keep, send = combine([grads_last[0], swap(grads_last[1], 1, 32)], 2)
+    if packed:
+        keep_inner, send = combine(inner_step, 2)
+        inner_step = [keep_inner, turned_swap(send, 0)]
+        keep_cross, send = combine(cross_step, 2)
+        cross_step = [keep_cross, turned_swap(send, 2)]
+        keep, send = combine(after([grads_last[0], swap(grads_last[1], 1, 32)], keep_inner, keep_cross), 2)
+        last_step = [keep, turned_swap(send, 3)]
+        in_send = after(in_send, last_step[1])
+        keep_cross, send = combine(cross_step, 2)
+        cross_step = [keep_cross, turned_swap(send, 1)]
+        keep, send = combine(after(last_step, keep_cross), 2)
         last_step = [keep, turned_swap(send, 2)]
-        cross_step = lowest(cross_step)
-        keep, send = combine(after(last_step, cross_step[0]), 2)
-        last_step = lowest(after([keep, turned_swap(send, 1)], *cross_step))
+        keep_cross, send = combine(cross_step, 2)
+        cross_step = [keep_cross, turned_swap(send, 0)]
+        keep, send = combine(after(last_step, keep_cross), 2)
+        last_step = [keep, turned_swap(send, 1)]
+        keep, send = combine(last_step, 2)
+        last_step = [keep, turned_swap(send, 0)]
 
         def plan(me_ref, *refs):
             me = me_ref[0]
-            steps, outs = [refs[:4], refs[4:8], refs[8:12]], refs[12:]
+            steps, outs = [refs[:2], refs[2:4], refs[4:6]], refs[6:]
             inner, cross, last = (sum(r[0].astype(F32) for r in given) for given in steps)
             for i in range(blocks):
                 outs[0][:, i * width : (i + 1) * width] = inner[i * narrow : (i + 1) * narrow, :]
@@ -1119,6 +1105,15 @@
         sums = reduce_all(jnp.concatenate([grads_cross[2], grads_last[2]], axis=0), devices)
         inner_bias_share = lax.dynamic_slice(sums[3 : 3 + blocks].reshape(hidden), (me * wide,), (wide,))
         sums = lax.dynamic_slice(sums, (0, me * narrow), (sums.shape[0], narrow))
+    def regroup(mine, came):
+        came = came.astype(F32)
+        return jnp.where(turn == 0, jnp.stack([mine, came]), jnp.stack([came, mine]))
+
+    output = regroup(out_own, out_came)
+    in_came = swap(in_send, parts, devices)
+    input_gradient = regroup(in_own, in_came[:block])
+    memory_gradient = regroup(memory_own, in_came[block:])
+
     return (
         output,
         input_gradient,

time: 218 us -> 186 us (0.85)
  waiting for transfers between devices: 100 us -> 80.5 us
  starting transfers between devices: 40.8 us -> 36 us
  local copies, waits for them, and re-layouts: 12.3 us -> 7.59 us
  Pallas kernels: 58.6 us -> 55.6 us
    ppermute x30 -> x17, waiting for transfers between devices: 39.5 us -> 0.59 us  [swap(): return lax.ppermute(array, AXES, [(i, i ^ mask) for i in range(devices)])]
    ppermute x30 -> x17, starting transfers between devices: 26.5 us -> 7.3 us  [swap(): return lax.ppermute(array, AXES, [(i, i ^ mask) for i in range(devices)])]
    ppermute x12 -> x24, waiting for transfers between devices: 60.8 us -> 79.9 us  [turned_swap(): lax.ppermute(array, AXES, [(i, i ^ ORDERS[i % 2][step]) for i in range(32)])]
    ppermute x12 -> x24, starting transfers between devices: 14.3 us -> 28.7 us  [turned_swap(): lax.ppermute(array, AXES, [(i, i ^ ORDERS[i % 2][step]) for i in range(32)])]
    unnamed x102 -> x66, local copies, waits for them, and re-layouts: 11.7 us -> 6.96 us
    pallas_call x12 -> x11, Pallas kernels: 56.5 us -> 53.3 us  [call(): pl.pallas_call(kernel, out_shape=[jax.ShapeDtypeStruct(s, d) for s, d in...]
  transfers between devices with their start and end apart: 42 -> 41, of which waited for: 18 -> 17; matrix products, arithmetic and copies ran while one was open for 2% -> 2% of each run, Pallas kernels for 16% -> 23%
where the time goes in v5:
time: 186 us; the launch traced here: 185 us
  waiting for transfers between devices  80.5 us (43%)
  Pallas kernels  55.6 us (30%)
  starting transfers between devices  36 us (19%)
  local copies, waits for them, and re-layouts  7.59 us (4%)
  other arithmetic  3.93 us (2%)
    ppermute x24, waiting for transfers between devices, turned_swap(): lax.ppermute(array, AXES, [(i, i ^ ORDERS[i % 2][step]) for i in range(32)])  79.9 us
    pallas_call x11, Pallas kernels, call(): pl.pallas_call(kernel, out_shape=[jax.ShapeDtypeStruct(s, d) for s, d in...  53.3 us
    ppermute x24, starting transfers between devices, turned_swap(): lax.ppermute(array, AXES, [(i, i ^ ORDERS[i % 2][step]) for i in range(32)])  28.7 us
    ppermute x17, starting transfers between devices, swap(): return lax.ppermute(array, AXES, [(i, i ^ mask) for i in range(devices)])  7.3 us
    unnamed x66, local copies, waits for them, and re-layouts  6.96 us
  transfers between devices with their start and end apart: 41, of which 17 were waited for; matrix products, arithmetic and copies ran while one was open for 2% of the time, Pallas kernels for 23%

profile of v5, /device:TPU:0, one launch (start us, length us, event | category | flops | bytes accessed | tf_op | source)
XLA Modules:
  0.0 185.3 jit_solution(7233452790856890508)
XLA Ops:
  5.4 3.0 %collective-permute-start.8 = (bf16[584,512]{1,0:T(8,128)(2,1)S(1)}, bf16[584,512]{1,0:T(8,128)(2,1)S(1)}, u32[]{:S(2)}, u32[]{:S(2)}) collective-permute-start(bf16[584,512]{1,0:T(8,128)(2,1)S(1)} %get-tuple-element.156), channel_id=1, source_target_pairs={{0,2},{1,3},{2,0},{3,1},{4,6},{5,7},{6,4},{7,5},{8,10},{9,11},{10,... | collective-permute-start | bytes 1794056 | tf_op jit(solution)/shard_map/ppermute | solution.py:161
  10.5 3.2 %collective-permute-done.refs_1_ = bf16[56,512]{1,0:T(8,128)(2,1)S(1)} collective-permute-done((bf16[56,512]{1,0:T(8,128)(2,1)S(1)}, bf16[56,512]{1,0:T(8,128)(2,1)S(1)}, u32[]{:S(2)}, u32[]{:S(2)}) %collective-permute-start) | collective-permute-done | bytes 57376 | tf_op jit(solution)/shard_map/ppermute | solution.py:168
  13.7 2.1 %collective-permute-start.5 = (bf16[112,512]{1,0:T(8,128)(2,1)S(1)}, bf16[112,512]{1,0:T(8,128)(2,1)S(1)}, u32[]{:S(2)}, u32[]{:S(2)}) collective-permute-start(bf16[112,512]{1,0:T(8,128)(2,1)S(1)} %join.9.refs_0_), channel_id=1, source_target_pairs={{0,16},{1,9},{2,18},{3,11},{4,20},{5,13},{6,22},{7,15},{8,24},{9,1... | collective-permute-start | bytes 344072 | tf_op jit(solution)/shard_map/ppermute | solution.py:168
  17.5 3.5 %collective-permute-done.1.refs_1_ = bf16[96,512]{1,0:T(8,128)(2,1)S(1)} collective-permute-done((bf16[96,512]{1,0:T(8,128)(2,1)S(1)}, bf16[96,512]{1,0:T(8,128)(2,1)S(1)}, u32[]{:S(2)}, u32[]{:S(2)}) %collective-permute-start.1) | collective-permute-done | bytes 98336 | tf_op jit(solution)/shard_map/ppermute | solution.py:168
  24.2 2.7 %collective-permute-start.2 = (bf16[128,512]{1,0:T(8,128)(2,1)S(1)}, bf16[128,512]{1,0:T(8,128)(2,1)S(1)}, u32[]{:S(2)}, u32[]{:S(2)}) collective-permute-start(bf16[128,512]{1,0:T(8,128)(2,1)S(1)} %get-tuple-element.159.refs_0_), channel_id=1, source_target_pairs={{0,8},{1,17},{2,10},{3,19},{4,12},{5,21},{6,14},{7,23},{8,0},{9,25... | collective-permute-start | bytes 393224 | tf_op jit(solution)/shard_map/ppermute | solution.py:168
  26.9 5.9 %collective-permute-done.2.refs_1_ = bf16[128,512]{1,0:T(8,128)(2,1)S(1)} collective-permute-done((bf16[128,512]{1,0:T(8,128)(2,1)S(1)}, bf16[128,512]{1,0:T(8,128)(2,1)S(1)}, u32[]{:S(2)}, u32[]{:S(2)}) %collective-permute-start.2) | collective-permute-done | bytes 131104 | tf_op jit(solution)/shard_map/ppermute | solution.py:168
  32.8 1.7 collective-permute-done.7.refs_1_
  34.6 1.8 collective-permute-start.10
  38.1 9.5 %collective-permute-done.3.refs_1_ = bf16[256,512]{1,0:T(8,128)(2,1)S(1)} collective-permute-done((bf16[256,512]{1,0:T(8,128)(2,1)S(1)}, bf16[256,512]{1,0:T(8,128)(2,1)S(1)}, u32[]{:S(2)}, u32[]{:S(2)}) %collective-permute-start.3) | collective-permute-done | bytes 262176 | tf_op jit(solution)/shard_map/ppermute | solution.py:168
  51.9 12.0 %collective-permute-done.4.refs_1_ = bf16[512,512]{1,0:T(8,128)(2,1)S(1)} collective-permute-done((bf16[512,512]{1,0:T(8,128)(2,1)S(1)}, bf16[512,512]{1,0:T(8,128)(2,1)S(1)}, u32[]{:S(2)}, u32[]{:S(2)}) %collective-permute-start.4) | collective-permute-done | bytes 524320 | tf_op jit(solution)/shard_map/ppermute | solution.py:168
  65.9 8.3 %self_attention.1 = (bf16[256,512]{1,0:T(8,128)(2,1)S(1)}, bf16[256,512]{1,0:T(8,128)(2,1)S(1)}, f32[4,1,512]{2,1,0:T(1,128)S(1)}, f32[4,1,512]{2,1,0:T(1,128)S(1)}) custom-call(s32[1]{0:T(128)} %bitcast.me_ref.refs_0_, bf16[256,512]{1,0:T(8,128)(2,1)S(1)} %get-tuple-element.170.refs_0_, bf16[256,512]{1,0:T(8,128)(2,1)S(1)} %get-tuple-element.171.refs_1_, ...), custom_call_target="tpu_custom_call" | custom-call | flops 13799999488 | bytes 3166208 | tf_op jit(solution)/shard_map/self_attention/pallas_call | solution.py:247
  74.2 4.7 %collective-permute-done.15.refs_2_ = bf16[1024,512]{1,0:T(8,128)(2,1)S(1)} collective-permute-done((bf16[1024,512]{1,0:T(8,128)(2,1)S(1)}, bf16[1024,512]{1,0:T(8,128)(2,1)S(1)}, u32[]{:S(2)}, u32[]{:S(2)}) %collective-permute-start.15) | collective-permute-done | bytes 1048608 | tf_op jit(solution)/shard_map/ppermute | solution.py:168
  78.9 5.4 %cross_forward.1 = (f32[512,512]{1,0:T(8,128)S(1)}, f32[512,512]{1,0:T(8,128)S(1)}, bf16[512,512]{1,0:T(8,128)(2,1)S(1)}, bf16[256,512]{1,0:T(8,128)(2,1)S(1)}, ...) custom-call(s32[1]{0:T(128)} %bitcast.me_ref.refs_0_, ...), custom_call_target="tpu_custom_call" | custom-call | flops 10350000128 | bytes 8852480 | tf_op jit(solution)/shard_map/cross_forward/pallas_call | solution.py:247
  84.3 12.4 %inner.1 = (f32[256,512]{1,0:T(8,128)S(1)}, bf16[256,512]{1,0:T(8,128)(2,1)S(1)}, f32[512,512]{1,0:T(8,128)S(1)}, f32[8,512]{1,0:T(8,128)S(1)}, bf16[16,128,512]...) custom-call(s32[1]{0:T(128)} %bitcast.me_ref.refs_0_, bf16[1024,512]{1,0:T(8,128)(2,1)S(1)} %join.17.refs_1_, ...), custom_call_target="tpu_custom_call" | custom-call | flops 20700000256 | bytes 12517376 | tf_op jit(solution)/shard_map/inner/pallas_call | solution.py:247
  97.8 8.4 %cross_back.1 = (f32[512,512]{1,0:T(8,128)S(1)}, f32[128,512]{1,0:T(8,128)S(1)}, f32[128,512]{1,0:T(8,128)S(1)}, f32[16,512]{1,0:T(8,128)S(1)}, bf16[512,256]{1,...) custom-call(s32[1]{0:T(128)} %bitcast.me_ref.refs_0_, ...), custom_call_target="tpu_custom_call" | custom-call | flops 16099999744 | bytes 12964864 | tf_op jit(solution)/shard_map/cross_back/pallas_call | solution.py:247
  108.3 7.2 %self_back_upper.1 = (bf16[512,256]{1,0:T(8,128)(2,1)S(1)}, f32[1024,256]{1,0:T(8,128)S(1)}, f32[64,512]{1,0:T(8,128)S(1)}, bf16[64,512]{1,0:T(8,128)(2,1)S(1)},...) custom-call(s32[1]{0:T(128)} %bitcast.me_ref.refs_0_, ...), custom_call_target="tpu_custom_call" | custom-call | flops 13799999488 | bytes 13766656 | tf_op jit(solution)/shard_map/self_back_upper/pallas_call | solution.py:247
  116.1 5.6 %collective-permute-done.23.refs_1_ = bf16[8,128,512]{2,1,0:T(8,128)(2,1)S(1)} collective-permute-done((bf16[8,128,512]{2,1,0:T(8,128)(2,1)S(1)}, bf16[8,128,512]{2,1,0:T(8,128)(2,1)S(1)}, u32[]{:S(2)}, u32[]{:S(2)}) %collective-permute-start.23) | collective-permute-done | bytes 1048608 | tf_op jit(solution)/shard_map/ppermute | solution.py:168
  123.5 7.1 %self_back_lower.1 = (f32[512,512]{1,0:T(8,128)S(1)}, f32[8,512]{1,0:T(8,128)S(1)}, bf16[512,512]{1,0:T(8,128)(2,1)S(1)}, f32[1024,256]{1,0:T(8,128)S(1)}, bf16[1024,256]{1,0:T(8,128)(2,1)S(1)}) custom-call(s32[1]{0:T(128)} %bitcast.me_ref.refs_0_, bf16[448,512]{1,0:T(8,128)(2,1)S(1)} %join.14.refs_1_, bf16[448,512]{1,0:T(8,128)(2,1)S(1)} %collective-permute-done.10.refs_2_, ...), custom_call_target="tpu_custom_call" | custom-call | flops 12650000384 | bytes 9359360 | tf_op jit(solution)/shard_map/self_back_lower/pallas_call | solution.py:247
  135.0 9.6 %collective-permute-done.30.refs_1_ = bf16[2,128,512]{2,1,0:T(8,128)(2,1)S(1)} collective-permute-done((bf16[2,128,512]{2,1,0:T(8,128)(2,1)S(1)}, bf16[2,128,512]{2,1,0:T(8,128)(2,1)S(1)}, u32[]{:S(2)}, u32[]{:S(2)}) %collective-permute-start.30) | collective-permute-done | bytes 262176 | tf_op jit(solution)/shard_map/ppermute | solution.py:168
  149.7 7.9 %collective-permute-done.35.refs_1_ = bf16[4,96,512]{2,1,0:T(8,128)(2,1)S(1)} collective-permute-done((bf16[4,96,512]{2,1,0:T(8,128)(2,1)S(1)}, bf16[4,96,512]{2,1,0:T(8,128)(2,1)S(1)}, u32[]{:S(2)}, u32[]{:S(2)}) %collective-permute-start.35) | collective-permute-done | bytes 393248 | tf_op jit(solution)/shard_map/ppermute | solution.py:168
  164.5 6.9 %collective-permute-done.36.refs_1_ = bf16[2,96,512]{2,1,0:T(8,128)(2,1)S(1)} collective-permute-done((bf16[2,96,512]{2,1,0:T(8,128)(2,1)S(1)}, bf16[2,96,512]{2,1,0:T(8,128)(2,1)S(1)}, u32[]{:S(2)}, u32[]{:S(2)}) %collective-permute-start.36) | collective-permute-done | bytes 196640 | tf_op jit(solution)/shard_map/ppermute | solution.py:168
  171.6 2.6 %collective-permute-start.39 = (bf16[2,56,512]{2,1,0:T(8,128)(2,1)S(1)}, bf16[2,56,512]{2,1,0:T(8,128)(2,1)S(1)}, u32[]{:S(2)}, u32[]{:S(2)}) collective-permute-start(bf16[2,56,512]{2,1,0:T(8,128)(2,1)S(1)} %get-tuple-element.264), channel_id=1, source_target_pairs={{0,16},{1,9},{2,18},{3,11},{4,20},{5,13},{6,22},{7,15},{8,24},{9,1... | collective-permute-start | bytes 344072 | tf_op jit(solution)/shard_map/ppermute | solution.py:168
  175.3 3.8 %collective-permute-done.39.refs_1_ = bf16[2,56,512]{2,1,0:T(8,128)(2,1)S(1)} collective-permute-done((bf16[2,56,512]{2,1,0:T(8,128)(2,1)S(1)}, bf16[2,56,512]{2,1,0:T(8,128)(2,1)S(1)}, u32[]{:S(2)}, u32[]{:S(2)}) %collective-permute-start.39) | collective-permute-done | bytes 114720 | tf_op jit(solution)/shard_map/ppermute | solution.py:168
  180.3 3.2 %collective-permute-done.40.refs_5_ = bf16[1,56,512]{2,1,0:T(8,128)(2,1)S(1)} collective-permute-done((bf16[1,56,512]{2,1,0:T(8,128)(2,1)S(1)}, bf16[1,56,512]{2,1,0:T(8,128)(2,1)S(1)}, u32[]{:S(2)}, u32[]{:S(2)}) %collective-permute-start.40) | collective-permute-done | bytes 57376 | tf_op jit(solution)/shard_map/ppermute | solution.py:168
  (164 shorter events, 45.2 us)
Async XLA Ops:
  5.4 18.8 %collective-permute-start.8 = (bf16[584,512]{1,0:T(8,128)(2,1)S(1)}, bf16[584,512]{1,0:T(8,128)(2,1)S(1)}, u32[]{:S(2)}, u32[]{:S(2)}) collective-permute-start(bf16[584,512]{1,0:T(8,128)(2,1)S(1)} %get-tuple-element.156), channel_id=1, source_target_pairs={{0,2},{1,3},{2,0},{3,1},{4,6},{5,7},{6,4},{7,5},{8,10},{9,11},{10,... | collective-permute-start | bytes 1794056 | tf_op jit(solution)/shard_map/ppermute | solution.py:161
  8.4 26.2 %collective-permute-start.9 = (bf16[584,512]{1,0:T(8,128)(2,1)S(1)}, bf16[584,512]{1,0:T(8,128)(2,1)S(1)}, u32[]{:S(2)}, u32[]{:S(2)}) collective-permute-start(bf16[584,512]{1,0:T(8,128)(2,1)S(1)} %get-tuple-element.162.refs_5_.refs_6_), channel_id=1, source_target_pairs={{0,1},{1,0},{2,3},{3,2},{4,5},{5,4},{6,7},{7,6},{8,9},{9,8},{10,11... | collective-permute-start | bytes 1794056 | tf_op jit(solution)/shard_map/ppermute | solution.py:161
  22.6 11.9 %collective-permute-start.6 = (bf16[224,512]{1,0:T(8,128)(2,1)S(1)}, bf16[224,512]{1,0:T(8,128)(2,1)S(1)}, u32[]{:S(2)}, u32[]{:S(2)}) collective-permute-start(bf16[224,512]{1,0:T(8,128)(2,1)S(1)} %join.13.refs_0_), channel_id=1, source_target_pairs={{0,2},{1,5},{2,0},{3,7},{4,6},{5,1},{6,4},{7,3},{8,10},{9,13},{10,... | collective-permute-start | bytes 688136 | tf_op jit(solution)/shard_map/ppermute | solution.py:168
  23.0 11.6 %collective-permute-start.7 = (bf16[192,512]{1,0:T(8,128)(2,1)S(1)}, bf16[192,512]{1,0:T(8,128)(2,1)S(1)}, u32[]{:S(2)}, u32[]{:S(2)}) collective-permute-start(bf16[192,512]{1,0:T(8,128)(2,1)S(1)} %join.10.refs_0_), channel_id=1, source_target_pairs={{0,16},{1,9},{2,18},{3,11},{4,20},{5,13},{6,22},{7,15},{8,24},{9,1... | collective-permute-start | bytes 589832 | tf_op jit(solution)/shard_map/ppermute | solution.py:168
  24.2 23.6 %collective-permute-start.12 = (bf16[584,512]{1,0:T(8,128)(2,1)S(1)}, bf16[584,512]{1,0:T(8,128)(2,1)S(1)}, u32[]{:S(2)}, u32[]{:S(2)}) collective-permute-start(bf16[584,512]{1,0:T(8,128)(2,1)S(1)} %collective-permute-done.8.refs_6_.refs_7_), channel_id=1, source_target_pairs={{0,1},{1,0},{2,3},{3,2},{4,5},{5,4},{6,7},{7,6},{8,9},{9,8},{10,11... | collective-permute-start | bytes 1794056 | tf_op jit(solution)/shard_map/ppermute | solution.py:161
  34.6 13.2 %collective-permute-start.10 = (bf16[448,512]{1,0:T(8,128)(2,1)S(1)}, bf16[448,512]{1,0:T(8,128)(2,1)S(1)}, u32[]{:S(2)}, u32[]{:S(2)}) collective-permute-start(bf16[448,512]{1,0:T(8,128)(2,1)S(1)} %join.14.refs_1_), channel_id=1, source_target_pairs={{0,4},{1,3},{2,6},{3,1},{4,0},{5,7},{6,2},{7,5},{8,12},{9,11},{10,... | collective-permute-start | bytes 1376264 | tf_op jit(solution)/shard_map/ppermute | solution.py:168
  36.4 11.3 %collective-permute-start.11 = (bf16[384,512]{1,0:T(8,128)(2,1)S(1)}, bf16[384,512]{1,0:T(8,128)(2,1)S(1)}, u32[]{:S(2)}, u32[]{:S(2)}) collective-permute-start(bf16[384,512]{1,0:T(8,128)(2,1)S(1)} %join.15.refs_0_), channel_id=1, source_target_pairs={{0,2},{1,5},{2,0},{3,7},{4,6},{5,1},{6,4},{7,3},{8,10},{9,13},{10,... | collective-permute-start | bytes 1179656 | tf_op jit(solution)/shard_map/ppermute | solution.py:168
  48.4 17.1 %collective-permute-start.16 = (bf16[768,512]{1,0:T(8,128)(2,1)S(1)}, bf16[768,512]{1,0:T(8,128)(2,1)S(1)}, u32[]{:S(2)}, u32[]{:S(2)}) collective-permute-start(bf16[768,512]{1,0:T(8,128)(2,1)S(1)} %join.16.refs_1_), channel_id=1, source_target_pairs={{0,4},{1,3},{2,6},{3,1},{4,0},{5,7},{6,2},{7,5},{8,12},{9,11},{10,... | collective-permute-start | bytes 2359304 | tf_op jit(solution)/shard_map/ppermute | solution.py:168
  49.1 14.9 %collective-permute-start.4 = (bf16[512,512]{1,0:T(8,128)(2,1)S(1)}, bf16[512,512]{1,0:T(8,128)(2,1)S(1)}, u32[]{:S(2)}, u32[]{:S(2)}) collective-permute-start(bf16[512,512]{1,0:T(8,128)(2,1)S(1)} %join.12.refs_0_), channel_id=1, source_target_pairs={{0,2},{1,5},{2,0},{3,7},{4,6},{5,1},{6,4},{7,3},{8,10},{9,13},{10,... | collective-permute-start | bytes 1572872 | tf_op jit(solution)/shard_map/ppermute | solution.py:168
  49.7 29.2 %collective-permute-start.19 = (bf16[768,512]{1,0:T(8,128)(2,1)S(1)}, bf16[768,512]{1,0:T(8,128)(2,1)S(1)}, u32[]{:S(2)}, u32[]{:S(2)}) collective-permute-start(bf16[768,512]{1,0:T(8,128)(2,1)S(1)} %join.16.refs_1_), channel_id=1, source_target_pairs={{0,1},{1,0},{2,3},{3,2},{4,5},{5,4},{6,7},{7,6},{8,9},{9,8},{10,11... | collective-permute-start | bytes 2359304 | tf_op jit(solution)/shard_map/ppermute | solution.py:161
  64.0 14.9 %collective-permute-start.15 = (bf16[1024,512]{1,0:T(8,128)(2,1)S(1)}, bf16[1024,512]{1,0:T(8,128)(2,1)S(1)}, u32[]{:S(2)}, u32[]{:S(2)}) collective-permute-start(bf16[1024,512]{1,0:T(8,128)(2,1)S(1)} %join.17.refs_1_), channel_id=1, source_target_pairs={{0,4},{1,3},{2,6},{3,1},{4,0},{5,7},{6,2},{7,5},{8,12},{9,11},{10,... | collective-permute-start | bytes 3145736 | tf_op jit(solution)/shard_map/ppermute | solution.py:168
  65.4 18.9 %collective-permute-start.17 = (bf16[1024,512]{1,0:T(8,128)(2,1)S(1)}, bf16[1024,512]{1,0:T(8,128)(2,1)S(1)}, u32[]{:S(2)}, u32[]{:S(2)}) collective-permute-start(bf16[1024,512]{1,0:T(8,128)(2,1)S(1)} %join.17.refs_1_), channel_id=1, source_target_pairs={{0,1},{1,0},{2,3},{3,2},{4,5},{5,4},{6,7},{7,6},{8,9},{9,8},{10,11... | collective-permute-start | bytes 3145736 | tf_op jit(solution)/shard_map/ppermute | solution.py:161
  65.5 13.4 %collective-permute-start.20 = (bf16[768,512]{1,0:T(8,128)(2,1)S(1)}, bf16[768,512]{1,0:T(8,128)(2,1)S(1)}, u32[]{:S(2)}, u32[]{:S(2)}) collective-permute-start(bf16[768,512]{1,0:T(8,128)(2,1)S(1)} %collective-permute-done.16.refs_2_), channel_id=1, source_target_pairs={{0,1},{1,0},{2,3},{3,2},{4,5},{5,4},{6,7},{7,6},{8,9},{9,8},{10,11... | collective-permute-start | bytes 2359304 | tf_op jit(solution)/shard_map/ppermute | solution.py:161
  97.3 11.1 %collective-permute-start.21 = (bf16[256,512]{1,0:T(8,128)(2,1)S(1)}, bf16[256,512]{1,0:T(8,128)(2,1)}, u32[]{:S(2)}, u32[]{:S(2)}) collective-permute-start(bf16[256,512]{1,0:T(8,128)(2,1)S(1)} %get-tuple-element.186), channel_id=1, source_target_pairs={{0,2},{1,3},{2,0},{3,1},{4,6},{5,7},{6,4},{7,5},{8,10},{9,11},{10,... | collective-permute-start | bytes 786440 | tf_op jit(solution)/shard_map/ppermute | solution.py:161
  106.8 14.9 %collective-permute-start.23 = (bf16[8,128,512]{2,1,0:T(8,128)(2,1)S(1)}, bf16[8,128,512]{2,1,0:T(8,128)(2,1)S(1)}, u32[]{:S(2)}, u32[]{:S(2)}) collective-permute-start(bf16[8,128,512]{2,1,0:T(8,128)(2,1)S(1)} %get-tuple-element.191), channel_id=1, source_target_pairs={{0,4},{1,3},{2,6},{3,1},{4,0},{5,7},{6,2},{7,5},{8,12},{9,11},{10,... | collective-permute-start | bytes 3145736 | tf_op jit(solution)/shard_map/ppermute | solution.py:168
  115.5 15.8 %collective-permute-start.26 = (bf16[16,96,512]{2,1,0:T(8,128)(2,1)S(1)}, bf16[16,96,512]{2,1,0:T(8,128)(2,1)S(1)}, u32[]{:S(2)}, u32[]{:S(2)}) collective-permute-start(bf16[16,96,512]{2,1,0:T(8,128)(2,1)S(1)} %get-tuple-element.227), channel_id=1, source_target_pairs={{0,1},{1,0},{2,3},{3,2},{4,5},{5,4},{6,7},{7,6},{8,9},{9,8},{10,11... | collective-permute-start | bytes 4718600 | tf_op jit(solution)/shard_map/ppermute | solution.py:161
  115.8 17.4 %collective-permute-start.27 = (bf16[1024,256]{1,0:T(8,128)(2,1)S(1)}, bf16[1024,256]{1,0:T(8,128)(2,1)S(1)}, u32[]{:S(2)}, u32[]{:S(2)}) collective-permute-start(bf16[1024,256]{1,0:T(8,128)(2,1)S(1)} %get-tuple-element.235), channel_id=1, source_target_pairs={{0,1},{1,0},{2,3},{3,2},{4,5},{5,4},{6,7},{7,6},{8,9},{9,8},{10,11... | collective-permute-start | bytes 1572872 | tf_op jit(solution)/shard_map/ppermute | solution.py:161
  131.7 12.9 %collective-permute-start.31 = (bf16[8,96,512]{2,1,0:T(8,128)(2,1)S(1)}, bf16[8,96,512]{2,1,0:T(8,128)(2,1)S(1)}, u32[]{:S(2)}, u32[]{:S(2)}) collective-permute-start(bf16[8,96,512]{2,1,0:T(8,128)(2,1)S(1)} %get-tuple-element.243), channel_id=1, source_target_pairs={{0,4},{1,3},{2,6},{3,1},{4,0},{5,7},{6,2},{7,5},{8,12},{9,11},{10,... | collective-permute-start | bytes 2359304 | tf_op jit(solution)/shard_map/ppermute | solution.py:168
  134.9 12.1 %collective-permute-start.29 = (bf16[16,56,512]{2,1,0:T(8,128)(2,1)S(1)}, bf16[16,56,512]{2,1,0:T(8,128)(2,1)S(1)}, u32[]{:S(2)}, u32[]{:S(2)}) collective-permute-start(bf16[16,56,512]{2,1,0:T(8,128)(2,1)S(1)} %get-tuple-element.240), channel_id=1, source_target_pairs={{0,1},{1,0},{2,3},{3,2},{4,5},{5,4},{6,7},{7,6},{8,9},{9,8},{10,11... | collective-permute-start | bytes 2752520 | tf_op jit(solution)/shard_map/ppermute | solution.py:161
  145.6 11.9 %collective-permute-start.35 = (bf16[4,96,512]{2,1,0:T(8,128)(2,1)S(1)}, bf16[4,96,512]{2,1,0:T(8,128)(2,1)S(1)}, u32[]{:S(2)}, u32[]{:S(2)}) collective-permute-start(bf16[4,96,512]{2,1,0:T(8,128)(2,1)S(1)} %get-tuple-element.251), channel_id=1, source_target_pairs={{0,2},{1,5},{2,0},{3,7},{4,6},{5,1},{6,4},{7,3},{8,10},{9,13},{10,... | collective-permute-start | bytes 1179656 | tf_op jit(solution)/shard_map/ppermute | solution.py:168
  147.9 11.2 %collective-permute-start.32 = (bf16[8,56,512]{2,1,0:T(8,128)(2,1)S(1)}, bf16[8,56,512]{2,1,0:T(8,128)(2,1)S(1)}, u32[]{:S(2)}, u32[]{:S(2)}) collective-permute-start(bf16[8,56,512]{2,1,0:T(8,128)(2,1)S(1)} %get-tuple-element.247), channel_id=1, source_target_pairs={{0,4},{1,3},{2,6},{3,1},{4,0},{5,7},{6,2},{7,5},{8,12},{9,11},{10,... | collective-permute-start | bytes 1376264 | tf_op jit(solution)/shard_map/ppermute | solution.py:168
  158.7 12.7 %collective-permute-start.36 = (bf16[2,96,512]{2,1,0:T(8,128)(2,1)S(1)}, bf16[2,96,512]{2,1,0:T(8,128)(2,1)S(1)}, u32[]{:S(2)}, u32[]{:S(2)}) collective-permute-start(bf16[2,96,512]{2,1,0:T(8,128)(2,1)S(1)} %get-tuple-element.253), channel_id=1, source_target_pairs={{0,16},{1,9},{2,18},{3,11},{4,20},{5,13},{6,22},{7,15},{8,24},{9,1... | collective-permute-start | bytes 589832 | tf_op jit(solution)/shard_map/ppermute | solution.py:168
  159.2 12.3 %collective-permute-start.38 = (bf16[4,56,512]{2,1,0:T(8,128)(2,1)S(1)}, bf16[4,56,512]{2,1,0:T(8,128)(2,1)S(1)}, u32[]{:S(2)}, u32[]{:S(2)}) collective-permute-start(bf16[4,56,512]{2,1,0:T(8,128)(2,1)S(1)} %get-tuple-element.260), channel_id=1, source_target_pairs={{0,2},{1,5},{2,0},{3,7},{4,6},{5,1},{6,4},{7,3},{8,10},{9,13},{10,... | collective-permute-start | bytes 688136 | tf_op jit(solution)/shard_map/ppermute | solution.py:168
  161.7 18.6 %collective-permute-start.34 = (bf16[1,128,512]{2,1,0:T(8,128)(2,1)S(1)}, bf16[1,128,512]{2,1,0:T(8,128)(2,1)S(1)}, u32[]{:S(2)}, u32[]{:S(2)}) collective-permute-start(bf16[1,128,512]{2,1,0:T(8,128)(2,1)S(1)} %get-tuple-element.250), channel_id=1, source_target_pairs={{0,8},{1,17},{2,10},{3,19},{4,12},{5,21},{6,14},{7,23},{8,0},{9,25... | collective-permute-start | bytes 393224 | tf_op jit(solution)/shard_map/ppermute | solution.py:168
  (50 other events, 209.8 us)

commit v6 on v5

--- a/solution.py
+++ b/solution.py
@@ -239,6 +239,10 @@
     return math.prod(shape[:-2]) * tall * last * jnp.dtype(dtype).itemsize
 
 
+def snug(arrays):
+    return 2 * sum(padded(a.shape, a.dtype) for a in arrays) + (3 << 20)
+
+
 def call(kernel, outs, args, scratch, micros, name, room=10):
     moved = sum(math.prod(a.shape) * a.dtype.itemsize for a in args[1:])
     moved += sum(math.prod(s) * jnp.dtype(d).itemsize for s, d in outs)
@@ -258,24 +262,42 @@
     )(*args)
 
 
-def make_tokens_packet(block, memory_block, width):
+def tokens_packet(turn, tokens, memory, target_ids, source_ids, cotangent):
+    block, width = tokens.shape[1:]
+    memory_block = memory.shape[1]
     first = block + memory_block + 8
 
-    def kernel(turn, tokens, memory, target_ids, source_ids, cotangent, sent, kept):
-        mine = turn[0]
+    def kernel(turn_ref, targets, sources, tokens_ref, memory_ref, cot_ref, sent, kept, semaphores):
+        mine = turn_ref[0]
+        copies = []
+        for i, (row, out) in enumerate(((1 - mine, sent), (mine, kept))):
+            pieces = ((tokens_ref, 0, block), (memory_ref, block, memory_block), (cot_ref, first, block))
+            for j, (ref, at, count) in enumerate(pieces):
+                copies.append(pltpu.make_async_copy(ref.at[row], out.at[pl.ds(at, count), :], semaphores.at[i, j]))
+        for copy in copies:
+            copy.start()
         for row, out in ((1 - mine, sent), (mine, kept)):
-            out[:block, :] = tokens[row]
-            out[block : block + memory_block, :] = memory[row]
-            ids = target_ids[pl.ds(row, 1), :].astype(F32)
+            ids = targets[pl.ds(row, 1), :].astype(F32)
             ids = jnp.concatenate([ids, jnp.zeros((1, width - block), F32)], axis=1)
-            others = source_ids[pl.ds(row, 1), :].astype(F32)
+            others = sources[pl.ds(row, 1), :].astype(F32)
             others = jnp.concatenate([others, jnp.zeros((1, width - memory_block), F32)], axis=1)
             place = lax.broadcasted_iota(jnp.int32, (8, width), 0)
             found = jnp.where(place == 0, ids, jnp.where(place == 1, others, 0.0))
             out[block + memory_block : first, :] = found.astype(BF16)
-            out[first:, :] = cotangent[row]
-
-    return kernel, [((first + block, width), BF16)] * 2
+        for copy in copies:
+            copy.wait()
+
+    anywhere = pl.BlockSpec(memory_space=pl.ANY)
+    return pl.pallas_call(
+        kernel,
+        out_shape=[jax.ShapeDtypeStruct((first + block, width), BF16)] * 2,
+        in_specs=[SM, VM, VM, anywhere, anywhere, anywhere],
+        out_specs=[VM, VM],
+        scratch_shapes=[pltpu.SemaphoreType.DMA((2, 3))],
+        compiler_params=pltpu.CompilerParams(vmem_limit_bytes=4 << 20),
+        cost_estimate=pl.CostEstimate(flops=1 << 30, bytes_accessed=0, transcendentals=0),
+        name="tokens_packet",
+    )(turn, target_ids, source_ids, tokens, memory, cotangent)
 
 
 def placed(me, parts, width):
@@ -289,26 +311,39 @@
 
     def kernel(me_ref, *refs):
         weights, inner, outer, short, wide = refs[:8], refs[8], refs[9], refs[10], refs[11]
-        first, second, third = refs[12:]
-        me = me_ref[0]
+        first, rest = refs[12:]
+        me, middle = me_ref[0], 5 * narrow + 16
         for i, ref in enumerate(weights):
             if i < 3:
                 first[i * narrow : (i + 1) * narrow, :] = ref[...]
             else:
-                second[(i - 3) * narrow : (i - 2) * narrow, :] = ref[...]
+                rest[(i - 3) * narrow : (i - 2) * narrow, :] = ref[...]
         found = placed(me, short[...], width)
         first[3 * narrow :, :] = jnp.concatenate([found[:2, :], jnp.zeros((6, width), F32)], axis=0).astype(BF16)
         per = width // wide.shape[1]
         row = placed(lax.rem(me, per), wide[...], width)
         place = lax.broadcasted_iota(jnp.int32, (blocks, width), 0)
         spread_row = jnp.where(place == lax.div(me, per), row, 0.0)
-        rest = jnp.zeros((16 - (found.shape[0] - 2) - blocks, width), F32)
-        second[5 * narrow :, :] = jnp.concatenate([found[2:, :], spread_row, rest], axis=0).astype(BF16)
+        none = jnp.zeros((16 - (found.shape[0] - 2) - blocks, width), F32)
+        rest[5 * narrow : middle, :] = jnp.concatenate([found[2:, :], spread_row, none], axis=0).astype(BF16)
         for i in range(blocks):
-            third[i * narrow : (i + 1) * narrow, :] = inner[:, i * width : (i + 1) * width]
-        third[tall:, :] = outer[...]
-
-    return kernel, [((rows, width), BF16) for rows in (3 * narrow + 8, 5 * narrow + 16, 2 * tall)]
+            rest[middle + i * narrow : middle + (i + 1) * narrow, :] = inner[:, i * width : (i + 1) * width]
+        rest[middle + tall :, :] = outer[...]
+
+    return kernel, [((rows, width), BF16) for rows in (3 * narrow + 8, 5 * narrow + 16 + 2 * tall)]
+
+
+def make_part(sizes, width):
+    tall = sum(sizes)
+
+    def kernel(me_ref, upper, lower, *outs):
+        for i in range(4):
+            ref, at = (upper, lower)[i // 2], i % 2 * tall
+            for size, out in zip(sizes, outs):
+                out[i * size : (i + 1) * size, :] = ref[at : at + size, :]
+                at += size
+
+    return kernel, [((4 * size, width), BF16) for size in sizes]
 
 
 def join(arrays):
@@ -324,7 +359,7 @@
         out_shape=jax.ShapeDtypeStruct((rows, arrays[0].shape[1]), arrays[0].dtype),
         in_specs=[VM] * len(arrays),
         out_specs=VM,
-        compiler_params=pltpu.CompilerParams(vmem_limit_bytes=16 << 20),
+        compiler_params=pltpu.CompilerParams(vmem_limit_bytes=snug(arrays)),
         cost_estimate=pl.CostEstimate(flops=1 << 20, bytes_accessed=0, transcendentals=0),
         name="join",
     )(*arrays)
@@ -683,31 +718,28 @@
         send[share:, :] = value_grad[here, :].astype(BF16)
 
 
-def make_self_back_upper(packed, parts, rows, block, memory_block, width, narrow, n_pieces):
-    share, memory_share = rows * block, rows * memory_block
-    length, half = parts * share, width // 2
+def make_memory_back(packed, parts, rows, block, memory_block, width, narrow, n_pieces):
+    memory_share = rows * memory_block
 
     def kernel(*refs):
         me_ref, refs = refs[0], list(refs[1:])
         pieces, refs = refs[:n_pieces], refs[n_pieces:]
         tokens, refs = refs[:rows], refs[rows:]
-        operands, refs = refs[:8], refs[8:]
         memory_key_own, memory_value_own, sums_in = refs[:3]
         early, refs = refs[3:6], refs[6:]
         memory_received, refs = refs[: parts - 1], refs[parts - 1 :]
-        query_grad, own, memory_own, memory_send = refs[:4]
-        sends, refs = refs[4 : 4 + parts - 1], refs[4 + parts - 1 :]
+        memory_own, memory_send = refs[:2]
         n_grads = 2 if packed else 3
-        grad_refs, scratch = refs[:n_grads], refs[n_grads:]
-        sums = scratch[7]
+        grad_refs, scratch = refs[2 : 2 + n_grads], refs[2 + n_grads :]
+        sums = scratch[0]
         me = me_ref[0]
         if packed:
             for i in range(2):
-                unpack(me, pieces, 5 * narrow + 16, (2 + i) * narrow, narrow, scratch[8 + i])
-            source_key, source_value = scratch[8:10]
+                unpack(me, pieces, 5 * narrow + 16, (2 + i) * narrow, narrow, scratch[1 + i])
+            source_key, source_value = scratch[1:3]
         else:
             source_key, source_value = pieces
-        grads = Grads(me, grad_refs, scratch[10] if packed else None, narrow)
+        grads = Grads(me, grad_refs, scratch[3] if packed else None, narrow)
         memory = jnp.concatenate([t[block : block + memory_block, :] for t in tokens], axis=0)
         key_sum, value_sum = memory_key_own[...], memory_value_own[...]
         for ref in memory_received:
@@ -725,25 +757,30 @@
         grad = dot_nt(key_low, source_key[...]) + dot_nt(value_low, source_value[...])
         memory_own[...] = grad[:memory_block, :]
         memory_send[...] = grad[memory_block:, :].astype(BF16)
-        attention_back_half(operands, share, scratch[:7])
-        query_grad[...] = scratch[4][...].T.astype(BF16)
-        give_half(share, scratch, own, sends)
-
-    outs = [
-        ((share, half), BF16),
-        ((2 * share, half), F32),
-        ((memory_block, width), F32),
-        ((memory_block, width), BF16),
-    ]
-    outs += [((2 * share, half), BF16)] * (parts - 1)
+
+    outs = [((memory_block, width), F32), ((memory_block, width), BF16)]
     if packed:
         outs += [((16, 5 * narrow + 16, width), BF16)] * 2
     else:
         outs += [((width, width), F32)] * 2 + [((16, width), F32)]
-    scratch = half_scratch(share, length, half) + [((16, width), F32)]
+    scratch = [((16, width), F32)]
     if packed:
         scratch += [((width, width), BF16)] * 2 + [((width, width), F32)]
     return kernel, outs, scratch
+
+
+def make_self_back_upper(parts, share, width):
+    length, half = parts * share, width // 2
+
+    def kernel(*refs):
+        operands, (query_grad, own), refs = refs[1:9], refs[9:11], refs[11:]
+        sends, scratch = refs[: parts - 1], refs[parts - 1 :]
+        attention_back_half(operands, share, scratch)
+        query_grad[...] = scratch[4][...].T.astype(BF16)
+        give_half(share, scratch, own, sends)
+
+    outs = [((share, half), BF16), ((2 * share, half), F32)] + [((2 * share, half), BF16)] * (parts - 1)
+    return kernel, outs, half_scratch(share, length, half)
 
 
 def make_self_back_lower(packed, parts, rows, block, width, narrow, n_pieces):
@@ -857,7 +894,7 @@
         out_shape=[jax.ShapeDtypeStruct(shape, BF16)] * splits,
         in_specs=[VM] * len(arrays),
         out_specs=[VM] * splits,
-        compiler_params=pltpu.CompilerParams(vmem_limit_bytes=20 << 20),
+        compiler_params=pltpu.CompilerParams(vmem_limit_bytes=snug(arrays)),
         cost_estimate=pl.CostEstimate(flops=2 << 30, bytes_accessed=0, transcendentals=0),
         name="combine",
     )(*arrays)
@@ -904,12 +941,6 @@
         kernel, outs, *scratch = made
         return call(kernel, outs, (me_array,) + args, scratch[0] if scratch else [], micros, name)
 
-    turn_array = turn.reshape(1).astype(jnp.int32)
-
-    def turned(made, name, *args):
-        kernel, outs = made
-        return call(kernel, outs, (turn_array,) + args, [], 1.0, name)
-
     short = jnp.stack([query_bias, value_bias, output_bias, attention_gain, attention_shift,
                        source_query_bias, source_value_bias, source_output_bias, source_gain,
                        source_shift, outer_bias, final_gain, final_shift])
@@ -917,9 +948,8 @@
     def whole(array):
         return lax.all_gather(array, AXES, axis=0, tiled=True)
 
-    sent, kept = turned(
-        make_tokens_packet(block, memory_block, width), "tokens_packet", tokens, memory,
-        target_ids, source_ids, cotangent,
+    sent, kept = tokens_packet(
+        turn.reshape(1).astype(jnp.int32), tokens, memory, target_ids, source_ids, cotangent
     )
     came = swap(sent, parts, devices)
     row_tokens = [kept, came]
@@ -930,25 +960,24 @@
     own_tokens = row_tokens[:rows]
 
     if packed:
-        first, second, third = run(make_weights_packet(narrow, width, blocks), 1.0, "weights_packet",
-                                   query_weight, key_weight, value_weight, output_weight,
-                                   source_query, source_key, source_value, source_output,
-                                   inner_weight, outer_weight, short, inner_bias.reshape(1, wide))
+        first, rest = run(make_weights_packet(narrow, width, blocks), 1.0, "weights_packet",
+                          query_weight, key_weight, value_weight, output_weight, source_query,
+                          source_key, source_value, source_output, inner_weight, outer_weight,
+                          short, inner_bias.reshape(1, wide))
         first = after(first, sent)
         first = join([first, turned_swap(first, 0)])
         first_b = turned_swap(first, 1)
-        second = after(second, first)
-        second_b = turned_swap(second, 0)
-        first = join(after([first, first_b], second_b))
-        second = join([second, second_b])
-        third = after(third, second)
-        first_b, second_b, third_b = turned_swap(first, 2), turned_swap(second, 1), turned_swap(third, 0)
-        first_c = join(after([first, first_b], second_b, third_b, came, *kept_swaps))
-        second, third = join([second, second_b]), join([third, third_b])
-        first_d, second_b, third_b = turned_swap(first_c, 3), turned_swap(second, 2), turned_swap(third, 1)
-        second_c, third = join([second, second_b]), join([third, third_b])
-        first_d = after(first_d, second_c, third, *came_swaps)
-        second_d, third_b = turned_swap(second_c, 3), turned_swap(third, 2)
+        rest = after(rest, first)
+        rest_b = turned_swap(rest, 0)
+        first = join(after([first, first_b], rest_b))
+        rest = join(after([rest, rest_b], first_b, came, *kept_swaps))
+        first_b, rest_b = turned_swap(first, 2), turned_swap(rest, 1)
+        first_c = join(after([first, first_b], rest_b))
+        second, third = run(make_part((5 * narrow + 16, 2 * blocks * narrow), width), 1.0, "part", rest, rest_b)
+        first_d, second_b, third_b = turned_swap(first_c, 3), turned_swap(second, 2), turned_swap(third, 2)
+        second_c, third_c = join([second, second_b]), join([third, third_b])
+        first_d = after(first_d, second_c, third_c, *came_swaps)
+        second_d, third_d = turned_swap(second_c, 3), turned_swap(third_c, 3)
         set_self = [first_c, first_d, swap(first_c, 1, 32), swap(first_d, 1, 32)]
     else:
         full = [whole(w) for w in (query_weight, key_weight, value_weight, output_weight, source_query, source_key, source_value, source_output)]
@@ -975,11 +1004,8 @@
     row_memory, ids, memory_ids = found[10:]
     query_t = list(query_t)
     if packed:
-        third_c = join(after([third, third_b], query_t[0]))
-        third_d = turned_swap(third_c, 3)
-        second_d = after(second_d, query_t[0])
         set_cross = [second_c, second_d, swap(second_c, 1, 32), swap(second_d, 1, 32)]
-        query_t[0] = after(query_t[0], third_c, second_d)
+        query_t[0] = after(query_t[0], second_d)
         set_back, set_query, set_last, set_memory = set_cross, set_self, set_self, set_cross
     else:
         set_back, set_query, set_last, set_memory = [full[3], full[4], full[7]], full[:1], full[1:3], full[5:7]
@@ -1013,21 +1039,28 @@
     query = list(query)
     if packed:
         keep, send = combine([grads_inner[0], swap(grads_inner[1], 1, 32)], 2)
-        query[0] = after(query[0], keep, out_came)
         inner_step = [keep, turned_swap(send, 3)]
+        memory_key_own = after(memory_key_own, keep, out_came)
+    memory_own, memory_send, *grads_cross = run(
+        make_memory_back(packed, parts, rows, block, memory_block, width, narrow, len(set_memory)),
+        2.0, "memory_back", *set_memory, *own_tokens, memory_key_own, memory_value_own, sums_cross,
+        *grads_early, *memory_received,
+    )
+    if packed:
+        cross_came = swap(grads_cross[1], 1, 32)
+        query[0] = after(query[0], grads_cross[0])
     found = run(
-        make_self_back_upper(packed, parts, rows, block, memory_block, width, narrow, len(set_memory)),
-        12.0, "self_back_upper", *set_memory, *own_tokens, query[0], keys[0], values[0], slope[0],
-        slope_t[0], logs[0], deltas[0], ids, memory_key_own, memory_value_own, sums_cross,
-        *grads_early, *memory_received,
-    )
-    query_upper, own_upper, memory_own, memory_send = found[:4]
-    received_upper = [swap(a, m + 1, devices) for m, a in enumerate(found[4 : 4 + parts - 1])]
-    grads_cross = found[4 + parts - 1 :]
+        make_self_back_upper(parts, share, width), 7.0, "self_back_upper", query[0], keys[0],
+        values[0], slope[0], slope_t[0], logs[0], deltas[0], ids,
+    )
+    query_upper, own_upper = found[:2]
+    received_upper = [swap(a, m + 1, devices) for m, a in enumerate(found[2:])]
     if packed:
         keep, send = combine(inner_step, 2)
         inner_step = [keep, turned_swap(send, 2)]
-        query[1] = after(query[1], keep)
+        keep_cross, send = combine([grads_cross[0], cross_came], 2)
+        cross_step = [keep_cross, turned_swap(send, 3)]
+        query[1] = after(query[1], keep, keep_cross)
     in_part, query_sum, query_w_grad, own_lower, *sends = run(
         make_self_back_lower(packed, parts, rows, block, width, narrow, len(set_query)), 11.0,
         "self_back_lower", *set_query, *own_tokens, query[1], keys[1], values[1], slope[1],
@@ -1037,8 +1070,8 @@
     if packed:
         keep, send = combine(inner_step, 2)
         inner_step = [keep, turned_swap(send, 1)]
-        keep_cross, send = combine([grads_cross[0], swap(grads_cross[1], 1, 32)], 2)
-        cross_step = [keep_cross, turned_swap(send, 3)]
+        keep_cross, send = combine(cross_step, 2)
+        cross_step = [keep_cross, turned_swap(send, 2)]
         in_part = after(in_part, keep, keep_cross)
     in_own, in_send, *grads_last = run(
         make_last(packed, parts, rows, block, memory_block, width, narrow, len(set_last)), 6.0,
@@ -1047,16 +1080,14 @@
     )
 
     if packed:
+        keep, send = combine([grads_last[0], swap(grads_last[1], 1, 32)], 2)
+        last_step = [keep, turned_swap(send, 3)]
+        in_send = after(in_send, last_step[1])
         keep_inner, send = combine(inner_step, 2)
         inner_step = [keep_inner, turned_swap(send, 0)]
         keep_cross, send = combine(cross_step, 2)
-        cross_step = [keep_cross, turned_swap(send, 2)]
-        keep, send = combine(after([grads_last[0], swap(grads_last[1], 1, 32)], keep_inner, keep_cross), 2)
-        last_step = [keep, turned_swap(send, 3)]
-        in_send = after(in_send, last_step[1])
-        keep_cross, send = combine(cross_step, 2)
         cross_step = [keep_cross, turned_swap(send, 1)]
-        keep, send = combine(after(last_step, keep_cross), 2)
+        keep, send = combine(after(last_step, keep_inner, keep_cross), 2)
         last_step = [keep, turned_swap(send, 2)]
         keep_cross, send = combine(cross_step, 2)
         cross_step = [keep_cross, turned_swap(send, 0)]

time: 186 us -> 186 us (level)
  waiting for transfers between devices: 80.5 us -> 73.8 us
  starting transfers between devices: 36 us -> 42.1 us
  local copies, waits for them, and re-layouts: 7.59 us -> 9.52 us
    ppermute x24 -> x22, waiting for transfers between devices: 79.9 us -> 72.7 us  [turned_swap(): lax.ppermute(array, AXES, [(i, i ^ ORDERS[i % 2][step]) for i in range(32)])]
    ppermute x24 -> x22, starting transfers between devices: 28.7 us -> 35.3 us  [turned_swap(): lax.ppermute(array, AXES, [(i, i ^ ORDERS[i % 2][step]) for i in range(32)])]
    unnamed x66 -> x80, local copies, waits for them, and re-layouts: 6.96 us -> 8.89 us
    pallas_call x11 -> x12, Pallas kernels: 53.3 us -> 53 us  [call(): pl.pallas_call(kernel, out_shape=[jax.ShapeDtypeStruct(s, d) for s, d in...]
  transfers between devices with their start and end apart: 41 -> 39, of which waited for: 17 -> 15; matrix products, arithmetic and copies ran while one was open for 2% -> 2% of each run, Pallas kernels for 23% -> 21%
where the time goes in v6:
time: 186 us
  waiting for transfers between devices  73.8 us (40%)
  Pallas kernels  55.6 us (30%)
  starting transfers between devices  42.1 us (23%)
  local copies, waits for them, and re-layouts  9.52 us (5%)
  other arithmetic  2.97 us (2%)
    ppermute x22, waiting for transfers between devices, turned_swap(): lax.ppermute(array, AXES, [(i, i ^ ORDERS[i % 2][step]) for i in range(32)])  72.7 us
    pallas_call x12, Pallas kernels, call(): pl.pallas_call(kernel, out_shape=[jax.ShapeDtypeStruct(s, d) for s, d in...  53 us
    ppermute x22, starting transfers between devices, turned_swap(): lax.ppermute(array, AXES, [(i, i ^ ORDERS[i % 2][step]) for i in range(32)])  35.3 us
    unnamed x80, local copies, waits for them, and re-layouts  8.89 us
    ppermute x17, starting transfers between devices, swap(): return lax.ppermute(array, AXES, [(i, i ^ mask) for i in range(devices)])  6.8 us
  transfers between devices with their start and end apart: 39, of which 15 were waited for; matrix products, arithmetic and copies ran while one was open for 2% of the time, Pallas kernels for 21%

profile of v6, /device:TPU:0, one launch (start us, length us, event | category | flops | bytes accessed | tf_op | source)
XLA Modules:
  0.0 185.6 jit_solution(18410482482578392138)
XLA Ops:
  5.7 3.0 %collective-permute-start.3 = (bf16[584,512]{1,0:T(8,128)(2,1)S(1)}, bf16[584,512]{1,0:T(8,128)(2,1)S(1)}, u32[]{:S(2)}, u32[]{:S(2)}) collective-permute-start(bf16[584,512]{1,0:T(8,128)(2,1)S(1)} %get-tuple-element.153), channel_id=1, source_target_pairs={{0,2},{1,3},{2,0},{3,1},{4,6},{5,7},{6,4},{7,5},{8,10},{9,11},{10,... | collective-permute-start | bytes 1794056 | tf_op jit(solution)/shard_map/ppermute | solution.py:161
  10.8 3.2 %collective-permute-done.refs_1_ = bf16[56,512]{1,0:T(8,128)(2,1)S(1)} collective-permute-done((bf16[56,512]{1,0:T(8,128)(2,1)S(1)}, bf16[56,512]{1,0:T(8,128)(2,1)S(1)}, u32[]{:S(2)}, u32[]{:S(2)}) %collective-permute-start) | collective-permute-done | bytes 57376 | tf_op jit(solution)/shard_map/ppermute | solution.py:168
  15.2 2.6 %collective-permute-start.2 = (bf16[112,512]{1,0:T(8,128)(2,1)S(1)}, bf16[112,512]{1,0:T(8,128)(2,1)S(1)}, u32[]{:S(2)}, u32[]{:S(2)}) collective-permute-start(bf16[112,512]{1,0:T(8,128)(2,1)S(1)} %join.6.refs_0_), channel_id=1, source_target_pairs={{0,16},{1,9},{2,18},{3,11},{4,20},{5,13},{6,22},{7,15},{8,24},{9,1... | collective-permute-start | bytes 344072 | tf_op jit(solution)/shard_map/ppermute | solution.py:168
  17.8 5.7 %collective-permute-done.2.refs_1_ = bf16[112,512]{1,0:T(8,128)(2,1)S(1)} collective-permute-done((bf16[112,512]{1,0:T(8,128)(2,1)S(1)}, bf16[112,512]{1,0:T(8,128)(2,1)S(1)}, u32[]{:S(2)}, u32[]{:S(2)}) %collective-permute-start.2) | collective-permute-done | bytes 114720 | tf_op jit(solution)/shard_map/ppermute | solution.py:168
  24.7 2.1 %collective-permute-start.5 = (bf16[448,512]{1,0:T(8,128)(2,1)S(1)}, bf16[448,512]{1,0:T(8,128)(2,1)S(1)}, u32[]{:S(2)}, u32[]{:S(2)}) collective-permute-start(bf16[448,512]{1,0:T(8,128)(2,1)S(1)} %join.7.upper), channel_id=1, source_target_pairs={{0,16},{1,9},{2,18},{3,11},{4,20},{5,13},{6,22},{7,15},{8,24},{9,1... | collective-permute-start | bytes 1376264 | tf_op jit(solution)/shard_map/ppermute | solution.py:168
  27.4 10.3 %collective-permute-done.5.lower = bf16[448,512]{1,0:T(8,128)(2,1)S(1)} collective-permute-done((bf16[448,512]{1,0:T(8,128)(2,1)S(1)}, bf16[448,512]{1,0:T(8,128)(2,1)S(1)}, u32[]{:S(2)}, u32[]{:S(2)}) %collective-permute-start.5) | collective-permute-done | bytes 458784 | tf_op jit(solution)/shard_map/ppermute | solution.py:168
  41.5 13.7 %collective-permute-done.10.refs_1_ = bf16[384,512]{1,0:T(8,128)(2,1)S(1)} collective-permute-done((bf16[384,512]{1,0:T(8,128)(2,1)S(1)}, bf16[384,512]{1,0:T(8,128)(2,1)S(1)}, u32[]{:S(2)}, u32[]{:S(2)}) %collective-permute-start.10) | collective-permute-done | bytes 393248 | tf_op jit(solution)/shard_map/ppermute | solution.py:168
  59.3 8.2 %collective-permute-done.14.refs_2_ = bf16[768,512]{1,0:T(8,128)(2,1)S(1)} collective-permute-done((bf16[768,512]{1,0:T(8,128)(2,1)S(1)}, bf16[768,512]{1,0:T(8,128)(2,1)S(1)}, u32[]{:S(2)}, u32[]{:S(2)}) %collective-permute-start.14) | collective-permute-done | bytes 786464 | tf_op jit(solution)/shard_map/ppermute | solution.py:168
  67.5 8.1 %self_attention.1 = (bf16[256,512]{1,0:T(8,128)(2,1)S(1)}, bf16[256,512]{1,0:T(8,128)(2,1)S(1)}, f32[4,1,512]{2,1,0:T(1,128)S(1)}, f32[4,1,512]{2,1,0:T(1,128)S(1)}) custom-call(s32[1]{0:T(128)} %bitcast.me_ref.refs_0_, bf16[256,512]{1,0:T(8,128)(2,1)S(1)} %get-tuple-element.167.refs_0_, bf16[256,512]{1,0:T(8,128)(2,1)S(1)} %get-tuple-element.168.refs_1_, ...), custom_call_target="tpu_custom_call" | custom-call | flops 13799999488 | bytes 3166208 | tf_op jit(solution)/shard_map/self_attention/pallas_call | solution.py:251
  75.6 3.2 %collective-permute-done.7.refs_2_ = bf16[1024,512]{1,0:T(8,128)(2,1)S(1)} collective-permute-done((bf16[1024,512]{1,0:T(8,128)(2,1)S(1)}, bf16[1024,512]{1,0:T(8,128)(2,1)S(1)}, u32[]{:S(2)}, u32[]{:S(2)}) %collective-permute-start.7) | collective-permute-done | bytes 1048608 | tf_op jit(solution)/shard_map/ppermute | solution.py:168
  78.7 5.4 %cross_forward.1 = (f32[512,512]{1,0:T(8,128)S(1)}, f32[512,512]{1,0:T(8,128)S(1)}, bf16[512,512]{1,0:T(8,128)(2,1)S(1)}, bf16[256,512]{1,0:T(8,128)(2,1)S(1)}, ...) custom-call(s32[1]{0:T(128)} %bitcast.me_ref.refs_0_, ...), custom_call_target="tpu_custom_call" | custom-call | flops 10350000128 | bytes 8852480 | tf_op jit(solution)/shard_map/cross_forward/pallas_call | solution.py:251
  84.1 12.5 %inner.1 = (f32[256,512]{1,0:T(8,128)S(1)}, bf16[256,512]{1,0:T(8,128)(2,1)S(1)}, f32[512,512]{1,0:T(8,128)S(1)}, f32[8,512]{1,0:T(8,128)S(1)}, bf16[16,128,512]...) custom-call(s32[1]{0:T(128)} %bitcast.me_ref.refs_0_, bf16[1024,512]{1,0:T(8,128)(2,1)S(1)} %join.8.refs_1_, ...), custom_call_target="tpu_custom_call" | custom-call | flops 20700000256 | bytes 12517376 | tf_op jit(solution)/shard_map/inner/pallas_call | solution.py:251
  97.7 8.2 %cross_back.1 = (f32[512,512]{1,0:T(8,128)S(1)}, f32[128,512]{1,0:T(8,128)S(1)}, f32[128,512]{1,0:T(8,128)S(1)}, f32[16,512]{1,0:T(8,128)S(1)}, bf16[512,256]{1,...) custom-call(s32[1]{0:T(128)} %bitcast.me_ref.refs_0_, ...), custom_call_target="tpu_custom_call" | custom-call | flops 16099999744 | bytes 12964864 | tf_op jit(solution)/shard_map/cross_back/pallas_call | solution.py:251
  109.9 6.3 %self_back_upper.1 = (bf16[512,256]{1,0:T(8,128)(2,1)S(1)}, f32[1024,256]{1,0:T(8,128)S(1)}, bf16[1024,256]{1,0:T(8,128)(2,1)S(1)}) custom-call(s32[1]{0:T(128)} %bitcast.me_ref.refs_0_, bf16[512,256]{1,0:T(8,128)(2,1)S(1)} %get-tuple-element.217.refs_1_, bf16[1024,256]{1,0:T(8,128)(2,1)S(1)} %get-tuple-element.169.refs_2_, ...), custom_call_target="tpu_custom_call" | custom-call | flops 8049999872 | bytes 3690496 | tf_op jit(solution)/shard_map/self_back_upper/pallas_call | solution.py:251
  116.9 6.9 %collective-permute-done.21.refs_1_ = bf16[8,128,512]{2,1,0:T(8,128)(2,1)S(1)} collective-permute-done((bf16[8,128,512]{2,1,0:T(8,128)(2,1)S(1)}, bf16[8,128,512]{2,1,0:T(8,128)(2,1)S(1)}, u32[]{:S(2)}, u32[]{:S(2)}) %collective-permute-start.21) | collective-permute-done | bytes 1048608 | tf_op jit(solution)/shard_map/ppermute | solution.py:168
  126.6 6.8 %self_back_lower.1 = (f32[512,512]{1,0:T(8,128)S(1)}, f32[8,512]{1,0:T(8,128)S(1)}, bf16[512,512]{1,0:T(8,128)(2,1)S(1)}, f32[1024,256]{1,0:T(8,128)S(1)}, bf16[1024,256]{1,0:T(8,128)(2,1)S(1)}) custom-call(s32[1]{0:T(128)} %bitcast.me_ref.refs_0_, bf16[448,512]{1,0:T(8,128)(2,1)S(1)} %join.10.refs_1_, bf16[448,512]{1,0:T(8,128)(2,1)S(1)} %collective-permute-done.9.refs_2_, ...), custom_call_target="tpu_custom_call" | custom-call | flops 12650000384 | bytes 9359360 | tf_op jit(solution)/shard_map/self_back_lower/pallas_call | solution.py:251
  133.5 5.3 %collective-permute-done.24.refs_1_ = bf16[4,128,512]{2,1,0:T(8,128)(2,1)S(1)} collective-permute-done((bf16[4,128,512]{2,1,0:T(8,128)(2,1)S(1)}, bf16[4,128,512]{2,1,0:T(8,128)(2,1)S(1)}, u32[]{:S(2)}, u32[]{:S(2)}) %collective-permute-start.24) | collective-permute-done | bytes 524320 | tf_op jit(solution)/shard_map/ppermute | solution.py:168
  152.0 4.2 %collective-permute-done.31.refs_1_ = bf16[2,128,512]{2,1,0:T(8,128)(2,1)S(1)} collective-permute-done((bf16[2,128,512]{2,1,0:T(8,128)(2,1)S(1)}, bf16[2,128,512]{2,1,0:T(8,128)(2,1)S(1)}, u32[]{:S(2)}, u32[]{:S(2)}) %collective-permute-start.31) | collective-permute-done | bytes 262176 | tf_op jit(solution)/shard_map/ppermute | solution.py:168
  156.2 2.2 %collective-permute-done.33.refs_1_ = bf16[4,96,512]{2,1,0:T(8,128)(2,1)S(1)} collective-permute-done((bf16[4,96,512]{2,1,0:T(8,128)(2,1)}, bf16[4,96,512]{2,1,0:T(8,128)(2,1)S(1)}, u32[]{:S(2)}, u32[]{:S(2)}) %collective-permute-start.33) | collective-permute-done | bytes 393248 | tf_op jit(solution)/shard_map/ppermute | solution.py:168
  161.9 2.7 %collective-permute-start.32 = (bf16[1,128,512]{2,1,0:T(8,128)(2,1)S(1)}, bf16[1,128,512]{2,1,0:T(8,128)(2,1)S(1)}, u32[]{:S(2)}, u32[]{:S(2)}) collective-permute-start(bf16[1,128,512]{2,1,0:T(8,128)(2,1)S(1)} %get-tuple-element.246), channel_id=1, source_target_pairs={{0,8},{1,17},{2,10},{3,19},{4,12},{5,21},{6,14},{7,23},{8,0},{9,25... | collective-permute-start | bytes 393224 | tf_op jit(solution)/shard_map/ppermute | solution.py:168
  165.2 5.7 %collective-permute-start.35 = (bf16[1,96,512]{2,1,0:T(8,128)(2,1)S(1)}, bf16[1,96,512]{2,1,0:T(8,128)(2,1)S(1)}, u32[]{:S(2)}, u32[]{:S(2)}) collective-permute-start(bf16[1,96,512]{2,1,0:T(8,128)(2,1)S(1)} %get-tuple-element.251), channel_id=1, source_target_pairs={{0,8},{1,17},{2,10},{3,19},{4,12},{5,21},{6,14},{7,23},{8,0},{9,25... | collective-permute-start | bytes 294920 | tf_op jit(solution)/shard_map/ppermute | solution.py:168
  171.0 3.5 %collective-permute-start.37 = (bf16[2,56,512]{2,1,0:T(8,128)(2,1)S(1)}, bf16[2,56,512]{2,1,0:T(8,128)(2,1)S(1)}, u32[]{:S(2)}, u32[]{:S(2)}) collective-permute-start(bf16[2,56,512]{2,1,0:T(8,128)(2,1)S(1)} %get-tuple-element.260), channel_id=1, source_target_pairs={{0,16},{1,9},{2,18},{3,11},{4,20},{5,13},{6,22},{7,15},{8,24},{9,1... | collective-permute-start | bytes 344072 | tf_op jit(solution)/shard_map/ppermute | solution.py:168
  175.6 3.9 %collective-permute-done.37.refs_1_ = bf16[2,56,512]{2,1,0:T(8,128)(2,1)S(1)} collective-permute-done((bf16[2,56,512]{2,1,0:T(8,128)(2,1)S(1)}, bf16[2,56,512]{2,1,0:T(8,128)(2,1)S(1)}, u32[]{:S(2)}, u32[]{:S(2)}) %collective-permute-start.37) | collective-permute-done | bytes 114720 | tf_op jit(solution)/shard_map/ppermute | solution.py:168
  180.3 3.4 %collective-permute-done.38.refs_5_ = bf16[1,56,512]{2,1,0:T(8,128)(2,1)S(1)} collective-permute-done((bf16[1,56,512]{2,1,0:T(8,128)(2,1)S(1)}, bf16[1,56,512]{2,1,0:T(8,128)(2,1)S(1)}, u32[]{:S(2)}, u32[]{:S(2)}) %collective-permute-start.38) | collective-permute-done | bytes 57376 | tf_op jit(solution)/shard_map/ppermute | solution.py:168
  (173 shorter events, 46.9 us)
Async XLA Ops:
  5.7 19.0 %collective-permute-start.3 = (bf16[584,512]{1,0:T(8,128)(2,1)S(1)}, bf16[584,512]{1,0:T(8,128)(2,1)S(1)}, u32[]{:S(2)}, u32[]{:S(2)}) collective-permute-start(bf16[584,512]{1,0:T(8,128)(2,1)S(1)} %get-tuple-element.153), channel_id=1, source_target_pairs={{0,2},{1,3},{2,0},{3,1},{4,6},{5,7},{6,4},{7,5},{8,10},{9,11},{10,... | collective-permute-start | bytes 1794056 | tf_op jit(solution)/shard_map/ppermute | solution.py:161
  8.7 16.0 %collective-permute-start.4 = (bf16[584,512]{1,0:T(8,128)(2,1)S(1)}, bf16[584,512]{1,0:T(8,128)(2,1)S(1)}, u32[]{:S(2)}, u32[]{:S(2)}) collective-permute-start(bf16[584,512]{1,0:T(8,128)(2,1)S(1)} %get-tuple-element.156.refs_5_.refs_6_), channel_id=1, source_target_pairs={{0,1},{1,0},{2,3},{3,2},{4,5},{5,4},{6,7},{7,6},{8,9},{9,8},{10,11... | collective-permute-start | bytes 1794056 | tf_op jit(solution)/shard_map/ppermute | solution.py:161
  14.0 10.7 %collective-permute-start.1 = (bf16[224,512]{1,0:T(8,128)(2,1)S(1)}, bf16[224,512]{1,0:T(8,128)(2,1)S(1)}, u32[]{:S(2)}, u32[]{:S(2)}) collective-permute-start(bf16[224,512]{1,0:T(8,128)(2,1)S(1)} %get-tuple-element.157.refs_0_), channel_id=1, source_target_pairs={{0,8},{1,17},{2,10},{3,19},{4,12},{5,21},{6,14},{7,23},{8,0},{9,25... | collective-permute-start | bytes 688136 | tf_op jit(solution)/shard_map/ppermute | solution.py:168
  24.7 13.0 %collective-permute-start.5 = (bf16[448,512]{1,0:T(8,128)(2,1)S(1)}, bf16[448,512]{1,0:T(8,128)(2,1)S(1)}, u32[]{:S(2)}, u32[]{:S(2)}) collective-permute-start(bf16[448,512]{1,0:T(8,128)(2,1)S(1)} %join.7.upper), channel_id=1, source_target_pairs={{0,16},{1,9},{2,18},{3,11},{4,20},{5,13},{6,22},{7,15},{8,24},{9,1... | collective-permute-start | bytes 1376264 | tf_op jit(solution)/shard_map/ppermute | solution.py:168
  26.8 11.0 %collective-permute-start.8 = (bf16[224,512]{1,0:T(8,128)(2,1)S(1)}, bf16[224,512]{1,0:T(8,128)(2,1)S(1)}, u32[]{:S(2)}, u32[]{:S(2)}) collective-permute-start(bf16[224,512]{1,0:T(8,128)(2,1)S(1)} %join.9.refs_0_), channel_id=1, source_target_pairs={{0,2},{1,5},{2,0},{3,7},{4,6},{5,1},{6,4},{7,3},{8,10},{9,13},{10,... | collective-permute-start | bytes 688136 | tf_op jit(solution)/shard_map/ppermute | solution.py:168
  27.4 27.9 %collective-permute-start.11 = (bf16[584,512]{1,0:T(8,128)(2,1)S(1)}, bf16[584,512]{1,0:T(8,128)(2,1)S(1)}, u32[]{:S(2)}, u32[]{:S(2)}) collective-permute-start(bf16[584,512]{1,0:T(8,128)(2,1)S(1)} %collective-permute-done.3.refs_6_.refs_7_), channel_id=1, source_target_pairs={{0,1},{1,0},{2,3},{3,2},{4,5},{5,4},{6,7},{7,6},{8,9},{9,8},{10,11... | collective-permute-start | bytes 1794056 | tf_op jit(solution)/shard_map/ppermute | solution.py:161
  37.8 17.5 %collective-permute-start.6 = (bf16[512,512]{1,0:T(8,128)(2,1)S(1)}, bf16[512,512]{1,0:T(8,128)(2,1)S(1)}, u32[]{:S(2)}, u32[]{:S(2)}) collective-permute-start(bf16[512,512]{1,0:T(8,128)(2,1)S(1)} %get-tuple-element.159.refs_0_), channel_id=1, source_target_pairs={{0,2},{1,5},{2,0},{3,7},{4,6},{5,1},{6,4},{7,3},{8,10},{9,13},{10,... | collective-permute-start | bytes 1572872 | tf_op jit(solution)/shard_map/ppermute | solution.py:168
  37.9 17.5 %collective-permute-start.9 = (bf16[448,512]{1,0:T(8,128)(2,1)S(1)}, bf16[448,512]{1,0:T(8,128)(2,1)S(1)}, u32[]{:S(2)}, u32[]{:S(2)}) collective-permute-start(bf16[448,512]{1,0:T(8,128)(2,1)S(1)} %join.10.refs_1_), channel_id=1, source_target_pairs={{0,4},{1,3},{2,6},{3,1},{4,0},{5,7},{6,2},{7,5},{8,12},{9,11},{10,... | collective-permute-start | bytes 1376264 | tf_op jit(solution)/shard_map/ppermute | solution.py:168
  39.9 15.3 %collective-permute-start.10 = (bf16[384,512]{1,0:T(8,128)(2,1)S(1)}, bf16[384,512]{1,0:T(8,128)(2,1)S(1)}, u32[]{:S(2)}, u32[]{:S(2)}) collective-permute-start(bf16[384,512]{1,0:T(8,128)(2,1)S(1)} %get-tuple-element.164.refs_0_), channel_id=1, source_target_pairs={{0,2},{1,5},{2,0},{3,7},{4,6},{5,1},{6,4},{7,3},{8,10},{9,13},{10,... | collective-permute-start | bytes 1179656 | tf_op jit(solution)/shard_map/ppermute | solution.py:168
  41.5 16.1 %collective-permute-start.12 = (bf16[448,512]{1,0:T(8,128)(2,1)S(1)}, bf16[448,512]{1,0:T(8,128)(2,1)S(1)}, u32[]{:S(2)}, u32[]{:S(2)}) collective-permute-start(bf16[448,512]{1,0:T(8,128)(2,1)S(1)} %join.10.refs_1_), channel_id=1, source_target_pairs={{0,1},{1,0},{2,3},{3,2},{4,5},{5,4},{6,7},{7,6},{8,9},{9,8},{10,11... | collective-permute-start | bytes 1376264 | tf_op jit(solution)/shard_map/ppermute | solution.py:161
  55.4 12.1 %collective-permute-start.14 = (bf16[768,512]{1,0:T(8,128)(2,1)S(1)}, bf16[768,512]{1,0:T(8,128)(2,1)S(1)}, u32[]{:S(2)}, u32[]{:S(2)}) collective-permute-start(bf16[768,512]{1,0:T(8,128)(2,1)S(1)} %join.11.refs_1_), channel_id=1, source_target_pairs={{0,4},{1,3},{2,6},{3,1},{4,0},{5,7},{6,2},{7,5},{8,12},{9,11},{10,... | collective-permute-start | bytes 2359304 | tf_op jit(solution)/shard_map/ppermute | solution.py:168
  56.0 22.7 %collective-permute-start.17 = (bf16[768,512]{1,0:T(8,128)(2,1)S(1)}, bf16[768,512]{1,0:T(8,128)(2,1)S(1)}, u32[]{:S(2)}, u32[]{:S(2)}) collective-permute-start(bf16[768,512]{1,0:T(8,128)(2,1)S(1)} %join.11.refs_1_), channel_id=1, source_target_pairs={{0,1},{1,0},{2,3},{3,2},{4,5},{5,4},{6,7},{7,6},{8,9},{9,8},{10,11... | collective-permute-start | bytes 2359304 | tf_op jit(solution)/shard_map/ppermute | solution.py:161
  56.2 22.6 %collective-permute-start.7 = (bf16[1024,512]{1,0:T(8,128)(2,1)S(1)}, bf16[1024,512]{1,0:T(8,128)(2,1)S(1)}, u32[]{:S(2)}, u32[]{:S(2)}) collective-permute-start(bf16[1024,512]{1,0:T(8,128)(2,1)S(1)} %join.8.refs_1_), channel_id=1, source_target_pairs={{0,4},{1,3},{2,6},{3,1},{4,0},{5,7},{6,2},{7,5},{8,12},{9,11},{10,... | collective-permute-start | bytes 3145736 | tf_op jit(solution)/shard_map/ppermute | solution.py:168
  57.5 26.6 %collective-permute-start.15 = (bf16[1024,512]{1,0:T(8,128)(2,1)S(1)}, bf16[1024,512]{1,0:T(8,128)(2,1)S(1)}, u32[]{:S(2)}, u32[]{:S(2)}) collective-permute-start(bf16[1024,512]{1,0:T(8,128)(2,1)S(1)} %join.8.refs_1_), channel_id=1, source_target_pairs={{0,1},{1,0},{2,3},{3,2},{4,5},{5,4},{6,7},{7,6},{8,9},{9,8},{10,11... | collective-permute-start | bytes 3145736 | tf_op jit(solution)/shard_map/ppermute | solution.py:161
  67.5 11.2 %collective-permute-start.18 = (bf16[768,512]{1,0:T(8,128)(2,1)S(1)}, bf16[768,512]{1,0:T(8,128)(2,1)S(1)}, u32[]{:S(2)}, u32[]{:S(2)}) collective-permute-start(bf16[768,512]{1,0:T(8,128)(2,1)S(1)} %collective-permute-done.14.refs_2_), channel_id=1, source_target_pairs={{0,1},{1,0},{2,3},{3,2},{4,5},{5,4},{6,7},{7,6},{8,9},{9,8},{10,11... | collective-permute-start | bytes 2359304 | tf_op jit(solution)/shard_map/ppermute | solution.py:161
  108.7 16.9 %collective-permute-start.23 = (bf16[16,96,512]{2,1,0:T(8,128)(2,1)S(1)}, bf16[16,96,512]{2,1,0:T(8,128)(2,1)S(1)}, u32[]{:S(2)}, u32[]{:S(2)}) collective-permute-start(bf16[16,96,512]{2,1,0:T(8,128)(2,1)S(1)} %get-tuple-element.207), channel_id=1, source_target_pairs={{0,1},{1,0},{2,3},{3,2},{4,5},{5,4},{6,7},{7,6},{8,9},{9,8},{10,11... | collective-permute-start | bytes 4718600 | tf_op jit(solution)/shard_map/ppermute | solution.py:161
  109.0 14.8 %collective-permute-start.21 = (bf16[8,128,512]{2,1,0:T(8,128)(2,1)S(1)}, bf16[8,128,512]{2,1,0:T(8,128)(2,1)S(1)}, u32[]{:S(2)}, u32[]{:S(2)}) collective-permute-start(bf16[8,128,512]{2,1,0:T(8,128)(2,1)S(1)} %get-tuple-element.188), channel_id=1, source_target_pairs={{0,4},{1,3},{2,6},{3,1},{4,0},{5,7},{6,2},{7,5},{8,12},{9,11},{10,... | collective-permute-start | bytes 3145736 | tf_op jit(solution)/shard_map/ppermute | solution.py:168
  116.3 25.7 %collective-permute-start.26 = (bf16[1024,256]{1,0:T(8,128)(2,1)S(1)}, bf16[1024,256]{1,0:T(8,128)(2,1)S(1)}, u32[]{:S(2)}, u32[]{:S(2)}) collective-permute-start(bf16[1024,256]{1,0:T(8,128)(2,1)S(1)} %get-tuple-element.235), channel_id=1, source_target_pairs={{0,1},{1,0},{2,3},{3,2},{4,5},{5,4},{6,7},{7,6},{8,9},{9,8},{10,11... | collective-permute-start | bytes 1572872 | tf_op jit(solution)/shard_map/ppermute | solution.py:161
  124.0 14.8 %collective-permute-start.24 = (bf16[4,128,512]{2,1,0:T(8,128)(2,1)S(1)}, bf16[4,128,512]{2,1,0:T(8,128)(2,1)S(1)}, u32[]{:S(2)}, u32[]{:S(2)}) collective-permute-start(bf16[4,128,512]{2,1,0:T(8,128)(2,1)S(1)} %get-tuple-element.225), channel_id=1, source_target_pairs={{0,2},{1,5},{2,0},{3,7},{4,6},{5,1},{6,4},{7,3},{8,10},{9,13},{10,... | collective-permute-start | bytes 1572872 | tf_op jit(solution)/shard_map/ppermute | solution.py:168
  126.0 14.2 %collective-permute-start.25 = (bf16[8,96,512]{2,1,0:T(8,128)(2,1)S(1)}, bf16[8,96,512]{2,1,0:T(8,128)(2,1)S(1)}, u32[]{:S(2)}, u32[]{:S(2)}) collective-permute-start(bf16[8,96,512]{2,1,0:T(8,128)(2,1)S(1)} %get-tuple-element.227), channel_id=1, source_target_pairs={{0,4},{1,3},{2,6},{3,1},{4,0},{5,7},{6,2},{7,5},{8,12},{9,11},{10,... | collective-permute-start | bytes 2359304 | tf_op jit(solution)/shard_map/ppermute | solution.py:168
  147.6 10.9 %collective-permute-start.33 = (bf16[4,96,512]{2,1,0:T(8,128)(2,1)}, bf16[4,96,512]{2,1,0:T(8,128)(2,1)S(1)}, u32[]{:S(2)}, u32[]{:S(2)}) collective-permute-start(bf16[4,96,512]{2,1,0:T(8,128)(2,1)} %copy-done.2), channel_id=1, source_target_pairs={{0,2},{1,5},{2,0},{3,7},{4,6},{5,1},{6,4},{7,3},{8,10},{9,13},{10,... | collective-permute-start | bytes 1179656 | tf_op jit(solution)/shard_map/ppermute | solution.py:168
  160.0 10.9 %collective-permute-start.36 = (bf16[4,56,512]{2,1,0:T(8,128)(2,1)S(1)}, bf16[4,56,512]{2,1,0:T(8,128)(2,1)S(1)}, u32[]{:S(2)}, u32[]{:S(2)}) collective-permute-start(bf16[4,56,512]{2,1,0:T(8,128)(2,1)S(1)} %get-tuple-element.256), channel_id=1, source_target_pairs={{0,2},{1,5},{2,0},{3,7},{4,6},{5,1},{6,4},{7,3},{8,10},{9,13},{10,... | collective-permute-start | bytes 688136 | tf_op jit(solution)/shard_map/ppermute | solution.py:168
  161.9 18.4 %collective-permute-start.32 = (bf16[1,128,512]{2,1,0:T(8,128)(2,1)S(1)}, bf16[1,128,512]{2,1,0:T(8,128)(2,1)S(1)}, u32[]{:S(2)}, u32[]{:S(2)}) collective-permute-start(bf16[1,128,512]{2,1,0:T(8,128)(2,1)S(1)} %get-tuple-element.246), channel_id=1, source_target_pairs={{0,8},{1,17},{2,10},{3,19},{4,12},{5,21},{6,14},{7,23},{8,0},{9,25... | collective-permute-start | bytes 393224 | tf_op jit(solution)/shard_map/ppermute | solution.py:168
  165.2 15.1 %collective-permute-start.35 = (bf16[1,96,512]{2,1,0:T(8,128)(2,1)S(1)}, bf16[1,96,512]{2,1,0:T(8,128)(2,1)S(1)}, u32[]{:S(2)}, u32[]{:S(2)}) collective-permute-start(bf16[1,96,512]{2,1,0:T(8,128)(2,1)S(1)} %get-tuple-element.251), channel_id=1, source_target_pairs={{0,8},{1,17},{2,10},{3,19},{4,12},{5,21},{6,14},{7,23},{8,0},{9,25... | collective-permute-start | bytes 294920 | tf_op jit(solution)/shard_map/ppermute | solution.py:168
  (55 other events, 289.8 us)

commit v7 on v6

--- a/solution.py
+++ b/solution.py
@@ -161,22 +161,23 @@
     return lax.ppermute(array, AXES, [(i, i ^ mask) for i in range(devices)])
 
 
-ORDERS = ((8, 16, 2, 4), (16, 8, 4, 2))
-
-
-def turned_swap(array, step):
-    return lax.ppermute(array, AXES, [(i, i ^ ORDERS[i % 2][step]) for i in range(32)])
+Z_FIRST = ((8, 16, 2, 4), (16, 8, 4, 2))
+Z_LAST = ((2, 4, 8, 16), (4, 2, 16, 8))
+
+
+def turned_swap(array, step, orders=Z_FIRST):
+    return lax.ppermute(array, AXES, [(i, i ^ orders[i % 2][step]) for i in range(32)])
 
 
 def after(value, *others):
     return lax.optimization_barrier((value, others))[0]
 
 
-def places(me):
+def places(me, orders=Z_FIRST):
     found = []
     for core in range(2):
         even = ((me & 1) ^ core) == 0
-        masks = [jnp.where(even, first, second) for first, second in zip(*ORDERS)]
+        masks = [jnp.where(even, first, second) for first, second in zip(*orders)]
         for far in range(2):
             for slot in range(8):
                 device = me ^ core if core else me
@@ -187,8 +188,8 @@
     return found
 
 
-def unpack(me, pieces, stride, first, rows, scratch):
-    for core, far, slot, device in places(me):
+def unpack(me, pieces, stride, first, rows, scratch, orders=Z_FIRST):
+    for core, far, slot, device in places(me, orders):
         ref = pieces[2 * core + far]
         at = slot * stride + first
         scratch[pl.ds(pl.multiple_of(device * rows, rows), rows), :] = ref[at : at + rows, :]
@@ -204,8 +205,8 @@
 
 
 class Grads:
-    def __init__(self, me, refs, dense, rows):
-        self.me, self.refs, self.dense, self.rows = me, refs, dense, rows
+    def __init__(self, me, refs, dense, rows, orders=Z_FIRST):
+        self.me, self.refs, self.dense, self.rows, self.orders = me, refs, dense, rows, orders
 
     def put(self, index, grad):
         if self.dense is None:
@@ -213,7 +214,7 @@
             return
         self.dense[...] = grad
         rows = self.rows
-        for core, far, slot, device in places(self.me):
+        for core, far, slot, device in places(self.me, self.orders):
             found = self.dense[pl.ds(pl.multiple_of(device * rows, rows), rows), :]
             self.refs[core][far * 8 + slot, index * rows : (index + 1) * rows, :] = found.astype(BF16)
 
@@ -256,7 +257,7 @@
         scratch_shapes=[pltpu.VMEM(s, d) for s, d in scratch],
         compiler_params=pltpu.CompilerParams(vmem_limit_bytes=min(need + (room << 20), 58 << 20)),
         cost_estimate=pl.CostEstimate(
-            flops=int(micros * 1.15e9), bytes_accessed=moved, transcendentals=0
+            flops=int(micros * 0.15e9), bytes_accessed=moved // 8, transcendentals=0
         ),
         name=name,
     )(*args)
@@ -267,15 +268,21 @@
     memory_block = memory.shape[1]
     first = block + memory_block + 8
 
-    def kernel(turn_ref, targets, sources, tokens_ref, memory_ref, cot_ref, sent, kept, semaphores):
+    def kernel(turn_ref, target_ref, source_ref, tokens_ref, memory_ref, cot_ref, sent, kept,
+               targets, sources, semaphores):
         mine = turn_ref[0]
-        copies = []
+        copies = [
+            pltpu.make_async_copy(target_ref, targets, semaphores.at[2, 0]),
+            pltpu.make_async_copy(source_ref, sources, semaphores.at[2, 1]),
+        ]
         for i, (row, out) in enumerate(((1 - mine, sent), (mine, kept))):
             pieces = ((tokens_ref, 0, block), (memory_ref, block, memory_block), (cot_ref, first, block))
             for j, (ref, at, count) in enumerate(pieces):
                 copies.append(pltpu.make_async_copy(ref.at[row], out.at[pl.ds(at, count), :], semaphores.at[i, j]))
         for copy in copies:
             copy.start()
+        for copy in copies[:2]:
+            copy.wait()
         for row, out in ((1 - mine, sent), (mine, kept)):
             ids = targets[pl.ds(row, 1), :].astype(F32)
             ids = jnp.concatenate([ids, jnp.zeros((1, width - block), F32)], axis=1)
@@ -284,18 +291,21 @@
             place = lax.broadcasted_iota(jnp.int32, (8, width), 0)
             found = jnp.where(place == 0, ids, jnp.where(place == 1, others, 0.0))
             out[block + memory_block : first, :] = found.astype(BF16)
-        for copy in copies:
+        for copy in copies[2:]:
             copy.wait()
 
-    anywhere = pl.BlockSpec(memory_space=pl.ANY)
     return pl.pallas_call(
         kernel,
         out_shape=[jax.ShapeDtypeStruct((first + block, width), BF16)] * 2,
-        in_specs=[SM, VM, VM, anywhere, anywhere, anywhere],
+        in_specs=[SM] + [pl.BlockSpec(memory_space=pltpu.HBM)] * 5,
         out_specs=[VM, VM],
-        scratch_shapes=[pltpu.SemaphoreType.DMA((2, 3))],
+        scratch_shapes=[
+            pltpu.VMEM(target_ids.shape, jnp.int32),
+            pltpu.VMEM(source_ids.shape, jnp.int32),
+            pltpu.SemaphoreType.DMA((3, 3)),
+        ],
         compiler_params=pltpu.CompilerParams(vmem_limit_bytes=4 << 20),
-        cost_estimate=pl.CostEstimate(flops=1 << 30, bytes_accessed=0, transcendentals=0),
+        cost_estimate=pl.CostEstimate(flops=1 << 27, bytes_accessed=0, transcendentals=0),
         name="tokens_packet",
     )(turn, target_ids, source_ids, tokens, memory, cotangent)
 
@@ -337,13 +347,13 @@
     tall = sum(sizes)
 
     def kernel(me_ref, upper, lower, *outs):
-        for i in range(4):
-            ref, at = (upper, lower)[i // 2], i % 2 * tall
+        for i in range(8):
+            ref, at = (upper, lower)[i // 4], i % 4 * tall
             for size, out in zip(sizes, outs):
                 out[i * size : (i + 1) * size, :] = ref[at : at + size, :]
                 at += size
 
-    return kernel, [((4 * size, width), BF16) for size in sizes]
+    return kernel, [((8 * size, width), BF16) for size in sizes]
 
 
 def join(arrays):
@@ -382,7 +392,7 @@
         me = me_ref[0]
         if packed:
             for i in range(3):
-                unpack(me, pieces, stride, i * narrow, narrow, scratch[i])
+                unpack(me, pieces, stride, i * narrow, narrow, scratch[i], Z_LAST)
             query_w, key_w, value_w = scratch
             biases = vector_sum(pieces, stride, 3 * narrow)
         else:
@@ -739,7 +749,7 @@
             source_key, source_value = scratch[1:3]
         else:
             source_key, source_value = pieces
-        grads = Grads(me, grad_refs, scratch[3] if packed else None, narrow)
+        grads = Grads(me, grad_refs, scratch[3] if packed else None, narrow, Z_LAST)
         memory = jnp.concatenate([t[block : block + memory_block, :] for t in tokens], axis=0)
         key_sum, value_sum = memory_key_own[...], memory_value_own[...]
         for ref in memory_received:
@@ -796,7 +806,7 @@
         in_part, query_sum, query_w_grad, own = refs[2:6]
         sends, scratch = refs[6 : 6 + parts - 1], refs[6 + parts - 1 :]
         if packed:
-            unpack(me_ref[0], pieces, 3 * narrow + 8, 0, narrow, scratch[7])
+            unpack(me_ref[0], pieces, 3 * narrow + 8, 0, narrow, scratch[7], Z_LAST)
             query_w = scratch[7]
         else:
             (query_w,) = pieces
@@ -839,7 +849,7 @@
         me = me_ref[0]
         if packed:
             for i in range(2):
-                unpack(me, pieces, 3 * narrow + 8, (1 + i) * narrow, narrow, scratch[1 + i])
+                unpack(me, pieces, 3 * narrow + 8, (1 + i) * narrow, narrow, scratch[1 + i], Z_LAST)
             key_w, value_w = scratch[1:3]
         else:
             key_w, value_w = pieces
@@ -876,7 +886,7 @@
     return kernel, outs, scratch
 
 
-def combine(arrays, splits):
+def combine(arrays, splits, micros=0.1):
     count = arrays[0].shape[0] // splits
     shape = (count,) + arrays[0].shape[1:]
 
@@ -895,7 +905,7 @@
         in_specs=[VM] * len(arrays),
         out_specs=[VM] * splits,
         compiler_params=pltpu.CompilerParams(vmem_limit_bytes=snug(arrays)),
-        cost_estimate=pl.CostEstimate(flops=2 << 30, bytes_accessed=0, transcendentals=0),
+        cost_estimate=pl.CostEstimate(flops=int(micros * 1.15e9), bytes_accessed=0, transcendentals=0),
         name="combine",
     )(*arrays)
 
@@ -965,19 +975,18 @@
                           source_key, source_value, source_output, inner_weight, outer_weight,
                           short, inner_bias.reshape(1, wide))
         first = after(first, sent)
-        first = join([first, turned_swap(first, 0)])
-        first_b = turned_swap(first, 1)
-        rest = after(rest, first)
-        rest_b = turned_swap(rest, 0)
-        first = join(after([first, first_b], rest_b))
-        rest = join(after([rest, rest_b], first_b, came, *kept_swaps))
-        first_b, rest_b = turned_swap(first, 2), turned_swap(rest, 1)
-        first_c = join(after([first, first_b], rest_b))
-        second, third = run(make_part((5 * narrow + 16, 2 * blocks * narrow), width), 1.0, "part", rest, rest_b)
-        first_d, second_b, third_b = turned_swap(first_c, 3), turned_swap(second, 2), turned_swap(third, 2)
-        second_c, third_c = join([second, second_b]), join([third, third_b])
-        first_d = after(first_d, second_c, third_c, *came_swaps)
-        second_d, third_d = turned_swap(second_c, 3), turned_swap(third_c, 3)
+        first_b, rest_b = turned_swap(first, 0, Z_LAST), turned_swap(rest, 0)
+        first, rest = join(after([first, first_b], rest_b)), join(after([rest, rest_b], first_b))
+        first_b, rest_b = turned_swap(first, 1, Z_LAST), turned_swap(rest, 1)
+        first = join(after([first, first_b], came, *kept_swaps))
+        first_b = turned_swap(first, 2, Z_LAST)
+        first_c, rest = join(after([first, first_b], rest_b)), join(after([rest, rest_b], first_b))
+        first_d, rest_b = turned_swap(first_c, 3, Z_LAST), turned_swap(rest, 2)
+        second_c, third_c = run(
+            make_part((5 * narrow + 16, 2 * blocks * narrow), width), 1.0, "part", rest, rest_b
+        )
+        first_d = after(first_d, second_c, *came_swaps)
+        second_d, third_d = turned_swap(second_c, 3), turned_swap(after(third_c, first_d), 3)
         set_self = [first_c, first_d, swap(first_c, 1, 32), swap(first_d, 1, 32)]
     else:
         full = [whole(w) for w in (query_weight, key_weight, value_weight, output_weight, source_query, source_key, source_value, source_output)]
@@ -1056,10 +1065,10 @@
     query_upper, own_upper = found[:2]
     received_upper = [swap(a, m + 1, devices) for m, a in enumerate(found[2:])]
     if packed:
-        keep, send = combine(inner_step, 2)
+        keep_cross, send = combine([grads_cross[0], cross_came], 2)
+        cross_step = [keep_cross, turned_swap(send, 3, Z_LAST)]
+        keep, send = combine(after(inner_step, keep_cross), 2)
         inner_step = [keep, turned_swap(send, 2)]
-        keep_cross, send = combine([grads_cross[0], cross_came], 2)
-        cross_step = [keep_cross, turned_swap(send, 3)]
         query[1] = after(query[1], keep, keep_cross)
     in_part, query_sum, query_w_grad, own_lower, *sends = run(
         make_self_back_lower(packed, parts, rows, block, width, narrow, len(set_query)), 11.0,
@@ -1070,9 +1079,7 @@
     if packed:
         keep, send = combine(inner_step, 2)
         inner_step = [keep, turned_swap(send, 1)]
-        keep_cross, send = combine(cross_step, 2)
-        cross_step = [keep_cross, turned_swap(send, 2)]
-        in_part = after(in_part, keep, keep_cross)
+        in_part = after(in_part, keep)
     in_own, in_send, *grads_last = run(
         make_last(packed, parts, rows, block, memory_block, width, narrow, len(set_last)), 6.0,
         "last", *set_last, *own_tokens, in_part, query_sum, query_w_grad, memory_send, own_upper,
@@ -1080,20 +1087,22 @@
     )
 
     if packed:
-        keep, send = combine([grads_last[0], swap(grads_last[1], 1, 32)], 2)
+        keep_cross, send = combine(cross_step, 2, 8.0)
+        cross_step = [keep_cross, turned_swap(send, 2, Z_LAST)]
+        keep, send = combine(after([grads_last[0], swap(grads_last[1], 1, 32)], keep_cross), 2)
         last_step = [keep, turned_swap(send, 3)]
         in_send = after(in_send, last_step[1])
+        keep, send = combine(last_step, 2)
+        last_step = [keep, turned_swap(send, 2)]
         keep_inner, send = combine(inner_step, 2)
         inner_step = [keep_inner, turned_swap(send, 0)]
         keep_cross, send = combine(cross_step, 2)
-        cross_step = [keep_cross, turned_swap(send, 1)]
-        keep, send = combine(after(last_step, keep_inner, keep_cross), 2)
-        last_step = [keep, turned_swap(send, 2)]
+        cross_step = [keep_cross, turned_swap(send, 1, Z_LAST)]
+        keep, send = combine(after(last_step, keep_cross, keep_inner), 2)
+        last_step = [keep, turned_swap(send, 1)]
         keep_cross, send = combine(cross_step, 2)
-        cross_step = [keep_cross, turned_swap(send, 0)]
+        cross_step = [keep_cross, turned_swap(send, 0, Z_LAST)]
         keep, send = combine(after(last_step, keep_cross), 2)
-        last_step = [keep, turned_swap(send, 1)]
-        keep, send = combine(last_step, 2)
         last_step = [keep, turned_swap(send, 0)]
 
         def plan(me_ref, *refs):

time: 186 us -> 207 us (1.11)
  waiting for transfers between devices: 73.8 us -> 99.9 us
  starting transfers between devices: 42.1 us -> 29.2 us
  local copies, waits for them, and re-layouts: 9.52 us -> 14.5 us
    ppermute x22 -> x21, waiting for transfers between devices: 72.7 us -> 91.6 us  [turned_swap(): lax.ppermute(array, AXES, [(i, i ^ orders[i % 2][step]) for i in range(32)])]
    ppermute x22 -> x21, starting transfers between devices: 35.3 us -> 22.2 us  [turned_swap(): lax.ppermute(array, AXES, [(i, i ^ orders[i % 2][step]) for i in range(32)])]
    ppermute x17, waiting for transfers between devices: 1.05 us -> 8.36 us  [swap(): return lax.ppermute(array, AXES, [(i, i ^ mask) for i in range(devices)])]
    unnamed x80 -> x38, local copies, waits for them, and re-layouts: 8.89 us -> 12.4 us
  transfers between devices with their start and end apart: 39 -> 38, of which waited for: 15 -> 21; matrix products, arithmetic and copies ran while one was open for 2% -> 3% of each run, Pallas kernels for 21% -> 20%
where the time goes in v7:
time: 207 us; the launch traced here: 206 us
  waiting for transfers between devices  99.9 us (48%)
  Pallas kernels  57.1 us (28%)
  starting transfers between devices  29.2 us (14%)
  local copies, waits for them, and re-layouts  14.5 us (7%)
  other arithmetic  3.92 us (2%)
    ppermute x21, waiting for transfers between devices, turned_swap(): lax.ppermute(array, AXES, [(i, i ^ orders[i % 2][step]) for i in range(32)])  91.6 us
    pallas_call x12, Pallas kernels, call(): pl.pallas_call(kernel, out_shape=[jax.ShapeDtypeStruct(s, d) for s, d in...  53.3 us
    ppermute x21, starting transfers between devices, turned_swap(): lax.ppermute(array, AXES, [(i, i ^ orders[i % 2][step]) for i in range(32)])  22.2 us
    unnamed x38, local copies, waits for them, and re-layouts  12.4 us
    ppermute x17, waiting for transfers between devices, swap(): return lax.ppermute(array, AXES, [(i, i ^ mask) for i in range(devices)])  8.36 us
    ppermute x17, starting transfers between devices, swap(): return lax.ppermute(array, AXES, [(i, i ^ mask) for i in range(devices)])  7.02 us
  transfers between devices with their start and end apart: 38, of which 21 were waited for; matrix products, arithmetic and copies ran while one was open for 3% of the time, Pallas kernels for 20%

profile of v7, /device:TPU:0, one launch (start us, length us, event | category | flops | bytes accessed | tf_op | source)
XLA Modules:
  0.0 205.9 jit_solution(5906244418874584720)
XLA Ops:
  5.4 3.0 %collective-permute-start.4 = (bf16[584,512]{1,0:T(8,128)(2,1)S(1)}, bf16[584,512]{1,0:T(8,128)(2,1)S(1)}, u32[]{:S(2)}, u32[]{:S(2)}) collective-permute-start(bf16[584,512]{1,0:T(8,128)(2,1)S(1)} %get-tuple-element.161), channel_id=1, source_target_pairs={{0,2},{1,3},{2,0},{3,1},{4,6},{5,7},{6,4},{7,5},{8,10},{9,11},{10,... | collective-permute-start | bytes 1794056 | tf_op jit(solution)/shard_map/ppermute | solution.py:161
  20.3 3.7 %collective-permute-done.1.refs_1_ = bf16[56,512]{1,0:T(8,128)(2,1)S(1)} collective-permute-done((bf16[56,512]{1,0:T(8,128)(2,1)S(1)}, bf16[56,512]{1,0:T(8,128)(2,1)S(1)}, u32[]{:S(2)}, u32[]{:S(2)}) %collective-permute-start.1) | collective-permute-done | bytes 57376 | tf_op jit(solution)/shard_map/ppermute | solution.py:169
  24.0 2.7 %collective-permute-done.refs_1_ = bf16[224,512]{1,0:T(8,128)(2,1)S(1)} collective-permute-done((bf16[224,512]{1,0:T(8,128)(2,1)S(1)}, bf16[224,512]{1,0:T(8,128)(2,1)S(1)}, u32[]{:S(2)}, u32[]{:S(2)}) %collective-permute-start) | collective-permute-done | bytes 229408 | tf_op jit(solution)/shard_map/ppermute | solution.py:169
  26.7 2.1 %collective-permute-start.2 = (bf16[448,512]{1,0:T(8,128)(2,1)S(1)}, bf16[448,512]{1,0:T(8,128)(2,1)S(1)}, u32[]{:S(2)}, u32[]{:S(2)}) collective-permute-start(bf16[448,512]{1,0:T(8,128)(2,1)S(1)} %join.5.refs_0_), channel_id=1, source_target_pairs={{0,16},{1,9},{2,18},{3,11},{4,20},{5,13},{6,22},{7,15},{8,24},{9,1... | collective-permute-start | bytes 1376264 | tf_op jit(solution)/shard_map/ppermute | solution.py:169
  30.4 3.3 %collective-permute-done.3.refs_1_ = bf16[112,512]{1,0:T(8,128)(2,1)S(1)} collective-permute-done((bf16[112,512]{1,0:T(8,128)(2,1)S(1)}, bf16[112,512]{1,0:T(8,128)(2,1)S(1)}, u32[]{:S(2)}, u32[]{:S(2)}) %collective-permute-start.3) | collective-permute-done | bytes 114720 | tf_op jit(solution)/shard_map/ppermute | solution.py:169
  35.5 10.3 %collective-permute-done.2.refs_1_ = bf16[448,512]{1,0:T(8,128)(2,1)S(1)} collective-permute-done((bf16[448,512]{1,0:T(8,128)(2,1)S(1)}, bf16[448,512]{1,0:T(8,128)(2,1)S(1)}, u32[]{:S(2)}, u32[]{:S(2)}) %collective-permute-start.2) | collective-permute-done | bytes 458784 | tf_op jit(solution)/shard_map/ppermute | solution.py:169
  47.5 11.8 %collective-permute-done.7.lower = bf16[896,512]{1,0:T(8,128)(2,1)S(1)} collective-permute-done((bf16[896,512]{1,0:T(8,128)(2,1)S(1)}, bf16[896,512]{1,0:T(8,128)(2,1)S(1)}, u32[]{:S(2)}, u32[]{:S(2)}) %collective-permute-start.7) | collective-permute-done | bytes 917536 | tf_op jit(solution)/shard_map/ppermute | solution.py:169
  59.5 2.1 %collective-permute-done.8.refs_2_ = bf16[448,512]{1,0:T(8,128)(2,1)S(1)} collective-permute-done((bf16[448,512]{1,0:T(8,128)(2,1)S(1)}, bf16[448,512]{1,0:T(8,128)(2,1)S(1)}, u32[]{:S(2)}, u32[]{:S(2)}) %collective-permute-start.8) | collective-permute-done | bytes 458784 | tf_op jit(solution)/shard_map/ppermute | solution.py:169
  67.8 17.0 %collective-permute-done.13.refs_2_ = bf16[768,512]{1,0:T(8,128)(2,1)S(1)} collective-permute-done((bf16[768,512]{1,0:T(8,128)(2,1)S(1)}, bf16[768,512]{1,0:T(8,128)(2,1)S(1)}, u32[]{:S(2)}, u32[]{:S(2)}) %collective-permute-start.13) | collective-permute-done | bytes 786464 | tf_op jit(solution)/shard_map/ppermute | solution.py:169
  84.8 8.1 %self_attention.1 = (bf16[256,512]{1,0:T(8,128)(2,1)S(1)}, bf16[256,512]{1,0:T(8,128)(2,1)S(1)}, f32[4,1,512]{2,1,0:T(1,128)S(1)}, f32[4,1,512]{2,1,0:T(1,128)S(1)}) custom-call(s32[1]{0:T(128)} %bitcast.me_ref.refs_0_, bf16[256,512]{1,0:T(8,128)(2,1)S(1)} %get-tuple-element.179.refs_0_, bf16[256,512]{1,0:T(8,128)(2,1)S(1)} %get-tuple-element.180.refs_1_, ...), custom_call_target="tpu_custom_call" | custom-call | flops 1800000000 | bytes 395776 | tf_op jit(solution)/shard_map/self_attention/pallas_call | solution.py:252
  93.5 3.2 %collective-permute-done.16.refs_3_ = bf16[768,512]{1,0:T(8,128)(2,1)S(1)} collective-permute-done((bf16[768,512]{1,0:T(8,128)(2,1)S(1)}, bf16[768,512]{1,0:T(8,128)(2,1)S(1)}, u32[]{:S(2)}, u32[]{:S(2)}) %collective-permute-start.16) | collective-permute-done | bytes 786464 | tf_op jit(solution)/shard_map/ppermute | solution.py:161
  97.9 5.4 %cross_forward.1 = (f32[512,512]{1,0:T(8,128)S(1)}, f32[512,512]{1,0:T(8,128)S(1)}, bf16[512,512]{1,0:T(8,128)(2,1)S(1)}, bf16[256,512]{1,0:T(8,128)(2,1)S(1)}, ...) custom-call(s32[1]{0:T(128)} %bitcast.me_ref.refs_0_, ...), custom_call_target="tpu_custom_call" | custom-call | flops 1350000000 | bytes 1106560 | tf_op jit(solution)/shard_map/cross_forward/pallas_call | solution.py:252
  103.3 12.5 %inner.1 = (f32[256,512]{1,0:T(8,128)S(1)}, bf16[256,512]{1,0:T(8,128)(2,1)S(1)}, f32[512,512]{1,0:T(8,128)S(1)}, f32[8,512]{1,0:T(8,128)S(1)}, bf16[16,128,512]...) custom-call(s32[1]{0:T(128)} %bitcast.me_ref.refs_0_, bf16[1024,512]{1,0:T(8,128)(2,1)S(1)} %get-tuple-element.177.refs_1_, ...), custom_call_target="tpu_custom_call" | custom-call | flops 2700000000 | bytes 1564672 | tf_op jit(solution)/shard_map/inner/pallas_call | solution.py:252
  116.4 8.2 %cross_back.1 = (f32[512,512]{1,0:T(8,128)S(1)}, f32[128,512]{1,0:T(8,128)S(1)}, f32[128,512]{1,0:T(8,128)S(1)}, f32[16,512]{1,0:T(8,128)S(1)}, bf16[512,256]{1,...) custom-call(s32[1]{0:T(128)} %bitcast.me_ref.refs_0_, ...), custom_call_target="tpu_custom_call" | custom-call | flops 2100000000 | bytes 1620608 | tf_op jit(solution)/shard_map/cross_back/pallas_call | solution.py:252
  129.2 6.3 %self_back_upper.1 = (bf16[512,256]{1,0:T(8,128)(2,1)S(1)}, f32[1024,256]{1,0:T(8,128)S(1)}, bf16[1024,256]{1,0:T(8,128)(2,1)S(1)}) custom-call(s32[1]{0:T(128)} %bitcast.me_ref.refs_0_, bf16[512,256]{1,0:T(8,128)(2,1)S(1)} %get-tuple-element.231.refs_1_, bf16[1024,256]{1,0:T(8,128)(2,1)S(1)} %get-tuple-element.181.refs_2_, ...), custom_call_target="tpu_custom_call" | custom-call | flops 1050000000 | bytes 461312 | tf_op jit(solution)/shard_map/self_back_upper/pallas_call | solution.py:252
  136.2 6.4 %collective-permute-done.20.refs_1_ = bf16[8,128,512]{2,1,0:T(8,128)(2,1)S(1)} collective-permute-done((bf16[8,128,512]{2,1,0:T(8,128)(2,1)S(1)}, bf16[8,128,512]{2,1,0:T(8,128)(2,1)S(1)}, u32[]{:S(2)}, u32[]{:S(2)}) %collective-permute-start.20) | collective-permute-done | bytes 1048608 | tf_op jit(solution)/shard_map/ppermute | solution.py:169
  144.5 6.8 %self_back_lower.1 = (f32[512,512]{1,0:T(8,128)S(1)}, f32[8,512]{1,0:T(8,128)S(1)}, bf16[512,512]{1,0:T(8,128)(2,1)S(1)}, f32[1024,256]{1,0:T(8,128)S(1)}, bf16[1024,256]{1,0:T(8,128)(2,1)S(1)}) custom-call(s32[1]{0:T(128)} %bitcast.me_ref.refs_0_, bf16[448,512]{1,0:T(8,128)(2,1)S(1)} %join.9.refs_1_, bf16[448,512]{1,0:T(8,128)(2,1)S(1)} %collective-permute-done.8.refs_2_, ...), custom_call_target="tpu_custom_call" | custom-call | flops 1650000000 | bytes 1169920 | tf_op jit(solution)/shard_map/self_back_lower/pallas_call | solution.py:252
  155.1 10.5 %collective-permute-done.27.refs_1_ = bf16[8,96,512]{2,1,0:T(8,128)(2,1)S(1)} collective-permute-done((bf16[8,96,512]{2,1,0:T(8,128)(2,1)S(1)}, bf16[8,96,512]{2,1,0:T(8,128)(2,1)S(1)}, u32[]{:S(2)}, u32[]{:S(2)}) %collective-permute-start.27) | collective-permute-done | bytes 786464 | tf_op jit(solution)/shard_map/ppermute | solution.py:169
  168.0 2.7 %collective-permute-start.30 = (bf16[2,128,512]{2,1,0:T(8,128)(2,1)}, bf16[2,128,512]{2,1,0:T(8,128)(2,1)S(1)}, u32[]{:S(2)}, u32[]{:S(2)}) collective-permute-start(bf16[2,128,512]{2,1,0:T(8,128)(2,1)} %copy-done.6), channel_id=1, source_target_pairs={{0,16},{1,9},{2,18},{3,11},{4,20},{5,13},{6,22},{7,15},{8,24},{9,1... | collective-permute-start | bytes 786440 | tf_op jit(solution)/shard_map/ppermute | solution.py:169
  170.7 10.5 %collective-permute-done.32.refs_1_ = bf16[4,96,512]{2,1,0:T(8,128)(2,1)S(1)} collective-permute-done((bf16[4,96,512]{2,1,0:T(8,128)(2,1)}, bf16[4,96,512]{2,1,0:T(8,128)(2,1)S(1)}, u32[]{:S(2)}, u32[]{:S(2)}) %collective-permute-start.32) | collective-permute-done | bytes 393248 | tf_op jit(solution)/shard_map/ppermute | solution.py:169
  181.3 2.7 %collective-permute-start.33 = (bf16[2,96,512]{2,1,0:T(8,128)(2,1)S(1)}, bf16[2,96,512]{2,1,0:T(8,128)(2,1)S(1)}, u32[]{:S(2)}, u32[]{:S(2)}) collective-permute-start(bf16[2,96,512]{2,1,0:T(8,128)(2,1)S(1)} %get-tuple-element.265), channel_id=1, source_target_pairs={{0,4},{1,3},{2,6},{3,1},{4,0},{5,7},{6,2},{7,5},{8,12},{9,11},{10,... | collective-permute-start | bytes 589832 | tf_op jit(solution)/shard_map/ppermute | solution.py:169
  189.5 4.2 %collective-permute-done.35.refs_1_ = bf16[4,56,512]{2,1,0:T(8,128)(2,1)S(1)} collective-permute-done((bf16[4,56,512]{2,1,0:T(8,128)(2,1)S(1)}, bf16[4,56,512]{2,1,0:T(8,128)(2,1)S(1)}, u32[]{:S(2)}, u32[]{:S(2)}) %collective-permute-start.35) | collective-permute-done | bytes 229408 | tf_op jit(solution)/shard_map/ppermute | solution.py:169
  195.0 4.8 %collective-permute-done.36.refs_1_ = bf16[2,56,512]{2,1,0:T(8,128)(2,1)S(1)} collective-permute-done((bf16[2,56,512]{2,1,0:T(8,128)(2,1)S(1)}, bf16[2,56,512]{2,1,0:T(8,128)(2,1)S(1)}, u32[]{:S(2)}, u32[]{:S(2)}) %collective-permute-start.36) | collective-permute-done | bytes 114720 | tf_op jit(solution)/shard_map/ppermute | solution.py:169
  200.7 3.4 %collective-permute-done.37.refs_5_ = bf16[1,56,512]{2,1,0:T(8,128)(2,1)S(1)} collective-permute-done((bf16[1,56,512]{2,1,0:T(8,128)(2,1)S(1)}, bf16[1,56,512]{2,1,0:T(8,128)(2,1)S(1)}, u32[]{:S(2)}, u32[]{:S(2)}) %collective-permute-start.37) | collective-permute-done | bytes 57376 | tf_op jit(solution)/shard_map/ppermute | solution.py:169
  (128 shorter events, 53.0 us)
Async XLA Ops:
  5.4 28.3 %collective-permute-start.4 = (bf16[584,512]{1,0:T(8,128)(2,1)S(1)}, bf16[584,512]{1,0:T(8,128)(2,1)S(1)}, u32[]{:S(2)}, u32[]{:S(2)}) collective-permute-start(bf16[584,512]{1,0:T(8,128)(2,1)S(1)} %get-tuple-element.161), channel_id=1, source_target_pairs={{0,2},{1,3},{2,0},{3,1},{4,6},{5,7},{6,4},{7,5},{8,10},{9,11},{10,... | collective-permute-start | bytes 1794056 | tf_op jit(solution)/shard_map/ppermute | solution.py:161
  8.4 25.3 %collective-permute-start.5 = (bf16[584,512]{1,0:T(8,128)(2,1)S(1)}, bf16[584,512]{1,0:T(8,128)(2,1)S(1)}, u32[]{:S(2)}, u32[]{:S(2)}) collective-permute-start(bf16[584,512]{1,0:T(8,128)(2,1)S(1)} %get-tuple-element.167.refs_5_.refs_6_), channel_id=1, source_target_pairs={{0,1},{1,0},{2,3},{3,2},{4,5},{5,4},{6,7},{7,6},{8,9},{9,8},{10,11... | collective-permute-start | bytes 1794056 | tf_op jit(solution)/shard_map/ppermute | solution.py:161
  26.7 19.1 %collective-permute-start.2 = (bf16[448,512]{1,0:T(8,128)(2,1)S(1)}, bf16[448,512]{1,0:T(8,128)(2,1)S(1)}, u32[]{:S(2)}, u32[]{:S(2)}) collective-permute-start(bf16[448,512]{1,0:T(8,128)(2,1)S(1)} %join.5.refs_0_), channel_id=1, source_target_pairs={{0,16},{1,9},{2,18},{3,11},{4,20},{5,13},{6,22},{7,15},{8,24},{9,1... | collective-permute-start | bytes 1376264 | tf_op jit(solution)/shard_map/ppermute | solution.py:169
  33.7 12.1 %collective-permute-start.6 = (bf16[224,512]{1,0:T(8,128)(2,1)S(1)}, bf16[224,512]{1,0:T(8,128)(2,1)S(1)}, u32[]{:S(2)}, u32[]{:S(2)}) collective-permute-start(bf16[224,512]{1,0:T(8,128)(2,1)S(1)} %join.7.refs_0_), channel_id=1, source_target_pairs={{0,8},{1,17},{2,10},{3,19},{4,12},{5,21},{6,14},{7,23},{8,0},{9,25... | collective-permute-start | bytes 688136 | tf_op jit(solution)/shard_map/ppermute | solution.py:169
  45.9 13.5 %collective-permute-start.7 = (bf16[896,512]{1,0:T(8,128)(2,1)S(1)}, bf16[896,512]{1,0:T(8,128)(2,1)S(1)}, u32[]{:S(2)}, u32[]{:S(2)}) collective-permute-start(bf16[896,512]{1,0:T(8,128)(2,1)S(1)} %join.8.upper), channel_id=1, source_target_pairs={{0,2},{1,5},{2,0},{3,7},{4,6},{5,1},{6,4},{7,3},{8,10},{9,13},{10,... | collective-permute-start | bytes 2752520 | tf_op jit(solution)/shard_map/ppermute | solution.py:169
  45.9 13.5 %collective-permute-start.9 = (bf16[584,512]{1,0:T(8,128)(2,1)S(1)}, bf16[584,512]{1,0:T(8,128)(2,1)S(1)}, u32[]{:S(2)}, u32[]{:S(2)}) collective-permute-start(bf16[584,512]{1,0:T(8,128)(2,1)S(1)} %collective-permute-done.4.refs_6_.refs_7_), channel_id=1, source_target_pairs={{0,1},{1,0},{2,3},{3,2},{4,5},{5,4},{6,7},{7,6},{8,9},{9,8},{10,11... | collective-permute-start | bytes 1794056 | tf_op jit(solution)/shard_map/ppermute | solution.py:161
  47.3 14.3 %collective-permute-start.8 = (bf16[448,512]{1,0:T(8,128)(2,1)S(1)}, bf16[448,512]{1,0:T(8,128)(2,1)S(1)}, u32[]{:S(2)}, u32[]{:S(2)}) collective-permute-start(bf16[448,512]{1,0:T(8,128)(2,1)S(1)} %join.9.refs_1_), channel_id=1, source_target_pairs={{0,16},{1,9},{2,18},{3,11},{4,20},{5,13},{6,22},{7,15},{8,24},{9,1... | collective-permute-start | bytes 1376264 | tf_op jit(solution)/shard_map/ppermute | solution.py:169
  61.5 31.3 %collective-permute-start.10 = (bf16[1024,512]{1,0:T(8,128)(2,1)S(1)}, bf16[1024,512]{1,0:T(8,128)(2,1)S(1)}, u32[]{:S(2)}, u32[]{:S(2)}) collective-permute-start(bf16[1024,512]{1,0:T(8,128)(2,1)S(1)} %get-tuple-element.177.refs_1_), channel_id=1, source_target_pairs={{0,4},{1,3},{2,6},{3,1},{4,0},{5,7},{6,2},{7,5},{8,12},{9,11},{10,... | collective-permute-start | bytes 3145736 | tf_op jit(solution)/shard_map/ppermute | solution.py:169
  61.9 22.8 %collective-permute-start.13 = (bf16[768,512]{1,0:T(8,128)(2,1)S(1)}, bf16[768,512]{1,0:T(8,128)(2,1)S(1)}, u32[]{:S(2)}, u32[]{:S(2)}) collective-permute-start(bf16[768,512]{1,0:T(8,128)(2,1)S(1)} %get-tuple-element.175.refs_1_), channel_id=1, source_target_pairs={{0,4},{1,3},{2,6},{3,1},{4,0},{5,7},{6,2},{7,5},{8,12},{9,11},{10,... | collective-permute-start | bytes 2359304 | tf_op jit(solution)/shard_map/ppermute | solution.py:169
  64.1 39.2 %collective-permute-start.14 = (bf16[1024,512]{1,0:T(8,128)(2,1)S(1)}, bf16[1024,512]{1,0:T(8,128)(2,1)S(1)}, u32[]{:S(2)}, u32[]{:S(2)}) collective-permute-start(bf16[1024,512]{1,0:T(8,128)(2,1)S(1)} %get-tuple-element.177.refs_1_), channel_id=1, source_target_pairs={{0,1},{1,0},{2,3},{3,2},{4,5},{5,4},{6,7},{7,6},{8,9},{9,8},{10,11... | collective-permute-start | bytes 3145736 | tf_op jit(solution)/shard_map/ppermute | solution.py:161
  92.9 10.4 %collective-permute-start.15 = (bf16[1024,512]{1,0:T(8,128)(2,1)S(1)}, bf16[1024,512]{1,0:T(8,128)(2,1)S(1)}, u32[]{:S(2)}, u32[]{:S(2)}) collective-permute-start(bf16[1024,512]{1,0:T(8,128)(2,1)S(1)} %collective-permute-done.10.refs_2_), channel_id=1, source_target_pairs={{0,1},{1,0},{2,3},{3,2},{4,5},{5,4},{6,7},{7,6},{8,9},{9,8},{10,11... | collective-permute-start | bytes 3145736 | tf_op jit(solution)/shard_map/ppermute | solution.py:161
  116.0 9.3 %collective-permute-start.18 = (bf16[256,512]{1,0:T(8,128)(2,1)S(1)}, bf16[256,512]{1,0:T(8,128)(2,1)S(1)}, u32[]{:S(2)}, u32[]{:S(2)}) collective-permute-start(bf16[256,512]{1,0:T(8,128)(2,1)S(1)} %get-tuple-element.195), channel_id=1, source_target_pairs={{0,2},{1,3},{2,0},{3,1},{4,6},{5,7},{6,4},{7,5},{8,10},{9,11},{10,... | collective-permute-start | bytes 786440 | tf_op jit(solution)/shard_map/ppermute | solution.py:161
  127.8 14.8 %collective-permute-start.20 = (bf16[8,128,512]{2,1,0:T(8,128)(2,1)S(1)}, bf16[8,128,512]{2,1,0:T(8,128)(2,1)S(1)}, u32[]{:S(2)}, u32[]{:S(2)}) collective-permute-start(bf16[8,128,512]{2,1,0:T(8,128)(2,1)S(1)} %get-tuple-element.200), channel_id=1, source_target_pairs={{0,4},{1,3},{2,6},{3,1},{4,0},{5,7},{6,2},{7,5},{8,12},{9,11},{10,... | collective-permute-start | bytes 3145736 | tf_op jit(solution)/shard_map/ppermute | solution.py:169
  135.5 16.7 %collective-permute-start.24 = (bf16[1024,256]{1,0:T(8,128)(2,1)S(1)}, bf16[1024,256]{1,0:T(8,128)(2,1)S(1)}, u32[]{:S(2)}, u32[]{:S(2)}) collective-permute-start(bf16[1024,256]{1,0:T(8,128)(2,1)S(1)} %get-tuple-element.247), channel_id=1, source_target_pairs={{0,1},{1,0},{2,3},{3,2},{4,5},{5,4},{6,7},{7,6},{8,9},{9,8},{10,11... | collective-permute-start | bytes 1572872 | tf_op jit(solution)/shard_map/ppermute | solution.py:161
  142.8 9.2 %collective-permute-start.23 = (bf16[4,128,512]{2,1,0:T(8,128)(2,1)S(1)}, bf16[4,128,512]{2,1,0:T(8,128)(2,1)S(1)}, u32[]{:S(2)}, u32[]{:S(2)}) collective-permute-start(bf16[4,128,512]{2,1,0:T(8,128)(2,1)S(1)} %get-tuple-element.239), channel_id=1, source_target_pairs={{0,2},{1,5},{2,0},{3,7},{4,6},{5,1},{6,4},{7,3},{8,10},{9,13},{10,... | collective-permute-start | bytes 1572872 | tf_op jit(solution)/shard_map/ppermute | solution.py:169
  144.5 21.1 %collective-permute-start.27 = (bf16[8,96,512]{2,1,0:T(8,128)(2,1)S(1)}, bf16[8,96,512]{2,1,0:T(8,128)(2,1)S(1)}, u32[]{:S(2)}, u32[]{:S(2)}) collective-permute-start(bf16[8,96,512]{2,1,0:T(8,128)(2,1)S(1)} %get-tuple-element.253), channel_id=1, source_target_pairs={{0,16},{1,9},{2,18},{3,11},{4,20},{5,13},{6,22},{7,15},{8,24},{9,1... | collective-permute-start | bytes 2359304 | tf_op jit(solution)/shard_map/ppermute | solution.py:169
  154.9 11.5 %collective-permute-start.26 = (bf16[16,56,512]{2,1,0:T(8,128)(2,1)S(1)}, bf16[16,56,512]{2,1,0:T(8,128)(2,1)S(1)}, u32[]{:S(2)}, u32[]{:S(2)}) collective-permute-start(bf16[16,56,512]{2,1,0:T(8,128)(2,1)S(1)} %get-tuple-element.252), channel_id=1, source_target_pairs={{0,1},{1,0},{2,3},{3,2},{4,5},{5,4},{6,7},{7,6},{8,9},{9,8},{10,11... | collective-permute-start | bytes 2752520 | tf_op jit(solution)/shard_map/ppermute | solution.py:161
  167.4 16.6 %collective-permute-start.28 = (bf16[8,56,512]{2,1,0:T(8,128)(2,1)}, bf16[8,56,512]{2,1,0:T(8,128)(2,1)S(1)}, u32[]{:S(2)}, u32[]{:S(2)}) collective-permute-start(bf16[8,56,512]{2,1,0:T(8,128)(2,1)} %get-tuple-element.257), channel_id=1, source_target_pairs={{0,4},{1,3},{2,6},{3,1},{4,0},{5,7},{6,2},{7,5},{8,12},{9,11},{10,... | collective-permute-start | bytes 1376264 | tf_op jit(solution)/shard_map/ppermute | solution.py:169
  168.0 13.2 %collective-permute-start.32 = (bf16[4,96,512]{2,1,0:T(8,128)(2,1)}, bf16[4,96,512]{2,1,0:T(8,128)(2,1)S(1)}, u32[]{:S(2)}, u32[]{:S(2)}) collective-permute-start(bf16[4,96,512]{2,1,0:T(8,128)(2,1)} %get-tuple-element.263), channel_id=1, source_target_pairs={{0,8},{1,17},{2,10},{3,19},{4,12},{5,21},{6,14},{7,23},{8,0},{9,25... | collective-permute-start | bytes 1179656 | tf_op jit(solution)/shard_map/ppermute | solution.py:169
  168.0 20.3 %collective-permute-start.30 = (bf16[2,128,512]{2,1,0:T(8,128)(2,1)}, bf16[2,128,512]{2,1,0:T(8,128)(2,1)S(1)}, u32[]{:S(2)}, u32[]{:S(2)}) collective-permute-start(bf16[2,128,512]{2,1,0:T(8,128)(2,1)} %copy-done.6), channel_id=1, source_target_pairs={{0,16},{1,9},{2,18},{3,11},{4,20},{5,13},{6,22},{7,15},{8,24},{9,1... | collective-permute-start | bytes 786440 | tf_op jit(solution)/shard_map/ppermute | solution.py:169
  184.0 9.9 %collective-permute-start.29 = (bf16[320,512]{1,0:T(8,128)(2,1)}, bf16[320,512]{1,0:T(8,128)(2,1)S(1)}, u32[]{:S(2)}, u32[]{:S(2)}) collective-permute-start(bf16[320,512]{1,0:T(8,128)(2,1)} %copy-done.5), channel_id=1, source_target_pairs={{0,2},{1,3},{2,0},{3,1},{4,6},{5,7},{6,4},{7,5},{8,10},{9,11},{10,... | collective-permute-start | bytes 983048 | tf_op jit(solution)/shard_map/ppermute | solution.py:161
  184.1 9.6 %collective-permute-start.35 = (bf16[4,56,512]{2,1,0:T(8,128)(2,1)S(1)}, bf16[4,56,512]{2,1,0:T(8,128)(2,1)S(1)}, u32[]{:S(2)}, u32[]{:S(2)}) collective-permute-start(bf16[4,56,512]{2,1,0:T(8,128)(2,1)S(1)} %get-tuple-element.270), channel_id=1, source_target_pairs={{0,2},{1,5},{2,0},{3,7},{4,6},{5,1},{6,4},{7,3},{8,10},{9,13},{10,... | collective-permute-start | bytes 688136 | tf_op jit(solution)/shard_map/ppermute | solution.py:169
  188.3 12.4 %collective-permute-start.31 = (bf16[1,128,512]{2,1,0:T(8,128)(2,1)S(1)}, bf16[1,128,512]{2,1,0:T(8,128)(2,1)S(1)}, u32[]{:S(2)}, u32[]{:S(2)}) collective-permute-start(bf16[1,128,512]{2,1,0:T(8,128)(2,1)S(1)} %get-tuple-element.262), channel_id=1, source_target_pairs={{0,8},{1,17},{2,10},{3,19},{4,12},{5,21},{6,14},{7,23},{8,0},{9,25... | collective-permute-start | bytes 393224 | tf_op jit(solution)/shard_map/ppermute | solution.py:169
  188.7 12.0 %collective-permute-start.34 = (bf16[1,96,512]{2,1,0:T(8,128)(2,1)S(1)}, bf16[1,96,512]{2,1,0:T(8,128)(2,1)S(1)}, u32[]{:S(2)}, u32[]{:S(2)}) collective-permute-start(bf16[1,96,512]{2,1,0:T(8,128)(2,1)S(1)} %get-tuple-element.267), channel_id=1, source_target_pairs={{0,2},{1,5},{2,0},{3,7},{4,6},{5,1},{6,4},{7,3},{8,10},{9,13},{10,... | collective-permute-start | bytes 294920 | tf_op jit(solution)/shard_map/ppermute | solution.py:169
  (33 other events, 117.6 us)

commit v8 on v6

--- a/solution.py
+++ b/solution.py
@@ -256,7 +256,7 @@
         scratch_shapes=[pltpu.VMEM(s, d) for s, d in scratch],
         compiler_params=pltpu.CompilerParams(vmem_limit_bytes=min(need + (room << 20), 58 << 20)),
         cost_estimate=pl.CostEstimate(
-            flops=int(micros * 1.15e9), bytes_accessed=moved, transcendentals=0
+            flops=1, bytes_accessed=1, transcendentals=0
         ),
         name=name,
     )(*args)
@@ -267,16 +267,11 @@
     memory_block = memory.shape[1]
     first = block + memory_block + 8
 
-    def kernel(turn_ref, targets, sources, tokens_ref, memory_ref, cot_ref, sent, kept, semaphores):
+    def kernel(turn_ref, targets, sources, tokens_ref, memory_ref, cot_ref, sent, kept):
         mine = turn_ref[0]
-        copies = []
-        for i, (row, out) in enumerate(((1 - mine, sent), (mine, kept))):
-            pieces = ((tokens_ref, 0, block), (memory_ref, block, memory_block), (cot_ref, first, block))
-            for j, (ref, at, count) in enumerate(pieces):
-                copies.append(pltpu.make_async_copy(ref.at[row], out.at[pl.ds(at, count), :], semaphores.at[i, j]))
-        for copy in copies:
-            copy.start()
         for row, out in ((1 - mine, sent), (mine, kept)):
+            out[:block, :] = tokens_ref[row]
+            out[block : block + memory_block, :] = memory_ref[row]
             ids = targets[pl.ds(row, 1), :].astype(F32)
             ids = jnp.concatenate([ids, jnp.zeros((1, width - block), F32)], axis=1)
             others = sources[pl.ds(row, 1), :].astype(F32)
@@ -284,20 +279,11 @@
             place = lax.broadcasted_iota(jnp.int32, (8, width), 0)
             found = jnp.where(place == 0, ids, jnp.where(place == 1, others, 0.0))
             out[block + memory_block : first, :] = found.astype(BF16)
-        for copy in copies:
-            copy.wait()
-
-    anywhere = pl.BlockSpec(memory_space=pl.ANY)
-    return pl.pallas_call(
-        kernel,
-        out_shape=[jax.ShapeDtypeStruct((first + block, width), BF16)] * 2,
-        in_specs=[SM, VM, VM, anywhere, anywhere, anywhere],
-        out_specs=[VM, VM],
-        scratch_shapes=[pltpu.SemaphoreType.DMA((2, 3))],
-        compiler_params=pltpu.CompilerParams(vmem_limit_bytes=4 << 20),
-        cost_estimate=pl.CostEstimate(flops=1 << 30, bytes_accessed=0, transcendentals=0),
-        name="tokens_packet",
-    )(turn, target_ids, source_ids, tokens, memory, cotangent)
+            out[first:, :] = cot_ref[row]
+
+    shape = (first + block, width)
+    return call(kernel, [(shape, BF16)] * 2, (turn, target_ids, source_ids, tokens, memory, cotangent),
+                [], 1.0, "tokens_packet", 58)
 
 
 def placed(me, parts, width):
@@ -713,9 +699,8 @@
     own[:share, :] = key_grad[:share, :]
     own[share:, :] = value_grad[:share, :]
     for i, send in enumerate(sends):
-        here = slice((i + 1) * share, (i + 2) * share)
-        send[:share, :] = key_grad[here, :].astype(BF16)
-        send[share:, :] = value_grad[here, :].astype(BF16)
+        here = slice((i // 2 + 1) * share, (i // 2 + 2) * share)
+        send[...] = (key_grad, value_grad)[i % 2][here, :].astype(BF16)
 
 
 def make_memory_back(packed, parts, rows, block, memory_block, width, narrow, n_pieces):
@@ -774,12 +759,12 @@
 
     def kernel(*refs):
         operands, (query_grad, own), refs = refs[1:9], refs[9:11], refs[11:]
-        sends, scratch = refs[: parts - 1], refs[parts - 1 :]
+        sends, scratch = refs[: 2 * parts - 2], refs[2 * parts - 2 :]
         attention_back_half(operands, share, scratch)
         query_grad[...] = scratch[4][...].T.astype(BF16)
         give_half(share, scratch, own, sends)
 
-    outs = [((share, half), BF16), ((2 * share, half), F32)] + [((2 * share, half), BF16)] * (parts - 1)
+    outs = [((share, half), BF16), ((2 * share, half), F32)] + [((share, half), BF16)] * (2 * parts - 2)
     return kernel, outs, half_scratch(share, length, half)
 
 
@@ -794,7 +779,7 @@
         operands, refs = refs[:8], refs[8:]
         back1, query_upper = refs[:2]
         in_part, query_sum, query_w_grad, own = refs[2:6]
-        sends, scratch = refs[6 : 6 + parts - 1], refs[6 + parts - 1 :]
+        sends, scratch = refs[6 : 4 + 2 * parts], refs[4 + 2 * parts :]
         if packed:
             unpack(me_ref[0], pieces, 3 * narrow + 8, 0, narrow, scratch[7])
             query_w = scratch[7]
@@ -814,7 +799,7 @@
         ((width, width), BF16 if packed else F32),
         ((2 * share, half), F32),
     ]
-    outs += [((2 * share, half), BF16)] * (parts - 1)
+    outs += [((share, half), BF16)] * (2 * parts - 2)
     scratch = half_scratch(share, length, half)
     if packed:
         scratch += [((width, width), BF16)]
@@ -830,8 +815,8 @@
         tokens, refs = refs[:rows], refs[rows:]
         in_part, query_sum, query_w_grad, memory_send = refs[:4]
         owns, refs = refs[4:6], refs[6:]
-        received = [refs[: parts - 1], refs[parts - 1 : 2 * (parts - 1)]]
-        refs = refs[2 * (parts - 1) :]
+        received = [refs[: 2 * parts - 2], refs[2 * parts - 2 : 4 * parts - 4]]
+        refs = refs[4 * parts - 4 :]
         in_own, in_send = refs[:2]
         n_grads = 2 if packed else 3
         grad_refs, scratch = refs[2 : 2 + n_grads], refs[2 + n_grads :]
@@ -849,8 +834,8 @@
         lows = []
         for own, others in zip(owns, received):
             found = own[...]
-            for ref in others:
-                found = found + ref[...].astype(F32)
+            for key, value in zip(others[::2], others[1::2]):
+                found = found + jnp.concatenate([key[...], value[...]], axis=0).astype(F32)
             lows.append(found.astype(BF16))
         key_low = jnp.concatenate([low[:share, :] for low in lows], axis=1)
         value_low = jnp.concatenate([low[share:, :] for low in lows], axis=1)
@@ -876,7 +861,7 @@
     return kernel, outs, scratch
 
 
-def combine(arrays, splits):
+def combine(arrays, splits, micros=0.1):
     count = arrays[0].shape[0] // splits
     shape = (count,) + arrays[0].shape[1:]
 
@@ -895,7 +880,7 @@
         in_specs=[VM] * len(arrays),
         out_specs=[VM] * splits,
         compiler_params=pltpu.CompilerParams(vmem_limit_bytes=snug(arrays)),
-        cost_estimate=pl.CostEstimate(flops=2 << 30, bytes_accessed=0, transcendentals=0),
+        cost_estimate=pl.CostEstimate(flops=int(micros * 1.15e9), bytes_accessed=0, transcendentals=0),
         name="combine",
     )(*arrays)
 
@@ -937,9 +922,9 @@
     turn = lax.rem(lax.div(me, parts), rows)
     narrow, wide = width // devices, hidden // devices
 
-    def run(made, micros, name, *args):
+    def run(made, micros, name, *args, room=10):
         kernel, outs, *scratch = made
-        return call(kernel, outs, (me_array,) + args, scratch[0] if scratch else [], micros, name)
+        return call(kernel, outs, (me_array,) + args, scratch[0] if scratch else [], micros, name, room)
 
     short = jnp.stack([query_bias, value_bias, output_bias, attention_gain, attention_shift,
                        source_query_bias, source_value_bias, source_output_bias, source_gain,
@@ -963,7 +948,7 @@
         first, rest = run(make_weights_packet(narrow, width, blocks), 1.0, "weights_packet",
                           query_weight, key_weight, value_weight, output_weight, source_query,
                           source_key, source_value, source_output, inner_weight, outer_weight,
-                          short, inner_bias.reshape(1, wide))
+                          short, inner_bias.reshape(1, wide), room=58)
         first = after(first, sent)
         first = join([first, turned_swap(first, 0)])
         first_b = turned_swap(first, 1)
@@ -972,12 +957,13 @@
         first = join(after([first, first_b], rest_b))
         rest = join(after([rest, rest_b], first_b, came, *kept_swaps))
         first_b, rest_b = turned_swap(first, 2), turned_swap(rest, 1)
-        first_c = join(after([first, first_b], rest_b))
+        first_c = join([first, first_b])
+        first_d = turned_swap(first_c, 3)
         second, third = run(make_part((5 * narrow + 16, 2 * blocks * narrow), width), 1.0, "part", rest, rest_b)
-        first_d, second_b, third_b = turned_swap(first_c, 3), turned_swap(second, 2), turned_swap(third, 2)
-        second_c, third_c = join([second, second_b]), join([third, third_b])
-        first_d = after(first_d, second_c, third_c, *came_swaps)
-        second_d, third_d = turned_swap(second_c, 3), turned_swap(third_c, 3)
+        second_b, third_b = turned_swap(second, 2), turned_swap(third, 2)
+        second_c = join([second, second_b])
+        second_d = turned_swap(second_c, 3)
+        first_d = after(first_d, second_c, *came_swaps)
         set_self = [first_c, first_d, swap(first_c, 1, 32), swap(first_d, 1, 32)]
     else:
         full = [whole(w) for w in (query_weight, key_weight, value_weight, output_weight, source_query, source_key, source_value, source_output)]
@@ -1004,8 +990,11 @@
     row_memory, ids, memory_ids = found[10:]
     query_t = list(query_t)
     if packed:
+        third_c = join(after([third, third_b], query_t[0]))
+        third_d = turned_swap(third_c, 3)
+        second_d = after(second_d, query_t[0])
         set_cross = [second_c, second_d, swap(second_c, 1, 32), swap(second_d, 1, 32)]
-        query_t[0] = after(query_t[0], second_d)
+        query_t[0] = after(query_t[0], third_c, second_d)
         set_back, set_query, set_last, set_memory = set_cross, set_self, set_self, set_cross
     else:
         set_back, set_query, set_last, set_memory = [full[3], full[4], full[7]], full[:1], full[1:3], full[5:7]
@@ -1017,7 +1006,6 @@
     if packed:
         third_d = after(third_d, mixtures[0])
         set_inner = [third_c, third_d, swap(third_c, 1, 32), swap(third_d, 1, 32)]
-        mixtures = [after(mixtures[0], third_d), mixtures[1]]
     first_sum, second_sum, cross_query, memory_keys, memory_values, cross_t, cross_logs, vectors = run(
         make_cross_forward(packed, rows, block, parts * memory_share, width, narrow, len(set_cross)),
         9.0, "cross_forward", *set_cross, *own_tokens, row_memory, ids, memory_ids, *mixtures,
@@ -1038,9 +1026,9 @@
     grads_early = found[10 + parts - 1 :]
     query = list(query)
     if packed:
-        keep, send = combine([grads_inner[0], swap(grads_inner[1], 1, 32)], 2)
+        keep, send = combine(after([grads_inner[0], swap(grads_inner[1], 1, 32)], back1, out_came), 2)
         inner_step = [keep, turned_swap(send, 3)]
-        memory_key_own = after(memory_key_own, keep, out_came)
+        memory_key_own = after(memory_key_own, keep)
     memory_own, memory_send, *grads_cross = run(
         make_memory_back(packed, parts, rows, block, memory_block, width, narrow, len(set_memory)),
         2.0, "memory_back", *set_memory, *own_tokens, memory_key_own, memory_value_own, sums_cross,
@@ -1054,11 +1042,11 @@
         values[0], slope[0], slope_t[0], logs[0], deltas[0], ids,
     )
     query_upper, own_upper = found[:2]
-    received_upper = [swap(a, m + 1, devices) for m, a in enumerate(found[2:])]
-    if packed:
-        keep, send = combine(inner_step, 2)
+    received_upper = [swap(a, m // 2 + 1, devices) for m, a in enumerate(found[2:])]
+    if packed:
+        keep, send = combine(after(inner_step, query_upper), 2, 8.0)
         inner_step = [keep, turned_swap(send, 2)]
-        keep_cross, send = combine([grads_cross[0], cross_came], 2)
+        keep_cross, send = combine(after([grads_cross[0], cross_came], keep), 2)
         cross_step = [keep_cross, turned_swap(send, 3)]
         query[1] = after(query[1], keep, keep_cross)
     in_part, query_sum, query_w_grad, own_lower, *sends = run(
@@ -1066,13 +1054,7 @@
         "self_back_lower", *set_query, *own_tokens, query[1], keys[1], values[1], slope[1],
         slope_t[1], logs[1], deltas[1], ids, back1, query_upper,
     )
-    received_lower = [swap(a, m + 1, devices) for m, a in enumerate(sends)]
-    if packed:
-        keep, send = combine(inner_step, 2)
-        inner_step = [keep, turned_swap(send, 1)]
-        keep_cross, send = combine(cross_step, 2)
-        cross_step = [keep_cross, turned_swap(send, 2)]
-        in_part = after(in_part, keep, keep_cross)
+    received_lower = [swap(a, m // 2 + 1, devices) for m, a in enumerate(sends)]
     in_own, in_send, *grads_last = run(
         make_last(packed, parts, rows, block, memory_block, width, narrow, len(set_last)), 6.0,
         "last", *set_last, *own_tokens, in_part, query_sum, query_w_grad, memory_send, own_upper,
@@ -1080,6 +1062,11 @@
     )
 
     if packed:
+        keep_inner, send = combine(after(inner_step, in_own), 2)
+        inner_step = [keep_inner, turned_swap(send, 1)]
+        keep_cross, send = combine(after(cross_step, keep_inner), 2)
+        cross_step = [keep_cross, turned_swap(send, 2)]
+        grads_last[1] = after(grads_last[1], keep_cross)
         keep, send = combine([grads_last[0], swap(grads_last[1], 1, 32)], 2)
         last_step = [keep, turned_swap(send, 3)]
         in_send = after(in_send, last_step[1])

time: 186 us -> 198 us (1.065)
  waiting for transfers between devices: 73.8 us -> 80.6 us
  Pallas kernels: 55.6 us -> 61.8 us
  local copies, waits for them, and re-layouts: 9.52 us -> 5.24 us
  starting transfers between devices: 42.1 us -> 45.4 us
    ppermute x17 -> x19, waiting for transfers between devices: 1.05 us -> 11.6 us  [swap(): return lax.ppermute(array, AXES, [(i, i ^ mask) for i in range(devices)])]
    unnamed x80 -> x14, local copies, waits for them, and re-layouts: 8.89 us -> 1.99 us
    ppermute x22, starting transfers between devices: 35.3 us -> 40 us  [turned_swap(): lax.ppermute(array, AXES, [(i, i ^ ORDERS[i % 2][step]) for i in range(32)])]
    pallas_call x12 -> x13, Pallas kernels: 53 us -> 57.6 us  [call(): pl.pallas_call(kernel, out_shape=[jax.ShapeDtypeStruct(s, d) for s, d in...]
    ppermute x22, waiting for transfers between devices: 72.7 us -> 69 us  [turned_swap(): lax.ppermute(array, AXES, [(i, i ^ ORDERS[i % 2][step]) for i in range(32)])]
    another operation x1, local copies, waits for them, and re-layouts: 0.07 us -> 2.68 us  [per_device(): jnp.stack([query_bias, value_bias, output_bias, attention_gain, attention...]
    pallas_call x12, Pallas kernels: 2 us -> 3.99 us  [combine(): pl.pallas_call(kernel, out_shape=[jax.ShapeDtypeStruct(shape, BF16)] * sp...]
    ppermute x17 -> x19, starting transfers between devices: 6.8 us -> 5.44 us  [swap(): return lax.ppermute(array, AXES, [(i, i ^ mask) for i in range(devices)])]
  transfers between devices with their start and end apart: 39 -> 41, of which waited for: 15 -> 22; matrix products, arithmetic and copies ran while one was open for 2% -> 3% of each run, Pallas kernels for 21% -> 22%
where the time goes in v8:
time: 198 us; the launch traced here: 197 us
  waiting for transfers between devices  80.6 us (41%)
  Pallas kernels  61.8 us (31%)
  starting transfers between devices  45.4 us (23%)
  local copies, waits for them, and re-layouts  5.24 us (3%)
  other arithmetic  2.97 us (2%)
    ppermute x22, waiting for transfers between devices, turned_swap(): lax.ppermute(array, AXES, [(i, i ^ ORDERS[i % 2][step]) for i in range(32)])  69 us
    pallas_call x13, Pallas kernels, call(): pl.pallas_call(kernel, out_shape=[jax.ShapeDtypeStruct(s, d) for s, d in...  57.6 us
    ppermute x22, starting transfers between devices, turned_swap(): lax.ppermute(array, AXES, [(i, i ^ ORDERS[i % 2][step]) for i in range(32)])  40 us
    ppermute x19, waiting for transfers between devices, swap(): return lax.ppermute(array, AXES, [(i, i ^ mask) for i in range(devices)])  11.6 us
    ppermute x19, starting transfers between devices, swap(): return lax.ppermute(array, AXES, [(i, i ^ mask) for i in range(devices)])  5.44 us
    pallas_call x12, Pallas kernels, combine(): pl.pallas_call(kernel, out_shape=[jax.ShapeDtypeStruct(shape, BF16)] * sp...  3.99 us
  transfers between devices with their start and end apart: 41, of which 22 were waited for; matrix products, arithmetic and copies ran while one was open for 3% of the time, Pallas kernels for 22%

profile of v8, /device:TPU:0, one launch (start us, length us, event | category | flops | bytes accessed | tf_op | source)
XLA Modules:
  0.0 197.2 jit_solution(7590234314584259541)
XLA Ops:
  3.1 3.0 %collective-permute-start.3 = (bf16[584,512]{1,0:T(8,128)(2,1)}, bf16[584,512]{1,0:T(8,128)(2,1)S(1)}, u32[]{:S(2)}, u32[]{:S(2)}) collective-permute-start(bf16[584,512]{1,0:T(8,128)(2,1)} %get-tuple-element.165), channel_id=1, source_target_pairs={{0,2},{1,3},{2,0},{3,1},{4,6},{5,7},{6,4},{7,5},{8,10},{9,11},{10,... | collective-permute-start | bytes 1794056 | tf_op jit(solution)/shard_map/ppermute | solution.py:161
  6.1 2.7 %stack.106.refs_10_ = bf16[13,16]{1,0:T(8,128)(2,1)} concatenate(bf16[1,16]{1,0:T(2,128)(2,1)} %bitcast.63, bf16[1,16]{1,0:T(2,128)(2,1)} %bitcast.64, bf16[1,16]{1,0:T(2,128)(2,1)} %bitcast.65, bf16[1,16]{1,0:T(2,128)(2,1)} %bitcast.66, bf16[1,16]{1,0:T(2,128)(2,1)} %bitcast.67, bf16[1,16]{1,0:T(2,128)(2,1)} %bitcast.68, bf16[1,16]{1,0:T(2,128)(2,1)} %bitcast.69, ...), dimensions={0} | concatenate | bytes 832 | tf_op jit(solution)/shard_map/stack | solution.py:929
  12.1 3.4 %collective-permute-done.refs_1_ = bf16[56,512]{1,0:T(8,128)(2,1)S(1)} collective-permute-done((bf16[56,512]{1,0:T(8,128)(2,1)}, bf16[56,512]{1,0:T(8,128)(2,1)S(1)}, u32[]{:S(2)}, u32[]{:S(2)}) %collective-permute-start) | collective-permute-done | bytes 57376 | tf_op jit(solution)/shard_map/ppermute | solution.py:168
  17.6 2.6 %collective-permute-start.2 = (bf16[112,512]{1,0:T(8,128)(2,1)S(1)}, bf16[112,512]{1,0:T(8,128)(2,1)S(1)}, u32[]{:S(2)}, u32[]{:S(2)}) collective-permute-start(bf16[112,512]{1,0:T(8,128)(2,1)S(1)} %join.6.refs_0_), channel_id=1, source_target_pairs={{0,16},{1,9},{2,18},{3,11},{4,20},{5,13},{6,22},{7,15},{8,24},{9,1... | collective-permute-start | bytes 344072 | tf_op jit(solution)/shard_map/ppermute | solution.py:168
  20.2 5.9 %collective-permute-done.2.refs_1_ = bf16[112,512]{1,0:T(8,128)(2,1)S(1)} collective-permute-done((bf16[112,512]{1,0:T(8,128)(2,1)S(1)}, bf16[112,512]{1,0:T(8,128)(2,1)S(1)}, u32[]{:S(2)}, u32[]{:S(2)}) %collective-permute-start.2) | collective-permute-done | bytes 114720 | tf_op jit(solution)/shard_map/ppermute | solution.py:168
  30.9 5.5 %collective-permute-done.7.refs_1_ = bf16[224,512]{1,0:T(8,128)(2,1)S(1)} collective-permute-done((bf16[224,512]{1,0:T(8,128)(2,1)S(1)}, bf16[224,512]{1,0:T(8,128)(2,1)S(1)}, u32[]{:S(2)}, u32[]{:S(2)}) %collective-permute-start.7) | collective-permute-done | bytes 229408 | tf_op jit(solution)/shard_map/ppermute | solution.py:168
  38.0 3.2 %collective-permute-done.5.lower = bf16[448,512]{1,0:T(8,128)(2,1)S(1)} collective-permute-done((bf16[448,512]{1,0:T(8,128)(2,1)S(1)}, bf16[448,512]{1,0:T(8,128)(2,1)S(1)}, u32[]{:S(2)}, u32[]{:S(2)}) %collective-permute-start.5) | collective-permute-done | bytes 458784 | tf_op jit(solution)/shard_map/ppermute | solution.py:168
  43.4 5.7 %collective-permute-done.9.refs_1_ = bf16[384,512]{1,0:T(8,128)(2,1)S(1)} collective-permute-done((bf16[384,512]{1,0:T(8,128)(2,1)S(1)}, bf16[384,512]{1,0:T(8,128)(2,1)S(1)}, u32[]{:S(2)}, u32[]{:S(2)}) %collective-permute-start.9) | collective-permute-done | bytes 393248 | tf_op jit(solution)/shard_map/ppermute | solution.py:168
  57.0 21.2 %collective-permute-done.14.refs_2_ = bf16[768,512]{1,0:T(8,128)(2,1)S(1)} collective-permute-done((bf16[768,512]{1,0:T(8,128)(2,1)S(1)}, bf16[768,512]{1,0:T(8,128)(2,1)S(1)}, u32[]{:S(2)}, u32[]{:S(2)}) %collective-permute-start.14) | collective-permute-done | bytes 786464 | tf_op jit(solution)/shard_map/ppermute | solution.py:168
  78.2 8.3 %self_attention.1 = (bf16[256,512]{1,0:T(8,128)(2,1)S(1)}, bf16[256,512]{1,0:T(8,128)(2,1)S(1)}, f32[4,1,512]{2,1,0:T(1,128)S(1)}, f32[4,1,512]{2,1,0:T(1,128)S(1)}) custom-call(s32[1]{0:T(128)} %bitcast.me_ref.refs_0_, bf16[256,512]{1,0:T(8,128)(2,1)S(1)} %get-tuple-element.180.refs_0_, bf16[256,512]{1,0:T(8,128)(2,1)S(1)} %get-tuple-element.181.refs_1_, ...), custom_call_target="tpu_custom_call" | custom-call | flops 1 | bytes 1 | tf_op jit(solution)/shard_map/self_attention/pallas_call | solution.py:251
  87.1 3.2 %collective-permute-done.17.refs_3_ = bf16[768,512]{1,0:T(8,128)(2,1)S(1)} collective-permute-done((bf16[768,512]{1,0:T(8,128)(2,1)S(1)}, bf16[768,512]{1,0:T(8,128)(2,1)S(1)}, u32[]{:S(2)}, u32[]{:S(2)}) %collective-permute-start.17) | collective-permute-done | bytes 786464 | tf_op jit(solution)/shard_map/ppermute | solution.py:161
  91.4 5.4 %cross_forward.1 = (f32[512,512]{1,0:T(8,128)S(1)}, f32[512,512]{1,0:T(8,128)S(1)}, bf16[512,512]{1,0:T(8,128)(2,1)S(1)}, bf16[256,512]{1,0:T(8,128)(2,1)S(1)}, ...) custom-call(s32[1]{0:T(128)} %bitcast.me_ref.refs_0_, ...), custom_call_target="tpu_custom_call" | custom-call | flops 1 | bytes 1 | tf_op jit(solution)/shard_map/cross_forward/pallas_call | solution.py:251
  96.9 12.4 %inner.1 = (f32[256,512]{1,0:T(8,128)S(1)}, bf16[256,512]{1,0:T(8,128)(2,1)S(1)}, f32[512,512]{1,0:T(8,128)S(1)}, f32[8,512]{1,0:T(8,128)S(1)}, bf16[16,128,512]...) custom-call(s32[1]{0:T(128)} %bitcast.me_ref.refs_0_, bf16[1024,512]{1,0:T(8,128)(2,1)S(1)} %join.11.refs_1_, ...), custom_call_target="tpu_custom_call" | custom-call | flops 1 | bytes 1 | tf_op jit(solution)/shard_map/inner/pallas_call | solution.py:251
  109.5 8.4 %cross_back.1 = (f32[512,512]{1,0:T(8,128)S(1)}, f32[128,512]{1,0:T(8,128)S(1)}, f32[128,512]{1,0:T(8,128)S(1)}, f32[16,512]{1,0:T(8,128)S(1)}, bf16[512,256]{1,...) custom-call(s32[1]{0:T(128)} %bitcast.me_ref.refs_0_, ...), custom_call_target="tpu_custom_call" | custom-call | flops 1 | bytes 1 | tf_op jit(solution)/shard_map/cross_back/pallas_call | solution.py:251
  123.6 6.1 %self_back_upper.1 = (bf16[512,256]{1,0:T(8,128)(2,1)S(1)}, f32[1024,256]{1,0:T(8,128)S(1)}, bf16[512,256]{1,0:T(8,128)(2,1)S(1)}, bf16[512,256]{1,0:T(8,128)(2,1)S(1)}) custom-call(s32[1]{0:T(128)} %bitcast.me_ref.refs_0_, bf16[512,256]{1,0:T(8,128)(2,1)S(1)} %get-tuple-element.222.refs_1_, bf16[1024,256]{1,0:T(8,128)(2,1)S(1)} %get-tuple-element.182.refs_2_, ...), custom_call_target="tpu_custom_call" | custom-call | flops 1 | bytes 1 | tf_op jit(solution)/shard_map/self_back_upper/pallas_call | solution.py:251
  129.7 3.8 %collective-permute-done.21.refs_1_ = bf16[8,128,512]{2,1,0:T(8,128)(2,1)S(1)} collective-permute-done((bf16[8,128,512]{2,1,0:T(8,128)(2,1)S(1)}, bf16[8,128,512]{2,1,0:T(8,128)(2,1)S(1)}, u32[]{:S(2)}, u32[]{:S(2)}) %collective-permute-start.21) | collective-permute-done | bytes 1048608 | tf_op jit(solution)/shard_map/ppermute | solution.py:168
  137.6 7.1 %self_back_lower.1 = (f32[512,512]{1,0:T(8,128)S(1)}, f32[8,512]{1,0:T(8,128)S(1)}, bf16[512,512]{1,0:T(8,128)(2,1)S(1)}, f32[1024,256]{1,0:T(8,128)S(1)}, bf16[...) custom-call(s32[1]{0:T(128)} %bitcast.me_ref.refs_0_, bf16[448,512]{1,0:T(8,128)(2,1)S(1)} %join.9.refs_1_, ...), custom_call_target="tpu_custom_call" | custom-call | flops 1 | bytes 1 | tf_op jit(solution)/shard_map/self_back_lower/pallas_call | solution.py:251
  152.7 2.5 %collective-permute-done.30.refs_1_ = bf16[16,56,512]{2,1,0:T(8,128)(2,1)S(1)} collective-permute-done((bf16[16,56,512]{2,1,0:T(8,128)(2,1)S(1)}, bf16[16,56,512]{2,1,0:T(8,128)(2,1)S(1)}, u32[]{:S(2)}, u32[]{:S(2)}) %collective-permute-start.30) | collective-permute-done | bytes 917536 | tf_op jit(solution)/shard_map/ppermute | solution.py:161
  161.5 6.8 %collective-permute-done.33.refs_1_ = bf16[2,128,512]{2,1,0:T(8,128)(2,1)S(1)} collective-permute-done((bf16[2,128,512]{2,1,0:T(8,128)(2,1)}, bf16[2,128,512]{2,1,0:T(8,128)(2,1)S(1)}, u32[]{:S(2)}, u32[]{:S(2)}) %collective-permute-start.33) | collective-permute-done | bytes 262176 | tf_op jit(solution)/shard_map/ppermute | solution.py:168
  174.0 3.4 %collective-permute-start.34 = (bf16[1,128,512]{2,1,0:T(8,128)(2,1)S(1)}, bf16[1,128,512]{2,1,0:T(8,128)(2,1)S(1)}, u32[]{:S(2)}, u32[]{:S(2)}) collective-permute-start(bf16[1,128,512]{2,1,0:T(8,128)(2,1)S(1)} %get-tuple-element.270), channel_id=1, source_target_pairs={{0,8},{1,17},{2,10},{3,19},{4,12},{5,21},{6,14},{7,23},{8,0},{9,25... | collective-permute-start | bytes 393224 | tf_op jit(solution)/shard_map/ppermute | solution.py:168
  177.5 4.7 %collective-permute-start.37 = (bf16[1,96,512]{2,1,0:T(8,128)(2,1)S(1)}, bf16[1,96,512]{2,1,0:T(8,128)(2,1)S(1)}, u32[]{:S(2)}, u32[]{:S(2)}) collective-permute-start(bf16[1,96,512]{2,1,0:T(8,128)(2,1)S(1)} %get-tuple-element.275), channel_id=1, source_target_pairs={{0,8},{1,17},{2,10},{3,19},{4,12},{5,21},{6,14},{7,23},{8,0},{9,25... | collective-permute-start | bytes 294920 | tf_op jit(solution)/shard_map/ppermute | solution.py:168
  182.3 3.6 %collective-permute-start.39 = (bf16[2,56,512]{2,1,0:T(8,128)(2,1)S(1)}, bf16[2,56,512]{2,1,0:T(8,128)(2,1)S(1)}, u32[]{:S(2)}, u32[]{:S(2)}) collective-permute-start(bf16[2,56,512]{2,1,0:T(8,128)(2,1)S(1)} %get-tuple-element.284), channel_id=1, source_target_pairs={{0,16},{1,9},{2,18},{3,11},{4,20},{5,13},{6,22},{7,15},{8,24},{9,1... | collective-permute-start | bytes 344072 | tf_op jit(solution)/shard_map/ppermute | solution.py:168
  187.0 4.1 %collective-permute-done.39.refs_1_ = bf16[2,56,512]{2,1,0:T(8,128)(2,1)S(1)} collective-permute-done((bf16[2,56,512]{2,1,0:T(8,128)(2,1)S(1)}, bf16[2,56,512]{2,1,0:T(8,128)(2,1)S(1)}, u32[]{:S(2)}, u32[]{:S(2)}) %collective-permute-start.39) | collective-permute-done | bytes 114720 | tf_op jit(solution)/shard_map/ppermute | solution.py:168
  192.0 3.4 %collective-permute-done.40.refs_5_ = bf16[1,56,512]{2,1,0:T(8,128)(2,1)S(1)} collective-permute-done((bf16[1,56,512]{2,1,0:T(8,128)(2,1)S(1)}, bf16[1,56,512]{2,1,0:T(8,128)(2,1)S(1)}, u32[]{:S(2)}, u32[]{:S(2)}) %collective-permute-start.40) | collective-permute-done | bytes 57376 | tf_op jit(solution)/shard_map/ppermute | solution.py:168
  (111 shorter events, 59.6 us)
Async XLA Ops:
  3.1 24.2 %collective-permute-start.3 = (bf16[584,512]{1,0:T(8,128)(2,1)}, bf16[584,512]{1,0:T(8,128)(2,1)S(1)}, u32[]{:S(2)}, u32[]{:S(2)}) collective-permute-start(bf16[584,512]{1,0:T(8,128)(2,1)} %get-tuple-element.165), channel_id=1, source_target_pairs={{0,2},{1,3},{2,0},{3,1},{4,6},{5,7},{6,4},{7,5},{8,10},{9,11},{10,... | collective-permute-start | bytes 1794056 | tf_op jit(solution)/shard_map/ppermute | solution.py:161
  6.0 21.3 %collective-permute-start.4 = (bf16[584,512]{1,0:T(8,128)(2,1)}, bf16[584,512]{1,0:T(8,128)(2,1)S(1)}, u32[]{:S(2)}, u32[]{:S(2)}) collective-permute-start(bf16[584,512]{1,0:T(8,128)(2,1)} %get-tuple-element.168.refs_5_.refs_6_), channel_id=1, source_target_pairs={{0,1},{1,0},{2,3},{3,2},{4,5},{5,4},{6,7},{7,6},{8,9},{9,8},{10,11... | collective-permute-start | bytes 1794056 | tf_op jit(solution)/shard_map/ppermute | solution.py:161
  16.4 10.9 %collective-permute-start.1 = (bf16[224,512]{1,0:T(8,128)(2,1)}, bf16[224,512]{1,0:T(8,128)(2,1)S(1)}, u32[]{:S(2)}, u32[]{:S(2)}) collective-permute-start(bf16[224,512]{1,0:T(8,128)(2,1)} %get-tuple-element.169.refs_0_), channel_id=1, source_target_pairs={{0,8},{1,17},{2,10},{3,19},{4,12},{5,21},{6,14},{7,23},{8,0},{9,25... | collective-permute-start | bytes 688136 | tf_op jit(solution)/shard_map/ppermute | solution.py:168
  28.3 13.0 %collective-permute-start.5 = (bf16[448,512]{1,0:T(8,128)(2,1)S(1)}, bf16[448,512]{1,0:T(8,128)(2,1)S(1)}, u32[]{:S(2)}, u32[]{:S(2)}) collective-permute-start(bf16[448,512]{1,0:T(8,128)(2,1)S(1)} %join.7.upper), channel_id=1, source_target_pairs={{0,16},{1,9},{2,18},{3,11},{4,20},{5,13},{6,22},{7,15},{8,24},{9,1... | collective-permute-start | bytes 1376264 | tf_op jit(solution)/shard_map/ppermute | solution.py:168
  30.9 18.3 %collective-permute-start.10 = (bf16[584,512]{1,0:T(8,128)(2,1)S(1)}, bf16[584,512]{1,0:T(8,128)(2,1)S(1)}, u32[]{:S(2)}, u32[]{:S(2)}) collective-permute-start(bf16[584,512]{1,0:T(8,128)(2,1)S(1)} %collective-permute-done.3.refs_6_.refs_7_), channel_id=1, source_target_pairs={{0,1},{1,0},{2,3},{3,2},{4,5},{5,4},{6,7},{7,6},{8,9},{9,8},{10,11... | collective-permute-start | bytes 1794056 | tf_op jit(solution)/shard_map/ppermute | solution.py:161
  36.5 12.8 %collective-permute-start.8 = (bf16[448,512]{1,0:T(8,128)(2,1)S(1)}, bf16[448,512]{1,0:T(8,128)(2,1)S(1)}, u32[]{:S(2)}, u32[]{:S(2)}) collective-permute-start(bf16[448,512]{1,0:T(8,128)(2,1)S(1)} %join.9.refs_1_), channel_id=1, source_target_pairs={{0,4},{1,3},{2,6},{3,1},{4,0},{5,7},{6,2},{7,5},{8,12},{9,11},{10,... | collective-permute-start | bytes 1376264 | tf_op jit(solution)/shard_map/ppermute | solution.py:168
  41.4 13.4 %collective-permute-start.6 = (bf16[512,512]{1,0:T(8,128)(2,1)S(1)}, bf16[512,512]{1,0:T(8,128)(2,1)S(1)}, u32[]{:S(2)}, u32[]{:S(2)}) collective-permute-start(bf16[512,512]{1,0:T(8,128)(2,1)S(1)} %get-tuple-element.177.refs_0_), channel_id=1, source_target_pairs={{0,2},{1,5},{2,0},{3,7},{4,6},{5,1},{6,4},{7,3},{8,10},{9,13},{10,... | collective-permute-start | bytes 1572872 | tf_op jit(solution)/shard_map/ppermute | solution.py:168
  54.9 31.6 %collective-permute-start.13 = (bf16[1024,512]{1,0:T(8,128)(2,1)S(1)}, bf16[1024,512]{1,0:T(8,128)(2,1)S(1)}, u32[]{:S(2)}, u32[]{:S(2)}) collective-permute-start(bf16[1024,512]{1,0:T(8,128)(2,1)S(1)} %join.11.refs_1_), channel_id=1, source_target_pairs={{0,4},{1,3},{2,6},{3,1},{4,0},{5,7},{6,2},{7,5},{8,12},{9,11},{10,... | collective-permute-start | bytes 3145736 | tf_op jit(solution)/shard_map/ppermute | solution.py:168
  56.4 21.7 %collective-permute-start.14 = (bf16[768,512]{1,0:T(8,128)(2,1)S(1)}, bf16[768,512]{1,0:T(8,128)(2,1)S(1)}, u32[]{:S(2)}, u32[]{:S(2)}) collective-permute-start(bf16[768,512]{1,0:T(8,128)(2,1)S(1)} %join.10.refs_1_), channel_id=1, source_target_pairs={{0,4},{1,3},{2,6},{3,1},{4,0},{5,7},{6,2},{7,5},{8,12},{9,11},{10,... | collective-permute-start | bytes 2359304 | tf_op jit(solution)/shard_map/ppermute | solution.py:168
  57.0 39.9 %collective-permute-start.15 = (bf16[1024,512]{1,0:T(8,128)(2,1)S(1)}, bf16[1024,512]{1,0:T(8,128)(2,1)S(1)}, u32[]{:S(2)}, u32[]{:S(2)}) collective-permute-start(bf16[1024,512]{1,0:T(8,128)(2,1)S(1)} %join.11.refs_1_), channel_id=1, source_target_pairs={{0,1},{1,0},{2,3},{3,2},{4,5},{5,4},{6,7},{7,6},{8,9},{9,8},{10,11... | collective-permute-start | bytes 3145736 | tf_op jit(solution)/shard_map/ppermute | solution.py:161
  86.5 10.4 %collective-permute-start.16 = (bf16[1024,512]{1,0:T(8,128)(2,1)S(1)}, bf16[1024,512]{1,0:T(8,128)(2,1)S(1)}, u32[]{:S(2)}, u32[]{:S(2)}) collective-permute-start(bf16[1024,512]{1,0:T(8,128)(2,1)S(1)} %collective-permute-done.13.refs_2_), channel_id=1, source_target_pairs={{0,1},{1,0},{2,3},{3,2},{4,5},{5,4},{6,7},{7,6},{8,9},{9,8},{10,11... | collective-permute-start | bytes 3145736 | tf_op jit(solution)/shard_map/ppermute | solution.py:161
  118.7 14.8 %collective-permute-start.21 = (bf16[8,128,512]{2,1,0:T(8,128)(2,1)S(1)}, bf16[8,128,512]{2,1,0:T(8,128)(2,1)S(1)}, u32[]{:S(2)}, u32[]{:S(2)}) collective-permute-start(bf16[8,128,512]{2,1,0:T(8,128)(2,1)S(1)} %get-tuple-element.211), channel_id=1, source_target_pairs={{0,4},{1,3},{2,6},{3,1},{4,0},{5,7},{6,2},{7,5},{8,12},{9,11},{10,... | collective-permute-start | bytes 3145736 | tf_op jit(solution)/shard_map/ppermute | solution.py:168
  123.4 10.3 %collective-permute-start.23 = (bf16[16,96,512]{2,1,0:T(8,128)(2,1)S(1)}, bf16[16,96,512]{2,1,0:T(8,128)(2,1)S(1)}, u32[]{:S(2)}, u32[]{:S(2)}) collective-permute-start(bf16[16,96,512]{2,1,0:T(8,128)(2,1)S(1)} %get-tuple-element.232), channel_id=1, source_target_pairs={{0,1},{1,0},{2,3},{3,2},{4,5},{5,4},{6,7},{7,6},{8,9},{9,8},{10,11... | collective-permute-start | bytes 4718600 | tf_op jit(solution)/shard_map/ppermute | solution.py:161
  134.2 17.7 %collective-permute-start.28 = (bf16[8,96,512]{2,1,0:T(8,128)(2,1)S(1)}, bf16[8,96,512]{2,1,0:T(8,128)(2,1)S(1)}, u32[]{:S(2)}, u32[]{:S(2)}) collective-permute-start(bf16[8,96,512]{2,1,0:T(8,128)(2,1)S(1)} %get-tuple-element.256), channel_id=1, source_target_pairs={{0,4},{1,3},{2,6},{3,1},{4,0},{5,7},{6,2},{7,5},{8,12},{9,11},{10,... | collective-permute-start | bytes 2359304 | tf_op jit(solution)/shard_map/ppermute | solution.py:168
  136.1 9.2 %collective-permute-start.24 = (bf16[512,256]{1,0:T(8,128)(2,1)S(1)}, bf16[512,256]{1,0:T(8,128)(2,1)S(1)}, u32[]{:S(2)}, u32[]{:S(2)}) collective-permute-start(bf16[512,256]{1,0:T(8,128)(2,1)S(1)} %get-tuple-element.248), channel_id=1, source_target_pairs={{0,1},{1,0},{2,3},{3,2},{4,5},{5,4},{6,7},{7,6},{8,9},{9,8},{10,11... | collective-permute-start | bytes 786440 | tf_op jit(solution)/shard_map/ppermute | solution.py:161
  136.1 14.2 %collective-permute-start.29 = (bf16[4,128,512]{2,1,0:T(8,128)(2,1)S(1)}, bf16[4,128,512]{2,1,0:T(8,128)(2,1)S(1)}, u32[]{:S(2)}, u32[]{:S(2)}) collective-permute-start(bf16[4,128,512]{2,1,0:T(8,128)(2,1)S(1)} %get-tuple-element.257), channel_id=1, source_target_pairs={{0,2},{1,5},{2,0},{3,7},{4,6},{5,1},{6,4},{7,3},{8,10},{9,13},{10,... | collective-permute-start | bytes 1572872 | tf_op jit(solution)/shard_map/ppermute | solution.py:168
  156.1 14.6 %collective-permute-start.31 = (bf16[8,56,512]{2,1,0:T(8,128)(2,1)}, bf16[8,56,512]{2,1,0:T(8,128)(2,1)S(1)}, u32[]{:S(2)}, u32[]{:S(2)}) collective-permute-start(bf16[8,56,512]{2,1,0:T(8,128)(2,1)} %get-tuple-element.265), channel_id=1, source_target_pairs={{0,4},{1,3},{2,6},{3,1},{4,0},{5,7},{6,2},{7,5},{8,12},{9,11},{10,... | collective-permute-start | bytes 1376264 | tf_op jit(solution)/shard_map/ppermute | solution.py:168
  157.7 10.6 %collective-permute-start.35 = (bf16[4,96,512]{2,1,0:T(8,128)(2,1)}, bf16[4,96,512]{2,1,0:T(8,128)(2,1)S(1)}, u32[]{:S(2)}, u32[]{:S(2)}) collective-permute-start(bf16[4,96,512]{2,1,0:T(8,128)(2,1)} %get-tuple-element.271), channel_id=1, source_target_pairs={{0,2},{1,5},{2,0},{3,7},{4,6},{5,1},{6,4},{7,3},{8,10},{9,13},{10,... | collective-permute-start | bytes 1179656 | tf_op jit(solution)/shard_map/ppermute | solution.py:168
  159.4 8.9 %collective-permute-start.33 = (bf16[2,128,512]{2,1,0:T(8,128)(2,1)}, bf16[2,128,512]{2,1,0:T(8,128)(2,1)S(1)}, u32[]{:S(2)}, u32[]{:S(2)}) collective-permute-start(bf16[2,128,512]{2,1,0:T(8,128)(2,1)} %get-tuple-element.268), channel_id=1, source_target_pairs={{0,16},{1,9},{2,18},{3,11},{4,20},{5,13},{6,22},{7,15},{8,24},{9,1... | collective-permute-start | bytes 786440 | tf_op jit(solution)/shard_map/ppermute | solution.py:168
  168.5 8.9 %collective-permute-start.36 = (bf16[2,96,512]{2,1,0:T(8,128)(2,1)S(1)}, bf16[2,96,512]{2,1,0:T(8,128)(2,1)S(1)}, u32[]{:S(2)}, u32[]{:S(2)}) collective-permute-start(bf16[2,96,512]{2,1,0:T(8,128)(2,1)S(1)} %get-tuple-element.273), channel_id=1, source_target_pairs={{0,16},{1,9},{2,18},{3,11},{4,20},{5,13},{6,22},{7,15},{8,24},{9,1... | collective-permute-start | bytes 589832 | tf_op jit(solution)/shard_map/ppermute | solution.py:168
  170.8 11.4 %collective-permute-start.38 = (bf16[4,56,512]{2,1,0:T(8,128)(2,1)S(1)}, bf16[4,56,512]{2,1,0:T(8,128)(2,1)S(1)}, u32[]{:S(2)}, u32[]{:S(2)}) collective-permute-start(bf16[4,56,512]{2,1,0:T(8,128)(2,1)S(1)} %get-tuple-element.280), channel_id=1, source_target_pairs={{0,2},{1,5},{2,0},{3,7},{4,6},{5,1},{6,4},{7,3},{8,10},{9,13},{10,... | collective-permute-start | bytes 688136 | tf_op jit(solution)/shard_map/ppermute | solution.py:168
  172.4 13.5 %collective-permute-start.32 = (bf16[320,512]{1,0:T(8,128)(2,1)S(1)}, bf16[320,512]{1,0:T(8,128)(2,1)S(1)}, u32[]{:S(2)}, u32[]{:S(2)}) collective-permute-start(bf16[320,512]{1,0:T(8,128)(2,1)S(1)} %copy-done.4), channel_id=1, source_target_pairs={{0,2},{1,3},{2,0},{3,1},{4,6},{5,7},{6,4},{7,5},{8,10},{9,11},{10,... | collective-permute-start | bytes 983048 | tf_op jit(solution)/shard_map/ppermute | solution.py:161
  174.0 17.9 %collective-permute-start.34 = (bf16[1,128,512]{2,1,0:T(8,128)(2,1)S(1)}, bf16[1,128,512]{2,1,0:T(8,128)(2,1)S(1)}, u32[]{:S(2)}, u32[]{:S(2)}) collective-permute-start(bf16[1,128,512]{2,1,0:T(8,128)(2,1)S(1)} %get-tuple-element.270), channel_id=1, source_target_pairs={{0,8},{1,17},{2,10},{3,19},{4,12},{5,21},{6,14},{7,23},{8,0},{9,25... | collective-permute-start | bytes 393224 | tf_op jit(solution)/shard_map/ppermute | solution.py:168
  177.5 14.5 %collective-permute-start.37 = (bf16[1,96,512]{2,1,0:T(8,128)(2,1)S(1)}, bf16[1,96,512]{2,1,0:T(8,128)(2,1)S(1)}, u32[]{:S(2)}, u32[]{:S(2)}) collective-permute-start(bf16[1,96,512]{2,1,0:T(8,128)(2,1)S(1)} %get-tuple-element.275), channel_id=1, source_target_pairs={{0,8},{1,17},{2,10},{3,19},{4,12},{5,21},{6,14},{7,23},{8,0},{9,25... | collective-permute-start | bytes 294920 | tf_op jit(solution)/shard_map/ppermute | solution.py:168
  (24 other events, 144.4 us)

commit v9 on v8

--- a/solution.py
+++ b/solution.py
@@ -233,6 +233,9 @@
     return [((width, width), F32)] * count + [((sums, width), F32)]
 
 
+COSTS = {"self_attention": 8.0}
+
+
 def padded(shape, dtype):
     last = -(-shape[-1] // 128) * 128
     tall = -(-shape[-2] // 16) * 16 if len(shape) > 1 else 16
@@ -256,7 +259,7 @@
         scratch_shapes=[pltpu.VMEM(s, d) for s, d in scratch],
         compiler_params=pltpu.CompilerParams(vmem_limit_bytes=min(need + (room << 20), 58 << 20)),
         cost_estimate=pl.CostEstimate(
-            flops=1, bytes_accessed=1, transcendentals=0
+            flops=int(COSTS.get(name, 0) * 1.15e9) + 1, bytes_accessed=1, transcendentals=0
         ),
         name=name,
     )(*args)
@@ -296,15 +299,16 @@
     tall = blocks * narrow
 
     def kernel(me_ref, *refs):
-        weights, inner, outer, short, wide = refs[:8], refs[8], refs[9], refs[10], refs[11]
-        first, rest = refs[12:]
+        weights, inner, outer, wide, short = refs[:8], refs[8], refs[9], refs[10], refs[11:24]
+        first, rest = refs[24:]
         me, middle = me_ref[0], 5 * narrow + 16
         for i, ref in enumerate(weights):
             if i < 3:
                 first[i * narrow : (i + 1) * narrow, :] = ref[...]
             else:
                 rest[(i - 3) * narrow : (i - 2) * narrow, :] = ref[...]
-        found = placed(me, short[...], width)
+        short = jnp.concatenate([ref[...].astype(F32) for ref in short], axis=0).astype(BF16)
+        found = placed(me, short, width)
         first[3 * narrow :, :] = jnp.concatenate([found[:2, :], jnp.zeros((6, width), F32)], axis=0).astype(BF16)
         per = width // wide.shape[1]
         row = placed(lax.rem(me, per), wide[...], width)
@@ -885,6 +889,35 @@
     )(*arrays)
 
 
+def combine_joint(groups, splits):
+    count, sizes = groups[0][0].shape[0] // splits, [g[0].shape[1] for g in groups]
+    shape = (count, sum(sizes)) + groups[0][0].shape[2:]
+    flat = [a for group in groups for a in group]
+
+    def kernel(*refs):
+        outs, at, row = refs[len(flat) :], 0, 0
+        for group, size in zip(groups, sizes):
+            given = refs[at : at + len(group)]
+            at += len(group)
+            for i, out in enumerate(outs):
+                here = slice(i * count, (i + 1) * count)
+                found = given[0][here].astype(F32)
+                for ref in given[1:]:
+                    found = found + ref[here].astype(F32)
+                out[:, row : row + size, :] = found.astype(BF16)
+            row += size
+
+    return pl.pallas_call(
+        kernel,
+        out_shape=[jax.ShapeDtypeStruct(shape, BF16)] * splits,
+        in_specs=[VM] * len(flat),
+        out_specs=[VM] * splits,
+        compiler_params=pltpu.CompilerParams(vmem_limit_bytes=snug(flat)),
+        cost_estimate=pl.CostEstimate(flops=1, bytes_accessed=1, transcendentals=0),
+        name="combine_joint",
+    )(*flat)
+
+
 def chosen(me, rows, wide):
     width = rows.shape[1]
     line = lax.broadcasted_iota(jnp.int32, (width, wide), 0)
@@ -926,9 +959,9 @@
         kernel, outs, *scratch = made
         return call(kernel, outs, (me_array,) + args, scratch[0] if scratch else [], micros, name, room)
 
-    short = jnp.stack([query_bias, value_bias, output_bias, attention_gain, attention_shift,
-                       source_query_bias, source_value_bias, source_output_bias, source_gain,
-                       source_shift, outer_bias, final_gain, final_shift])
+    short = [query_bias, value_bias, output_bias, attention_gain, attention_shift, source_query_bias,
+             source_value_bias, source_output_bias, source_gain, source_shift, outer_bias, final_gain,
+             final_shift]
 
     def whole(array):
         return lax.all_gather(array, AXES, axis=0, tiled=True)
@@ -948,7 +981,7 @@
         first, rest = run(make_weights_packet(narrow, width, blocks), 1.0, "weights_packet",
                           query_weight, key_weight, value_weight, output_weight, source_query,
                           source_key, source_value, source_output, inner_weight, outer_weight,
-                          short, inner_bias.reshape(1, wide), room=58)
+                          inner_bias.reshape(1, wide), *[v.reshape(1, narrow) for v in short], room=58)
         first = after(first, sent)
         first = join([first, turned_swap(first, 0)])
         first_b = turned_swap(first, 1)
@@ -974,7 +1007,7 @@
         def natural(rows):
             return jnp.where(lane // narrow == me, jnp.tile(rows, (1, devices)), 0)
 
-        vectors = jnp.concatenate([natural(short[:2]), jnp.zeros((6, width), BF16), natural(short[2:]), spread_wide, jnp.zeros((1, width), BF16)])
+        vectors = jnp.concatenate([natural(jnp.stack(short[:2])), jnp.zeros((6, width), BF16), natural(jnp.stack(short[2:])), spread_wide, jnp.zeros((1, width), BF16)])
         vectors = reduce_all(vectors, devices).astype(F32)
         set_self = full[:3] + [vectors[:8]]
         set_cross = full[3:] + [vectors[8:]]
@@ -1044,17 +1077,19 @@
     query_upper, own_upper = found[:2]
     received_upper = [swap(a, m // 2 + 1, devices) for m, a in enumerate(found[2:])]
     if packed:
-        keep, send = combine(after(inner_step, query_upper), 2, 8.0)
-        inner_step = [keep, turned_swap(send, 2)]
-        keep_cross, send = combine(after([grads_cross[0], cross_came], keep), 2)
+        keep_cross, send = combine(after([grads_cross[0], cross_came], query_upper), 2)
         cross_step = [keep_cross, turned_swap(send, 3)]
-        query[1] = after(query[1], keep, keep_cross)
+        query[1] = after(query[1], keep_cross)
     in_part, query_sum, query_w_grad, own_lower, *sends = run(
         make_self_back_lower(packed, parts, rows, block, width, narrow, len(set_query)), 11.0,
         "self_back_lower", *set_query, *own_tokens, query[1], keys[1], values[1], slope[1],
         slope_t[1], logs[1], deltas[1], ids, back1, query_upper,
     )
     received_lower = [swap(a, m // 2 + 1, devices) for m, a in enumerate(sends)]
+    if packed:
+        keep_joint, send = combine_joint(after([inner_step, cross_step], in_part), 2)
+        joint_step = [keep_joint, turned_swap(send, 2)]
+        in_part = after(in_part, keep_joint)
     in_own, in_send, *grads_last = run(
         make_last(packed, parts, rows, block, memory_block, width, narrow, len(set_last)), 6.0,
         "last", *set_last, *own_tokens, in_part, query_sum, query_w_grad, memory_send, own_upper,
@@ -1062,31 +1097,25 @@
     )
 
     if packed:
-        keep_inner, send = combine(after(inner_step, in_own), 2)
-        inner_step = [keep_inner, turned_swap(send, 1)]
-        keep_cross, send = combine(after(cross_step, keep_inner), 2)
-        cross_step = [keep_cross, turned_swap(send, 2)]
-        grads_last[1] = after(grads_last[1], keep_cross)
         keep, send = combine([grads_last[0], swap(grads_last[1], 1, 32)], 2)
         last_step = [keep, turned_swap(send, 3)]
         in_send = after(in_send, last_step[1])
-        keep_inner, send = combine(inner_step, 2)
-        inner_step = [keep_inner, turned_swap(send, 0)]
-        keep_cross, send = combine(cross_step, 2)
-        cross_step = [keep_cross, turned_swap(send, 1)]
-        keep, send = combine(after(last_step, keep_inner, keep_cross), 2)
+        keep_joint, send = combine(after(joint_step, in_own), 2)
+        joint_step = [keep_joint, turned_swap(send, 1)]
+        keep, send = combine(after(last_step, keep_joint), 2)
         last_step = [keep, turned_swap(send, 2)]
-        keep_cross, send = combine(cross_step, 2)
-        cross_step = [keep_cross, turned_swap(send, 0)]
-        keep, send = combine(after(last_step, keep_cross), 2)
+        keep_joint, send = combine(joint_step, 2)
+        joint_step = [keep_joint, turned_swap(send, 0)]
+        keep, send = combine(after(last_step, keep_joint), 2)
         last_step = [keep, turned_swap(send, 1)]
         keep, send = combine(last_step, 2)
         last_step = [keep, turned_swap(send, 0)]
 
         def plan(me_ref, *refs):
             me = me_ref[0]
-            steps, outs = [refs[:2], refs[2:4], refs[4:6]], refs[6:]
-            inner, cross, last = (sum(r[0].astype(F32) for r in given) for given in steps)
+            joint, last = (sum(r[0].astype(F32) for r in given) for given in (refs[:2], refs[2:4]))
+            outs = refs[4:]
+            inner, cross = joint[: 2 * blocks * narrow, :], joint[2 * blocks * narrow :, :]
             for i in range(blocks):
                 outs[0][:, i * width : (i + 1) * width] = inner[i * narrow : (i + 1) * narrow, :]
             outs[1][...] = inner[blocks * narrow :, :]
@@ -1106,7 +1135,7 @@
         (inner_share, outer_share, source_key_share, source_value_share, source_output_share,
          source_query_share, output_share, key_share, value_share, query_share, sums,
          inner_bias_share) = call(
-            plan, [(s, F32) for s in shapes], (me_array, *inner_step, *cross_step, *last_step), [], 2.0,
+            plan, [(s, F32) for s in shapes], (me_array, *joint_step, *last_step), [], 2.0,
             "finish",
         )
         inner_bias_share = inner_bias_share.reshape(wide)

time: 198 us -> 193 us (0.975)
  starting transfers between devices: 45.4 us -> 36.7 us
  waiting for transfers between devices: 80.6 us -> 87.6 us
  local copies, waits for them, and re-layouts: 5.24 us -> 2.54 us
    ppermute x22 -> x19, starting transfers between devices: 40 us -> 29 us  [turned_swap(): lax.ppermute(array, AXES, [(i, i ^ ORDERS[i % 2][step]) for i in range(32)])]
    ppermute x22 -> x19, waiting for transfers between devices: 69 us -> 79.5 us  [turned_swap(): lax.ppermute(array, AXES, [(i, i ^ ORDERS[i % 2][step]) for i in range(32)])]
    ppermute x19, waiting for transfers between devices: 11.6 us -> 8.17 us  [swap(): return lax.ppermute(array, AXES, [(i, i ^ mask) for i in range(devices)])]
    another operation x1 -> x0, local copies, waits for them, and re-layouts: 2.68 us -> none  [per_device(): jnp.stack([query_bias, value_bias, output_bias, attention_gain, attention...]
    ppermute x19, starting transfers between devices: 5.44 us -> 7.7 us  [swap(): return lax.ppermute(array, AXES, [(i, i ^ mask) for i in range(devices)])]
    pallas_call x12 -> x8, Pallas kernels: 3.99 us -> 2.25 us  [combine(): pl.pallas_call(kernel, out_shape=[jax.ShapeDtypeStruct(shape, BF16)] * sp...]
  transfers between devices with their start and end apart: 41 -> 38, of which waited for: 22 -> 18; matrix products, arithmetic and copies ran while one was open for 3% -> 2% of each run, Pallas kernels for 22% -> 22%
where the time goes in v9:
time: 193 us
  waiting for transfers between devices  87.6 us (45%)
  Pallas kernels  60.5 us (31%)
  starting transfers between devices  36.7 us (19%)
  other arithmetic  3.96 us (2%)
  local copies, waits for them, and re-layouts  2.54 us (1%)
    ppermute x19, waiting for transfers between devices, turned_swap(): lax.ppermute(array, AXES, [(i, i ^ ORDERS[i % 2][step]) for i in range(32)])  79.5 us
    pallas_call x13, Pallas kernels, call(): pl.pallas_call(kernel, out_shape=[jax.ShapeDtypeStruct(s, d) for s, d in...  57.7 us
    ppermute x19, starting transfers between devices, turned_swap(): lax.ppermute(array, AXES, [(i, i ^ ORDERS[i % 2][step]) for i in range(32)])  29 us
    ppermute x19, waiting for transfers between devices, swap(): return lax.ppermute(array, AXES, [(i, i ^ mask) for i in range(devices)])  8.17 us
    ppermute x19, starting transfers between devices, swap(): return lax.ppermute(array, AXES, [(i, i ^ mask) for i in range(devices)])  7.7 us
  transfers between devices with their start and end apart: 38, of which 18 were waited for; matrix products, arithmetic and copies ran while one was open for 2% of the time, Pallas kernels for 22%

profile of v9, /device:TPU:0, one launch (start us, length us, event | category | flops | bytes accessed | tf_op | source)
XLA Modules:
  0.0 192.5 jit_solution(15788600584275142514)
XLA Ops:
  0.7 2.4 %tokens_packet.1 = (bf16[584,512]{1,0:T(8,128)(2,1)}, bf16[584,512]{1,0:T(8,128)(2,1)}) custom-call(s32[1]{0:T(128)} %bitcast.15.turn_ref, s32[2,256]{1,0:T(2,128)} %targets.1, s32[2,64]{1,0:T(2,128)} %sources.1, bf16[2,256,512]{2,1,0:T(8,128)(2,1)} %tokens_ref.1, bf16[2,64,512]{2,1,0:T(8,128)(2,1)} %memory_ref.1, bf16[2,256,512]{2,1,0:T(8,128)(2,1)} %cot_ref.1), custom_call_target="tpu_custom_call" | custom-call | flops 1 | bytes 1 | tf_op jit(solution)/shard_map/tokens_packet/pallas_call | solution.py:254
  3.1 3.0 %collective-permute-start.3 = (bf16[584,512]{1,0:T(8,128)(2,1)}, bf16[584,512]{1,0:T(8,128)(2,1)S(1)}, u32[]{:S(2)}, u32[]{:S(2)}) collective-permute-start(bf16[584,512]{1,0:T(8,128)(2,1)} %get-tuple-element.159), channel_id=1, source_target_pairs={{0,2},{1,3},{2,0},{3,1},{4,6},{5,7},{6,4},{7,5},{8,10},{9,11},{10,... | collective-permute-start | bytes 1794056 | tf_op jit(solution)/shard_map/ppermute | solution.py:161
  9.5 3.4 %collective-permute-done.refs_1_ = bf16[56,512]{1,0:T(8,128)(2,1)S(1)} collective-permute-done((bf16[56,512]{1,0:T(8,128)(2,1)}, bf16[56,512]{1,0:T(8,128)(2,1)S(1)}, u32[]{:S(2)}, u32[]{:S(2)}) %collective-permute-start) | collective-permute-done | bytes 57376 | tf_op jit(solution)/shard_map/ppermute | solution.py:168
  15.0 2.6 %collective-permute-start.2 = (bf16[112,512]{1,0:T(8,128)(2,1)S(1)}, bf16[112,512]{1,0:T(8,128)(2,1)S(1)}, u32[]{:S(2)}, u32[]{:S(2)}) collective-permute-start(bf16[112,512]{1,0:T(8,128)(2,1)S(1)} %join.6.refs_0_), channel_id=1, source_target_pairs={{0,16},{1,9},{2,18},{3,11},{4,20},{5,13},{6,22},{7,15},{8,24},{9,1... | collective-permute-start | bytes 344072 | tf_op jit(solution)/shard_map/ppermute | solution.py:168
  17.6 5.9 %collective-permute-done.2.refs_1_ = bf16[112,512]{1,0:T(8,128)(2,1)S(1)} collective-permute-done((bf16[112,512]{1,0:T(8,128)(2,1)S(1)}, bf16[112,512]{1,0:T(8,128)(2,1)S(1)}, u32[]{:S(2)}, u32[]{:S(2)}) %collective-permute-start.2) | collective-permute-done | bytes 114720 | tf_op jit(solution)/shard_map/ppermute | solution.py:168
  28.3 10.3 %collective-permute-done.5.lower = bf16[448,512]{1,0:T(8,128)(2,1)S(1)} collective-permute-done((bf16[448,512]{1,0:T(8,128)(2,1)S(1)}, bf16[448,512]{1,0:T(8,128)(2,1)S(1)}, u32[]{:S(2)}, u32[]{:S(2)}) %collective-permute-start.5) | collective-permute-done | bytes 458784 | tf_op jit(solution)/shard_map/ppermute | solution.py:168
  38.9 2.0 %collective-permute-start.8 = (bf16[448,512]{1,0:T(8,128)(2,1)S(1)}, bf16[448,512]{1,0:T(8,128)(2,1)S(1)}, u32[]{:S(2)}, u32[]{:S(2)}) collective-permute-start(bf16[448,512]{1,0:T(8,128)(2,1)S(1)} %join.9.refs_1_), channel_id=1, source_target_pairs={{0,4},{1,3},{2,6},{3,1},{4,0},{5,7},{6,2},{7,5},{8,12},{9,11},{10,... | collective-permute-start | bytes 1376264 | tf_op jit(solution)/shard_map/ppermute | solution.py:168
  40.9 9.9 %collective-permute-done.9.refs_1_ = bf16[384,512]{1,0:T(8,128)(2,1)S(1)} collective-permute-done((bf16[384,512]{1,0:T(8,128)(2,1)S(1)}, bf16[384,512]{1,0:T(8,128)(2,1)S(1)}, u32[]{:S(2)}, u32[]{:S(2)}) %collective-permute-start.9) | collective-permute-done | bytes 393248 | tf_op jit(solution)/shard_map/ppermute | solution.py:168
  57.2 10.0 %collective-permute-done.6.refs_1_ = bf16[512,512]{1,0:T(8,128)(2,1)S(1)} collective-permute-done((bf16[512,512]{1,0:T(8,128)(2,1)S(1)}, bf16[512,512]{1,0:T(8,128)(2,1)S(1)}, u32[]{:S(2)}, u32[]{:S(2)}) %collective-permute-start.6) | collective-permute-done | bytes 524320 | tf_op jit(solution)/shard_map/ppermute | solution.py:168
  67.9 8.3 %self_attention.1 = (bf16[256,512]{1,0:T(8,128)(2,1)S(1)}, bf16[256,512]{1,0:T(8,128)(2,1)S(1)}, f32[4,1,512]{2,1,0:T(1,128)S(1)}, f32[4,1,512]{2,1,0:T(1,128)S(1)}) custom-call(s32[1]{0:T(128)} %bitcast.me_ref.refs_0_, bf16[256,512]{1,0:T(8,128)(2,1)S(1)} %get-tuple-element.174.refs_0_, bf16[256,512]{1,0:T(8,128)(2,1)S(1)} %get-tuple-element.175.refs_1_, ...), custom_call_target="tpu_custom_call" | custom-call | flops 9200000000 | bytes 1 | tf_op jit(solution)/shard_map/self_attention/pallas_call | solution.py:254
  76.2 5.9 %collective-permute-done.13.refs_2_ = bf16[1024,512]{1,0:T(8,128)(2,1)S(1)} collective-permute-done((bf16[1024,512]{1,0:T(8,128)(2,1)S(1)}, bf16[1024,512]{1,0:T(8,128)(2,1)S(1)}, u32[]{:S(2)}, u32[]{:S(2)}) %collective-permute-start.13) | collective-permute-done | bytes 1048608 | tf_op jit(solution)/shard_map/ppermute | solution.py:168
  82.6 3.3 %collective-permute-done.17.refs_3_ = bf16[768,512]{1,0:T(8,128)(2,1)S(1)} collective-permute-done((bf16[768,512]{1,0:T(8,128)(2,1)S(1)}, bf16[768,512]{1,0:T(8,128)(2,1)S(1)}, u32[]{:S(2)}, u32[]{:S(2)}) %collective-permute-start.17) | collective-permute-done | bytes 786464 | tf_op jit(solution)/shard_map/ppermute | solution.py:161
  87.0 5.4 %cross_forward.1 = (f32[512,512]{1,0:T(8,128)S(1)}, f32[512,512]{1,0:T(8,128)S(1)}, bf16[512,512]{1,0:T(8,128)(2,1)S(1)}, bf16[256,512]{1,0:T(8,128)(2,1)S(1)}, ...) custom-call(s32[1]{0:T(128)} %bitcast.me_ref.refs_0_, ...), custom_call_target="tpu_custom_call" | custom-call | flops 1 | bytes 1 | tf_op jit(solution)/shard_map/cross_forward/pallas_call | solution.py:254
  92.4 12.4 %inner.1 = (f32[256,512]{1,0:T(8,128)S(1)}, bf16[256,512]{1,0:T(8,128)(2,1)S(1)}, f32[512,512]{1,0:T(8,128)S(1)}, f32[8,512]{1,0:T(8,128)S(1)}, bf16[16,128,512]...) custom-call(s32[1]{0:T(128)} %bitcast.me_ref.refs_0_, bf16[1024,512]{1,0:T(8,128)(2,1)S(1)} %join.11.refs_1_, ...), custom_call_target="tpu_custom_call" | custom-call | flops 1 | bytes 1 | tf_op jit(solution)/shard_map/inner/pallas_call | solution.py:254
  105.7 8.4 %cross_back.1 = (f32[512,512]{1,0:T(8,128)S(1)}, f32[128,512]{1,0:T(8,128)S(1)}, f32[128,512]{1,0:T(8,128)S(1)}, f32[16,512]{1,0:T(8,128)S(1)}, bf16[512,256]{1,...) custom-call(s32[1]{0:T(128)} %bitcast.me_ref.refs_0_, ...), custom_call_target="tpu_custom_call" | custom-call | flops 1 | bytes 1 | tf_op jit(solution)/shard_map/cross_back/pallas_call | solution.py:254
  117.4 6.1 %self_back_upper.1 = (bf16[512,256]{1,0:T(8,128)(2,1)S(1)}, f32[1024,256]{1,0:T(8,128)S(1)}, bf16[512,256]{1,0:T(8,128)(2,1)S(1)}, bf16[512,256]{1,0:T(8,128)(2,1)S(1)}) custom-call(s32[1]{0:T(128)} %bitcast.me_ref.refs_0_, bf16[512,256]{1,0:T(8,128)(2,1)S(1)} %get-tuple-element.216.refs_1_, bf16[1024,256]{1,0:T(8,128)(2,1)S(1)} %get-tuple-element.176.refs_2_, ...), custom_call_target="tpu_custom_call" | custom-call | flops 1 | bytes 1 | tf_op jit(solution)/shard_map/self_back_upper/pallas_call | solution.py:254
  126.3 7.1 %self_back_lower.1 = (f32[512,512]{1,0:T(8,128)S(1)}, f32[8,512]{1,0:T(8,128)S(1)}, bf16[512,512]{1,0:T(8,128)(2,1)S(1)}, f32[1024,256]{1,0:T(8,128)S(1)}, bf16[...) custom-call(s32[1]{0:T(128)} %bitcast.me_ref.refs_0_, bf16[448,512]{1,0:T(8,128)(2,1)S(1)} %join.9.refs_1_, ...), custom_call_target="tpu_custom_call" | custom-call | flops 1 | bytes 1 | tf_op jit(solution)/shard_map/self_back_lower/pallas_call | solution.py:254
  134.0 6.5 %collective-permute-done.24.refs_3_ = bf16[8,96,512]{2,1,0:T(8,128)(2,1)S(1)} collective-permute-done((bf16[8,96,512]{2,1,0:T(8,128)(2,1)S(1)}, bf16[8,96,512]{2,1,0:T(8,128)(2,1)S(1)}, u32[]{:S(2)}, u32[]{:S(2)}) %collective-permute-start.24) | collective-permute-done | bytes 786464 | tf_op jit(solution)/shard_map/ppermute | solution.py:168
  146.1 14.8 %collective-permute-done.32.refs_1_ = bf16[4,224,512]{2,1,0:T(8,128)(2,1)S(1)} collective-permute-done((bf16[4,224,512]{2,1,0:T(8,128)(2,1)S(1)}, bf16[4,224,512]{2,1,0:T(8,128)(2,1)S(1)}, u32[]{:S(2)}, u32[]{:S(2)}) %collective-permute-start.32) | collective-permute-done | bytes 917536 | tf_op jit(solution)/shard_map/ppermute | solution.py:168
  161.2 2.1 %collective-permute-start.33 = (bf16[2,224,512]{2,1,0:T(8,128)(2,1)S(1)}, bf16[2,224,512]{2,1,0:T(8,128)(2,1)S(1)}, u32[]{:S(2)}, u32[]{:S(2)}) collective-permute-start(bf16[2,224,512]{2,1,0:T(8,128)(2,1)S(1)} %get-tuple-element.261), channel_id=1, source_target_pairs={{0,16},{1,9},{2,18},{3,11},{4,20},{5,13},{6,22},{7,15},{8,24},{9,1... | collective-permute-start | bytes 1376264 | tf_op jit(solution)/shard_map/ppermute | solution.py:168
  167.6 7.9 %collective-permute-done.33.refs_1_ = bf16[2,224,512]{2,1,0:T(8,128)(2,1)S(1)} collective-permute-done((bf16[2,224,512]{2,1,0:T(8,128)(2,1)S(1)}, bf16[2,224,512]{2,1,0:T(8,128)(2,1)S(1)}, u32[]{:S(2)}, u32[]{:S(2)}) %collective-permute-start.33) | collective-permute-done | bytes 458784 | tf_op jit(solution)/shard_map/ppermute | solution.py:168
  176.7 6.0 %collective-permute-start.36 = (bf16[2,56,512]{2,1,0:T(8,128)(2,1)S(1)}, bf16[2,56,512]{2,1,0:T(8,128)(2,1)S(1)}, u32[]{:S(2)}, u32[]{:S(2)}) collective-permute-start(bf16[2,56,512]{2,1,0:T(8,128)(2,1)S(1)} %get-tuple-element.272), channel_id=1, source_target_pairs={{0,16},{1,9},{2,18},{3,11},{4,20},{5,13},{6,22},{7,15},{8,24},{9,1... | collective-permute-start | bytes 344072 | tf_op jit(solution)/shard_map/ppermute | solution.py:168
  183.9 2.1 %collective-permute-done.36.refs_1_ = bf16[2,56,512]{2,1,0:T(8,128)(2,1)S(1)} collective-permute-done((bf16[2,56,512]{2,1,0:T(8,128)(2,1)S(1)}, bf16[2,56,512]{2,1,0:T(8,128)(2,1)S(1)}, u32[]{:S(2)}, u32[]{:S(2)}) %collective-permute-start.36) | collective-permute-done | bytes 114720 | tf_op jit(solution)/shard_map/ppermute | solution.py:168
  186.0 2.5 %collective-permute-start.37 = (bf16[1,56,512]{2,1,0:T(8,128)(2,1)S(1)}, bf16[1,56,512]{2,1,0:T(8,128)(2,1)S(1)}, u32[]{:S(2)}, u32[]{:S(2)}) collective-permute-start(bf16[1,56,512]{2,1,0:T(8,128)(2,1)S(1)} %get-tuple-element.274), channel_id=1, source_target_pairs={{0,8},{1,17},{2,10},{3,19},{4,12},{5,21},{6,14},{7,23},{8,0},{9,25... | collective-permute-start | bytes 172040 | tf_op jit(solution)/shard_map/ppermute | solution.py:168
  (97 shorter events, 43.0 us)
Async XLA Ops:
  3.1 21.6 %collective-permute-start.3 = (bf16[584,512]{1,0:T(8,128)(2,1)}, bf16[584,512]{1,0:T(8,128)(2,1)S(1)}, u32[]{:S(2)}, u32[]{:S(2)}) collective-permute-start(bf16[584,512]{1,0:T(8,128)(2,1)} %get-tuple-element.159), channel_id=1, source_target_pairs={{0,2},{1,3},{2,0},{3,1},{4,6},{5,7},{6,4},{7,5},{8,10},{9,11},{10,... | collective-permute-start | bytes 1794056 | tf_op jit(solution)/shard_map/ppermute | solution.py:161
  6.0 18.7 %collective-permute-start.4 = (bf16[584,512]{1,0:T(8,128)(2,1)}, bf16[584,512]{1,0:T(8,128)(2,1)S(1)}, u32[]{:S(2)}, u32[]{:S(2)}) collective-permute-start(bf16[584,512]{1,0:T(8,128)(2,1)} %get-tuple-element.162.refs_5_.refs_6_), channel_id=1, source_target_pairs={{0,1},{1,0},{2,3},{3,2},{4,5},{5,4},{6,7},{7,6},{8,9},{9,8},{10,11... | collective-permute-start | bytes 1794056 | tf_op jit(solution)/shard_map/ppermute | solution.py:161
  13.8 10.9 %collective-permute-start.1 = (bf16[224,512]{1,0:T(8,128)(2,1)}, bf16[224,512]{1,0:T(8,128)(2,1)S(1)}, u32[]{:S(2)}, u32[]{:S(2)}) collective-permute-start(bf16[224,512]{1,0:T(8,128)(2,1)} %get-tuple-element.163.refs_0_), channel_id=1, source_target_pairs={{0,8},{1,17},{2,10},{3,19},{4,12},{5,21},{6,14},{7,23},{8,0},{9,25... | collective-permute-start | bytes 688136 | tf_op jit(solution)/shard_map/ppermute | solution.py:168
  25.7 13.0 %collective-permute-start.5 = (bf16[448,512]{1,0:T(8,128)(2,1)S(1)}, bf16[448,512]{1,0:T(8,128)(2,1)S(1)}, u32[]{:S(2)}, u32[]{:S(2)}) collective-permute-start(bf16[448,512]{1,0:T(8,128)(2,1)S(1)} %join.7.upper), channel_id=1, source_target_pairs={{0,16},{1,9},{2,18},{3,11},{4,20},{5,13},{6,22},{7,15},{8,24},{9,1... | collective-permute-start | bytes 1376264 | tf_op jit(solution)/shard_map/ppermute | solution.py:168
  27.7 11.1 %collective-permute-start.7 = (bf16[224,512]{1,0:T(8,128)(2,1)S(1)}, bf16[224,512]{1,0:T(8,128)(2,1)S(1)}, u32[]{:S(2)}, u32[]{:S(2)}) collective-permute-start(bf16[224,512]{1,0:T(8,128)(2,1)S(1)} %join.8.refs_0_), channel_id=1, source_target_pairs={{0,2},{1,5},{2,0},{3,7},{4,6},{5,1},{6,4},{7,3},{8,10},{9,13},{10,... | collective-permute-start | bytes 688136 | tf_op jit(solution)/shard_map/ppermute | solution.py:168
  28.3 24.7 %collective-permute-start.10 = (bf16[584,512]{1,0:T(8,128)(2,1)S(1)}, bf16[584,512]{1,0:T(8,128)(2,1)S(1)}, u32[]{:S(2)}, u32[]{:S(2)}) collective-permute-start(bf16[584,512]{1,0:T(8,128)(2,1)S(1)} %collective-permute-done.3.refs_6_.refs_7_), channel_id=1, source_target_pairs={{0,1},{1,0},{2,3},{3,2},{4,5},{5,4},{6,7},{7,6},{8,9},{9,8},{10,11... | collective-permute-start | bytes 1794056 | tf_op jit(solution)/shard_map/ppermute | solution.py:161
  38.7 12.0 %collective-permute-start.9 = (bf16[384,512]{1,0:T(8,128)(2,1)S(1)}, bf16[384,512]{1,0:T(8,128)(2,1)S(1)}, u32[]{:S(2)}, u32[]{:S(2)}) collective-permute-start(bf16[384,512]{1,0:T(8,128)(2,1)S(1)} %get-tuple-element.168.refs_0_), channel_id=1, source_target_pairs={{0,2},{1,5},{2,0},{3,7},{4,6},{5,1},{6,4},{7,3},{8,10},{9,13},{10,... | collective-permute-start | bytes 1179656 | tf_op jit(solution)/shard_map/ppermute | solution.py:168
  38.9 14.1 %collective-permute-start.8 = (bf16[448,512]{1,0:T(8,128)(2,1)S(1)}, bf16[448,512]{1,0:T(8,128)(2,1)S(1)}, u32[]{:S(2)}, u32[]{:S(2)}) collective-permute-start(bf16[448,512]{1,0:T(8,128)(2,1)S(1)} %join.9.refs_1_), channel_id=1, source_target_pairs={{0,4},{1,3},{2,6},{3,1},{4,0},{5,7},{6,2},{7,5},{8,12},{9,11},{10,... | collective-permute-start | bytes 1376264 | tf_op jit(solution)/shard_map/ppermute | solution.py:168
  50.8 17.1 %collective-permute-start.14 = (bf16[768,512]{1,0:T(8,128)(2,1)S(1)}, bf16[768,512]{1,0:T(8,128)(2,1)S(1)}, u32[]{:S(2)}, u32[]{:S(2)}) collective-permute-start(bf16[768,512]{1,0:T(8,128)(2,1)S(1)} %join.10.refs_1_), channel_id=1, source_target_pairs={{0,4},{1,3},{2,6},{3,1},{4,0},{5,7},{6,2},{7,5},{8,12},{9,11},{10,... | collective-permute-start | bytes 2359304 | tf_op jit(solution)/shard_map/ppermute | solution.py:168
  52.3 14.9 %collective-permute-start.6 = (bf16[512,512]{1,0:T(8,128)(2,1)S(1)}, bf16[512,512]{1,0:T(8,128)(2,1)S(1)}, u32[]{:S(2)}, u32[]{:S(2)}) collective-permute-start(bf16[512,512]{1,0:T(8,128)(2,1)S(1)} %get-tuple-element.171.refs_0_), channel_id=1, source_target_pairs={{0,2},{1,5},{2,0},{3,7},{4,6},{5,1},{6,4},{7,3},{8,10},{9,13},{10,... | collective-permute-start | bytes 1572872 | tf_op jit(solution)/shard_map/ppermute | solution.py:168
  67.2 14.9 %collective-permute-start.13 = (bf16[1024,512]{1,0:T(8,128)(2,1)S(1)}, bf16[1024,512]{1,0:T(8,128)(2,1)S(1)}, u32[]{:S(2)}, u32[]{:S(2)}) collective-permute-start(bf16[1024,512]{1,0:T(8,128)(2,1)S(1)} %join.11.refs_1_), channel_id=1, source_target_pairs={{0,4},{1,3},{2,6},{3,1},{4,0},{5,7},{6,2},{7,5},{8,12},{9,11},{10,... | collective-permute-start | bytes 3145736 | tf_op jit(solution)/shard_map/ppermute | solution.py:168
  67.9 24.5 %collective-permute-start.15 = (bf16[1024,512]{1,0:T(8,128)(2,1)S(1)}, bf16[1024,512]{1,0:T(8,128)(2,1)S(1)}, u32[]{:S(2)}, u32[]{:S(2)}) collective-permute-start(bf16[1024,512]{1,0:T(8,128)(2,1)S(1)} %join.11.refs_1_), channel_id=1, source_target_pairs={{0,1},{1,0},{2,3},{3,2},{4,5},{5,4},{6,7},{7,6},{8,9},{9,8},{10,11... | collective-permute-start | bytes 3145736 | tf_op jit(solution)/shard_map/ppermute | solution.py:161
  82.1 10.3 %collective-permute-start.16 = (bf16[1024,512]{1,0:T(8,128)(2,1)S(1)}, bf16[1024,512]{1,0:T(8,128)(2,1)S(1)}, u32[]{:S(2)}, u32[]{:S(2)}) collective-permute-start(bf16[1024,512]{1,0:T(8,128)(2,1)S(1)} %collective-permute-done.13.refs_2_), channel_id=1, source_target_pairs={{0,1},{1,0},{2,3},{3,2},{4,5},{5,4},{6,7},{7,6},{8,9},{9,8},{10,11... | collective-permute-start | bytes 3145736 | tf_op jit(solution)/shard_map/ppermute | solution.py:161
  104.8 9.4 %collective-permute-start.20 = (bf16[16,128,512]{2,1,0:T(8,128)(2,1)S(1)}, bf16[16,128,512]{2,1,0:T(8,128)(2,1)S(1)}, u32[]{:S(2)}, u32[]{:S(2)}) collective-permute-start(bf16[16,128,512]{2,1,0:T(8,128)(2,1)S(1)} %get-tuple-element.201), channel_id=1, source_target_pairs={{0,1},{1,0},{2,3},{3,2},{4,5},{5,4},{6,7},{7,6},{8,9},{9,8},{10,11... | collective-permute-start | bytes 6291464 | tf_op jit(solution)/shard_map/ppermute | solution.py:161
  117.2 16.3 %collective-permute-start.23 = (bf16[8,128,512]{2,1,0:T(8,128)(2,1)S(1)}, bf16[8,128,512]{2,1,0:T(8,128)(2,1)S(1)}, u32[]{:S(2)}, u32[]{:S(2)}) collective-permute-start(bf16[8,128,512]{2,1,0:T(8,128)(2,1)S(1)} %get-tuple-element.233), channel_id=1, source_target_pairs={{0,4},{1,3},{2,6},{3,1},{4,0},{5,7},{6,2},{7,5},{8,12},{9,11},{10,... | collective-permute-start | bytes 3145736 | tf_op jit(solution)/shard_map/ppermute | solution.py:168
  123.9 16.5 %collective-permute-start.24 = (bf16[8,96,512]{2,1,0:T(8,128)(2,1)S(1)}, bf16[8,96,512]{2,1,0:T(8,128)(2,1)S(1)}, u32[]{:S(2)}, u32[]{:S(2)}) collective-permute-start(bf16[8,96,512]{2,1,0:T(8,128)(2,1)S(1)} %get-tuple-element.234), channel_id=1, source_target_pairs={{0,4},{1,3},{2,6},{3,1},{4,0},{5,7},{6,2},{7,5},{8,12},{9,11},{10,... | collective-permute-start | bytes 2359304 | tf_op jit(solution)/shard_map/ppermute | solution.py:168
  125.8 15.1 %collective-permute-start.25 = (bf16[512,256]{1,0:T(8,128)(2,1)S(1)}, bf16[512,256]{1,0:T(8,128)(2,1)S(1)}, u32[]{:S(2)}, u32[]{:S(2)}) collective-permute-start(bf16[512,256]{1,0:T(8,128)(2,1)S(1)} %get-tuple-element.246), channel_id=1, source_target_pairs={{0,1},{1,0},{2,3},{3,2},{4,5},{5,4},{6,7},{7,6},{8,9},{9,8},{10,11... | collective-permute-start | bytes 786440 | tf_op jit(solution)/shard_map/ppermute | solution.py:161
  125.8 15.1 %collective-permute-start.26 = (bf16[512,256]{1,0:T(8,128)(2,1)S(1)}, bf16[512,256]{1,0:T(8,128)(2,1)S(1)}, u32[]{:S(2)}, u32[]{:S(2)}) collective-permute-start(bf16[512,256]{1,0:T(8,128)(2,1)S(1)} %get-tuple-element.247), channel_id=1, source_target_pairs={{0,1},{1,0},{2,3},{3,2},{4,5},{5,4},{6,7},{7,6},{8,9},{9,8},{10,11... | collective-permute-start | bytes 786440 | tf_op jit(solution)/shard_map/ppermute | solution.py:161
  142.6 18.4 %collective-permute-start.32 = (bf16[4,224,512]{2,1,0:T(8,128)(2,1)S(1)}, bf16[4,224,512]{2,1,0:T(8,128)(2,1)S(1)}, u32[]{:S(2)}, u32[]{:S(2)}) collective-permute-start(bf16[4,224,512]{2,1,0:T(8,128)(2,1)S(1)} %get-tuple-element.257), channel_id=1, source_target_pairs={{0,2},{1,5},{2,0},{3,7},{4,6},{5,1},{6,4},{7,3},{8,10},{9,13},{10,... | collective-permute-start | bytes 2752520 | tf_op jit(solution)/shard_map/ppermute | solution.py:168
  145.9 17.4 %collective-permute-start.30 = (bf16[8,56,512]{2,1,0:T(8,128)(2,1)}, bf16[8,56,512]{2,1,0:T(8,128)(2,1)S(1)}, u32[]{:S(2)}, u32[]{:S(2)}) collective-permute-start(bf16[8,56,512]{2,1,0:T(8,128)(2,1)} %get-tuple-element.254), channel_id=1, source_target_pairs={{0,4},{1,3},{2,6},{3,1},{4,0},{5,7},{6,2},{7,5},{8,12},{9,11},{10,... | collective-permute-start | bytes 1376264 | tf_op jit(solution)/shard_map/ppermute | solution.py:168
  161.2 14.4 %collective-permute-start.33 = (bf16[2,224,512]{2,1,0:T(8,128)(2,1)S(1)}, bf16[2,224,512]{2,1,0:T(8,128)(2,1)S(1)}, u32[]{:S(2)}, u32[]{:S(2)}) collective-permute-start(bf16[2,224,512]{2,1,0:T(8,128)(2,1)S(1)} %get-tuple-element.261), channel_id=1, source_target_pairs={{0,16},{1,9},{2,18},{3,11},{4,20},{5,13},{6,22},{7,15},{8,24},{9,1... | collective-permute-start | bytes 1376264 | tf_op jit(solution)/shard_map/ppermute | solution.py:168
  163.3 19.4 %collective-permute-start.31 = (bf16[320,512]{1,0:T(8,128)(2,1)}, bf16[320,512]{1,0:T(8,128)(2,1)S(1)}, u32[]{:S(2)}, u32[]{:S(2)}) collective-permute-start(bf16[320,512]{1,0:T(8,128)(2,1)} %copy-done.3), channel_id=1, source_target_pairs={{0,2},{1,3},{2,0},{3,1},{4,6},{5,7},{6,4},{7,5},{8,10},{9,11},{10,... | collective-permute-start | bytes 983048 | tf_op jit(solution)/shard_map/ppermute | solution.py:161
  164.8 11.9 %collective-permute-start.35 = (bf16[4,56,512]{2,1,0:T(8,128)(2,1)S(1)}, bf16[4,56,512]{2,1,0:T(8,128)(2,1)S(1)}, u32[]{:S(2)}, u32[]{:S(2)}) collective-permute-start(bf16[4,56,512]{2,1,0:T(8,128)(2,1)S(1)} %get-tuple-element.268), channel_id=1, source_target_pairs={{0,2},{1,5},{2,0},{3,7},{4,6},{5,1},{6,4},{7,3},{8,10},{9,13},{10,... | collective-permute-start | bytes 688136 | tf_op jit(solution)/shard_map/ppermute | solution.py:168
  175.6 13.6 %collective-permute-start.34 = (bf16[1,224,512]{2,1,0:T(8,128)(2,1)S(1)}, bf16[1,224,512]{2,1,0:T(8,128)(2,1)S(1)}, u32[]{:S(2)}, u32[]{:S(2)}) collective-permute-start(bf16[1,224,512]{2,1,0:T(8,128)(2,1)S(1)} %get-tuple-element.263), channel_id=1, source_target_pairs={{0,8},{1,17},{2,10},{3,19},{4,12},{5,21},{6,14},{7,23},{8,0},{9,25... | collective-permute-start | bytes 688136 | tf_op jit(solution)/shard_map/ppermute | solution.py:168
  (19 other events, 125.6 us)

commit v10 on v9

--- a/solution.py
+++ b/solution.py
@@ -161,22 +161,23 @@
     return lax.ppermute(array, AXES, [(i, i ^ mask) for i in range(devices)])
 
 
-ORDERS = ((8, 16, 2, 4), (16, 8, 4, 2))
-
-
-def turned_swap(array, step):
-    return lax.ppermute(array, AXES, [(i, i ^ ORDERS[i % 2][step]) for i in range(32)])
+Z_FIRST = ((8, 16, 2, 4), (16, 8, 4, 2))
+CROSSED = ((8, 16, 4, 2), (16, 8, 2, 4))
+
+
+def turned_swap(array, step, orders=Z_FIRST):
+    return lax.ppermute(array, AXES, [(i, i ^ orders[i % 2][step]) for i in range(32)])
 
 
 def after(value, *others):
     return lax.optimization_barrier((value, others))[0]
 
 
-def places(me):
+def places(me, orders=Z_FIRST):
     found = []
     for core in range(2):
         even = ((me & 1) ^ core) == 0
-        masks = [jnp.where(even, first, second) for first, second in zip(*ORDERS)]
+        masks = [jnp.where(even, first, second) for first, second in zip(*orders)]
         for far in range(2):
             for slot in range(8):
                 device = me ^ core if core else me
@@ -187,8 +188,8 @@
     return found
 
 
-def unpack(me, pieces, stride, first, rows, scratch):
-    for core, far, slot, device in places(me):
+def unpack(me, pieces, stride, first, rows, scratch, orders=Z_FIRST):
+    for core, far, slot, device in places(me, orders):
         ref = pieces[2 * core + far]
         at = slot * stride + first
         scratch[pl.ds(pl.multiple_of(device * rows, rows), rows), :] = ref[at : at + rows, :]
@@ -204,8 +205,8 @@
 
 
 class Grads:
-    def __init__(self, me, refs, dense, rows):
-        self.me, self.refs, self.dense, self.rows = me, refs, dense, rows
+    def __init__(self, me, refs, dense, rows, orders=Z_FIRST):
+        self.me, self.refs, self.dense, self.rows, self.orders = me, refs, dense, rows, orders
 
     def put(self, index, grad):
         if self.dense is None:
@@ -213,7 +214,7 @@
             return
         self.dense[...] = grad
         rows = self.rows
-        for core, far, slot, device in places(self.me):
+        for core, far, slot, device in places(self.me, self.orders):
             found = self.dense[pl.ds(pl.multiple_of(device * rows, rows), rows), :]
             self.refs[core][far * 8 + slot, index * rows : (index + 1) * rows, :] = found.astype(BF16)
 
@@ -233,7 +234,7 @@
     return [((width, width), F32)] * count + [((sums, width), F32)]
 
 
-COSTS = {"self_attention": 8.0}
+COSTS = {}
 
 
 def padded(shape, dtype):
@@ -372,7 +373,7 @@
         me = me_ref[0]
         if packed:
             for i in range(3):
-                unpack(me, pieces, stride, i * narrow, narrow, scratch[i])
+                unpack(me, pieces, stride, i * narrow, narrow, scratch[i], CROSSED)
             query_w, key_w, value_w = scratch
             biases = vector_sum(pieces, stride, 3 * narrow)
         else:
@@ -496,7 +497,7 @@
         if packed:
             inner_w, outer_w, gathered, dense = scratch[4:8]
             tall = blocks * narrow
-            for core, far, slot, device in places(me_ref[0]):
+            for core, far, slot, device in places(me_ref[0], CROSSED):
                 ref, at = pieces[2 * core + far], slot * 2 * tall
                 row = pl.multiple_of(device * narrow, narrow)
                 for i in range(blocks):
@@ -728,7 +729,7 @@
             source_key, source_value = scratch[1:3]
         else:
             source_key, source_value = pieces
-        grads = Grads(me, grad_refs, scratch[3] if packed else None, narrow)
+        grads = Grads(me, grad_refs, scratch[3] if packed else None, narrow, CROSSED)
         memory = jnp.concatenate([t[block : block + memory_block, :] for t in tokens], axis=0)
         key_sum, value_sum = memory_key_own[...], memory_value_own[...]
         for ref in memory_received:
@@ -785,7 +786,7 @@
         in_part, query_sum, query_w_grad, own = refs[2:6]
         sends, scratch = refs[6 : 4 + 2 * parts], refs[4 + 2 * parts :]
         if packed:
-            unpack(me_ref[0], pieces, 3 * narrow + 8, 0, narrow, scratch[7])
+            unpack(me_ref[0], pieces, 3 * narrow + 8, 0, narrow, scratch[7], CROSSED)
             query_w = scratch[7]
         else:
             (query_w,) = pieces
@@ -828,7 +829,7 @@
         me = me_ref[0]
         if packed:
             for i in range(2):
-                unpack(me, pieces, 3 * narrow + 8, (1 + i) * narrow, narrow, scratch[1 + i])
+                unpack(me, pieces, 3 * narrow + 8, (1 + i) * narrow, narrow, scratch[1 + i], CROSSED)
             key_w, value_w = scratch[1:3]
         else:
             key_w, value_w = pieces
@@ -989,14 +990,15 @@
         rest_b = turned_swap(rest, 0)
         first = join(after([first, first_b], rest_b))
         rest = join(after([rest, rest_b], first_b, came, *kept_swaps))
-        first_b, rest_b = turned_swap(first, 2), turned_swap(rest, 1)
+        first_b, rest_b = turned_swap(first, 2, CROSSED), turned_swap(rest, 1)
         first_c = join([first, first_b])
-        first_d = turned_swap(first_c, 3)
-        second, third = run(make_part((5 * narrow + 16, 2 * blocks * narrow), width), 1.0, "part", rest, rest_b)
-        second_b, third_b = turned_swap(second, 2), turned_swap(third, 2)
-        second_c = join([second, second_b])
-        second_d = turned_swap(second_c, 3)
-        first_d = after(first_d, second_c, *came_swaps)
+        first_d = turned_swap(first_c, 3, CROSSED)
+        second, third = run(make_part((5 * narrow + 16, 2 * blocks * narrow), width), 1.0, "part", rest, after(rest_b, first_b))
+        second_b, third_b = turned_swap(second, 2), turned_swap(third, 2, CROSSED)
+        second_c = join(after([second, second_b], first_d, third_b))
+        third_c = join(after([third, third_b], first_d, second_b))
+        second_d, third_d = turned_swap(second_c, 3), turned_swap(third_c, 3, CROSSED)
+        first_d = after(first_d, second_c, third_c, *came_swaps)
         set_self = [first_c, first_d, swap(first_c, 1, 32), swap(first_d, 1, 32)]
     else:
         full = [whole(w) for w in (query_weight, key_weight, value_weight, output_weight, source_query, source_key, source_value, source_output)]
@@ -1023,12 +1025,7 @@
     row_memory, ids, memory_ids = found[10:]
     query_t = list(query_t)
     if packed:
-        third_c = join(after([third, third_b], query_t[0]))
-        third_d = turned_swap(third_c, 3)
-        second_d = after(second_d, query_t[0])
-        set_cross = [second_c, second_d, swap(second_c, 1, 32), swap(second_d, 1, 32)]
-        query_t[0] = after(query_t[0], third_c, second_d)
-        set_back, set_query, set_last, set_memory = set_cross, set_self, set_self, set_cross
+        set_query, set_last = set_self, set_self
     else:
         set_back, set_query, set_last, set_memory = [full[3], full[4], full[7]], full[:1], full[1:3], full[5:7]
     found = run(
@@ -1037,8 +1034,10 @@
     )
     mixtures, logs = found[:2], found[2:]
     if packed:
-        third_d = after(third_d, mixtures[0])
+        second_d, third_d = after(second_d, mixtures[0]), after(third_d, mixtures[0])
+        set_cross = [second_c, second_d, swap(second_c, 1, 32), swap(second_d, 1, 32)]
         set_inner = [third_c, third_d, swap(third_c, 1, 32), swap(third_d, 1, 32)]
+        set_back, set_memory = set_cross, set_cross
     first_sum, second_sum, cross_query, memory_keys, memory_values, cross_t, cross_logs, vectors = run(
         make_cross_forward(packed, rows, block, parts * memory_share, width, narrow, len(set_cross)),
         9.0, "cross_forward", *set_cross, *own_tokens, row_memory, ids, memory_ids, *mixtures,
@@ -1078,7 +1077,7 @@
     received_upper = [swap(a, m // 2 + 1, devices) for m, a in enumerate(found[2:])]
     if packed:
         keep_cross, send = combine(after([grads_cross[0], cross_came], query_upper), 2)
-        cross_step = [keep_cross, turned_swap(send, 3)]
+        cross_step = [keep_cross, turned_swap(send, 3, CROSSED)]
         query[1] = after(query[1], keep_cross)
     in_part, query_sum, query_w_grad, own_lower, *sends = run(
         make_self_back_lower(packed, parts, rows, block, width, narrow, len(set_query)), 11.0,
@@ -1087,9 +1086,11 @@
     )
     received_lower = [swap(a, m // 2 + 1, devices) for m, a in enumerate(sends)]
     if packed:
-        keep_joint, send = combine_joint(after([inner_step, cross_step], in_part), 2)
-        joint_step = [keep_joint, turned_swap(send, 2)]
-        in_part = after(in_part, keep_joint)
+        keep, send = combine(after(inner_step, query_sum), 2)
+        inner_step = [keep, turned_swap(send, 2)]
+        keep_cross, send = combine(after(cross_step, query_sum), 2)
+        cross_step = [keep_cross, turned_swap(send, 2, CROSSED)]
+        in_part = after(in_part, keep, keep_cross)
     in_own, in_send, *grads_last = run(
         make_last(packed, parts, rows, block, memory_block, width, narrow, len(set_last)), 6.0,
         "last", *set_last, *own_tokens, in_part, query_sum, query_w_grad, memory_send, own_upper,
@@ -1100,7 +1101,7 @@
         keep, send = combine([grads_last[0], swap(grads_last[1], 1, 32)], 2)
         last_step = [keep, turned_swap(send, 3)]
         in_send = after(in_send, last_step[1])
-        keep_joint, send = combine(after(joint_step, in_own), 2)
+        keep_joint, send = combine_joint(after([inner_step, cross_step], in_own), 2)
         joint_step = [keep_joint, turned_swap(send, 1)]
         keep, send = combine(after(last_step, keep_joint), 2)
         last_step = [keep, turned_swap(send, 2)]

time: 193 us -> 186 us (0.964)
  waiting for transfers between devices: 87.6 us -> 81 us
    ppermute x19 -> x20, waiting for transfers between devices: 79.5 us -> 73.2 us  [turned_swap(): lax.ppermute(array, AXES, [(i, i ^ orders[i % 2][step]) for i in range(32)])]
    ppermute x19 -> x20, starting transfers between devices: 29 us -> 28.2 us  [turned_swap(): lax.ppermute(array, AXES, [(i, i ^ orders[i % 2][step]) for i in range(32)])]
  transfers between devices with their start and end apart: 38 -> 39, of which waited for: 18 -> 22; matrix products, arithmetic and copies ran while one was open for 2% -> 2% of each run, Pallas kernels for 22% -> 23%
where the time goes in v10:
time: 186 us; the launch traced here: 185 us
  waiting for transfers between devices  81 us (44%)
  Pallas kernels  60.5 us (33%)
  starting transfers between devices  35.9 us (19%)
  other arithmetic  3.95 us (2%)
  local copies, waits for them, and re-layouts  2.48 us (1%)
    ppermute x20, waiting for transfers between devices, turned_swap(): lax.ppermute(array, AXES, [(i, i ^ orders[i % 2][step]) for i in range(32)])  73.2 us
    pallas_call x13, Pallas kernels, call(): pl.pallas_call(kernel, out_shape=[jax.ShapeDtypeStruct(s, d) for s, d in...  57.6 us
    ppermute x20, starting transfers between devices, turned_swap(): lax.ppermute(array, AXES, [(i, i ^ orders[i % 2][step]) for i in range(32)])  28.2 us
    ppermute x19, waiting for transfers between devices, swap(): return lax.ppermute(array, AXES, [(i, i ^ mask) for i in range(devices)])  7.79 us
    ppermute x19, starting transfers between devices, swap(): return lax.ppermute(array, AXES, [(i, i ^ mask) for i in range(devices)])  7.66 us
  transfers between devices with their start and end apart: 39, of which 22 were waited for; matrix products, arithmetic and copies ran while one was open for 2% of the time, Pallas kernels for 23%

profile of v10, /device:TPU:0, one launch (start us, length us, event | category | flops | bytes accessed | tf_op | source)
XLA Modules:
  0.0 185.0 jit_solution(16225516029520632621)
XLA Ops:
  0.7 2.4 %tokens_packet.1 = (bf16[584,512]{1,0:T(8,128)(2,1)}, bf16[584,512]{1,0:T(8,128)(2,1)}) custom-call(s32[1]{0:T(128)} %bitcast.15.turn_ref, s32[2,256]{1,0:T(2,128)} %targets.1, s32[2,64]{1,0:T(2,128)} %sources.1, bf16[2,256,512]{2,1,0:T(8,128)(2,1)} %tokens_ref.1, bf16[2,64,512]{2,1,0:T(8,128)(2,1)} %memory_ref.1, bf16[2,256,512]{2,1,0:T(8,128)(2,1)} %cot_ref.1), custom_call_target="tpu_custom_call" | custom-call | flops 1 | bytes 1 | tf_op jit(solution)/shard_map/tokens_packet/pallas_call | solution.py:255
  3.1 3.0 %collective-permute-start.3 = (bf16[584,512]{1,0:T(8,128)(2,1)}, bf16[584,512]{1,0:T(8,128)(2,1)S(1)}, u32[]{:S(2)}, u32[]{:S(2)}) collective-permute-start(bf16[584,512]{1,0:T(8,128)(2,1)} %get-tuple-element.165), channel_id=1, source_target_pairs={{0,2},{1,3},{2,0},{3,1},{4,6},{5,7},{6,4},{7,5},{8,10},{9,11},{10,... | collective-permute-start | bytes 1794056 | tf_op jit(solution)/shard_map/ppermute | solution.py:161
  9.5 3.4 %collective-permute-done.refs_1_ = bf16[56,512]{1,0:T(8,128)(2,1)S(1)} collective-permute-done((bf16[56,512]{1,0:T(8,128)(2,1)}, bf16[56,512]{1,0:T(8,128)(2,1)S(1)}, u32[]{:S(2)}, u32[]{:S(2)}) %collective-permute-start) | collective-permute-done | bytes 57376 | tf_op jit(solution)/shard_map/ppermute | solution.py:169
  15.0 2.6 %collective-permute-start.2 = (bf16[112,512]{1,0:T(8,128)(2,1)S(1)}, bf16[112,512]{1,0:T(8,128)(2,1)S(1)}, u32[]{:S(2)}, u32[]{:S(2)}) collective-permute-start(bf16[112,512]{1,0:T(8,128)(2,1)S(1)} %join.6.refs_0_), channel_id=1, source_target_pairs={{0,16},{1,9},{2,18},{3,11},{4,20},{5,13},{6,22},{7,15},{8,24},{9,1... | collective-permute-start | bytes 344072 | tf_op jit(solution)/shard_map/ppermute | solution.py:169
  17.6 5.9 %collective-permute-done.2.refs_1_ = bf16[112,512]{1,0:T(8,128)(2,1)S(1)} collective-permute-done((bf16[112,512]{1,0:T(8,128)(2,1)S(1)}, bf16[112,512]{1,0:T(8,128)(2,1)S(1)}, u32[]{:S(2)}, u32[]{:S(2)}) %collective-permute-start.2) | collective-permute-done | bytes 114720 | tf_op jit(solution)/shard_map/ppermute | solution.py:169
  29.3 4.5 %collective-permute-done.6.refs_1_ = bf16[224,512]{1,0:T(8,128)(2,1)S(1)} collective-permute-done((bf16[224,512]{1,0:T(8,128)(2,1)S(1)}, bf16[224,512]{1,0:T(8,128)(2,1)S(1)}, u32[]{:S(2)}, u32[]{:S(2)}) %collective-permute-start.6) | collective-permute-done | bytes 229408 | tf_op jit(solution)/shard_map/ppermute | solution.py:169
  33.8 4.8 %collective-permute-done.5.lower = bf16[448,512]{1,0:T(8,128)(2,1)S(1)} collective-permute-done((bf16[448,512]{1,0:T(8,128)(2,1)S(1)}, bf16[448,512]{1,0:T(8,128)(2,1)S(1)}, u32[]{:S(2)}, u32[]{:S(2)}) %collective-permute-start.5) | collective-permute-done | bytes 458784 | tf_op jit(solution)/shard_map/ppermute | solution.py:169
  42.4 8.2 %collective-permute-done.8.refs_2_ = bf16[448,512]{1,0:T(8,128)(2,1)S(1)} collective-permute-done((bf16[448,512]{1,0:T(8,128)(2,1)S(1)}, bf16[448,512]{1,0:T(8,128)(2,1)S(1)}, u32[]{:S(2)}, u32[]{:S(2)}) %collective-permute-start.8) | collective-permute-done | bytes 458784 | tf_op jit(solution)/shard_map/ppermute | solution.py:169
  50.6 4.2 %collective-permute-done.9.refs_1_ = bf16[384,512]{1,0:T(8,128)(2,1)S(1)} collective-permute-done((bf16[384,512]{1,0:T(8,128)(2,1)S(1)}, bf16[384,512]{1,0:T(8,128)(2,1)S(1)}, u32[]{:S(2)}, u32[]{:S(2)}) %collective-permute-start.9) | collective-permute-done | bytes 393248 | tf_op jit(solution)/shard_map/ppermute | solution.py:169
  61.5 8.3 %self_attention.1 = (bf16[256,512]{1,0:T(8,128)(2,1)S(1)}, bf16[256,512]{1,0:T(8,128)(2,1)S(1)}, f32[4,1,512]{2,1,0:T(1,128)S(1)}, f32[4,1,512]{2,1,0:T(1,128)S(1)}) custom-call(s32[1]{0:T(128)} %bitcast.me_ref.refs_0_, bf16[256,512]{1,0:T(8,128)(2,1)S(1)} %get-tuple-element.181.refs_0_, bf16[256,512]{1,0:T(8,128)(2,1)S(1)} %get-tuple-element.182.refs_1_, ...), custom_call_target="tpu_custom_call" | custom-call | flops 1 | bytes 1 | tf_op jit(solution)/shard_map/self_attention/pallas_call | solution.py:255
  69.7 8.4 %collective-permute-done.10.refs_2_ = bf16[1024,512]{1,0:T(8,128)(2,1)S(1)} collective-permute-done((bf16[1024,512]{1,0:T(8,128)(2,1)S(1)}, bf16[1024,512]{1,0:T(8,128)(2,1)S(1)}, u32[]{:S(2)}, u32[]{:S(2)}) %collective-permute-start.10) | collective-permute-done | bytes 1048608 | tf_op jit(solution)/shard_map/ppermute | solution.py:169
  78.7 3.3 %collective-permute-done.17.refs_3_ = bf16[768,512]{1,0:T(8,128)(2,1)S(1)} collective-permute-done((bf16[768,512]{1,0:T(8,128)(2,1)S(1)}, bf16[768,512]{1,0:T(8,128)(2,1)S(1)}, u32[]{:S(2)}, u32[]{:S(2)}) %collective-permute-start.17) | collective-permute-done | bytes 786464 | tf_op jit(solution)/shard_map/ppermute | solution.py:161
  83.1 5.4 %cross_forward.1 = (f32[512,512]{1,0:T(8,128)S(1)}, f32[512,512]{1,0:T(8,128)S(1)}, bf16[512,512]{1,0:T(8,128)(2,1)S(1)}, bf16[256,512]{1,0:T(8,128)(2,1)S(1)}, ...) custom-call(s32[1]{0:T(128)} %bitcast.me_ref.refs_0_, ...), custom_call_target="tpu_custom_call" | custom-call | flops 1 | bytes 1 | tf_op jit(solution)/shard_map/cross_forward/pallas_call | solution.py:255
  88.5 12.4 %inner.1 = (f32[256,512]{1,0:T(8,128)S(1)}, bf16[256,512]{1,0:T(8,128)(2,1)S(1)}, f32[512,512]{1,0:T(8,128)S(1)}, f32[8,512]{1,0:T(8,128)S(1)}, bf16[16,128,512]...) custom-call(s32[1]{0:T(128)} %bitcast.me_ref.refs_0_, bf16[1024,512]{1,0:T(8,128)(2,1)S(1)} %join.10.refs_1_, ...), custom_call_target="tpu_custom_call" | custom-call | flops 1 | bytes 1 | tf_op jit(solution)/shard_map/inner/pallas_call | solution.py:255
  102.0 8.4 %cross_back.1 = (f32[512,512]{1,0:T(8,128)S(1)}, f32[128,512]{1,0:T(8,128)S(1)}, f32[128,512]{1,0:T(8,128)S(1)}, f32[16,512]{1,0:T(8,128)S(1)}, bf16[512,256]{1,...) custom-call(s32[1]{0:T(128)} %bitcast.me_ref.refs_0_, ...), custom_call_target="tpu_custom_call" | custom-call | flops 1 | bytes 1 | tf_op jit(solution)/shard_map/cross_back/pallas_call | solution.py:255
  114.6 6.1 %self_back_upper.1 = (bf16[512,256]{1,0:T(8,128)(2,1)S(1)}, f32[1024,256]{1,0:T(8,128)S(1)}, bf16[512,256]{1,0:T(8,128)(2,1)S(1)}, bf16[512,256]{1,0:T(8,128)(2,1)S(1)}) custom-call(s32[1]{0:T(128)} %bitcast.me_ref.refs_0_, bf16[512,256]{1,0:T(8,128)(2,1)S(1)} %get-tuple-element.224.refs_1_, bf16[1024,256]{1,0:T(8,128)(2,1)S(1)} %get-tuple-element.183.refs_2_, ...), custom_call_target="tpu_custom_call" | custom-call | flops 1 | bytes 1 | tf_op jit(solution)/shard_map/self_back_upper/pallas_call | solution.py:255
  123.2 7.1 %self_back_lower.1 = (f32[512,512]{1,0:T(8,128)S(1)}, f32[8,512]{1,0:T(8,128)S(1)}, bf16[512,512]{1,0:T(8,128)(2,1)S(1)}, f32[1024,256]{1,0:T(8,128)S(1)}, bf16[...) custom-call(s32[1]{0:T(128)} %bitcast.me_ref.refs_0_, bf16[448,512]{1,0:T(8,128)(2,1)S(1)} %join.9.refs_1_, ...), custom_call_target="tpu_custom_call" | custom-call | flops 1 | bytes 1 | tf_op jit(solution)/shard_map/self_back_lower/pallas_call | solution.py:255
  130.3 2.4 %collective-permute-done.23.refs_1_ = bf16[8,128,512]{2,1,0:T(8,128)(2,1)S(1)} collective-permute-done((bf16[8,128,512]{2,1,0:T(8,128)(2,1)S(1)}, bf16[8,128,512]{2,1,0:T(8,128)(2,1)S(1)}, u32[]{:S(2)}, u32[]{:S(2)}) %collective-permute-start.23) | collective-permute-done | bytes 1048608 | tf_op jit(solution)/shard_map/ppermute | solution.py:169
  133.0 3.2 %collective-permute-done.24.refs_1_ = bf16[8,96,512]{2,1,0:T(8,128)(2,1)S(1)} collective-permute-done((bf16[8,96,512]{2,1,0:T(8,128)(2,1)S(1)}, bf16[8,96,512]{2,1,0:T(8,128)(2,1)S(1)}, u32[]{:S(2)}, u32[]{:S(2)}) %collective-permute-start.24) | collective-permute-done | bytes 786464 | tf_op jit(solution)/shard_map/ppermute | solution.py:169
  143.5 7.1 %collective-permute-done.32.refs_1_ = bf16[4,128,512]{2,1,0:T(8,128)(2,1)S(1)} collective-permute-done((bf16[4,128,512]{2,1,0:T(8,128)(2,1)S(1)}, bf16[4,128,512]{2,1,0:T(8,128)(2,1)S(1)}, u32[]{:S(2)}, u32[]{:S(2)}) %collective-permute-start.32) | collective-permute-done | bytes 524320 | tf_op jit(solution)/shard_map/ppermute | solution.py:169
  150.6 5.3 %collective-permute-done.33.refs_3_ = bf16[4,96,512]{2,1,0:T(8,128)(2,1)S(1)} collective-permute-done((bf16[4,96,512]{2,1,0:T(8,128)(2,1)S(1)}, bf16[4,96,512]{2,1,0:T(8,128)(2,1)S(1)}, u32[]{:S(2)}, u32[]{:S(2)}) %collective-permute-start.33) | collective-permute-done | bytes 393248 | tf_op jit(solution)/shard_map/ppermute | solution.py:169
  162.0 8.5 %collective-permute-done.34.refs_1_ = bf16[2,224,512]{2,1,0:T(8,128)(2,1)S(1)} collective-permute-done((bf16[2,224,512]{2,1,0:T(8,128)(2,1)S(1)}, bf16[2,224,512]{2,1,0:T(8,128)(2,1)S(1)}, u32[]{:S(2)}, u32[]{:S(2)}) %collective-permute-start.34) | collective-permute-done | bytes 458784 | tf_op jit(solution)/shard_map/ppermute | solution.py:169
  171.3 2.7 %collective-permute-start.37 = (bf16[2,56,512]{2,1,0:T(8,128)(2,1)S(1)}, bf16[2,56,512]{2,1,0:T(8,128)(2,1)S(1)}, u32[]{:S(2)}, u32[]{:S(2)}) collective-permute-start(bf16[2,56,512]{2,1,0:T(8,128)(2,1)S(1)} %get-tuple-element.284), channel_id=1, source_target_pairs={{0,16},{1,9},{2,18},{3,11},{4,20},{5,13},{6,22},{7,15},{8,24},{9,1... | collective-permute-start | bytes 344072 | tf_op jit(solution)/shard_map/ppermute | solution.py:169
  175.2 3.7 %collective-permute-done.37.refs_1_ = bf16[2,56,512]{2,1,0:T(8,128)(2,1)S(1)} collective-permute-done((bf16[2,56,512]{2,1,0:T(8,128)(2,1)S(1)}, bf16[2,56,512]{2,1,0:T(8,128)(2,1)S(1)}, u32[]{:S(2)}, u32[]{:S(2)}) %collective-permute-start.37) | collective-permute-done | bytes 114720 | tf_op jit(solution)/shard_map/ppermute | solution.py:169
  (100 shorter events, 52.6 us)
Async XLA Ops:
  3.1 21.6 %collective-permute-start.3 = (bf16[584,512]{1,0:T(8,128)(2,1)}, bf16[584,512]{1,0:T(8,128)(2,1)S(1)}, u32[]{:S(2)}, u32[]{:S(2)}) collective-permute-start(bf16[584,512]{1,0:T(8,128)(2,1)} %get-tuple-element.165), channel_id=1, source_target_pairs={{0,2},{1,3},{2,0},{3,1},{4,6},{5,7},{6,4},{7,5},{8,10},{9,11},{10,... | collective-permute-start | bytes 1794056 | tf_op jit(solution)/shard_map/ppermute | solution.py:161
  6.0 18.7 %collective-permute-start.4 = (bf16[584,512]{1,0:T(8,128)(2,1)}, bf16[584,512]{1,0:T(8,128)(2,1)S(1)}, u32[]{:S(2)}, u32[]{:S(2)}) collective-permute-start(bf16[584,512]{1,0:T(8,128)(2,1)} %get-tuple-element.168.refs_5_.refs_6_), channel_id=1, source_target_pairs={{0,1},{1,0},{2,3},{3,2},{4,5},{5,4},{6,7},{7,6},{8,9},{9,8},{10,11... | collective-permute-start | bytes 1794056 | tf_op jit(solution)/shard_map/ppermute | solution.py:161
  13.8 10.9 %collective-permute-start.1 = (bf16[224,512]{1,0:T(8,128)(2,1)}, bf16[224,512]{1,0:T(8,128)(2,1)S(1)}, u32[]{:S(2)}, u32[]{:S(2)}) collective-permute-start(bf16[224,512]{1,0:T(8,128)(2,1)} %get-tuple-element.169.refs_0_), channel_id=1, source_target_pairs={{0,8},{1,17},{2,10},{3,19},{4,12},{5,21},{6,14},{7,23},{8,0},{9,25... | collective-permute-start | bytes 688136 | tf_op jit(solution)/shard_map/ppermute | solution.py:169
  25.7 13.0 %collective-permute-start.5 = (bf16[448,512]{1,0:T(8,128)(2,1)S(1)}, bf16[448,512]{1,0:T(8,128)(2,1)S(1)}, u32[]{:S(2)}, u32[]{:S(2)}) collective-permute-start(bf16[448,512]{1,0:T(8,128)(2,1)S(1)} %join.7.upper), channel_id=1, source_target_pairs={{0,16},{1,9},{2,18},{3,11},{4,20},{5,13},{6,22},{7,15},{8,24},{9,1... | collective-permute-start | bytes 1376264 | tf_op jit(solution)/shard_map/ppermute | solution.py:169
  38.7 16.1 %collective-permute-start.7 = (bf16[512,512]{1,0:T(8,128)(2,1)S(1)}, bf16[512,512]{1,0:T(8,128)(2,1)S(1)}, u32[]{:S(2)}, u32[]{:S(2)}) collective-permute-start(bf16[512,512]{1,0:T(8,128)(2,1)S(1)} %get-tuple-element.176.refs_0_), channel_id=1, source_target_pairs={{0,4},{1,3},{2,6},{3,1},{4,0},{5,7},{6,2},{7,5},{8,12},{9,11},{10,... | collective-permute-start | bytes 1572872 | tf_op jit(solution)/shard_map/ppermute | solution.py:169
  40.3 10.3 %collective-permute-start.8 = (bf16[448,512]{1,0:T(8,128)(2,1)S(1)}, bf16[448,512]{1,0:T(8,128)(2,1)S(1)}, u32[]{:S(2)}, u32[]{:S(2)}) collective-permute-start(bf16[448,512]{1,0:T(8,128)(2,1)S(1)} %join.9.refs_1_), channel_id=1, source_target_pairs={{0,2},{1,5},{2,0},{3,7},{4,6},{5,1},{6,4},{7,3},{8,10},{9,13},{10,... | collective-permute-start | bytes 1376264 | tf_op jit(solution)/shard_map/ppermute | solution.py:169
  40.9 13.9 %collective-permute-start.9 = (bf16[384,512]{1,0:T(8,128)(2,1)S(1)}, bf16[384,512]{1,0:T(8,128)(2,1)S(1)}, u32[]{:S(2)}, u32[]{:S(2)}) collective-permute-start(bf16[384,512]{1,0:T(8,128)(2,1)S(1)} %get-tuple-element.178.refs_0_), channel_id=1, source_target_pairs={{0,2},{1,5},{2,0},{3,7},{4,6},{5,1},{6,4},{7,3},{8,10},{9,13},{10,... | collective-permute-start | bytes 1179656 | tf_op jit(solution)/shard_map/ppermute | solution.py:169
  42.4 15.3 %collective-permute-start.11 = (bf16[584,512]{1,0:T(8,128)(2,1)S(1)}, bf16[584,512]{1,0:T(8,128)(2,1)S(1)}, u32[]{:S(2)}, u32[]{:S(2)}) collective-permute-start(bf16[584,512]{1,0:T(8,128)(2,1)S(1)} %collective-permute-done.3.refs_6_.refs_7_), channel_id=1, source_target_pairs={{0,1},{1,0},{2,3},{3,2},{4,5},{5,4},{6,7},{7,6},{8,9},{9,8},{10,11... | collective-permute-start | bytes 1794056 | tf_op jit(solution)/shard_map/ppermute | solution.py:161
  54.9 23.3 %collective-permute-start.10 = (bf16[1024,512]{1,0:T(8,128)(2,1)S(1)}, bf16[1024,512]{1,0:T(8,128)(2,1)S(1)}, u32[]{:S(2)}, u32[]{:S(2)}) collective-permute-start(bf16[1024,512]{1,0:T(8,128)(2,1)S(1)} %join.10.refs_1_), channel_id=1, source_target_pairs={{0,2},{1,5},{2,0},{3,7},{4,6},{5,1},{6,4},{7,3},{8,10},{9,13},{10,... | collective-permute-start | bytes 3145736 | tf_op jit(solution)/shard_map/ppermute | solution.py:169
  56.0 22.7 %collective-permute-start.16 = (bf16[768,512]{1,0:T(8,128)(2,1)S(1)}, bf16[768,512]{1,0:T(8,128)(2,1)S(1)}, u32[]{:S(2)}, u32[]{:S(2)}) collective-permute-start(bf16[768,512]{1,0:T(8,128)(2,1)S(1)} %join.11.refs_1_), channel_id=1, source_target_pairs={{0,4},{1,3},{2,6},{3,1},{4,0},{5,7},{6,2},{7,5},{8,12},{9,11},{10,... | collective-permute-start | bytes 2359304 | tf_op jit(solution)/shard_map/ppermute | solution.py:169
  57.7 30.8 %collective-permute-start.14 = (bf16[1024,512]{1,0:T(8,128)(2,1)S(1)}, bf16[1024,512]{1,0:T(8,128)(2,1)S(1)}, u32[]{:S(2)}, u32[]{:S(2)}) collective-permute-start(bf16[1024,512]{1,0:T(8,128)(2,1)S(1)} %join.10.refs_1_), channel_id=1, source_target_pairs={{0,1},{1,0},{2,3},{3,2},{4,5},{5,4},{6,7},{7,6},{8,9},{9,8},{10,11... | collective-permute-start | bytes 3145736 | tf_op jit(solution)/shard_map/ppermute | solution.py:161
  78.2 10.3 %collective-permute-start.15 = (bf16[1024,512]{1,0:T(8,128)(2,1)S(1)}, bf16[1024,512]{1,0:T(8,128)(2,1)S(1)}, u32[]{:S(2)}, u32[]{:S(2)}) collective-permute-start(bf16[1024,512]{1,0:T(8,128)(2,1)S(1)} %collective-permute-done.10.refs_2_), channel_id=1, source_target_pairs={{0,1},{1,0},{2,3},{3,2},{4,5},{5,4},{6,7},{7,6},{8,9},{9,8},{10,11... | collective-permute-start | bytes 3145736 | tf_op jit(solution)/shard_map/ppermute | solution.py:161
  100.9 9.7 %collective-permute-start.20 = (bf16[16,128,512]{2,1,0:T(8,128)(2,1)S(1)}, bf16[16,128,512]{2,1,0:T(8,128)(2,1)S(1)}, u32[]{:S(2)}, u32[]{:S(2)}) collective-permute-start(bf16[16,128,512]{2,1,0:T(8,128)(2,1)S(1)} %get-tuple-element.209), channel_id=1, source_target_pairs={{0,1},{1,0},{2,3},{3,2},{4,5},{5,4},{6,7},{7,6},{8,9},{9,8},{10,11... | collective-permute-start | bytes 6291464 | tf_op jit(solution)/shard_map/ppermute | solution.py:161
  113.5 19.2 %collective-permute-start.23 = (bf16[8,128,512]{2,1,0:T(8,128)(2,1)S(1)}, bf16[8,128,512]{2,1,0:T(8,128)(2,1)S(1)}, u32[]{:S(2)}, u32[]{:S(2)}) collective-permute-start(bf16[8,128,512]{2,1,0:T(8,128)(2,1)S(1)} %get-tuple-element.241), channel_id=1, source_target_pairs={{0,4},{1,3},{2,6},{3,1},{4,0},{5,7},{6,2},{7,5},{8,12},{9,11},{10,... | collective-permute-start | bytes 3145736 | tf_op jit(solution)/shard_map/ppermute | solution.py:169
  121.1 15.1 %collective-permute-start.24 = (bf16[8,96,512]{2,1,0:T(8,128)(2,1)S(1)}, bf16[8,96,512]{2,1,0:T(8,128)(2,1)S(1)}, u32[]{:S(2)}, u32[]{:S(2)}) collective-permute-start(bf16[8,96,512]{2,1,0:T(8,128)(2,1)S(1)} %get-tuple-element.246), channel_id=1, source_target_pairs={{0,2},{1,5},{2,0},{3,7},{4,6},{5,1},{6,4},{7,3},{8,10},{9,13},{10,... | collective-permute-start | bytes 2359304 | tf_op jit(solution)/shard_map/ppermute | solution.py:169
  122.7 13.7 %collective-permute-start.25 = (bf16[512,256]{1,0:T(8,128)(2,1)S(1)}, bf16[512,256]{1,0:T(8,128)(2,1)S(1)}, u32[]{:S(2)}, u32[]{:S(2)}) collective-permute-start(bf16[512,256]{1,0:T(8,128)(2,1)S(1)} %get-tuple-element.255), channel_id=1, source_target_pairs={{0,1},{1,0},{2,3},{3,2},{4,5},{5,4},{6,7},{7,6},{8,9},{9,8},{10,11... | collective-permute-start | bytes 786440 | tf_op jit(solution)/shard_map/ppermute | solution.py:161
  122.7 13.7 %collective-permute-start.26 = (bf16[512,256]{1,0:T(8,128)(2,1)S(1)}, bf16[512,256]{1,0:T(8,128)(2,1)S(1)}, u32[]{:S(2)}, u32[]{:S(2)}) collective-permute-start(bf16[512,256]{1,0:T(8,128)(2,1)S(1)} %get-tuple-element.256), channel_id=1, source_target_pairs={{0,1},{1,0},{2,3},{3,2},{4,5},{5,4},{6,7},{7,6},{8,9},{9,8},{10,11... | collective-permute-start | bytes 786440 | tf_op jit(solution)/shard_map/ppermute | solution.py:161
  138.5 12.1 %collective-permute-start.32 = (bf16[4,128,512]{2,1,0:T(8,128)(2,1)S(1)}, bf16[4,128,512]{2,1,0:T(8,128)(2,1)S(1)}, u32[]{:S(2)}, u32[]{:S(2)}) collective-permute-start(bf16[4,128,512]{2,1,0:T(8,128)(2,1)S(1)} %get-tuple-element.266), channel_id=1, source_target_pairs={{0,2},{1,5},{2,0},{3,7},{4,6},{5,1},{6,4},{7,3},{8,10},{9,13},{10,... | collective-permute-start | bytes 1572872 | tf_op jit(solution)/shard_map/ppermute | solution.py:169
  141.5 16.2 %collective-permute-start.30 = (bf16[8,56,512]{2,1,0:T(8,128)(2,1)}, bf16[8,56,512]{2,1,0:T(8,128)(2,1)S(1)}, u32[]{:S(2)}, u32[]{:S(2)}) collective-permute-start(bf16[8,56,512]{2,1,0:T(8,128)(2,1)} %get-tuple-element.263), channel_id=1, source_target_pairs={{0,4},{1,3},{2,6},{3,1},{4,0},{5,7},{6,2},{7,5},{8,12},{9,11},{10,... | collective-permute-start | bytes 1376264 | tf_op jit(solution)/shard_map/ppermute | solution.py:169
  142.5 13.4 %collective-permute-start.33 = (bf16[4,96,512]{2,1,0:T(8,128)(2,1)S(1)}, bf16[4,96,512]{2,1,0:T(8,128)(2,1)S(1)}, u32[]{:S(2)}, u32[]{:S(2)}) collective-permute-start(bf16[4,96,512]{2,1,0:T(8,128)(2,1)S(1)} %get-tuple-element.267), channel_id=1, source_target_pairs={{0,4},{1,3},{2,6},{3,1},{4,0},{5,7},{6,2},{7,5},{8,12},{9,11},{10,... | collective-permute-start | bytes 1179656 | tf_op jit(solution)/shard_map/ppermute | solution.py:169
  156.1 14.3 %collective-permute-start.34 = (bf16[2,224,512]{2,1,0:T(8,128)(2,1)S(1)}, bf16[2,224,512]{2,1,0:T(8,128)(2,1)S(1)}, u32[]{:S(2)}, u32[]{:S(2)}) collective-permute-start(bf16[2,224,512]{2,1,0:T(8,128)(2,1)S(1)} %get-tuple-element.273), channel_id=1, source_target_pairs={{0,16},{1,9},{2,18},{3,11},{4,20},{5,13},{6,22},{7,15},{8,24},{9,1... | collective-permute-start | bytes 1376264 | tf_op jit(solution)/shard_map/ppermute | solution.py:169
  157.8 13.5 %collective-permute-start.36 = (bf16[4,56,512]{2,1,0:T(8,128)(2,1)S(1)}, bf16[4,56,512]{2,1,0:T(8,128)(2,1)S(1)}, u32[]{:S(2)}, u32[]{:S(2)}) collective-permute-start(bf16[4,56,512]{2,1,0:T(8,128)(2,1)S(1)} %get-tuple-element.280), channel_id=1, source_target_pairs={{0,2},{1,5},{2,0},{3,7},{4,6},{5,1},{6,4},{7,3},{8,10},{9,13},{10,... | collective-permute-start | bytes 688136 | tf_op jit(solution)/shard_map/ppermute | solution.py:169
  159.4 14.7 %collective-permute-start.31 = (bf16[320,512]{1,0:T(8,128)(2,1)}, bf16[320,512]{1,0:T(8,128)(2,1)S(1)}, u32[]{:S(2)}, u32[]{:S(2)}) collective-permute-start(bf16[320,512]{1,0:T(8,128)(2,1)} %copy-done.3), channel_id=1, source_target_pairs={{0,2},{1,3},{2,0},{3,1},{4,6},{5,7},{6,4},{7,5},{8,10},{9,11},{10,... | collective-permute-start | bytes 983048 | tf_op jit(solution)/shard_map/ppermute | solution.py:161
  170.6 10.5 %collective-permute-start.35 = (bf16[1,224,512]{2,1,0:T(8,128)(2,1)S(1)}, bf16[1,224,512]{2,1,0:T(8,128)(2,1)S(1)}, u32[]{:S(2)}, u32[]{:S(2)}) collective-permute-start(bf16[1,224,512]{2,1,0:T(8,128)(2,1)S(1)} %get-tuple-element.275), channel_id=1, source_target_pairs={{0,8},{1,17},{2,10},{3,19},{4,12},{5,21},{6,14},{7,23},{8,0},{9,25... | collective-permute-start | bytes 688136 | tf_op jit(solution)/shard_map/ppermute | solution.py:169
  (20 other events, 116.3 us)

commit v11 on v10

--- a/solution.py
+++ b/solution.py
@@ -161,8 +161,8 @@
     return lax.ppermute(array, AXES, [(i, i ^ mask) for i in range(devices)])
 
 
-Z_FIRST = ((8, 16, 2, 4), (16, 8, 4, 2))
-CROSSED = ((8, 16, 4, 2), (16, 8, 2, 4))
+Z_FIRST = ((8, 24, 2, 4), (24, 8, 4, 2))
+CROSSED = ((8, 24, 4, 2), (24, 8, 2, 4))
 
 
 def turned_swap(array, step, orders=Z_FIRST):
@@ -1034,14 +1034,18 @@
     )
     mixtures, logs = found[:2], found[2:]
     if packed:
-        second_d, third_d = after(second_d, mixtures[0]), after(third_d, mixtures[0])
-        set_cross = [second_c, second_d, swap(second_c, 1, 32), swap(second_d, 1, 32)]
-        set_inner = [third_c, third_d, swap(third_c, 1, 32), swap(third_d, 1, 32)]
+        second_d = after(second_d, mixtures[0])
+        second_e = swap(after(second_c, mixtures[0]), 1, 32)
+        set_cross = [second_c, second_d, second_e, swap(second_d, 1, 32)]
         set_back, set_memory = set_cross, set_cross
     first_sum, second_sum, cross_query, memory_keys, memory_values, cross_t, cross_logs, vectors = run(
         make_cross_forward(packed, rows, block, parts * memory_share, width, narrow, len(set_cross)),
         9.0, "cross_forward", *set_cross, *own_tokens, row_memory, ids, memory_ids, *mixtures,
     )
+    if packed:
+        third_d = after(third_d, second_sum)
+        third_e = swap(after(third_c, mixtures[0]), 1, 32)
+        set_inner = [third_c, third_d, third_e, swap(third_d, 1, 32)]
     out_own, out_send, back2_in, sums_inner, *grads_inner = run(
         make_inner(packed, rows, block, width, hidden, narrow, len(set_inner)), 18.0, "inner",
         *set_inner, second_sum, kept, came, vectors,
@@ -1060,25 +1064,25 @@
     if packed:
         keep, send = combine(after([grads_inner[0], swap(grads_inner[1], 1, 32)], back1, out_came), 2)
         inner_step = [keep, turned_swap(send, 3)]
-        memory_key_own = after(memory_key_own, keep)
-    memory_own, memory_send, *grads_cross = run(
-        make_memory_back(packed, parts, rows, block, memory_block, width, narrow, len(set_memory)),
-        2.0, "memory_back", *set_memory, *own_tokens, memory_key_own, memory_value_own, sums_cross,
-        *grads_early, *memory_received,
-    )
-    if packed:
-        cross_came = swap(grads_cross[1], 1, 32)
-        query[0] = after(query[0], grads_cross[0])
+        query[0] = after(query[0], keep)
     found = run(
         make_self_back_upper(parts, share, width), 7.0, "self_back_upper", query[0], keys[0],
         values[0], slope[0], slope_t[0], logs[0], deltas[0], ids,
     )
     query_upper, own_upper = found[:2]
     received_upper = [swap(a, m // 2 + 1, devices) for m, a in enumerate(found[2:])]
-    if packed:
-        keep_cross, send = combine(after([grads_cross[0], cross_came], query_upper), 2)
+    memory_own, memory_send, *grads_cross = run(
+        make_memory_back(packed, parts, rows, block, memory_block, width, narrow, len(set_memory)),
+        2.0, "memory_back", *set_memory, *own_tokens, after(memory_key_own, query_upper),
+        memory_value_own, sums_cross, *grads_early, *memory_received,
+    )
+    if packed:
+        cross_came = swap(grads_cross[1], 1, 32)
+        keep, send = combine(after(inner_step, grads_cross[0]), 2, 8.0)
+        inner_step = [keep, turned_swap(send, 2)]
+        keep_cross, send = combine(after([grads_cross[0], cross_came], keep), 2)
         cross_step = [keep_cross, turned_swap(send, 3, CROSSED)]
-        query[1] = after(query[1], keep_cross)
+        query[1] = after(query[1], keep, keep_cross)
     in_part, query_sum, query_w_grad, own_lower, *sends = run(
         make_self_back_lower(packed, parts, rows, block, width, narrow, len(set_query)), 11.0,
         "self_back_lower", *set_query, *own_tokens, query[1], keys[1], values[1], slope[1],
@@ -1086,11 +1090,9 @@
     )
     received_lower = [swap(a, m // 2 + 1, devices) for m, a in enumerate(sends)]
     if packed:
-        keep, send = combine(after(inner_step, query_sum), 2)
-        inner_step = [keep, turned_swap(send, 2)]
         keep_cross, send = combine(after(cross_step, query_sum), 2)
         cross_step = [keep_cross, turned_swap(send, 2, CROSSED)]
-        in_part = after(in_part, keep, keep_cross)
+        in_part = after(in_part, keep_cross, inner_step[1])
     in_own, in_send, *grads_last = run(
         make_last(packed, parts, rows, block, memory_block, width, narrow, len(set_last)), 6.0,
         "last", *set_last, *own_tokens, in_part, query_sum, query_w_grad, memory_send, own_upper,
@@ -1101,11 +1103,11 @@
         keep, send = combine([grads_last[0], swap(grads_last[1], 1, 32)], 2)
         last_step = [keep, turned_swap(send, 3)]
         in_send = after(in_send, last_step[1])
-        keep_joint, send = combine_joint(after([inner_step, cross_step], in_own), 2)
+        keep_joint, send = combine_joint(after([inner_step, cross_step], keep), 2)
         joint_step = [keep_joint, turned_swap(send, 1)]
         keep, send = combine(after(last_step, keep_joint), 2)
         last_step = [keep, turned_swap(send, 2)]
-        keep_joint, send = combine(joint_step, 2)
+        keep_joint, send = combine(after(joint_step, keep), 2)
         joint_step = [keep_joint, turned_swap(send, 0)]
         keep, send = combine(after(last_step, keep_joint), 2)
         last_step = [keep, turned_swap(send, 1)]

time: 186 us -> 189 us (1.016)
  waiting for transfers between devices: 81 us -> 90.6 us
  starting transfers between devices: 35.9 us -> 29.7 us
    ppermute x20, waiting for transfers between devices: 73.2 us -> 81.8 us  [turned_swap(): lax.ppermute(array, AXES, [(i, i ^ orders[i % 2][step]) for i in range(32)])]
    ppermute x20, starting transfers between devices: 28.2 us -> 22.5 us  [turned_swap(): lax.ppermute(array, AXES, [(i, i ^ orders[i % 2][step]) for i in range(32)])]
  transfers between devices with their start and end apart: 39 -> 39, of which waited for: 22 -> 20; matrix products, arithmetic and copies ran while one was open for 2% -> 2% of each run, Pallas kernels for 23% -> 22%
where the time goes in v11:
time: 189 us
  waiting for transfers between devices  90.6 us (48%)
  Pallas kernels  60.5 us (32%)
  starting transfers between devices  29.7 us (16%)
  other arithmetic  3.96 us (2%)
  local copies, waits for them, and re-layouts  2.48 us (1%)
    ppermute x20, waiting for transfers between devices, turned_swap(): lax.ppermute(array, AXES, [(i, i ^ orders[i % 2][step]) for i in range(32)])  81.8 us
    pallas_call x13, Pallas kernels, call(): pl.pallas_call(kernel, out_shape=[jax.ShapeDtypeStruct(s, d) for s, d in...  57.6 us
    ppermute x20, starting transfers between devices, turned_swap(): lax.ppermute(array, AXES, [(i, i ^ orders[i % 2][step]) for i in range(32)])  22.5 us
    ppermute x19, waiting for transfers between devices, swap(): return lax.ppermute(array, AXES, [(i, i ^ mask) for i in range(devices)])  8.79 us
    ppermute x19, starting transfers between devices, swap(): return lax.ppermute(array, AXES, [(i, i ^ mask) for i in range(devices)])  7.28 us
  transfers between devices with their start and end apart: 39, of which 20 were waited for; matrix products, arithmetic and copies ran while one was open for 2% of the time, Pallas kernels for 22%

profile of v11, /device:TPU:0, one launch (start us, length us, event | category | flops | bytes accessed | tf_op | source)
XLA Modules:
  0.0 188.5 jit_solution(1723490650379554039)
XLA Ops:
  3.1 3.0 %collective-permute-start.3 = (bf16[584,512]{1,0:T(8,128)(2,1)}, bf16[584,512]{1,0:T(8,128)(2,1)S(1)}, u32[]{:S(2)}, u32[]{:S(2)}) collective-permute-start(bf16[584,512]{1,0:T(8,128)(2,1)} %get-tuple-element.169), channel_id=1, source_target_pairs={{0,2},{1,3},{2,0},{3,1},{4,6},{5,7},{6,4},{7,5},{8,10},{9,11},{10,... | collective-permute-start | bytes 1794056 | tf_op jit(solution)/shard_map/ppermute | solution.py:161
  9.5 2.8 %collective-permute-done.refs_1_ = bf16[56,512]{1,0:T(8,128)(2,1)S(1)} collective-permute-done((bf16[56,512]{1,0:T(8,128)(2,1)}, bf16[56,512]{1,0:T(8,128)(2,1)S(1)}, u32[]{:S(2)}, u32[]{:S(2)}) %collective-permute-start) | collective-permute-done | bytes 57376 | tf_op jit(solution)/shard_map/ppermute | solution.py:169
  14.8 2.5 %collective-permute-start.2 = (bf16[112,512]{1,0:T(8,128)(2,1)S(1)}, bf16[112,512]{1,0:T(8,128)(2,1)S(1)}, u32[]{:S(2)}, u32[]{:S(2)}) collective-permute-start(bf16[112,512]{1,0:T(8,128)(2,1)S(1)} %join.6.refs_0_), channel_id=1, source_target_pairs={{0,24},{1,9},{2,26},{3,11},{4,28},{5,13},{6,30},{7,15},{8,16},{9,1... | collective-permute-start | bytes 344072 | tf_op jit(solution)/shard_map/ppermute | solution.py:169
  17.3 9.1 %collective-permute-done.2.refs_1_ = bf16[112,512]{1,0:T(8,128)(2,1)S(1)} collective-permute-done((bf16[112,512]{1,0:T(8,128)(2,1)S(1)}, bf16[112,512]{1,0:T(8,128)(2,1)S(1)}, u32[]{:S(2)}, u32[]{:S(2)}) %collective-permute-start.2) | collective-permute-done | bytes 114720 | tf_op jit(solution)/shard_map/ppermute | solution.py:169
  30.6 4.5 %collective-permute-done.6.refs_1_ = bf16[224,512]{1,0:T(8,128)(2,1)S(1)} collective-permute-done((bf16[224,512]{1,0:T(8,128)(2,1)S(1)}, bf16[224,512]{1,0:T(8,128)(2,1)S(1)}, u32[]{:S(2)}, u32[]{:S(2)}) %collective-permute-start.6) | collective-permute-done | bytes 229408 | tf_op jit(solution)/shard_map/ppermute | solution.py:169
  35.2 4.6 %collective-permute-done.5.lower = bf16[448,512]{1,0:T(8,128)(2,1)S(1)} collective-permute-done((bf16[448,512]{1,0:T(8,128)(2,1)S(1)}, bf16[448,512]{1,0:T(8,128)(2,1)S(1)}, u32[]{:S(2)}, u32[]{:S(2)}) %collective-permute-start.5) | collective-permute-done | bytes 458784 | tf_op jit(solution)/shard_map/ppermute | solution.py:169
  43.5 6.4 %collective-permute-done.8.refs_2_ = bf16[448,512]{1,0:T(8,128)(2,1)S(1)} collective-permute-done((bf16[448,512]{1,0:T(8,128)(2,1)S(1)}, bf16[448,512]{1,0:T(8,128)(2,1)S(1)}, u32[]{:S(2)}, u32[]{:S(2)}) %collective-permute-start.8) | collective-permute-done | bytes 458784 | tf_op jit(solution)/shard_map/ppermute | solution.py:169
  49.9 6.2 %collective-permute-done.9.refs_1_ = bf16[384,512]{1,0:T(8,128)(2,1)S(1)} collective-permute-done((bf16[384,512]{1,0:T(8,128)(2,1)S(1)}, bf16[384,512]{1,0:T(8,128)(2,1)S(1)}, u32[]{:S(2)}, u32[]{:S(2)}) %collective-permute-start.9) | collective-permute-done | bytes 393248 | tf_op jit(solution)/shard_map/ppermute | solution.py:169
  60.6 8.3 %self_attention.1 = (bf16[256,512]{1,0:T(8,128)(2,1)S(1)}, bf16[256,512]{1,0:T(8,128)(2,1)S(1)}, f32[4,1,512]{2,1,0:T(1,128)S(1)}, f32[4,1,512]{2,1,0:T(1,128)S(1)}) custom-call(s32[1]{0:T(128)} %bitcast.me_ref.refs_0_, bf16[256,512]{1,0:T(8,128)(2,1)S(1)} %get-tuple-element.185.refs_0_, bf16[256,512]{1,0:T(8,128)(2,1)S(1)} %get-tuple-element.186.refs_1_, ...), custom_call_target="tpu_custom_call" | custom-call | flops 1 | bytes 1 | tf_op jit(solution)/shard_map/self_attention/pallas_call | solution.py:255
  69.1 7.6 %collective-permute-done.11.refs_2_ = bf16[768,512]{1,0:T(8,128)(2,1)S(1)} collective-permute-done((bf16[768,512]{1,0:T(8,128)(2,1)S(1)}, bf16[768,512]{1,0:T(8,128)(2,1)S(1)}, u32[]{:S(2)}, u32[]{:S(2)}) %collective-permute-start.11) | collective-permute-done | bytes 786464 | tf_op jit(solution)/shard_map/ppermute | solution.py:169
  79.0 5.4 %cross_forward.1 = (f32[512,512]{1,0:T(8,128)S(1)}, f32[512,512]{1,0:T(8,128)S(1)}, bf16[512,512]{1,0:T(8,128)(2,1)S(1)}, bf16[256,512]{1,0:T(8,128)(2,1)S(1)}, ...) custom-call(s32[1]{0:T(128)} %bitcast.me_ref.refs_0_, ...), custom_call_target="tpu_custom_call" | custom-call | flops 1 | bytes 1 | tf_op jit(solution)/shard_map/cross_forward/pallas_call | solution.py:255
  84.5 2.5 %collective-permute-done.18.refs_4_ = bf16[1024,512]{1,0:T(8,128)(2,1)S(1)} collective-permute-done((bf16[1024,512]{1,0:T(8,128)(2,1)S(1)}, bf16[1024,512]{1,0:T(8,128)(2,1)S(1)}, u32[]{:S(2)}, u32[]{:S(2)}) %collective-permute-start.18) | collective-permute-done | bytes 1048608 | tf_op jit(solution)/shard_map/ppermute | solution.py:161
  87.1 12.4 %inner.1 = (f32[256,512]{1,0:T(8,128)S(1)}, bf16[256,512]{1,0:T(8,128)(2,1)S(1)}, f32[512,512]{1,0:T(8,128)S(1)}, f32[8,512]{1,0:T(8,128)S(1)}, bf16[16,128,512]...) custom-call(s32[1]{0:T(128)} %bitcast.me_ref.refs_0_, bf16[1024,512]{1,0:T(8,128)(2,1)S(1)} %join.10.refs_1_, ...), custom_call_target="tpu_custom_call" | custom-call | flops 1 | bytes 1 | tf_op jit(solution)/shard_map/inner/pallas_call | solution.py:255
  99.7 8.4 %cross_back.1 = (f32[512,512]{1,0:T(8,128)S(1)}, f32[128,512]{1,0:T(8,128)S(1)}, f32[128,512]{1,0:T(8,128)S(1)}, f32[16,512]{1,0:T(8,128)S(1)}, bf16[512,256]{1,...) custom-call(s32[1]{0:T(128)} %bitcast.me_ref.refs_0_, ...), custom_call_target="tpu_custom_call" | custom-call | flops 1 | bytes 1 | tf_op jit(solution)/shard_map/cross_back/pallas_call | solution.py:255
  110.6 6.1 %self_back_upper.1 = (bf16[512,256]{1,0:T(8,128)(2,1)S(1)}, f32[1024,256]{1,0:T(8,128)S(1)}, bf16[512,256]{1,0:T(8,128)(2,1)S(1)}, bf16[512,256]{1,0:T(8,128)(2,1)S(1)}) custom-call(s32[1]{0:T(128)} %bitcast.me_ref.refs_0_, bf16[512,256]{1,0:T(8,128)(2,1)S(1)} %get-tuple-element.222.refs_1_, bf16[1024,256]{1,0:T(8,128)(2,1)S(1)} %get-tuple-element.187.refs_2_, ...), custom_call_target="tpu_custom_call" | custom-call | flops 1 | bytes 1 | tf_op jit(solution)/shard_map/self_back_upper/pallas_call | solution.py:255
  118.1 5.6 %collective-permute-done.21.refs_1_ = bf16[8,128,512]{2,1,0:T(8,128)(2,1)S(1)} collective-permute-done((bf16[8,128,512]{2,1,0:T(8,128)(2,1)S(1)}, bf16[8,128,512]{2,1,0:T(8,128)(2,1)S(1)}, u32[]{:S(2)}, u32[]{:S(2)}) %collective-permute-start.21) | collective-permute-done | bytes 1048608 | tf_op jit(solution)/shard_map/ppermute | solution.py:169
  127.0 7.1 %self_back_lower.1 = (f32[512,512]{1,0:T(8,128)S(1)}, f32[8,512]{1,0:T(8,128)S(1)}, bf16[512,512]{1,0:T(8,128)(2,1)S(1)}, f32[1024,256]{1,0:T(8,128)S(1)}, bf16[...) custom-call(s32[1]{0:T(128)} %bitcast.me_ref.refs_0_, bf16[448,512]{1,0:T(8,128)(2,1)S(1)} %join.9.refs_1_, ...), custom_call_target="tpu_custom_call" | custom-call | flops 1 | bytes 1 | tf_op jit(solution)/shard_map/self_back_lower/pallas_call | solution.py:255
  136.6 5.4 %collective-permute-done.25.refs_1_ = bf16[4,128,512]{2,1,0:T(8,128)(2,1)S(1)} collective-permute-done((bf16[4,128,512]{2,1,0:T(8,128)(2,1)S(1)}, bf16[4,128,512]{2,1,0:T(8,128)(2,1)S(1)}, u32[]{:S(2)}, u32[]{:S(2)}) %collective-permute-start.25) | collective-permute-done | bytes 524320 | tf_op jit(solution)/shard_map/ppermute | solution.py:169
  143.7 2.5 %collective-permute-done.30.refs_1_ = bf16[16,56,512]{2,1,0:T(8,128)(2,1)S(1)} collective-permute-done((bf16[16,56,512]{2,1,0:T(8,128)(2,1)S(1)}, bf16[16,56,512]{2,1,0:T(8,128)(2,1)S(1)}, u32[]{:S(2)}, u32[]{:S(2)}) %collective-permute-start.30) | collective-permute-done | bytes 917536 | tf_op jit(solution)/shard_map/ppermute | solution.py:161
  149.1 10.9 %collective-permute-done.33.refs_3_ = bf16[4,96,512]{2,1,0:T(8,128)(2,1)S(1)} collective-permute-done((bf16[4,96,512]{2,1,0:T(8,128)(2,1)S(1)}, bf16[4,96,512]{2,1,0:T(8,128)(2,1)S(1)}, u32[]{:S(2)}, u32[]{:S(2)}) %collective-permute-start.33) | collective-permute-done | bytes 393248 | tf_op jit(solution)/shard_map/ppermute | solution.py:169
  164.6 6.1 %collective-permute-done.34.refs_1_ = bf16[2,224,512]{2,1,0:T(8,128)(2,1)S(1)} collective-permute-done((bf16[2,224,512]{2,1,0:T(8,128)(2,1)S(1)}, bf16[2,224,512]{2,1,0:T(8,128)(2,1)S(1)}, u32[]{:S(2)}, u32[]{:S(2)}) %collective-permute-start.34) | collective-permute-done | bytes 458784 | tf_op jit(solution)/shard_map/ppermute | solution.py:169
  171.0 3.5 %collective-permute-start.37 = (bf16[2,56,512]{2,1,0:T(8,128)(2,1)S(1)}, bf16[2,56,512]{2,1,0:T(8,128)(2,1)S(1)}, u32[]{:S(2)}, u32[]{:S(2)}) collective-permute-start(bf16[2,56,512]{2,1,0:T(8,128)(2,1)S(1)} %get-tuple-element.292), channel_id=1, source_target_pairs={{0,24},{1,9},{2,26},{3,11},{4,28},{5,13},{6,30},{7,15},{8,16},{9,1... | collective-permute-start | bytes 344072 | tf_op jit(solution)/shard_map/ppermute | solution.py:169
  175.7 6.7 %collective-permute-done.37.refs_1_ = bf16[2,56,512]{2,1,0:T(8,128)(2,1)S(1)} collective-permute-done((bf16[2,56,512]{2,1,0:T(8,128)(2,1)S(1)}, bf16[2,56,512]{2,1,0:T(8,128)(2,1)S(1)}, u32[]{:S(2)}, u32[]{:S(2)}) %collective-permute-start.37) | collective-permute-done | bytes 114720 | tf_op jit(solution)/shard_map/ppermute | solution.py:169
  183.3 3.4 %collective-permute-done.38.refs_3_ = bf16[1,56,512]{2,1,0:T(8,128)(2,1)S(1)} collective-permute-done((bf16[1,56,512]{2,1,0:T(8,128)(2,1)S(1)}, bf16[1,56,512]{2,1,0:T(8,128)(2,1)S(1)}, u32[]{:S(2)}, u32[]{:S(2)}) %collective-permute-start.38) | collective-permute-done | bytes 57376 | tf_op jit(solution)/shard_map/ppermute | solution.py:169
  (100 shorter events, 46.2 us)
Async XLA Ops:
  3.1 23.3 %collective-permute-start.3 = (bf16[584,512]{1,0:T(8,128)(2,1)}, bf16[584,512]{1,0:T(8,128)(2,1)S(1)}, u32[]{:S(2)}, u32[]{:S(2)}) collective-permute-start(bf16[584,512]{1,0:T(8,128)(2,1)} %get-tuple-element.169), channel_id=1, source_target_pairs={{0,2},{1,3},{2,0},{3,1},{4,6},{5,7},{6,4},{7,5},{8,10},{9,11},{10,... | collective-permute-start | bytes 1794056 | tf_op jit(solution)/shard_map/ppermute | solution.py:161
  6.0 20.4 %collective-permute-start.4 = (bf16[584,512]{1,0:T(8,128)(2,1)}, bf16[584,512]{1,0:T(8,128)(2,1)S(1)}, u32[]{:S(2)}, u32[]{:S(2)}) collective-permute-start(bf16[584,512]{1,0:T(8,128)(2,1)} %get-tuple-element.172.refs_5_.refs_6_), channel_id=1, source_target_pairs={{0,1},{1,0},{2,3},{3,2},{4,5},{5,4},{6,7},{7,6},{8,9},{9,8},{10,11... | collective-permute-start | bytes 1794056 | tf_op jit(solution)/shard_map/ppermute | solution.py:161
  13.2 13.2 %collective-permute-start.1 = (bf16[224,512]{1,0:T(8,128)(2,1)}, bf16[224,512]{1,0:T(8,128)(2,1)S(1)}, u32[]{:S(2)}, u32[]{:S(2)}) collective-permute-start(bf16[224,512]{1,0:T(8,128)(2,1)} %get-tuple-element.173.refs_0_), channel_id=1, source_target_pairs={{0,8},{1,25},{2,10},{3,27},{4,12},{5,29},{6,14},{7,31},{8,0},{9,17... | collective-permute-start | bytes 688136 | tf_op jit(solution)/shard_map/ppermute | solution.py:169
  14.8 11.6 %collective-permute-start.2 = (bf16[112,512]{1,0:T(8,128)(2,1)S(1)}, bf16[112,512]{1,0:T(8,128)(2,1)S(1)}, u32[]{:S(2)}, u32[]{:S(2)}) collective-permute-start(bf16[112,512]{1,0:T(8,128)(2,1)S(1)} %join.6.refs_0_), channel_id=1, source_target_pairs={{0,24},{1,9},{2,26},{3,11},{4,28},{5,13},{6,30},{7,15},{8,16},{9,1... | collective-permute-start | bytes 344072 | tf_op jit(solution)/shard_map/ppermute | solution.py:169
  27.4 12.3 %collective-permute-start.5 = (bf16[448,512]{1,0:T(8,128)(2,1)S(1)}, bf16[448,512]{1,0:T(8,128)(2,1)S(1)}, u32[]{:S(2)}, u32[]{:S(2)}) collective-permute-start(bf16[448,512]{1,0:T(8,128)(2,1)S(1)} %join.7.upper), channel_id=1, source_target_pairs={{0,24},{1,9},{2,26},{3,11},{4,28},{5,13},{6,30},{7,15},{8,16},{9,1... | collective-permute-start | bytes 1376264 | tf_op jit(solution)/shard_map/ppermute | solution.py:169
  39.8 16.4 %collective-permute-start.7 = (bf16[512,512]{1,0:T(8,128)(2,1)S(1)}, bf16[512,512]{1,0:T(8,128)(2,1)S(1)}, u32[]{:S(2)}, u32[]{:S(2)}) collective-permute-start(bf16[512,512]{1,0:T(8,128)(2,1)S(1)} %get-tuple-element.180.refs_0_), channel_id=1, source_target_pairs={{0,4},{1,3},{2,6},{3,1},{4,0},{5,7},{6,2},{7,5},{8,12},{9,11},{10,... | collective-permute-start | bytes 1572872 | tf_op jit(solution)/shard_map/ppermute | solution.py:169
  42.0 14.2 %collective-permute-start.9 = (bf16[384,512]{1,0:T(8,128)(2,1)S(1)}, bf16[384,512]{1,0:T(8,128)(2,1)S(1)}, u32[]{:S(2)}, u32[]{:S(2)}) collective-permute-start(bf16[384,512]{1,0:T(8,128)(2,1)S(1)} %get-tuple-element.182.refs_0_), channel_id=1, source_target_pairs={{0,2},{1,5},{2,0},{3,7},{4,6},{5,1},{6,4},{7,3},{8,10},{9,13},{10,... | collective-permute-start | bytes 1179656 | tf_op jit(solution)/shard_map/ppermute | solution.py:169
  43.5 13.0 %collective-permute-start.12 = (bf16[584,512]{1,0:T(8,128)(2,1)S(1)}, bf16[584,512]{1,0:T(8,128)(2,1)S(1)}, u32[]{:S(2)}, u32[]{:S(2)}) collective-permute-start(bf16[584,512]{1,0:T(8,128)(2,1)S(1)} %collective-permute-done.3.refs_6_.refs_7_), channel_id=1, source_target_pairs={{0,1},{1,0},{2,3},{3,2},{4,5},{5,4},{6,7},{7,6},{8,9},{9,8},{10,11... | collective-permute-start | bytes 1794056 | tf_op jit(solution)/shard_map/ppermute | solution.py:161
  56.2 20.4 %collective-permute-start.11 = (bf16[768,512]{1,0:T(8,128)(2,1)S(1)}, bf16[768,512]{1,0:T(8,128)(2,1)S(1)}, u32[]{:S(2)}, u32[]{:S(2)}) collective-permute-start(bf16[768,512]{1,0:T(8,128)(2,1)S(1)} %join.11.refs_1_), channel_id=1, source_target_pairs={{0,4},{1,3},{2,6},{3,1},{4,0},{5,7},{6,2},{7,5},{8,12},{9,11},{10,... | collective-permute-start | bytes 2359304 | tf_op jit(solution)/shard_map/ppermute | solution.py:169
  57.0 27.3 %collective-permute-start.10 = (bf16[1024,512]{1,0:T(8,128)(2,1)S(1)}, bf16[1024,512]{1,0:T(8,128)(2,1)S(1)}, u32[]{:S(2)}, u32[]{:S(2)}) collective-permute-start(bf16[1024,512]{1,0:T(8,128)(2,1)S(1)} %join.10.refs_1_), channel_id=1, source_target_pairs={{0,2},{1,5},{2,0},{3,7},{4,6},{5,1},{6,4},{7,3},{8,10},{9,13},{10,... | collective-permute-start | bytes 3145736 | tf_op jit(solution)/shard_map/ppermute | solution.py:169
  99.5 8.8 %collective-permute-start.20 = (bf16[16,128,512]{2,1,0:T(8,128)(2,1)S(1)}, bf16[16,128,512]{2,1,0:T(8,128)(2,1)S(1)}, u32[]{:S(2)}, u32[]{:S(2)}) collective-permute-start(bf16[16,128,512]{2,1,0:T(8,128)(2,1)S(1)} %get-tuple-element.206), channel_id=1, source_target_pairs={{0,1},{1,0},{2,3},{3,2},{4,5},{5,4},{6,7},{7,6},{8,9},{9,8},{10,11... | collective-permute-start | bytes 6291464 | tf_op jit(solution)/shard_map/ppermute | solution.py:161
  99.7 8.6 %collective-permute-start.19 = (bf16[256,512]{1,0:T(8,128)(2,1)S(1)}, bf16[256,512]{1,0:T(8,128)(2,1)S(1)}, u32[]{:S(2)}, u32[]{:S(2)}) collective-permute-start(bf16[256,512]{1,0:T(8,128)(2,1)S(1)} %get-tuple-element.203), channel_id=1, source_target_pairs={{0,2},{1,3},{2,0},{3,1},{4,6},{5,7},{6,4},{7,5},{8,10},{9,11},{10,... | collective-permute-start | bytes 786440 | tf_op jit(solution)/shard_map/ppermute | solution.py:161
  109.0 14.8 %collective-permute-start.21 = (bf16[8,128,512]{2,1,0:T(8,128)(2,1)S(1)}, bf16[8,128,512]{2,1,0:T(8,128)(2,1)S(1)}, u32[]{:S(2)}, u32[]{:S(2)}) collective-permute-start(bf16[8,128,512]{2,1,0:T(8,128)(2,1)S(1)} %get-tuple-element.219), channel_id=1, source_target_pairs={{0,4},{1,3},{2,6},{3,1},{4,0},{5,7},{6,2},{7,5},{8,12},{9,11},{10,... | collective-permute-start | bytes 3145736 | tf_op jit(solution)/shard_map/ppermute | solution.py:169
  124.4 12.1 %collective-permute-start.24 = (bf16[8,96,512]{2,1,0:T(8,128)(2,1)S(1)}, bf16[8,96,512]{2,1,0:T(8,128)(2,1)S(1)}, u32[]{:S(2)}, u32[]{:S(2)}) collective-permute-start(bf16[8,96,512]{2,1,0:T(8,128)(2,1)S(1)} %get-tuple-element.251), channel_id=1, source_target_pairs={{0,2},{1,5},{2,0},{3,7},{4,6},{5,1},{6,4},{7,3},{8,10},{9,13},{10,... | collective-permute-start | bytes 2359304 | tf_op jit(solution)/shard_map/ppermute | solution.py:169
  126.3 15.8 %collective-permute-start.25 = (bf16[4,128,512]{2,1,0:T(8,128)(2,1)S(1)}, bf16[4,128,512]{2,1,0:T(8,128)(2,1)S(1)}, u32[]{:S(2)}, u32[]{:S(2)}) collective-permute-start(bf16[4,128,512]{2,1,0:T(8,128)(2,1)S(1)} %get-tuple-element.256), channel_id=1, source_target_pairs={{0,2},{1,5},{2,0},{3,7},{4,6},{5,1},{6,4},{7,3},{8,10},{9,13},{10,... | collective-permute-start | bytes 1572872 | tf_op jit(solution)/shard_map/ppermute | solution.py:169
  126.5 15.6 %collective-permute-start.26 = (bf16[512,256]{1,0:T(8,128)(2,1)S(1)}, bf16[512,256]{1,0:T(8,128)(2,1)S(1)}, u32[]{:S(2)}, u32[]{:S(2)}) collective-permute-start(bf16[512,256]{1,0:T(8,128)(2,1)S(1)} %get-tuple-element.262), channel_id=1, source_target_pairs={{0,1},{1,0},{2,3},{3,2},{4,5},{5,4},{6,7},{7,6},{8,9},{9,8},{10,11... | collective-permute-start | bytes 786440 | tf_op jit(solution)/shard_map/ppermute | solution.py:161
  126.5 15.6 %collective-permute-start.27 = (bf16[512,256]{1,0:T(8,128)(2,1)S(1)}, bf16[512,256]{1,0:T(8,128)(2,1)S(1)}, u32[]{:S(2)}, u32[]{:S(2)}) collective-permute-start(bf16[512,256]{1,0:T(8,128)(2,1)S(1)} %get-tuple-element.263), channel_id=1, source_target_pairs={{0,1},{1,0},{2,3},{3,2},{4,5},{5,4},{6,7},{7,6},{8,9},{9,8},{10,11... | collective-permute-start | bytes 786440 | tf_op jit(solution)/shard_map/ppermute | solution.py:161
  147.1 13.2 %collective-permute-start.31 = (bf16[8,56,512]{2,1,0:T(8,128)(2,1)}, bf16[8,56,512]{2,1,0:T(8,128)(2,1)S(1)}, u32[]{:S(2)}, u32[]{:S(2)}) collective-permute-start(bf16[8,56,512]{2,1,0:T(8,128)(2,1)} %get-tuple-element.270), channel_id=1, source_target_pairs={{0,4},{1,3},{2,6},{3,1},{4,0},{5,7},{6,2},{7,5},{8,12},{9,11},{10,... | collective-permute-start | bytes 1376264 | tf_op jit(solution)/shard_map/ppermute | solution.py:169
  147.1 12.9 %collective-permute-start.33 = (bf16[4,96,512]{2,1,0:T(8,128)(2,1)S(1)}, bf16[4,96,512]{2,1,0:T(8,128)(2,1)S(1)}, u32[]{:S(2)}, u32[]{:S(2)}) collective-permute-start(bf16[4,96,512]{2,1,0:T(8,128)(2,1)S(1)} %get-tuple-element.273), channel_id=1, source_target_pairs={{0,4},{1,3},{2,6},{3,1},{4,0},{5,7},{6,2},{7,5},{8,12},{9,11},{10,... | collective-permute-start | bytes 1179656 | tf_op jit(solution)/shard_map/ppermute | solution.py:169
  160.2 10.5 %collective-permute-start.34 = (bf16[2,224,512]{2,1,0:T(8,128)(2,1)S(1)}, bf16[2,224,512]{2,1,0:T(8,128)(2,1)S(1)}, u32[]{:S(2)}, u32[]{:S(2)}) collective-permute-start(bf16[2,224,512]{2,1,0:T(8,128)(2,1)S(1)} %get-tuple-element.280), channel_id=1, source_target_pairs={{0,24},{1,9},{2,26},{3,11},{4,28},{5,13},{6,30},{7,15},{8,16},{9,1... | collective-permute-start | bytes 1376264 | tf_op jit(solution)/shard_map/ppermute | solution.py:169
  160.4 10.5 %collective-permute-start.36 = (bf16[4,56,512]{2,1,0:T(8,128)(2,1)S(1)}, bf16[4,56,512]{2,1,0:T(8,128)(2,1)S(1)}, u32[]{:S(2)}, u32[]{:S(2)}) collective-permute-start(bf16[4,56,512]{2,1,0:T(8,128)(2,1)S(1)} %get-tuple-element.288), channel_id=1, source_target_pairs={{0,2},{1,5},{2,0},{3,7},{4,6},{5,1},{6,4},{7,3},{8,10},{9,13},{10,... | collective-permute-start | bytes 688136 | tf_op jit(solution)/shard_map/ppermute | solution.py:169
  162.4 12.2 %collective-permute-start.32 = (bf16[320,512]{1,0:T(8,128)(2,1)}, bf16[320,512]{1,0:T(8,128)(2,1)S(1)}, u32[]{:S(2)}, u32[]{:S(2)}) collective-permute-start(bf16[320,512]{1,0:T(8,128)(2,1)} %copy-done.3), channel_id=1, source_target_pairs={{0,2},{1,3},{2,0},{3,1},{4,6},{5,7},{6,4},{7,5},{8,10},{9,11},{10,... | collective-permute-start | bytes 983048 | tf_op jit(solution)/shard_map/ppermute | solution.py:161
  170.8 12.4 %collective-permute-start.35 = (bf16[1,224,512]{2,1,0:T(8,128)(2,1)S(1)}, bf16[1,224,512]{2,1,0:T(8,128)(2,1)S(1)}, u32[]{:S(2)}, u32[]{:S(2)}) collective-permute-start(bf16[1,224,512]{2,1,0:T(8,128)(2,1)S(1)} %get-tuple-element.287), channel_id=1, source_target_pairs={{0,8},{1,25},{2,10},{3,27},{4,12},{5,29},{6,14},{7,31},{8,0},{9,17... | collective-permute-start | bytes 688136 | tf_op jit(solution)/shard_map/ppermute | solution.py:169
  171.0 11.4 %collective-permute-start.37 = (bf16[2,56,512]{2,1,0:T(8,128)(2,1)S(1)}, bf16[2,56,512]{2,1,0:T(8,128)(2,1)S(1)}, u32[]{:S(2)}, u32[]{:S(2)}) collective-permute-start(bf16[2,56,512]{2,1,0:T(8,128)(2,1)S(1)} %get-tuple-element.292), channel_id=1, source_target_pairs={{0,24},{1,9},{2,26},{3,11},{4,28},{5,13},{6,30},{7,15},{8,16},{9,1... | collective-permute-start | bytes 344072 | tf_op jit(solution)/shard_map/ppermute | solution.py:169
  (20 other events, 116.8 us)

commit v12 on v8

--- a/solution.py
+++ b/solution.py
@@ -161,11 +161,20 @@
     return lax.ppermute(array, AXES, [(i, i ^ mask) for i in range(devices)])
 
 
-ORDERS = ((8, 16, 2, 4), (16, 8, 4, 2))
+PLANE = (0, 2, 4, 6)
+TURNS = ((8, 24), (24, 8))
+
+
+def exchanged(array):
+    return [array] + [swap(array, mask, 32) for mask in PLANE[1:]]
+
+
+def handed(arrays):
+    return [arrays[0]] + [swap(array, mask, 32) for array, mask in zip(arrays[1:], PLANE[1:])]
 
 
 def turned_swap(array, step):
-    return lax.ppermute(array, AXES, [(i, i ^ ORDERS[i % 2][step]) for i in range(32)])
+    return lax.ppermute(array, AXES, [(i, i ^ TURNS[i % 2][step]) for i in range(32)])
 
 
 def after(value, *others):
@@ -176,29 +185,26 @@
     found = []
     for core in range(2):
         even = ((me & 1) ^ core) == 0
-        masks = [jnp.where(even, first, second) for first, second in zip(*ORDERS)]
-        for far in range(2):
-            for slot in range(8):
-                device = me ^ core if core else me
-                for step, bit in enumerate((slot & 1, slot & 2, slot & 4, far)):
-                    if bit:
-                        device = device ^ masks[step]
-                found.append((core, far, slot, device))
+        lines = (0, jnp.where(even, 8, 24), jnp.where(even, 24, 8), 16)
+        for i, plane in enumerate(PLANE):
+            for j, line in enumerate(lines):
+                device = me ^ (core | plane) if core | plane else me
+                found.append((core, i, j, device ^ line if j else device))
     return found
 
 
 def unpack(me, pieces, stride, first, rows, scratch):
-    for core, far, slot, device in places(me):
-        ref = pieces[2 * core + far]
-        at = slot * stride + first
-        scratch[pl.ds(pl.multiple_of(device * rows, rows), rows), :] = ref[at : at + rows, :]
+    for core, plane, line, device in places(me):
+        at = line * stride + first
+        found = pieces[4 * core + plane][at : at + rows, :]
+        scratch[pl.ds(pl.multiple_of(device * rows, rows), rows), :] = found
 
 
 def vector_sum(pieces, stride, first):
     found = None
     for ref in pieces:
-        for slot in range(8):
-            part = ref[slot * stride + first : (slot + 1) * stride, :].astype(F32)
+        for line in range(4):
+            part = ref[line * stride + first : (line + 1) * stride, :].astype(F32)
             found = part if found is None else found + part
     return found
 
@@ -213,9 +219,9 @@
             return
         self.dense[...] = grad
         rows = self.rows
-        for core, far, slot, device in places(self.me):
+        for core, plane, line, device in places(self.me):
             found = self.dense[pl.ds(pl.multiple_of(device * rows, rows), rows), :]
-            self.refs[core][far * 8 + slot, index * rows : (index + 1) * rows, :] = found.astype(BF16)
+            self.refs[core][plane * 4 + line, index * rows : (index + 1) * rows, :] = found.astype(BF16)
 
     def put_sums(self, first, sums):
         if self.dense is None:
@@ -231,6 +237,9 @@
     if packed:
         return [((16, count * rows + sums, width), BF16)] * 2
     return [((width, width), F32)] * count + [((sums, width), F32)]
+
+
+COSTS = {}
 
 
 def padded(shape, dtype):
@@ -256,7 +265,7 @@
         scratch_shapes=[pltpu.VMEM(s, d) for s, d in scratch],
         compiler_params=pltpu.CompilerParams(vmem_limit_bytes=min(need + (room << 20), 58 << 20)),
         cost_estimate=pl.CostEstimate(
-            flops=1, bytes_accessed=1, transcendentals=0
+            flops=int(COSTS.get(name, 0) * 1.15e9) + 1, bytes_accessed=1, transcendentals=0
         ),
         name=name,
     )(*args)
@@ -296,15 +305,16 @@
     tall = blocks * narrow
 
     def kernel(me_ref, *refs):
-        weights, inner, outer, short, wide = refs[:8], refs[8], refs[9], refs[10], refs[11]
-        first, rest = refs[12:]
+        weights, inner, outer, wide, short = refs[:8], refs[8], refs[9], refs[10], refs[11:24]
+        first, rest = refs[24:]
         me, middle = me_ref[0], 5 * narrow + 16
         for i, ref in enumerate(weights):
             if i < 3:
                 first[i * narrow : (i + 1) * narrow, :] = ref[...]
             else:
                 rest[(i - 3) * narrow : (i - 2) * narrow, :] = ref[...]
-        found = placed(me, short[...], width)
+        short = jnp.concatenate([ref[...].astype(F32) for ref in short], axis=0).astype(BF16)
+        found = placed(me, short, width)
         first[3 * narrow :, :] = jnp.concatenate([found[:2, :], jnp.zeros((6, width), F32)], axis=0).astype(BF16)
         per = width // wide.shape[1]
         row = placed(lax.rem(me, per), wide[...], width)
@@ -492,8 +502,8 @@
         if packed:
             inner_w, outer_w, gathered, dense = scratch[4:8]
             tall = blocks * narrow
-            for core, far, slot, device in places(me_ref[0]):
-                ref, at = pieces[2 * core + far], slot * 2 * tall
+            for core, plane, line, device in places(me_ref[0]):
+                ref, at = pieces[4 * core + plane], line * 2 * tall
                 row = pl.multiple_of(device * narrow, narrow)
                 for i in range(blocks):
                     inner_w[i, pl.ds(row, narrow), :] = ref[at + i * narrow : at + (i + 1) * narrow, :]
@@ -543,9 +553,9 @@
                 dense[...] = inner_grad
                 gathered[i] = outer_grad.astype(BF16)
                 here = pl.ds(pl.multiple_of(i * narrow, narrow), narrow)
-                for core, far, slot, device in places(me_ref[0]):
+                for core, plane, line, device in places(me_ref[0]):
                     row = pl.multiple_of(device * narrow, narrow)
-                    grads[core][far * 8 + slot, here, :] = dense[pl.ds(row, narrow), :].astype(BF16)
+                    grads[core][plane * 4 + line, here, :] = dense[pl.ds(row, narrow), :].astype(BF16)
             else:
                 grads[0][i] = inner_grad
                 grads[1][i] = outer_grad
@@ -554,9 +564,9 @@
         lax.fori_loop(0, blocks, backward, 0)
         if packed:
             tall = blocks * narrow
-            for core, far, slot, device in places(me_ref[0]):
+            for core, plane, line, device in places(me_ref[0]):
                 row = pl.multiple_of(lax.rem(device, per) * tall, tall)
-                grads[core][far * 8 + slot, tall:, :] = gathered[lax.div(device, per), pl.ds(row, tall), :]
+                grads[core][plane * 4 + line, tall:, :] = gathered[lax.div(device, per), pl.ds(row, tall), :]
 
     outs = [((block, width), F32), ((block, width), BF16), ((share, width), F32), ((8, width), F32)]
     if packed:
@@ -926,9 +936,9 @@
         kernel, outs, *scratch = made
         return call(kernel, outs, (me_array,) + args, scratch[0] if scratch else [], micros, name, room)
 
-    short = jnp.stack([query_bias, value_bias, output_bias, attention_gain, attention_shift,
-                       source_query_bias, source_value_bias, source_output_bias, source_gain,
-                       source_shift, outer_bias, final_gain, final_shift])
+    short = [query_bias, value_bias, output_bias, attention_gain, attention_shift, source_query_bias,
+             source_value_bias, source_output_bias, source_gain, source_shift, outer_bias, final_gain,
+             final_shift]
 
     def whole(array):
         return lax.all_gather(array, AXES, axis=0, tiled=True)
@@ -948,7 +958,7 @@
         first, rest = run(make_weights_packet(narrow, width, blocks), 1.0, "weights_packet",
                           query_weight, key_weight, value_weight, output_weight, source_query,
                           source_key, source_value, source_output, inner_weight, outer_weight,
-                          short, inner_bias.reshape(1, wide), room=58)
+                          inner_bias.reshape(1, wide), *[v.reshape(1, narrow) for v in short], room=58)
         first = after(first, sent)
         first = join([first, turned_swap(first, 0)])
         first_b = turned_swap(first, 1)
@@ -956,15 +966,14 @@
         rest_b = turned_swap(rest, 0)
         first = join(after([first, first_b], rest_b))
         rest = join(after([rest, rest_b], first_b, came, *kept_swaps))
-        first_b, rest_b = turned_swap(first, 2), turned_swap(rest, 1)
-        first_c = join([first, first_b])
-        first_d = turned_swap(first_c, 3)
-        second, third = run(make_part((5 * narrow + 16, 2 * blocks * narrow), width), 1.0, "part", rest, rest_b)
-        second_b, third_b = turned_swap(second, 2), turned_swap(third, 2)
-        second_c = join([second, second_b])
-        second_d = turned_swap(second_c, 3)
-        first_d = after(first_d, second_c, *came_swaps)
-        set_self = [first_c, first_d, swap(first_c, 1, 32), swap(first_d, 1, 32)]
+        first_plane, rest_b = exchanged(first), turned_swap(rest, 1)
+        second, third = run(
+            make_part((5 * narrow + 16, 2 * blocks * narrow), width), 1.0, "part", rest,
+            after(rest_b, first_plane[1:]),
+        )
+        first_plane[1:] = after(first_plane[1:], rest_b, *came_swaps)
+        set_self = first_plane + [swap(a, 1, 32) for a in first_plane]
+        second_plane = exchanged(second)
     else:
         full = [whole(w) for w in (query_weight, key_weight, value_weight, output_weight, source_query, source_key, source_value, source_output)]
         lane = lax.broadcasted_iota(jnp.int32, (1, width), 1)
@@ -974,7 +983,7 @@
         def natural(rows):
             return jnp.where(lane // narrow == me, jnp.tile(rows, (1, devices)), 0)
 
-        vectors = jnp.concatenate([natural(short[:2]), jnp.zeros((6, width), BF16), natural(short[2:]), spread_wide, jnp.zeros((1, width), BF16)])
+        vectors = jnp.concatenate([natural(jnp.stack(short[:2])), jnp.zeros((6, width), BF16), natural(jnp.stack(short[2:])), spread_wide, jnp.zeros((1, width), BF16)])
         vectors = reduce_all(vectors, devices).astype(F32)
         set_self = full[:3] + [vectors[:8]]
         set_cross = full[3:] + [vectors[8:]]
@@ -990,12 +999,7 @@
     row_memory, ids, memory_ids = found[10:]
     query_t = list(query_t)
     if packed:
-        third_c = join(after([third, third_b], query_t[0]))
-        third_d = turned_swap(third_c, 3)
-        second_d = after(second_d, query_t[0])
-        set_cross = [second_c, second_d, swap(second_c, 1, 32), swap(second_d, 1, 32)]
-        query_t[0] = after(query_t[0], third_c, second_d)
-        set_back, set_query, set_last, set_memory = set_cross, set_self, set_self, set_cross
+        set_query, set_last = set_self, set_self
     else:
         set_back, set_query, set_last, set_memory = [full[3], full[4], full[7]], full[:1], full[1:3], full[5:7]
     found = run(
@@ -1004,12 +1008,17 @@
     )
     mixtures, logs = found[:2], found[2:]
     if packed:
-        third_d = after(third_d, mixtures[0])
-        set_inner = [third_c, third_d, swap(third_c, 1, 32), swap(third_d, 1, 32)]
+        third_plane = exchanged(after(third, mixtures[0]))
+        second_plane = after(second_plane, mixtures[0])
+        set_cross = second_plane + [swap(a, 1, 32) for a in second_plane]
+        set_back, set_memory = set_cross, set_cross
     first_sum, second_sum, cross_query, memory_keys, memory_values, cross_t, cross_logs, vectors = run(
         make_cross_forward(packed, rows, block, parts * memory_share, width, narrow, len(set_cross)),
         9.0, "cross_forward", *set_cross, *own_tokens, row_memory, ids, memory_ids, *mixtures,
     )
+    if packed:
+        third_plane[1:] = after(third_plane[1:], second_sum)
+        set_inner = third_plane + [swap(a, 1, 32) for a in third_plane]
     out_own, out_send, back2_in, sums_inner, *grads_inner = run(
         make_inner(packed, rows, block, width, hidden, narrow, len(set_inner)), 18.0, "inner",
         *set_inner, second_sum, kept, came, vectors,
@@ -1026,35 +1035,34 @@
     grads_early = found[10 + parts - 1 :]
     query = list(query)
     if packed:
-        keep, send = combine(after([grads_inner[0], swap(grads_inner[1], 1, 32)], back1, out_came), 2)
-        inner_step = [keep, turned_swap(send, 3)]
-        memory_key_own = after(memory_key_own, keep)
+        parts_inner = combine(after([grads_inner[0], swap(grads_inner[1], 1, 32)], back1, out_came), 4)
+        step_inner = handed(parts_inner)
+        memory_key_own = after(memory_key_own, parts_inner[0])
     memory_own, memory_send, *grads_cross = run(
         make_memory_back(packed, parts, rows, block, memory_block, width, narrow, len(set_memory)),
-        2.0, "memory_back", *set_memory, *own_tokens, memory_key_own, memory_value_own, sums_cross,
-        *grads_early, *memory_received,
-    )
-    if packed:
+        2.0, "memory_back", *set_memory, *own_tokens, memory_key_own,
+        memory_value_own, sums_cross, *grads_early, *memory_received,
+    )
+    if packed:
+        query[0] = after(query[0], grads_cross[0])
         cross_came = swap(grads_cross[1], 1, 32)
-        query[0] = after(query[0], grads_cross[0])
     found = run(
         make_self_back_upper(parts, share, width), 7.0, "self_back_upper", query[0], keys[0],
         values[0], slope[0], slope_t[0], logs[0], deltas[0], ids,
     )
     query_upper, own_upper = found[:2]
     received_upper = [swap(a, m // 2 + 1, devices) for m, a in enumerate(found[2:])]
-    if packed:
-        keep, send = combine(after(inner_step, query_upper), 2, 8.0)
-        inner_step = [keep, turned_swap(send, 2)]
-        keep_cross, send = combine(after([grads_cross[0], cross_came], keep), 2)
-        cross_step = [keep_cross, turned_swap(send, 3)]
-        query[1] = after(query[1], keep, keep_cross)
     in_part, query_sum, query_w_grad, own_lower, *sends = run(
         make_self_back_lower(packed, parts, rows, block, width, narrow, len(set_query)), 11.0,
         "self_back_lower", *set_query, *own_tokens, query[1], keys[1], values[1], slope[1],
         slope_t[1], logs[1], deltas[1], ids, back1, query_upper,
     )
     received_lower = [swap(a, m // 2 + 1, devices) for m, a in enumerate(sends)]
+    if packed:
+        parts_inner = combine(after(step_inner, query_sum), 2)
+        keep_inner, send = parts_inner
+        step_inner = [keep_inner, turned_swap(send, 1)]
+        in_part = after(in_part, keep_inner)
     in_own, in_send, *grads_last = run(
         make_last(packed, parts, rows, block, memory_block, width, narrow, len(set_last)), 6.0,
         "last", *set_last, *own_tokens, in_part, query_sum, query_w_grad, memory_send, own_upper,
@@ -1062,30 +1070,25 @@
     )
 
     if packed:
-        keep_inner, send = combine(after(inner_step, in_own), 2)
-        inner_step = [keep_inner, turned_swap(send, 1)]
-        keep_cross, send = combine(after(cross_step, keep_inner), 2)
-        cross_step = [keep_cross, turned_swap(send, 2)]
-        grads_last[1] = after(grads_last[1], keep_cross)
-        keep, send = combine([grads_last[0], swap(grads_last[1], 1, 32)], 2)
-        last_step = [keep, turned_swap(send, 3)]
-        in_send = after(in_send, last_step[1])
-        keep_inner, send = combine(inner_step, 2)
-        inner_step = [keep_inner, turned_swap(send, 0)]
-        keep_cross, send = combine(cross_step, 2)
-        cross_step = [keep_cross, turned_swap(send, 1)]
-        keep, send = combine(after(last_step, keep_inner, keep_cross), 2)
-        last_step = [keep, turned_swap(send, 2)]
-        keep_cross, send = combine(cross_step, 2)
-        cross_step = [keep_cross, turned_swap(send, 0)]
-        keep, send = combine(after(last_step, keep_cross), 2)
-        last_step = [keep, turned_swap(send, 1)]
-        keep, send = combine(last_step, 2)
-        last_step = [keep, turned_swap(send, 0)]
+        parts_cross = combine(after([grads_cross[0], cross_came], in_own), 4)
+        step_cross = handed(parts_cross)
+        parts_last = combine(after([grads_last[0], swap(grads_last[1], 1, 32)], parts_cross[0]), 4)
+        step_last = handed(parts_last)
+        keep_inner, send = combine(after(step_inner, parts_last[0]), 2)
+        step_inner = [keep_inner, turned_swap(send, 0)]
+        keep_cross, send = combine(after(step_cross, keep_inner), 2)
+        step_cross = [keep_cross, turned_swap(send, 1)]
+        in_send = after(in_send, keep_cross)
+        keep, send = combine(after(step_last, keep_cross), 2)
+        step_last = [keep, turned_swap(send, 1)]
+        keep_cross, send = combine(after(step_cross, keep), 2)
+        step_cross = [keep_cross, turned_swap(send, 0)]
+        keep, send = combine(after(step_last, keep_cross), 2)
+        step_last = [keep, turned_swap(send, 0)]
 
         def plan(me_ref, *refs):
             me = me_ref[0]
-            steps, outs = [refs[:2], refs[2:4], refs[4:6]], refs[6:]
+            steps, outs = (refs[:2], refs[2:4], refs[4:6]), refs[6:]
             inner, cross, last = (sum(r[0].astype(F32) for r in given) for given in steps)
             for i in range(blocks):
                 outs[0][:, i * width : (i + 1) * width] = inner[i * narrow : (i + 1) * narrow, :]
@@ -1106,7 +1109,7 @@
         (inner_share, outer_share, source_key_share, source_value_share, source_output_share,
          source_query_share, output_share, key_share, value_share, query_share, sums,
          inner_bias_share) = call(
-            plan, [(s, F32) for s in shapes], (me_array, *inner_step, *cross_step, *last_step), [], 2.0,
+            plan, [(s, F32) for s in shapes], (me_array, *step_inner, *step_cross, *step_last), [], 2.0,
             "finish",
         )
         inner_bias_share = inner_bias_share.reshape(wide)

time: 198 us -> 207 us (1.045)
  starting transfers between devices: 45.4 us -> 51.9 us
  waiting for transfers between devices: 80.6 us -> 86.1 us
  local copies, waits for them, and re-layouts: 5.24 us -> 3.03 us
    ppermute x19 -> x43, waiting for transfers between devices: 11.6 us -> 65.4 us  [swap(): return lax.ppermute(array, AXES, [(i, i ^ mask) for i in range(devices)])]
    ppermute x22 -> x10, waiting for transfers between devices: 69 us -> 20.7 us  [turned_swap(): lax.ppermute(array, AXES, [(i, i ^ TURNS[i % 2][step]) for i in range(32)])]
    ppermute x19 -> x43, starting transfers between devices: 5.44 us -> 30.2 us  [swap(): return lax.ppermute(array, AXES, [(i, i ^ mask) for i in range(devices)])]
    ppermute x22 -> x10, starting transfers between devices: 40 us -> 21.7 us  [turned_swap(): lax.ppermute(array, AXES, [(i, i ^ TURNS[i % 2][step]) for i in range(32)])]
    another operation x1 -> x0, local copies, waits for them, and re-layouts: 2.68 us -> none  [per_device(): jnp.stack([query_bias, value_bias, output_bias, attention_gain, attention...]
    pallas_call x12 -> x9, Pallas kernels: 3.99 us -> 4.48 us  [combine(): pl.pallas_call(kernel, out_shape=[jax.ShapeDtypeStruct(shape, BF16)] * sp...]
  transfers between devices with their start and end apart: 41 -> 53, of which waited for: 22 -> 30; matrix products, arithmetic and copies ran while one was open for 3% -> 1% of each run, Pallas kernels for 22% -> 22%
where the time goes in v12:
time: 207 us
  waiting for transfers between devices  86.1 us (42%)
  Pallas kernels  62.1 us (30%)
  starting transfers between devices  51.9 us (25%)
  local copies, waits for them, and re-layouts  3.03 us (1%)
  other arithmetic  2.99 us (1%)
    ppermute x43, waiting for transfers between devices, swap(): return lax.ppermute(array, AXES, [(i, i ^ mask) for i in range(devices)])  65.4 us
    pallas_call x13, Pallas kernels, call(): pl.pallas_call(kernel, out_shape=[jax.ShapeDtypeStruct(s, d) for s, d in...  57.6 us
    ppermute x43, starting transfers between devices, swap(): return lax.ppermute(array, AXES, [(i, i ^ mask) for i in range(devices)])  30.2 us
    ppermute x10, starting transfers between devices, turned_swap(): lax.ppermute(array, AXES, [(i, i ^ TURNS[i % 2][step]) for i in range(32)])  21.7 us
    ppermute x10, waiting for transfers between devices, turned_swap(): lax.ppermute(array, AXES, [(i, i ^ TURNS[i % 2][step]) for i in range(32)])  20.7 us
    pallas_call x9, Pallas kernels, combine(): pl.pallas_call(kernel, out_shape=[jax.ShapeDtypeStruct(shape, BF16)] * sp...  4.48 us
  transfers between devices with their start and end apart: 53, of which 30 were waited for; matrix products, arithmetic and copies ran while one was open for 1% of the time, Pallas kernels for 22%

profile of v12, /device:TPU:0, one launch (start us, length us, event | category | flops | bytes accessed | tf_op | source)
XLA Modules:
  0.0 207.1 jit_solution(5719423469471984269)
XLA Ops:
  3.1 3.0 %collective-permute-start.3 = (bf16[584,512]{1,0:T(8,128)(2,1)}, bf16[584,512]{1,0:T(8,128)(2,1)S(1)}, u32[]{:S(2)}, u32[]{:S(2)}) collective-permute-start(bf16[584,512]{1,0:T(8,128)(2,1)} %get-tuple-element.180), channel_id=1, source_target_pairs={{0,2},{1,3},{2,0},{3,1},{4,6},{5,7},{6,4},{7,5},{8,10},{9,11},{10,... | collective-permute-start | bytes 1794056 | tf_op jit(solution)/shard_map/ppermute | solution.py:161
  9.5 2.8 %collective-permute-done.refs_1_ = bf16[56,512]{1,0:T(8,128)(2,1)S(1)} collective-permute-done((bf16[56,512]{1,0:T(8,128)(2,1)}, bf16[56,512]{1,0:T(8,128)(2,1)S(1)}, u32[]{:S(2)}, u32[]{:S(2)}) %collective-permute-start) | collective-permute-done | bytes 57376 | tf_op jit(solution)/shard_map/ppermute | solution.py:177
  14.8 4.9 %collective-permute-done.3.refs_10_.refs_11_ = bf16[584,512]{1,0:T(8,128)(2,1)S(1)} collective-permute-done((bf16[584,512]{1,0:T(8,128)(2,1)}, bf16[584,512]{1,0:T(8,128)(2,1)S(1)}, u32[]{:S(2)}, u32[]{:S(2)}) %collective-permute-start.3) | collective-permute-done | bytes 598048 | tf_op jit(solution)/shard_map/ppermute | solution.py:161
  19.8 3.8 %collective-permute-start.2 = (bf16[112,512]{1,0:T(8,128)(2,1)S(1)}, bf16[112,512]{1,0:T(8,128)(2,1)S(1)}, u32[]{:S(2)}, u32[]{:S(2)}) collective-permute-start(bf16[112,512]{1,0:T(8,128)(2,1)S(1)} %join.3.refs_0_), channel_id=1, source_target_pairs={{0,24},{1,9},{2,26},{3,11},{4,28},{5,13},{6,30},{7,15},{8,16},{9,1... | collective-permute-start | bytes 344072 | tf_op jit(solution)/shard_map/ppermute | solution.py:177
  23.6 4.0 %collective-permute-done.2.refs_1_ = bf16[112,512]{1,0:T(8,128)(2,1)S(1)} collective-permute-done((bf16[112,512]{1,0:T(8,128)(2,1)S(1)}, bf16[112,512]{1,0:T(8,128)(2,1)S(1)}, u32[]{:S(2)}, u32[]{:S(2)}) %collective-permute-start.2) | collective-permute-done | bytes 114720 | tf_op jit(solution)/shard_map/ppermute | solution.py:177
  28.6 2.7 %collective-permute-start.5 = (bf16[448,512]{1,0:T(8,128)(2,1)S(1)}, bf16[448,512]{1,0:T(8,128)(2,1)S(1)}, u32[]{:S(2)}, u32[]{:S(2)}) collective-permute-start(bf16[448,512]{1,0:T(8,128)(2,1)S(1)} %join.4.upper), channel_id=1, source_target_pairs={{0,24},{1,9},{2,26},{3,11},{4,28},{5,13},{6,30},{7,15},{8,16},{9,1... | collective-permute-start | bytes 1376264 | tf_op jit(solution)/shard_map/ppermute | solution.py:177
  34.8 3.5 %collective-permute-done.8.refs_4_ = bf16[224,512]{1,0:T(8,128)(2,1)S(1)} collective-permute-done((bf16[224,512]{1,0:T(8,128)(2,1)S(1)}, bf16[224,512]{1,0:T(8,128)(2,1)S(1)}, u32[]{:S(2)}, u32[]{:S(2)}) %collective-permute-start.8) | collective-permute-done | bytes 229408 | tf_op jit(solution)/shard_map/ppermute | solution.py:161
  48.1 8.3 %self_attention.1 = (bf16[256,512]{1,0:T(8,128)(2,1)S(1)}, bf16[256,512]{1,0:T(8,128)(2,1)S(1)}, f32[4,1,512]{2,1,0:T(1,128)S(1)}, f32[4,1,512]{2,1,0:T(1,128)S(1)}) custom-call(s32[1]{0:T(128)} %bitcast.me_ref.refs_0_, bf16[256,512]{1,0:T(8,128)(2,1)S(1)} %get-tuple-element.193.refs_0_, bf16[256,512]{1,0:T(8,128)(2,1)S(1)} %get-tuple-element.194.refs_1_, ...), custom_call_target="tpu_custom_call" | custom-call | flops 1 | bytes 1 | tf_op jit(solution)/shard_map/self_attention/pallas_call | solution.py:260
  56.4 5.4 %collective-permute-done.18.refs_3_ = bf16[384,512]{1,0:T(8,128)(2,1)S(1)} collective-permute-done((bf16[384,512]{1,0:T(8,128)(2,1)S(1)}, bf16[384,512]{1,0:T(8,128)(2,1)S(1)}, u32[]{:S(2)}, u32[]{:S(2)}) %collective-permute-start.18) | collective-permute-done | bytes 393248 | tf_op jit(solution)/shard_map/ppermute | solution.py:161
  68.2 5.3 %cross_forward.1 = (f32[512,512]{1,0:T(8,128)S(1)}, f32[512,512]{1,0:T(8,128)S(1)}, bf16[512,512]{1,0:T(8,128)(2,1)S(1)}, bf16[256,512]{1,0:T(8,128)(2,1)S(1)}, ...) custom-call(s32[1]{0:T(128)} %bitcast.me_ref.refs_0_, ...), custom_call_target="tpu_custom_call" | custom-call | flops 1 | bytes 1 | tf_op jit(solution)/shard_map/cross_forward/pallas_call | solution.py:260
  73.5 4.6 %collective-permute-done.16.refs_4_ = bf16[512,512]{1,0:T(8,128)(2,1)S(1)} collective-permute-done((bf16[512,512]{1,0:T(8,128)(2,1)S(1)}, bf16[512,512]{1,0:T(8,128)(2,1)S(1)}, u32[]{:S(2)}, u32[]{:S(2)}) %collective-permute-start.16) | collective-permute-done | bytes 524320 | tf_op jit(solution)/shard_map/ppermute | solution.py:161
  78.1 10.2 %collective-permute-done.15.refs_3_ = bf16[512,512]{1,0:T(8,128)(2,1)S(1)} collective-permute-done((bf16[512,512]{1,0:T(8,128)(2,1)S(1)}, bf16[512,512]{1,0:T(8,128)(2,1)S(1)}, u32[]{:S(2)}, u32[]{:S(2)}) %collective-permute-start.15) | collective-permute-done | bytes 524320 | tf_op jit(solution)/shard_map/ppermute | solution.py:161
  91.8 12.6 %inner.1 = (f32[256,512]{1,0:T(8,128)S(1)}, bf16[256,512]{1,0:T(8,128)(2,1)S(1)}, f32[512,512]{1,0:T(8,128)S(1)}, f32[8,512]{1,0:T(8,128)S(1)}, bf16[16,128,512]...) custom-call(s32[1]{0:T(128)} %bitcast.me_ref.refs_0_, bf16[512,512]{1,0:T(8,128)(2,1)S(1)} %get-tuple-element.201.refs_1_, ...), custom_call_target="tpu_custom_call" | custom-call | flops 1 | bytes 1 | tf_op jit(solution)/shard_map/inner/pallas_call | solution.py:260
  105.9 8.2 %cross_back.1 = (f32[512,512]{1,0:T(8,128)S(1)}, f32[128,512]{1,0:T(8,128)S(1)}, f32[128,512]{1,0:T(8,128)S(1)}, f32[16,512]{1,0:T(8,128)S(1)}, bf16[512,256]{1,...) custom-call(s32[1]{0:T(128)} %bitcast.me_ref.refs_0_, ...), custom_call_target="tpu_custom_call" | custom-call | flops 1 | bytes 1 | tf_op jit(solution)/shard_map/cross_back/pallas_call | solution.py:260
  120.8 6.1 %self_back_upper.1 = (bf16[512,256]{1,0:T(8,128)(2,1)S(1)}, f32[1024,256]{1,0:T(8,128)S(1)}, bf16[512,256]{1,0:T(8,128)(2,1)S(1)}, bf16[512,256]{1,0:T(8,128)(2,1)S(1)}) custom-call(s32[1]{0:T(128)} %bitcast.me_ref.refs_0_, bf16[512,256]{1,0:T(8,128)(2,1)S(1)} %get-tuple-element.247.refs_1_, bf16[1024,256]{1,0:T(8,128)(2,1)S(1)} %get-tuple-element.195.refs_2_, ...), custom_call_target="tpu_custom_call" | custom-call | flops 1 | bytes 1 | tf_op jit(solution)/shard_map/self_back_upper/pallas_call | solution.py:260
  126.8 7.1 %self_back_lower.1 = (f32[512,512]{1,0:T(8,128)S(1)}, f32[8,512]{1,0:T(8,128)S(1)}, bf16[512,512]{1,0:T(8,128)(2,1)S(1)}, f32[1024,256]{1,0:T(8,128)S(1)}, bf16[...) custom-call(s32[1]{0:T(128)} %bitcast.me_ref.refs_0_, bf16[224,512]{1,0:T(8,128)(2,1)S(1)} %join.5.refs_1_, ...), custom_call_target="tpu_custom_call" | custom-call | flops 1 | bytes 1 | tf_op jit(solution)/shard_map/self_back_lower/pallas_call | solution.py:260
  134.6 9.2 %collective-permute-done.33.refs_3_ = bf16[4,128,512]{2,1,0:T(8,128)(2,1)S(1)} collective-permute-done((bf16[4,128,512]{2,1,0:T(8,128)(2,1)S(1)}, bf16[4,128,512]{2,1,0:T(8,128)(2,1)S(1)}, u32[]{:S(2)}, u32[]{:S(2)}) %collective-permute-start.33) | collective-permute-done | bytes 524320 | tf_op jit(solution)/shard_map/ppermute | solution.py:161
  149.0 2.7 %collective-permute-start.42 = (bf16[2,128,512]{2,1,0:T(8,128)(2,1)S(1)}, bf16[2,128,512]{2,1,0:T(8,128)(2,1)S(1)}, u32[]{:S(2)}, u32[]{:S(2)}) collective-permute-start(bf16[2,128,512]{2,1,0:T(8,128)(2,1)S(1)} %get-tuple-element.282), channel_id=1, source_target_pairs={{0,24},{1,9},{2,26},{3,11},{4,28},{5,13},{6,30},{7,15},{8,16},{9,1... | collective-permute-start | bytes 786440 | tf_op jit(solution)/shard_map/ppermute | solution.py:177
  160.0 3.0 %collective-permute-done.39.refs_1_ = bf16[4,96,512]{2,1,0:T(8,128)(2,1)S(1)} collective-permute-done((bf16[4,96,512]{2,1,0:T(8,128)(2,1)S(1)}, bf16[4,96,512]{2,1,0:T(8,128)(2,1)S(1)}, u32[]{:S(2)}, u32[]{:S(2)}) %collective-permute-start.39) | collective-permute-done | bytes 393248 | tf_op jit(solution)/shard_map/ppermute | solution.py:161
  164.8 8.5 %collective-permute-done.41.refs_3_ = bf16[4,96,512]{2,1,0:T(8,128)(2,1)S(1)} collective-permute-done((bf16[4,96,512]{2,1,0:T(8,128)(2,1)}, bf16[4,96,512]{2,1,0:T(8,128)(2,1)S(1)}, u32[]{:S(2)}, u32[]{:S(2)}) %collective-permute-start.41) | collective-permute-done | bytes 393248 | tf_op jit(solution)/shard_map/ppermute | solution.py:161
  176.3 3.2 %collective-permute-done.49.refs_3_ = bf16[4,56,512]{2,1,0:T(8,128)(2,1)} collective-permute-done((bf16[4,56,512]{2,1,0:T(8,128)(2,1)}, bf16[4,56,512]{2,1,0:T(8,128)(2,1)}, u32[]{:S(2)}, u32[]{:S(2)}) %collective-permute-start.49) | collective-permute-done | bytes 229408 | tf_op jit(solution)/shard_map/ppermute | solution.py:161
  180.8 3.0 %collective-permute-start.51 = (bf16[2,56,512]{2,1,0:T(8,128)(2,1)S(1)}, bf16[2,56,512]{2,1,0:T(8,128)(2,1)S(1)}, u32[]{:S(2)}, u32[]{:S(2)}) collective-permute-start(bf16[2,56,512]{2,1,0:T(8,128)(2,1)S(1)} %get-tuple-element.312), channel_id=1, source_target_pairs={{0,24},{1,9},{2,26},{3,11},{4,28},{5,13},{6,30},{7,15},{8,16},{9,1... | collective-permute-start | bytes 344072 | tf_op jit(solution)/shard_map/ppermute | solution.py:177
  185.6 8.0 %collective-permute-done.46.refs_1_ = bf16[2,96,512]{2,1,0:T(8,128)(2,1)S(1)} collective-permute-done((bf16[2,96,512]{2,1,0:T(8,128)(2,1)S(1)}, bf16[2,96,512]{2,1,0:T(8,128)(2,1)S(1)}, u32[]{:S(2)}, u32[]{:S(2)}) %collective-permute-start.46) | collective-permute-done | bytes 196640 | tf_op jit(solution)/shard_map/ppermute | solution.py:177
  193.7 5.2 %collective-permute-start.52 = (bf16[1,56,512]{2,1,0:T(8,128)(2,1)S(1)}, bf16[1,56,512]{2,1,0:T(8,128)(2,1)S(1)}, u32[]{:S(2)}, u32[]{:S(2)}) collective-permute-start(bf16[1,56,512]{2,1,0:T(8,128)(2,1)S(1)} %get-tuple-element.316), channel_id=1, source_target_pairs={{0,8},{1,25},{2,10},{3,27},{4,12},{5,29},{6,14},{7,31},{8,0},{9,17... | collective-permute-start | bytes 172040 | tf_op jit(solution)/shard_map/ppermute | solution.py:177
  (128 shorter events, 70.8 us)
Async XLA Ops:
  3.1 16.7 %collective-permute-start.3 = (bf16[584,512]{1,0:T(8,128)(2,1)}, bf16[584,512]{1,0:T(8,128)(2,1)S(1)}, u32[]{:S(2)}, u32[]{:S(2)}) collective-permute-start(bf16[584,512]{1,0:T(8,128)(2,1)} %get-tuple-element.180), channel_id=1, source_target_pairs={{0,2},{1,3},{2,0},{3,1},{4,6},{5,7},{6,4},{7,5},{8,10},{9,11},{10,... | collective-permute-start | bytes 1794056 | tf_op jit(solution)/shard_map/ppermute | solution.py:161
  6.1 21.5 %collective-permute-start.4 = (bf16[584,512]{1,0:T(8,128)(2,1)}, bf16[584,512]{1,0:T(8,128)(2,1)S(1)}, u32[]{:S(2)}, u32[]{:S(2)}) collective-permute-start(bf16[584,512]{1,0:T(8,128)(2,1)} %get-tuple-element.183.refs_9_.refs_10_), channel_id=1, source_target_pairs={{0,1},{1,0},{2,3},{3,2},{4,5},{5,4},{6,7},{7,6},{8,9},{9,8},{10,11... | collective-permute-start | bytes 1794056 | tf_op jit(solution)/shard_map/ppermute | solution.py:161
  13.2 14.4 %collective-permute-start.1 = (bf16[224,512]{1,0:T(8,128)(2,1)}, bf16[224,512]{1,0:T(8,128)(2,1)S(1)}, u32[]{:S(2)}, u32[]{:S(2)}) collective-permute-start(bf16[224,512]{1,0:T(8,128)(2,1)} %get-tuple-element.184.refs_0_), channel_id=1, source_target_pairs={{0,8},{1,25},{2,10},{3,27},{4,12},{5,29},{6,14},{7,31},{8,0},{9,17... | collective-permute-start | bytes 688136 | tf_op jit(solution)/shard_map/ppermute | solution.py:177
  19.8 21.1 %collective-permute-start.9 = (bf16[584,512]{1,0:T(8,128)(2,1)S(1)}, bf16[584,512]{1,0:T(8,128)(2,1)S(1)}, u32[]{:S(2)}, u32[]{:S(2)}) collective-permute-start(bf16[584,512]{1,0:T(8,128)(2,1)S(1)} %collective-permute-done.3.refs_10_.refs_11_), channel_id=1, source_target_pairs={{0,1},{1,0},{2,3},{3,2},{4,5},{5,4},{6,7},{7,6},{8,9},{9,8},{10,11... | collective-permute-start | bytes 1794056 | tf_op jit(solution)/shard_map/ppermute | solution.py:161
  41.0 15.4 %collective-permute-start.19 = (bf16[384,512]{1,0:T(8,128)(2,1)S(1)}, bf16[384,512]{1,0:T(8,128)(2,1)S(1)}, u32[]{:S(2)}, u32[]{:S(2)}) collective-permute-start(bf16[384,512]{1,0:T(8,128)(2,1)S(1)} %get-tuple-element.203.refs_1_), channel_id=1, source_target_pairs={{0,6},{1,7},{2,4},{3,5},{4,2},{5,3},{6,0},{7,1},{8,14},{9,15},{10,... | collective-permute-start | bytes 1179656 | tf_op jit(solution)/shard_map/ppermute | solution.py:161
  43.3 18.5 %collective-permute-start.18 = (bf16[384,512]{1,0:T(8,128)(2,1)S(1)}, bf16[384,512]{1,0:T(8,128)(2,1)S(1)}, u32[]{:S(2)}, u32[]{:S(2)}) collective-permute-start(bf16[384,512]{1,0:T(8,128)(2,1)S(1)} %get-tuple-element.203.refs_1_), channel_id=1, source_target_pairs={{0,4},{1,5},{2,6},{3,7},{4,0},{5,1},{6,2},{7,3},{8,12},{9,13},{10,... | collective-permute-start | bytes 1179656 | tf_op jit(solution)/shard_map/ppermute | solution.py:161
  43.8 18.1 %collective-permute-start.17 = (bf16[384,512]{1,0:T(8,128)(2,1)S(1)}, bf16[384,512]{1,0:T(8,128)(2,1)S(1)}, u32[]{:S(2)}, u32[]{:S(2)}) collective-permute-start(bf16[384,512]{1,0:T(8,128)(2,1)S(1)} %get-tuple-element.203.refs_1_), channel_id=1, source_target_pairs={{0,2},{1,3},{2,0},{3,1},{4,6},{5,7},{6,4},{7,5},{8,10},{9,11},{10,... | collective-permute-start | bytes 1179656 | tf_op jit(solution)/shard_map/ppermute | solution.py:161
  62.4 15.7 %collective-permute-start.16 = (bf16[512,512]{1,0:T(8,128)(2,1)S(1)}, bf16[512,512]{1,0:T(8,128)(2,1)S(1)}, u32[]{:S(2)}, u32[]{:S(2)}) collective-permute-start(bf16[512,512]{1,0:T(8,128)(2,1)S(1)} %get-tuple-element.201.refs_1_), channel_id=1, source_target_pairs={{0,6},{1,7},{2,4},{3,5},{4,2},{5,3},{6,0},{7,1},{8,14},{9,15},{10,... | collective-permute-start | bytes 1572872 | tf_op jit(solution)/shard_map/ppermute | solution.py:161
  64.6 23.6 %collective-permute-start.15 = (bf16[512,512]{1,0:T(8,128)(2,1)S(1)}, bf16[512,512]{1,0:T(8,128)(2,1)S(1)}, u32[]{:S(2)}, u32[]{:S(2)}) collective-permute-start(bf16[512,512]{1,0:T(8,128)(2,1)S(1)} %get-tuple-element.201.refs_1_), channel_id=1, source_target_pairs={{0,4},{1,5},{2,6},{3,7},{4,0},{5,1},{6,2},{7,3},{8,12},{9,13},{10,... | collective-permute-start | bytes 1572872 | tf_op jit(solution)/shard_map/ppermute | solution.py:161
  65.2 23.2 %collective-permute-start.14 = (bf16[512,512]{1,0:T(8,128)(2,1)S(1)}, bf16[512,512]{1,0:T(8,128)(2,1)S(1)}, u32[]{:S(2)}, u32[]{:S(2)}) collective-permute-start(bf16[512,512]{1,0:T(8,128)(2,1)S(1)} %get-tuple-element.201.refs_1_), channel_id=1, source_target_pairs={{0,2},{1,3},{2,0},{3,1},{4,6},{5,7},{6,4},{7,5},{8,10},{9,11},{10,... | collective-permute-start | bytes 1572872 | tf_op jit(solution)/shard_map/ppermute | solution.py:161
  67.6 21.3 %collective-permute-start.24 = (bf16[512,512]{1,0:T(8,128)(2,1)S(1)}, bf16[512,512]{1,0:T(8,128)(2,1)S(1)}, u32[]{:S(2)}, u32[]{:S(2)}) collective-permute-start(bf16[512,512]{1,0:T(8,128)(2,1)S(1)} %get-tuple-element.201.refs_1_), channel_id=1, source_target_pairs={{0,1},{1,0},{2,3},{3,2},{4,5},{5,4},{6,7},{7,6},{8,9},{9,8},{10,11... | collective-permute-start | bytes 1572872 | tf_op jit(solution)/shard_map/ppermute | solution.py:161
  117.0 30.2 %collective-permute-start.38 = (bf16[16,96,512]{2,1,0:T(8,128)(2,1)S(1)}, bf16[16,96,512]{2,1,0:T(8,128)(2,1)S(1)}, u32[]{:S(2)}, u32[]{:S(2)}) collective-permute-start(bf16[16,96,512]{2,1,0:T(8,128)(2,1)S(1)} %get-tuple-element.275), channel_id=1, source_target_pairs={{0,1},{1,0},{2,3},{3,2},{4,5},{5,4},{6,7},{7,6},{8,9},{9,8},{10,11... | collective-permute-start | bytes 4718600 | tf_op jit(solution)/shard_map/ppermute | solution.py:161
  117.3 16.8 %collective-permute-start.31 = (bf16[4,128,512]{2,1,0:T(8,128)(2,1)S(1)}, bf16[4,128,512]{2,1,0:T(8,128)(2,1)S(1)}, u32[]{:S(2)}, u32[]{:S(2)}) collective-permute-start(bf16[4,128,512]{2,1,0:T(8,128)(2,1)S(1)} %get-tuple-element.255), channel_id=1, source_target_pairs={{0,2},{1,3},{2,0},{3,1},{4,6},{5,7},{6,4},{7,5},{8,10},{9,11},{10,... | collective-permute-start | bytes 1572872 | tf_op jit(solution)/shard_map/ppermute | solution.py:161
  118.0 16.6 %collective-permute-start.32 = (bf16[4,128,512]{2,1,0:T(8,128)(2,1)S(1)}, bf16[4,128,512]{2,1,0:T(8,128)(2,1)S(1)}, u32[]{:S(2)}, u32[]{:S(2)}) collective-permute-start(bf16[4,128,512]{2,1,0:T(8,128)(2,1)S(1)} %get-tuple-element.256), channel_id=1, source_target_pairs={{0,4},{1,5},{2,6},{3,7},{4,0},{5,1},{6,2},{7,3},{8,12},{9,13},{10,... | collective-permute-start | bytes 1572872 | tf_op jit(solution)/shard_map/ppermute | solution.py:161
  119.4 24.4 %collective-permute-start.33 = (bf16[4,128,512]{2,1,0:T(8,128)(2,1)S(1)}, bf16[4,128,512]{2,1,0:T(8,128)(2,1)S(1)}, u32[]{:S(2)}, u32[]{:S(2)}) collective-permute-start(bf16[4,128,512]{2,1,0:T(8,128)(2,1)S(1)} %get-tuple-element.257), channel_id=1, source_target_pairs={{0,6},{1,7},{2,4},{3,5},{4,2},{5,3},{6,0},{7,1},{8,14},{9,15},{10,... | collective-permute-start | bytes 1572872 | tf_op jit(solution)/shard_map/ppermute | solution.py:161
  148.3 14.7 %collective-permute-start.39 = (bf16[4,96,512]{2,1,0:T(8,128)(2,1)S(1)}, bf16[4,96,512]{2,1,0:T(8,128)(2,1)S(1)}, u32[]{:S(2)}, u32[]{:S(2)}) collective-permute-start(bf16[4,96,512]{2,1,0:T(8,128)(2,1)S(1)} %get-tuple-element.279), channel_id=1, source_target_pairs={{0,2},{1,3},{2,0},{3,1},{4,6},{5,7},{6,4},{7,5},{8,10},{9,11},{10,... | collective-permute-start | bytes 1179656 | tf_op jit(solution)/shard_map/ppermute | solution.py:161
  151.8 13.0 %collective-permute-start.40 = (bf16[4,96,512]{2,1,0:T(8,128)(2,1)}, bf16[4,96,512]{2,1,0:T(8,128)(2,1)S(1)}, u32[]{:S(2)}, u32[]{:S(2)}) collective-permute-start(bf16[4,96,512]{2,1,0:T(8,128)(2,1)} %get-tuple-element.280), channel_id=1, source_target_pairs={{0,4},{1,5},{2,6},{3,7},{4,0},{5,1},{6,2},{7,3},{8,12},{9,13},{10,... | collective-permute-start | bytes 1179656 | tf_op jit(solution)/shard_map/ppermute | solution.py:161
  153.2 20.0 %collective-permute-start.41 = (bf16[4,96,512]{2,1,0:T(8,128)(2,1)}, bf16[4,96,512]{2,1,0:T(8,128)(2,1)S(1)}, u32[]{:S(2)}, u32[]{:S(2)}) collective-permute-start(bf16[4,96,512]{2,1,0:T(8,128)(2,1)} %get-tuple-element.281), channel_id=1, source_target_pairs={{0,6},{1,7},{2,4},{3,5},{4,2},{5,3},{6,0},{7,1},{8,14},{9,15},{10,... | collective-permute-start | bytes 1179656 | tf_op jit(solution)/shard_map/ppermute | solution.py:161
  155.5 19.9 %collective-permute-start.47 = (bf16[4,56,512]{2,1,0:T(8,128)(2,1)}, bf16[4,56,512]{2,1,0:T(8,128)(2,1)}, u32[]{:S(2)}, u32[]{:S(2)}) collective-permute-start(bf16[4,56,512]{2,1,0:T(8,128)(2,1)} %get-tuple-element.300), channel_id=1, source_target_pairs={{0,2},{1,3},{2,0},{3,1},{4,6},{5,7},{6,4},{7,5},{8,10},{9,11},{10,... | collective-permute-start | bytes 688136 | tf_op jit(solution)/shard_map/ppermute | solution.py:161
  158.5 17.8 %collective-permute-start.48 = (bf16[4,56,512]{2,1,0:T(8,128)(2,1)}, bf16[4,56,512]{2,1,0:T(8,128)(2,1)}, u32[]{:S(2)}, u32[]{:S(2)}) collective-permute-start(bf16[4,56,512]{2,1,0:T(8,128)(2,1)} %get-tuple-element.301), channel_id=1, source_target_pairs={{0,4},{1,5},{2,6},{3,7},{4,0},{5,1},{6,2},{7,3},{8,12},{9,13},{10,... | collective-permute-start | bytes 688136 | tf_op jit(solution)/shard_map/ppermute | solution.py:161
  163.0 16.5 %collective-permute-start.49 = (bf16[4,56,512]{2,1,0:T(8,128)(2,1)}, bf16[4,56,512]{2,1,0:T(8,128)(2,1)}, u32[]{:S(2)}, u32[]{:S(2)}) collective-permute-start(bf16[4,56,512]{2,1,0:T(8,128)(2,1)} %get-tuple-element.302), channel_id=1, source_target_pairs={{0,6},{1,7},{2,4},{3,5},{4,2},{5,3},{6,0},{7,1},{8,14},{9,15},{10,... | collective-permute-start | bytes 688136 | tf_op jit(solution)/shard_map/ppermute | solution.py:161
  180.8 12.8 %collective-permute-start.51 = (bf16[2,56,512]{2,1,0:T(8,128)(2,1)S(1)}, bf16[2,56,512]{2,1,0:T(8,128)(2,1)S(1)}, u32[]{:S(2)}, u32[]{:S(2)}) collective-permute-start(bf16[2,56,512]{2,1,0:T(8,128)(2,1)S(1)} %get-tuple-element.312), channel_id=1, source_target_pairs={{0,24},{1,9},{2,26},{3,11},{4,28},{5,13},{6,30},{7,15},{8,16},{9,1... | collective-permute-start | bytes 344072 | tf_op jit(solution)/shard_map/ppermute | solution.py:177
  184.8 15.3 %collective-permute-start.45 = (bf16[1,128,512]{2,1,0:T(8,128)(2,1)S(1)}, bf16[1,128,512]{2,1,0:T(8,128)(2,1)S(1)}, u32[]{:S(2)}, u32[]{:S(2)}) collective-permute-start(bf16[1,128,512]{2,1,0:T(8,128)(2,1)S(1)} %get-tuple-element.298), channel_id=1, source_target_pairs={{0,8},{1,25},{2,10},{3,27},{4,12},{5,29},{6,14},{7,31},{8,0},{9,17... | collective-permute-start | bytes 393224 | tf_op jit(solution)/shard_map/ppermute | solution.py:177
  184.8 20.3 %collective-permute-start.44 = (bf16[320,512]{1,0:T(8,128)(2,1)S(1)}, bf16[320,512]{1,0:T(8,128)(2,1)S(1)}, u32[]{:S(2)}, u32[]{:S(2)}) collective-permute-start(bf16[320,512]{1,0:T(8,128)(2,1)S(1)} %copy-done.4), channel_id=1, source_target_pairs={{0,2},{1,3},{2,0},{3,1},{4,6},{5,7},{6,4},{7,5},{8,10},{9,11},{10,... | collective-permute-start | bytes 983048 | tf_op jit(solution)/shard_map/ppermute | solution.py:161
  (36 other events, 257.0 us)

commit v13 on v10

--- a/solution.py
+++ b/solution.py
@@ -161,8 +161,8 @@
     return lax.ppermute(array, AXES, [(i, i ^ mask) for i in range(devices)])
 
 
-Z_FIRST = ((8, 16, 2, 4), (16, 8, 4, 2))
-CROSSED = ((8, 16, 4, 2), (16, 8, 2, 4))
+Z_FIRST = ((8, 24, 2, 4), (24, 8, 4, 2))
+CROSSED = ((8, 24, 4, 2), (24, 8, 2, 4))
 
 
 def turned_swap(array, step, orders=Z_FIRST):
@@ -301,13 +301,13 @@
 
     def kernel(me_ref, *refs):
         weights, inner, outer, wide, short = refs[:8], refs[8], refs[9], refs[10], refs[11:24]
-        first, rest = refs[24:]
-        me, middle = me_ref[0], 5 * narrow + 16
+        first, second, third = refs[24:]
+        me = me_ref[0]
         for i, ref in enumerate(weights):
             if i < 3:
                 first[i * narrow : (i + 1) * narrow, :] = ref[...]
             else:
-                rest[(i - 3) * narrow : (i - 2) * narrow, :] = ref[...]
+                second[(i - 3) * narrow : (i - 2) * narrow, :] = ref[...]
         short = jnp.concatenate([ref[...].astype(F32) for ref in short], axis=0).astype(BF16)
         found = placed(me, short, width)
         first[3 * narrow :, :] = jnp.concatenate([found[:2, :], jnp.zeros((6, width), F32)], axis=0).astype(BF16)
@@ -316,25 +316,12 @@
         place = lax.broadcasted_iota(jnp.int32, (blocks, width), 0)
         spread_row = jnp.where(place == lax.div(me, per), row, 0.0)
         none = jnp.zeros((16 - (found.shape[0] - 2) - blocks, width), F32)
-        rest[5 * narrow : middle, :] = jnp.concatenate([found[2:, :], spread_row, none], axis=0).astype(BF16)
+        second[5 * narrow :, :] = jnp.concatenate([found[2:, :], spread_row, none], axis=0).astype(BF16)
         for i in range(blocks):
-            rest[middle + i * narrow : middle + (i + 1) * narrow, :] = inner[:, i * width : (i + 1) * width]
-        rest[middle + tall :, :] = outer[...]
-
-    return kernel, [((rows, width), BF16) for rows in (3 * narrow + 8, 5 * narrow + 16 + 2 * tall)]
-
-
-def make_part(sizes, width):
-    tall = sum(sizes)
-
-    def kernel(me_ref, upper, lower, *outs):
-        for i in range(4):
-            ref, at = (upper, lower)[i // 2], i % 2 * tall
-            for size, out in zip(sizes, outs):
-                out[i * size : (i + 1) * size, :] = ref[at : at + size, :]
-                at += size
-
-    return kernel, [((4 * size, width), BF16) for size in sizes]
+            third[i * narrow : (i + 1) * narrow, :] = inner[:, i * width : (i + 1) * width]
+        third[tall:, :] = outer[...]
+
+    return kernel, [((rows, width), BF16) for rows in (3 * narrow + 8, 5 * narrow + 16, 2 * tall)]
 
 
 def join(arrays):
@@ -373,7 +360,7 @@
         me = me_ref[0]
         if packed:
             for i in range(3):
-                unpack(me, pieces, stride, i * narrow, narrow, scratch[i], CROSSED)
+                unpack(me, pieces, stride, i * narrow, narrow, scratch[i])
             query_w, key_w, value_w = scratch
             biases = vector_sum(pieces, stride, 3 * narrow)
         else:
@@ -497,7 +484,7 @@
         if packed:
             inner_w, outer_w, gathered, dense = scratch[4:8]
             tall = blocks * narrow
-            for core, far, slot, device in places(me_ref[0], CROSSED):
+            for core, far, slot, device in places(me_ref[0]):
                 ref, at = pieces[2 * core + far], slot * 2 * tall
                 row = pl.multiple_of(device * narrow, narrow)
                 for i in range(blocks):
@@ -786,7 +773,7 @@
         in_part, query_sum, query_w_grad, own = refs[2:6]
         sends, scratch = refs[6 : 4 + 2 * parts], refs[4 + 2 * parts :]
         if packed:
-            unpack(me_ref[0], pieces, 3 * narrow + 8, 0, narrow, scratch[7], CROSSED)
+            unpack(me_ref[0], pieces, 3 * narrow + 8, 0, narrow, scratch[7])
             query_w = scratch[7]
         else:
             (query_w,) = pieces
@@ -829,7 +816,7 @@
         me = me_ref[0]
         if packed:
             for i in range(2):
-                unpack(me, pieces, 3 * narrow + 8, (1 + i) * narrow, narrow, scratch[1 + i], CROSSED)
+                unpack(me, pieces, 3 * narrow + 8, (1 + i) * narrow, narrow, scratch[1 + i])
             key_w, value_w = scratch[1:3]
         else:
             key_w, value_w = pieces
@@ -979,26 +966,26 @@
     own_tokens = row_tokens[:rows]
 
     if packed:
-        first, rest = run(make_weights_packet(narrow, width, blocks), 1.0, "weights_packet",
+        first, second, third = run(make_weights_packet(narrow, width, blocks), 1.0, "weights_packet",
                           query_weight, key_weight, value_weight, output_weight, source_query,
                           source_key, source_value, source_output, inner_weight, outer_weight,
                           inner_bias.reshape(1, wide), *[v.reshape(1, narrow) for v in short], room=58)
         first = after(first, sent)
         first = join([first, turned_swap(first, 0)])
         first_b = turned_swap(first, 1)
-        rest = after(rest, first)
-        rest_b = turned_swap(rest, 0)
-        first = join(after([first, first_b], rest_b))
-        rest = join(after([rest, rest_b], first_b, came, *kept_swaps))
-        first_b, rest_b = turned_swap(first, 2, CROSSED), turned_swap(rest, 1)
-        first_c = join([first, first_b])
-        first_d = turned_swap(first_c, 3, CROSSED)
-        second, third = run(make_part((5 * narrow + 16, 2 * blocks * narrow), width), 1.0, "part", rest, after(rest_b, first_b))
-        second_b, third_b = turned_swap(second, 2), turned_swap(third, 2, CROSSED)
+        second = after(second, first)
+        second_b = turned_swap(second, 0)
+        first, second = join(after([first, first_b], second_b)), join(after([second, second_b], first_b))
+        third = after(third, second)
+        first_b, second_b, third_b = turned_swap(first, 2), turned_swap(second, 1), turned_swap(third, 0)
+        first_c = join(after([first, first_b], second_b, third_b, came, *kept_swaps))
+        second = join(after([second, second_b], first_b, third_b))
+        third = join(after([third, third_b], first_b, second_b))
+        first_d, second_b, third_b = turned_swap(first_c, 3), turned_swap(second, 2), turned_swap(third, 1)
         second_c = join(after([second, second_b], first_d, third_b))
-        third_c = join(after([third, third_b], first_d, second_b))
-        second_d, third_d = turned_swap(second_c, 3), turned_swap(third_c, 3, CROSSED)
-        first_d = after(first_d, second_c, third_c, *came_swaps)
+        third = join(after([third, third_b], first_d, second_b))
+        first_d = after(first_d, second_c, third, *came_swaps)
+        second_d, third_b = turned_swap(second_c, 3), turned_swap(third, 2)
         set_self = [first_c, first_d, swap(first_c, 1, 32), swap(first_d, 1, 32)]
     else:
         full = [whole(w) for w in (query_weight, key_weight, value_weight, output_weight, source_query, source_key, source_value, source_output)]
@@ -1034,14 +1021,18 @@
     )
     mixtures, logs = found[:2], found[2:]
     if packed:
-        second_d, third_d = after(second_d, mixtures[0]), after(third_d, mixtures[0])
+        third_c = join(after([third, third_b], mixtures[0]))
+        third_d = turned_swap(third_c, 3)
+        second_d = after(second_d, mixtures[0])
         set_cross = [second_c, second_d, swap(second_c, 1, 32), swap(second_d, 1, 32)]
-        set_inner = [third_c, third_d, swap(third_c, 1, 32), swap(third_d, 1, 32)]
         set_back, set_memory = set_cross, set_cross
     first_sum, second_sum, cross_query, memory_keys, memory_values, cross_t, cross_logs, vectors = run(
         make_cross_forward(packed, rows, block, parts * memory_share, width, narrow, len(set_cross)),
         9.0, "cross_forward", *set_cross, *own_tokens, row_memory, ids, memory_ids, *mixtures,
     )
+    if packed:
+        third_d = after(third_d, second_sum)
+        set_inner = [third_c, third_d, swap(third_c, 1, 32), swap(third_d, 1, 32)]
     out_own, out_send, back2_in, sums_inner, *grads_inner = run(
         make_inner(packed, rows, block, width, hidden, narrow, len(set_inner)), 18.0, "inner",
         *set_inner, second_sum, kept, came, vectors,

time: 186 us -> 179 us (0.962)
  waiting for transfers between devices: 81 us -> 75.8 us
    ppermute x20 -> x22, waiting for transfers between devices: 73.2 us -> 66.2 us  [turned_swap(): lax.ppermute(array, AXES, [(i, i ^ orders[i % 2][step]) for i in range(32)])]
    ppermute x20 -> x22, starting transfers between devices: 28.2 us -> 24.9 us  [turned_swap(): lax.ppermute(array, AXES, [(i, i ^ orders[i % 2][step]) for i in range(32)])]
    ppermute x19, starting transfers between devices: 7.66 us -> 9.82 us  [swap(): return lax.ppermute(array, AXES, [(i, i ^ mask) for i in range(devices)])]
    pallas_call x13 -> x12, Pallas kernels: 57.6 us -> 57.5 us  [call(): pl.pallas_call(kernel, out_shape=[jax.ShapeDtypeStruct(s, d) for s, d in...]
  transfers between devices with their start and end apart: 39 -> 41, of which waited for: 22 -> 23; matrix products, arithmetic and copies ran while one was open for 2% -> 2% of each run, Pallas kernels for 23% -> 23%
where the time goes in v13:
time: 179 us; the launch traced here: 178 us
  waiting for transfers between devices  75.8 us (42%)
  Pallas kernels  60.5 us (34%)
  starting transfers between devices  34.7 us (19%)
  other arithmetic  3.95 us (2%)
  local copies, waits for them, and re-layouts  2.29 us (1%)
    ppermute x22, waiting for transfers between devices, turned_swap(): lax.ppermute(array, AXES, [(i, i ^ orders[i % 2][step]) for i in range(32)])  66.2 us
    pallas_call x12, Pallas kernels, call(): pl.pallas_call(kernel, out_shape=[jax.ShapeDtypeStruct(s, d) for s, d in...  57.5 us
    ppermute x22, starting transfers between devices, turned_swap(): lax.ppermute(array, AXES, [(i, i ^ orders[i % 2][step]) for i in range(32)])  24.9 us
    ppermute x19, starting transfers between devices, swap(): return lax.ppermute(array, AXES, [(i, i ^ mask) for i in range(devices)])  9.82 us
    ppermute x19, waiting for transfers between devices, swap(): return lax.ppermute(array, AXES, [(i, i ^ mask) for i in range(devices)])  9.55 us
  transfers between devices with their start and end apart: 41, of which 23 were waited for; matrix products, arithmetic and copies ran while one was open for 2% of the time, Pallas kernels for 23%

profile of v13, /device:TPU:0, one launch (start us, length us, event | category | flops | bytes accessed | tf_op | source)
XLA Modules:
  0.0 178.3 jit_solution(1994158704130413271)
XLA Ops:
  0.7 2.4 %tokens_packet.1 = (bf16[584,512]{1,0:T(8,128)(2,1)}, bf16[584,512]{1,0:T(8,128)(2,1)}) custom-call(s32[1]{0:T(128)} %bitcast.15.turn_ref, s32[2,256]{1,0:T(2,128)} %targets.1, s32[2,64]{1,0:T(2,128)} %sources.1, bf16[2,256,512]{2,1,0:T(8,128)(2,1)} %tokens_ref.1, bf16[2,64,512]{2,1,0:T(8,128)(2,1)} %memory_ref.1, bf16[2,256,512]{2,1,0:T(8,128)(2,1)} %cot_ref.1), custom_call_target="tpu_custom_call" | custom-call | flops 1 | bytes 1 | tf_op jit(solution)/shard_map/tokens_packet/pallas_call | solution.py:255
  3.1 3.0 %collective-permute-start.7 = (bf16[584,512]{1,0:T(8,128)(2,1)}, bf16[584,512]{1,0:T(8,128)(2,1)S(1)}, u32[]{:S(2)}, u32[]{:S(2)}) collective-permute-start(bf16[584,512]{1,0:T(8,128)(2,1)} %get-tuple-element.173), channel_id=1, source_target_pairs={{0,2},{1,3},{2,0},{3,1},{4,6},{5,7},{6,4},{7,5},{8,10},{9,11},{10,... | collective-permute-start | bytes 1794056 | tf_op jit(solution)/shard_map/ppermute | solution.py:161
  6.1 1.9 %weights_packet.1 = (bf16[56,512]{1,0:T(8,128)(2,1)}, bf16[96,512]{1,0:T(8,128)(2,1)}, bf16[128,512]{1,0:T(8,128)(2,1)}) custom-call(s32[1]{0:T(128)} %bitcast.me_ref.refs_0_, bf16[16,512]{1,0:T(8,128)(2,1)} %refs_0_.1, bf16[16,512]{1,0:T(8,128)(2,1)} %refs_1_.1, bf16[16,512]{1,0:T(8,128)(2,1)} %refs_2_.1, bf16[16,512]{1,0:T(8,128)(2,1)} %refs_3_.1, ...), custom_call_target="tpu_custom_call" | custom-call | flops 1 | bytes 1 | tf_op jit(solution)/shard_map/weights_packet/pallas_call | solution.py:255
  9.6 2.8 %collective-permute-done.refs_1_ = bf16[56,512]{1,0:T(8,128)(2,1)S(1)} collective-permute-done((bf16[56,512]{1,0:T(8,128)(2,1)}, bf16[56,512]{1,0:T(8,128)(2,1)S(1)}, u32[]{:S(2)}, u32[]{:S(2)}) %collective-permute-start) | collective-permute-done | bytes 57376 | tf_op jit(solution)/shard_map/ppermute | solution.py:169
  13.2 3.7 %collective-permute-start.2 = (bf16[112,512]{1,0:T(8,128)(2,1)S(1)}, bf16[112,512]{1,0:T(8,128)(2,1)S(1)}, u32[]{:S(2)}, u32[]{:S(2)}) collective-permute-start(bf16[112,512]{1,0:T(8,128)(2,1)S(1)} %join.9.refs_0_), channel_id=1, source_target_pairs={{0,24},{1,9},{2,26},{3,11},{4,28},{5,13},{6,30},{7,15},{8,16},{9,1... | collective-permute-start | bytes 344072 | tf_op jit(solution)/shard_map/ppermute | solution.py:169
  16.9 5.4 %collective-permute-done.1.refs_1_ = bf16[96,512]{1,0:T(8,128)(2,1)S(1)} collective-permute-done((bf16[96,512]{1,0:T(8,128)(2,1)}, bf16[96,512]{1,0:T(8,128)(2,1)S(1)}, u32[]{:S(2)}, u32[]{:S(2)}) %collective-permute-start.1) | collective-permute-done | bytes 98336 | tf_op jit(solution)/shard_map/ppermute | solution.py:169
  23.7 3.0 %collective-permute-start.5 = (bf16[192,512]{1,0:T(8,128)(2,1)S(1)}, bf16[192,512]{1,0:T(8,128)(2,1)S(1)}, u32[]{:S(2)}, u32[]{:S(2)}) collective-permute-start(bf16[192,512]{1,0:T(8,128)(2,1)S(1)} %join.10.refs_0_), channel_id=1, source_target_pairs={{0,24},{1,9},{2,26},{3,11},{4,28},{5,13},{6,30},{7,15},{8,16},{9,1... | collective-permute-start | bytes 589832 | tf_op jit(solution)/shard_map/ppermute | solution.py:169
  27.5 7.2 %collective-permute-done.3.refs_1_ = bf16[128,512]{1,0:T(8,128)(2,1)S(1)} collective-permute-done((bf16[128,512]{1,0:T(8,128)(2,1)}, bf16[128,512]{1,0:T(8,128)(2,1)S(1)}, u32[]{:S(2)}, u32[]{:S(2)}) %collective-permute-start.3) | collective-permute-done | bytes 131104 | tf_op jit(solution)/shard_map/ppermute | solution.py:169
  38.7 6.8 %collective-permute-done.6.refs_1_ = bf16[256,512]{1,0:T(8,128)(2,1)S(1)} collective-permute-done((bf16[256,512]{1,0:T(8,128)(2,1)S(1)}, bf16[256,512]{1,0:T(8,128)(2,1)S(1)}, u32[]{:S(2)}, u32[]{:S(2)}) %collective-permute-start.6) | collective-permute-done | bytes 262176 | tf_op jit(solution)/shard_map/ppermute | solution.py:169
  53.4 8.3 %self_attention.1 = (bf16[256,512]{1,0:T(8,128)(2,1)S(1)}, bf16[256,512]{1,0:T(8,128)(2,1)S(1)}, f32[4,1,512]{2,1,0:T(1,128)S(1)}, f32[4,1,512]{2,1,0:T(1,128)S(1)}) custom-call(s32[1]{0:T(128)} %bitcast.me_ref.refs_0_, bf16[256,512]{1,0:T(8,128)(2,1)S(1)} %get-tuple-element.193.refs_0_, bf16[256,512]{1,0:T(8,128)(2,1)S(1)} %get-tuple-element.194.refs_1_, ...), custom_call_target="tpu_custom_call" | custom-call | flops 1 | bytes 1 | tf_op jit(solution)/shard_map/self_attention/pallas_call | solution.py:255
  67.0 5.4 %cross_forward.1 = (f32[512,512]{1,0:T(8,128)S(1)}, f32[512,512]{1,0:T(8,128)S(1)}, bf16[512,512]{1,0:T(8,128)(2,1)S(1)}, bf16[256,512]{1,0:T(8,128)(2,1)S(1)}, ...) custom-call(s32[1]{0:T(128)} %bitcast.me_ref.refs_0_, ...), custom_call_target="tpu_custom_call" | custom-call | flops 1 | bytes 1 | tf_op jit(solution)/shard_map/cross_forward/pallas_call | solution.py:255
  72.4 4.9 %collective-permute-done.15.refs_2_ = bf16[1024,512]{1,0:T(8,128)(2,1)S(1)} collective-permute-done((bf16[1024,512]{1,0:T(8,128)(2,1)S(1)}, bf16[1024,512]{1,0:T(8,128)(2,1)S(1)}, u32[]{:S(2)}, u32[]{:S(2)}) %collective-permute-start.15) | collective-permute-done | bytes 1048608 | tf_op jit(solution)/shard_map/ppermute | solution.py:169
  77.3 2.7 %collective-permute-done.20.refs_4_ = bf16[1024,512]{1,0:T(8,128)(2,1)S(1)} collective-permute-done((bf16[1024,512]{1,0:T(8,128)(2,1)S(1)}, bf16[1024,512]{1,0:T(8,128)(2,1)S(1)}, u32[]{:S(2)}, u32[]{:S(2)}) %collective-permute-start.20) | collective-permute-done | bytes 1048608 | tf_op jit(solution)/shard_map/ppermute | solution.py:161
  80.0 12.4 %inner.1 = (f32[256,512]{1,0:T(8,128)S(1)}, bf16[256,512]{1,0:T(8,128)(2,1)S(1)}, f32[512,512]{1,0:T(8,128)S(1)}, f32[8,512]{1,0:T(8,128)S(1)}, bf16[16,128,512]...) custom-call(s32[1]{0:T(128)} %bitcast.me_ref.refs_0_, bf16[1024,512]{1,0:T(8,128)(2,1)S(1)} %join.17.refs_1_, ...), custom_call_target="tpu_custom_call" | custom-call | flops 1 | bytes 1 | tf_op jit(solution)/shard_map/inner/pallas_call | solution.py:255
  94.3 8.4 %cross_back.1 = (f32[512,512]{1,0:T(8,128)S(1)}, f32[128,512]{1,0:T(8,128)S(1)}, f32[128,512]{1,0:T(8,128)S(1)}, f32[16,512]{1,0:T(8,128)S(1)}, bf16[512,256]{1,...) custom-call(s32[1]{0:T(128)} %bitcast.me_ref.refs_0_, ...), custom_call_target="tpu_custom_call" | custom-call | flops 1 | bytes 1 | tf_op jit(solution)/shard_map/cross_back/pallas_call | solution.py:255
  106.4 6.0 %self_back_upper.1 = (bf16[512,256]{1,0:T(8,128)(2,1)S(1)}, f32[1024,256]{1,0:T(8,128)S(1)}, bf16[512,256]{1,0:T(8,128)(2,1)S(1)}, bf16[512,256]{1,0:T(8,128)(2,1)S(1)}) custom-call(s32[1]{0:T(128)} %bitcast.me_ref.refs_0_, bf16[512,256]{1,0:T(8,128)(2,1)S(1)} %get-tuple-element.238.refs_1_, bf16[1024,256]{1,0:T(8,128)(2,1)S(1)} %get-tuple-element.195.refs_2_, ...), custom_call_target="tpu_custom_call" | custom-call | flops 1 | bytes 1 | tf_op jit(solution)/shard_map/self_back_upper/pallas_call | solution.py:255
  114.2 7.0 %self_back_lower.1 = (f32[512,512]{1,0:T(8,128)S(1)}, f32[8,512]{1,0:T(8,128)S(1)}, bf16[512,512]{1,0:T(8,128)(2,1)S(1)}, f32[1024,256]{1,0:T(8,128)S(1)}, bf16[...) custom-call(s32[1]{0:T(128)} %bitcast.me_ref.refs_0_, bf16[448,512]{1,0:T(8,128)(2,1)S(1)} %join.13.refs_1_, ...), custom_call_target="tpu_custom_call" | custom-call | flops 1 | bytes 1 | tf_op jit(solution)/shard_map/self_back_lower/pallas_call | solution.py:255
  121.4 4.5 %collective-permute-done.25.refs_1_ = bf16[8,128,512]{2,1,0:T(8,128)(2,1)S(1)} collective-permute-done((bf16[8,128,512]{2,1,0:T(8,128)(2,1)S(1)}, bf16[8,128,512]{2,1,0:T(8,128)(2,1)S(1)}, u32[]{:S(2)}, u32[]{:S(2)}) %collective-permute-start.25) | collective-permute-done | bytes 1048608 | tf_op jit(solution)/shard_map/ppermute | solution.py:169
  126.1 2.4 %collective-permute-done.26.refs_1_ = bf16[8,96,512]{2,1,0:T(8,128)(2,1)S(1)} collective-permute-done((bf16[8,96,512]{2,1,0:T(8,128)(2,1)S(1)}, bf16[8,96,512]{2,1,0:T(8,128)(2,1)S(1)}, u32[]{:S(2)}, u32[]{:S(2)}) %collective-permute-start.26) | collective-permute-done | bytes 786464 | tf_op jit(solution)/shard_map/ppermute | solution.py:169
  135.8 7.1 %collective-permute-done.34.refs_1_ = bf16[4,128,512]{2,1,0:T(8,128)(2,1)S(1)} collective-permute-done((bf16[4,128,512]{2,1,0:T(8,128)(2,1)S(1)}, bf16[4,128,512]{2,1,0:T(8,128)(2,1)S(1)}, u32[]{:S(2)}, u32[]{:S(2)}) %collective-permute-start.34) | collective-permute-done | bytes 524320 | tf_op jit(solution)/shard_map/ppermute | solution.py:169
  142.9 5.3 %collective-permute-done.35.refs_3_ = bf16[4,96,512]{2,1,0:T(8,128)(2,1)S(1)} collective-permute-done((bf16[4,96,512]{2,1,0:T(8,128)(2,1)S(1)}, bf16[4,96,512]{2,1,0:T(8,128)(2,1)S(1)}, u32[]{:S(2)}, u32[]{:S(2)}) %collective-permute-start.35) | collective-permute-done | bytes 393248 | tf_op jit(solution)/shard_map/ppermute | solution.py:169
  154.5 7.7 %collective-permute-done.36.refs_1_ = bf16[2,224,512]{2,1,0:T(8,128)(2,1)S(1)} collective-permute-done((bf16[2,224,512]{2,1,0:T(8,128)(2,1)S(1)}, bf16[2,224,512]{2,1,0:T(8,128)(2,1)S(1)}, u32[]{:S(2)}, u32[]{:S(2)}) %collective-permute-start.36) | collective-permute-done | bytes 458784 | tf_op jit(solution)/shard_map/ppermute | solution.py:169
  166.3 5.9 %collective-permute-done.39.refs_1_ = bf16[2,56,512]{2,1,0:T(8,128)(2,1)S(1)} collective-permute-done((bf16[2,56,512]{2,1,0:T(8,128)(2,1)S(1)}, bf16[2,56,512]{2,1,0:T(8,128)(2,1)S(1)}, u32[]{:S(2)}, u32[]{:S(2)}) %collective-permute-start.39) | collective-permute-done | bytes 114720 | tf_op jit(solution)/shard_map/ppermute | solution.py:169
  173.1 3.4 %collective-permute-done.40.refs_3_ = bf16[1,56,512]{2,1,0:T(8,128)(2,1)S(1)} collective-permute-done((bf16[1,56,512]{2,1,0:T(8,128)(2,1)S(1)}, bf16[1,56,512]{2,1,0:T(8,128)(2,1)S(1)}, u32[]{:S(2)}, u32[]{:S(2)}) %collective-permute-start.40) | collective-permute-done | bytes 57376 | tf_op jit(solution)/shard_map/ppermute | solution.py:169
  (108 shorter events, 49.6 us)
Async XLA Ops:
  3.1 23.6 %collective-permute-start.7 = (bf16[584,512]{1,0:T(8,128)(2,1)}, bf16[584,512]{1,0:T(8,128)(2,1)S(1)}, u32[]{:S(2)}, u32[]{:S(2)}) collective-permute-start(bf16[584,512]{1,0:T(8,128)(2,1)} %get-tuple-element.173), channel_id=1, source_target_pairs={{0,2},{1,3},{2,0},{3,1},{4,6},{5,7},{6,4},{7,5},{8,10},{9,11},{10,... | collective-permute-start | bytes 1794056 | tf_op jit(solution)/shard_map/ppermute | solution.py:161
  6.0 28.6 %collective-permute-start.8 = (bf16[584,512]{1,0:T(8,128)(2,1)}, bf16[584,512]{1,0:T(8,128)(2,1)S(1)}, u32[]{:S(2)}, u32[]{:S(2)}) collective-permute-start(bf16[584,512]{1,0:T(8,128)(2,1)} %get-tuple-element.183.refs_5_.refs_6_), channel_id=1, source_target_pairs={{0,1},{1,0},{2,3},{3,2},{4,5},{5,4},{6,7},{7,6},{8,9},{9,8},{10,11... | collective-permute-start | bytes 1794056 | tf_op jit(solution)/shard_map/ppermute | solution.py:161
  22.3 12.4 %collective-permute-start.4 = (bf16[224,512]{1,0:T(8,128)(2,1)S(1)}, bf16[224,512]{1,0:T(8,128)(2,1)S(1)}, u32[]{:S(2)}, u32[]{:S(2)}) collective-permute-start(bf16[224,512]{1,0:T(8,128)(2,1)S(1)} %join.11.refs_0_), channel_id=1, source_target_pairs={{0,2},{1,5},{2,0},{3,7},{4,6},{5,1},{6,4},{7,3},{8,10},{9,13},{10,... | collective-permute-start | bytes 688136 | tf_op jit(solution)/shard_map/ppermute | solution.py:169
  23.7 11.0 %collective-permute-start.5 = (bf16[192,512]{1,0:T(8,128)(2,1)S(1)}, bf16[192,512]{1,0:T(8,128)(2,1)S(1)}, u32[]{:S(2)}, u32[]{:S(2)}) collective-permute-start(bf16[192,512]{1,0:T(8,128)(2,1)S(1)} %join.10.refs_0_), channel_id=1, source_target_pairs={{0,24},{1,9},{2,26},{3,11},{4,28},{5,13},{6,30},{7,15},{8,16},{9,1... | collective-permute-start | bytes 589832 | tf_op jit(solution)/shard_map/ppermute | solution.py:169
  26.7 22.5 %collective-permute-start.12 = (bf16[584,512]{1,0:T(8,128)(2,1)S(1)}, bf16[584,512]{1,0:T(8,128)(2,1)S(1)}, u32[]{:S(2)}, u32[]{:S(2)}) collective-permute-start(bf16[584,512]{1,0:T(8,128)(2,1)S(1)} %collective-permute-done.7.refs_6_.refs_7_), channel_id=1, source_target_pairs={{0,1},{1,0},{2,3},{3,2},{4,5},{5,4},{6,7},{7,6},{8,9},{9,8},{10,11... | collective-permute-start | bytes 1794056 | tf_op jit(solution)/shard_map/ppermute | solution.py:161
  34.7 12.3 %collective-permute-start.9 = (bf16[448,512]{1,0:T(8,128)(2,1)S(1)}, bf16[448,512]{1,0:T(8,128)(2,1)S(1)}, u32[]{:S(2)}, u32[]{:S(2)}) collective-permute-start(bf16[448,512]{1,0:T(8,128)(2,1)S(1)} %join.13.refs_1_), channel_id=1, source_target_pairs={{0,4},{1,3},{2,6},{3,1},{4,0},{5,7},{6,2},{7,5},{8,12},{9,11},{10,... | collective-permute-start | bytes 1376264 | tf_op jit(solution)/shard_map/ppermute | solution.py:169
  36.4 10.5 %collective-permute-start.10 = (bf16[384,512]{1,0:T(8,128)(2,1)S(1)}, bf16[384,512]{1,0:T(8,128)(2,1)S(1)}, u32[]{:S(2)}, u32[]{:S(2)}) collective-permute-start(bf16[384,512]{1,0:T(8,128)(2,1)S(1)} %join.14.refs_0_), channel_id=1, source_target_pairs={{0,2},{1,5},{2,0},{3,7},{4,6},{5,1},{6,4},{7,3},{8,10},{9,13},{10,... | collective-permute-start | bytes 1179656 | tf_op jit(solution)/shard_map/ppermute | solution.py:169
  47.0 17.3 %collective-permute-start.16 = (bf16[768,512]{1,0:T(8,128)(2,1)S(1)}, bf16[768,512]{1,0:T(8,128)(2,1)S(1)}, u32[]{:S(2)}, u32[]{:S(2)}) collective-permute-start(bf16[768,512]{1,0:T(8,128)(2,1)S(1)} %join.16.refs_1_), channel_id=1, source_target_pairs={{0,4},{1,3},{2,6},{3,1},{4,0},{5,7},{6,2},{7,5},{8,12},{9,11},{10,... | collective-permute-start | bytes 2359304 | tf_op jit(solution)/shard_map/ppermute | solution.py:169
  47.4 14.9 %collective-permute-start.11 = (bf16[512,512]{1,0:T(8,128)(2,1)S(1)}, bf16[512,512]{1,0:T(8,128)(2,1)S(1)}, u32[]{:S(2)}, u32[]{:S(2)}) collective-permute-start(bf16[512,512]{1,0:T(8,128)(2,1)S(1)} %join.15.refs_0_), channel_id=1, source_target_pairs={{0,2},{1,5},{2,0},{3,7},{4,6},{5,1},{6,4},{7,3},{8,10},{9,13},{10,... | collective-permute-start | bytes 1572872 | tf_op jit(solution)/shard_map/ppermute | solution.py:169
  62.4 14.9 %collective-permute-start.15 = (bf16[1024,512]{1,0:T(8,128)(2,1)S(1)}, bf16[1024,512]{1,0:T(8,128)(2,1)S(1)}, u32[]{:S(2)}, u32[]{:S(2)}) collective-permute-start(bf16[1024,512]{1,0:T(8,128)(2,1)S(1)} %join.17.refs_1_), channel_id=1, source_target_pairs={{0,4},{1,3},{2,6},{3,1},{4,0},{5,7},{6,2},{7,5},{8,12},{9,11},{10,... | collective-permute-start | bytes 3145736 | tf_op jit(solution)/shard_map/ppermute | solution.py:169
  64.4 12.9 %collective-permute-start.19 = (bf16[1024,512]{1,0:T(8,128)(2,1)S(1)}, bf16[1024,512]{1,0:T(8,128)(2,1)S(1)}, u32[]{:S(2)}, u32[]{:S(2)}) collective-permute-start(bf16[1024,512]{1,0:T(8,128)(2,1)S(1)} %join.17.refs_1_), channel_id=1, source_target_pairs={{0,1},{1,0},{2,3},{3,2},{4,5},{5,4},{6,7},{7,6},{8,9},{9,8},{10,11... | collective-permute-start | bytes 3145736 | tf_op jit(solution)/shard_map/ppermute | solution.py:161
  92.3 10.5 %collective-permute-start.22 = (bf16[16,128,512]{2,1,0:T(8,128)(2,1)S(1)}, bf16[16,128,512]{2,1,0:T(8,128)(2,1)S(1)}, u32[]{:S(2)}, u32[]{:S(2)}) collective-permute-start(bf16[16,128,512]{2,1,0:T(8,128)(2,1)S(1)} %get-tuple-element.223), channel_id=1, source_target_pairs={{0,1},{1,0},{2,3},{3,2},{4,5},{5,4},{6,7},{7,6},{8,9},{9,8},{10,11... | collective-permute-start | bytes 6291464 | tf_op jit(solution)/shard_map/ppermute | solution.py:161
  92.5 10.3 %collective-permute-start.21 = (bf16[256,512]{1,0:T(8,128)(2,1)S(1)}, bf16[256,512]{1,0:T(8,128)(2,1)S(1)}, u32[]{:S(2)}, u32[]{:S(2)}) collective-permute-start(bf16[256,512]{1,0:T(8,128)(2,1)S(1)} %get-tuple-element.211), channel_id=1, source_target_pairs={{0,2},{1,3},{2,0},{3,1},{4,6},{5,7},{6,4},{7,5},{8,10},{9,11},{10,... | collective-permute-start | bytes 786440 | tf_op jit(solution)/shard_map/ppermute | solution.py:161
  105.8 20.0 %collective-permute-start.25 = (bf16[8,128,512]{2,1,0:T(8,128)(2,1)S(1)}, bf16[8,128,512]{2,1,0:T(8,128)(2,1)S(1)}, u32[]{:S(2)}, u32[]{:S(2)}) collective-permute-start(bf16[8,128,512]{2,1,0:T(8,128)(2,1)S(1)} %get-tuple-element.255), channel_id=1, source_target_pairs={{0,4},{1,3},{2,6},{3,1},{4,0},{5,7},{6,2},{7,5},{8,12},{9,11},{10,... | collective-permute-start | bytes 3145736 | tf_op jit(solution)/shard_map/ppermute | solution.py:169
  112.8 15.7 %collective-permute-start.26 = (bf16[8,96,512]{2,1,0:T(8,128)(2,1)S(1)}, bf16[8,96,512]{2,1,0:T(8,128)(2,1)S(1)}, u32[]{:S(2)}, u32[]{:S(2)}) collective-permute-start(bf16[8,96,512]{2,1,0:T(8,128)(2,1)S(1)} %get-tuple-element.260), channel_id=1, source_target_pairs={{0,2},{1,5},{2,0},{3,7},{4,6},{5,1},{6,4},{7,3},{8,10},{9,13},{10,... | collective-permute-start | bytes 2359304 | tf_op jit(solution)/shard_map/ppermute | solution.py:169
  113.7 14.9 %collective-permute-start.27 = (bf16[512,256]{1,0:T(8,128)(2,1)S(1)}, bf16[512,256]{1,0:T(8,128)(2,1)S(1)}, u32[]{:S(2)}, u32[]{:S(2)}) collective-permute-start(bf16[512,256]{1,0:T(8,128)(2,1)S(1)} %get-tuple-element.269), channel_id=1, source_target_pairs={{0,1},{1,0},{2,3},{3,2},{4,5},{5,4},{6,7},{7,6},{8,9},{9,8},{10,11... | collective-permute-start | bytes 786440 | tf_op jit(solution)/shard_map/ppermute | solution.py:161
  113.7 14.9 %collective-permute-start.28 = (bf16[512,256]{1,0:T(8,128)(2,1)S(1)}, bf16[512,256]{1,0:T(8,128)(2,1)S(1)}, u32[]{:S(2)}, u32[]{:S(2)}) collective-permute-start(bf16[512,256]{1,0:T(8,128)(2,1)S(1)} %get-tuple-element.270), channel_id=1, source_target_pairs={{0,1},{1,0},{2,3},{3,2},{4,5},{5,4},{6,7},{7,6},{8,9},{9,8},{10,11... | collective-permute-start | bytes 786440 | tf_op jit(solution)/shard_map/ppermute | solution.py:161
  130.8 12.1 %collective-permute-start.34 = (bf16[4,128,512]{2,1,0:T(8,128)(2,1)S(1)}, bf16[4,128,512]{2,1,0:T(8,128)(2,1)S(1)}, u32[]{:S(2)}, u32[]{:S(2)}) collective-permute-start(bf16[4,128,512]{2,1,0:T(8,128)(2,1)S(1)} %get-tuple-element.280), channel_id=1, source_target_pairs={{0,2},{1,5},{2,0},{3,7},{4,6},{5,1},{6,4},{7,3},{8,10},{9,13},{10,... | collective-permute-start | bytes 1572872 | tf_op jit(solution)/shard_map/ppermute | solution.py:169
  133.8 16.4 %collective-permute-start.32 = (bf16[8,56,512]{2,1,0:T(8,128)(2,1)}, bf16[8,56,512]{2,1,0:T(8,128)(2,1)S(1)}, u32[]{:S(2)}, u32[]{:S(2)}) collective-permute-start(bf16[8,56,512]{2,1,0:T(8,128)(2,1)} %get-tuple-element.277), channel_id=1, source_target_pairs={{0,4},{1,3},{2,6},{3,1},{4,0},{5,7},{6,2},{7,5},{8,12},{9,11},{10,... | collective-permute-start | bytes 1376264 | tf_op jit(solution)/shard_map/ppermute | solution.py:169
  134.3 13.9 %collective-permute-start.35 = (bf16[4,96,512]{2,1,0:T(8,128)(2,1)S(1)}, bf16[4,96,512]{2,1,0:T(8,128)(2,1)S(1)}, u32[]{:S(2)}, u32[]{:S(2)}) collective-permute-start(bf16[4,96,512]{2,1,0:T(8,128)(2,1)S(1)} %get-tuple-element.281), channel_id=1, source_target_pairs={{0,4},{1,3},{2,6},{3,1},{4,0},{5,7},{6,2},{7,5},{8,12},{9,11},{10,... | collective-permute-start | bytes 1179656 | tf_op jit(solution)/shard_map/ppermute | solution.py:169
  148.5 13.8 %collective-permute-start.36 = (bf16[2,224,512]{2,1,0:T(8,128)(2,1)S(1)}, bf16[2,224,512]{2,1,0:T(8,128)(2,1)S(1)}, u32[]{:S(2)}, u32[]{:S(2)}) collective-permute-start(bf16[2,224,512]{2,1,0:T(8,128)(2,1)S(1)} %get-tuple-element.287), channel_id=1, source_target_pairs={{0,24},{1,9},{2,26},{3,11},{4,28},{5,13},{6,30},{7,15},{8,16},{9,1... | collective-permute-start | bytes 1376264 | tf_op jit(solution)/shard_map/ppermute | solution.py:169
  150.3 13.2 %collective-permute-start.38 = (bf16[4,56,512]{2,1,0:T(8,128)(2,1)S(1)}, bf16[4,56,512]{2,1,0:T(8,128)(2,1)S(1)}, u32[]{:S(2)}, u32[]{:S(2)}) collective-permute-start(bf16[4,56,512]{2,1,0:T(8,128)(2,1)S(1)} %get-tuple-element.294), channel_id=1, source_target_pairs={{0,2},{1,5},{2,0},{3,7},{4,6},{5,1},{6,4},{7,3},{8,10},{9,13},{10,... | collective-permute-start | bytes 688136 | tf_op jit(solution)/shard_map/ppermute | solution.py:169
  150.7 14.5 %collective-permute-start.33 = (bf16[320,512]{1,0:T(8,128)(2,1)}, bf16[320,512]{1,0:T(8,128)(2,1)S(1)}, u32[]{:S(2)}, u32[]{:S(2)}) collective-permute-start(bf16[320,512]{1,0:T(8,128)(2,1)} %copy-done.4), channel_id=1, source_target_pairs={{0,2},{1,3},{2,0},{3,1},{4,6},{5,7},{6,4},{7,5},{8,10},{9,11},{10,... | collective-permute-start | bytes 983048 | tf_op jit(solution)/shard_map/ppermute | solution.py:161
  162.3 10.7 %collective-permute-start.37 = (bf16[1,224,512]{2,1,0:T(8,128)(2,1)S(1)}, bf16[1,224,512]{2,1,0:T(8,128)(2,1)S(1)}, u32[]{:S(2)}, u32[]{:S(2)}) collective-permute-start(bf16[1,224,512]{2,1,0:T(8,128)(2,1)S(1)} %get-tuple-element.289), channel_id=1, source_target_pairs={{0,8},{1,25},{2,10},{3,27},{4,12},{5,29},{6,14},{7,31},{8,0},{9,17... | collective-permute-start | bytes 688136 | tf_op jit(solution)/shard_map/ppermute | solution.py:169
  (23 other events, 150.7 us)

commit v14 on v13

--- a/solution.py
+++ b/solution.py
@@ -1012,6 +1012,9 @@
     row_memory, ids, memory_ids = found[10:]
     query_t = list(query_t)
     if packed:
+        third_c = join(after([third, third_b], query_t[1]))
+        third_d = turned_swap(third_c, 3)
+        query_t[0] = after(query_t[0], third_c)
         set_query, set_last = set_self, set_self
     else:
         set_back, set_query, set_last, set_memory = [full[3], full[4], full[7]], full[:1], full[1:3], full[5:7]
@@ -1021,8 +1024,6 @@
     )
     mixtures, logs = found[:2], found[2:]
     if packed:
-        third_c = join(after([third, third_b], mixtures[0]))
-        third_d = turned_swap(third_c, 3)
         second_d = after(second_d, mixtures[0])
         set_cross = [second_c, second_d, swap(second_c, 1, 32), swap(second_d, 1, 32)]
         set_back, set_memory = set_cross, set_cross
@@ -1091,16 +1092,16 @@
     if packed:
         keep, send = combine([grads_last[0], swap(grads_last[1], 1, 32)], 2)
         last_step = [keep, turned_swap(send, 3)]
-        in_send = after(in_send, last_step[1])
-        keep_joint, send = combine_joint(after([inner_step, cross_step], in_own), 2)
+        keep, send = combine(last_step, 2)
+        last_step = [keep, turned_swap(send, 2)]
+        keep_joint, send = combine_joint(after([inner_step, cross_step], in_own, keep), 2)
         joint_step = [keep_joint, turned_swap(send, 1)]
         keep, send = combine(after(last_step, keep_joint), 2)
-        last_step = [keep, turned_swap(send, 2)]
-        keep_joint, send = combine(joint_step, 2)
+        last_step = [keep, turned_swap(send, 1)]
+        in_send = after(in_send, keep)
+        keep_joint, send = combine(after(joint_step, keep), 2)
         joint_step = [keep_joint, turned_swap(send, 0)]
         keep, send = combine(after(last_step, keep_joint), 2)
-        last_step = [keep, turned_swap(send, 1)]
-        keep, send = combine(last_step, 2)
         last_step = [keep, turned_swap(send, 0)]
 
         def plan(me_ref, *refs):

time: 179 us -> 188 us (1.050)
  starting transfers between devices: 34.7 us -> 43.6 us
    ppermute x22, starting transfers between devices: 24.9 us -> 33.9 us  [turned_swap(): lax.ppermute(array, AXES, [(i, i ^ orders[i % 2][step]) for i in range(32)])]
  transfers between devices with their start and end apart: 41 -> 41, of which waited for: 23 -> 22; matrix products, arithmetic and copies ran while one was open for 2% -> 2% of each run, Pallas kernels for 23% -> 22%
where the time goes in v14:
time: 188 us
  waiting for transfers between devices  76.3 us (41%)
  Pallas kernels  60.4 us (32%)
  starting transfers between devices  43.6 us (23%)
  other arithmetic  3.94 us (2%)
  local copies, waits for them, and re-layouts  2.29 us (1%)
    ppermute x22, waiting for transfers between devices, turned_swap(): lax.ppermute(array, AXES, [(i, i ^ orders[i % 2][step]) for i in range(32)])  67.1 us
    pallas_call x12, Pallas kernels, call(): pl.pallas_call(kernel, out_shape=[jax.ShapeDtypeStruct(s, d) for s, d in...  57.6 us
    ppermute x22, starting transfers between devices, turned_swap(): lax.ppermute(array, AXES, [(i, i ^ orders[i % 2][step]) for i in range(32)])  33.9 us
    ppermute x19, starting transfers between devices, swap(): return lax.ppermute(array, AXES, [(i, i ^ mask) for i in range(devices)])  9.7 us
    ppermute x19, waiting for transfers between devices, swap(): return lax.ppermute(array, AXES, [(i, i ^ mask) for i in range(devices)])  9.21 us
  transfers between devices with their start and end apart: 41, of which 22 were waited for; matrix products, arithmetic and copies ran while one was open for 2% of the time, Pallas kernels for 22%

profile of v14, /device:TPU:0, one launch (start us, length us, event | category | flops | bytes accessed | tf_op | source)
XLA Modules:
  0.0 187.8 jit_solution(14917831565579091815)
XLA Ops:
  0.7 2.4 %tokens_packet.1 = (bf16[584,512]{1,0:T(8,128)(2,1)}, bf16[584,512]{1,0:T(8,128)(2,1)}) custom-call(s32[1]{0:T(128)} %bitcast.15.turn_ref, s32[2,256]{1,0:T(2,128)} %targets.1, s32[2,64]{1,0:T(2,128)} %sources.1, bf16[2,256,512]{2,1,0:T(8,128)(2,1)} %tokens_ref.1, bf16[2,64,512]{2,1,0:T(8,128)(2,1)} %memory_ref.1, bf16[2,256,512]{2,1,0:T(8,128)(2,1)} %cot_ref.1), custom_call_target="tpu_custom_call" | custom-call | flops 1 | bytes 1 | tf_op jit(solution)/shard_map/tokens_packet/pallas_call | solution.py:255
  3.1 3.0 %collective-permute-start.7 = (bf16[584,512]{1,0:T(8,128)(2,1)}, bf16[584,512]{1,0:T(8,128)(2,1)S(1)}, u32[]{:S(2)}, u32[]{:S(2)}) collective-permute-start(bf16[584,512]{1,0:T(8,128)(2,1)} %get-tuple-element.176), channel_id=1, source_target_pairs={{0,2},{1,3},{2,0},{3,1},{4,6},{5,7},{6,4},{7,5},{8,10},{9,11},{10,... | collective-permute-start | bytes 1794056 | tf_op jit(solution)/shard_map/ppermute | solution.py:161
  9.6 2.8 %collective-permute-done.refs_1_ = bf16[56,512]{1,0:T(8,128)(2,1)S(1)} collective-permute-done((bf16[56,512]{1,0:T(8,128)(2,1)}, bf16[56,512]{1,0:T(8,128)(2,1)S(1)}, u32[]{:S(2)}, u32[]{:S(2)}) %collective-permute-start) | collective-permute-done | bytes 57376 | tf_op jit(solution)/shard_map/ppermute | solution.py:169
  13.2 3.7 %collective-permute-start.2 = (bf16[112,512]{1,0:T(8,128)(2,1)S(1)}, bf16[112,512]{1,0:T(8,128)(2,1)S(1)}, u32[]{:S(2)}, u32[]{:S(2)}) collective-permute-start(bf16[112,512]{1,0:T(8,128)(2,1)S(1)} %join.9.refs_0_), channel_id=1, source_target_pairs={{0,24},{1,9},{2,26},{3,11},{4,28},{5,13},{6,30},{7,15},{8,16},{9,1... | collective-permute-start | bytes 344072 | tf_op jit(solution)/shard_map/ppermute | solution.py:169
  16.9 5.4 %collective-permute-done.1.refs_1_ = bf16[96,512]{1,0:T(8,128)(2,1)S(1)} collective-permute-done((bf16[96,512]{1,0:T(8,128)(2,1)}, bf16[96,512]{1,0:T(8,128)(2,1)S(1)}, u32[]{:S(2)}, u32[]{:S(2)}) %collective-permute-start.1) | collective-permute-done | bytes 98336 | tf_op jit(solution)/shard_map/ppermute | solution.py:169
  23.7 3.0 %collective-permute-start.5 = (bf16[192,512]{1,0:T(8,128)(2,1)S(1)}, bf16[192,512]{1,0:T(8,128)(2,1)S(1)}, u32[]{:S(2)}, u32[]{:S(2)}) collective-permute-start(bf16[192,512]{1,0:T(8,128)(2,1)S(1)} %join.10.refs_0_), channel_id=1, source_target_pairs={{0,24},{1,9},{2,26},{3,11},{4,28},{5,13},{6,30},{7,15},{8,16},{9,1... | collective-permute-start | bytes 589832 | tf_op jit(solution)/shard_map/ppermute | solution.py:169
  27.5 7.2 %collective-permute-done.3.refs_1_ = bf16[128,512]{1,0:T(8,128)(2,1)S(1)} collective-permute-done((bf16[128,512]{1,0:T(8,128)(2,1)}, bf16[128,512]{1,0:T(8,128)(2,1)S(1)}, u32[]{:S(2)}, u32[]{:S(2)}) %collective-permute-start.3) | collective-permute-done | bytes 131104 | tf_op jit(solution)/shard_map/ppermute | solution.py:169
  38.7 6.8 %collective-permute-done.6.refs_1_ = bf16[256,512]{1,0:T(8,128)(2,1)S(1)} collective-permute-done((bf16[256,512]{1,0:T(8,128)(2,1)S(1)}, bf16[256,512]{1,0:T(8,128)(2,1)S(1)}, u32[]{:S(2)}, u32[]{:S(2)}) %collective-permute-start.6) | collective-permute-done | bytes 262176 | tf_op jit(solution)/shard_map/ppermute | solution.py:169
  53.4 8.9 %collective-permute-done.11.refs_1_ = bf16[512,512]{1,0:T(8,128)(2,1)S(1)} collective-permute-done((bf16[512,512]{1,0:T(8,128)(2,1)S(1)}, bf16[512,512]{1,0:T(8,128)(2,1)S(1)}, u32[]{:S(2)}, u32[]{:S(2)}) %collective-permute-start.11) | collective-permute-done | bytes 524320 | tf_op jit(solution)/shard_map/ppermute | solution.py:169
  63.0 8.3 %self_attention.1 = (bf16[256,512]{1,0:T(8,128)(2,1)S(1)}, bf16[256,512]{1,0:T(8,128)(2,1)S(1)}, f32[4,1,512]{2,1,0:T(1,128)S(1)}, f32[4,1,512]{2,1,0:T(1,128)S(1)}) custom-call(s32[1]{0:T(128)} %bitcast.me_ref.refs_0_, bf16[256,512]{1,0:T(8,128)(2,1)S(1)} %get-tuple-element.200.refs_0_, bf16[256,512]{1,0:T(8,128)(2,1)S(1)} %get-tuple-element.196.refs_1_, ...), custom_call_target="tpu_custom_call" | custom-call | flops 1 | bytes 1 | tf_op jit(solution)/shard_map/self_attention/pallas_call | solution.py:255
  73.8 5.4 %cross_forward.1 = (f32[512,512]{1,0:T(8,128)S(1)}, f32[512,512]{1,0:T(8,128)S(1)}, bf16[512,512]{1,0:T(8,128)(2,1)S(1)}, bf16[256,512]{1,0:T(8,128)(2,1)S(1)}, ...) custom-call(s32[1]{0:T(128)} %bitcast.me_ref.refs_0_, ...), custom_call_target="tpu_custom_call" | custom-call | flops 1 | bytes 1 | tf_op jit(solution)/shard_map/cross_forward/pallas_call | solution.py:255
  79.7 2.3 %collective-permute-done.20.refs_4_ = bf16[1024,512]{1,0:T(8,128)(2,1)S(1)} collective-permute-done((bf16[1024,512]{1,0:T(8,128)(2,1)S(1)}, bf16[1024,512]{1,0:T(8,128)(2,1)S(1)}, u32[]{:S(2)}, u32[]{:S(2)}) %collective-permute-start.20) | collective-permute-done | bytes 1048608 | tf_op jit(solution)/shard_map/ppermute | solution.py:161
  82.0 12.4 %inner.1 = (f32[256,512]{1,0:T(8,128)S(1)}, bf16[256,512]{1,0:T(8,128)(2,1)S(1)}, f32[512,512]{1,0:T(8,128)S(1)}, f32[8,512]{1,0:T(8,128)S(1)}, bf16[16,128,512]...) custom-call(s32[1]{0:T(128)} %bitcast.me_ref.refs_0_, bf16[1024,512]{1,0:T(8,128)(2,1)S(1)} %join.17.refs_1_, ...), custom_call_target="tpu_custom_call" | custom-call | flops 1 | bytes 1 | tf_op jit(solution)/shard_map/inner/pallas_call | solution.py:255
  96.5 8.4 %cross_back.1 = (f32[512,512]{1,0:T(8,128)S(1)}, f32[128,512]{1,0:T(8,128)S(1)}, f32[128,512]{1,0:T(8,128)S(1)}, f32[16,512]{1,0:T(8,128)S(1)}, bf16[512,256]{1,...) custom-call(s32[1]{0:T(128)} %bitcast.me_ref.refs_0_, ...), custom_call_target="tpu_custom_call" | custom-call | flops 1 | bytes 1 | tf_op jit(solution)/shard_map/cross_back/pallas_call | solution.py:255
  109.5 6.0 %self_back_upper.1 = (bf16[512,256]{1,0:T(8,128)(2,1)S(1)}, f32[1024,256]{1,0:T(8,128)S(1)}, bf16[512,256]{1,0:T(8,128)(2,1)S(1)}, bf16[512,256]{1,0:T(8,128)(2,1)S(1)}) custom-call(s32[1]{0:T(128)} %bitcast.me_ref.refs_0_, bf16[512,256]{1,0:T(8,128)(2,1)S(1)} %get-tuple-element.242.refs_1_, bf16[1024,256]{1,0:T(8,128)(2,1)S(1)} %get-tuple-element.201.refs_2_, ...), custom_call_target="tpu_custom_call" | custom-call | flops 1 | bytes 1 | tf_op jit(solution)/shard_map/self_back_upper/pallas_call | solution.py:255
  116.8 7.0 %self_back_lower.1 = (f32[512,512]{1,0:T(8,128)S(1)}, f32[8,512]{1,0:T(8,128)S(1)}, bf16[512,512]{1,0:T(8,128)(2,1)S(1)}, f32[1024,256]{1,0:T(8,128)S(1)}, bf16[...) custom-call(s32[1]{0:T(128)} %bitcast.me_ref.refs_0_, bf16[448,512]{1,0:T(8,128)(2,1)S(1)} %join.13.refs_1_, ...), custom_call_target="tpu_custom_call" | custom-call | flops 1 | bytes 1 | tf_op jit(solution)/shard_map/self_back_lower/pallas_call | solution.py:255
  124.0 4.1 %collective-permute-done.25.refs_1_ = bf16[8,128,512]{2,1,0:T(8,128)(2,1)S(1)} collective-permute-done((bf16[8,128,512]{2,1,0:T(8,128)(2,1)S(1)}, bf16[8,128,512]{2,1,0:T(8,128)(2,1)S(1)}, u32[]{:S(2)}, u32[]{:S(2)}) %collective-permute-start.25) | collective-permute-done | bytes 1048608 | tf_op jit(solution)/shard_map/ppermute | solution.py:169
  128.4 2.3 %collective-permute-done.26.refs_1_ = bf16[8,96,512]{2,1,0:T(8,128)(2,1)S(1)} collective-permute-done((bf16[8,96,512]{2,1,0:T(8,128)(2,1)S(1)}, bf16[8,96,512]{2,1,0:T(8,128)(2,1)S(1)}, u32[]{:S(2)}, u32[]{:S(2)}) %collective-permute-start.26) | collective-permute-done | bytes 786464 | tf_op jit(solution)/shard_map/ppermute | solution.py:169
  137.7 11.0 %collective-permute-done.32.refs_1_ = bf16[8,56,512]{2,1,0:T(8,128)(2,1)S(1)} collective-permute-done((bf16[8,56,512]{2,1,0:T(8,128)(2,1)S(1)}, bf16[8,56,512]{2,1,0:T(8,128)(2,1)S(1)}, u32[]{:S(2)}, u32[]{:S(2)}) %collective-permute-start.32) | collective-permute-done | bytes 458784 | tf_op jit(solution)/shard_map/ppermute | solution.py:169
  149.5 2.3 %collective-permute-done.34.refs_1_ = bf16[4,128,512]{2,1,0:T(8,128)(2,1)S(1)} collective-permute-done((bf16[4,128,512]{2,1,0:T(8,128)(2,1)S(1)}, bf16[4,128,512]{2,1,0:T(8,128)(2,1)S(1)}, u32[]{:S(2)}, u32[]{:S(2)}) %collective-permute-start.34) | collective-permute-done | bytes 524320 | tf_op jit(solution)/shard_map/ppermute | solution.py:169
  151.7 3.9 %collective-permute-done.35.refs_3_ = bf16[4,96,512]{2,1,0:T(8,128)(2,1)S(1)} collective-permute-done((bf16[4,96,512]{2,1,0:T(8,128)(2,1)S(1)}, bf16[4,96,512]{2,1,0:T(8,128)(2,1)S(1)}, u32[]{:S(2)}, u32[]{:S(2)}) %collective-permute-start.35) | collective-permute-done | bytes 393248 | tf_op jit(solution)/shard_map/ppermute | solution.py:169
  162.8 5.5 %collective-permute-done.37.refs_1_ = bf16[2,224,512]{2,1,0:T(8,128)(2,1)S(1)} collective-permute-done((bf16[2,224,512]{2,1,0:T(8,128)(2,1)S(1)}, bf16[2,224,512]{2,1,0:T(8,128)(2,1)S(1)}, u32[]{:S(2)}, u32[]{:S(2)}) %collective-permute-start.37) | collective-permute-done | bytes 458784 | tf_op jit(solution)/shard_map/ppermute | solution.py:169
  169.8 10.2 %collective-permute-start.40 = (bf16[1,56,512]{2,1,0:T(8,128)(2,1)S(1)}, bf16[1,56,512]{2,1,0:T(8,128)(2,1)S(1)}, u32[]{:S(2)}, u32[]{:S(2)}) collective-permute-start(bf16[1,56,512]{2,1,0:T(8,128)(2,1)S(1)} %get-tuple-element.306), channel_id=1, source_target_pairs={{0,8},{1,25},{2,10},{3,27},{4,12},{5,29},{6,14},{7,31},{8,0},{9,17... | collective-permute-start | bytes 172040 | tf_op jit(solution)/shard_map/ppermute | solution.py:169
  182.1 3.9 %collective-permute-done.38.refs_1_ = bf16[1,224,512]{2,1,0:T(8,128)(2,1)S(1)} collective-permute-done((bf16[1,224,512]{2,1,0:T(8,128)(2,1)S(1)}, bf16[1,224,512]{2,1,0:T(8,128)(2,1)S(1)}, u32[]{:S(2)}, u32[]{:S(2)}) %collective-permute-start.38) | collective-permute-done | bytes 229408 | tf_op jit(solution)/shard_map/ppermute | solution.py:169
  (106 shorter events, 50.4 us)
Async XLA Ops:
  3.1 23.6 %collective-permute-start.7 = (bf16[584,512]{1,0:T(8,128)(2,1)}, bf16[584,512]{1,0:T(8,128)(2,1)S(1)}, u32[]{:S(2)}, u32[]{:S(2)}) collective-permute-start(bf16[584,512]{1,0:T(8,128)(2,1)} %get-tuple-element.176), channel_id=1, source_target_pairs={{0,2},{1,3},{2,0},{3,1},{4,6},{5,7},{6,4},{7,5},{8,10},{9,11},{10,... | collective-permute-start | bytes 1794056 | tf_op jit(solution)/shard_map/ppermute | solution.py:161
  6.0 28.6 %collective-permute-start.8 = (bf16[584,512]{1,0:T(8,128)(2,1)}, bf16[584,512]{1,0:T(8,128)(2,1)S(1)}, u32[]{:S(2)}, u32[]{:S(2)}) collective-permute-start(bf16[584,512]{1,0:T(8,128)(2,1)} %get-tuple-element.186.refs_5_.refs_6_), channel_id=1, source_target_pairs={{0,1},{1,0},{2,3},{3,2},{4,5},{5,4},{6,7},{7,6},{8,9},{9,8},{10,11... | collective-permute-start | bytes 1794056 | tf_op jit(solution)/shard_map/ppermute | solution.py:161
  13.2 9.1 %collective-permute-start.2 = (bf16[112,512]{1,0:T(8,128)(2,1)S(1)}, bf16[112,512]{1,0:T(8,128)(2,1)S(1)}, u32[]{:S(2)}, u32[]{:S(2)}) collective-permute-start(bf16[112,512]{1,0:T(8,128)(2,1)S(1)} %join.9.refs_0_), channel_id=1, source_target_pairs={{0,24},{1,9},{2,26},{3,11},{4,28},{5,13},{6,30},{7,15},{8,16},{9,1... | collective-permute-start | bytes 344072 | tf_op jit(solution)/shard_map/ppermute | solution.py:169
  22.3 12.4 %collective-permute-start.4 = (bf16[224,512]{1,0:T(8,128)(2,1)S(1)}, bf16[224,512]{1,0:T(8,128)(2,1)S(1)}, u32[]{:S(2)}, u32[]{:S(2)}) collective-permute-start(bf16[224,512]{1,0:T(8,128)(2,1)S(1)} %join.11.refs_0_), channel_id=1, source_target_pairs={{0,2},{1,5},{2,0},{3,7},{4,6},{5,1},{6,4},{7,3},{8,10},{9,13},{10,... | collective-permute-start | bytes 688136 | tf_op jit(solution)/shard_map/ppermute | solution.py:169
  23.7 11.0 %collective-permute-start.5 = (bf16[192,512]{1,0:T(8,128)(2,1)S(1)}, bf16[192,512]{1,0:T(8,128)(2,1)S(1)}, u32[]{:S(2)}, u32[]{:S(2)}) collective-permute-start(bf16[192,512]{1,0:T(8,128)(2,1)S(1)} %join.10.refs_0_), channel_id=1, source_target_pairs={{0,24},{1,9},{2,26},{3,11},{4,28},{5,13},{6,30},{7,15},{8,16},{9,1... | collective-permute-start | bytes 589832 | tf_op jit(solution)/shard_map/ppermute | solution.py:169
  26.7 22.5 %collective-permute-start.12 = (bf16[584,512]{1,0:T(8,128)(2,1)S(1)}, bf16[584,512]{1,0:T(8,128)(2,1)S(1)}, u32[]{:S(2)}, u32[]{:S(2)}) collective-permute-start(bf16[584,512]{1,0:T(8,128)(2,1)S(1)} %collective-permute-done.7.refs_6_.refs_7_), channel_id=1, source_target_pairs={{0,1},{1,0},{2,3},{3,2},{4,5},{5,4},{6,7},{7,6},{8,9},{9,8},{10,11... | collective-permute-start | bytes 1794056 | tf_op jit(solution)/shard_map/ppermute | solution.py:161
  34.7 12.3 %collective-permute-start.9 = (bf16[448,512]{1,0:T(8,128)(2,1)S(1)}, bf16[448,512]{1,0:T(8,128)(2,1)S(1)}, u32[]{:S(2)}, u32[]{:S(2)}) collective-permute-start(bf16[448,512]{1,0:T(8,128)(2,1)S(1)} %join.13.refs_1_), channel_id=1, source_target_pairs={{0,4},{1,3},{2,6},{3,1},{4,0},{5,7},{6,2},{7,5},{8,12},{9,11},{10,... | collective-permute-start | bytes 1376264 | tf_op jit(solution)/shard_map/ppermute | solution.py:169
  36.4 10.5 %collective-permute-start.10 = (bf16[384,512]{1,0:T(8,128)(2,1)S(1)}, bf16[384,512]{1,0:T(8,128)(2,1)S(1)}, u32[]{:S(2)}, u32[]{:S(2)}) collective-permute-start(bf16[384,512]{1,0:T(8,128)(2,1)S(1)} %join.14.refs_0_), channel_id=1, source_target_pairs={{0,2},{1,5},{2,0},{3,7},{4,6},{5,1},{6,4},{7,3},{8,10},{9,13},{10,... | collective-permute-start | bytes 1179656 | tf_op jit(solution)/shard_map/ppermute | solution.py:169
  47.0 24.3 %collective-permute-start.16 = (bf16[768,512]{1,0:T(8,128)(2,1)S(1)}, bf16[768,512]{1,0:T(8,128)(2,1)S(1)}, u32[]{:S(2)}, u32[]{:S(2)}) collective-permute-start(bf16[768,512]{1,0:T(8,128)(2,1)S(1)} %join.16.refs_1_), channel_id=1, source_target_pairs={{0,4},{1,3},{2,6},{3,1},{4,0},{5,7},{6,2},{7,5},{8,12},{9,11},{10,... | collective-permute-start | bytes 2359304 | tf_op jit(solution)/shard_map/ppermute | solution.py:169
  47.4 14.9 %collective-permute-start.11 = (bf16[512,512]{1,0:T(8,128)(2,1)S(1)}, bf16[512,512]{1,0:T(8,128)(2,1)S(1)}, u32[]{:S(2)}, u32[]{:S(2)}) collective-permute-start(bf16[512,512]{1,0:T(8,128)(2,1)S(1)} %join.15.refs_0_), channel_id=1, source_target_pairs={{0,2},{1,5},{2,0},{3,7},{4,6},{5,1},{6,4},{7,3},{8,10},{9,13},{10,... | collective-permute-start | bytes 1572872 | tf_op jit(solution)/shard_map/ppermute | solution.py:169
  62.4 16.8 %collective-permute-start.15 = (bf16[1024,512]{1,0:T(8,128)(2,1)S(1)}, bf16[1024,512]{1,0:T(8,128)(2,1)S(1)}, u32[]{:S(2)}, u32[]{:S(2)}) collective-permute-start(bf16[1024,512]{1,0:T(8,128)(2,1)S(1)} %join.17.refs_1_), channel_id=1, source_target_pairs={{0,4},{1,3},{2,6},{3,1},{4,0},{5,7},{6,2},{7,5},{8,12},{9,11},{10,... | collective-permute-start | bytes 3145736 | tf_op jit(solution)/shard_map/ppermute | solution.py:169
  94.3 10.7 %collective-permute-start.22 = (bf16[16,128,512]{2,1,0:T(8,128)(2,1)S(1)}, bf16[16,128,512]{2,1,0:T(8,128)(2,1)S(1)}, u32[]{:S(2)}, u32[]{:S(2)}) collective-permute-start(bf16[16,128,512]{2,1,0:T(8,128)(2,1)S(1)} %get-tuple-element.227), channel_id=1, source_target_pairs={{0,1},{1,0},{2,3},{3,2},{4,5},{5,4},{6,7},{7,6},{8,9},{9,8},{10,11... | collective-permute-start | bytes 6291464 | tf_op jit(solution)/shard_map/ppermute | solution.py:161
  94.8 10.3 %collective-permute-start.21 = (bf16[256,512]{1,0:T(8,128)(2,1)S(1)}, bf16[256,512]{1,0:T(8,128)(2,1)S(1)}, u32[]{:S(2)}, u32[]{:S(2)}) collective-permute-start(bf16[256,512]{1,0:T(8,128)(2,1)S(1)} %get-tuple-element.215), channel_id=1, source_target_pairs={{0,2},{1,3},{2,0},{3,1},{4,6},{5,7},{6,4},{7,5},{8,10},{9,11},{10,... | collective-permute-start | bytes 786440 | tf_op jit(solution)/shard_map/ppermute | solution.py:161
  108.1 20.0 %collective-permute-start.25 = (bf16[8,128,512]{2,1,0:T(8,128)(2,1)S(1)}, bf16[8,128,512]{2,1,0:T(8,128)(2,1)S(1)}, u32[]{:S(2)}, u32[]{:S(2)}) collective-permute-start(bf16[8,128,512]{2,1,0:T(8,128)(2,1)S(1)} %get-tuple-element.259), channel_id=1, source_target_pairs={{0,4},{1,3},{2,6},{3,1},{4,0},{5,7},{6,2},{7,5},{8,12},{9,11},{10,... | collective-permute-start | bytes 3145736 | tf_op jit(solution)/shard_map/ppermute | solution.py:169
  116.0 14.7 %collective-permute-start.26 = (bf16[8,96,512]{2,1,0:T(8,128)(2,1)S(1)}, bf16[8,96,512]{2,1,0:T(8,128)(2,1)S(1)}, u32[]{:S(2)}, u32[]{:S(2)}) collective-permute-start(bf16[8,96,512]{2,1,0:T(8,128)(2,1)S(1)} %get-tuple-element.264), channel_id=1, source_target_pairs={{0,2},{1,5},{2,0},{3,7},{4,6},{5,1},{6,4},{7,3},{8,10},{9,13},{10,... | collective-permute-start | bytes 2359304 | tf_op jit(solution)/shard_map/ppermute | solution.py:169
  116.3 14.6 %collective-permute-start.27 = (bf16[512,256]{1,0:T(8,128)(2,1)S(1)}, bf16[512,256]{1,0:T(8,128)(2,1)S(1)}, u32[]{:S(2)}, u32[]{:S(2)}) collective-permute-start(bf16[512,256]{1,0:T(8,128)(2,1)S(1)} %get-tuple-element.273), channel_id=1, source_target_pairs={{0,1},{1,0},{2,3},{3,2},{4,5},{5,4},{6,7},{7,6},{8,9},{9,8},{10,11... | collective-permute-start | bytes 786440 | tf_op jit(solution)/shard_map/ppermute | solution.py:161
  116.3 14.6 %collective-permute-start.28 = (bf16[512,256]{1,0:T(8,128)(2,1)S(1)}, bf16[512,256]{1,0:T(8,128)(2,1)S(1)}, u32[]{:S(2)}, u32[]{:S(2)}) collective-permute-start(bf16[512,256]{1,0:T(8,128)(2,1)S(1)} %get-tuple-element.274), channel_id=1, source_target_pairs={{0,1},{1,0},{2,3},{3,2},{4,5},{5,4},{6,7},{7,6},{8,9},{9,8},{10,11... | collective-permute-start | bytes 786440 | tf_op jit(solution)/shard_map/ppermute | solution.py:161
  135.3 13.4 %collective-permute-start.32 = (bf16[8,56,512]{2,1,0:T(8,128)(2,1)S(1)}, bf16[8,56,512]{2,1,0:T(8,128)(2,1)S(1)}, u32[]{:S(2)}, u32[]{:S(2)}) collective-permute-start(bf16[8,56,512]{2,1,0:T(8,128)(2,1)S(1)} %get-tuple-element.282), channel_id=1, source_target_pairs={{0,4},{1,3},{2,6},{3,1},{4,0},{5,7},{6,2},{7,5},{8,12},{9,11},{10,... | collective-permute-start | bytes 1376264 | tf_op jit(solution)/shard_map/ppermute | solution.py:169
  136.9 14.9 %collective-permute-start.34 = (bf16[4,128,512]{2,1,0:T(8,128)(2,1)S(1)}, bf16[4,128,512]{2,1,0:T(8,128)(2,1)S(1)}, u32[]{:S(2)}, u32[]{:S(2)}) collective-permute-start(bf16[4,128,512]{2,1,0:T(8,128)(2,1)S(1)} %get-tuple-element.285), channel_id=1, source_target_pairs={{0,2},{1,5},{2,0},{3,7},{4,6},{5,1},{6,4},{7,3},{8,10},{9,13},{10,... | collective-permute-start | bytes 1572872 | tf_op jit(solution)/shard_map/ppermute | solution.py:169
  137.2 18.5 %collective-permute-start.35 = (bf16[4,96,512]{2,1,0:T(8,128)(2,1)S(1)}, bf16[4,96,512]{2,1,0:T(8,128)(2,1)S(1)}, u32[]{:S(2)}, u32[]{:S(2)}) collective-permute-start(bf16[4,96,512]{2,1,0:T(8,128)(2,1)S(1)} %get-tuple-element.286), channel_id=1, source_target_pairs={{0,4},{1,3},{2,6},{3,1},{4,0},{5,7},{6,2},{7,5},{8,12},{9,11},{10,... | collective-permute-start | bytes 1179656 | tf_op jit(solution)/shard_map/ppermute | solution.py:169
  155.9 12.5 %collective-permute-start.37 = (bf16[2,224,512]{2,1,0:T(8,128)(2,1)S(1)}, bf16[2,224,512]{2,1,0:T(8,128)(2,1)S(1)}, u32[]{:S(2)}, u32[]{:S(2)}) collective-permute-start(bf16[2,224,512]{2,1,0:T(8,128)(2,1)S(1)} %get-tuple-element.297), channel_id=1, source_target_pairs={{0,24},{1,9},{2,26},{3,11},{4,28},{5,13},{6,30},{7,15},{8,16},{9,1... | collective-permute-start | bytes 1376264 | tf_op jit(solution)/shard_map/ppermute | solution.py:169
  157.7 22.3 %collective-permute-start.36 = (bf16[320,512]{1,0:T(8,128)(2,1)S(1)}, bf16[320,512]{1,0:T(8,128)(2,1)S(1)}, u32[]{:S(2)}, u32[]{:S(2)}) collective-permute-start(bf16[320,512]{1,0:T(8,128)(2,1)S(1)} %get-tuple-element.295), channel_id=1, source_target_pairs={{0,2},{1,3},{2,0},{3,1},{4,6},{5,7},{6,4},{7,5},{8,10},{9,11},{10,... | collective-permute-start | bytes 983048 | tf_op jit(solution)/shard_map/ppermute | solution.py:161
  159.6 10.2 %collective-permute-start.39 = (bf16[2,56,512]{2,1,0:T(8,128)(2,1)S(1)}, bf16[2,56,512]{2,1,0:T(8,128)(2,1)S(1)}, u32[]{:S(2)}, u32[]{:S(2)}) collective-permute-start(bf16[2,56,512]{2,1,0:T(8,128)(2,1)S(1)} %get-tuple-element.302), channel_id=1, source_target_pairs={{0,24},{1,9},{2,26},{3,11},{4,28},{5,13},{6,30},{7,15},{8,16},{9,1... | collective-permute-start | bytes 344072 | tf_op jit(solution)/shard_map/ppermute | solution.py:169
  169.8 12.4 %collective-permute-start.40 = (bf16[1,56,512]{2,1,0:T(8,128)(2,1)S(1)}, bf16[1,56,512]{2,1,0:T(8,128)(2,1)S(1)}, u32[]{:S(2)}, u32[]{:S(2)}) collective-permute-start(bf16[1,56,512]{2,1,0:T(8,128)(2,1)S(1)} %get-tuple-element.306), channel_id=1, source_target_pairs={{0,8},{1,25},{2,10},{3,27},{4,12},{5,29},{6,14},{7,31},{8,0},{9,17... | collective-permute-start | bytes 172040 | tf_op jit(solution)/shard_map/ppermute | solution.py:169
  (22 other events, 140.7 us)

commit v15 on v13

--- a/solution.py
+++ b/solution.py
@@ -195,13 +195,21 @@
         scratch[pl.ds(pl.multiple_of(device * rows, rows), rows), :] = ref[at : at + rows, :]
 
 
-def vector_sum(pieces, stride, first):
-    found = None
-    for ref in pieces:
-        for slot in range(8):
-            part = ref[slot * stride + first : (slot + 1) * stride, :].astype(F32)
-            found = part if found is None else found + part
-    return found
+def sort_vectors(me, pieces, stride, first, narrow, sheet):
+    width, blocks = sheet.shape[1], sheet.shape[0]
+    lane = lax.broadcasted_iota(jnp.int32, (8, width), 1)
+    per = width // (blocks * narrow)
+    near, far = jnp.zeros((8, width), F32), jnp.zeros((8, width), F32)
+    sheet[...] = jnp.zeros_like(sheet)
+    for core, distant, slot, device in places(me):
+        part = pieces[2 * core + distant][slot * stride + first : (slot + 1) * stride, :].astype(F32)
+        group = lane // narrow
+        near = near + jnp.where(group == device, part, 0.0)
+        far = far + jnp.where(group == lax.rem(device + 1, width // narrow), part, 0.0)
+        wide = jnp.where(lane[7:8, :] // (blocks * narrow) == lax.rem(device, per), part[7:8, :], 0.0)
+        sheet[pl.ds(lax.div(device, per), 1), :] += wide
+    far = pltpu.roll(far, width - narrow, 1)
+    return jnp.concatenate([near[:7, :], far[:6, :]], axis=0)
 
 
 class Grads:
@@ -309,19 +317,16 @@
             else:
                 second[(i - 3) * narrow : (i - 2) * narrow, :] = ref[...]
         short = jnp.concatenate([ref[...].astype(F32) for ref in short], axis=0).astype(BF16)
-        found = placed(me, short, width)
-        first[3 * narrow :, :] = jnp.concatenate([found[:2, :], jnp.zeros((6, width), F32)], axis=0).astype(BF16)
-        per = width // wide.shape[1]
-        row = placed(lax.rem(me, per), wide[...], width)
-        place = lax.broadcasted_iota(jnp.int32, (blocks, width), 0)
-        spread_row = jnp.where(place == lax.div(me, per), row, 0.0)
-        none = jnp.zeros((16 - (found.shape[0] - 2) - blocks, width), F32)
-        second[5 * narrow :, :] = jnp.concatenate([found[2:, :], spread_row, none], axis=0).astype(BF16)
+        near = placed(me, short[:7, :], width)
+        far = placed(lax.rem(me + 1, width // narrow), short[7:, :], width)
+        far = jnp.concatenate([far, jnp.zeros((1, width), F32)], axis=0)
+        row = placed(lax.rem(me, width // wide.shape[1]), wide[...], width)
+        first[3 * narrow :, :] = jnp.concatenate([near + far, row], axis=0).astype(BF16)
         for i in range(blocks):
             third[i * narrow : (i + 1) * narrow, :] = inner[:, i * width : (i + 1) * width]
         third[tall:, :] = outer[...]
 
-    return kernel, [((rows, width), BF16) for rows in (3 * narrow + 8, 5 * narrow + 16, 2 * tall)]
+    return kernel, [((rows, width), BF16) for rows in (3 * narrow + 8, 5 * narrow, 2 * tall)]
 
 
 def join(arrays):
@@ -343,7 +348,7 @@
     )(*arrays)
 
 
-def make_project(packed, parts, rows, block, memory_block, width, narrow, n_pieces):
+def make_project(packed, parts, rows, block, memory_block, width, narrow, blocks, n_pieces):
     share = rows * block
     length = parts * share
     memory_share = rows * memory_block
@@ -355,17 +360,20 @@
         pieces, refs = refs[:n_pieces], refs[n_pieces:]
         tokens, refs = refs[: parts * rows], refs[parts * rows :]
         query, query_t, keys, values, value_t = (refs[2 * i : 2 * i + 2] for i in range(5))
-        memory, ids, memory_ids = refs[10:13]
-        scratch = refs[13:]
+        memory, ids, memory_ids, vectors = refs[10:14]
+        scratch = refs[14:]
         me = me_ref[0]
         if packed:
             for i in range(3):
                 unpack(me, pieces, stride, i * narrow, narrow, scratch[i])
-            query_w, key_w, value_w = scratch
-            biases = vector_sum(pieces, stride, 3 * narrow)
+            query_w, key_w, value_w, sheet = scratch
+            biases = sort_vectors(me, pieces, stride, 3 * narrow, narrow, sheet)
+            rest = jnp.zeros((5 - sheet.shape[0], width), F32)
+            vectors[...] = jnp.concatenate([biases[2:, :], sheet[...], rest], axis=0)
         else:
             query_w, key_w, value_w = pieces[:3]
-            biases = pieces[3][...]
+            biases = pieces[3][:8, :]
+            vectors[...] = pieces[3][8:, :]
         for i in range(parts):
             here = slice(i * share, (i + 1) * share)
             some = tokens[i * rows : (i + 1) * rows]
@@ -395,8 +403,9 @@
         ((parts * memory_share, width), BF16),
         ((1, length), jnp.int32),
         ((1, parts * memory_share), jnp.int32),
+        ((16, width), F32),
     ]
-    return kernel, outs, [((width, width), BF16)] * 3 if packed else []
+    return kernel, outs, [((width, width), BF16)] * 3 + [((blocks, width), F32)] if packed else []
 
 
 def make_self_attention(share, length, width):
@@ -414,24 +423,22 @@
 
 def make_cross_forward(packed, rows, block, memory_length, width, narrow, n_pieces):
     share = rows * block
-    stride = 5 * narrow + 16
+    stride = 5 * narrow
 
     def kernel(*refs):
         me_ref, refs = refs[0], list(refs[1:])
         pieces, refs = refs[:n_pieces], refs[n_pieces:]
         tokens, refs = refs[:rows], refs[rows:]
-        memory, ids, memory_ids, upper, lower = refs[:5]
-        first_sum, second_sum, query, memory_keys, memory_values, cross_t, logs, vectors = refs[5:13]
+        memory, ids, memory_ids, upper, lower, vectors = refs[:6]
+        first_sum, second_sum, query, memory_keys, memory_values, cross_t, logs = refs[6:13]
         scratch = refs[13:]
         query_t, value_t, hot, penalty = scratch[:4]
         if packed:
             for i in range(5):
                 unpack(me_ref[0], pieces, stride, i * narrow, narrow, scratch[4 + i])
             output_w, query_w, key_w, value_w, source_w = scratch[4:]
-            vectors[...] = vector_sum(pieces, stride, 5 * narrow)
         else:
             output_w, query_w, key_w, value_w, source_w = pieces[:5]
-            vectors[...] = pieces[5][...]
 
         def vector(i):
             return vectors[i : i + 1, :]
@@ -461,7 +468,6 @@
         ((memory_length, width), BF16),
         ((width, share), BF16),
         ((HEADS, 1, share), F32),
-        ((16, width), F32),
     ]
     scratch = [((width, share), BF16), ((width, memory_length), BF16), ((memory_length, PAIR), BF16), ((PAIR, share), BF16)]
     if packed:
@@ -563,7 +569,7 @@
 
 def make_cross_back(packed, parts, share, memory_share, width, narrow, n_pieces):
     memory_length = parts * memory_share
-    stride = 5 * narrow + 16
+    stride = 5 * narrow
 
     def kernel(*refs):
         me_ref, refs = refs[0], list(refs[1:])
@@ -712,7 +718,7 @@
         me = me_ref[0]
         if packed:
             for i in range(2):
-                unpack(me, pieces, 5 * narrow + 16, (2 + i) * narrow, narrow, scratch[1 + i])
+                unpack(me, pieces, 5 * narrow, (2 + i) * narrow, narrow, scratch[1 + i])
             source_key, source_value = scratch[1:3]
         else:
             source_key, source_value = pieces
@@ -998,18 +1004,18 @@
 
         vectors = jnp.concatenate([natural(jnp.stack(short[:2])), jnp.zeros((6, width), BF16), natural(jnp.stack(short[2:])), spread_wide, jnp.zeros((1, width), BF16)])
         vectors = reduce_all(vectors, devices).astype(F32)
-        set_self = full[:3] + [vectors[:8]]
-        set_cross = full[3:] + [vectors[8:]]
+        set_self = full[:3] + [vectors]
+        set_cross = full[3:]
         set_inner = [
             whole(inner_weight).reshape(width, blocks, width).transpose(1, 0, 2),
             whole(outer_weight).reshape(blocks, width, width),
         ]
     found = run(
-        make_project(packed, parts, rows, block, memory_block, width, narrow, len(set_self)), 5.0,
+        make_project(packed, parts, rows, block, memory_block, width, narrow, blocks, len(set_self)), 5.0,
         "project", *set_self, *row_tokens,
     )
     query, query_t, keys, values, value_t = (found[2 * i : 2 * i + 2] for i in range(5))
-    row_memory, ids, memory_ids = found[10:]
+    row_memory, ids, memory_ids, vectors = found[10:]
     query_t = list(query_t)
     if packed:
         set_query, set_last = set_self, set_self
@@ -1026,9 +1032,9 @@
         second_d = after(second_d, mixtures[0])
         set_cross = [second_c, second_d, swap(second_c, 1, 32), swap(second_d, 1, 32)]
         set_back, set_memory = set_cross, set_cross
-    first_sum, second_sum, cross_query, memory_keys, memory_values, cross_t, cross_logs, vectors = run(
+    first_sum, second_sum, cross_query, memory_keys, memory_values, cross_t, cross_logs = run(
         make_cross_forward(packed, rows, block, parts * memory_share, width, narrow, len(set_cross)),
-        9.0, "cross_forward", *set_cross, *own_tokens, row_memory, ids, memory_ids, *mixtures,
+        9.0, "cross_forward", *set_cross, *own_tokens, row_memory, ids, memory_ids, *mixtures, vectors,
     )
     if packed:
         third_d = after(third_d, second_sum)
@@ -1092,10 +1098,10 @@
         keep, send = combine([grads_last[0], swap(grads_last[1], 1, 32)], 2)
         last_step = [keep, turned_swap(send, 3)]
         in_send = after(in_send, last_step[1])
-        keep_joint, send = combine_joint(after([inner_step, cross_step], in_own), 2)
+        keep, send = combine(last_step, 2)
+        last_step = [keep, turned_swap(send, 2)]
+        keep_joint, send = combine_joint(after([inner_step, cross_step], in_own, keep), 2)
         joint_step = [keep_joint, turned_swap(send, 1)]
-        keep, send = combine(after(last_step, keep_joint), 2)
-        last_step = [keep, turned_swap(send, 2)]
         keep_joint, send = combine(joint_step, 2)
         joint_step = [keep_joint, turned_swap(send, 0)]
         keep, send = combine(after(last_step, keep_joint), 2)

time: 179 us -> 178 us (level)
    ppermute x22, waiting for transfers between devices: 66.2 us -> 61.3 us  [turned_swap(): lax.ppermute(array, AXES, [(i, i ^ orders[i % 2][step]) for i in range(32)])]
    ppermute x19, waiting for transfers between devices: 9.55 us -> 13.2 us  [swap(): return lax.ppermute(array, AXES, [(i, i ^ mask) for i in range(devices)])]
  transfers between devices with their start and end apart: 41 -> 41, of which waited for: 23 -> 22; matrix products, arithmetic and copies ran while one was open for 2% -> 2% of each run, Pallas kernels for 23% -> 23%
where the time goes in v15:
time: 178 us
  waiting for transfers between devices  74.5 us (42%)
  Pallas kernels  61.3 us (34%)
  starting transfers between devices  34.9 us (20%)
  other arithmetic  3.96 us (2%)
  local copies, waits for them, and re-layouts  2.29 us (1%)
    ppermute x22, waiting for transfers between devices, turned_swap(): lax.ppermute(array, AXES, [(i, i ^ orders[i % 2][step]) for i in range(32)])  61.3 us
    pallas_call x12, Pallas kernels, call(): pl.pallas_call(kernel, out_shape=[jax.ShapeDtypeStruct(s, d) for s, d in...  57.7 us
    ppermute x22, starting transfers between devices, turned_swap(): lax.ppermute(array, AXES, [(i, i ^ orders[i % 2][step]) for i in range(32)])  25.1 us
    ppermute x19, waiting for transfers between devices, swap(): return lax.ppermute(array, AXES, [(i, i ^ mask) for i in range(devices)])  13.2 us
    ppermute x19, starting transfers between devices, swap(): return lax.ppermute(array, AXES, [(i, i ^ mask) for i in range(devices)])  9.73 us
  transfers between devices with their start and end apart: 41, of which 22 were waited for; matrix products, arithmetic and copies ran while one was open for 2% of the time, Pallas kernels for 23%

profile of v15, /device:TPU:0, one launch (start us, length us, event | category | flops | bytes accessed | tf_op | source)
XLA Modules:
  0.0 178.1 jit_solution(2504082696070483189)
XLA Ops:
  0.7 2.4 %tokens_packet.1 = (bf16[584,512]{1,0:T(8,128)(2,1)}, bf16[584,512]{1,0:T(8,128)(2,1)}) custom-call(s32[1]{0:T(128)} %bitcast.15.turn_ref, s32[2,256]{1,0:T(2,128)} %targets.1, s32[2,64]{1,0:T(2,128)} %sources.1, bf16[2,256,512]{2,1,0:T(8,128)(2,1)} %tokens_ref.1, bf16[2,64,512]{2,1,0:T(8,128)(2,1)} %memory_ref.1, bf16[2,256,512]{2,1,0:T(8,128)(2,1)} %cot_ref.1), custom_call_target="tpu_custom_call" | custom-call | flops 1 | bytes 1 | tf_op jit(solution)/shard_map/tokens_packet/pallas_call | solution.py:263
  3.1 3.0 %collective-permute-start.7 = (bf16[584,512]{1,0:T(8,128)(2,1)}, bf16[584,512]{1,0:T(8,128)(2,1)S(1)}, u32[]{:S(2)}, u32[]{:S(2)}) collective-permute-start(bf16[584,512]{1,0:T(8,128)(2,1)} %get-tuple-element.171), channel_id=1, source_target_pairs={{0,2},{1,3},{2,0},{3,1},{4,6},{5,7},{6,4},{7,5},{8,10},{9,11},{10,... | collective-permute-start | bytes 1794056 | tf_op jit(solution)/shard_map/ppermute | solution.py:161
  9.5 2.8 %collective-permute-done.refs_1_ = bf16[56,512]{1,0:T(8,128)(2,1)S(1)} collective-permute-done((bf16[56,512]{1,0:T(8,128)(2,1)}, bf16[56,512]{1,0:T(8,128)(2,1)S(1)}, u32[]{:S(2)}, u32[]{:S(2)}) %collective-permute-start) | collective-permute-done | bytes 57376 | tf_op jit(solution)/shard_map/ppermute | solution.py:169
  13.2 3.7 %collective-permute-start.2 = (bf16[112,512]{1,0:T(8,128)(2,1)S(1)}, bf16[112,512]{1,0:T(8,128)(2,1)S(1)}, u32[]{:S(2)}, u32[]{:S(2)}) collective-permute-start(bf16[112,512]{1,0:T(8,128)(2,1)S(1)} %join.9.refs_0_), channel_id=1, source_target_pairs={{0,24},{1,9},{2,26},{3,11},{4,28},{5,13},{6,30},{7,15},{8,16},{9,1... | collective-permute-start | bytes 344072 | tf_op jit(solution)/shard_map/ppermute | solution.py:169
  16.8 5.0 %collective-permute-done.1.refs_1_ = bf16[80,512]{1,0:T(8,128)(2,1)S(1)} collective-permute-done((bf16[80,512]{1,0:T(8,128)(2,1)}, bf16[80,512]{1,0:T(8,128)(2,1)S(1)}, u32[]{:S(2)}, u32[]{:S(2)}) %collective-permute-start.1) | collective-permute-done | bytes 81952 | tf_op jit(solution)/shard_map/ppermute | solution.py:169
  23.2 2.9 %collective-permute-start.5 = (bf16[160,512]{1,0:T(8,128)(2,1)S(1)}, bf16[160,512]{1,0:T(8,128)(2,1)S(1)}, u32[]{:S(2)}, u32[]{:S(2)}) collective-permute-start(bf16[160,512]{1,0:T(8,128)(2,1)S(1)} %join.10.refs_0_), channel_id=1, source_target_pairs={{0,24},{1,9},{2,26},{3,11},{4,28},{5,13},{6,30},{7,15},{8,16},{9,1... | collective-permute-start | bytes 491528 | tf_op jit(solution)/shard_map/ppermute | solution.py:169
  27.1 6.5 %collective-permute-done.3.refs_1_ = bf16[128,512]{1,0:T(8,128)(2,1)S(1)} collective-permute-done((bf16[128,512]{1,0:T(8,128)(2,1)}, bf16[128,512]{1,0:T(8,128)(2,1)S(1)}, u32[]{:S(2)}, u32[]{:S(2)}) %collective-permute-start.3) | collective-permute-done | bytes 131104 | tf_op jit(solution)/shard_map/ppermute | solution.py:169
  37.9 6.6 %collective-permute-done.6.refs_1_ = bf16[256,512]{1,0:T(8,128)(2,1)S(1)} collective-permute-done((bf16[256,512]{1,0:T(8,128)(2,1)S(1)}, bf16[256,512]{1,0:T(8,128)(2,1)S(1)}, u32[]{:S(2)}, u32[]{:S(2)}) %collective-permute-start.6) | collective-permute-done | bytes 262176 | tf_op jit(solution)/shard_map/ppermute | solution.py:169
  51.3 8.3 %self_attention.1 = (bf16[256,512]{1,0:T(8,128)(2,1)S(1)}, bf16[256,512]{1,0:T(8,128)(2,1)S(1)}, f32[4,1,512]{2,1,0:T(1,128)S(1)}, f32[4,1,512]{2,1,0:T(1,128)S(1)}) custom-call(s32[1]{0:T(128)} %bitcast.me_ref.refs_0_, bf16[256,512]{1,0:T(8,128)(2,1)S(1)} %get-tuple-element.191.refs_0_, bf16[256,512]{1,0:T(8,128)(2,1)S(1)} %get-tuple-element.192.refs_1_, ...), custom_call_target="tpu_custom_call" | custom-call | flops 1 | bytes 1 | tf_op jit(solution)/shard_map/self_attention/pallas_call | solution.py:263
  63.1 5.4 %cross_forward.1 = (f32[512,512]{1,0:T(8,128)S(1)}, f32[512,512]{1,0:T(8,128)S(1)}, bf16[512,512]{1,0:T(8,128)(2,1)S(1)}, bf16[256,512]{1,0:T(8,128)(2,1)S(1)}, ...) custom-call(s32[1]{0:T(128)} %bitcast.me_ref.refs_0_, ...), custom_call_target="tpu_custom_call" | custom-call | flops 1 | bytes 1 | tf_op jit(solution)/shard_map/cross_forward/pallas_call | solution.py:263
  68.4 6.1 %collective-permute-done.15.refs_2_ = bf16[1024,512]{1,0:T(8,128)(2,1)S(1)} collective-permute-done((bf16[1024,512]{1,0:T(8,128)(2,1)S(1)}, bf16[1024,512]{1,0:T(8,128)(2,1)S(1)}, u32[]{:S(2)}, u32[]{:S(2)}) %collective-permute-start.15) | collective-permute-done | bytes 1048608 | tf_op jit(solution)/shard_map/ppermute | solution.py:169
  74.5 2.7 %collective-permute-done.20.refs_4_ = bf16[1024,512]{1,0:T(8,128)(2,1)S(1)} collective-permute-done((bf16[1024,512]{1,0:T(8,128)(2,1)S(1)}, bf16[1024,512]{1,0:T(8,128)(2,1)S(1)}, u32[]{:S(2)}, u32[]{:S(2)}) %collective-permute-start.20) | collective-permute-done | bytes 1048608 | tf_op jit(solution)/shard_map/ppermute | solution.py:161
  77.2 12.4 %inner.1 = (f32[256,512]{1,0:T(8,128)S(1)}, bf16[256,512]{1,0:T(8,128)(2,1)S(1)}, f32[512,512]{1,0:T(8,128)S(1)}, f32[8,512]{1,0:T(8,128)S(1)}, bf16[16,128,512]...) custom-call(s32[1]{0:T(128)} %bitcast.me_ref.refs_0_, bf16[1024,512]{1,0:T(8,128)(2,1)S(1)} %join.17.refs_1_, ...), custom_call_target="tpu_custom_call" | custom-call | flops 1 | bytes 1 | tf_op jit(solution)/shard_map/inner/pallas_call | solution.py:263
  91.9 8.4 %cross_back.1 = (f32[512,512]{1,0:T(8,128)S(1)}, f32[128,512]{1,0:T(8,128)S(1)}, f32[128,512]{1,0:T(8,128)S(1)}, f32[16,512]{1,0:T(8,128)S(1)}, bf16[512,256]{1,...) custom-call(s32[1]{0:T(128)} %bitcast.me_ref.refs_0_, ...), custom_call_target="tpu_custom_call" | custom-call | flops 1 | bytes 1 | tf_op jit(solution)/shard_map/cross_back/pallas_call | solution.py:263
  103.5 6.1 %self_back_upper.1 = (bf16[512,256]{1,0:T(8,128)(2,1)S(1)}, f32[1024,256]{1,0:T(8,128)S(1)}, bf16[512,256]{1,0:T(8,128)(2,1)S(1)}, bf16[512,256]{1,0:T(8,128)(2,1)S(1)}) custom-call(s32[1]{0:T(128)} %bitcast.me_ref.refs_0_, bf16[512,256]{1,0:T(8,128)(2,1)S(1)} %get-tuple-element.236.refs_1_, bf16[1024,256]{1,0:T(8,128)(2,1)S(1)} %get-tuple-element.193.refs_2_, ...), custom_call_target="tpu_custom_call" | custom-call | flops 1 | bytes 1 | tf_op jit(solution)/shard_map/self_back_upper/pallas_call | solution.py:263
  110.8 7.1 %self_back_lower.1 = (f32[512,512]{1,0:T(8,128)S(1)}, f32[8,512]{1,0:T(8,128)S(1)}, bf16[512,512]{1,0:T(8,128)(2,1)S(1)}, f32[1024,256]{1,0:T(8,128)S(1)}, bf16[...) custom-call(s32[1]{0:T(128)} %bitcast.me_ref.refs_0_, bf16[448,512]{1,0:T(8,128)(2,1)S(1)} %join.13.refs_1_, ...), custom_call_target="tpu_custom_call" | custom-call | flops 1 | bytes 1 | tf_op jit(solution)/shard_map/self_back_lower/pallas_call | solution.py:263
  118.1 5.4 %collective-permute-done.25.refs_1_ = bf16[8,128,512]{2,1,0:T(8,128)(2,1)S(1)} collective-permute-done((bf16[8,128,512]{2,1,0:T(8,128)(2,1)S(1)}, bf16[8,128,512]{2,1,0:T(8,128)(2,1)S(1)}, u32[]{:S(2)}, u32[]{:S(2)}) %collective-permute-start.25) | collective-permute-done | bytes 1048608 | tf_op jit(solution)/shard_map/ppermute | solution.py:169
  133.7 11.3 %collective-permute-done.32.refs_1_ = bf16[8,56,512]{2,1,0:T(8,128)(2,1)S(1)} collective-permute-done((bf16[8,56,512]{2,1,0:T(8,128)(2,1)}, bf16[8,56,512]{2,1,0:T(8,128)(2,1)S(1)}, u32[]{:S(2)}, u32[]{:S(2)}) %collective-permute-start.32) | collective-permute-done | bytes 458784 | tf_op jit(solution)/shard_map/ppermute | solution.py:169
  147.2 2.3 %collective-permute-done.35.refs_3_ = bf16[4,96,512]{2,1,0:T(8,128)(2,1)S(1)} collective-permute-done((bf16[4,96,512]{2,1,0:T(8,128)(2,1)}, bf16[4,96,512]{2,1,0:T(8,128)(2,1)S(1)}, u32[]{:S(2)}, u32[]{:S(2)}) %collective-permute-start.35) | collective-permute-done | bytes 393248 | tf_op jit(solution)/shard_map/ppermute | solution.py:169
  151.8 4.1 %collective-permute-done.33 = bf16[320,512]{1,0:T(8,128)(2,1)S(1)} collective-permute-done((bf16[320,512]{1,0:T(8,128)(2,1)}, bf16[320,512]{1,0:T(8,128)(2,1)S(1)}, u32[]{:S(2)}, u32[]{:S(2)}) %collective-permute-start.33) | collective-permute-done | bytes 327712 | tf_op jit(solution)/shard_map/ppermute | solution.py:161
  155.9 7.4 %collective-permute-done.36.refs_1_ = bf16[2,224,512]{2,1,0:T(8,128)(2,1)S(1)} collective-permute-done((bf16[2,224,512]{2,1,0:T(8,128)(2,1)S(1)}, bf16[2,224,512]{2,1,0:T(8,128)(2,1)S(1)}, u32[]{:S(2)}, u32[]{:S(2)}) %collective-permute-start.36) | collective-permute-done | bytes 458784 | tf_op jit(solution)/shard_map/ppermute | solution.py:169
  163.5 2.4 %collective-permute-start.39 = (bf16[2,56,512]{2,1,0:T(8,128)(2,1)S(1)}, bf16[2,56,512]{2,1,0:T(8,128)(2,1)S(1)}, u32[]{:S(2)}, u32[]{:S(2)}) collective-permute-start(bf16[2,56,512]{2,1,0:T(8,128)(2,1)S(1)} %get-tuple-element.294), channel_id=1, source_target_pairs={{0,24},{1,9},{2,26},{3,11},{4,28},{5,13},{6,30},{7,15},{8,16},{9,1... | collective-permute-start | bytes 344072 | tf_op jit(solution)/shard_map/ppermute | solution.py:169
  167.0 4.3 %collective-permute-done.39.refs_1_ = bf16[2,56,512]{2,1,0:T(8,128)(2,1)S(1)} collective-permute-done((bf16[2,56,512]{2,1,0:T(8,128)(2,1)S(1)}, bf16[2,56,512]{2,1,0:T(8,128)(2,1)S(1)}, u32[]{:S(2)}, u32[]{:S(2)}) %collective-permute-start.39) | collective-permute-done | bytes 114720 | tf_op jit(solution)/shard_map/ppermute | solution.py:169
  171.4 2.7 %collective-permute-start.40 = (bf16[1,56,512]{2,1,0:T(8,128)(2,1)S(1)}, bf16[1,56,512]{2,1,0:T(8,128)(2,1)S(1)}, u32[]{:S(2)}, u32[]{:S(2)}) collective-permute-start(bf16[1,56,512]{2,1,0:T(8,128)(2,1)S(1)} %get-tuple-element.296), channel_id=1, source_target_pairs={{0,8},{1,25},{2,10},{3,27},{4,12},{5,29},{6,14},{7,31},{8,0},{9,17... | collective-permute-start | bytes 172040 | tf_op jit(solution)/shard_map/ppermute | solution.py:169
  (110 shorter events, 47.9 us)
Async XLA Ops:
  3.1 23.0 %collective-permute-start.7 = (bf16[584,512]{1,0:T(8,128)(2,1)}, bf16[584,512]{1,0:T(8,128)(2,1)S(1)}, u32[]{:S(2)}, u32[]{:S(2)}) collective-permute-start(bf16[584,512]{1,0:T(8,128)(2,1)} %get-tuple-element.171), channel_id=1, source_target_pairs={{0,2},{1,3},{2,0},{3,1},{4,6},{5,7},{6,4},{7,5},{8,10},{9,11},{10,... | collective-permute-start | bytes 1794056 | tf_op jit(solution)/shard_map/ppermute | solution.py:161
  6.0 27.5 %collective-permute-start.8 = (bf16[584,512]{1,0:T(8,128)(2,1)}, bf16[584,512]{1,0:T(8,128)(2,1)S(1)}, u32[]{:S(2)}, u32[]{:S(2)}) collective-permute-start(bf16[584,512]{1,0:T(8,128)(2,1)} %get-tuple-element.181.refs_5_.refs_6_), channel_id=1, source_target_pairs={{0,1},{1,0},{2,3},{3,2},{4,5},{5,4},{6,7},{7,6},{8,9},{9,8},{10,11... | collective-permute-start | bytes 1794056 | tf_op jit(solution)/shard_map/ppermute | solution.py:161
  21.9 11.6 %collective-permute-start.4 = (bf16[224,512]{1,0:T(8,128)(2,1)S(1)}, bf16[224,512]{1,0:T(8,128)(2,1)S(1)}, u32[]{:S(2)}, u32[]{:S(2)}) collective-permute-start(bf16[224,512]{1,0:T(8,128)(2,1)S(1)} %join.11.refs_0_), channel_id=1, source_target_pairs={{0,2},{1,5},{2,0},{3,7},{4,6},{5,1},{6,4},{7,3},{8,10},{9,13},{10,... | collective-permute-start | bytes 688136 | tf_op jit(solution)/shard_map/ppermute | solution.py:169
  23.2 10.3 %collective-permute-start.5 = (bf16[160,512]{1,0:T(8,128)(2,1)S(1)}, bf16[160,512]{1,0:T(8,128)(2,1)S(1)}, u32[]{:S(2)}, u32[]{:S(2)}) collective-permute-start(bf16[160,512]{1,0:T(8,128)(2,1)S(1)} %join.10.refs_0_), channel_id=1, source_target_pairs={{0,24},{1,9},{2,26},{3,11},{4,28},{5,13},{6,30},{7,15},{8,16},{9,1... | collective-permute-start | bytes 491528 | tf_op jit(solution)/shard_map/ppermute | solution.py:169
  26.1 20.9 %collective-permute-start.12 = (bf16[584,512]{1,0:T(8,128)(2,1)S(1)}, bf16[584,512]{1,0:T(8,128)(2,1)S(1)}, u32[]{:S(2)}, u32[]{:S(2)}) collective-permute-start(bf16[584,512]{1,0:T(8,128)(2,1)S(1)} %collective-permute-done.7.refs_6_.refs_7_), channel_id=1, source_target_pairs={{0,1},{1,0},{2,3},{3,2},{4,5},{5,4},{6,7},{7,6},{8,9},{9,8},{10,11... | collective-permute-start | bytes 1794056 | tf_op jit(solution)/shard_map/ppermute | solution.py:161
  33.6 11.6 %collective-permute-start.9 = (bf16[448,512]{1,0:T(8,128)(2,1)S(1)}, bf16[448,512]{1,0:T(8,128)(2,1)S(1)}, u32[]{:S(2)}, u32[]{:S(2)}) collective-permute-start(bf16[448,512]{1,0:T(8,128)(2,1)S(1)} %join.13.refs_1_), channel_id=1, source_target_pairs={{0,4},{1,3},{2,6},{3,1},{4,0},{5,7},{6,2},{7,5},{8,12},{9,11},{10,... | collective-permute-start | bytes 1376264 | tf_op jit(solution)/shard_map/ppermute | solution.py:169
  35.3 9.8 %collective-permute-start.10 = (bf16[320,512]{1,0:T(8,128)(2,1)S(1)}, bf16[320,512]{1,0:T(8,128)(2,1)S(1)}, u32[]{:S(2)}, u32[]{:S(2)}) collective-permute-start(bf16[320,512]{1,0:T(8,128)(2,1)S(1)} %join.14.refs_0_), channel_id=1, source_target_pairs={{0,2},{1,5},{2,0},{3,7},{4,6},{5,1},{6,4},{7,3},{8,10},{9,13},{10,... | collective-permute-start | bytes 983048 | tf_op jit(solution)/shard_map/ppermute | solution.py:169
  45.2 14.4 %collective-permute-start.11 = (bf16[512,512]{1,0:T(8,128)(2,1)S(1)}, bf16[512,512]{1,0:T(8,128)(2,1)S(1)}, u32[]{:S(2)}, u32[]{:S(2)}) collective-permute-start(bf16[512,512]{1,0:T(8,128)(2,1)S(1)} %join.15.refs_0_), channel_id=1, source_target_pairs={{0,2},{1,5},{2,0},{3,7},{4,6},{5,1},{6,4},{7,3},{8,10},{9,13},{10,... | collective-permute-start | bytes 1572872 | tf_op jit(solution)/shard_map/ppermute | solution.py:169
  47.6 12.4 %collective-permute-start.16 = (bf16[640,512]{1,0:T(8,128)(2,1)S(1)}, bf16[640,512]{1,0:T(8,128)(2,1)S(1)}, u32[]{:S(2)}, u32[]{:S(2)}) collective-permute-start(bf16[640,512]{1,0:T(8,128)(2,1)S(1)} %join.16.refs_1_), channel_id=1, source_target_pairs={{0,4},{1,3},{2,6},{3,1},{4,0},{5,7},{6,2},{7,5},{8,12},{9,11},{10,... | collective-permute-start | bytes 1966088 | tf_op jit(solution)/shard_map/ppermute | solution.py:169
  59.7 14.9 %collective-permute-start.15 = (bf16[1024,512]{1,0:T(8,128)(2,1)S(1)}, bf16[1024,512]{1,0:T(8,128)(2,1)S(1)}, u32[]{:S(2)}, u32[]{:S(2)}) collective-permute-start(bf16[1024,512]{1,0:T(8,128)(2,1)S(1)} %join.17.refs_1_), channel_id=1, source_target_pairs={{0,4},{1,3},{2,6},{3,1},{4,0},{5,7},{6,2},{7,5},{8,12},{9,11},{10,... | collective-permute-start | bytes 3145736 | tf_op jit(solution)/shard_map/ppermute | solution.py:169
  61.3 13.3 %collective-permute-start.19 = (bf16[1024,512]{1,0:T(8,128)(2,1)S(1)}, bf16[1024,512]{1,0:T(8,128)(2,1)S(1)}, u32[]{:S(2)}, u32[]{:S(2)}) collective-permute-start(bf16[1024,512]{1,0:T(8,128)(2,1)S(1)} %join.17.refs_1_), channel_id=1, source_target_pairs={{0,1},{1,0},{2,3},{3,2},{4,5},{5,4},{6,7},{7,6},{8,9},{9,8},{10,11... | collective-permute-start | bytes 3145736 | tf_op jit(solution)/shard_map/ppermute | solution.py:161
  89.6 10.9 %collective-permute-start.22 = (bf16[16,128,512]{2,1,0:T(8,128)(2,1)S(1)}, bf16[16,128,512]{2,1,0:T(8,128)(2,1)S(1)}, u32[]{:S(2)}, u32[]{:S(2)}) collective-permute-start(bf16[16,128,512]{2,1,0:T(8,128)(2,1)S(1)} %get-tuple-element.221), channel_id=1, source_target_pairs={{0,1},{1,0},{2,3},{3,2},{4,5},{5,4},{6,7},{7,6},{8,9},{9,8},{10,11... | collective-permute-start | bytes 6291464 | tf_op jit(solution)/shard_map/ppermute | solution.py:161
  89.8 10.7 %collective-permute-start.21 = (bf16[256,512]{1,0:T(8,128)(2,1)S(1)}, bf16[256,512]{1,0:T(8,128)(2,1)S(1)}, u32[]{:S(2)}, u32[]{:S(2)}) collective-permute-start(bf16[256,512]{1,0:T(8,128)(2,1)S(1)} %get-tuple-element.209), channel_id=1, source_target_pairs={{0,2},{1,3},{2,0},{3,1},{4,6},{5,7},{6,4},{7,5},{8,10},{9,11},{10,... | collective-permute-start | bytes 786440 | tf_op jit(solution)/shard_map/ppermute | solution.py:161
  103.5 20.0 %collective-permute-start.25 = (bf16[8,128,512]{2,1,0:T(8,128)(2,1)S(1)}, bf16[8,128,512]{2,1,0:T(8,128)(2,1)S(1)}, u32[]{:S(2)}, u32[]{:S(2)}) collective-permute-start(bf16[8,128,512]{2,1,0:T(8,128)(2,1)S(1)} %get-tuple-element.253), channel_id=1, source_target_pairs={{0,4},{1,3},{2,6},{3,1},{4,0},{5,7},{6,2},{7,5},{8,12},{9,11},{10,... | collective-permute-start | bytes 3145736 | tf_op jit(solution)/shard_map/ppermute | solution.py:169
  110.0 16.1 %collective-permute-start.26 = (bf16[8,96,512]{2,1,0:T(8,128)(2,1)S(1)}, bf16[8,96,512]{2,1,0:T(8,128)(2,1)S(1)}, u32[]{:S(2)}, u32[]{:S(2)}) collective-permute-start(bf16[8,96,512]{2,1,0:T(8,128)(2,1)S(1)} %get-tuple-element.258), channel_id=1, source_target_pairs={{0,2},{1,5},{2,0},{3,7},{4,6},{5,1},{6,4},{7,3},{8,10},{9,13},{10,... | collective-permute-start | bytes 2359304 | tf_op jit(solution)/shard_map/ppermute | solution.py:169
  110.3 16.0 %collective-permute-start.27 = (bf16[512,256]{1,0:T(8,128)(2,1)S(1)}, bf16[512,256]{1,0:T(8,128)(2,1)S(1)}, u32[]{:S(2)}, u32[]{:S(2)}) collective-permute-start(bf16[512,256]{1,0:T(8,128)(2,1)S(1)} %get-tuple-element.267), channel_id=1, source_target_pairs={{0,1},{1,0},{2,3},{3,2},{4,5},{5,4},{6,7},{7,6},{8,9},{9,8},{10,11... | collective-permute-start | bytes 786440 | tf_op jit(solution)/shard_map/ppermute | solution.py:161
  110.5 15.8 %collective-permute-start.28 = (bf16[512,256]{1,0:T(8,128)(2,1)S(1)}, bf16[512,256]{1,0:T(8,128)(2,1)S(1)}, u32[]{:S(2)}, u32[]{:S(2)}) collective-permute-start(bf16[512,256]{1,0:T(8,128)(2,1)S(1)} %get-tuple-element.268), channel_id=1, source_target_pairs={{0,1},{1,0},{2,3},{3,2},{4,5},{5,4},{6,7},{7,6},{8,9},{9,8},{10,11... | collective-permute-start | bytes 786440 | tf_op jit(solution)/shard_map/ppermute | solution.py:161
  131.5 13.5 %collective-permute-start.32 = (bf16[8,56,512]{2,1,0:T(8,128)(2,1)}, bf16[8,56,512]{2,1,0:T(8,128)(2,1)S(1)}, u32[]{:S(2)}, u32[]{:S(2)}) collective-permute-start(bf16[8,56,512]{2,1,0:T(8,128)(2,1)} %get-tuple-element.275), channel_id=1, source_target_pairs={{0,4},{1,3},{2,6},{3,1},{4,0},{5,7},{6,2},{7,5},{8,12},{9,11},{10,... | collective-permute-start | bytes 1376264 | tf_op jit(solution)/shard_map/ppermute | solution.py:169
  131.5 15.7 %collective-permute-start.34 = (bf16[4,128,512]{2,1,0:T(8,128)(2,1)}, bf16[4,128,512]{2,1,0:T(8,128)(2,1)S(1)}, u32[]{:S(2)}, u32[]{:S(2)}) collective-permute-start(bf16[4,128,512]{2,1,0:T(8,128)(2,1)} %get-tuple-element.278), channel_id=1, source_target_pairs={{0,2},{1,5},{2,0},{3,7},{4,6},{5,1},{6,4},{7,3},{8,10},{9,13},{10,... | collective-permute-start | bytes 1572872 | tf_op jit(solution)/shard_map/ppermute | solution.py:169
  131.8 17.7 %collective-permute-start.35 = (bf16[4,96,512]{2,1,0:T(8,128)(2,1)}, bf16[4,96,512]{2,1,0:T(8,128)(2,1)S(1)}, u32[]{:S(2)}, u32[]{:S(2)}) collective-permute-start(bf16[4,96,512]{2,1,0:T(8,128)(2,1)} %copy-done.4), channel_id=1, source_target_pairs={{0,4},{1,3},{2,6},{3,1},{4,0},{5,7},{6,2},{7,5},{8,12},{9,11},{10,... | collective-permute-start | bytes 1179656 | tf_op jit(solution)/shard_map/ppermute | solution.py:169
  145.0 10.9 %collective-permute-start.33 = (bf16[320,512]{1,0:T(8,128)(2,1)}, bf16[320,512]{1,0:T(8,128)(2,1)S(1)}, u32[]{:S(2)}, u32[]{:S(2)}) collective-permute-start(bf16[320,512]{1,0:T(8,128)(2,1)} %copy-done.5), channel_id=1, source_target_pairs={{0,2},{1,3},{2,0},{3,1},{4,6},{5,7},{6,4},{7,5},{8,10},{9,11},{10,... | collective-permute-start | bytes 983048 | tf_op jit(solution)/shard_map/ppermute | solution.py:161
  149.5 14.0 %collective-permute-start.38 = (bf16[4,56,512]{2,1,0:T(8,128)(2,1)S(1)}, bf16[4,56,512]{2,1,0:T(8,128)(2,1)S(1)}, u32[]{:S(2)}, u32[]{:S(2)}) collective-permute-start(bf16[4,56,512]{2,1,0:T(8,128)(2,1)S(1)} %get-tuple-element.290), channel_id=1, source_target_pairs={{0,2},{1,5},{2,0},{3,7},{4,6},{5,1},{6,4},{7,3},{8,10},{9,13},{10,... | collective-permute-start | bytes 688136 | tf_op jit(solution)/shard_map/ppermute | solution.py:169
  150.4 12.9 %collective-permute-start.36 = (bf16[2,224,512]{2,1,0:T(8,128)(2,1)S(1)}, bf16[2,224,512]{2,1,0:T(8,128)(2,1)S(1)}, u32[]{:S(2)}, u32[]{:S(2)}) collective-permute-start(bf16[2,224,512]{2,1,0:T(8,128)(2,1)S(1)} %get-tuple-element.287), channel_id=1, source_target_pairs={{0,24},{1,9},{2,26},{3,11},{4,28},{5,13},{6,30},{7,15},{8,16},{9,1... | collective-permute-start | bytes 1376264 | tf_op jit(solution)/shard_map/ppermute | solution.py:169
  166.0 10.3 %collective-permute-start.37 = (bf16[1,224,512]{2,1,0:T(8,128)(2,1)S(1)}, bf16[1,224,512]{2,1,0:T(8,128)(2,1)S(1)}, u32[]{:S(2)}, u32[]{:S(2)}) collective-permute-start(bf16[1,224,512]{2,1,0:T(8,128)(2,1)S(1)} %get-tuple-element.289), channel_id=1, source_target_pairs={{0,8},{1,25},{2,10},{3,27},{4,12},{5,29},{6,14},{7,31},{8,0},{9,17... | collective-permute-start | bytes 688136 | tf_op jit(solution)/shard_map/ppermute | solution.py:169
  (24 other events, 152.0 us)

commit v16 on v15

--- a/solution.py
+++ b/solution.py
@@ -1098,10 +1098,10 @@
         keep, send = combine([grads_last[0], swap(grads_last[1], 1, 32)], 2)
         last_step = [keep, turned_swap(send, 3)]
         in_send = after(in_send, last_step[1])
-        keep, send = combine(last_step, 2)
+        keep_joint, send = combine_joint(after([inner_step, cross_step], in_own), 2)
+        joint_step = [keep_joint, turned_swap(send, 1)]
+        keep, send = combine(after(last_step, keep_joint), 2)
         last_step = [keep, turned_swap(send, 2)]
-        keep_joint, send = combine_joint(after([inner_step, cross_step], in_own, keep), 2)
-        joint_step = [keep_joint, turned_swap(send, 1)]
         keep_joint, send = combine(joint_step, 2)
         joint_step = [keep_joint, turned_swap(send, 0)]
         keep, send = combine(after(last_step, keep_joint), 2)

time: 178 us -> 177 us (level)
    ppermute x22, waiting for transfers between devices: 61.3 us -> 65.7 us  [turned_swap(): lax.ppermute(array, AXES, [(i, i ^ orders[i % 2][step]) for i in range(32)])]
    ppermute x19, waiting for transfers between devices: 13.2 us -> 8.86 us  [swap(): return lax.ppermute(array, AXES, [(i, i ^ mask) for i in range(devices)])]
    ppermute x22, starting transfers between devices: 25.1 us -> 22.6 us  [turned_swap(): lax.ppermute(array, AXES, [(i, i ^ orders[i % 2][step]) for i in range(32)])]
  transfers between devices with their start and end apart: 41 -> 41, of which waited for: 22 -> 21; matrix products, arithmetic and copies ran while one was open for 2% -> 2% of each run, Pallas kernels for 23% -> 24%
where the time goes in v16:
time: 177 us
  waiting for transfers between devices  74.5 us (42%)
  Pallas kernels  60.6 us (34%)
  starting transfers between devices  34.1 us (19%)
  other arithmetic  3.95 us (2%)
  local copies, waits for them, and re-layouts  2.29 us (1%)
    ppermute x22, waiting for transfers between devices, turned_swap(): lax.ppermute(array, AXES, [(i, i ^ orders[i % 2][step]) for i in range(32)])  65.7 us
    pallas_call x12, Pallas kernels, call(): pl.pallas_call(kernel, out_shape=[jax.ShapeDtypeStruct(s, d) for s, d in...  57.7 us
    ppermute x22, starting transfers between devices, turned_swap(): lax.ppermute(array, AXES, [(i, i ^ orders[i % 2][step]) for i in range(32)])  22.6 us
    ppermute x19, starting transfers between devices, swap(): return lax.ppermute(array, AXES, [(i, i ^ mask) for i in range(devices)])  11.5 us
    ppermute x19, waiting for transfers between devices, swap(): return lax.ppermute(array, AXES, [(i, i ^ mask) for i in range(devices)])  8.86 us
  transfers between devices with their start and end apart: 41, of which 21 were waited for; matrix products, arithmetic and copies ran while one was open for 2% of the time, Pallas kernels for 24%

profile of v16, /device:TPU:0, one launch (start us, length us, event | category | flops | bytes accessed | tf_op | source)
XLA Modules:
  0.0 176.7 jit_solution(18125515404251846308)
XLA Ops:
  0.7 2.4 %tokens_packet.1 = (bf16[584,512]{1,0:T(8,128)(2,1)}, bf16[584,512]{1,0:T(8,128)(2,1)}) custom-call(s32[1]{0:T(128)} %bitcast.15.turn_ref, s32[2,256]{1,0:T(2,128)} %targets.1, s32[2,64]{1,0:T(2,128)} %sources.1, bf16[2,256,512]{2,1,0:T(8,128)(2,1)} %tokens_ref.1, bf16[2,64,512]{2,1,0:T(8,128)(2,1)} %memory_ref.1, bf16[2,256,512]{2,1,0:T(8,128)(2,1)} %cot_ref.1), custom_call_target="tpu_custom_call" | custom-call | flops 1 | bytes 1 | tf_op jit(solution)/shard_map/tokens_packet/pallas_call | solution.py:263
  3.1 3.0 %collective-permute-start.7 = (bf16[584,512]{1,0:T(8,128)(2,1)}, bf16[584,512]{1,0:T(8,128)(2,1)S(1)}, u32[]{:S(2)}, u32[]{:S(2)}) collective-permute-start(bf16[584,512]{1,0:T(8,128)(2,1)} %get-tuple-element.173), channel_id=1, source_target_pairs={{0,2},{1,3},{2,0},{3,1},{4,6},{5,7},{6,4},{7,5},{8,10},{9,11},{10,... | collective-permute-start | bytes 1794056 | tf_op jit(solution)/shard_map/ppermute | solution.py:161
  9.5 2.8 %collective-permute-done.refs_1_ = bf16[56,512]{1,0:T(8,128)(2,1)S(1)} collective-permute-done((bf16[56,512]{1,0:T(8,128)(2,1)}, bf16[56,512]{1,0:T(8,128)(2,1)S(1)}, u32[]{:S(2)}, u32[]{:S(2)}) %collective-permute-start) | collective-permute-done | bytes 57376 | tf_op jit(solution)/shard_map/ppermute | solution.py:169
  13.2 3.7 %collective-permute-start.2 = (bf16[112,512]{1,0:T(8,128)(2,1)S(1)}, bf16[112,512]{1,0:T(8,128)(2,1)S(1)}, u32[]{:S(2)}, u32[]{:S(2)}) collective-permute-start(bf16[112,512]{1,0:T(8,128)(2,1)S(1)} %join.9.refs_0_), channel_id=1, source_target_pairs={{0,24},{1,9},{2,26},{3,11},{4,28},{5,13},{6,30},{7,15},{8,16},{9,1... | collective-permute-start | bytes 344072 | tf_op jit(solution)/shard_map/ppermute | solution.py:169
  16.8 5.0 %collective-permute-done.1.refs_1_ = bf16[80,512]{1,0:T(8,128)(2,1)S(1)} collective-permute-done((bf16[80,512]{1,0:T(8,128)(2,1)}, bf16[80,512]{1,0:T(8,128)(2,1)S(1)}, u32[]{:S(2)}, u32[]{:S(2)}) %collective-permute-start.1) | collective-permute-done | bytes 81952 | tf_op jit(solution)/shard_map/ppermute | solution.py:169
  23.2 2.9 %collective-permute-start.5 = (bf16[160,512]{1,0:T(8,128)(2,1)S(1)}, bf16[160,512]{1,0:T(8,128)(2,1)S(1)}, u32[]{:S(2)}, u32[]{:S(2)}) collective-permute-start(bf16[160,512]{1,0:T(8,128)(2,1)S(1)} %join.10.refs_0_), channel_id=1, source_target_pairs={{0,24},{1,9},{2,26},{3,11},{4,28},{5,13},{6,30},{7,15},{8,16},{9,1... | collective-permute-start | bytes 491528 | tf_op jit(solution)/shard_map/ppermute | solution.py:169
  27.1 6.5 %collective-permute-done.3.refs_1_ = bf16[128,512]{1,0:T(8,128)(2,1)S(1)} collective-permute-done((bf16[128,512]{1,0:T(8,128)(2,1)}, bf16[128,512]{1,0:T(8,128)(2,1)S(1)}, u32[]{:S(2)}, u32[]{:S(2)}) %collective-permute-start.3) | collective-permute-done | bytes 131104 | tf_op jit(solution)/shard_map/ppermute | solution.py:169
  37.9 6.6 %collective-permute-done.6.refs_1_ = bf16[256,512]{1,0:T(8,128)(2,1)S(1)} collective-permute-done((bf16[256,512]{1,0:T(8,128)(2,1)S(1)}, bf16[256,512]{1,0:T(8,128)(2,1)S(1)}, u32[]{:S(2)}, u32[]{:S(2)}) %collective-permute-start.6) | collective-permute-done | bytes 262176 | tf_op jit(solution)/shard_map/ppermute | solution.py:169
  51.3 8.3 %self_attention.1 = (bf16[256,512]{1,0:T(8,128)(2,1)S(1)}, bf16[256,512]{1,0:T(8,128)(2,1)S(1)}, f32[4,1,512]{2,1,0:T(1,128)S(1)}, f32[4,1,512]{2,1,0:T(1,128)S(1)}) custom-call(s32[1]{0:T(128)} %bitcast.me_ref.refs_0_, bf16[256,512]{1,0:T(8,128)(2,1)S(1)} %get-tuple-element.193.refs_0_, bf16[256,512]{1,0:T(8,128)(2,1)S(1)} %get-tuple-element.194.refs_1_, ...), custom_call_target="tpu_custom_call" | custom-call | flops 1 | bytes 1 | tf_op jit(solution)/shard_map/self_attention/pallas_call | solution.py:263
  63.1 5.4 %cross_forward.1 = (f32[512,512]{1,0:T(8,128)S(1)}, f32[512,512]{1,0:T(8,128)S(1)}, bf16[512,512]{1,0:T(8,128)(2,1)S(1)}, bf16[256,512]{1,0:T(8,128)(2,1)S(1)}, ...) custom-call(s32[1]{0:T(128)} %bitcast.me_ref.refs_0_, ...), custom_call_target="tpu_custom_call" | custom-call | flops 1 | bytes 1 | tf_op jit(solution)/shard_map/cross_forward/pallas_call | solution.py:263
  68.4 6.1 %collective-permute-done.15.refs_2_ = bf16[1024,512]{1,0:T(8,128)(2,1)S(1)} collective-permute-done((bf16[1024,512]{1,0:T(8,128)(2,1)S(1)}, bf16[1024,512]{1,0:T(8,128)(2,1)S(1)}, u32[]{:S(2)}, u32[]{:S(2)}) %collective-permute-start.15) | collective-permute-done | bytes 1048608 | tf_op jit(solution)/shard_map/ppermute | solution.py:169
  74.5 2.7 %collective-permute-done.20.refs_4_ = bf16[1024,512]{1,0:T(8,128)(2,1)S(1)} collective-permute-done((bf16[1024,512]{1,0:T(8,128)(2,1)S(1)}, bf16[1024,512]{1,0:T(8,128)(2,1)S(1)}, u32[]{:S(2)}, u32[]{:S(2)}) %collective-permute-start.20) | collective-permute-done | bytes 1048608 | tf_op jit(solution)/shard_map/ppermute | solution.py:161
  77.2 12.4 %inner.1 = (f32[256,512]{1,0:T(8,128)S(1)}, bf16[256,512]{1,0:T(8,128)(2,1)S(1)}, f32[512,512]{1,0:T(8,128)S(1)}, f32[8,512]{1,0:T(8,128)S(1)}, bf16[16,128,512]...) custom-call(s32[1]{0:T(128)} %bitcast.me_ref.refs_0_, bf16[1024,512]{1,0:T(8,128)(2,1)S(1)} %join.17.refs_1_, ...), custom_call_target="tpu_custom_call" | custom-call | flops 1 | bytes 1 | tf_op jit(solution)/shard_map/inner/pallas_call | solution.py:263
  89.8 2.1 %collective-permute-start.21 = (bf16[256,512]{1,0:T(8,128)(2,1)S(1)}, bf16[256,512]{1,0:T(8,128)(2,1)S(1)}, u32[]{:S(2)}, u32[]{:S(2)}) collective-permute-start(bf16[256,512]{1,0:T(8,128)(2,1)S(1)} %get-tuple-element.211), channel_id=1, source_target_pairs={{0,2},{1,3},{2,0},{3,1},{4,6},{5,7},{6,4},{7,5},{8,10},{9,11},{10,... | collective-permute-start | bytes 786440 | tf_op jit(solution)/shard_map/ppermute | solution.py:161
  91.9 8.4 %cross_back.1 = (f32[512,512]{1,0:T(8,128)S(1)}, f32[128,512]{1,0:T(8,128)S(1)}, f32[128,512]{1,0:T(8,128)S(1)}, f32[16,512]{1,0:T(8,128)S(1)}, bf16[512,256]{1,...) custom-call(s32[1]{0:T(128)} %bitcast.me_ref.refs_0_, ...), custom_call_target="tpu_custom_call" | custom-call | flops 1 | bytes 1 | tf_op jit(solution)/shard_map/cross_back/pallas_call | solution.py:263
  103.5 6.1 %self_back_upper.1 = (bf16[512,256]{1,0:T(8,128)(2,1)S(1)}, f32[1024,256]{1,0:T(8,128)S(1)}, bf16[512,256]{1,0:T(8,128)(2,1)S(1)}, bf16[512,256]{1,0:T(8,128)(2,1)S(1)}) custom-call(s32[1]{0:T(128)} %bitcast.me_ref.refs_0_, bf16[512,256]{1,0:T(8,128)(2,1)S(1)} %get-tuple-element.238.refs_1_, bf16[1024,256]{1,0:T(8,128)(2,1)S(1)} %get-tuple-element.195.refs_2_, ...), custom_call_target="tpu_custom_call" | custom-call | flops 1 | bytes 1 | tf_op jit(solution)/shard_map/self_back_upper/pallas_call | solution.py:263
  110.8 7.1 %self_back_lower.1 = (f32[512,512]{1,0:T(8,128)S(1)}, f32[8,512]{1,0:T(8,128)S(1)}, bf16[512,512]{1,0:T(8,128)(2,1)S(1)}, f32[1024,256]{1,0:T(8,128)S(1)}, bf16[...) custom-call(s32[1]{0:T(128)} %bitcast.me_ref.refs_0_, bf16[448,512]{1,0:T(8,128)(2,1)S(1)} %join.13.refs_1_, ...), custom_call_target="tpu_custom_call" | custom-call | flops 1 | bytes 1 | tf_op jit(solution)/shard_map/self_back_lower/pallas_call | solution.py:263
  118.1 5.4 %collective-permute-done.25.refs_1_ = bf16[8,128,512]{2,1,0:T(8,128)(2,1)S(1)} collective-permute-done((bf16[8,128,512]{2,1,0:T(8,128)(2,1)S(1)}, bf16[8,128,512]{2,1,0:T(8,128)(2,1)S(1)}, u32[]{:S(2)}, u32[]{:S(2)}) %collective-permute-start.25) | collective-permute-done | bytes 1048608 | tf_op jit(solution)/shard_map/ppermute | solution.py:169
  123.7 2.4 %collective-permute-done.26.refs_1_ = bf16[8,96,512]{2,1,0:T(8,128)(2,1)S(1)} collective-permute-done((bf16[8,96,512]{2,1,0:T(8,128)(2,1)S(1)}, bf16[8,96,512]{2,1,0:T(8,128)(2,1)S(1)}, u32[]{:S(2)}, u32[]{:S(2)}) %collective-permute-start.26) | collective-permute-done | bytes 786464 | tf_op jit(solution)/shard_map/ppermute | solution.py:169
  133.5 7.1 %collective-permute-done.34.refs_1_ = bf16[4,128,512]{2,1,0:T(8,128)(2,1)S(1)} collective-permute-done((bf16[4,128,512]{2,1,0:T(8,128)(2,1)S(1)}, bf16[4,128,512]{2,1,0:T(8,128)(2,1)S(1)}, u32[]{:S(2)}, u32[]{:S(2)}) %collective-permute-start.34) | collective-permute-done | bytes 524320 | tf_op jit(solution)/shard_map/ppermute | solution.py:169
  140.6 5.3 %collective-permute-done.35.refs_3_ = bf16[4,96,512]{2,1,0:T(8,128)(2,1)S(1)} collective-permute-done((bf16[4,96,512]{2,1,0:T(8,128)(2,1)S(1)}, bf16[4,96,512]{2,1,0:T(8,128)(2,1)S(1)}, u32[]{:S(2)}, u32[]{:S(2)}) %collective-permute-start.35) | collective-permute-done | bytes 393248 | tf_op jit(solution)/shard_map/ppermute | solution.py:169
  151.7 7.3 %collective-permute-done.36.refs_1_ = bf16[2,224,512]{2,1,0:T(8,128)(2,1)S(1)} collective-permute-done((bf16[2,224,512]{2,1,0:T(8,128)(2,1)S(1)}, bf16[2,224,512]{2,1,0:T(8,128)(2,1)S(1)}, u32[]{:S(2)}, u32[]{:S(2)}) %collective-permute-start.36) | collective-permute-done | bytes 458784 | tf_op jit(solution)/shard_map/ppermute | solution.py:169
  163.3 7.2 %collective-permute-done.39.refs_1_ = bf16[2,56,512]{2,1,0:T(8,128)(2,1)S(1)} collective-permute-done((bf16[2,56,512]{2,1,0:T(8,128)(2,1)S(1)}, bf16[2,56,512]{2,1,0:T(8,128)(2,1)S(1)}, u32[]{:S(2)}, u32[]{:S(2)}) %collective-permute-start.39) | collective-permute-done | bytes 114720 | tf_op jit(solution)/shard_map/ppermute | solution.py:169
  171.4 3.4 %collective-permute-done.40.refs_3_ = bf16[1,56,512]{2,1,0:T(8,128)(2,1)S(1)} collective-permute-done((bf16[1,56,512]{2,1,0:T(8,128)(2,1)S(1)}, bf16[1,56,512]{2,1,0:T(8,128)(2,1)S(1)}, u32[]{:S(2)}, u32[]{:S(2)}) %collective-permute-start.40) | collective-permute-done | bytes 57376 | tf_op jit(solution)/shard_map/ppermute | solution.py:169
  (108 shorter events, 46.1 us)
Async XLA Ops:
  3.1 23.0 %collective-permute-start.7 = (bf16[584,512]{1,0:T(8,128)(2,1)}, bf16[584,512]{1,0:T(8,128)(2,1)S(1)}, u32[]{:S(2)}, u32[]{:S(2)}) collective-permute-start(bf16[584,512]{1,0:T(8,128)(2,1)} %get-tuple-element.173), channel_id=1, source_target_pairs={{0,2},{1,3},{2,0},{3,1},{4,6},{5,7},{6,4},{7,5},{8,10},{9,11},{10,... | collective-permute-start | bytes 1794056 | tf_op jit(solution)/shard_map/ppermute | solution.py:161
  6.0 27.5 %collective-permute-start.8 = (bf16[584,512]{1,0:T(8,128)(2,1)}, bf16[584,512]{1,0:T(8,128)(2,1)S(1)}, u32[]{:S(2)}, u32[]{:S(2)}) collective-permute-start(bf16[584,512]{1,0:T(8,128)(2,1)} %get-tuple-element.183.refs_5_.refs_6_), channel_id=1, source_target_pairs={{0,1},{1,0},{2,3},{3,2},{4,5},{5,4},{6,7},{7,6},{8,9},{9,8},{10,11... | collective-permute-start | bytes 1794056 | tf_op jit(solution)/shard_map/ppermute | solution.py:161
  21.9 11.6 %collective-permute-start.4 = (bf16[224,512]{1,0:T(8,128)(2,1)S(1)}, bf16[224,512]{1,0:T(8,128)(2,1)S(1)}, u32[]{:S(2)}, u32[]{:S(2)}) collective-permute-start(bf16[224,512]{1,0:T(8,128)(2,1)S(1)} %join.11.refs_0_), channel_id=1, source_target_pairs={{0,2},{1,5},{2,0},{3,7},{4,6},{5,1},{6,4},{7,3},{8,10},{9,13},{10,... | collective-permute-start | bytes 688136 | tf_op jit(solution)/shard_map/ppermute | solution.py:169
  23.2 10.3 %collective-permute-start.5 = (bf16[160,512]{1,0:T(8,128)(2,1)S(1)}, bf16[160,512]{1,0:T(8,128)(2,1)S(1)}, u32[]{:S(2)}, u32[]{:S(2)}) collective-permute-start(bf16[160,512]{1,0:T(8,128)(2,1)S(1)} %join.10.refs_0_), channel_id=1, source_target_pairs={{0,24},{1,9},{2,26},{3,11},{4,28},{5,13},{6,30},{7,15},{8,16},{9,1... | collective-permute-start | bytes 491528 | tf_op jit(solution)/shard_map/ppermute | solution.py:169
  26.1 20.9 %collective-permute-start.12 = (bf16[584,512]{1,0:T(8,128)(2,1)S(1)}, bf16[584,512]{1,0:T(8,128)(2,1)S(1)}, u32[]{:S(2)}, u32[]{:S(2)}) collective-permute-start(bf16[584,512]{1,0:T(8,128)(2,1)S(1)} %collective-permute-done.7.refs_6_.refs_7_), channel_id=1, source_target_pairs={{0,1},{1,0},{2,3},{3,2},{4,5},{5,4},{6,7},{7,6},{8,9},{9,8},{10,11... | collective-permute-start | bytes 1794056 | tf_op jit(solution)/shard_map/ppermute | solution.py:161
  33.6 11.6 %collective-permute-start.9 = (bf16[448,512]{1,0:T(8,128)(2,1)S(1)}, bf16[448,512]{1,0:T(8,128)(2,1)S(1)}, u32[]{:S(2)}, u32[]{:S(2)}) collective-permute-start(bf16[448,512]{1,0:T(8,128)(2,1)S(1)} %join.13.refs_1_), channel_id=1, source_target_pairs={{0,4},{1,3},{2,6},{3,1},{4,0},{5,7},{6,2},{7,5},{8,12},{9,11},{10,... | collective-permute-start | bytes 1376264 | tf_op jit(solution)/shard_map/ppermute | solution.py:169
  45.2 14.4 %collective-permute-start.11 = (bf16[512,512]{1,0:T(8,128)(2,1)S(1)}, bf16[512,512]{1,0:T(8,128)(2,1)S(1)}, u32[]{:S(2)}, u32[]{:S(2)}) collective-permute-start(bf16[512,512]{1,0:T(8,128)(2,1)S(1)} %join.15.refs_0_), channel_id=1, source_target_pairs={{0,2},{1,5},{2,0},{3,7},{4,6},{5,1},{6,4},{7,3},{8,10},{9,13},{10,... | collective-permute-start | bytes 1572872 | tf_op jit(solution)/shard_map/ppermute | solution.py:169
  47.6 12.4 %collective-permute-start.16 = (bf16[640,512]{1,0:T(8,128)(2,1)S(1)}, bf16[640,512]{1,0:T(8,128)(2,1)S(1)}, u32[]{:S(2)}, u32[]{:S(2)}) collective-permute-start(bf16[640,512]{1,0:T(8,128)(2,1)S(1)} %join.16.refs_1_), channel_id=1, source_target_pairs={{0,4},{1,3},{2,6},{3,1},{4,0},{5,7},{6,2},{7,5},{8,12},{9,11},{10,... | collective-permute-start | bytes 1966088 | tf_op jit(solution)/shard_map/ppermute | solution.py:169
  59.7 14.9 %collective-permute-start.15 = (bf16[1024,512]{1,0:T(8,128)(2,1)S(1)}, bf16[1024,512]{1,0:T(8,128)(2,1)S(1)}, u32[]{:S(2)}, u32[]{:S(2)}) collective-permute-start(bf16[1024,512]{1,0:T(8,128)(2,1)S(1)} %join.17.refs_1_), channel_id=1, source_target_pairs={{0,4},{1,3},{2,6},{3,1},{4,0},{5,7},{6,2},{7,5},{8,12},{9,11},{10,... | collective-permute-start | bytes 3145736 | tf_op jit(solution)/shard_map/ppermute | solution.py:169
  61.3 13.3 %collective-permute-start.19 = (bf16[1024,512]{1,0:T(8,128)(2,1)S(1)}, bf16[1024,512]{1,0:T(8,128)(2,1)S(1)}, u32[]{:S(2)}, u32[]{:S(2)}) collective-permute-start(bf16[1024,512]{1,0:T(8,128)(2,1)S(1)} %join.17.refs_1_), channel_id=1, source_target_pairs={{0,1},{1,0},{2,3},{3,2},{4,5},{5,4},{6,7},{7,6},{8,9},{9,8},{10,11... | collective-permute-start | bytes 3145736 | tf_op jit(solution)/shard_map/ppermute | solution.py:161
  89.6 10.9 %collective-permute-start.22 = (bf16[16,128,512]{2,1,0:T(8,128)(2,1)S(1)}, bf16[16,128,512]{2,1,0:T(8,128)(2,1)S(1)}, u32[]{:S(2)}, u32[]{:S(2)}) collective-permute-start(bf16[16,128,512]{2,1,0:T(8,128)(2,1)S(1)} %get-tuple-element.223), channel_id=1, source_target_pairs={{0,1},{1,0},{2,3},{3,2},{4,5},{5,4},{6,7},{7,6},{8,9},{9,8},{10,11... | collective-permute-start | bytes 6291464 | tf_op jit(solution)/shard_map/ppermute | solution.py:161
  89.8 10.7 %collective-permute-start.21 = (bf16[256,512]{1,0:T(8,128)(2,1)S(1)}, bf16[256,512]{1,0:T(8,128)(2,1)S(1)}, u32[]{:S(2)}, u32[]{:S(2)}) collective-permute-start(bf16[256,512]{1,0:T(8,128)(2,1)S(1)} %get-tuple-element.211), channel_id=1, source_target_pairs={{0,2},{1,3},{2,0},{3,1},{4,6},{5,7},{6,4},{7,5},{8,10},{9,11},{10,... | collective-permute-start | bytes 786440 | tf_op jit(solution)/shard_map/ppermute | solution.py:161
  103.5 20.0 %collective-permute-start.25 = (bf16[8,128,512]{2,1,0:T(8,128)(2,1)S(1)}, bf16[8,128,512]{2,1,0:T(8,128)(2,1)S(1)}, u32[]{:S(2)}, u32[]{:S(2)}) collective-permute-start(bf16[8,128,512]{2,1,0:T(8,128)(2,1)S(1)} %get-tuple-element.255), channel_id=1, source_target_pairs={{0,4},{1,3},{2,6},{3,1},{4,0},{5,7},{6,2},{7,5},{8,12},{9,11},{10,... | collective-permute-start | bytes 3145736 | tf_op jit(solution)/shard_map/ppermute | solution.py:169
  110.0 16.1 %collective-permute-start.26 = (bf16[8,96,512]{2,1,0:T(8,128)(2,1)S(1)}, bf16[8,96,512]{2,1,0:T(8,128)(2,1)S(1)}, u32[]{:S(2)}, u32[]{:S(2)}) collective-permute-start(bf16[8,96,512]{2,1,0:T(8,128)(2,1)S(1)} %get-tuple-element.260), channel_id=1, source_target_pairs={{0,2},{1,5},{2,0},{3,7},{4,6},{5,1},{6,4},{7,3},{8,10},{9,13},{10,... | collective-permute-start | bytes 2359304 | tf_op jit(solution)/shard_map/ppermute | solution.py:169
  110.3 16.0 %collective-permute-start.27 = (bf16[512,256]{1,0:T(8,128)(2,1)S(1)}, bf16[512,256]{1,0:T(8,128)(2,1)S(1)}, u32[]{:S(2)}, u32[]{:S(2)}) collective-permute-start(bf16[512,256]{1,0:T(8,128)(2,1)S(1)} %get-tuple-element.269), channel_id=1, source_target_pairs={{0,1},{1,0},{2,3},{3,2},{4,5},{5,4},{6,7},{7,6},{8,9},{9,8},{10,11... | collective-permute-start | bytes 786440 | tf_op jit(solution)/shard_map/ppermute | solution.py:161
  110.5 15.8 %collective-permute-start.28 = (bf16[512,256]{1,0:T(8,128)(2,1)S(1)}, bf16[512,256]{1,0:T(8,128)(2,1)S(1)}, u32[]{:S(2)}, u32[]{:S(2)}) collective-permute-start(bf16[512,256]{1,0:T(8,128)(2,1)S(1)} %get-tuple-element.270), channel_id=1, source_target_pairs={{0,1},{1,0},{2,3},{3,2},{4,5},{5,4},{6,7},{7,6},{8,9},{9,8},{10,11... | collective-permute-start | bytes 786440 | tf_op jit(solution)/shard_map/ppermute | solution.py:161
  128.4 12.1 %collective-permute-start.34 = (bf16[4,128,512]{2,1,0:T(8,128)(2,1)S(1)}, bf16[4,128,512]{2,1,0:T(8,128)(2,1)S(1)}, u32[]{:S(2)}, u32[]{:S(2)}) collective-permute-start(bf16[4,128,512]{2,1,0:T(8,128)(2,1)S(1)} %get-tuple-element.280), channel_id=1, source_target_pairs={{0,2},{1,5},{2,0},{3,7},{4,6},{5,1},{6,4},{7,3},{8,10},{9,13},{10,... | collective-permute-start | bytes 1572872 | tf_op jit(solution)/shard_map/ppermute | solution.py:169
  131.5 16.0 %collective-permute-start.32 = (bf16[8,56,512]{2,1,0:T(8,128)(2,1)}, bf16[8,56,512]{2,1,0:T(8,128)(2,1)S(1)}, u32[]{:S(2)}, u32[]{:S(2)}) collective-permute-start(bf16[8,56,512]{2,1,0:T(8,128)(2,1)} %get-tuple-element.277), channel_id=1, source_target_pairs={{0,4},{1,3},{2,6},{3,1},{4,0},{5,7},{6,2},{7,5},{8,12},{9,11},{10,... | collective-permute-start | bytes 1376264 | tf_op jit(solution)/shard_map/ppermute | solution.py:169
  131.5 14.4 %collective-permute-start.35 = (bf16[4,96,512]{2,1,0:T(8,128)(2,1)S(1)}, bf16[4,96,512]{2,1,0:T(8,128)(2,1)S(1)}, u32[]{:S(2)}, u32[]{:S(2)}) collective-permute-start(bf16[4,96,512]{2,1,0:T(8,128)(2,1)S(1)} %get-tuple-element.281), channel_id=1, source_target_pairs={{0,4},{1,3},{2,6},{3,1},{4,0},{5,7},{6,2},{7,5},{8,12},{9,11},{10,... | collective-permute-start | bytes 1179656 | tf_op jit(solution)/shard_map/ppermute | solution.py:169
  146.1 12.9 %collective-permute-start.36 = (bf16[2,224,512]{2,1,0:T(8,128)(2,1)S(1)}, bf16[2,224,512]{2,1,0:T(8,128)(2,1)S(1)}, u32[]{:S(2)}, u32[]{:S(2)}) collective-permute-start(bf16[2,224,512]{2,1,0:T(8,128)(2,1)S(1)} %get-tuple-element.287), channel_id=1, source_target_pairs={{0,24},{1,9},{2,26},{3,11},{4,28},{5,13},{6,30},{7,15},{8,16},{9,1... | collective-permute-start | bytes 1376264 | tf_op jit(solution)/shard_map/ppermute | solution.py:169
  147.6 12.9 %collective-permute-start.38 = (bf16[4,56,512]{2,1,0:T(8,128)(2,1)S(1)}, bf16[4,56,512]{2,1,0:T(8,128)(2,1)S(1)}, u32[]{:S(2)}, u32[]{:S(2)}) collective-permute-start(bf16[4,56,512]{2,1,0:T(8,128)(2,1)S(1)} %get-tuple-element.294), channel_id=1, source_target_pairs={{0,2},{1,5},{2,0},{3,7},{4,6},{5,1},{6,4},{7,3},{8,10},{9,13},{10,... | collective-permute-start | bytes 688136 | tf_op jit(solution)/shard_map/ppermute | solution.py:169
  147.9 14.3 %collective-permute-start.33 = (bf16[320,512]{1,0:T(8,128)(2,1)}, bf16[320,512]{1,0:T(8,128)(2,1)S(1)}, u32[]{:S(2)}, u32[]{:S(2)}) collective-permute-start(bf16[320,512]{1,0:T(8,128)(2,1)} %copy-done.4), channel_id=1, source_target_pairs={{0,2},{1,3},{2,0},{3,1},{4,6},{5,7},{6,4},{7,5},{8,10},{9,11},{10,... | collective-permute-start | bytes 983048 | tf_op jit(solution)/shard_map/ppermute | solution.py:161
  159.1 12.3 %collective-permute-start.37 = (bf16[1,224,512]{2,1,0:T(8,128)(2,1)S(1)}, bf16[1,224,512]{2,1,0:T(8,128)(2,1)S(1)}, u32[]{:S(2)}, u32[]{:S(2)}) collective-permute-start(bf16[1,224,512]{2,1,0:T(8,128)(2,1)S(1)} %get-tuple-element.289), channel_id=1, source_target_pairs={{0,8},{1,25},{2,10},{3,27},{4,12},{5,29},{6,14},{7,31},{8,0},{9,17... | collective-permute-start | bytes 688136 | tf_op jit(solution)/shard_map/ppermute | solution.py:169
  160.5 10.0 %collective-permute-start.39 = (bf16[2,56,512]{2,1,0:T(8,128)(2,1)S(1)}, bf16[2,56,512]{2,1,0:T(8,128)(2,1)S(1)}, u32[]{:S(2)}, u32[]{:S(2)}) collective-permute-start(bf16[2,56,512]{2,1,0:T(8,128)(2,1)S(1)} %get-tuple-element.298), channel_id=1, source_target_pairs={{0,24},{1,9},{2,26},{3,11},{4,28},{5,13},{6,30},{7,15},{8,16},{9,1... | collective-permute-start | bytes 344072 | tf_op jit(solution)/shard_map/ppermute | solution.py:169
  (23 other events, 162.7 us)

commit v17 on v16

--- a/solution.py
+++ b/solution.py
@@ -1043,7 +1043,6 @@
         make_inner(packed, rows, block, width, hidden, narrow, len(set_inner)), 18.0, "inner",
         *set_inner, second_sum, kept, came, vectors,
     )
-    out_came = swap(out_send, parts, devices)
     found = run(
         make_cross_back(packed, parts, share, memory_share, width, narrow, len(set_back)), 14.0,
         "cross_back", *set_back, back2_in, first_sum, second_sum, cross_query, memory_keys,
@@ -1055,7 +1054,7 @@
     grads_early = found[10 + parts - 1 :]
     query = list(query)
     if packed:
-        keep, send = combine(after([grads_inner[0], swap(grads_inner[1], 1, 32)], back1, out_came), 2)
+        keep, send = combine(after([grads_inner[0], swap(grads_inner[1], 1, 32)], back1), 2)
         inner_step = [keep, turned_swap(send, 3)]
         memory_key_own = after(memory_key_own, keep)
     memory_own, memory_send, *grads_cross = run(
@@ -1097,7 +1096,7 @@
     if packed:
         keep, send = combine([grads_last[0], swap(grads_last[1], 1, 32)], 2)
         last_step = [keep, turned_swap(send, 3)]
-        in_send = after(in_send, last_step[1])
+        in_send, out_send = after((in_send, out_send), last_step[1])
         keep_joint, send = combine_joint(after([inner_step, cross_step], in_own), 2)
         joint_step = [keep_joint, turned_swap(send, 1)]
         keep, send = combine(after(last_step, keep_joint), 2)
@@ -1154,7 +1153,7 @@
         came = came.astype(F32)
         return jnp.where(turn == 0, jnp.stack([mine, came]), jnp.stack([came, mine]))
 
-    output = regroup(out_own, out_came)
+    output = regroup(out_own, swap(out_send, parts, devices))
     in_came = swap(in_send, parts, devices)
     input_gradient = regroup(in_own, in_came[:block])
     memory_gradient = regroup(memory_own, in_came[block:])

time: 177 us -> 176 us (level)
  waiting for transfers between devices: 74.5 us -> 66 us
  starting transfers between devices: 34.1 us -> 41.2 us
    ppermute x22, starting transfers between devices: 22.6 us -> 31.6 us  [turned_swap(): lax.ppermute(array, AXES, [(i, i ^ orders[i % 2][step]) for i in range(32)])]
    ppermute x22, waiting for transfers between devices: 65.7 us -> 57.5 us  [turned_swap(): lax.ppermute(array, AXES, [(i, i ^ orders[i % 2][step]) for i in range(32)])]
    ppermute x19, starting transfers between devices: 11.5 us -> 9.63 us  [swap(): return lax.ppermute(array, AXES, [(i, i ^ mask) for i in range(devices)])]
  transfers between devices with their start and end apart: 41 -> 41, of which waited for: 21 -> 22; matrix products, arithmetic and copies ran while one was open for 2% -> 2% of each run, Pallas kernels for 24% -> 24%
where the time goes in v17:
time: 176 us
  waiting for transfers between devices  66 us (38%)
  Pallas kernels  61.3 us (35%)
  starting transfers between devices  41.2 us (23%)
  other arithmetic  3.94 us (2%)
  local copies, waits for them, and re-layouts  2.28 us (1%)
    pallas_call x12, Pallas kernels, call(): pl.pallas_call(kernel, out_shape=[jax.ShapeDtypeStruct(s, d) for s, d in...  58.4 us
    ppermute x22, waiting for transfers between devices, turned_swap(): lax.ppermute(array, AXES, [(i, i ^ orders[i % 2][step]) for i in range(32)])  57.5 us
    ppermute x22, starting transfers between devices, turned_swap(): lax.ppermute(array, AXES, [(i, i ^ orders[i % 2][step]) for i in range(32)])  31.6 us
    ppermute x19, starting transfers between devices, swap(): return lax.ppermute(array, AXES, [(i, i ^ mask) for i in range(devices)])  9.63 us
    ppermute x19, waiting for transfers between devices, swap(): return lax.ppermute(array, AXES, [(i, i ^ mask) for i in range(devices)])  8.45 us
  transfers between devices with their start and end apart: 41, of which 22 were waited for; matrix products, arithmetic and copies ran while one was open for 2% of the time, Pallas kernels for 24%

profile of v17, /device:TPU:0, one launch (start us, length us, event | category | flops | bytes accessed | tf_op | source)
XLA Modules:
  0.0 175.8 jit_solution(2688537724289444211)
XLA Ops:
  0.7 2.4 %tokens_packet.1 = (bf16[584,512]{1,0:T(8,128)(2,1)}, bf16[584,512]{1,0:T(8,128)(2,1)}) custom-call(s32[1]{0:T(128)} %bitcast.15.turn_ref, s32[2,256]{1,0:T(2,128)} %targets.1, s32[2,64]{1,0:T(2,128)} %sources.1, bf16[2,256,512]{2,1,0:T(8,128)(2,1)} %tokens_ref.1, bf16[2,64,512]{2,1,0:T(8,128)(2,1)} %memory_ref.1, bf16[2,256,512]{2,1,0:T(8,128)(2,1)} %cot_ref.1), custom_call_target="tpu_custom_call" | custom-call | flops 1 | bytes 1 | tf_op jit(solution)/shard_map/tokens_packet/pallas_call | solution.py:263
  3.1 3.0 %collective-permute-start.7 = (bf16[584,512]{1,0:T(8,128)(2,1)}, bf16[584,512]{1,0:T(8,128)(2,1)S(1)}, u32[]{:S(2)}, u32[]{:S(2)}) collective-permute-start(bf16[584,512]{1,0:T(8,128)(2,1)} %get-tuple-element.174), channel_id=1, source_target_pairs={{0,2},{1,3},{2,0},{3,1},{4,6},{5,7},{6,4},{7,5},{8,10},{9,11},{10,... | collective-permute-start | bytes 1794056 | tf_op jit(solution)/shard_map/ppermute | solution.py:161
  9.5 2.8 %collective-permute-done.refs_1_ = bf16[56,512]{1,0:T(8,128)(2,1)S(1)} collective-permute-done((bf16[56,512]{1,0:T(8,128)(2,1)}, bf16[56,512]{1,0:T(8,128)(2,1)S(1)}, u32[]{:S(2)}, u32[]{:S(2)}) %collective-permute-start) | collective-permute-done | bytes 57376 | tf_op jit(solution)/shard_map/ppermute | solution.py:169
  13.2 3.7 %collective-permute-start.2 = (bf16[112,512]{1,0:T(8,128)(2,1)S(1)}, bf16[112,512]{1,0:T(8,128)(2,1)S(1)}, u32[]{:S(2)}, u32[]{:S(2)}) collective-permute-start(bf16[112,512]{1,0:T(8,128)(2,1)S(1)} %join.9.refs_0_), channel_id=1, source_target_pairs={{0,24},{1,9},{2,26},{3,11},{4,28},{5,13},{6,30},{7,15},{8,16},{9,1... | collective-permute-start | bytes 344072 | tf_op jit(solution)/shard_map/ppermute | solution.py:169
  16.8 5.0 %collective-permute-done.1.refs_1_ = bf16[80,512]{1,0:T(8,128)(2,1)S(1)} collective-permute-done((bf16[80,512]{1,0:T(8,128)(2,1)}, bf16[80,512]{1,0:T(8,128)(2,1)S(1)}, u32[]{:S(2)}, u32[]{:S(2)}) %collective-permute-start.1) | collective-permute-done | bytes 81952 | tf_op jit(solution)/shard_map/ppermute | solution.py:169
  23.2 2.9 %collective-permute-start.5 = (bf16[160,512]{1,0:T(8,128)(2,1)S(1)}, bf16[160,512]{1,0:T(8,128)(2,1)S(1)}, u32[]{:S(2)}, u32[]{:S(2)}) collective-permute-start(bf16[160,512]{1,0:T(8,128)(2,1)S(1)} %join.10.refs_0_), channel_id=1, source_target_pairs={{0,24},{1,9},{2,26},{3,11},{4,28},{5,13},{6,30},{7,15},{8,16},{9,1... | collective-permute-start | bytes 491528 | tf_op jit(solution)/shard_map/ppermute | solution.py:169
  27.1 6.5 %collective-permute-done.3.refs_1_ = bf16[128,512]{1,0:T(8,128)(2,1)S(1)} collective-permute-done((bf16[128,512]{1,0:T(8,128)(2,1)}, bf16[128,512]{1,0:T(8,128)(2,1)S(1)}, u32[]{:S(2)}, u32[]{:S(2)}) %collective-permute-start.3) | collective-permute-done | bytes 131104 | tf_op jit(solution)/shard_map/ppermute | solution.py:169
  35.9 2.1 %collective-permute-start.6 = (bf16[256,512]{1,0:T(8,128)(2,1)S(1)}, bf16[256,512]{1,0:T(8,128)(2,1)S(1)}, u32[]{:S(2)}, u32[]{:S(2)}) collective-permute-start(bf16[256,512]{1,0:T(8,128)(2,1)S(1)} %join.12.refs_0_), channel_id=1, source_target_pairs={{0,24},{1,9},{2,26},{3,11},{4,28},{5,13},{6,30},{7,15},{8,16},{9,1... | collective-permute-start | bytes 786440 | tf_op jit(solution)/shard_map/ppermute | solution.py:169
  37.9 6.6 %collective-permute-done.6.refs_1_ = bf16[256,512]{1,0:T(8,128)(2,1)S(1)} collective-permute-done((bf16[256,512]{1,0:T(8,128)(2,1)S(1)}, bf16[256,512]{1,0:T(8,128)(2,1)S(1)}, u32[]{:S(2)}, u32[]{:S(2)}) %collective-permute-start.6) | collective-permute-done | bytes 262176 | tf_op jit(solution)/shard_map/ppermute | solution.py:169
  51.3 8.3 %self_attention.1 = (bf16[256,512]{1,0:T(8,128)(2,1)S(1)}, bf16[256,512]{1,0:T(8,128)(2,1)S(1)}, f32[4,1,512]{2,1,0:T(1,128)S(1)}, f32[4,1,512]{2,1,0:T(1,128)S(1)}) custom-call(s32[1]{0:T(128)} %bitcast.me_ref.refs_0_, bf16[256,512]{1,0:T(8,128)(2,1)S(1)} %get-tuple-element.194.refs_0_, bf16[256,512]{1,0:T(8,128)(2,1)S(1)} %get-tuple-element.195.refs_1_, ...), custom_call_target="tpu_custom_call" | custom-call | flops 1 | bytes 1 | tf_op jit(solution)/shard_map/self_attention/pallas_call | solution.py:263
  63.1 5.4 %cross_forward.1 = (f32[512,512]{1,0:T(8,128)S(1)}, f32[512,512]{1,0:T(8,128)S(1)}, bf16[512,512]{1,0:T(8,128)(2,1)S(1)}, bf16[256,512]{1,0:T(8,128)(2,1)S(1)}, ...) custom-call(s32[1]{0:T(128)} %bitcast.me_ref.refs_0_, ...), custom_call_target="tpu_custom_call" | custom-call | flops 1 | bytes 1 | tf_op jit(solution)/shard_map/cross_forward/pallas_call | solution.py:263
  68.4 6.1 %collective-permute-done.15.refs_2_ = bf16[1024,512]{1,0:T(8,128)(2,1)S(1)} collective-permute-done((bf16[1024,512]{1,0:T(8,128)(2,1)S(1)}, bf16[1024,512]{1,0:T(8,128)(2,1)S(1)}, u32[]{:S(2)}, u32[]{:S(2)}) %collective-permute-start.15) | collective-permute-done | bytes 1048608 | tf_op jit(solution)/shard_map/ppermute | solution.py:169
  74.5 2.7 %collective-permute-done.20.refs_4_ = bf16[1024,512]{1,0:T(8,128)(2,1)S(1)} collective-permute-done((bf16[1024,512]{1,0:T(8,128)(2,1)S(1)}, bf16[1024,512]{1,0:T(8,128)(2,1)S(1)}, u32[]{:S(2)}, u32[]{:S(2)}) %collective-permute-start.20) | collective-permute-done | bytes 1048608 | tf_op jit(solution)/shard_map/ppermute | solution.py:161
  77.2 13.1 %inner.1 = (f32[256,512]{1,0:T(8,128)S(1)}, bf16[256,512]{1,0:T(8,128)(2,1)}, f32[512,512]{1,0:T(8,128)S(1)}, f32[8,512]{1,0:T(8,128)S(1)}, bf16[16,128,512]{2,1...) custom-call(s32[1]{0:T(128)} %bitcast.me_ref.refs_0_, bf16[1024,512]{1,0:T(8,128)(2,1)S(1)} %join.17.refs_1_, ...), custom_call_target="tpu_custom_call" | custom-call | flops 1 | bytes 1 | tf_op jit(solution)/shard_map/inner/pallas_call | solution.py:263
  90.4 8.4 %cross_back.1 = (f32[512,512]{1,0:T(8,128)S(1)}, f32[128,512]{1,0:T(8,128)S(1)}, f32[128,512]{1,0:T(8,128)S(1)}, f32[16,512]{1,0:T(8,128)S(1)}, bf16[512,256]{1,...) custom-call(s32[1]{0:T(128)} %bitcast.me_ref.refs_0_, ...), custom_call_target="tpu_custom_call" | custom-call | flops 1 | bytes 1 | tf_op jit(solution)/shard_map/cross_back/pallas_call | solution.py:263
  102.5 6.1 %self_back_upper.1 = (bf16[512,256]{1,0:T(8,128)(2,1)S(1)}, f32[1024,256]{1,0:T(8,128)S(1)}, bf16[512,256]{1,0:T(8,128)(2,1)S(1)}, bf16[512,256]{1,0:T(8,128)(2,1)S(1)}) custom-call(s32[1]{0:T(128)} %bitcast.me_ref.refs_0_, bf16[512,256]{1,0:T(8,128)(2,1)S(1)} %get-tuple-element.238.refs_1_, bf16[1024,256]{1,0:T(8,128)(2,1)S(1)} %get-tuple-element.196.refs_2_, ...), custom_call_target="tpu_custom_call" | custom-call | flops 1 | bytes 1 | tf_op jit(solution)/shard_map/self_back_upper/pallas_call | solution.py:263
  111.4 7.1 %self_back_lower.1 = (f32[512,512]{1,0:T(8,128)S(1)}, f32[8,512]{1,0:T(8,128)S(1)}, bf16[512,512]{1,0:T(8,128)(2,1)S(1)}, f32[1024,256]{1,0:T(8,128)S(1)}, bf16[...) custom-call(s32[1]{0:T(128)} %bitcast.me_ref.refs_0_, bf16[448,512]{1,0:T(8,128)(2,1)S(1)} %join.13.refs_1_, ...), custom_call_target="tpu_custom_call" | custom-call | flops 1 | bytes 1 | tf_op jit(solution)/shard_map/self_back_lower/pallas_call | solution.py:263
  120.9 4.1 %collective-permute-done.25.refs_1_ = bf16[8,96,512]{2,1,0:T(8,128)(2,1)S(1)} collective-permute-done((bf16[8,96,512]{2,1,0:T(8,128)(2,1)S(1)}, bf16[8,96,512]{2,1,0:T(8,128)(2,1)S(1)}, u32[]{:S(2)}, u32[]{:S(2)}) %collective-permute-start.25) | collective-permute-done | bytes 786464 | tf_op jit(solution)/shard_map/ppermute | solution.py:169
  127.2 2.1 %collective-permute-start.34 = (bf16[4,128,512]{2,1,0:T(8,128)(2,1)S(1)}, bf16[4,128,512]{2,1,0:T(8,128)(2,1)S(1)}, u32[]{:S(2)}, u32[]{:S(2)}) collective-permute-start(bf16[4,128,512]{2,1,0:T(8,128)(2,1)S(1)} %get-tuple-element.282), channel_id=1, source_target_pairs={{0,2},{1,5},{2,0},{3,7},{4,6},{5,1},{6,4},{7,3},{8,10},{9,13},{10,... | collective-permute-start | bytes 1572872 | tf_op jit(solution)/shard_map/ppermute | solution.py:169
  131.6 10.4 %collective-permute-done.34.refs_1_ = bf16[4,128,512]{2,1,0:T(8,128)(2,1)S(1)} collective-permute-done((bf16[4,128,512]{2,1,0:T(8,128)(2,1)S(1)}, bf16[4,128,512]{2,1,0:T(8,128)(2,1)S(1)}, u32[]{:S(2)}, u32[]{:S(2)}) %collective-permute-start.34) | collective-permute-done | bytes 524320 | tf_op jit(solution)/shard_map/ppermute | solution.py:169
  147.5 7.9 %collective-permute-done.36.refs_1_ = bf16[2,224,512]{2,1,0:T(8,128)(2,1)S(1)} collective-permute-done((bf16[2,224,512]{2,1,0:T(8,128)(2,1)S(1)}, bf16[2,224,512]{2,1,0:T(8,128)(2,1)S(1)}, u32[]{:S(2)}, u32[]{:S(2)}) %collective-permute-start.36) | collective-permute-done | bytes 458784 | tf_op jit(solution)/shard_map/ppermute | solution.py:169
  155.5 5.2 %collective-permute-start.37 = (bf16[1,224,512]{2,1,0:T(8,128)(2,1)S(1)}, bf16[1,224,512]{2,1,0:T(8,128)(2,1)S(1)}, u32[]{:S(2)}, u32[]{:S(2)}) collective-permute-start(bf16[1,224,512]{2,1,0:T(8,128)(2,1)S(1)} %get-tuple-element.291), channel_id=1, source_target_pairs={{0,8},{1,25},{2,10},{3,27},{4,12},{5,29},{6,14},{7,31},{8,0},{9,17... | collective-permute-start | bytes 688136 | tf_op jit(solution)/shard_map/ppermute | solution.py:169
  160.8 3.2 %collective-permute-start.39 = (bf16[2,56,512]{2,1,0:T(8,128)(2,1)S(1)}, bf16[2,56,512]{2,1,0:T(8,128)(2,1)S(1)}, u32[]{:S(2)}, u32[]{:S(2)}) collective-permute-start(bf16[2,56,512]{2,1,0:T(8,128)(2,1)S(1)} %get-tuple-element.300), channel_id=1, source_target_pairs={{0,24},{1,9},{2,26},{3,11},{4,28},{5,13},{6,30},{7,15},{8,16},{9,1... | collective-permute-start | bytes 344072 | tf_op jit(solution)/shard_map/ppermute | solution.py:169
  170.5 3.4 %collective-permute-done.40.refs_3_ = bf16[1,56,512]{2,1,0:T(8,128)(2,1)S(1)} collective-permute-done((bf16[1,56,512]{2,1,0:T(8,128)(2,1)S(1)}, bf16[1,56,512]{2,1,0:T(8,128)(2,1)S(1)}, u32[]{:S(2)}, u32[]{:S(2)}) %collective-permute-start.40) | collective-permute-done | bytes 57376 | tf_op jit(solution)/shard_map/ppermute | solution.py:169
  (104 shorter events, 46.3 us)
Async XLA Ops:
  3.1 23.0 %collective-permute-start.7 = (bf16[584,512]{1,0:T(8,128)(2,1)}, bf16[584,512]{1,0:T(8,128)(2,1)S(1)}, u32[]{:S(2)}, u32[]{:S(2)}) collective-permute-start(bf16[584,512]{1,0:T(8,128)(2,1)} %get-tuple-element.174), channel_id=1, source_target_pairs={{0,2},{1,3},{2,0},{3,1},{4,6},{5,7},{6,4},{7,5},{8,10},{9,11},{10,... | collective-permute-start | bytes 1794056 | tf_op jit(solution)/shard_map/ppermute | solution.py:161
  6.0 27.5 %collective-permute-start.8 = (bf16[584,512]{1,0:T(8,128)(2,1)}, bf16[584,512]{1,0:T(8,128)(2,1)S(1)}, u32[]{:S(2)}, u32[]{:S(2)}) collective-permute-start(bf16[584,512]{1,0:T(8,128)(2,1)} %get-tuple-element.184.refs_5_.refs_6_), channel_id=1, source_target_pairs={{0,1},{1,0},{2,3},{3,2},{4,5},{5,4},{6,7},{7,6},{8,9},{9,8},{10,11... | collective-permute-start | bytes 1794056 | tf_op jit(solution)/shard_map/ppermute | solution.py:161
  21.9 11.6 %collective-permute-start.4 = (bf16[224,512]{1,0:T(8,128)(2,1)S(1)}, bf16[224,512]{1,0:T(8,128)(2,1)S(1)}, u32[]{:S(2)}, u32[]{:S(2)}) collective-permute-start(bf16[224,512]{1,0:T(8,128)(2,1)S(1)} %join.11.refs_0_), channel_id=1, source_target_pairs={{0,2},{1,5},{2,0},{3,7},{4,6},{5,1},{6,4},{7,3},{8,10},{9,13},{10,... | collective-permute-start | bytes 688136 | tf_op jit(solution)/shard_map/ppermute | solution.py:169
  23.2 10.3 %collective-permute-start.5 = (bf16[160,512]{1,0:T(8,128)(2,1)S(1)}, bf16[160,512]{1,0:T(8,128)(2,1)S(1)}, u32[]{:S(2)}, u32[]{:S(2)}) collective-permute-start(bf16[160,512]{1,0:T(8,128)(2,1)S(1)} %join.10.refs_0_), channel_id=1, source_target_pairs={{0,24},{1,9},{2,26},{3,11},{4,28},{5,13},{6,30},{7,15},{8,16},{9,1... | collective-permute-start | bytes 491528 | tf_op jit(solution)/shard_map/ppermute | solution.py:169
  26.1 20.9 %collective-permute-start.12 = (bf16[584,512]{1,0:T(8,128)(2,1)S(1)}, bf16[584,512]{1,0:T(8,128)(2,1)S(1)}, u32[]{:S(2)}, u32[]{:S(2)}) collective-permute-start(bf16[584,512]{1,0:T(8,128)(2,1)S(1)} %collective-permute-done.7.refs_6_.refs_7_), channel_id=1, source_target_pairs={{0,1},{1,0},{2,3},{3,2},{4,5},{5,4},{6,7},{7,6},{8,9},{9,8},{10,11... | collective-permute-start | bytes 1794056 | tf_op jit(solution)/shard_map/ppermute | solution.py:161
  33.6 11.6 %collective-permute-start.9 = (bf16[448,512]{1,0:T(8,128)(2,1)S(1)}, bf16[448,512]{1,0:T(8,128)(2,1)S(1)}, u32[]{:S(2)}, u32[]{:S(2)}) collective-permute-start(bf16[448,512]{1,0:T(8,128)(2,1)S(1)} %join.13.refs_1_), channel_id=1, source_target_pairs={{0,4},{1,3},{2,6},{3,1},{4,0},{5,7},{6,2},{7,5},{8,12},{9,11},{10,... | collective-permute-start | bytes 1376264 | tf_op jit(solution)/shard_map/ppermute | solution.py:169
  35.3 9.8 %collective-permute-start.10 = (bf16[320,512]{1,0:T(8,128)(2,1)S(1)}, bf16[320,512]{1,0:T(8,128)(2,1)S(1)}, u32[]{:S(2)}, u32[]{:S(2)}) collective-permute-start(bf16[320,512]{1,0:T(8,128)(2,1)S(1)} %join.14.refs_0_), channel_id=1, source_target_pairs={{0,2},{1,5},{2,0},{3,7},{4,6},{5,1},{6,4},{7,3},{8,10},{9,13},{10,... | collective-permute-start | bytes 983048 | tf_op jit(solution)/shard_map/ppermute | solution.py:169
  45.2 14.4 %collective-permute-start.11 = (bf16[512,512]{1,0:T(8,128)(2,1)S(1)}, bf16[512,512]{1,0:T(8,128)(2,1)S(1)}, u32[]{:S(2)}, u32[]{:S(2)}) collective-permute-start(bf16[512,512]{1,0:T(8,128)(2,1)S(1)} %join.15.refs_0_), channel_id=1, source_target_pairs={{0,2},{1,5},{2,0},{3,7},{4,6},{5,1},{6,4},{7,3},{8,10},{9,13},{10,... | collective-permute-start | bytes 1572872 | tf_op jit(solution)/shard_map/ppermute | solution.py:169
  47.6 12.4 %collective-permute-start.16 = (bf16[640,512]{1,0:T(8,128)(2,1)S(1)}, bf16[640,512]{1,0:T(8,128)(2,1)S(1)}, u32[]{:S(2)}, u32[]{:S(2)}) collective-permute-start(bf16[640,512]{1,0:T(8,128)(2,1)S(1)} %join.16.refs_1_), channel_id=1, source_target_pairs={{0,4},{1,3},{2,6},{3,1},{4,0},{5,7},{6,2},{7,5},{8,12},{9,11},{10,... | collective-permute-start | bytes 1966088 | tf_op jit(solution)/shard_map/ppermute | solution.py:169
  59.7 14.9 %collective-permute-start.15 = (bf16[1024,512]{1,0:T(8,128)(2,1)S(1)}, bf16[1024,512]{1,0:T(8,128)(2,1)S(1)}, u32[]{:S(2)}, u32[]{:S(2)}) collective-permute-start(bf16[1024,512]{1,0:T(8,128)(2,1)S(1)} %join.17.refs_1_), channel_id=1, source_target_pairs={{0,4},{1,3},{2,6},{3,1},{4,0},{5,7},{6,2},{7,5},{8,12},{9,11},{10,... | collective-permute-start | bytes 3145736 | tf_op jit(solution)/shard_map/ppermute | solution.py:169
  61.3 13.3 %collective-permute-start.19 = (bf16[1024,512]{1,0:T(8,128)(2,1)S(1)}, bf16[1024,512]{1,0:T(8,128)(2,1)S(1)}, u32[]{:S(2)}, u32[]{:S(2)}) collective-permute-start(bf16[1024,512]{1,0:T(8,128)(2,1)S(1)} %join.17.refs_1_), channel_id=1, source_target_pairs={{0,1},{1,0},{2,3},{3,2},{4,5},{5,4},{6,7},{7,6},{8,9},{9,8},{10,11... | collective-permute-start | bytes 3145736 | tf_op jit(solution)/shard_map/ppermute | solution.py:161
  90.3 9.0 %collective-permute-start.21 = (bf16[16,128,512]{2,1,0:T(8,128)(2,1)S(1)}, bf16[16,128,512]{2,1,0:T(8,128)(2,1)S(1)}, u32[]{:S(2)}, u32[]{:S(2)}) collective-permute-start(bf16[16,128,512]{2,1,0:T(8,128)(2,1)S(1)} %get-tuple-element.223), channel_id=1, source_target_pairs={{0,1},{1,0},{2,3},{3,2},{4,5},{5,4},{6,7},{7,6},{8,9},{9,8},{10,11... | collective-permute-start | bytes 6291464 | tf_op jit(solution)/shard_map/ppermute | solution.py:161
  102.2 18.4 %collective-permute-start.24 = (bf16[8,128,512]{2,1,0:T(8,128)(2,1)S(1)}, bf16[8,128,512]{2,1,0:T(8,128)(2,1)S(1)}, u32[]{:S(2)}, u32[]{:S(2)}) collective-permute-start(bf16[8,128,512]{2,1,0:T(8,128)(2,1)S(1)} %get-tuple-element.255), channel_id=1, source_target_pairs={{0,4},{1,3},{2,6},{3,1},{4,0},{5,7},{6,2},{7,5},{8,12},{9,11},{10,... | collective-permute-start | bytes 3145736 | tf_op jit(solution)/shard_map/ppermute | solution.py:169
  109.0 16.0 %collective-permute-start.25 = (bf16[8,96,512]{2,1,0:T(8,128)(2,1)S(1)}, bf16[8,96,512]{2,1,0:T(8,128)(2,1)S(1)}, u32[]{:S(2)}, u32[]{:S(2)}) collective-permute-start(bf16[8,96,512]{2,1,0:T(8,128)(2,1)S(1)} %get-tuple-element.260), channel_id=1, source_target_pairs={{0,2},{1,5},{2,0},{3,7},{4,6},{5,1},{6,4},{7,3},{8,10},{9,13},{10,... | collective-permute-start | bytes 2359304 | tf_op jit(solution)/shard_map/ppermute | solution.py:169
  110.9 14.3 %collective-permute-start.26 = (bf16[512,256]{1,0:T(8,128)(2,1)S(1)}, bf16[512,256]{1,0:T(8,128)(2,1)S(1)}, u32[]{:S(2)}, u32[]{:S(2)}) collective-permute-start(bf16[512,256]{1,0:T(8,128)(2,1)S(1)} %get-tuple-element.269), channel_id=1, source_target_pairs={{0,1},{1,0},{2,3},{3,2},{4,5},{5,4},{6,7},{7,6},{8,9},{9,8},{10,11... | collective-permute-start | bytes 786440 | tf_op jit(solution)/shard_map/ppermute | solution.py:161
  110.9 14.3 %collective-permute-start.27 = (bf16[512,256]{1,0:T(8,128)(2,1)S(1)}, bf16[512,256]{1,0:T(8,128)(2,1)S(1)}, u32[]{:S(2)}, u32[]{:S(2)}) collective-permute-start(bf16[512,256]{1,0:T(8,128)(2,1)S(1)} %get-tuple-element.270), channel_id=1, source_target_pairs={{0,1},{1,0},{2,3},{3,2},{4,5},{5,4},{6,7},{7,6},{8,9},{9,8},{10,11... | collective-permute-start | bytes 786440 | tf_op jit(solution)/shard_map/ppermute | solution.py:161
  127.2 14.8 %collective-permute-start.34 = (bf16[4,128,512]{2,1,0:T(8,128)(2,1)S(1)}, bf16[4,128,512]{2,1,0:T(8,128)(2,1)S(1)}, u32[]{:S(2)}, u32[]{:S(2)}) collective-permute-start(bf16[4,128,512]{2,1,0:T(8,128)(2,1)S(1)} %get-tuple-element.282), channel_id=1, source_target_pairs={{0,2},{1,5},{2,0},{3,7},{4,6},{5,1},{6,4},{7,3},{8,10},{9,13},{10,... | collective-permute-start | bytes 1572872 | tf_op jit(solution)/shard_map/ppermute | solution.py:169
  129.3 12.7 %collective-permute-start.35 = (bf16[4,96,512]{2,1,0:T(8,128)(2,1)S(1)}, bf16[4,96,512]{2,1,0:T(8,128)(2,1)S(1)}, u32[]{:S(2)}, u32[]{:S(2)}) collective-permute-start(bf16[4,96,512]{2,1,0:T(8,128)(2,1)S(1)} %get-tuple-element.283), channel_id=1, source_target_pairs={{0,4},{1,3},{2,6},{3,1},{4,0},{5,7},{6,2},{7,5},{8,12},{9,11},{10,... | collective-permute-start | bytes 1179656 | tf_op jit(solution)/shard_map/ppermute | solution.py:169
  129.6 15.2 %collective-permute-start.31 = (bf16[8,56,512]{2,1,0:T(8,128)(2,1)S(1)}, bf16[8,56,512]{2,1,0:T(8,128)(2,1)S(1)}, u32[]{:S(2)}, u32[]{:S(2)}) collective-permute-start(bf16[8,56,512]{2,1,0:T(8,128)(2,1)S(1)} %get-tuple-element.277), channel_id=1, source_target_pairs={{0,4},{1,3},{2,6},{3,1},{4,0},{5,7},{6,2},{7,5},{8,12},{9,11},{10,... | collective-permute-start | bytes 1376264 | tf_op jit(solution)/shard_map/ppermute | solution.py:169
  142.2 13.2 %collective-permute-start.36 = (bf16[2,224,512]{2,1,0:T(8,128)(2,1)S(1)}, bf16[2,224,512]{2,1,0:T(8,128)(2,1)S(1)}, u32[]{:S(2)}, u32[]{:S(2)}) collective-permute-start(bf16[2,224,512]{2,1,0:T(8,128)(2,1)S(1)} %get-tuple-element.289), channel_id=1, source_target_pairs={{0,24},{1,9},{2,26},{3,11},{4,28},{5,13},{6,30},{7,15},{8,16},{9,1... | collective-permute-start | bytes 1376264 | tf_op jit(solution)/shard_map/ppermute | solution.py:169
  144.8 19.2 %collective-permute-start.32 = (bf16[256,512]{1,0:T(8,128)(2,1)}, bf16[256,512]{1,0:T(8,128)(2,1)}, u32[]{:S(2)}, u32[]{:S(2)}) collective-permute-start(bf16[256,512]{1,0:T(8,128)(2,1)} %get-tuple-element.278), channel_id=1, source_target_pairs={{0,2},{1,3},{2,0},{3,1},{4,6},{5,7},{6,4},{7,5},{8,10},{9,11},{10,... | collective-permute-start | bytes 786440 | tf_op jit(solution)/shard_map/ppermute | solution.py:161
  147.5 13.2 %collective-permute-start.38 = (bf16[4,56,512]{2,1,0:T(8,128)(2,1)}, bf16[4,56,512]{2,1,0:T(8,128)(2,1)S(1)}, u32[]{:S(2)}, u32[]{:S(2)}) collective-permute-start(bf16[4,56,512]{2,1,0:T(8,128)(2,1)} %get-tuple-element.296), channel_id=1, source_target_pairs={{0,2},{1,5},{2,0},{3,7},{4,6},{5,1},{6,4},{7,3},{8,10},{9,13},{10,... | collective-permute-start | bytes 688136 | tf_op jit(solution)/shard_map/ppermute | solution.py:169
  155.5 15.0 %collective-permute-start.37 = (bf16[1,224,512]{2,1,0:T(8,128)(2,1)S(1)}, bf16[1,224,512]{2,1,0:T(8,128)(2,1)S(1)}, u32[]{:S(2)}, u32[]{:S(2)}) collective-permute-start(bf16[1,224,512]{2,1,0:T(8,128)(2,1)S(1)} %get-tuple-element.291), channel_id=1, source_target_pairs={{0,8},{1,25},{2,10},{3,27},{4,12},{5,29},{6,14},{7,31},{8,0},{9,17... | collective-permute-start | bytes 688136 | tf_op jit(solution)/shard_map/ppermute | solution.py:169
  160.8 8.9 %collective-permute-start.39 = (bf16[2,56,512]{2,1,0:T(8,128)(2,1)S(1)}, bf16[2,56,512]{2,1,0:T(8,128)(2,1)S(1)}, u32[]{:S(2)}, u32[]{:S(2)}) collective-permute-start(bf16[2,56,512]{2,1,0:T(8,128)(2,1)S(1)} %get-tuple-element.300), channel_id=1, source_target_pairs={{0,24},{1,9},{2,26},{3,11},{4,28},{5,13},{6,30},{7,15},{8,16},{9,1... | collective-permute-start | bytes 344072 | tf_op jit(solution)/shard_map/ppermute | solution.py:169
  (21 other events, 132.9 us)

commit v18 on v17

--- a/solution.py
+++ b/solution.py
@@ -1101,18 +1101,16 @@
         joint_step = [keep_joint, turned_swap(send, 1)]
         keep, send = combine(after(last_step, keep_joint), 2)
         last_step = [keep, turned_swap(send, 2)]
-        keep_joint, send = combine(joint_step, 2)
-        joint_step = [keep_joint, turned_swap(send, 0)]
-        keep, send = combine(after(last_step, keep_joint), 2)
+        keep, send = combine(after(last_step, *joint_step), 2)
         last_step = [keep, turned_swap(send, 1)]
-        keep, send = combine(last_step, 2)
-        last_step = [keep, turned_swap(send, 0)]
+        keep, send = combine_joint([joint_step, last_step], 2)
+        final_step = [keep, turned_swap(send, 0)]
 
         def plan(me_ref, *refs):
             me = me_ref[0]
-            joint, last = (sum(r[0].astype(F32) for r in given) for given in (refs[:2], refs[2:4]))
-            outs = refs[4:]
-            inner, cross = joint[: 2 * blocks * narrow, :], joint[2 * blocks * narrow :, :]
+            found, outs = refs[0][0].astype(F32) + refs[1][0].astype(F32), refs[2:]
+            first, second = 2 * blocks * narrow, 2 * blocks * narrow + 5 * narrow + 16
+            inner, cross, last = found[:first, :], found[first:second, :], found[second:, :]
             for i in range(blocks):
                 outs[0][:, i * width : (i + 1) * width] = inner[i * narrow : (i + 1) * narrow, :]
             outs[1][...] = inner[blocks * narrow :, :]
@@ -1132,7 +1130,7 @@
         (inner_share, outer_share, source_key_share, source_value_share, source_output_share,
          source_query_share, output_share, key_share, value_share, query_share, sums,
          inner_bias_share) = call(
-            plan, [(s, F32) for s in shapes], (me_array, *joint_step, *last_step), [], 2.0,
+            plan, [(s, F32) for s in shapes], (me_array, *final_step), [], 2.0,
             "finish",
         )
         inner_bias_share = inner_bias_share.reshape(wide)

time: 176 us -> 177 us (level)
  starting transfers between devices: 41.2 us -> 38.5 us
  waiting for transfers between devices: 66 us -> 68.6 us
    ppermute x22 -> x21, starting transfers between devices: 31.6 us -> 27 us  [turned_swap(): lax.ppermute(array, AXES, [(i, i ^ orders[i % 2][step]) for i in range(32)])]
    ppermute x22 -> x21, waiting for transfers between devices: 57.5 us -> 61.5 us  [turned_swap(): lax.ppermute(array, AXES, [(i, i ^ orders[i % 2][step]) for i in range(32)])]
    ppermute x19, starting transfers between devices: 9.63 us -> 11.6 us  [swap(): return lax.ppermute(array, AXES, [(i, i ^ mask) for i in range(devices)])]
  transfers between devices with their start and end apart: 41 -> 40, of which waited for: 22 -> 23; matrix products, arithmetic and copies ran while one was open for 2% -> 2% of each run, Pallas kernels for 24% -> 24%
where the time goes in v18:
time: 177 us; the launch traced here: 176 us
  waiting for transfers between devices  68.6 us (39%)
  Pallas kernels  61.3 us (35%)
  starting transfers between devices  38.5 us (22%)
  other arithmetic  3.93 us (2%)
  local copies, waits for them, and re-layouts  2.28 us (1%)
    ppermute x21, waiting for transfers between devices, turned_swap(): lax.ppermute(array, AXES, [(i, i ^ orders[i % 2][step]) for i in range(32)])  61.5 us
    pallas_call x12, Pallas kernels, call(): pl.pallas_call(kernel, out_shape=[jax.ShapeDtypeStruct(s, d) for s, d in...  58.4 us
    ppermute x21, starting transfers between devices, turned_swap(): lax.ppermute(array, AXES, [(i, i ^ orders[i % 2][step]) for i in range(32)])  27 us
    ppermute x19, starting transfers between devices, swap(): return lax.ppermute(array, AXES, [(i, i ^ mask) for i in range(devices)])  11.6 us
    ppermute x19, waiting for transfers between devices, swap(): return lax.ppermute(array, AXES, [(i, i ^ mask) for i in range(devices)])  7.15 us
  transfers between devices with their start and end apart: 40, of which 23 were waited for; matrix products, arithmetic and copies ran while one was open for 2% of the time, Pallas kernels for 24%

profile of v18, /device:TPU:0, one launch (start us, length us, event | category | flops | bytes accessed | tf_op | source)
XLA Modules:
  0.0 175.8 jit_solution(15932993534603822894)
XLA Ops:
  0.7 2.4 %tokens_packet.1 = (bf16[584,512]{1,0:T(8,128)(2,1)}, bf16[584,512]{1,0:T(8,128)(2,1)}) custom-call(s32[1]{0:T(128)} %bitcast.15.turn_ref, s32[2,256]{1,0:T(2,128)} %targets.1, s32[2,64]{1,0:T(2,128)} %sources.1, bf16[2,256,512]{2,1,0:T(8,128)(2,1)} %tokens_ref.1, bf16[2,64,512]{2,1,0:T(8,128)(2,1)} %memory_ref.1, bf16[2,256,512]{2,1,0:T(8,128)(2,1)} %cot_ref.1), custom_call_target="tpu_custom_call" | custom-call | flops 1 | bytes 1 | tf_op jit(solution)/shard_map/tokens_packet/pallas_call | solution.py:263
  3.1 3.0 %collective-permute-start.7 = (bf16[584,512]{1,0:T(8,128)(2,1)}, bf16[584,512]{1,0:T(8,128)(2,1)S(1)}, u32[]{:S(2)}, u32[]{:S(2)}) collective-permute-start(bf16[584,512]{1,0:T(8,128)(2,1)} %get-tuple-element.172), channel_id=1, source_target_pairs={{0,2},{1,3},{2,0},{3,1},{4,6},{5,7},{6,4},{7,5},{8,10},{9,11},{10,... | collective-permute-start | bytes 1794056 | tf_op jit(solution)/shard_map/ppermute | solution.py:161
  9.5 2.8 %collective-permute-done.refs_1_ = bf16[56,512]{1,0:T(8,128)(2,1)S(1)} collective-permute-done((bf16[56,512]{1,0:T(8,128)(2,1)}, bf16[56,512]{1,0:T(8,128)(2,1)S(1)}, u32[]{:S(2)}, u32[]{:S(2)}) %collective-permute-start) | collective-permute-done | bytes 57376 | tf_op jit(solution)/shard_map/ppermute | solution.py:169
  13.2 3.7 %collective-permute-start.2 = (bf16[112,512]{1,0:T(8,128)(2,1)S(1)}, bf16[112,512]{1,0:T(8,128)(2,1)S(1)}, u32[]{:S(2)}, u32[]{:S(2)}) collective-permute-start(bf16[112,512]{1,0:T(8,128)(2,1)S(1)} %join.9.refs_0_), channel_id=1, source_target_pairs={{0,24},{1,9},{2,26},{3,11},{4,28},{5,13},{6,30},{7,15},{8,16},{9,1... | collective-permute-start | bytes 344072 | tf_op jit(solution)/shard_map/ppermute | solution.py:169
  16.8 5.0 %collective-permute-done.1.refs_1_ = bf16[80,512]{1,0:T(8,128)(2,1)S(1)} collective-permute-done((bf16[80,512]{1,0:T(8,128)(2,1)}, bf16[80,512]{1,0:T(8,128)(2,1)S(1)}, u32[]{:S(2)}, u32[]{:S(2)}) %collective-permute-start.1) | collective-permute-done | bytes 81952 | tf_op jit(solution)/shard_map/ppermute | solution.py:169
  23.2 2.9 %collective-permute-start.5 = (bf16[160,512]{1,0:T(8,128)(2,1)S(1)}, bf16[160,512]{1,0:T(8,128)(2,1)S(1)}, u32[]{:S(2)}, u32[]{:S(2)}) collective-permute-start(bf16[160,512]{1,0:T(8,128)(2,1)S(1)} %join.10.refs_0_), channel_id=1, source_target_pairs={{0,24},{1,9},{2,26},{3,11},{4,28},{5,13},{6,30},{7,15},{8,16},{9,1... | collective-permute-start | bytes 491528 | tf_op jit(solution)/shard_map/ppermute | solution.py:169
  27.1 6.5 %collective-permute-done.3.refs_1_ = bf16[128,512]{1,0:T(8,128)(2,1)S(1)} collective-permute-done((bf16[128,512]{1,0:T(8,128)(2,1)}, bf16[128,512]{1,0:T(8,128)(2,1)S(1)}, u32[]{:S(2)}, u32[]{:S(2)}) %collective-permute-start.3) | collective-permute-done | bytes 131104 | tf_op jit(solution)/shard_map/ppermute | solution.py:169
  37.9 6.6 %collective-permute-done.6.refs_1_ = bf16[256,512]{1,0:T(8,128)(2,1)S(1)} collective-permute-done((bf16[256,512]{1,0:T(8,128)(2,1)S(1)}, bf16[256,512]{1,0:T(8,128)(2,1)S(1)}, u32[]{:S(2)}, u32[]{:S(2)}) %collective-permute-start.6) | collective-permute-done | bytes 262176 | tf_op jit(solution)/shard_map/ppermute | solution.py:169
  51.3 8.3 %self_attention.1 = (bf16[256,512]{1,0:T(8,128)(2,1)S(1)}, bf16[256,512]{1,0:T(8,128)(2,1)S(1)}, f32[4,1,512]{2,1,0:T(1,128)S(1)}, f32[4,1,512]{2,1,0:T(1,128)S(1)}) custom-call(s32[1]{0:T(128)} %bitcast.me_ref.refs_0_, bf16[256,512]{1,0:T(8,128)(2,1)S(1)} %get-tuple-element.192.refs_0_, bf16[256,512]{1,0:T(8,128)(2,1)S(1)} %get-tuple-element.193.refs_1_, ...), custom_call_target="tpu_custom_call" | custom-call | flops 1 | bytes 1 | tf_op jit(solution)/shard_map/self_attention/pallas_call | solution.py:263
  63.1 5.4 %cross_forward.1 = (f32[512,512]{1,0:T(8,128)S(1)}, f32[512,512]{1,0:T(8,128)S(1)}, bf16[512,512]{1,0:T(8,128)(2,1)S(1)}, bf16[256,512]{1,0:T(8,128)(2,1)S(1)}, ...) custom-call(s32[1]{0:T(128)} %bitcast.me_ref.refs_0_, ...), custom_call_target="tpu_custom_call" | custom-call | flops 1 | bytes 1 | tf_op jit(solution)/shard_map/cross_forward/pallas_call | solution.py:263
  68.4 6.1 %collective-permute-done.15.refs_2_ = bf16[1024,512]{1,0:T(8,128)(2,1)S(1)} collective-permute-done((bf16[1024,512]{1,0:T(8,128)(2,1)S(1)}, bf16[1024,512]{1,0:T(8,128)(2,1)S(1)}, u32[]{:S(2)}, u32[]{:S(2)}) %collective-permute-start.15) | collective-permute-done | bytes 1048608 | tf_op jit(solution)/shard_map/ppermute | solution.py:169
  74.5 2.7 %collective-permute-done.20.refs_4_ = bf16[1024,512]{1,0:T(8,128)(2,1)S(1)} collective-permute-done((bf16[1024,512]{1,0:T(8,128)(2,1)S(1)}, bf16[1024,512]{1,0:T(8,128)(2,1)S(1)}, u32[]{:S(2)}, u32[]{:S(2)}) %collective-permute-start.20) | collective-permute-done | bytes 1048608 | tf_op jit(solution)/shard_map/ppermute | solution.py:161
  77.2 13.1 %inner.1 = (f32[256,512]{1,0:T(8,128)S(1)}, bf16[256,512]{1,0:T(8,128)(2,1)}, f32[512,512]{1,0:T(8,128)S(1)}, f32[8,512]{1,0:T(8,128)S(1)}, bf16[16,128,512]{2,1...) custom-call(s32[1]{0:T(128)} %bitcast.me_ref.refs_0_, bf16[1024,512]{1,0:T(8,128)(2,1)S(1)} %join.17.refs_1_, ...), custom_call_target="tpu_custom_call" | custom-call | flops 1 | bytes 1 | tf_op jit(solution)/shard_map/inner/pallas_call | solution.py:263
  90.4 8.4 %cross_back.1 = (f32[512,512]{1,0:T(8,128)S(1)}, f32[128,512]{1,0:T(8,128)S(1)}, f32[128,512]{1,0:T(8,128)S(1)}, f32[16,512]{1,0:T(8,128)S(1)}, bf16[512,256]{1,...) custom-call(s32[1]{0:T(128)} %bitcast.me_ref.refs_0_, ...), custom_call_target="tpu_custom_call" | custom-call | flops 1 | bytes 1 | tf_op jit(solution)/shard_map/cross_back/pallas_call | solution.py:263
  102.5 6.1 %self_back_upper.1 = (bf16[512,256]{1,0:T(8,128)(2,1)S(1)}, f32[1024,256]{1,0:T(8,128)S(1)}, bf16[512,256]{1,0:T(8,128)(2,1)S(1)}, bf16[512,256]{1,0:T(8,128)(2,1)S(1)}) custom-call(s32[1]{0:T(128)} %bitcast.me_ref.refs_0_, bf16[512,256]{1,0:T(8,128)(2,1)S(1)} %get-tuple-element.236.refs_1_, bf16[1024,256]{1,0:T(8,128)(2,1)S(1)} %get-tuple-element.194.refs_2_, ...), custom_call_target="tpu_custom_call" | custom-call | flops 1 | bytes 1 | tf_op jit(solution)/shard_map/self_back_upper/pallas_call | solution.py:263
  111.4 7.1 %self_back_lower.1 = (f32[512,512]{1,0:T(8,128)S(1)}, f32[8,512]{1,0:T(8,128)S(1)}, bf16[512,512]{1,0:T(8,128)(2,1)S(1)}, f32[1024,256]{1,0:T(8,128)S(1)}, bf16[...) custom-call(s32[1]{0:T(128)} %bitcast.me_ref.refs_0_, bf16[448,512]{1,0:T(8,128)(2,1)S(1)} %join.13.refs_1_, ...), custom_call_target="tpu_custom_call" | custom-call | flops 1 | bytes 1 | tf_op jit(solution)/shard_map/self_back_lower/pallas_call | solution.py:263
  120.9 4.1 %collective-permute-done.25.refs_1_ = bf16[8,96,512]{2,1,0:T(8,128)(2,1)S(1)} collective-permute-done((bf16[8,96,512]{2,1,0:T(8,128)(2,1)S(1)}, bf16[8,96,512]{2,1,0:T(8,128)(2,1)S(1)}, u32[]{:S(2)}, u32[]{:S(2)}) %collective-permute-start.25) | collective-permute-done | bytes 786464 | tf_op jit(solution)/shard_map/ppermute | solution.py:169
  127.2 2.1 %collective-permute-start.34 = (bf16[4,128,512]{2,1,0:T(8,128)(2,1)S(1)}, bf16[4,128,512]{2,1,0:T(8,128)(2,1)S(1)}, u32[]{:S(2)}, u32[]{:S(2)}) collective-permute-start(bf16[4,128,512]{2,1,0:T(8,128)(2,1)S(1)} %get-tuple-element.280), channel_id=1, source_target_pairs={{0,2},{1,5},{2,0},{3,7},{4,6},{5,1},{6,4},{7,3},{8,10},{9,13},{10,... | collective-permute-start | bytes 1572872 | tf_op jit(solution)/shard_map/ppermute | solution.py:169
  131.6 10.4 %collective-permute-done.34.refs_1_ = bf16[4,128,512]{2,1,0:T(8,128)(2,1)S(1)} collective-permute-done((bf16[4,128,512]{2,1,0:T(8,128)(2,1)S(1)}, bf16[4,128,512]{2,1,0:T(8,128)(2,1)S(1)}, u32[]{:S(2)}, u32[]{:S(2)}) %collective-permute-start.34) | collective-permute-done | bytes 524320 | tf_op jit(solution)/shard_map/ppermute | solution.py:169
  149.5 4.4 %collective-permute-done.36.refs_1_ = bf16[2,224,512]{2,1,0:T(8,128)(2,1)S(1)} collective-permute-done((bf16[2,224,512]{2,1,0:T(8,128)(2,1)S(1)}, bf16[2,224,512]{2,1,0:T(8,128)(2,1)S(1)}, u32[]{:S(2)}, u32[]{:S(2)}) %collective-permute-start.36) | collective-permute-done | bytes 458784 | tf_op jit(solution)/shard_map/ppermute | solution.py:169
  153.9 5.1 %collective-permute-done.37.refs_1_ = bf16[4,56,512]{2,1,0:T(8,128)(2,1)S(1)} collective-permute-done((bf16[4,56,512]{2,1,0:T(8,128)(2,1)}, bf16[4,56,512]{2,1,0:T(8,128)(2,1)S(1)}, u32[]{:S(2)}, u32[]{:S(2)}) %collective-permute-start.37) | collective-permute-done | bytes 229408 | tf_op jit(solution)/shard_map/ppermute | solution.py:169
  163.0 3.8 %collective-permute-done.38.refs_3_ = bf16[2,56,512]{2,1,0:T(8,128)(2,1)S(1)} collective-permute-done((bf16[2,56,512]{2,1,0:T(8,128)(2,1)S(1)}, bf16[2,56,512]{2,1,0:T(8,128)(2,1)S(1)}, u32[]{:S(2)}, u32[]{:S(2)}) %collective-permute-start.38) | collective-permute-done | bytes 114720 | tf_op jit(solution)/shard_map/ppermute | solution.py:169
  166.9 2.4 %collective-permute-start.39 = (bf16[1,280,512]{2,1,0:T(8,128)(2,1)S(1)}, bf16[1,280,512]{2,1,0:T(8,128)(2,1)S(1)}, u32[]{:S(2)}, u32[]{:S(2)}) collective-permute-start(bf16[1,280,512]{2,1,0:T(8,128)(2,1)S(1)} %get-tuple-element.298), channel_id=1, source_target_pairs={{0,8},{1,25},{2,10},{3,27},{4,12},{5,29},{6,14},{7,31},{8,0},{9,17... | collective-permute-start | bytes 860168 | tf_op jit(solution)/shard_map/ppermute | solution.py:169
  171.1 2.8 %collective-permute-done.39.refs_1_ = bf16[1,280,512]{2,1,0:T(8,128)(2,1)S(1)} collective-permute-done((bf16[1,280,512]{2,1,0:T(8,128)(2,1)S(1)}, bf16[1,280,512]{2,1,0:T(8,128)(2,1)S(1)}, u32[]{:S(2)}, u32[]{:S(2)}) %collective-permute-start.39) | collective-permute-done | bytes 286752 | tf_op jit(solution)/shard_map/ppermute | solution.py:169
  (101 shorter events, 49.6 us)
Async XLA Ops:
  3.1 23.0 %collective-permute-start.7 = (bf16[584,512]{1,0:T(8,128)(2,1)}, bf16[584,512]{1,0:T(8,128)(2,1)S(1)}, u32[]{:S(2)}, u32[]{:S(2)}) collective-permute-start(bf16[584,512]{1,0:T(8,128)(2,1)} %get-tuple-element.172), channel_id=1, source_target_pairs={{0,2},{1,3},{2,0},{3,1},{4,6},{5,7},{6,4},{7,5},{8,10},{9,11},{10,... | collective-permute-start | bytes 1794056 | tf_op jit(solution)/shard_map/ppermute | solution.py:161
  6.0 27.5 %collective-permute-start.8 = (bf16[584,512]{1,0:T(8,128)(2,1)}, bf16[584,512]{1,0:T(8,128)(2,1)S(1)}, u32[]{:S(2)}, u32[]{:S(2)}) collective-permute-start(bf16[584,512]{1,0:T(8,128)(2,1)} %get-tuple-element.182.refs_5_.refs_6_), channel_id=1, source_target_pairs={{0,1},{1,0},{2,3},{3,2},{4,5},{5,4},{6,7},{7,6},{8,9},{9,8},{10,11... | collective-permute-start | bytes 1794056 | tf_op jit(solution)/shard_map/ppermute | solution.py:161
  13.2 8.7 %collective-permute-start.2 = (bf16[112,512]{1,0:T(8,128)(2,1)S(1)}, bf16[112,512]{1,0:T(8,128)(2,1)S(1)}, u32[]{:S(2)}, u32[]{:S(2)}) collective-permute-start(bf16[112,512]{1,0:T(8,128)(2,1)S(1)} %join.9.refs_0_), channel_id=1, source_target_pairs={{0,24},{1,9},{2,26},{3,11},{4,28},{5,13},{6,30},{7,15},{8,16},{9,1... | collective-permute-start | bytes 344072 | tf_op jit(solution)/shard_map/ppermute | solution.py:169
  21.9 11.6 %collective-permute-start.4 = (bf16[224,512]{1,0:T(8,128)(2,1)S(1)}, bf16[224,512]{1,0:T(8,128)(2,1)S(1)}, u32[]{:S(2)}, u32[]{:S(2)}) collective-permute-start(bf16[224,512]{1,0:T(8,128)(2,1)S(1)} %join.11.refs_0_), channel_id=1, source_target_pairs={{0,2},{1,5},{2,0},{3,7},{4,6},{5,1},{6,4},{7,3},{8,10},{9,13},{10,... | collective-permute-start | bytes 688136 | tf_op jit(solution)/shard_map/ppermute | solution.py:169
  23.2 10.3 %collective-permute-start.5 = (bf16[160,512]{1,0:T(8,128)(2,1)S(1)}, bf16[160,512]{1,0:T(8,128)(2,1)S(1)}, u32[]{:S(2)}, u32[]{:S(2)}) collective-permute-start(bf16[160,512]{1,0:T(8,128)(2,1)S(1)} %join.10.refs_0_), channel_id=1, source_target_pairs={{0,24},{1,9},{2,26},{3,11},{4,28},{5,13},{6,30},{7,15},{8,16},{9,1... | collective-permute-start | bytes 491528 | tf_op jit(solution)/shard_map/ppermute | solution.py:169
  26.1 20.9 %collective-permute-start.12 = (bf16[584,512]{1,0:T(8,128)(2,1)S(1)}, bf16[584,512]{1,0:T(8,128)(2,1)S(1)}, u32[]{:S(2)}, u32[]{:S(2)}) collective-permute-start(bf16[584,512]{1,0:T(8,128)(2,1)S(1)} %collective-permute-done.7.refs_6_.refs_7_), channel_id=1, source_target_pairs={{0,1},{1,0},{2,3},{3,2},{4,5},{5,4},{6,7},{7,6},{8,9},{9,8},{10,11... | collective-permute-start | bytes 1794056 | tf_op jit(solution)/shard_map/ppermute | solution.py:161
  33.6 11.6 %collective-permute-start.9 = (bf16[448,512]{1,0:T(8,128)(2,1)S(1)}, bf16[448,512]{1,0:T(8,128)(2,1)S(1)}, u32[]{:S(2)}, u32[]{:S(2)}) collective-permute-start(bf16[448,512]{1,0:T(8,128)(2,1)S(1)} %join.13.refs_1_), channel_id=1, source_target_pairs={{0,4},{1,3},{2,6},{3,1},{4,0},{5,7},{6,2},{7,5},{8,12},{9,11},{10,... | collective-permute-start | bytes 1376264 | tf_op jit(solution)/shard_map/ppermute | solution.py:169
  35.3 9.8 %collective-permute-start.10 = (bf16[320,512]{1,0:T(8,128)(2,1)S(1)}, bf16[320,512]{1,0:T(8,128)(2,1)S(1)}, u32[]{:S(2)}, u32[]{:S(2)}) collective-permute-start(bf16[320,512]{1,0:T(8,128)(2,1)S(1)} %join.14.refs_0_), channel_id=1, source_target_pairs={{0,2},{1,5},{2,0},{3,7},{4,6},{5,1},{6,4},{7,3},{8,10},{9,13},{10,... | collective-permute-start | bytes 983048 | tf_op jit(solution)/shard_map/ppermute | solution.py:169
  45.2 14.4 %collective-permute-start.11 = (bf16[512,512]{1,0:T(8,128)(2,1)S(1)}, bf16[512,512]{1,0:T(8,128)(2,1)S(1)}, u32[]{:S(2)}, u32[]{:S(2)}) collective-permute-start(bf16[512,512]{1,0:T(8,128)(2,1)S(1)} %join.15.refs_0_), channel_id=1, source_target_pairs={{0,2},{1,5},{2,0},{3,7},{4,6},{5,1},{6,4},{7,3},{8,10},{9,13},{10,... | collective-permute-start | bytes 1572872 | tf_op jit(solution)/shard_map/ppermute | solution.py:169
  47.6 12.4 %collective-permute-start.16 = (bf16[640,512]{1,0:T(8,128)(2,1)S(1)}, bf16[640,512]{1,0:T(8,128)(2,1)S(1)}, u32[]{:S(2)}, u32[]{:S(2)}) collective-permute-start(bf16[640,512]{1,0:T(8,128)(2,1)S(1)} %join.16.refs_1_), channel_id=1, source_target_pairs={{0,4},{1,3},{2,6},{3,1},{4,0},{5,7},{6,2},{7,5},{8,12},{9,11},{10,... | collective-permute-start | bytes 1966088 | tf_op jit(solution)/shard_map/ppermute | solution.py:169
  59.7 14.9 %collective-permute-start.15 = (bf16[1024,512]{1,0:T(8,128)(2,1)S(1)}, bf16[1024,512]{1,0:T(8,128)(2,1)S(1)}, u32[]{:S(2)}, u32[]{:S(2)}) collective-permute-start(bf16[1024,512]{1,0:T(8,128)(2,1)S(1)} %join.17.refs_1_), channel_id=1, source_target_pairs={{0,4},{1,3},{2,6},{3,1},{4,0},{5,7},{6,2},{7,5},{8,12},{9,11},{10,... | collective-permute-start | bytes 3145736 | tf_op jit(solution)/shard_map/ppermute | solution.py:169
  61.3 13.3 %collective-permute-start.19 = (bf16[1024,512]{1,0:T(8,128)(2,1)S(1)}, bf16[1024,512]{1,0:T(8,128)(2,1)S(1)}, u32[]{:S(2)}, u32[]{:S(2)}) collective-permute-start(bf16[1024,512]{1,0:T(8,128)(2,1)S(1)} %join.17.refs_1_), channel_id=1, source_target_pairs={{0,1},{1,0},{2,3},{3,2},{4,5},{5,4},{6,7},{7,6},{8,9},{9,8},{10,11... | collective-permute-start | bytes 3145736 | tf_op jit(solution)/shard_map/ppermute | solution.py:161
  90.3 9.0 %collective-permute-start.21 = (bf16[16,128,512]{2,1,0:T(8,128)(2,1)S(1)}, bf16[16,128,512]{2,1,0:T(8,128)(2,1)S(1)}, u32[]{:S(2)}, u32[]{:S(2)}) collective-permute-start(bf16[16,128,512]{2,1,0:T(8,128)(2,1)S(1)} %get-tuple-element.221), channel_id=1, source_target_pairs={{0,1},{1,0},{2,3},{3,2},{4,5},{5,4},{6,7},{7,6},{8,9},{9,8},{10,11... | collective-permute-start | bytes 6291464 | tf_op jit(solution)/shard_map/ppermute | solution.py:161
  102.2 18.4 %collective-permute-start.24 = (bf16[8,128,512]{2,1,0:T(8,128)(2,1)S(1)}, bf16[8,128,512]{2,1,0:T(8,128)(2,1)S(1)}, u32[]{:S(2)}, u32[]{:S(2)}) collective-permute-start(bf16[8,128,512]{2,1,0:T(8,128)(2,1)S(1)} %get-tuple-element.253), channel_id=1, source_target_pairs={{0,4},{1,3},{2,6},{3,1},{4,0},{5,7},{6,2},{7,5},{8,12},{9,11},{10,... | collective-permute-start | bytes 3145736 | tf_op jit(solution)/shard_map/ppermute | solution.py:169
  109.0 16.0 %collective-permute-start.25 = (bf16[8,96,512]{2,1,0:T(8,128)(2,1)S(1)}, bf16[8,96,512]{2,1,0:T(8,128)(2,1)S(1)}, u32[]{:S(2)}, u32[]{:S(2)}) collective-permute-start(bf16[8,96,512]{2,1,0:T(8,128)(2,1)S(1)} %get-tuple-element.258), channel_id=1, source_target_pairs={{0,2},{1,5},{2,0},{3,7},{4,6},{5,1},{6,4},{7,3},{8,10},{9,13},{10,... | collective-permute-start | bytes 2359304 | tf_op jit(solution)/shard_map/ppermute | solution.py:169
  110.9 14.3 %collective-permute-start.26 = (bf16[512,256]{1,0:T(8,128)(2,1)S(1)}, bf16[512,256]{1,0:T(8,128)(2,1)S(1)}, u32[]{:S(2)}, u32[]{:S(2)}) collective-permute-start(bf16[512,256]{1,0:T(8,128)(2,1)S(1)} %get-tuple-element.267), channel_id=1, source_target_pairs={{0,1},{1,0},{2,3},{3,2},{4,5},{5,4},{6,7},{7,6},{8,9},{9,8},{10,11... | collective-permute-start | bytes 786440 | tf_op jit(solution)/shard_map/ppermute | solution.py:161
  110.9 14.3 %collective-permute-start.27 = (bf16[512,256]{1,0:T(8,128)(2,1)S(1)}, bf16[512,256]{1,0:T(8,128)(2,1)S(1)}, u32[]{:S(2)}, u32[]{:S(2)}) collective-permute-start(bf16[512,256]{1,0:T(8,128)(2,1)S(1)} %get-tuple-element.268), channel_id=1, source_target_pairs={{0,1},{1,0},{2,3},{3,2},{4,5},{5,4},{6,7},{7,6},{8,9},{9,8},{10,11... | collective-permute-start | bytes 786440 | tf_op jit(solution)/shard_map/ppermute | solution.py:161
  127.2 14.8 %collective-permute-start.34 = (bf16[4,128,512]{2,1,0:T(8,128)(2,1)S(1)}, bf16[4,128,512]{2,1,0:T(8,128)(2,1)S(1)}, u32[]{:S(2)}, u32[]{:S(2)}) collective-permute-start(bf16[4,128,512]{2,1,0:T(8,128)(2,1)S(1)} %get-tuple-element.280), channel_id=1, source_target_pairs={{0,2},{1,5},{2,0},{3,7},{4,6},{5,1},{6,4},{7,3},{8,10},{9,13},{10,... | collective-permute-start | bytes 1572872 | tf_op jit(solution)/shard_map/ppermute | solution.py:169
  129.3 12.7 %collective-permute-start.35 = (bf16[4,96,512]{2,1,0:T(8,128)(2,1)S(1)}, bf16[4,96,512]{2,1,0:T(8,128)(2,1)S(1)}, u32[]{:S(2)}, u32[]{:S(2)}) collective-permute-start(bf16[4,96,512]{2,1,0:T(8,128)(2,1)S(1)} %get-tuple-element.281), channel_id=1, source_target_pairs={{0,4},{1,3},{2,6},{3,1},{4,0},{5,7},{6,2},{7,5},{8,12},{9,11},{10,... | collective-permute-start | bytes 1179656 | tf_op jit(solution)/shard_map/ppermute | solution.py:169
  129.6 15.2 %collective-permute-start.31 = (bf16[8,56,512]{2,1,0:T(8,128)(2,1)S(1)}, bf16[8,56,512]{2,1,0:T(8,128)(2,1)S(1)}, u32[]{:S(2)}, u32[]{:S(2)}) collective-permute-start(bf16[8,56,512]{2,1,0:T(8,128)(2,1)S(1)} %get-tuple-element.275), channel_id=1, source_target_pairs={{0,4},{1,3},{2,6},{3,1},{4,0},{5,7},{6,2},{7,5},{8,12},{9,11},{10,... | collective-permute-start | bytes 1376264 | tf_op jit(solution)/shard_map/ppermute | solution.py:169
  142.2 11.7 %collective-permute-start.36 = (bf16[2,224,512]{2,1,0:T(8,128)(2,1)S(1)}, bf16[2,224,512]{2,1,0:T(8,128)(2,1)S(1)}, u32[]{:S(2)}, u32[]{:S(2)}) collective-permute-start(bf16[2,224,512]{2,1,0:T(8,128)(2,1)S(1)} %get-tuple-element.287), channel_id=1, source_target_pairs={{0,24},{1,9},{2,26},{3,11},{4,28},{5,13},{6,30},{7,15},{8,16},{9,1... | collective-permute-start | bytes 1376264 | tf_op jit(solution)/shard_map/ppermute | solution.py:169
  144.8 15.8 %collective-permute-start.32 = (bf16[256,512]{1,0:T(8,128)(2,1)}, bf16[256,512]{1,0:T(8,128)(2,1)}, u32[]{:S(2)}, u32[]{:S(2)}) collective-permute-start(bf16[256,512]{1,0:T(8,128)(2,1)} %get-tuple-element.276), channel_id=1, source_target_pairs={{0,2},{1,3},{2,0},{3,1},{4,6},{5,7},{6,4},{7,5},{8,10},{9,11},{10,... | collective-permute-start | bytes 786440 | tf_op jit(solution)/shard_map/ppermute | solution.py:161
  147.5 11.5 %collective-permute-start.37 = (bf16[4,56,512]{2,1,0:T(8,128)(2,1)}, bf16[4,56,512]{2,1,0:T(8,128)(2,1)S(1)}, u32[]{:S(2)}, u32[]{:S(2)}) collective-permute-start(bf16[4,56,512]{2,1,0:T(8,128)(2,1)} %get-tuple-element.292), channel_id=1, source_target_pairs={{0,2},{1,5},{2,0},{3,7},{4,6},{5,1},{6,4},{7,3},{8,10},{9,13},{10,... | collective-permute-start | bytes 688136 | tf_op jit(solution)/shard_map/ppermute | solution.py:169
  147.5 15.4 %collective-permute-start.33 = (bf16[320,512]{1,0:T(8,128)(2,1)S(1)}, bf16[320,512]{1,0:T(8,128)(2,1)S(1)}, u32[]{:S(2)}, u32[]{:S(2)}) collective-permute-start(bf16[320,512]{1,0:T(8,128)(2,1)S(1)} %get-tuple-element.278), channel_id=1, source_target_pairs={{0,2},{1,3},{2,0},{3,1},{4,6},{5,7},{6,4},{7,5},{8,10},{9,11},{10,... | collective-permute-start | bytes 983048 | tf_op jit(solution)/shard_map/ppermute | solution.py:161
  (20 other events, 127.6 us)

commit v19 on v17

--- a/solution.py
+++ b/solution.py
@@ -1096,11 +1096,12 @@
     if packed:
         keep, send = combine([grads_last[0], swap(grads_last[1], 1, 32)], 2)
         last_step = [keep, turned_swap(send, 3)]
-        in_send, out_send = after((in_send, out_send), last_step[1])
+        in_send = after(in_send, last_step[1])
         keep_joint, send = combine_joint(after([inner_step, cross_step], in_own), 2)
         joint_step = [keep_joint, turned_swap(send, 1)]
         keep, send = combine(after(last_step, keep_joint), 2)
         last_step = [keep, turned_swap(send, 2)]
+        out_send = after(out_send, keep)
         keep_joint, send = combine(joint_step, 2)
         joint_step = [keep_joint, turned_swap(send, 0)]
         keep, send = combine(after(last_step, keep_joint), 2)

time: 176 us -> 176 us (level)
  no operation moved by 1% of the time
where the time goes in v19:
time: 176 us
  waiting for transfers between devices  66 us (38%)
  Pallas kernels  61.3 us (35%)
  starting transfers between devices  41.2 us (23%)
  other arithmetic  3.94 us (2%)
  local copies, waits for them, and re-layouts  2.28 us (1%)
    pallas_call x12, Pallas kernels, call(): pl.pallas_call(kernel, out_shape=[jax.ShapeDtypeStruct(s, d) for s, d in...  58.4 us
    ppermute x22, waiting for transfers between devices, turned_swap(): lax.ppermute(array, AXES, [(i, i ^ orders[i % 2][step]) for i in range(32)])  57.5 us
    ppermute x22, starting transfers between devices, turned_swap(): lax.ppermute(array, AXES, [(i, i ^ orders[i % 2][step]) for i in range(32)])  31.6 us
    ppermute x19, starting transfers between devices, swap(): return lax.ppermute(array, AXES, [(i, i ^ mask) for i in range(devices)])  9.63 us
    ppermute x19, waiting for transfers between devices, swap(): return lax.ppermute(array, AXES, [(i, i ^ mask) for i in range(devices)])  8.45 us
  transfers between devices with their start and end apart: 41, of which 22 were waited for; matrix products, arithmetic and copies ran while one was open for 2% of the time, Pallas kernels for 24%

profile of v19, /device:TPU:0, one launch (start us, length us, event | category | flops | bytes accessed | tf_op | source)
XLA Modules:
  0.0 175.8 jit_solution(6250151164540802379)
XLA Ops:
  0.7 2.4 %tokens_packet.1 = (bf16[584,512]{1,0:T(8,128)(2,1)}, bf16[584,512]{1,0:T(8,128)(2,1)}) custom-call(s32[1]{0:T(128)} %bitcast.15.turn_ref, s32[2,256]{1,0:T(2,128)} %targets.1, s32[2,64]{1,0:T(2,128)} %sources.1, bf16[2,256,512]{2,1,0:T(8,128)(2,1)} %tokens_ref.1, bf16[2,64,512]{2,1,0:T(8,128)(2,1)} %memory_ref.1, bf16[2,256,512]{2,1,0:T(8,128)(2,1)} %cot_ref.1), custom_call_target="tpu_custom_call" | custom-call | flops 1 | bytes 1 | tf_op jit(solution)/shard_map/tokens_packet/pallas_call | solution.py:263
  3.1 3.0 %collective-permute-start.7 = (bf16[584,512]{1,0:T(8,128)(2,1)}, bf16[584,512]{1,0:T(8,128)(2,1)S(1)}, u32[]{:S(2)}, u32[]{:S(2)}) collective-permute-start(bf16[584,512]{1,0:T(8,128)(2,1)} %get-tuple-element.174), channel_id=1, source_target_pairs={{0,2},{1,3},{2,0},{3,1},{4,6},{5,7},{6,4},{7,5},{8,10},{9,11},{10,... | collective-permute-start | bytes 1794056 | tf_op jit(solution)/shard_map/ppermute | solution.py:161
  9.5 2.8 %collective-permute-done.refs_1_ = bf16[56,512]{1,0:T(8,128)(2,1)S(1)} collective-permute-done((bf16[56,512]{1,0:T(8,128)(2,1)}, bf16[56,512]{1,0:T(8,128)(2,1)S(1)}, u32[]{:S(2)}, u32[]{:S(2)}) %collective-permute-start) | collective-permute-done | bytes 57376 | tf_op jit(solution)/shard_map/ppermute | solution.py:169
  13.2 3.7 %collective-permute-start.2 = (bf16[112,512]{1,0:T(8,128)(2,1)S(1)}, bf16[112,512]{1,0:T(8,128)(2,1)S(1)}, u32[]{:S(2)}, u32[]{:S(2)}) collective-permute-start(bf16[112,512]{1,0:T(8,128)(2,1)S(1)} %join.9.refs_0_), channel_id=1, source_target_pairs={{0,24},{1,9},{2,26},{3,11},{4,28},{5,13},{6,30},{7,15},{8,16},{9,1... | collective-permute-start | bytes 344072 | tf_op jit(solution)/shard_map/ppermute | solution.py:169
  16.8 5.0 %collective-permute-done.1.refs_1_ = bf16[80,512]{1,0:T(8,128)(2,1)S(1)} collective-permute-done((bf16[80,512]{1,0:T(8,128)(2,1)}, bf16[80,512]{1,0:T(8,128)(2,1)S(1)}, u32[]{:S(2)}, u32[]{:S(2)}) %collective-permute-start.1) | collective-permute-done | bytes 81952 | tf_op jit(solution)/shard_map/ppermute | solution.py:169
  23.2 2.9 %collective-permute-start.5 = (bf16[160,512]{1,0:T(8,128)(2,1)S(1)}, bf16[160,512]{1,0:T(8,128)(2,1)S(1)}, u32[]{:S(2)}, u32[]{:S(2)}) collective-permute-start(bf16[160,512]{1,0:T(8,128)(2,1)S(1)} %join.10.refs_0_), channel_id=1, source_target_pairs={{0,24},{1,9},{2,26},{3,11},{4,28},{5,13},{6,30},{7,15},{8,16},{9,1... | collective-permute-start | bytes 491528 | tf_op jit(solution)/shard_map/ppermute | solution.py:169
  27.1 6.5 %collective-permute-done.3.refs_1_ = bf16[128,512]{1,0:T(8,128)(2,1)S(1)} collective-permute-done((bf16[128,512]{1,0:T(8,128)(2,1)}, bf16[128,512]{1,0:T(8,128)(2,1)S(1)}, u32[]{:S(2)}, u32[]{:S(2)}) %collective-permute-start.3) | collective-permute-done | bytes 131104 | tf_op jit(solution)/shard_map/ppermute | solution.py:169
  35.9 2.1 %collective-permute-start.6 = (bf16[256,512]{1,0:T(8,128)(2,1)S(1)}, bf16[256,512]{1,0:T(8,128)(2,1)S(1)}, u32[]{:S(2)}, u32[]{:S(2)}) collective-permute-start(bf16[256,512]{1,0:T(8,128)(2,1)S(1)} %join.12.refs_0_), channel_id=1, source_target_pairs={{0,24},{1,9},{2,26},{3,11},{4,28},{5,13},{6,30},{7,15},{8,16},{9,1... | collective-permute-start | bytes 786440 | tf_op jit(solution)/shard_map/ppermute | solution.py:169
  37.9 6.6 %collective-permute-done.6.refs_1_ = bf16[256,512]{1,0:T(8,128)(2,1)S(1)} collective-permute-done((bf16[256,512]{1,0:T(8,128)(2,1)S(1)}, bf16[256,512]{1,0:T(8,128)(2,1)S(1)}, u32[]{:S(2)}, u32[]{:S(2)}) %collective-permute-start.6) | collective-permute-done | bytes 262176 | tf_op jit(solution)/shard_map/ppermute | solution.py:169
  51.3 8.3 %self_attention.1 = (bf16[256,512]{1,0:T(8,128)(2,1)S(1)}, bf16[256,512]{1,0:T(8,128)(2,1)S(1)}, f32[4,1,512]{2,1,0:T(1,128)S(1)}, f32[4,1,512]{2,1,0:T(1,128)S(1)}) custom-call(s32[1]{0:T(128)} %bitcast.me_ref.refs_0_, bf16[256,512]{1,0:T(8,128)(2,1)S(1)} %get-tuple-element.194.refs_0_, bf16[256,512]{1,0:T(8,128)(2,1)S(1)} %get-tuple-element.195.refs_1_, ...), custom_call_target="tpu_custom_call" | custom-call | flops 1 | bytes 1 | tf_op jit(solution)/shard_map/self_attention/pallas_call | solution.py:263
  63.1 5.4 %cross_forward.1 = (f32[512,512]{1,0:T(8,128)S(1)}, f32[512,512]{1,0:T(8,128)S(1)}, bf16[512,512]{1,0:T(8,128)(2,1)S(1)}, bf16[256,512]{1,0:T(8,128)(2,1)S(1)}, ...) custom-call(s32[1]{0:T(128)} %bitcast.me_ref.refs_0_, ...), custom_call_target="tpu_custom_call" | custom-call | flops 1 | bytes 1 | tf_op jit(solution)/shard_map/cross_forward/pallas_call | solution.py:263
  68.4 6.1 %collective-permute-done.15.refs_2_ = bf16[1024,512]{1,0:T(8,128)(2,1)S(1)} collective-permute-done((bf16[1024,512]{1,0:T(8,128)(2,1)S(1)}, bf16[1024,512]{1,0:T(8,128)(2,1)S(1)}, u32[]{:S(2)}, u32[]{:S(2)}) %collective-permute-start.15) | collective-permute-done | bytes 1048608 | tf_op jit(solution)/shard_map/ppermute | solution.py:169
  74.5 2.7 %collective-permute-done.20.refs_4_ = bf16[1024,512]{1,0:T(8,128)(2,1)S(1)} collective-permute-done((bf16[1024,512]{1,0:T(8,128)(2,1)S(1)}, bf16[1024,512]{1,0:T(8,128)(2,1)S(1)}, u32[]{:S(2)}, u32[]{:S(2)}) %collective-permute-start.20) | collective-permute-done | bytes 1048608 | tf_op jit(solution)/shard_map/ppermute | solution.py:161
  77.2 13.1 %inner.1 = (f32[256,512]{1,0:T(8,128)S(1)}, bf16[256,512]{1,0:T(8,128)(2,1)}, f32[512,512]{1,0:T(8,128)S(1)}, f32[8,512]{1,0:T(8,128)S(1)}, bf16[16,128,512]{2,1...) custom-call(s32[1]{0:T(128)} %bitcast.me_ref.refs_0_, bf16[1024,512]{1,0:T(8,128)(2,1)S(1)} %join.17.refs_1_, ...), custom_call_target="tpu_custom_call" | custom-call | flops 1 | bytes 1 | tf_op jit(solution)/shard_map/inner/pallas_call | solution.py:263
  90.4 8.4 %cross_back.1 = (f32[512,512]{1,0:T(8,128)S(1)}, f32[128,512]{1,0:T(8,128)S(1)}, f32[128,512]{1,0:T(8,128)S(1)}, f32[16,512]{1,0:T(8,128)S(1)}, bf16[512,256]{1,...) custom-call(s32[1]{0:T(128)} %bitcast.me_ref.refs_0_, ...), custom_call_target="tpu_custom_call" | custom-call | flops 1 | bytes 1 | tf_op jit(solution)/shard_map/cross_back/pallas_call | solution.py:263
  102.5 6.1 %self_back_upper.1 = (bf16[512,256]{1,0:T(8,128)(2,1)S(1)}, f32[1024,256]{1,0:T(8,128)S(1)}, bf16[512,256]{1,0:T(8,128)(2,1)S(1)}, bf16[512,256]{1,0:T(8,128)(2,1)S(1)}) custom-call(s32[1]{0:T(128)} %bitcast.me_ref.refs_0_, bf16[512,256]{1,0:T(8,128)(2,1)S(1)} %get-tuple-element.239.refs_1_, bf16[1024,256]{1,0:T(8,128)(2,1)S(1)} %get-tuple-element.196.refs_2_, ...), custom_call_target="tpu_custom_call" | custom-call | flops 1 | bytes 1 | tf_op jit(solution)/shard_map/self_back_upper/pallas_call | solution.py:263
  111.4 7.1 %self_back_lower.1 = (f32[512,512]{1,0:T(8,128)S(1)}, f32[8,512]{1,0:T(8,128)S(1)}, bf16[512,512]{1,0:T(8,128)(2,1)S(1)}, f32[1024,256]{1,0:T(8,128)S(1)}, bf16[...) custom-call(s32[1]{0:T(128)} %bitcast.me_ref.refs_0_, bf16[448,512]{1,0:T(8,128)(2,1)S(1)} %join.13.refs_1_, ...), custom_call_target="tpu_custom_call" | custom-call | flops 1 | bytes 1 | tf_op jit(solution)/shard_map/self_back_lower/pallas_call | solution.py:263
  120.9 4.1 %collective-permute-done.25.refs_1_ = bf16[8,96,512]{2,1,0:T(8,128)(2,1)S(1)} collective-permute-done((bf16[8,96,512]{2,1,0:T(8,128)(2,1)S(1)}, bf16[8,96,512]{2,1,0:T(8,128)(2,1)S(1)}, u32[]{:S(2)}, u32[]{:S(2)}) %collective-permute-start.25) | collective-permute-done | bytes 786464 | tf_op jit(solution)/shard_map/ppermute | solution.py:169
  127.2 2.1 %collective-permute-start.32 = (bf16[4,128,512]{2,1,0:T(8,128)(2,1)S(1)}, bf16[4,128,512]{2,1,0:T(8,128)(2,1)S(1)}, u32[]{:S(2)}, u32[]{:S(2)}) collective-permute-start(bf16[4,128,512]{2,1,0:T(8,128)(2,1)S(1)} %get-tuple-element.278), channel_id=1, source_target_pairs={{0,2},{1,5},{2,0},{3,7},{4,6},{5,1},{6,4},{7,3},{8,10},{9,13},{10,... | collective-permute-start | bytes 1572872 | tf_op jit(solution)/shard_map/ppermute | solution.py:169
  131.6 10.4 %collective-permute-done.32.refs_1_ = bf16[4,128,512]{2,1,0:T(8,128)(2,1)S(1)} collective-permute-done((bf16[4,128,512]{2,1,0:T(8,128)(2,1)S(1)}, bf16[4,128,512]{2,1,0:T(8,128)(2,1)S(1)}, u32[]{:S(2)}, u32[]{:S(2)}) %collective-permute-start.32) | collective-permute-done | bytes 524320 | tf_op jit(solution)/shard_map/ppermute | solution.py:169
  147.5 7.9 %collective-permute-done.36.refs_1_ = bf16[2,224,512]{2,1,0:T(8,128)(2,1)S(1)} collective-permute-done((bf16[2,224,512]{2,1,0:T(8,128)(2,1)S(1)}, bf16[2,224,512]{2,1,0:T(8,128)(2,1)S(1)}, u32[]{:S(2)}, u32[]{:S(2)}) %collective-permute-start.36) | collective-permute-done | bytes 458784 | tf_op jit(solution)/shard_map/ppermute | solution.py:169
  155.5 5.2 %collective-permute-start.37 = (bf16[1,224,512]{2,1,0:T(8,128)(2,1)S(1)}, bf16[1,224,512]{2,1,0:T(8,128)(2,1)S(1)}, u32[]{:S(2)}, u32[]{:S(2)}) collective-permute-start(bf16[1,224,512]{2,1,0:T(8,128)(2,1)S(1)} %get-tuple-element.295), channel_id=1, source_target_pairs={{0,8},{1,25},{2,10},{3,27},{4,12},{5,29},{6,14},{7,31},{8,0},{9,17... | collective-permute-start | bytes 688136 | tf_op jit(solution)/shard_map/ppermute | solution.py:169
  160.8 3.2 %collective-permute-start.39 = (bf16[2,56,512]{2,1,0:T(8,128)(2,1)S(1)}, bf16[2,56,512]{2,1,0:T(8,128)(2,1)S(1)}, u32[]{:S(2)}, u32[]{:S(2)}) collective-permute-start(bf16[2,56,512]{2,1,0:T(8,128)(2,1)S(1)} %get-tuple-element.300), channel_id=1, source_target_pairs={{0,24},{1,9},{2,26},{3,11},{4,28},{5,13},{6,30},{7,15},{8,16},{9,1... | collective-permute-start | bytes 344072 | tf_op jit(solution)/shard_map/ppermute | solution.py:169
  170.5 3.4 %collective-permute-done.40.refs_3_ = bf16[1,56,512]{2,1,0:T(8,128)(2,1)S(1)} collective-permute-done((bf16[1,56,512]{2,1,0:T(8,128)(2,1)S(1)}, bf16[1,56,512]{2,1,0:T(8,128)(2,1)S(1)}, u32[]{:S(2)}, u32[]{:S(2)}) %collective-permute-start.40) | collective-permute-done | bytes 57376 | tf_op jit(solution)/shard_map/ppermute | solution.py:169
  (104 shorter events, 46.3 us)
Async XLA Ops:
  3.1 23.0 %collective-permute-start.7 = (bf16[584,512]{1,0:T(8,128)(2,1)}, bf16[584,512]{1,0:T(8,128)(2,1)S(1)}, u32[]{:S(2)}, u32[]{:S(2)}) collective-permute-start(bf16[584,512]{1,0:T(8,128)(2,1)} %get-tuple-element.174), channel_id=1, source_target_pairs={{0,2},{1,3},{2,0},{3,1},{4,6},{5,7},{6,4},{7,5},{8,10},{9,11},{10,... | collective-permute-start | bytes 1794056 | tf_op jit(solution)/shard_map/ppermute | solution.py:161
  6.0 27.5 %collective-permute-start.8 = (bf16[584,512]{1,0:T(8,128)(2,1)}, bf16[584,512]{1,0:T(8,128)(2,1)S(1)}, u32[]{:S(2)}, u32[]{:S(2)}) collective-permute-start(bf16[584,512]{1,0:T(8,128)(2,1)} %get-tuple-element.184.refs_5_.refs_6_), channel_id=1, source_target_pairs={{0,1},{1,0},{2,3},{3,2},{4,5},{5,4},{6,7},{7,6},{8,9},{9,8},{10,11... | collective-permute-start | bytes 1794056 | tf_op jit(solution)/shard_map/ppermute | solution.py:161
  21.9 11.6 %collective-permute-start.4 = (bf16[224,512]{1,0:T(8,128)(2,1)S(1)}, bf16[224,512]{1,0:T(8,128)(2,1)S(1)}, u32[]{:S(2)}, u32[]{:S(2)}) collective-permute-start(bf16[224,512]{1,0:T(8,128)(2,1)S(1)} %join.11.refs_0_), channel_id=1, source_target_pairs={{0,2},{1,5},{2,0},{3,7},{4,6},{5,1},{6,4},{7,3},{8,10},{9,13},{10,... | collective-permute-start | bytes 688136 | tf_op jit(solution)/shard_map/ppermute | solution.py:169
  23.2 10.3 %collective-permute-start.5 = (bf16[160,512]{1,0:T(8,128)(2,1)S(1)}, bf16[160,512]{1,0:T(8,128)(2,1)S(1)}, u32[]{:S(2)}, u32[]{:S(2)}) collective-permute-start(bf16[160,512]{1,0:T(8,128)(2,1)S(1)} %join.10.refs_0_), channel_id=1, source_target_pairs={{0,24},{1,9},{2,26},{3,11},{4,28},{5,13},{6,30},{7,15},{8,16},{9,1... | collective-permute-start | bytes 491528 | tf_op jit(solution)/shard_map/ppermute | solution.py:169
  26.1 20.9 %collective-permute-start.12 = (bf16[584,512]{1,0:T(8,128)(2,1)S(1)}, bf16[584,512]{1,0:T(8,128)(2,1)S(1)}, u32[]{:S(2)}, u32[]{:S(2)}) collective-permute-start(bf16[584,512]{1,0:T(8,128)(2,1)S(1)} %collective-permute-done.7.refs_6_.refs_7_), channel_id=1, source_target_pairs={{0,1},{1,0},{2,3},{3,2},{4,5},{5,4},{6,7},{7,6},{8,9},{9,8},{10,11... | collective-permute-start | bytes 1794056 | tf_op jit(solution)/shard_map/ppermute | solution.py:161
  33.6 11.6 %collective-permute-start.9 = (bf16[448,512]{1,0:T(8,128)(2,1)S(1)}, bf16[448,512]{1,0:T(8,128)(2,1)S(1)}, u32[]{:S(2)}, u32[]{:S(2)}) collective-permute-start(bf16[448,512]{1,0:T(8,128)(2,1)S(1)} %join.13.refs_1_), channel_id=1, source_target_pairs={{0,4},{1,3},{2,6},{3,1},{4,0},{5,7},{6,2},{7,5},{8,12},{9,11},{10,... | collective-permute-start | bytes 1376264 | tf_op jit(solution)/shard_map/ppermute | solution.py:169
  35.3 9.8 %collective-permute-start.10 = (bf16[320,512]{1,0:T(8,128)(2,1)S(1)}, bf16[320,512]{1,0:T(8,128)(2,1)S(1)}, u32[]{:S(2)}, u32[]{:S(2)}) collective-permute-start(bf16[320,512]{1,0:T(8,128)(2,1)S(1)} %join.14.refs_0_), channel_id=1, source_target_pairs={{0,2},{1,5},{2,0},{3,7},{4,6},{5,1},{6,4},{7,3},{8,10},{9,13},{10,... | collective-permute-start | bytes 983048 | tf_op jit(solution)/shard_map/ppermute | solution.py:169
  45.2 14.4 %collective-permute-start.11 = (bf16[512,512]{1,0:T(8,128)(2,1)S(1)}, bf16[512,512]{1,0:T(8,128)(2,1)S(1)}, u32[]{:S(2)}, u32[]{:S(2)}) collective-permute-start(bf16[512,512]{1,0:T(8,128)(2,1)S(1)} %join.15.refs_0_), channel_id=1, source_target_pairs={{0,2},{1,5},{2,0},{3,7},{4,6},{5,1},{6,4},{7,3},{8,10},{9,13},{10,... | collective-permute-start | bytes 1572872 | tf_op jit(solution)/shard_map/ppermute | solution.py:169
  47.6 12.4 %collective-permute-start.16 = (bf16[640,512]{1,0:T(8,128)(2,1)S(1)}, bf16[640,512]{1,0:T(8,128)(2,1)S(1)}, u32[]{:S(2)}, u32[]{:S(2)}) collective-permute-start(bf16[640,512]{1,0:T(8,128)(2,1)S(1)} %join.16.refs_1_), channel_id=1, source_target_pairs={{0,4},{1,3},{2,6},{3,1},{4,0},{5,7},{6,2},{7,5},{8,12},{9,11},{10,... | collective-permute-start | bytes 1966088 | tf_op jit(solution)/shard_map/ppermute | solution.py:169
  59.7 14.9 %collective-permute-start.15 = (bf16[1024,512]{1,0:T(8,128)(2,1)S(1)}, bf16[1024,512]{1,0:T(8,128)(2,1)S(1)}, u32[]{:S(2)}, u32[]{:S(2)}) collective-permute-start(bf16[1024,512]{1,0:T(8,128)(2,1)S(1)} %join.17.refs_1_), channel_id=1, source_target_pairs={{0,4},{1,3},{2,6},{3,1},{4,0},{5,7},{6,2},{7,5},{8,12},{9,11},{10,... | collective-permute-start | bytes 3145736 | tf_op jit(solution)/shard_map/ppermute | solution.py:169
  61.3 13.3 %collective-permute-start.19 = (bf16[1024,512]{1,0:T(8,128)(2,1)S(1)}, bf16[1024,512]{1,0:T(8,128)(2,1)S(1)}, u32[]{:S(2)}, u32[]{:S(2)}) collective-permute-start(bf16[1024,512]{1,0:T(8,128)(2,1)S(1)} %join.17.refs_1_), channel_id=1, source_target_pairs={{0,1},{1,0},{2,3},{3,2},{4,5},{5,4},{6,7},{7,6},{8,9},{9,8},{10,11... | collective-permute-start | bytes 3145736 | tf_op jit(solution)/shard_map/ppermute | solution.py:161
  90.3 9.0 %collective-permute-start.21 = (bf16[16,128,512]{2,1,0:T(8,128)(2,1)S(1)}, bf16[16,128,512]{2,1,0:T(8,128)(2,1)S(1)}, u32[]{:S(2)}, u32[]{:S(2)}) collective-permute-start(bf16[16,128,512]{2,1,0:T(8,128)(2,1)S(1)} %get-tuple-element.224), channel_id=1, source_target_pairs={{0,1},{1,0},{2,3},{3,2},{4,5},{5,4},{6,7},{7,6},{8,9},{9,8},{10,11... | collective-permute-start | bytes 6291464 | tf_op jit(solution)/shard_map/ppermute | solution.py:161
  102.2 18.4 %collective-permute-start.24 = (bf16[8,128,512]{2,1,0:T(8,128)(2,1)S(1)}, bf16[8,128,512]{2,1,0:T(8,128)(2,1)S(1)}, u32[]{:S(2)}, u32[]{:S(2)}) collective-permute-start(bf16[8,128,512]{2,1,0:T(8,128)(2,1)S(1)} %get-tuple-element.256), channel_id=1, source_target_pairs={{0,4},{1,3},{2,6},{3,1},{4,0},{5,7},{6,2},{7,5},{8,12},{9,11},{10,... | collective-permute-start | bytes 3145736 | tf_op jit(solution)/shard_map/ppermute | solution.py:169
  109.0 16.0 %collective-permute-start.25 = (bf16[8,96,512]{2,1,0:T(8,128)(2,1)S(1)}, bf16[8,96,512]{2,1,0:T(8,128)(2,1)S(1)}, u32[]{:S(2)}, u32[]{:S(2)}) collective-permute-start(bf16[8,96,512]{2,1,0:T(8,128)(2,1)S(1)} %get-tuple-element.261), channel_id=1, source_target_pairs={{0,2},{1,5},{2,0},{3,7},{4,6},{5,1},{6,4},{7,3},{8,10},{9,13},{10,... | collective-permute-start | bytes 2359304 | tf_op jit(solution)/shard_map/ppermute | solution.py:169
  110.9 14.3 %collective-permute-start.26 = (bf16[512,256]{1,0:T(8,128)(2,1)S(1)}, bf16[512,256]{1,0:T(8,128)(2,1)S(1)}, u32[]{:S(2)}, u32[]{:S(2)}) collective-permute-start(bf16[512,256]{1,0:T(8,128)(2,1)S(1)} %get-tuple-element.270), channel_id=1, source_target_pairs={{0,1},{1,0},{2,3},{3,2},{4,5},{5,4},{6,7},{7,6},{8,9},{9,8},{10,11... | collective-permute-start | bytes 786440 | tf_op jit(solution)/shard_map/ppermute | solution.py:161
  110.9 14.3 %collective-permute-start.27 = (bf16[512,256]{1,0:T(8,128)(2,1)S(1)}, bf16[512,256]{1,0:T(8,128)(2,1)S(1)}, u32[]{:S(2)}, u32[]{:S(2)}) collective-permute-start(bf16[512,256]{1,0:T(8,128)(2,1)S(1)} %get-tuple-element.271), channel_id=1, source_target_pairs={{0,1},{1,0},{2,3},{3,2},{4,5},{5,4},{6,7},{7,6},{8,9},{9,8},{10,11... | collective-permute-start | bytes 786440 | tf_op jit(solution)/shard_map/ppermute | solution.py:161
  127.2 14.8 %collective-permute-start.32 = (bf16[4,128,512]{2,1,0:T(8,128)(2,1)S(1)}, bf16[4,128,512]{2,1,0:T(8,128)(2,1)S(1)}, u32[]{:S(2)}, u32[]{:S(2)}) collective-permute-start(bf16[4,128,512]{2,1,0:T(8,128)(2,1)S(1)} %get-tuple-element.278), channel_id=1, source_target_pairs={{0,2},{1,5},{2,0},{3,7},{4,6},{5,1},{6,4},{7,3},{8,10},{9,13},{10,... | collective-permute-start | bytes 1572872 | tf_op jit(solution)/shard_map/ppermute | solution.py:169
  129.3 12.7 %collective-permute-start.33 = (bf16[4,96,512]{2,1,0:T(8,128)(2,1)S(1)}, bf16[4,96,512]{2,1,0:T(8,128)(2,1)S(1)}, u32[]{:S(2)}, u32[]{:S(2)}) collective-permute-start(bf16[4,96,512]{2,1,0:T(8,128)(2,1)S(1)} %get-tuple-element.279), channel_id=1, source_target_pairs={{0,4},{1,3},{2,6},{3,1},{4,0},{5,7},{6,2},{7,5},{8,12},{9,11},{10,... | collective-permute-start | bytes 1179656 | tf_op jit(solution)/shard_map/ppermute | solution.py:169
  129.6 15.2 %collective-permute-start.31 = (bf16[8,56,512]{2,1,0:T(8,128)(2,1)S(1)}, bf16[8,56,512]{2,1,0:T(8,128)(2,1)S(1)}, u32[]{:S(2)}, u32[]{:S(2)}) collective-permute-start(bf16[8,56,512]{2,1,0:T(8,128)(2,1)S(1)} %get-tuple-element.277), channel_id=1, source_target_pairs={{0,4},{1,3},{2,6},{3,1},{4,0},{5,7},{6,2},{7,5},{8,12},{9,11},{10,... | collective-permute-start | bytes 1376264 | tf_op jit(solution)/shard_map/ppermute | solution.py:169
  142.2 13.2 %collective-permute-start.36 = (bf16[2,224,512]{2,1,0:T(8,128)(2,1)S(1)}, bf16[2,224,512]{2,1,0:T(8,128)(2,1)S(1)}, u32[]{:S(2)}, u32[]{:S(2)}) collective-permute-start(bf16[2,224,512]{2,1,0:T(8,128)(2,1)S(1)} %get-tuple-element.293), channel_id=1, source_target_pairs={{0,24},{1,9},{2,26},{3,11},{4,28},{5,13},{6,30},{7,15},{8,16},{9,1... | collective-permute-start | bytes 1376264 | tf_op jit(solution)/shard_map/ppermute | solution.py:169
  145.5 18.5 %collective-permute-start.34 = (bf16[256,512]{1,0:T(8,128)(2,1)}, bf16[256,512]{1,0:T(8,128)(2,1)}, u32[]{:S(2)}, u32[]{:S(2)}) collective-permute-start(bf16[256,512]{1,0:T(8,128)(2,1)} %get-tuple-element.289), channel_id=1, source_target_pairs={{0,2},{1,3},{2,0},{3,1},{4,6},{5,7},{6,4},{7,5},{8,10},{9,11},{10,... | collective-permute-start | bytes 786440 | tf_op jit(solution)/shard_map/ppermute | solution.py:161
  147.5 13.3 %collective-permute-start.38 = (bf16[4,56,512]{2,1,0:T(8,128)(2,1)}, bf16[4,56,512]{2,1,0:T(8,128)(2,1)S(1)}, u32[]{:S(2)}, u32[]{:S(2)}) collective-permute-start(bf16[4,56,512]{2,1,0:T(8,128)(2,1)} %get-tuple-element.296), channel_id=1, source_target_pairs={{0,2},{1,5},{2,0},{3,7},{4,6},{5,1},{6,4},{7,3},{8,10},{9,13},{10,... | collective-permute-start | bytes 688136 | tf_op jit(solution)/shard_map/ppermute | solution.py:169
  155.5 15.0 %collective-permute-start.37 = (bf16[1,224,512]{2,1,0:T(8,128)(2,1)S(1)}, bf16[1,224,512]{2,1,0:T(8,128)(2,1)S(1)}, u32[]{:S(2)}, u32[]{:S(2)}) collective-permute-start(bf16[1,224,512]{2,1,0:T(8,128)(2,1)S(1)} %get-tuple-element.295), channel_id=1, source_target_pairs={{0,8},{1,25},{2,10},{3,27},{4,12},{5,29},{6,14},{7,31},{8,0},{9,17... | collective-permute-start | bytes 688136 | tf_op jit(solution)/shard_map/ppermute | solution.py:169
  160.8 8.9 %collective-permute-start.39 = (bf16[2,56,512]{2,1,0:T(8,128)(2,1)S(1)}, bf16[2,56,512]{2,1,0:T(8,128)(2,1)S(1)}, u32[]{:S(2)}, u32[]{:S(2)}) collective-permute-start(bf16[2,56,512]{2,1,0:T(8,128)(2,1)S(1)} %get-tuple-element.300), channel_id=1, source_target_pairs={{0,24},{1,9},{2,26},{3,11},{4,28},{5,13},{6,30},{7,15},{8,16},{9,1... | collective-permute-start | bytes 344072 | tf_op jit(solution)/shard_map/ppermute | solution.py:169
  (21 other events, 132.9 us)
